TPU v7x, 32 devices: a whole 2x2x4 slice. The times are simulated.
32 devices in a mesh: rep: 4 (over y, x), ctx: 8 (over z, core).
Axes of the slice: x: 2, y: 2, z: 4, core: 2. Of those that a mesh axis runs over, the one named last changes fastest.
Arguments:
- inputs: bfloat16 [4, 1024, 1536], P('rep', 'ctx'), may hold values from -6 to 6
- segments: int32 [4, 1024], P('rep', 'ctx'), may hold values from 0 to 8, as said below
- positions: int32 [4, 1024], P('rep', 'ctx'), may hold values from 0 to 3070, as said below
- expert_ids: int32 [4, 1024, 8], P('rep', 'ctx'), may hold values from 0 to 15, all different within a row; in each aligned block of 128 rows (0 to 127, 128 to 255, ..., all dimensions but the last counted through in order) at most 96 rows name the same one
- attn_gain: bfloat16 [1536], P('ctx'), may hold values from 0.099609375 to 1.8984375
- w_query: bfloat16 [1536, 1536], P('ctx'), may hold values from -0.15625 to 0.15625
- key_weight: bfloat16 [1536, 512], P('ctx'), may hold values from -0.15625 to 0.15625
- value_weight: bfloat16 [1536, 512], P('ctx'), may hold values from -0.15625 to 0.15625
- w_out: bfloat16 [1536, 1536], P('ctx'), may hold values from -1.25 to 1.25
- ffn_gain: bfloat16 [1536], P('ctx'), may hold values from 0.099609375 to 1.8984375
- router: bfloat16 [1536, 16], P('ctx'), may hold values from -0.078125 to 0.078125
- w_gate: bfloat16 [16, 1536, 512], P('ctx'), may hold values from -0.15625 to 0.15625
- w_up: bfloat16 [16, 1536, 512], P('ctx'), may hold values from -0.15625 to 0.15625
- w_down: bfloat16 [16, 512, 1536], P('ctx'), may hold values from -1 to 1
- grad_out: bfloat16 [4, 1024, 1536], P('rep', 'ctx'), may hold values from -6 to 6
Outputs:
- outputs: bfloat16 [4, 1024, 1536], P('rep', 'ctx')
- grad_in: float32 [4, 1024, 1536], P('rep', 'ctx')
- grad_attn_gain: float32 [1536], P('ctx')
- grad_query: float32 [1536, 1536], P('ctx')
- grad_key: float32 [1536, 512], P('ctx')
- grad_value: float32 [1536, 512], P('ctx')
- grad_proj_out: float32 [1536, 1536], P('ctx')
- grad_ffn_gain: float32 [1536], P('ctx')
- grad_router: float32 [1536, 16], P('ctx')
- grad_gate: float32 [16, 1536, 512], P('ctx')
- grad_up: float32 [16, 1536, 512], P('ctx')
- grad_down: float32 [16, 512, 1536], P('ctx')
Inputs may be any that keep to these rules, and one draw needn't show every extreme that they name: `segments`: per sequence, segment numbers rise from 1 to 8, each document one run of positions of heavy-tailed length, followed by a padding tail of segment 0 with at least 1 and fewer than 51 positions. Within a document the positions rise by one from a starting offset; offsets of all documents but the last are under 2048, and the last document ends at position 3070; in the padding they rise by one from 0. `expert_ids`: each token names 8 different experts; among the 128 tokens of one device (aligned blocks) no expert is named more than 96 times.
All inputs are finite; a program needn't handle non-finite values.
Results may differ from a plain program's by a relative error of at most 0.024.
Values may be sent and summed in bfloat16 or wider, within the bound.
No kernel may reach another device: no remote copies, remote signals or barrier semaphores. Data moves between devices by JAX's collectives and lax.ppermute only.
A program may use at most 192 MiB of HBM per device.

v0:
```python
import jax
import jax.numpy as jnp
from jax import lax
from jax.sharding import PartitionSpec as P

MODEL_WIDTH = 1536
QUERY_HEADS = 24
KEY_VALUE_HEADS = 8
HEAD_SIZE = 64
F = 512


EPS = 1e-06
THETA = 10000.0
MASK_FLOOR = -1e30


def rope_tables(position_row):
    steps = jnp.arange(HEAD_SIZE // 2, dtype=jnp.float32)
    inverse = THETA ** (-(2.0 * steps) / HEAD_SIZE)
    angles = position_row.astype(jnp.float32)[:, None] * inverse[None, :]
    cosine_table = jnp.cos(angles)
    sine_table = jnp.sin(angles)
    return (
        jnp.concatenate([cosine_table, cosine_table], -1),
        jnp.concatenate([sine_table, sine_table], -1),
    )


def apply_rotary(value_block, cosine_table, sine_table):
    half = value_block.shape[-1] // 2
    turned = jnp.concatenate([-value_block[..., half:], value_block[..., :half]], -1)
    return value_block * cosine_table[:, None, :] + turned * sine_table[:, None, :]


def inverse_rotary(grads, cosine_table, sine_table):
    half = grads.shape[-1] // 2
    scaled = grads * sine_table[:, None, :]
    turned = jnp.concatenate([scaled[..., half:], -scaled[..., :half]], -1)
    return grads * cosine_table[:, None, :] + turned


def norm_back(grad_base, base, scale):
    return scale * (grad_base - base * jnp.mean(grad_base * base, -1, keepdims=True))


def gather_keys(key_rows, value_matrix, segment_row):
    return (
        lax.all_gather(key_rows, "ctx", axis=0, tiled=True),
        lax.all_gather(value_matrix, "ctx", axis=0, tiled=True),
        lax.all_gather(segment_row, "ctx", axis=0, tiled=True),
    )


def replica_sum(value_block):
    return (
        lax.psum(value_block[0].astype(jnp.bfloat16), "rep").astype(jnp.float32),
        lax.psum(value_block[1].astype(jnp.bfloat16), "rep").astype(jnp.float32),
        lax.psum(value_block[2].astype(jnp.bfloat16), "rep").astype(jnp.float32),
        lax.psum(value_block[3].astype(jnp.bfloat16), "rep").astype(jnp.float32),
        lax.psum(value_block[4].astype(jnp.bfloat16), "rep").astype(jnp.float32),
        lax.psum(value_block[5].astype(jnp.bfloat16), "rep").astype(jnp.float32),
        lax.psum(value_block[6].astype(jnp.bfloat16), "rep").astype(jnp.float32),
        lax.psum(value_block[7].astype(jnp.bfloat16), "rep").astype(jnp.float32),
        lax.psum(value_block[8].astype(jnp.bfloat16), "rep").astype(jnp.float32),
        lax.psum(value_block[9].astype(jnp.bfloat16), "rep").astype(jnp.float32),
    )


def per_device(
    inputs,
    segments,
    positions,
    expert_ids,
    attn_gain,
    w_query,
    key_weight,
    value_weight,
    w_out,
    ffn_gain,
    router,
    w_gate,
    w_up,
    w_down,
    grad_out,
):
    context_size = lax.axis_size("ctx")
    context_index = lax.axis_index("ctx")
    hidden = inputs[0].astype(jnp.float32)
    token_rows = hidden.shape[0]
    head_group = QUERY_HEADS // KEY_VALUE_HEADS
    score_scale = HEAD_SIZE ** (-0.5)
    segment_row = segments[0]
    live = (segment_row != 0).astype(jnp.float32)[:, None]
    cosine_table, sine_table = rope_tables(positions[0])
    scale_one = lax.rsqrt(jnp.mean(hidden * hidden, -1, keepdims=True) + EPS)
    base_one = hidden * scale_one
    gain_part = lax.all_gather(attn_gain, "ctx", axis=0, tiled=True)
    query_part = lax.all_gather(w_query, "ctx", axis=0, tiled=True)
    key_portion = lax.all_gather(key_weight, "ctx", axis=0, tiled=True)
    value_portion = lax.all_gather(value_weight, "ctx", axis=0, tiled=True)
    columns = base_one
    columns = (columns * gain_part.astype(jnp.float32)).astype(jnp.bfloat16)
    query_raw = jnp.dot(columns, query_part, preferred_element_type=jnp.float32)
    unrotated_key = jnp.dot(columns, key_portion, preferred_element_type=jnp.float32)
    value_raw = jnp.dot(columns, value_portion, preferred_element_type=jnp.float32)
    rotated_query = apply_rotary(
        query_raw.reshape(token_rows, QUERY_HEADS, HEAD_SIZE), cosine_table, sine_table
    ).astype(jnp.bfloat16)
    grouped_query = rotated_query.reshape(token_rows, KEY_VALUE_HEADS, head_group, HEAD_SIZE)
    key_rot = (
        apply_rotary(
            unrotated_key.reshape(token_rows, KEY_VALUE_HEADS, HEAD_SIZE), cosine_table, sine_table
        )
        .astype(jnp.bfloat16)
        .reshape(token_rows, KEY_VALUE_HEADS * HEAD_SIZE)
    )
    value_matrix = value_raw.astype(jnp.bfloat16)
    all_keys, all_values, all_segments = gather_keys(key_rot, value_matrix, segment_row)
    query_place = context_index * token_rows + jnp.arange(token_rows, dtype=jnp.int32)

    def shard_scores(every_key, every_value, segments_all, shard):
        first_block = shard * token_rows
        key_block = lax.dynamic_slice_in_dim(every_key, first_block, token_rows, 0).reshape(
            token_rows, KEY_VALUE_HEADS, HEAD_SIZE
        )
        value_block = lax.dynamic_slice_in_dim(every_value, first_block, token_rows, 0).reshape(
            token_rows, KEY_VALUE_HEADS, HEAD_SIZE
        )
        key_segments = lax.dynamic_slice_in_dim(segments_all, first_block, token_rows, 0)
        scores = (
            jnp.einsum(
                "tvgd,kvd->vgtk", grouped_query, key_block, preferred_element_type=jnp.float32
            )
            * score_scale
        )
        key_place = first_block + jnp.arange(token_rows, dtype=jnp.int32)
        allowed = (segment_row[:, None] == key_segments[None, :]) & (
            key_place[None, :] <= query_place[:, None]
        )
        return (key_block, value_block, scores, allowed)

    def initial_sweep(shard, carry):
        top, total = carry
        key_block, value_block, scores, allowed = shard_scores(
            all_keys, all_values, all_segments, shard
        )
        masked = jnp.where(allowed, scores, MASK_FLOOR)
        new_top = jnp.maximum(top, jnp.max(masked, -1))
        weights = jnp.where(allowed, jnp.exp(masked - new_top[..., None]), 0.0)
        return (new_top, total * jnp.exp(top - new_top) + jnp.sum(weights, -1))

    upper_start = jnp.full((KEY_VALUE_HEADS, head_group, token_rows), MASK_FLOOR, jnp.float32)
    top, total = lax.fori_loop(
        0,
        context_index + 1,
        initial_sweep,
        (upper_start, jnp.zeros((KEY_VALUE_HEADS, head_group, token_rows), jnp.float32)),
    )
    log_total = top + jnp.log(total)

    def second_pass(shard, carry):
        mixed, rest = carry
        key_block, value_block, scores, allowed = shard_scores(
            all_keys, all_values, all_segments, shard
        )
        probs = jnp.where(allowed, jnp.exp(scores - log_total[..., None]), 0.0)
        probs_low = probs.astype(jnp.bfloat16)
        remainder = (probs - probs_low.astype(jnp.float32)).astype(jnp.bfloat16)
        mixed = mixed + jnp.einsum(
            "vgtk,kvd->tvgd", probs_low, value_block, preferred_element_type=jnp.float32
        )
        rest = rest + jnp.einsum(
            "vgtk,kvd->tvgd", remainder, value_block, preferred_element_type=jnp.float32
        )
        return (mixed, rest)

    mixed_zeroed = jnp.zeros((token_rows, KEY_VALUE_HEADS, head_group, HEAD_SIZE), jnp.float32)
    mixed, rest = lax.fori_loop(0, context_index + 1, second_pass, (mixed_zeroed, mixed_zeroed))
    exact = mixed + rest
    mixed_low = mixed.reshape(token_rows, QUERY_HEADS * HEAD_SIZE).astype(jnp.bfloat16)
    columns = mixed_low
    branch = jnp.dot(
        columns,
        lax.all_gather(w_out, "ctx", axis=0, tiled=True),
        preferred_element_type=jnp.float32,
    )
    middle = hidden + branch
    scale_two = lax.rsqrt(jnp.mean(middle * middle, -1, keepdims=True) + EPS)
    base_two = middle * scale_two
    gain_two, router_all = (
        lax.all_gather(ffn_gain, "ctx", axis=0, tiled=True),
        lax.all_gather(router, "ctx", axis=0, tiled=True),
    )
    normed_two = (base_two * gain_two.astype(jnp.float32)).astype(jnp.bfloat16)
    logits = jnp.dot(normed_two, router_all, preferred_element_type=jnp.float32)
    experts_all = router_all.shape[1]
    local_experts = w_gate.shape[0]
    chosen_ids = expert_ids[0]
    top_count = chosen_ids.shape[1]
    capacity = 3 * token_rows * top_count // (2 * experts_all)
    choose = (
        chosen_ids[:, :, None] == jnp.arange(experts_all, dtype=jnp.int32)[None, None, :]
    ).astype(jnp.float32)
    chosen = jnp.sum(choose * logits[:, None, :], -1)
    shifted = jnp.exp(chosen - jnp.max(chosen, -1, keepdims=True))
    gates = shifted / jnp.sum(shifted, -1, keepdims=True)
    flat_ids = chosen_ids.reshape(-1)
    marks = (flat_ids[:, None] == jnp.arange(experts_all, dtype=jnp.int32)[None, :]).astype(
        jnp.int32
    )
    earlier = jnp.cumsum(marks, 0) - marks
    rank = jnp.sum(earlier * marks, 1)
    slots = flat_ids * capacity + rank
    source = (
        jnp.full((experts_all * capacity,), -1, jnp.int32)
        .at[slots]
        .set(jnp.arange(token_rows * top_count, dtype=jnp.int32))
    )
    filled = (source >= 0)[:, None]
    picked = jnp.maximum(source, 0)
    send_rows = jnp.where(
        filled, normed_two[picked // top_count], jnp.zeros((), jnp.bfloat16)
    ).reshape(experts_all, capacity, MODEL_WIDTH)
    received = lax.all_to_all(send_rows, "ctx", split_axis=0, concat_axis=0, tiled=True)
    count = received.shape[1]
    grouped_rows = received.reshape(context_size, local_experts, count, MODEL_WIDTH)
    gate_pre = jnp.einsum(
        "nacd,adf->nacf", grouped_rows, w_gate, preferred_element_type=jnp.float32
    )
    up_pre = jnp.einsum("nacd,adf->nacf", grouped_rows, w_up, preferred_element_type=jnp.float32)
    acted = (gate_pre * jax.nn.sigmoid(gate_pre) * up_pre).astype(jnp.bfloat16)
    result = jnp.einsum("nacf,afd->nacd", acted, w_down, preferred_element_type=jnp.float32).astype(
        jnp.bfloat16
    )
    flat = context_size * local_experts
    returned = result.reshape(flat, count, MODEL_WIDTH)
    gate_kept = gate_pre.reshape(flat, count, F)
    up_kept = up_pre.reshape(flat, count, F)
    back = lax.all_to_all(returned, "ctx", split_axis=0, concat_axis=0, tiled=True).reshape(
        experts_all * capacity, MODEL_WIDTH
    )
    slot_out = back[slots].reshape(token_rows, top_count, MODEL_WIDTH).astype(jnp.float32)
    experts_sum = jnp.sum(gates[:, :, None] * slot_out, 1)
    output = (live * (middle + experts_sum)).astype(jnp.bfloat16)
    grad_live = live * grad_out[0].astype(jnp.float32)
    grad_gates = jnp.sum(grad_live[:, None, :] * slot_out, -1)
    grad_chosen = gates * (grad_gates - jnp.sum(gates * grad_gates, -1, keepdims=True))
    grad_logits = jnp.sum(choose * grad_chosen[:, :, None], 1).astype(jnp.bfloat16)
    grad_slots = (
        (gates[:, :, None] * grad_live[:, None, :])
        .astype(jnp.bfloat16)
        .reshape(token_rows * top_count, MODEL_WIDTH)
    )
    grad_send = jnp.where(filled, grad_slots[picked], jnp.zeros((), jnp.bfloat16)).reshape(
        experts_all, capacity, MODEL_WIDTH
    )
    grad_received = lax.all_to_all(grad_send, "ctx", split_axis=0, concat_axis=0, tiled=True)
    count = grad_received.shape[1]
    grad_grouped = grad_received.reshape(context_size, local_experts, count, MODEL_WIDTH)
    gate_grouped = gate_kept.reshape(context_size, local_experts, count, F)
    up_grouped = up_kept.reshape(context_size, local_experts, count, F)
    rows_grouped = received.reshape(context_size, local_experts, count, MODEL_WIDTH)
    sigma = jax.nn.sigmoid(gate_grouped)
    acted = (gate_grouped * sigma * up_grouped).astype(jnp.bfloat16)
    grad_acted = jnp.einsum(
        "nacd,afd->nacf", grad_grouped, w_down, preferred_element_type=jnp.float32
    )
    grad_down = jnp.einsum(
        "nacf,nacd->afd", acted, grad_grouped, preferred_element_type=jnp.float32
    )
    grad_gate_pre = (
        grad_acted * up_grouped * (sigma * (1.0 + gate_grouped * (1.0 - sigma)))
    ).astype(jnp.bfloat16)
    grad_up_pre = (grad_acted * gate_grouped * sigma).astype(jnp.bfloat16)
    grad_rows = jnp.einsum(
        "nacf,adf->nacd", grad_gate_pre, w_gate, preferred_element_type=jnp.float32
    )
    grad_rows = (
        grad_rows
        + jnp.einsum("nacf,adf->nacd", grad_up_pre, w_up, preferred_element_type=jnp.float32)
    ).astype(jnp.bfloat16)
    grad_gate = jnp.einsum(
        "nacd,nacf->adf", rows_grouped, grad_gate_pre, preferred_element_type=jnp.float32
    )
    grad_up = jnp.einsum(
        "nacd,nacf->adf", rows_grouped, grad_up_pre, preferred_element_type=jnp.float32
    )
    grad_back = lax.all_to_all(
        grad_rows.reshape(context_size * local_experts, count, MODEL_WIDTH),
        "ctx",
        split_axis=0,
        concat_axis=0,
        tiled=True,
    )
    grad_back = grad_back.reshape(experts_all * capacity, MODEL_WIDTH)
    grad_normed_two = jnp.sum(
        grad_back[slots].reshape(token_rows, top_count, MODEL_WIDTH).astype(jnp.float32), 1
    )
    grad_normed_two = grad_normed_two + lax.dot_general(
        grad_logits, router_all, (((1,), (1,)), ((), ())), preferred_element_type=jnp.float32
    )
    router_term = lax.dot_general(
        normed_two, grad_logits, (((0,), (0,)), ((), ())), preferred_element_type=jnp.float32
    )
    gain_two_term = jnp.sum(grad_normed_two * base_two, 0)
    grad_middle = grad_live + norm_back(
        grad_normed_two * gain_two.astype(jnp.float32), base_two, scale_two
    )
    expert_grads = (grad_gate, grad_up, grad_down)
    grad_branch = grad_middle.astype(jnp.bfloat16)
    columns = mixed_low
    grad_proj_out = lax.psum_scatter(
        lax.dot_general(
            columns, grad_branch, (((0,), (0,)), ((), ())), preferred_element_type=jnp.float32
        ).astype(jnp.bfloat16),
        "ctx",
        scatter_dimension=0,
        tiled=True,
    ).astype(jnp.float32)
    mixed_gradient = lax.dot_general(
        grad_branch,
        lax.all_gather(w_out, "ctx", axis=0, tiled=True),
        (((1,), (1,)), ((), ())),
        preferred_element_type=jnp.float32,
    ).astype(jnp.bfloat16)
    grouped_mixed_gradient = mixed_gradient.reshape(
        token_rows, KEY_VALUE_HEADS, head_group, HEAD_SIZE
    )
    delta = jnp.transpose(
        jnp.sum(grouped_mixed_gradient.astype(jnp.float32) * exact, -1), (1, 2, 0)
    )
    every_key, every_value, segments_all = gather_keys(key_rot, value_matrix, segment_row)

    def backward_pass(shard, carry):
        grad_query_acc, key_summand, value_summand = carry
        key_block, value_block, scores, allowed = shard_scores(
            every_key, every_value, segments_all, shard
        )
        probs = jnp.where(allowed, jnp.exp(scores - log_total[..., None]), 0.0)
        grad_probs = jnp.einsum(
            "tvgd,kvd->vgtk",
            grouped_mixed_gradient,
            value_block,
            preferred_element_type=jnp.float32,
        )
        grad_scores = (probs * (grad_probs - delta[..., None])).astype(jnp.bfloat16)
        grad_query_acc = (
            grad_query_acc
            + jnp.einsum(
                "vgtk,kvd->tvgd", grad_scores, key_block, preferred_element_type=jnp.float32
            )
            * score_scale
        )
        key_portion = (
            jnp.einsum(
                "vgtk,tvgd->kvd", grad_scores, grouped_query, preferred_element_type=jnp.float32
            )
            * score_scale
        )
        value_portion = jnp.einsum(
            "vgtk,tvgd->kvd",
            probs.astype(jnp.bfloat16),
            grouped_mixed_gradient,
            preferred_element_type=jnp.float32,
        )
        first_block = shard * token_rows
        key_summand = lax.dynamic_update_slice_in_dim(
            key_summand,
            key_portion.reshape(token_rows, KEY_VALUE_HEADS * HEAD_SIZE),
            first_block,
            0,
        )
        value_summand = lax.dynamic_update_slice_in_dim(
            value_summand,
            value_portion.reshape(token_rows, KEY_VALUE_HEADS * HEAD_SIZE),
            first_block,
            0,
        )
        return (grad_query_acc, key_summand, value_summand)

    zeroed_summand = jnp.zeros(
        (context_size * token_rows, KEY_VALUE_HEADS * HEAD_SIZE), jnp.float32
    )
    grad_query_acc, key_summand, value_summand = lax.fori_loop(
        0, context_index + 1, backward_pass, (mixed_zeroed, zeroed_summand, zeroed_summand)
    )
    own_key_gradient, grad_value_own = (
        lax.psum_scatter(
            key_summand.astype(jnp.bfloat16), "ctx", scatter_dimension=0, tiled=True
        ).astype(jnp.float32),
        lax.psum_scatter(
            value_summand.astype(jnp.bfloat16), "ctx", scatter_dimension=0, tiled=True
        ).astype(jnp.float32),
    )
    grad_query_low = (
        inverse_rotary(
            grad_query_acc.reshape(token_rows, QUERY_HEADS, HEAD_SIZE), cosine_table, sine_table
        )
        .astype(jnp.bfloat16)
        .reshape(token_rows, QUERY_HEADS * HEAD_SIZE)
    )
    grad_key_low = (
        inverse_rotary(
            own_key_gradient.reshape(token_rows, KEY_VALUE_HEADS, HEAD_SIZE),
            cosine_table,
            sine_table,
        )
        .astype(jnp.bfloat16)
        .reshape(token_rows, KEY_VALUE_HEADS * HEAD_SIZE)
    )
    grad_value_low = grad_value_own.astype(jnp.bfloat16)
    gain_part = lax.all_gather(attn_gain, "ctx", axis=0, tiled=True)
    query_part = lax.all_gather(w_query, "ctx", axis=0, tiled=True)
    key_portion = lax.all_gather(key_weight, "ctx", axis=0, tiled=True)
    value_portion = lax.all_gather(value_weight, "ctx", axis=0, tiled=True)
    contract = (((1,), (1,)), ((), ()))
    part = lax.dot_general(grad_query_low, query_part, contract, preferred_element_type=jnp.float32)
    part = part + lax.dot_general(
        grad_key_low, key_portion, contract, preferred_element_type=jnp.float32
    )
    part = part + lax.dot_general(
        grad_value_low, value_portion, contract, preferred_element_type=jnp.float32
    )
    first_normed = (base_one * gain_part.astype(jnp.float32)).astype(jnp.bfloat16)
    rows_contract = (((0,), (0,)), ((), ()))
    query_term = lax.dot_general(
        first_normed, grad_query_low, rows_contract, preferred_element_type=jnp.float32
    )
    key_weight_term = lax.dot_general(
        first_normed, grad_key_low, rows_contract, preferred_element_type=jnp.float32
    )
    value_weight_term = lax.dot_general(
        first_normed, grad_value_low, rows_contract, preferred_element_type=jnp.float32
    )
    gain_one_term = jnp.sum(part * base_one, 0)
    grad_in = grad_middle + norm_back(part * gain_part.astype(jnp.float32), base_one, scale_one)
    shares = (
        lax.psum_scatter(
            query_term.astype(jnp.bfloat16), "ctx", scatter_dimension=0, tiled=True
        ).astype(jnp.float32),
        lax.psum_scatter(
            key_weight_term.astype(jnp.bfloat16), "ctx", scatter_dimension=0, tiled=True
        ).astype(jnp.float32),
        lax.psum_scatter(
            value_weight_term.astype(jnp.bfloat16), "ctx", scatter_dimension=0, tiled=True
        ).astype(jnp.float32),
        lax.psum_scatter(
            gain_one_term.astype(jnp.bfloat16), "ctx", scatter_dimension=0, tiled=True
        ).astype(jnp.float32),
        lax.psum_scatter(
            router_term.astype(jnp.bfloat16), "ctx", scatter_dimension=0, tiled=True
        ).astype(jnp.float32),
        lax.psum_scatter(
            gain_two_term.astype(jnp.bfloat16), "ctx", scatter_dimension=0, tiled=True
        ).astype(jnp.float32),
    )
    summed_all = replica_sum(
        (
            shares[0],
            shares[1],
            shares[2],
            shares[3],
            shares[4],
            shares[5],
            grad_proj_out,
            expert_grads[0],
            expert_grads[1],
            expert_grads[2],
        )
    )
    summed = summed_all[:7]
    gate_total, up_total, down_total = (summed_all[7], summed_all[8], summed_all[9])
    return (
        output[None],
        grad_in[None],
        summed[3],
        summed[0],
        summed[1],
        summed[2],
        summed[6],
        summed[5],
        summed[4],
        gate_total,
        up_total,
        down_total,
    )


def solution(mesh):
    return jax.shard_map(
        per_device,
        mesh=mesh,
        in_specs=(
            P("rep", "ctx", None),
            P("rep", "ctx"),
            P("rep", "ctx"),
            P("rep", "ctx", None),
            P("ctx"),
            P("ctx", None),
            P("ctx", None),
            P("ctx", None),
            P("ctx", None),
            P("ctx"),
            P("ctx", None),
            P("ctx", None, None),
            P("ctx", None, None),
            P("ctx", None, None),
            P("rep", "ctx", None),
        ),
        out_specs=(
            P("rep", "ctx", None),
            P("rep", "ctx", None),
            P("ctx"),
            P("ctx", None),
            P("ctx", None),
            P("ctx", None),
            P("ctx", None),
            P("ctx"),
            P("ctx", None),
            P("ctx", None, None),
            P("ctx", None, None),
            P("ctx", None, None),
        ),
        check_vma=False,
    )
```

profile of v0, /device:TPU:0, one launch (start us, length us, event | category | flops | bytes accessed | tf_op | source)
XLA Modules:
  0.0 1381.9 jit_solution(1273379138594821238)
XLA Ops:
  12.4 19.3 %all-reduce.5 = (bf16[1536]{0:T(1024)(128)(2,1)S(1)}, bf16[1536]{0:T(1024)(128)(2,1)}) all-reduce(bf16[1536]{0:T(1024)(128)(2,1)S(1)} %dynamic-update-slice, bf16[1536]{0:T(1024)(128)(2,1)S(1)} %dynamic-update-slice.1), channel_id=1, replica_groups=mesh['rep'=4,'ctx'=8] {'ctx'}, use_global_device_ids=true, to_apply=%add | all-reduce | flops 3072 | bytes 12288
  33.0 4.8 all-gather.9.cloned.1.call-done
  42.4 21.6 %all-gather.13.cloned.1.call-done = bf16[1536,512]{1,0:T(8,128)(2,1)} async-done(((bf16[192,512]{1,0:T(8,128)(2,1)}), bf16[1536,512]{1,0:T(8,128)(2,1)}) %all-gather.13.cloned.1.call-update) | async-done | bytes 1572880 | tf_op jit(solution)/shard_map/all_gather | solution.py:100
  71.3 10.5 all-gather
  89.1 9.3 reduce-window.6
  107.1 4.5 scatter_custom_fusion
  115.4 14.7 %all-gather.1 = bf16[8,192,16]{1,2,0:T(8,128)(2,1)S(1)} all-gather(bf16[1,192,16]{1,2,0:T(8,128)(2,1)} %bitcast.436), channel_id=1, replica_groups=mesh['rep'=4,'ctx'=8] {'ctx'}, dimensions={0}, use_global_device_ids=true | all-gather | bytes 55296 | tf_op jit(solution)/shard_map/all_gather | solution.py:193
  141.0 6.6 copy.126
  147.6 3.9 fusion.73
  152.6 13.3 all-gather.15.cloned.1.call-done
  166.5 4.9 while.41
  174.6 6.2 while.42
  182.7 35.0 %all-gather.19.cloned.1.call-done = bf16[1536,1536]{1,0:T(8,128)(2,1)} async-done(((bf16[192,1536]{1,0:T(8,128)(2,1)}), bf16[1536,1536]{1,0:T(8,128)(2,1)}) %all-gather.19.cloned.1.call-update) | async-done | bytes 4718608 | tf_op jit(solution)/shard_map/all_gather | solution.py:185
  228.2 6.3 gather_fusion
  237.8 12.8 gather_fusion.2
  250.6 6.8 broadcast_select_fusion
  257.3 151.1 %all_to_all.20 = bf16[16,96,1536]{2,1,0:T(8,128)(2,1)} all-to-all(bf16[16,96,1536]{2,1,0:T(8,128)(2,1)S(1)} %get-tuple-element.523), channel_id=1, replica_groups=mesh['rep'=4,'ctx'=8] {'ctx'}, dimensions={0} | all-to-all | bytes 9437184 | tf_op jit(solution)/shard_map/all_to_all | solution.py:225
  408.4 5.2 all-to-all-start.2
  413.6 7.7 fusion.27
  421.3 4.3 fusion.29
  425.6 93.2 %all-to-all-done.2 = bf16[16,96,1536]{2,1,0:T(8,128)(2,1)} async-done(((bf16[16,96,1536]{2,1,0:T(8,128)(2,1)}), bf16[16,96,1536]{2,1,0:T(8,128)(2,1)}, u32[]{:S(2)}, u32[]{:S(2)}) %all-to-all-start.2) | async-done | bytes 4718624 | tf_op jit(solution)/shard_map/all_to_all | solution.py:258
  518.8 8.4 fusion.40
  532.5 4.9 all-to-all-start.1
  537.4 4.2 fusion.34
  541.5 4.8 fusion.31
  549.0 93.6 %all-to-all-done.1 = bf16[16,96,1536]{2,1,0:T(8,128)(2,1)} async-done(((bf16[16,96,1536]{2,1,0:T(8,128)(2,1)}), bf16[16,96,1536]{2,1,0:T(8,128)(2,1)}, u32[]{:S(2)}, u32[]{:S(2)}) %all-to-all-start.1) | async-done | bytes 4718624 | tf_op jit(solution)/shard_map/all_to_all | solution.py:240
  642.6 4.7 all-to-all-start.3
  648.2 9.7 gather_fusion.1
  657.9 4.4 fusion.22
  664.5 88.0 %all-to-all-done.3 = bf16[16,96,1536]{2,1,0:T(8,128)(2,1)} async-done(((bf16[16,96,1536]{2,1,0:T(8,128)(2,1)}), bf16[16,96,1536]{2,1,0:T(8,128)(2,1)}, u32[]{:S(2)}, u32[]{:S(2)}) %all-to-all-start.3) | async-done | bytes 4718624 | tf_op jit(solution)/shard_map/all_to_all | solution.py:289
  752.6 10.3 gather_fusion.3
  762.9 4.1 convert_reduce_fusion
  769.2 4.3 convolution_convert_fusion.4
  777.9 9.7 while.43
  791.5 95.8 %reduce-scatter.24.cloned.1.call-done = bf16[128,512]{1,0:T(8,128)(2,1)} async-done(((bf16[1024,512]{1,0:T(8,128)(2,1)}), bf16[128,512]{1,0:T(8,128)(2,1)}) %reduce-scatter.24.cloned.1.call-update) | async-done | bytes 131088
  890.4 30.4 %reduce-scatter.22.cloned.1.call-done = bf16[128,512]{1,0:T(8,128)(2,1)} async-done(((bf16[1024,512]{1,0:T(8,128)(2,1)}), bf16[128,512]{1,0:T(8,128)(2,1)}) %reduce-scatter.22.cloned.1.call-update) | async-done | bytes 131088
  928.7 3.7 convolution_convert_fusion.1
  932.5 7.3 bitcast_convert_fusion.1
  939.8 7.5 bitcast_convert_fusion.2
  948.7 7.2 bitcast_convert_fusion
  955.9 34.2 %reduce-scatter.16.cloned.1.call-done = bf16[192,512]{1,0:T(8,128)(2,1)} async-done(((bf16[1536,512]{1,0:T(8,128)(2,1)}), bf16[192,512]{1,0:T(8,128)(2,1)}) %reduce-scatter.16.cloned.1.call-update) | async-done | bytes 196624 | tf_op jit(solution)/shard_map/reduce_scatter | solution.py:442
  990.0 56.0 %reduce-scatter.20.cloned.1.call-done = bf16[192,1536]{1,0:T(8,128)(2,1)} async-done(((bf16[1536,1536]{1,0:T(8,128)(2,1)}), bf16[192,1536]{1,0:T(8,128)(2,1)}) %reduce-scatter.20.cloned.1.call-update) | async-done | bytes 589840 | tf_op jit(solution)/shard_map/reduce_scatter | solution.py:313
  1046.0 56.1 %reduce-scatter.14.cloned.1.call-done = bf16[192,1536]{1,0:T(8,128)(2,1)} async-done(((bf16[1536,1536]{1,0:T(8,128)(2,1)}), bf16[192,1536]{1,0:T(8,128)(2,1)}) %reduce-scatter.14.cloned.1.call-update) | async-done | bytes 589840 | tf_op jit(solution)/shard_map/reduce_scatter | solution.py:439
  1103.0 4.0 fusion.106
  1107.0 26.9 %reduce-scatter.26.cloned.1.call-done = bf16[192,16]{1,0:T(8,128)(2,1)} async-done(((bf16[1536,16]{1,0:T(8,128)(2,1)}), bf16[192,16]{1,0:T(8,128)(2,1)}) %reduce-scatter.26.cloned.1.call-update) | async-done | bytes 6160
  1139.1 14.0 %all-reduce.4 = (bf16[1536]{0:T(1024)(128)(2,1)S(1)}, bf16[1536]{0:T(1024)(128)(2,1)S(1)}) all-reduce(bf16[1536]{0:T(1024)(128)(2,1)S(1)} %get-tuple-element.411, bf16[1536]{0:T(1024)(128)(2,1)S(1)} %copy-done.51), channel_id=5, replica_groups=mesh['rep'=4,'ctx'=8] {'ctx'}, use_global_device_ids=true, to_apply=%region_28.29.clone | all-reduce | flops 3072 | bytes 12288
  1153.2 11.1 all-reduce.6
  1167.2 189.0 %all-reduce.10.cloned.1.call-done = (bf16[192,1536]{1,0:T(8,128)(2,1)}, bf16[192,512]{1,0:T(8,128)(2,1)}, bf16[192,512]{1,0:T(8,128)(2,1)}, bf16[192,1536]{1,0:T...) async-done(((bf16[192,1536]{1,0:T(8,128)(2,1)}, bf16[192,512]{1,0:T(8,128)(2,1)}, ...) | async-done | bytes 11010064 | tf_op jit(solution)/shard_map/psum | solution.py:57
  (289 shorter events, 150.3 us)
Async XLA Ops:
  7.2 511.6 %copy-start = (bf16[2,512,1536]{2,1,0:T(8,128)(2,1)S(1)}, bf16[2,512,1536]{2,1,0:T(8,128)(2,1)}, u32[]{:S(2)}) copy-start(bf16[2,512,1536]{2,1,0:T(8,128)(2,1)} %param.34) | copy-start | bytes 9437188
  7.2 33.8 %copy-start.57 = (s32[1,128]{1,0:T(1,128)S(1)}, s32[1,128]{1,0:T(1,128)}, u32[]{:S(2)}) copy-start(s32[1,128]{1,0:T(1,128)} %param.23) | copy-start | bytes 1540
  7.2 30.5 %all-gather.9.cloned.1.call-start = ((), (), s32[]{:S(2)}) async-start(), calls=%async_computation.11 | async-start | bytes 1769472 | tf_op jit(solution)/shard_map/all_gather | solution.py:101
  7.9 56.1 %all-gather.13.cloned.1.call-start = ((), (), s32[]{:S(2)}) async-start(), calls=%async_computation.13 | async-start | bytes 1769472 | tf_op jit(solution)/shard_map/all_gather | solution.py:100
  8.7 126.9 %all-gather.11.cloned.1.call-start = ((), (), s32[]{:S(2)}) async-start(), calls=%async_computation.12 | async-start | bytes 1179648 | tf_op jit(solution)/shard_map/all_gather | solution.py:50
  31.8 115.9 %copy-start.33 = (f32[1536]{0:T(1024)}, f32[1536]{0:T(1024)S(1)}, u32[]{:S(2)}) copy-start(f32[1536]{0:T(1024)S(1)} %convert_element_type.263) | copy-start | bytes 18436
  32.9 33.7 %copy-start.8 = (bf16[1,128,1536]{2,1,0:T(8,128)(2,1)S(1)}, bf16[1,128,1536]{2,1,0:T(8,128)(2,1)}, u32[]{:S(2)}) copy-start(bf16[1,128,1536]{2,1,0:T(8,128)(2,1)} %param.21) | copy-start | bytes 1179652
  32.9 31.0 %copy-start.48 = (f32[128]{0:T(128)}, f32[128]{0:T(128)S(1)}, u32[]{:S(2)}) copy-start(f32[128]{0:T(128)S(1)} %add_rsqrt_fusion.1) | copy-start | bytes 1540
  40.4 100.6 %all-gather.17.cloned.1.call-start = ((), (), s32[]{:S(2)}) async-start(), calls=%async_computation.15 | async-start | bytes 5308416 | tf_op jit(solution)/shard_map/all_gather | solution.py:99
  41.0 124.9 %all-gather.15.cloned.1.call-start = ((), (), s32[]{:S(2)}) async-start(), calls=%async_computation.14 | async-start | bytes 1179648 | tf_op jit(solution)/shard_map/all_gather | solution.py:49
  64.0 6.8 copy-start.41
  64.0 17.7 %copy-start.44 = (s32[1,128,8]{1,2,0:T(8,128)S(1)}, s32[1,128,8]{1,2,0:T(8,128)}, u32[]{:S(2)}) copy-start(s32[1,128,8]{1,2,0:T(8,128)} %param.24) | copy-start | bytes 12292
  70.2 147.5 %all-gather.19.cloned.1.call-start = ((), (), s32[]{:S(2)}) async-start(), calls=%async_computation.16 | async-start | bytes 5308416 | tf_op jit(solution)/shard_map/all_gather | solution.py:185
  141.0 6.6 copy-start.49
  408.4 110.4 %all-to-all-start.2 = ((bf16[16,96,1536]{2,1,0:T(8,128)(2,1)}), bf16[16,96,1536]{2,1,0:T(8,128)(2,1)}, u32[]{:S(2)}, u32[]{:S(2)}) async-start(bf16[16,96,1536]{2,1,0:T(8,128)(2,1)} %get-tuple-element.522), calls=%async_computation.2 | async-start | bytes 9437184 | tf_op jit(solution)/shard_map/all_to_all | solution.py:258
  413.6 7.7 copy-start.15
  413.6 7.7 copy-start.17
  532.5 110.1 %all-to-all-start.1 = ((bf16[16,96,1536]{2,1,0:T(8,128)(2,1)}), bf16[16,96,1536]{2,1,0:T(8,128)(2,1)}, u32[]{:S(2)}, u32[]{:S(2)}) async-start(bf16[16,96,1536]{2,1,0:T(8,128)(2,1)} %bitcast.404), calls=%async_computation.1 | async-start | bytes 9437184 | tf_op jit(solution)/shard_map/all_to_all | solution.py:240
  642.6 5.0 copy-start.52
  642.6 110.0 %all-to-all-start.3 = ((bf16[16,96,1536]{2,1,0:T(8,128)(2,1)}), bf16[16,96,1536]{2,1,0:T(8,128)(2,1)}, u32[]{:S(2)}, u32[]{:S(2)}) async-start(bf16[16,96,1536]{2,1,0:T(8,128)(2,1)} %bitcast.403), calls=%async_computation.3 | async-start | bytes 9437184 | tf_op jit(solution)/shard_map/all_to_all | solution.py:289
  647.3 240.0 %reduce-scatter.24.cloned.1.call-start = ((), (), s32[]{:S(2)}) async-start(), calls=%async_computation.22 | async-start | bytes 1179648
  664.5 102.5 %copy-start.46 = (bf16[128,16]{0,1:T(8,128)(2,1)}, bf16[128,16]{0,1:T(8,128)(2,1)S(1)}, u32[]{:S(2)}) copy-start(bf16[128,16]{0,1:T(8,128)(2,1)S(1)} %select_reduce_fusion.1) | copy-start | bytes 12292
  762.9 5.1 copy-start.19
  762.9 5.1 copy-start.25
  762.9 5.1 copy-start.56
  769.2 5.3 copy-start.12
  769.2 5.3 copy-start.4
  769.2 5.3 copy-start.7
  787.6 99.7 %copy-start.9 = (bf16[1,128,1536]{2,1,0:T(8,128)(2,1)S(1)}, bf16[1,128,1536]{2,1,0:T(8,128)(2,1)}, u32[]{:S(2)}) copy-start(bf16[1,128,1536]{2,1,0:T(8,128)(2,1)} %param.21) | copy-start | bytes 1179652
  787.6 99.7 %copy-start.34 = (f32[1536]{0:T(1024)S(1)}, f32[1536]{0:T(1024)}, u32[]{:S(2)}) copy-start(f32[1536]{0:T(1024)} %copy-done.33) | copy-start | bytes 18436
  787.6 99.7 %copy-start.50 = (f32[128]{0:T(128)S(1)}, f32[128]{0:T(128)}, u32[]{:S(2)}) copy-start(f32[128]{0:T(128)} %copy-done.48) | copy-start | bytes 1540
  790.0 130.7 %reduce-scatter.22.cloned.1.call-start = ((), (), s32[]{:S(2)}) async-start(), calls=%async_computation.21 | async-start | bytes 1179648
  790.1 131.7 %copy-start.32 = (f32[128,64]{0,1:T(8,128)S(1)}, f32[128,64]{0,1:T(8,128)}, u32[]{:S(2)}) copy-start(f32[128,64]{0,1:T(8,128)} %pad_maximum_fusion.3) | copy-start | bytes 98308
  791.4 130.5 %copy-start.27 = (f32[128,64]{0,1:T(8,128)S(1)}, f32[128,64]{0,1:T(8,128)}, u32[]{:S(2)}) copy-start(f32[128,64]{0,1:T(8,128)} %pad_maximum_fusion.2) | copy-start | bytes 98308
  791.5 164.4 %reduce-scatter.18.cloned.1.call-start = ((), (), s32[]{:S(2)}) async-start(), calls=%async_computation.19 | async-start | bytes 1769472 | tf_op jit(solution)/shard_map/reduce_scatter | solution.py:445
  890.1 33.8 %copy-start.13 = (f32[128,1536]{1,0:T(8,128)S(1)}, f32[128,1536]{1,0:T(8,128)}, u32[]{:S(2)}) copy-start(f32[128,1536]{1,0:T(8,128)} %copy-done.12) | copy-start | bytes 2359300
  890.1 33.8 %copy-start.14 = (bf16[128,8,3,64]{0,3,2,1:T(8,128)(2,1)S(1)}, bf16[128,8,3,64]{0,3,2,1:T(8,128)(2,1)}, u32[]{:S(2)}) copy-start(bf16[128,8,3,64]{0,3,2,1:T(8,128)(2,1)} %convert_element_type.273) | copy-start | bytes 1179652
  890.1 99.9 %reduce-scatter.16.cloned.1.call-start = ((), (), s32[]{:S(2)}) async-start(), calls=%async_computation.18 | async-start | bytes 1769472 | tf_op jit(solution)/shard_map/reduce_scatter | solution.py:442
  922.0 5.5 copy-start.29
  923.8 122.2 %reduce-scatter.20.cloned.1.call-start = ((), (), s32[]{:S(2)}) async-start(), calls=%async_computation.20 | async-start | bytes 5308416 | tf_op jit(solution)/shard_map/reduce_scatter | solution.py:313
  927.5 174.6 %reduce-scatter.14.cloned.1.call-start = ((), (), s32[]{:S(2)}) async-start(), calls=%async_computation.17 | async-start | bytes 5308416 | tf_op jit(solution)/shard_map/reduce_scatter | solution.py:439
  932.4 201.5 %reduce-scatter.26.cloned.1.call-start = ((), (), s32[]{:S(2)}) async-start(), calls=%async_computation.23 | async-start | bytes 442368
  932.5 7.3 copy-start.23
  939.8 7.5 copy-start.47
  948.4 407.9 %all-reduce.10.cloned.1.call-start = ((), (), s32[]{:S(2)}) async-start(), calls=%async_computation.24 | async-start | bytes 22020096 | tf_op jit(solution)/shard_map/psum | solution.py:57
  1102.9 31.8 %copy-start.30 = (bf16[128,512]{0,1:T(8,128)(2,1)S(1)}, bf16[128,512]{0,1:T(8,128)(2,1)}, u32[]{:S(2)}) copy-start(bf16[128,512]{0,1:T(8,128)(2,1)} %copy-done.29) | copy-start | bytes 393220
  1102.9 33.9 %copy-start.37 = (bf16[128,512]{1,0:T(8,128)(2,1)S(1)}, bf16[128,512]{1,0:T(8,128)(2,1)}, u32[]{:S(2)}) copy-start(bf16[128,512]{1,0:T(8,128)(2,1)} %reduce-scatter.24.cloned.1.call-done) | copy-start | bytes 393220
  1356.2 8.0 copy-start.22
  (28 other events, 88.7 us)
Sparse Core Ops, SparseCore 0:
  9.7 27.9 all-gather.8
  39.4 24.5 all-gather.12
  66.2 21.6 all-gather.10
  89.4 51.5 all-gather.16
  143.0 22.7 all-gather.14
  167.3 50.3 all-gather.18
  790.2 97.0 reduce-scatter.23
  890.1 30.5 reduce-scatter.21
  923.1 32.6 reduce-scatter.17
  957.9 32.0 reduce-scatter.15
  992.9 53.0 reduce-scatter.19
  1048.7 53.3 reduce-scatter.13
  1104.9 28.9 reduce-scatter.25
  1139.8 216.3 all-reduce.9
where the time goes:
time: 1390 us; the launch traced here: 1380 us
  waiting for transfers between devices  843 us (61%)
  blocking collectives  221 us (16%)
  local copies, waits for them, and re-layouts  105 us (8%)
  matrix products  101 us (7%)
  other arithmetic  79.1 us (6%)
  between operations  16.2 us (1%)
  starting transfers between devices  16 us (1%)
    psum x1, waiting for transfers between devices, replica_sum(): lax.psum(value_block[0].astype(jnp.bfloat16), 'rep').astype(jnp.float32)  189 us
    unnamed x17, waiting for transfers between devices  156 us
    all_to_all x1, blocking collectives, per_device(): lax.all_to_all(send_rows, 'ctx', split_axis=0, concat_axis=0, tiled=True)  151 us
    all_to_all x1, waiting for transfers between devices, per_device(): lax.all_to_all(returned, 'ctx', split_axis=0, concat_axis=0, tiled=True)  93.6 us
    all_to_all x1, waiting for transfers between devices, per_device(): lax.all_to_all(grad_send, 'ctx', split_axis=0, concat_axis=0, tiled=True)  93.2 us
    all_to_all x1, waiting for transfers between devices, per_device(): lax.all_to_all(grad_rows.reshape(context_size * local_experts, count, MOD...  88 us
    reduce_scatter x1, waiting for transfers between devices, per_device(): lax.psum_scatter(query_term.astype(jnp.bfloat16), 'ctx', scatter_dimensio...  56.1 us
    reduce_scatter x1, waiting for transfers between devices, per_device(): lax.psum_scatter(lax.dot_general(columns, grad_branch, (((0,), (0,)), (()...  56 us
  transfers between devices with their start and end apart: 17, of which 15 were waited for; matrix products, arithmetic and copies ran while one was open for 13% of the time, Pallas kernels for 0%

commit v1 on v0

v1 whole, which is shorter than its diff:
```python
import jax
import jax.numpy as jnp
from jax import lax
from jax.experimental import pallas as pl
from jax.experimental.pallas import tpu as pltpu
from jax.sharding import PartitionSpec as P

MODEL_WIDTH = 1536
QUERY_HEADS = 24
KEY_VALUE_HEADS = 8
HEAD_GROUP = QUERY_HEADS // KEY_VALUE_HEADS
HEAD_SIZE = 64

EPS = 1e-06
THETA = 10000.0
MASK_FLOOR = -1e30

ROWS = (((0,), (0,)), ((), ()))
COLUMNS = (((1,), (1,)), ((), ()))


def dot(left, right, contract=(((1,), (0,)), ((), ()))):
    return lax.dot_general(left, right, contract, preferred_element_type=jnp.float32)


def rope_tables(position_row):
    steps = jnp.arange(HEAD_SIZE // 2, dtype=jnp.float32)
    inverse = THETA ** (-(2.0 * steps) / HEAD_SIZE)
    angles = position_row.astype(jnp.float32)[:, None] * inverse[None, :]
    cosine_table = jnp.cos(angles)
    sine_table = jnp.sin(angles)
    return (
        jnp.concatenate([cosine_table, cosine_table], -1),
        jnp.concatenate([sine_table, sine_table], -1),
    )


def norm_back(grad_base, base, scale):
    return scale * (grad_base - base * jnp.mean(grad_base * base, -1, keepdims=True))


def turn(rows):
    half = HEAD_SIZE // 2
    return jnp.concatenate([-rows[:, half:], rows[:, :half]], 1)


def turn_back(rows):
    half = HEAD_SIZE // 2
    return jnp.concatenate([rows[:, half:], -rows[:, :half]], 1)


def stack_heads(rows):
    return jnp.concatenate(
        [rows[:, h * HEAD_SIZE : (h + 1) * HEAD_SIZE] for h in range(HEAD_GROUP)], 0
    )


def side_heads(rows):
    block = rows.shape[0] // HEAD_GROUP
    return jnp.concatenate([rows[h * block : (h + 1) * block] for h in range(HEAD_GROUP)], 1)


def lanes(values, combine):
    total = values[:, :128]
    for start in range(128, values.shape[1], 128):
        total = combine(total, values[:, start : start + 128])
    return total


def masked_scores(stacked, keys, row_segments, key_segments, row_start, key_start):
    block = row_segments.shape[0]
    scores = dot(stacked, keys, COLUMNS) * HEAD_SIZE ** (-0.5)
    row_place = row_start + lax.broadcasted_iota(jnp.int32, (block, block), 0)
    key_place = key_start + lax.broadcasted_iota(jnp.int32, (block, block), 1)
    allowed = (row_segments == key_segments) & (key_place <= row_place)
    scores = scores.reshape(HEAD_GROUP, block, block)
    return jnp.where(allowed[None], scores, MASK_FLOOR).reshape(HEAD_GROUP * block, block)


def attend_kernel(
    first_ref,
    hidden_ref,
    gain_ref,
    weight_ref,
    cosine_ref,
    sine_ref,
    row_segment_ref,
    key_segment_ref,
    normed_ref,
    query_ref,
    key_ref,
    value_ref,
    mixed_ref,
    log_ref,
    score_ref,
):
    step = pl.program_id(0)
    block = hidden_ref.shape[0]
    query_width = query_ref.shape[1]
    here = pl.ds(pl.multiple_of(step * block, block), block)
    hidden = hidden_ref[...].astype(jnp.float32)
    scale = lax.rsqrt(jnp.mean(hidden * hidden, -1, keepdims=True) + EPS)
    normed = (hidden * scale * gain_ref[...]).astype(jnp.bfloat16)
    normed_ref[...] = normed
    raw = dot(normed, weight_ref[...])
    cosine = cosine_ref[...]
    sine = sine_ref[...]
    key_raw = raw[:, query_width : query_width + HEAD_SIZE]
    key_ref[here, :] = (key_raw * cosine + turn(key_raw) * sine).astype(jnp.bfloat16)
    value_ref[here, :] = raw[:, query_width + HEAD_SIZE :].astype(jnp.bfloat16)
    query_raw = stack_heads(raw[:, :query_width])
    cosine = jnp.concatenate([cosine] * HEAD_GROUP, 0)
    sine = jnp.concatenate([sine] * HEAD_GROUP, 0)
    query = (query_raw * cosine + turn(query_raw) * sine).astype(jnp.bfloat16)
    query_ref[...] = side_heads(query)
    rows = HEAD_GROUP * block
    row_segments = row_segment_ref[...]

    def first_pass(index, top):
        there = pl.ds(pl.multiple_of(index * block, block), block)
        scores = masked_scores(
            query,
            key_ref[there, :],
            row_segments,
            key_segment_ref[:, there],
            step * block,
            index * block,
        )
        score_ref[index] = scores
        return jnp.maximum(top, lanes(scores, jnp.maximum))

    top = lax.fori_loop(
        first_ref[step], step + 1, first_pass, jnp.full((rows, 128), MASK_FLOOR, jnp.float32)
    )
    top = jnp.max(top, -1, keepdims=True)

    def second_pass(index, carry):
        total, mixed = carry
        there = pl.ds(pl.multiple_of(index * block, block), block)
        weights = jnp.exp(score_ref[index] - top)
        mixed = mixed + dot(weights.astype(jnp.bfloat16), value_ref[there, :])
        return total + lanes(weights, jnp.add), mixed

    total, mixed = lax.fori_loop(
        first_ref[step],
        step + 1,
        second_pass,
        (
            jnp.zeros((rows, 128), jnp.float32),
            jnp.zeros((rows, HEAD_SIZE), jnp.float32),
        ),
    )
    total = jnp.sum(total, -1, keepdims=True)
    mixed_ref[...] = side_heads((mixed / total).astype(jnp.bfloat16))
    log_ref[...] = (top + jnp.log(total)).reshape(HEAD_GROUP, block, 1)


def attend(hidden, gain, weight, cosine, sine, segment_row, block, first):
    tokens, features = hidden.shape
    query_width = HEAD_GROUP * HEAD_SIZE
    steps = tokens // block
    rows = lambda width: pl.BlockSpec((block, width), lambda i, f: (i, 0))
    whole = lambda height, width: pl.BlockSpec((height, width), lambda i, f: (0, 0))
    return pl.pallas_call(
        attend_kernel,
        out_shape=(
            jax.ShapeDtypeStruct((tokens, features), jnp.bfloat16),
            jax.ShapeDtypeStruct((tokens, query_width), jnp.bfloat16),
            jax.ShapeDtypeStruct((tokens, HEAD_SIZE), jnp.bfloat16),
            jax.ShapeDtypeStruct((tokens, HEAD_SIZE), jnp.bfloat16),
            jax.ShapeDtypeStruct((tokens, query_width), jnp.bfloat16),
            jax.ShapeDtypeStruct((HEAD_GROUP, tokens, 1), jnp.float32),
        ),
        grid_spec=pltpu.PrefetchScalarGridSpec(
            num_scalar_prefetch=1,
            grid=(steps,),
            in_specs=[
                rows(features),
                whole(1, features),
                whole(*weight.shape),
                rows(HEAD_SIZE),
                rows(HEAD_SIZE),
                rows(1),
                whole(1, tokens),
            ],
            out_specs=[
                rows(features),
                rows(query_width),
                whole(tokens, HEAD_SIZE),
                whole(tokens, HEAD_SIZE),
                rows(query_width),
                pl.BlockSpec((HEAD_GROUP, block, 1), lambda i, f: (0, i, 0)),
            ],
            scratch_shapes=[pltpu.VMEM((steps, HEAD_GROUP * block, block), jnp.float32)],
        ),
        compiler_params=pltpu.CompilerParams(vmem_limit_bytes=48 << 20),
        cost_estimate=pl.CostEstimate(
            flops=2 * tokens * features * weight.shape[1] + 4 * tokens * tokens * query_width,
            bytes_accessed=4 * tokens * features + 2 * weight.size,
            transcendentals=tokens * tokens * HEAD_GROUP // 2,
        ),
    )(
        first,
        hidden,
        gain[None, :],
        weight,
        cosine,
        sine,
        segment_row[:, None],
        segment_row[None, :],
    )


def attend_back_kernel(
    first_ref,
    query_ref,
    grad_ref,
    log_ref,
    cosine_ref,
    sine_ref,
    row_segment_ref,
    key_segment_ref,
    key_ref,
    value_ref,
    key_cosine_ref,
    key_sine_ref,
    grad_query_ref,
    grad_pair_ref,
    probs_ref,
    grad_probs_ref,
    grad_key_ref,
    grad_value_ref,
):
    step = pl.program_id(0)
    block = query_ref.shape[0]
    rows = HEAD_GROUP * block

    @pl.when(step == 0)
    def _():
        grad_key_ref[...] = jnp.zeros_like(grad_key_ref)
        grad_value_ref[...] = jnp.zeros_like(grad_value_ref)

    query = stack_heads(query_ref[...])
    grad = stack_heads(grad_ref[...])
    log_total = log_ref[...].reshape(rows, 1)
    row_segments = row_segment_ref[...]

    def first_pass(index, delta):
        there = pl.ds(pl.multiple_of(index * block, block), block)
        scores = masked_scores(
            query,
            key_ref[there, :],
            row_segments,
            key_segment_ref[:, there],
            step * block,
            index * block,
        )
        probs = jnp.exp(scores - log_total)
        grad_probs = dot(grad, value_ref[there, :], COLUMNS)
        probs_ref[index] = probs
        grad_probs_ref[index] = grad_probs
        grad_value_ref[there, :] += dot(probs.astype(jnp.bfloat16), grad, ROWS)
        return delta + lanes(probs * grad_probs, jnp.add)

    delta = lax.fori_loop(
        first_ref[step], step + 1, first_pass, jnp.zeros((rows, 128), jnp.float32)
    )
    delta = jnp.sum(delta, -1, keepdims=True)

    def second_pass(index, grad_query):
        there = pl.ds(pl.multiple_of(index * block, block), block)
        grad_scores = (probs_ref[index] * (grad_probs_ref[index] - delta)).astype(jnp.bfloat16)
        grad_key_ref[there, :] += dot(grad_scores, query, ROWS)
        return grad_query + dot(grad_scores, key_ref[there, :])

    grad_query = lax.fori_loop(
        first_ref[step], step + 1, second_pass, jnp.zeros((rows, HEAD_SIZE), jnp.float32)
    )
    score_scale = HEAD_SIZE ** (-0.5)
    cosine = jnp.concatenate([cosine_ref[...]] * HEAD_GROUP, 0)
    sine = jnp.concatenate([sine_ref[...]] * HEAD_GROUP, 0)
    grad_query = grad_query * score_scale
    grad_query = grad_query * cosine + turn_back(grad_query * sine)
    grad_query_ref[...] = side_heads(grad_query.astype(jnp.bfloat16))

    @pl.when(step == pl.num_programs(0) - 1)
    def _():
        grad_key = grad_key_ref[...] * score_scale
        grad_key = grad_key * key_cosine_ref[...] + turn_back(grad_key * key_sine_ref[...])
        grad_pair_ref[...] = jnp.concatenate([grad_key, grad_value_ref[...]], 1).astype(
            jnp.bfloat16
        )


def attend_back(query, grad, log_total, cosine, sine, segment_row, key, value, block, first):
    tokens, query_width = query.shape
    steps = tokens // block
    rows = lambda width: pl.BlockSpec((block, width), lambda i, f: (i, 0))
    whole = lambda height, width: pl.BlockSpec((height, width), lambda i, f: (0, 0))
    return pl.pallas_call(
        attend_back_kernel,
        out_shape=(
            jax.ShapeDtypeStruct((tokens, query_width), jnp.bfloat16),
            jax.ShapeDtypeStruct((tokens, 2 * HEAD_SIZE), jnp.bfloat16),
        ),
        grid_spec=pltpu.PrefetchScalarGridSpec(
            num_scalar_prefetch=1,
            grid=(steps,),
            in_specs=[
                rows(query_width),
                rows(query_width),
                pl.BlockSpec((HEAD_GROUP, block, 1), lambda i, f: (0, i, 0)),
                rows(HEAD_SIZE),
                rows(HEAD_SIZE),
                rows(1),
                whole(1, tokens),
                whole(tokens, HEAD_SIZE),
                whole(tokens, HEAD_SIZE),
                whole(tokens, HEAD_SIZE),
                whole(tokens, HEAD_SIZE),
            ],
            out_specs=[rows(query_width), whole(tokens, 2 * HEAD_SIZE)],
            scratch_shapes=[
                pltpu.VMEM((steps, HEAD_GROUP * block, block), jnp.float32),
                pltpu.VMEM((steps, HEAD_GROUP * block, block), jnp.float32),
                pltpu.VMEM((tokens, HEAD_SIZE), jnp.float32),
                pltpu.VMEM((tokens, HEAD_SIZE), jnp.float32),
            ],
        ),
        compiler_params=pltpu.CompilerParams(vmem_limit_bytes=48 << 20),
        cost_estimate=pl.CostEstimate(
            flops=10 * tokens * tokens * query_width,
            bytes_accessed=20 * tokens * query_width,
            transcendentals=tokens * tokens * HEAD_GROUP // 2,
        ),
    )(
        first,
        query,
        grad,
        log_total,
        cosine,
        sine,
        segment_row[:, None],
        segment_row[None, :],
        key,
        value,
        cosine,
        sine,
    )


def after(value, *others):
    return lax.optimization_barrier((value, *others))[0]


def swap(value, bit):
    size = lax.axis_size("rep")
    return lax.ppermute(value, "rep", [(i, i ^ bit) for i in range(size)])


def has(bit):
    return (lax.axis_index("rep") & bit) != 0


def halve(value, bit):
    half = value.shape[0] // 2
    kept = lax.dynamic_slice_in_dim(value, jnp.where(has(bit), half, 0), half, 0)
    sent = lax.dynamic_slice_in_dim(value, jnp.where(has(bit), 0, half), half, 0)
    return kept, sent.astype(jnp.bfloat16)


def join(value, came, bit, axis):
    upper = has(bit)
    return jnp.concatenate(
        [jnp.where(upper, came, value), jnp.where(upper, value, came)], axis
    )


def rep_sum(value, bits):
    for bit in bits:
        value, sent = halve(value, bit)
        value = value.astype(jnp.float32) + swap(sent, bit).astype(jnp.float32)
    value = value.astype(jnp.bfloat16)
    for bit in reversed(bits):
        value = join(value, swap(value, bit), bit, 0)
    return value


def gather_rows(block, bits):
    reps = lax.axis_size("rep")
    share = block.shape[0] // reps
    own = lax.dynamic_slice_in_dim(block, lax.axis_index("rep") * share, share, 0)
    fetched = lax.all_gather(own, "ctx", axis=0)
    size = fetched.shape[0]
    fetched = fetched.reshape((size,) + (1,) * len(bits) + fetched.shape[1:])
    width = fetched.shape[-1] // 2
    halves = []
    for start, order in ((0, bits), (width, bits[::-1])):
        value = fetched[..., start : start + width]
        for bit in order:
            value = join(value, swap(value, bit), bit, len(bits) - (bit.bit_length() - 1))
        halves.append(value.reshape(-1, width))
    return jnp.concatenate(halves, 1)


def per_device(
    inputs,
    segments,
    positions,
    expert_ids,
    attn_gain,
    w_query,
    key_weight,
    value_weight,
    w_out,
    ffn_gain,
    router,
    w_gate,
    w_up,
    w_down,
    grad_out,
):
    size = lax.axis_size("ctx")
    me = lax.axis_index("ctx")
    reps = lax.axis_size("rep")
    bits = [1 << i for i in range(reps.bit_length() - 1)]
    own = inputs.shape[1]
    tokens = size * own
    groups = KEY_VALUE_HEADS
    copies = size // groups
    query_width = HEAD_GROUP * HEAD_SIZE
    width = query_width + 2 * HEAD_SIZE
    copy_index = me % copies
    rows_own = w_out.shape[0]
    experts_own = w_gate.shape[0]
    experts_all = size * experts_own
    slots = expert_ids.shape[2]
    block = min(256, tokens)

    columns = jnp.concatenate(
        [segments[0][:, None], positions[0][:, None] // 64, positions[0][:, None] % 64, expert_ids[0]],
        1,
    ).astype(jnp.bfloat16)
    columns = jnp.pad(columns, ((0, 0), (0, 128 - columns.shape[1])))
    gathered = lax.all_gather(
        jnp.concatenate([inputs[0], columns], 1), "ctx", axis=0, tiled=True
    )
    hidden_low = gathered[:, :MODEL_WIDTH]
    numbers = gathered[:, MODEL_WIDTH:].astype(jnp.int32)
    segment_row = numbers[:, 0]
    position_row = numbers[:, 1] * 64 + numbers[:, 2]
    ids = numbers[:, 3 : 3 + slots]

    head_columns = jnp.concatenate(
        [
            w_query.reshape(rows_own, groups, query_width),
            key_weight.reshape(rows_own, groups, HEAD_SIZE),
            value_weight.reshape(rows_own, groups, HEAD_SIZE),
            jnp.broadcast_to(attn_gain[:, None, None], (rows_own, groups, 1)),
            jnp.broadcast_to(ffn_gain[:, None, None], (rows_own, groups, 1)),
            jnp.broadcast_to(router[:, None, :], (rows_own, groups, router.shape[1])),
        ],
        -1,
    )
    head_columns = jnp.repeat(jnp.transpose(head_columns, (1, 0, 2)), copies, 0)
    head_columns = lax.all_to_all(head_columns, "ctx", split_axis=0, concat_axis=0, tiled=True)
    head_columns = head_columns.reshape(size * rows_own, -1)
    w_heads = head_columns[:, :width]
    gain_one = head_columns[:, width].astype(jnp.float32)
    gain_two = head_columns[:, width + 1].astype(jnp.float32)
    router_all = head_columns[:, width + 2 :]

    live = segment_row != 0
    cosine_table, sine_table = rope_tables(position_row)
    places = jnp.arange(tokens, dtype=jnp.int32)
    starts = segment_row[:: block]
    first = jnp.min(
        jnp.where(segment_row[None, :] == starts[:, None], places[None, :], tokens), 1
    ) // block
    normed_one, query, key, value, mixed, log_total = attend(
        hidden_low, gain_one, w_heads, cosine_table, sine_table, segment_row, block, first
    )
    w_out_all = gather_rows(after(w_out, hidden_low), bits)

    share = tokens // copies
    mixed_all = lax.all_gather(
        lax.dynamic_slice_in_dim(mixed, copy_index * share, share, 0), "ctx", axis=0
    )
    cotangent = lax.all_gather(after(grad_out[0], mixed), "ctx", axis=0, tiled=True)
    mixed_all = jnp.transpose(mixed_all.reshape(groups, tokens, query_width), (1, 0, 2))
    mixed_all = mixed_all.reshape(tokens, QUERY_HEADS * HEAD_SIZE)
    hidden = hidden_low.astype(jnp.float32)
    middle = hidden + dot(mixed_all, w_out_all)
    scale_two = lax.rsqrt(jnp.mean(middle * middle, -1, keepdims=True) + EPS)
    base_two = middle * scale_two
    normed_two = (base_two * gain_two).astype(jnp.bfloat16)

    logits = dot(normed_two, router_all)
    named = jnp.any(ids[:, :, None] == jnp.arange(experts_all, dtype=jnp.int32)[None, None, :], 1)
    top = jnp.max(jnp.where(named, logits, MASK_FLOOR), -1, keepdims=True)
    shifted = jnp.where(named, jnp.exp(jnp.where(named, logits, top) - top), 0.0)
    gates = shifted / jnp.sum(shifted, -1, keepdims=True)
    gates_own = lax.dynamic_slice_in_dim(gates, me * experts_own, experts_own, 1)

    grad_live = jnp.where(live[:, None], cotangent, jnp.zeros((), jnp.bfloat16))
    gate_list = [gates_own[:, e : e + 1] for e in range(experts_own)]
    gate_pre = [dot(normed_two, w_gate[e]) for e in range(experts_own)]
    up_pre = [dot(normed_two, w_up[e]) for e in range(experts_own)]
    sigma = [jax.nn.sigmoid(v) for v in gate_pre]
    acted = [gate_pre[e] * sigma[e] * up_pre[e] for e in range(experts_own)]
    scaled = [(gate_list[e] * acted[e]).astype(jnp.bfloat16) for e in range(experts_own)]
    grad_plain = [dot(grad_live, w_down[e], COLUMNS) for e in range(experts_own)]
    grad_acted = [gate_list[e] * grad_plain[e] for e in range(experts_own)]
    grad_gate_pre = [
        (
            grad_acted[e] * up_pre[e] * (sigma[e] * (1.0 + gate_pre[e] * (1.0 - sigma[e])))
        ).astype(jnp.bfloat16)
        for e in range(experts_own)
    ]
    grad_up_pre = [
        (grad_acted[e] * gate_pre[e] * sigma[e]).astype(jnp.bfloat16) for e in range(experts_own)
    ]

    half = MODEL_WIDTH // 2
    chains = [
        (lambda e: scaled[e], lambda e: grad_live[:, :half], bits),
        (lambda e: scaled[e], lambda e: grad_live[:, half:], bits[::-1]),
        (lambda e: normed_two, lambda e: grad_gate_pre[e], bits),
        (lambda e: normed_two, lambda e: grad_up_pre[e], bits[::-1]),
    ]
    pick = experts_own // 2

    def product(left, right, upper):
        terms = [
            dot(
                jnp.where(upper, left(e + pick), left(e)),
                jnp.where(upper, right(e + pick), right(e)),
                ROWS,
            )
            for e in range(pick)
        ]
        return jnp.concatenate(terms, 0)

    kept, flying = [], []
    for left, right, order in chains:
        sent = product(left, right, jnp.logical_not(has(order[0]))).astype(jnp.bfloat16)
        flying.append(swap(sent, order[0]))

    grad_two_part = 0.0
    for e in range(experts_own):
        grad_two_part = (
            grad_two_part
            + dot(grad_gate_pre[e], w_gate[e], COLUMNS)
            + dot(grad_up_pre[e], w_up[e], COLUMNS)
        )
    expert_index = jnp.arange(experts_all, dtype=jnp.int32)[None, :]
    grad_gates = 0.0
    for e in range(experts_own):
        grad_gates = grad_gates + jnp.where(
            expert_index == me * experts_own + e,
            jnp.sum(acted[e] * grad_plain[e], -1, keepdims=True),
            0.0,
        )
    rough = lax.reduce_precision(grad_gates, 8, 7)
    extra = jnp.concatenate([rough, grad_gates - rough], 1).astype(jnp.bfloat16)
    extra = jnp.pad(extra, ((0, 0), (0, 128 - 2 * experts_all)))
    grad_two_sum = lax.psum_scatter(
        jnp.concatenate([grad_two_part.astype(jnp.bfloat16), extra], 1),
        "ctx",
        scatter_dimension=0,
        tiled=True,
    ).astype(jnp.float32)
    for left, right, order in chains:
        kept.append(product(left, right, has(order[0])))
    moe_part = 0.0
    for e in range(experts_own):
        moe_part = moe_part + dot(scaled[e], w_down[e])

    def mine(array):
        return lax.dynamic_slice_in_dim(array, me * own, own, 0)

    gates_mine = mine(gates)
    grad_gates = (
        grad_two_sum[:, MODEL_WIDTH : MODEL_WIDTH + experts_all]
        + grad_two_sum[:, MODEL_WIDTH + experts_all : MODEL_WIDTH + 2 * experts_all]
    )
    grad_logits = (
        gates_mine * (grad_gates - jnp.sum(gates_mine * grad_gates, -1, keepdims=True))
    ).astype(jnp.bfloat16)
    grad_normed_two = grad_two_sum[:, :MODEL_WIDTH] + dot(grad_logits, router_all, COLUMNS)
    base_two_own = mine(base_two)
    grad_middle = mine(grad_live).astype(jnp.float32) + norm_back(
        grad_normed_two * gain_two, base_two_own, mine(scale_two)
    )
    grad_branch = grad_middle.astype(jnp.bfloat16)
    grad_mixed = dot(grad_branch, w_out_all, COLUMNS).astype(jnp.bfloat16)
    grad_mixed = jnp.transpose(grad_mixed.reshape(own, groups, query_width), (1, 0, 2))
    grad_mixed = jnp.repeat(grad_mixed, copies, 0)
    grad_mixed_all = lax.all_to_all(
        grad_mixed, "ctx", split_axis=0, concat_axis=0, tiled=True
    ).reshape(tokens, query_width)
    grad_branch_all = lax.all_gather(grad_branch, "ctx", axis=0, tiled=True)

    stage = 1
    sent_list = []
    for c, (_, _, order) in enumerate(chains):
        came = after(flying[c], grad_mixed)
        kept[c] = kept[c] + came.astype(jnp.float32)
    while stage < len(bits):
        for c, (_, _, order) in enumerate(chains):
            kept[c], sent = halve(kept[c], order[stage])
            sent_list.append(sent)
            flying[c] = swap(sent, order[stage])
        stage += 1
        if stage < len(bits):
            for c in range(len(chains)):
                kept[c] = kept[c] + flying[c].astype(jnp.float32)

    grad_query, grad_pair = attend_back(
        query,
        after(grad_mixed_all, *sent_list),
        log_total,
        cosine_table,
        sine_table,
        segment_row,
        key,
        value,
        block,
        first,
    )
    if copies > 1:
        counted = (places // share == copy_index)[:, None]
        grad_query = jnp.where(counted, grad_query, jnp.zeros((), jnp.bfloat16))
        grad_pair = jnp.where(counted, grad_pair, jnp.zeros((), jnp.bfloat16))
    grad_one_part = dot(grad_query, w_heads[:, :query_width], COLUMNS) + dot(
        grad_pair, w_heads[:, query_width:], COLUMNS
    )
    grad_one_low = grad_one_part.astype(jnp.bfloat16)
    grad_one = lax.psum_scatter(
        grad_one_low, "ctx", scatter_dimension=0, tiled=True
    ).astype(jnp.float32)
    scale_one = lax.rsqrt(jnp.mean(hidden * hidden, -1, keepdims=True) + EPS)
    gain_one_term = jnp.sum(grad_one_part * (hidden * scale_one), 0)
    gain_two_term = jnp.sum(grad_normed_two * base_two_own, 0)
    head_grads = jnp.concatenate(
        [
            dot(normed_one, grad_query, ROWS),
            dot(normed_one, grad_pair, ROWS),
            gain_one_term[:, None],
            gain_two_term[:, None],
            dot(mine(normed_two), grad_logits, ROWS),
        ],
        1,
    ).astype(jnp.bfloat16)
    head_grads = head_grads.reshape(size, rows_own, -1)
    head_grads_all = lax.all_to_all(
        head_grads, "ctx", split_axis=0, concat_axis=0, tiled=True
    )

    shared = []
    flying_back = []
    for c, (_, _, order) in enumerate(chains):
        came = after(flying[c], grad_one_low, head_grads)
        shared.append((kept[c] + came.astype(jnp.float32)).astype(jnp.bfloat16))
        flying_back.append(swap(shared[c], order[-1]))

    grad_proj_out = dot(
        lax.dynamic_slice_in_dim(mixed, copy_index * rows_own, rows_own, 1), grad_branch_all, ROWS
    )
    small = jnp.sum(head_grads_all[:, :, width:].astype(jnp.float32), 0)
    projections = head_grads_all[:, :, :width]
    if copies > 1:
        projections = jnp.sum(
            projections.reshape(groups, copies, rows_own, width).astype(jnp.float32), 1
        )
    projections = jnp.transpose(projections.astype(jnp.bfloat16), (1, 0, 2))
    query_end = query_width + HEAD_SIZE
    last_one = jnp.concatenate(
        [
            projections[:, :, :query_width].reshape(rows_own, -1),
            projections[:, :, query_width:query_end].reshape(rows_own, -1),
        ],
        1,
    )
    last_two = jnp.concatenate(
        [
            projections[:, :, query_end:].reshape(rows_own, -1),
            grad_proj_out.astype(jnp.bfloat16),
            small.astype(jnp.bfloat16),
        ],
        1,
    )
    for stage in reversed(range(1, len(bits))):
        for c, (_, _, order) in enumerate(chains):
            shared[c] = join(shared[c], after(flying_back[c], last_one), order[stage], 0)
            flying_back[c] = swap(shared[c], order[stage - 1])
    last_one = rep_sum(last_one, bits).astype(jnp.float32)
    last_two = rep_sum(last_two, bits[::-1]).astype(jnp.float32)

    moe_sum = lax.psum_scatter(
        after(moe_part.astype(jnp.bfloat16), grad_branch),
        "ctx",
        scatter_dimension=0,
        tiled=True,
    ).astype(jnp.float32)
    output = jnp.where(mine(live)[:, None], mine(middle) + moe_sum, 0.0).astype(jnp.bfloat16)
    own_hidden = inputs[0].astype(jnp.float32)
    own_scale = lax.rsqrt(jnp.mean(own_hidden * own_hidden, -1, keepdims=True) + EPS)
    grad_in = grad_middle + norm_back(grad_one * gain_one, own_hidden * own_scale, own_scale)

    def whole(c):
        value = join(shared[c], flying_back[c], chains[c][2][0], 0)
        return value.astype(jnp.float32).reshape(experts_own, -1, value.shape[-1])

    grad_down = jnp.concatenate([whole(0), whole(1)], 2)
    kv_all = KEY_VALUE_HEADS * HEAD_SIZE
    query_all = QUERY_HEADS * HEAD_SIZE
    out_end = kv_all + MODEL_WIDTH
    return (
        output[None],
        grad_in[None],
        last_two[:, out_end],
        last_one[:, :query_all],
        last_one[:, query_all:],
        last_two[:, :kv_all],
        last_two[:, kv_all:out_end],
        last_two[:, out_end + 1],
        last_two[:, out_end + 2 :],
        whole(2),
        whole(3),
        grad_down,
    )


def solution(mesh):
    return jax.shard_map(
        per_device,
        mesh=mesh,
        in_specs=(
            P("rep", "ctx", None),
            P("rep", "ctx"),
            P("rep", "ctx"),
            P("rep", "ctx", None),
            P("ctx"),
            P("ctx", None),
            P("ctx", None),
            P("ctx", None),
            P("ctx", None),
            P("ctx"),
            P("ctx", None),
            P("ctx", None, None),
            P("ctx", None, None),
            P("ctx", None, None),
            P("rep", "ctx", None),
        ),
        out_specs=(
            P("rep", "ctx", None),
            P("rep", "ctx", None),
            P("ctx"),
            P("ctx", None),
            P("ctx", None),
            P("ctx", None),
            P("ctx", None),
            P("ctx"),
            P("ctx", None),
            P("ctx", None, None),
            P("ctx", None, None),
            P("ctx", None, None),
        ),
        check_vma=False,
    )
```

time: 1390 us -> 636 us (0.46)
  waiting for transfers between devices: 843 us -> 269 us
  blocking collectives: 221 us -> 0 us
  starting transfers between devices: 16 us -> 46.6 us
  local copies, waits for them, and re-layouts: 105 us -> 76.8 us
  Pallas kernels: 0 us -> 27.6 us
  other arithmetic: 79.1 us -> 95 us
    all_to_all x3, waiting for transfers between devices: 275 us -> 0.01 us  [the longest x1 0.01 us: per_device(): lax.all_to_all(head_columns, 'ctx', split_axis=0, concat_axis=0, tiled=True)]
    psum x1 -> x0, waiting for transfers between devices: 189 us -> none  [replica_sum(): lax.psum(value_block[0].astype(jnp.bfloat16), 'rep').astype(jnp.float32)]
    ppermute x0 -> x28, waiting for transfers between devices: none -> 171 us  [swap(): return lax.ppermute(value, 'rep', [(i, i ^ bit) for i in range(size)])]
    unnamed x17 -> x8, waiting for transfers between devices: 156 us -> 0.13 us
    all_to_all x1 -> x0, blocking collectives: 151 us -> none  [per_device(): lax.all_to_all(send_rows, 'ctx', split_axis=0, concat_axis=0, tiled=True)]
    reduce_scatter x4 -> x3, waiting for transfers between devices: 146 us -> 41.3 us  [the longest x1 41.3 us: per_device(): lax.psum_scatter(jnp.concatenate([grad_two_part.astype(jnp.bfloat16), ext...]
    gather x4 -> x0, local copies, waits for them, and re-layouts: 39.2 us -> none  [the longest x1 12.8 us: per_device(): grad_slots[picked]]
    unnamed x2 -> x0, blocking collectives: 33.3 us -> none
  transfers between devices with their start and end apart: 17 -> 39, of which waited for: 15 -> 17; matrix products, arithmetic and copies ran while one was open for 13% -> 30% of each run, Pallas kernels for 0% -> 4%
where the time goes in v1:
time: 636 us; the launch traced here: 628 us
  waiting for transfers between devices  269 us (42%)
  matrix products  96.6 us (15%)
  other arithmetic  95 us (15%)
  local copies, waits for them, and re-layouts  76.8 us (12%)
  starting transfers between devices  46.6 us (7%)
  Pallas kernels  27.6 us (4%)
  between operations  15.8 us (2%)
    ppermute x28, waiting for transfers between devices, swap(): return lax.ppermute(value, 'rep', [(i, i ^ bit) for i in range(size)])  171 us
    dot_general x30, matrix products, dot(): lax.dot_general(left, right, contract, preferred_element_type=jnp.float32)  96.6 us
    all_gather x1, waiting for transfers between devices, per_device(): lax.all_gather(jnp.concatenate([inputs[0], columns], 1), 'ctx', axis=0, t...  56.7 us
    reduce_scatter x1, waiting for transfers between devices, per_device(): lax.psum_scatter(jnp.concatenate([grad_two_part.astype(jnp.bfloat16), ext...  41.3 us
    ppermute x28, starting transfers between devices, swap(): return lax.ppermute(value, 'rep', [(i, i ^ bit) for i in range(size)])  30.9 us
    unnamed x166, local copies, waits for them, and re-layouts  21.5 us
    select_n x15, other arithmetic, join(): jnp.where(upper, came, value)  20.7 us
    pallas_call x1, Pallas kernels, attend(): pl.pallas_call(attend_kernel, out_shape=(jax.ShapeDtypeStruct((tokens, fe...  14.7 us
  transfers between devices with their start and end apart: 39, of which 17 were waited for; matrix products, arithmetic and copies ran while one was open for 30% of the time, Pallas kernels for 4%

profile of v1, /device:TPU:0, one launch (start us, length us, event | category | flops | bytes accessed | tf_op | source)
XLA Modules:
  0.0 627.6 jit_solution(7895813901915936297)
XLA Ops:
  16.8 6.3 %all-to-all-start = ((bf16[8,192,338]{2,1,0:T(8,128)(2,1)}), bf16[8,192,338]{2,1,0:T(8,128)(2,1)S(1)}, u32[]{:S(2)}, u32[]{:S(2)}) async-start(bf16[8,192,338]{2,1,0:T(8,128)(2,1)} %bitcast.6), calls=%async_computation | async-start | bytes 2359296 | tf_op jit(solution)/shard_map/all_to_all | solution.py:466
  23.1 56.7 %all-gather.8.cloned.1.call-done = bf16[1024,1664]{1,0:T(8,128)(2,1)} async-done(((bf16[128,1664]{1,0:T(8,128)(2,1)}), bf16[1024,1664]{1,0:T(8,128)(2,1)}) %all-gather.8.cloned.1.call-update) | async-done | bytes 3407888 | tf_op jit(solution)/shard_map/all_gather | solution.py:445
  79.9 3.8 slice.176.hidden_ref
  89.3 14.7 %shard_map.238 = (bf16[1024,1536]{1,0:T(8,128)(2,1)}, bf16[1024,192]{1,0:T(8,128)(2,1)S(1)}, bf16[1024,64]{1,0:T(8,128)(2,1)S(1)}, bf16[1024,64]{1,0:T(8,128)(2,...) custom-call(s32[4]{0:T(128)S(1)} %and_select_fusion.first_ref, bf16[1024,1536]{1,0:T(8,128)(2,1)} %slice.176.hidden_ref, ...), custom_call_target="tpu_custom_call" | custom-call | flops 1811939328 | bytes 7274496 | tf_op jit(solution)/shard_map/pallas_call | solution.py:164
  111.3 12.7 %collective-permute-done = bf16[8,1,1,48,768]{4,3,2,1,0:T(8,128)(2,1)S(1)} collective-permute-done((bf16[8,1,1,48,768]{4,3,2,1,0:T(8,128)(2,1)}, bf16[8,1,1,48,768]{4,3,2,1,0:T(8,128)(2,1)S(1)}, u32[]{:S(2)}, u32[]{:S(2)}) %collective-permute-start) | collective-permute-done | bytes 589856 | tf_op jit(solution)/shard_map/ppermute | solution.py:358
  135.9 20.8 %collective-permute-done.1 = bf16[8,1,2,48,768]{4,3,2,1,0:T(8,128)(2,1)} collective-permute-done((bf16[8,1,2,48,768]{4,3,2,1,0:T(8,128)(2,1)}, bf16[8,1,2,48,768]{4,3,2,1,0:T(8,128)(2,1)}, u32[]{:S(2)}, u32[]{:S(2)}) %collective-permute-start.1) | collective-permute-done | bytes 1179680 | tf_op jit(solution)/shard_map/ppermute | solution.py:358
  163.2 6.4 %copy.181 = bf16[8,1024,192]{1,2,0:T(8,128)(2,1)} copy(bf16[8,1024,192]{2,1,0:T(8,128)(2,1)} %bitcast.139) | data formatting | bytes 6291456 | tf_op jit(solution)/shard_map/all_gather | solution.py:486
  169.6 10.2 %multiply_reduce_fusion = (f32[1024]{0:T(1024)S(1)}, f32[1024,1536]{1,0:T(8,128)S(1)}) fusion(bf16[1024,1536]{0,1:T(8,128)(2,1)} %bitcast.140, bf16[1536,768]{1,0:T(8,128)(2,1)} %bitcast.144, bf16[1536,768]{1,0:T(8,128)(2,1)} %bitcast.142, bf16[1024,1664]{1,0:T(8,128)(2,1)} %all-gather.8.cloned.1.call-done), kind=kOutput, calls=%fused_computation.9 | convolution fusion | flops 4847565824 | bytes 17305600 | tf_op jit(solution)/shard_map/dot_general | solution.py:23
  179.8 3.9 multiply_convert_fusion
  187.4 3.2 fusion.9
  190.6 3.2 fusion.21
  196.7 3.2 fusion.5
  199.9 3.1 fusion.15
  203.0 10.6 %copy.184 = f32[1024,16]{1,0:T(8,128)S(1)} copy(f32[1024,16]{0,1:T(8,128)S(1)} %get-tuple-element.213) | data formatting | bytes 131072 | tf_op jit(solution)/shard_map/dot_general | solution.py:23
  215.2 7.1 %multiply_convert_fusion.2 = (bf16[1024,512]{0,1:T(8,128)(2,1)S(1)}, f32[1024]{0:T(1024)S(1)}, bf16[1024,512]{0,1:T(8,128)(2,1)S(1)}, bf16[1024,512]{0,1:T(8,128)(2,1)}) fusion(f32[1024,512]{0,1:T(8,128)} %fusion.9, f32[1024,512]{0,1:T(8,128)S(1)} %copy-done.79, f32[1024]{0:T(1024)S(1)} %get-tuple-element.150, bf16[1024,1536]{1,0:T(8,128)(2,1)} %copy-done.13, ...), kind=kOutput, calls=%fused_computation.34 | convolution fusion | flops 1621097472 | bytes 12066816 | tf_op jit(solution)/shard_map/dot_general | solution.py:23
  226.2 4.0 multiply_convert_fusion.4
  232.2 4.6 fusion.23
  237.3 5.6 add_convert_fusion
  245.0 41.3 %reduce-scatter.4.cloned.1.call-done = bf16[128,1664]{1,0:T(8,128)(2,1)} async-done(((bf16[1024,1664]{1,0:T(8,128)(2,1)}), bf16[128,1664]{1,0:T(8,128)(2,1)}) %reduce-scatter.4.cloned.1.call-update) | async-done | bytes 426000 | tf_op jit(solution)/shard_map/reduce_scatter | solution.py:567
  295.9 3.1 convolution_convert_fusion
  301.8 3.1 convolution_convert_fusion.1
  315.0 3.6 fusion.46
  318.7 3.8 fusion.49
  322.4 3.7 add_convert_fusion.1
  326.2 3.9 fusion.31
  332.3 4.0 fusion.4
  337.2 3.5 all-to-all-start.1
  342.6 8.6 %collective-permute-done.5 = bf16[512,768]{1,0:T(8,128)(2,1)} collective-permute-done((bf16[512,768]{1,0:T(8,128)(2,1)}, bf16[512,768]{1,0:T(8,128)(2,1)}, u32[]{:S(2)}, u32[]{:S(2)}) %collective-permute-start.5) | collective-permute-done | bytes 786464 | tf_op jit(solution)/shard_map/ppermute | solution.py:358
  351.2 4.6 collective-permute-done.4
  378.8 12.9 %shard_map.239 = (bf16[1024,192]{1,0:T(8,128)(2,1)S(1)}, bf16[1024,128]{1,0:T(8,128)(2,1)S(1)}) custom-call(s32[4]{0:T(128)S(1)} %and_select_fusion.first_ref, bf16[1024,192]{1,0:T(8,128)(2,1)S(1)} %copy-done.9, bf16[1024,192]{1,0:T(8,128)(2,1)S(1)} %bitcast.129, f32[3,1024,1]{2,1,0:T(8,128)S(1)} %copy-done.7, f32[1024,64]{1,0:T(8,128)S(1)} %copy-done.3, ...), custom_call_target="tpu_custom_call" | custom-call | flops 2013265920 | bytes 3932160 | tf_op jit(solution)/shard_map/pallas_call | solution.py:300
  397.6 2.9 fusion.2
  401.3 3.0 convolution_convert_fusion.4
  406.6 5.2 all-to-all-start.2
  417.9 6.9 %collective-permute-done.22 = bf16[256,768]{1,0:T(8,128)(2,1)S(1)} collective-permute-done((bf16[256,768]{1,0:T(8,128)(2,1)}, bf16[256,768]{1,0:T(8,128)(2,1)S(1)}, u32[]{:S(2)}, u32[]{:S(2)}) %collective-permute-start.22) | collective-permute-done | bytes 393248 | tf_op jit(solution)/shard_map/ppermute | solution.py:358
  428.8 14.3 %collective-permute-done.25 = bf16[256,768]{1,0:T(8,128)(2,1)} collective-permute-done((bf16[256,768]{1,0:T(8,128)(2,1)}, bf16[256,768]{1,0:T(8,128)(2,1)}, u32[]{:S(2)}, u32[]{:S(2)}) %collective-permute-start.25) | collective-permute-done | bytes 393248 | tf_op jit(solution)/shard_map/ppermute | solution.py:358
  445.2 2.9 add_convert_fusion.2
  463.7 10.4 %collective-permute-done.20 = bf16[768,512]{1,0:T(8,128)(2,1)} collective-permute-done((bf16[768,512]{1,0:T(8,128)(2,1)}, bf16[768,512]{1,0:T(8,128)(2,1)}, u32[]{:S(2)}, u32[]{:S(2)}) %collective-permute-start.20) | collective-permute-done | bytes 786464 | tf_op jit(solution)/shard_map/ppermute | solution.py:358
  477.5 20.0 %collective-permute-done.12 = bf16[96,2048]{1,0:T(8,128)(2,1)S(1)} collective-permute-done((bf16[96,2048]{1,0:T(8,128)(2,1)S(1)}, bf16[96,2048]{1,0:T(8,128)(2,1)S(1)}, u32[]{:S(2)}, u32[]{:S(2)}) %collective-permute-start.12) | collective-permute-done | bytes 393248 | tf_op jit(solution)/shard_map/ppermute | solution.py:358
  499.9 25.5 %collective-permute-done.13 = bf16[48,2048]{1,0:T(8,128)(2,1)S(1)} collective-permute-done((bf16[48,2048]{1,0:T(8,128)(2,1)S(1)}, bf16[48,2048]{1,0:T(8,128)(2,1)S(1)}, u32[]{:S(2)}, u32[]{:S(2)}) %collective-permute-start.13) | collective-permute-done | bytes 196640 | tf_op jit(solution)/shard_map/ppermute | solution.py:358
  538.8 3.6 maximum_convert_fusion
  542.4 27.9 %collective-permute-done.15 = bf16[96,2048]{1,0:T(8,128)(2,1)S(1)} collective-permute-done((bf16[96,2048]{1,0:T(8,128)(2,1)S(1)}, bf16[96,2048]{1,0:T(8,128)(2,1)S(1)}, u32[]{:S(2)}, u32[]{:S(2)}) %collective-permute-start.15) | collective-permute-done | bytes 393248 | tf_op jit(solution)/shard_map/ppermute | solution.py:358
  572.5 3.7 broadcast_select_fusion.2
  576.2 2.9 convolution_convert_fusion.2
  582.6 5.2 collective-permute-done.8
  589.2 6.8 %collective-permute-done.9 = bf16[48,2066]{1,0:T(8,128)(2,1)S(1)} collective-permute-done((bf16[48,2066]{1,0:T(8,128)(2,1)S(1)}, bf16[48,2066]{1,0:T(8,128)(2,1)S(1)}, u32[]{:S(2)}, u32[]{:S(2)}) %collective-permute-start.9) | collective-permute-done | bytes 198368 | tf_op jit(solution)/shard_map/ppermute | solution.py:358
  597.2 3.6 convert.61
  600.8 3.6 convert.60
  607.7 5.0 collective-permute-done.11
  (375 shorter events, 182.3 us)
Async XLA Ops:
  7.2 76.4 %copy-start = (bf16[192,1536]{1,0:T(8,128)(2,1)S(1)}, bf16[192,1536]{1,0:T(8,128)(2,1)}, u32[]{:S(2)}) copy-start(bf16[192,1536]{1,0:T(8,128)(2,1)} %param.23) | copy-start | bytes 1769476
  7.2 72.7 %all-gather.8.cloned.1.call-start = ((), (), s32[]{:S(2)}) async-start(), calls=%async_computation.6 | async-start | bytes 3833856 | tf_op jit(solution)/shard_map/all_gather | solution.py:445
  16.8 67.6 %all-to-all-start = ((bf16[8,192,338]{2,1,0:T(8,128)(2,1)}), bf16[8,192,338]{2,1,0:T(8,128)(2,1)S(1)}, u32[]{:S(2)}, u32[]{:S(2)}) async-start(bf16[8,192,338]{2,1,0:T(8,128)(2,1)} %bitcast.6), calls=%async_computation | async-start | bytes 2359296 | tf_op jit(solution)/shard_map/all_to_all | solution.py:466
  23.1 82.9 %all-gather.16.cloned.1.call-start = ((), (), s32[]{:S(2)}) async-start(), calls=%async_computation.13 | async-start | bytes 1327104 | tf_op jit(solution)/shard_map/all_gather | solution.py:393
  84.3 78.9 %all-gather.14.cloned.1.call-start = ((), (), s32[]{:S(2)}) async-start(), calls=%async_computation.12 | async-start | bytes 4718592 | tf_op jit(solution)/shard_map/all_gather | solution.py:486
  89.2 14.7 %copy-start.2 = (f32[1024,64]{1,0:T(8,128)}, f32[1024,64]{1,0:T(8,128)S(1)}, u32[]{:S(2)}) copy-start(f32[1024,64]{1,0:T(8,128)S(1)} %get-tuple-element.216.cosine_ref.key_cosine_ref) | copy-start | bytes 786436
  89.2 14.7 %copy-start.4 = (f32[1024,64]{1,0:T(8,128)}, f32[1024,64]{1,0:T(8,128)S(1)}, u32[]{:S(2)}) copy-start(f32[1024,64]{1,0:T(8,128)S(1)} %get-tuple-element.217.sine_ref.key_sine_ref) | copy-start | bytes 786436
  105.9 21.1 %copy-start.10 = (bf16[1024,64]{1,0:T(8,128)(2,1)}, bf16[1024,64]{1,0:T(8,128)(2,1)S(1)}, u32[]{:S(2)}) copy-start(bf16[1024,64]{1,0:T(8,128)(2,1)S(1)} %get-tuple-element.48.value_ref) | copy-start | bytes 393220
  105.9 87.9 %all-gather.10.cloned.1.call-start = ((), (), s32[]{:S(2)}) async-start(), calls=%async_computation.7 | async-start | bytes 3538944 | tf_op jit(solution)/shard_map/all_gather | solution.py:489
  108.3 15.7 %collective-permute-start = (bf16[8,1,1,48,768]{4,3,2,1,0:T(8,128)(2,1)}, bf16[8,1,1,48,768]{4,3,2,1,0:T(8,128)(2,1)S(1)}, u32[]{:S(2)}, u32[]{:S(2)}) collective-permute-start(bf16[8,1,1,48,768]{4,3,2,1,0:T(8,128)(2,1)} %get-tuple-element.188), channel_id=1, source_target_pairs={{0,8},{8,0},{16,24},{24,16},{1,9},{9,1},{17,25},{25,17},{2,10},{10... | collective-permute-start | bytes 1769480 | tf_op jit(solution)/shard_map/ppermute | solution.py:358
  109.7 15.5 %collective-permute-start.2 = (bf16[8,1,1,48,768]{4,3,2,1,0:T(8,128)(2,1)}, bf16[8,1,1,48,768]{4,3,2,1,0:T(8,128)(2,1)}, u32[]{:S(2)}, u32[]{:S(2)}) collective-permute-start(bf16[8,1,1,48,768]{4,3,2,1,0:T(8,128)(2,1)} %get-tuple-element.189), channel_id=1, source_target_pairs={{0,16},{8,24},{16,0},{24,8},{1,17},{9,25},{17,1},{25,9},{2,18},{10... | collective-permute-start | bytes 1769480 | tf_op jit(solution)/shard_map/ppermute | solution.py:358
  128.4 28.4 %collective-permute-start.1 = (bf16[8,1,2,48,768]{4,3,2,1,0:T(8,128)(2,1)}, bf16[8,1,2,48,768]{4,3,2,1,0:T(8,128)(2,1)}, u32[]{:S(2)}, u32[]{:S(2)}) collective-permute-start(bf16[8,1,2,48,768]{4,3,2,1,0:T(8,128)(2,1)} %pad_maximum_fusion.15), channel_id=1, source_target_pairs={{0,16},{8,24},{16,0},{24,8},{1,17},{9,25},{17,1},{25,9},{2,18},{10... | collective-permute-start | bytes 3538952 | tf_op jit(solution)/shard_map/ppermute | solution.py:358
  131.9 28.2 %collective-permute-start.3 = (bf16[8,2,1,48,768]{4,3,2,1,0:T(8,128)(2,1)}, bf16[8,2,1,48,768]{4,3,2,1,0:T(8,128)(2,1)}, u32[]{:S(2)}, u32[]{:S(2)}) collective-permute-start(bf16[8,2,1,48,768]{4,3,2,1,0:T(8,128)(2,1)} %pad_maximum_fusion.16), channel_id=1, source_target_pairs={{0,8},{8,0},{16,24},{24,16},{1,9},{9,1},{17,25},{25,17},{2,10},{10... | collective-permute-start | bytes 3538952 | tf_op jit(solution)/shard_map/ppermute | solution.py:358
  133.1 153.3 %reduce-scatter.4.cloned.1.call-start = ((), (), s32[]{:S(2)}) async-start(), calls=%async_computation.8 | async-start | bytes 3833856 | tf_op jit(solution)/shard_map/reduce_scatter | solution.py:567
  222.3 14.9 %copy-start.51 = (bf16[1024,512]{0,1:T(8,128)(2,1)}, bf16[1024,512]{0,1:T(8,128)(2,1)S(1)}, u32[]{:S(2)}) copy-start(bf16[1024,512]{0,1:T(8,128)(2,1)S(1)} %get-tuple-element.160) | copy-start | bytes 3145732
  244.9 331.3 %all-gather.12.cloned.1.call-start = ((), (), s32[]{:S(2)}) async-start(), calls=%async_computation.11 | async-start | bytes 3538944 | tf_op jit(solution)/shard_map/all_gather | solution.py:602
  292.6 313.0 %reduce-scatter.6.cloned.1.call-start = ((), (), s32[]{:S(2)}) async-start(), calls=%async_computation.9 | async-start | bytes 3538944 | tf_op jit(solution)/shard_map/reduce_scatter | solution.py:700
  299.0 41.7 %collective-permute-start.7 = (bf16[1536,512]{1,0:T(8,128)(2,1)}, bf16[1536,512]{1,0:T(8,128)(2,1)}, u32[]{:S(2)}, u32[]{:S(2)}) collective-permute-start(bf16[1536,512]{1,0:T(8,128)(2,1)} %convolution_convert_fusion), channel_id=1, source_target_pairs={{0,16},{8,24},{16,0},{24,8},{1,17},{9,25},{17,1},{25,9},{2,18},{10... | collective-permute-start | bytes 4718600 | tf_op jit(solution)/shard_map/ppermute | solution.py:358
  305.0 37.6 %collective-permute-start.6 = (bf16[1536,512]{1,0:T(8,128)(2,1)}, bf16[1536,512]{1,0:T(8,128)(2,1)}, u32[]{:S(2)}, u32[]{:S(2)}) collective-permute-start(bf16[1536,512]{1,0:T(8,128)(2,1)} %convolution_convert_fusion.1), channel_id=1, source_target_pairs={{0,8},{8,0},{16,24},{24,16},{1,9},{9,1},{17,25},{25,17},{2,10},{10... | collective-permute-start | bytes 4718600 | tf_op jit(solution)/shard_map/ppermute | solution.py:358
  308.3 42.9 %collective-permute-start.5 = (bf16[512,768]{1,0:T(8,128)(2,1)}, bf16[512,768]{1,0:T(8,128)(2,1)}, u32[]{:S(2)}, u32[]{:S(2)}) collective-permute-start(bf16[512,768]{1,0:T(8,128)(2,1)} %convolution_convert_fusion.6), channel_id=1, source_target_pairs={{0,16},{8,24},{16,0},{24,8},{1,17},{9,25},{17,1},{25,9},{2,18},{10... | collective-permute-start | bytes 2359304 | tf_op jit(solution)/shard_map/ppermute | solution.py:358
  310.3 45.5 %collective-permute-start.4 = (bf16[512,768]{1,0:T(8,128)(2,1)}, bf16[512,768]{1,0:T(8,128)(2,1)}, u32[]{:S(2)}, u32[]{:S(2)}) collective-permute-start(bf16[512,768]{1,0:T(8,128)(2,1)} %convolution_convert_fusion.7), channel_id=1, source_target_pairs={{0,8},{8,0},{16,24},{24,16},{1,9},{9,1},{17,25},{25,17},{2,10},{10... | collective-permute-start | bytes 2359304 | tf_op jit(solution)/shard_map/ppermute | solution.py:358
  337.2 35.8 %all-to-all-start.1 = ((bf16[8,128,192]{1,2,0:T(8,128)(2,1)}), bf16[8,128,192]{1,2,0:T(8,128)(2,1)S(1)}, u32[]{:S(2)}, u32[]{:S(2)}) async-start(bf16[8,128,192]{1,2,0:T(8,128)(2,1)} %bitcast.23), calls=%async_computation.3 | async-start | bytes 786432 | tf_op jit(solution)/shard_map/all_to_all | solution.py:599
  378.8 13.0 %copy-start.27 = (bf16[1024,1536]{1,0:T(8,128)(2,1)S(1)}, bf16[1024,1536]{1,0:T(8,128)(2,1)}, u32[]{:S(2)}) copy-start(bf16[1024,1536]{1,0:T(8,128)(2,1)} %get-tuple-element.51) | copy-start | bytes 9437188
  406.6 36.4 %copy-start.35 = (f32[512,768]{1,0:T(8,128)S(1)}, f32[512,768]{1,0:T(8,128)}, u32[]{:S(2)}) copy-start(f32[512,768]{1,0:T(8,128)} %copy-done.34) | copy-start | bytes 4718596
  406.6 45.9 %all-to-all-start.2 = ((bf16[8,192,338]{2,1,0:T(8,128)(2,1)}), bf16[8,192,338]{2,1,0:T(8,128)(2,1)S(1)}, u32[]{:S(2)}, u32[]{:S(2)}) async-start(bf16[8,192,338]{2,1,0:T(8,128)(2,1)} %concatenate.118), calls=%async_computation.5 | async-start | bytes 2359296 | tf_op jit(solution)/shard_map/all_to_all | solution.py:656
  411.8 204.6 %reduce-scatter.8.cloned.1.call-start = ((), (), s32[]{:S(2)}) async-start(), calls=%async_computation.10 | async-start | bytes 3538944 | tf_op jit(solution)/shard_map/reduce_scatter | solution.py:639
  412.0 12.8 %collective-permute-start.22 = (bf16[256,768]{1,0:T(8,128)(2,1)}, bf16[256,768]{1,0:T(8,128)(2,1)S(1)}, u32[]{:S(2)}, u32[]{:S(2)}) collective-permute-start(bf16[256,768]{1,0:T(8,128)(2,1)} %dynamic-slice_convert_fusion.3), channel_id=1, source_target_pairs={{0,16},{8,24},{16,0},{24,8},{1,17},{9,25},{17,1},{25,9},{2,18},{10... | collective-permute-start | bytes 1179656 | tf_op jit(solution)/shard_map/ppermute | solution.py:358
  414.6 30.5 %collective-permute-start.19 = (bf16[768,512]{1,0:T(8,128)(2,1)}, bf16[768,512]{1,0:T(8,128)(2,1)}, u32[]{:S(2)}, u32[]{:S(2)}) collective-permute-start(bf16[768,512]{1,0:T(8,128)(2,1)} %dynamic-slice_convert_fusion), channel_id=1, source_target_pairs={{0,8},{8,0},{16,24},{24,16},{1,9},{9,1},{17,25},{25,17},{2,10},{10... | collective-permute-start | bytes 2359304 | tf_op jit(solution)/shard_map/ppermute | solution.py:358
  415.2 27.8 %collective-permute-start.25 = (bf16[256,768]{1,0:T(8,128)(2,1)}, bf16[256,768]{1,0:T(8,128)(2,1)}, u32[]{:S(2)}, u32[]{:S(2)}) collective-permute-start(bf16[256,768]{1,0:T(8,128)(2,1)} %dynamic-slice_convert_fusion.2), channel_id=1, source_target_pairs={{0,8},{8,0},{16,24},{24,16},{1,9},{9,1},{17,25},{25,17},{2,10},{10... | collective-permute-start | bytes 1179656 | tf_op jit(solution)/shard_map/ppermute | solution.py:358
  417.2 32.6 %collective-permute-start.16 = (bf16[768,512]{1,0:T(8,128)(2,1)}, bf16[768,512]{1,0:T(8,128)(2,1)}, u32[]{:S(2)}, u32[]{:S(2)}) collective-permute-start(bf16[768,512]{1,0:T(8,128)(2,1)} %dynamic-slice_convert_fusion.1), channel_id=1, source_target_pairs={{0,16},{8,24},{16,0},{24,8},{1,17},{9,25},{17,1},{25,9},{2,18},{10... | collective-permute-start | bytes 2359304 | tf_op jit(solution)/shard_map/ppermute | solution.py:358
  426.8 30.5 %collective-permute-start.23 = (bf16[256,768]{1,0:T(8,128)(2,1)}, bf16[256,768]{1,0:T(8,128)(2,1)}, u32[]{:S(2)}, u32[]{:S(2)}) collective-permute-start(bf16[256,768]{1,0:T(8,128)(2,1)} %add_convert_fusion.5), channel_id=1, source_target_pairs={{0,16},{8,24},{16,0},{24,8},{1,17},{9,25},{17,1},{25,9},{2,18},{10... | collective-permute-start | bytes 1179656 | tf_op jit(solution)/shard_map/ppermute | solution.py:358
  444.8 15.0 %collective-permute-start.26 = (bf16[256,768]{1,0:T(8,128)(2,1)}, bf16[256,768]{1,0:T(8,128)(2,1)}, u32[]{:S(2)}, u32[]{:S(2)}) collective-permute-start(bf16[256,768]{1,0:T(8,128)(2,1)} %add_convert_fusion.4), channel_id=1, source_target_pairs={{0,8},{8,0},{16,24},{24,16},{1,9},{9,1},{17,25},{25,17},{2,10},{10... | collective-permute-start | bytes 1179656 | tf_op jit(solution)/shard_map/ppermute | solution.py:358
  448.1 25.9 %collective-permute-start.20 = (bf16[768,512]{1,0:T(8,128)(2,1)}, bf16[768,512]{1,0:T(8,128)(2,1)}, u32[]{:S(2)}, u32[]{:S(2)}) collective-permute-start(bf16[768,512]{1,0:T(8,128)(2,1)} %add_convert_fusion.2), channel_id=1, source_target_pairs={{0,8},{8,0},{16,24},{24,16},{1,9},{9,1},{17,25},{25,17},{2,10},{10... | collective-permute-start | bytes 2359304 | tf_op jit(solution)/shard_map/ppermute | solution.py:358
  452.2 25.3 %collective-permute-start.17 = (bf16[768,512]{1,0:T(8,128)(2,1)}, bf16[768,512]{1,0:T(8,128)(2,1)}, u32[]{:S(2)}, u32[]{:S(2)}) collective-permute-start(bf16[768,512]{1,0:T(8,128)(2,1)} %add_convert_fusion.3), channel_id=1, source_target_pairs={{0,16},{8,24},{16,0},{24,8},{1,17},{9,25},{17,1},{25,9},{2,18},{10... | collective-permute-start | bytes 2359304 | tf_op jit(solution)/shard_map/ppermute | solution.py:358
  459.5 75.9 %collective-permute-start.24 = (bf16[512,768]{1,0:T(8,128)(2,1)}, bf16[512,768]{1,0:T(8,128)(2,1)}, u32[]{:S(2)}, u32[]{:S(2)}) collective-permute-start(bf16[512,768]{1,0:T(8,128)(2,1)} %pad_maximum_fusion.18), channel_id=1, source_target_pairs={{0,8},{8,0},{16,24},{24,16},{1,9},{9,1},{17,25},{25,17},{2,10},{10... | collective-permute-start | bytes 2359304 | tf_op jit(solution)/shard_map/ppermute | solution.py:358
  461.0 13.1 %copy-start.39 = (bf16[256,768]{1,0:T(8,128)(2,1)}, bf16[256,768]{1,0:T(8,128)(2,1)S(1)}, u32[]{:S(2)}) copy-start(bf16[256,768]{1,0:T(8,128)(2,1)S(1)} %get-tuple-element.194) | copy-start | bytes 1179652
  461.0 13.1 %copy-start.41 = (bf16[256,768]{1,0:T(8,128)(2,1)}, bf16[256,768]{1,0:T(8,128)(2,1)S(1)}, u32[]{:S(2)}) copy-start(bf16[256,768]{1,0:T(8,128)(2,1)S(1)} %get-tuple-element.195) | copy-start | bytes 1179652
  462.0 75.1 %collective-permute-start.27 = (bf16[512,768]{1,0:T(8,128)(2,1)}, bf16[512,768]{1,0:T(8,128)(2,1)}, u32[]{:S(2)}, u32[]{:S(2)}) collective-permute-start(bf16[512,768]{1,0:T(8,128)(2,1)} %pad_maximum_fusion.19), channel_id=1, source_target_pairs={{0,16},{8,24},{16,0},{24,8},{1,17},{9,25},{17,1},{25,9},{2,18},{10... | collective-permute-start | bytes 2359304 | tf_op jit(solution)/shard_map/ppermute | solution.py:358
  474.1 23.4 %collective-permute-start.12 = (bf16[96,2048]{1,0:T(8,128)(2,1)S(1)}, bf16[96,2048]{1,0:T(8,128)(2,1)S(1)}, u32[]{:S(2)}, u32[]{:S(2)}) collective-permute-start(bf16[96,2048]{1,0:T(8,128)(2,1)S(1)} %fusion.83), channel_id=1, source_target_pairs={{0,8},{8,0},{16,24},{24,16},{1,9},{9,1},{17,25},{25,17},{2,10},{10... | collective-permute-start | bytes 1179656 | tf_op jit(solution)/shard_map/ppermute | solution.py:358
  477.2 95.4 %collective-permute-start.21 = (bf16[1536,512]{1,0:T(8,128)(2,1)}, bf16[1536,512]{1,0:T(8,128)(2,1)}, u32[]{:S(2)}, u32[]{:S(2)}) collective-permute-start(bf16[1536,512]{1,0:T(8,128)(2,1)} %pad_maximum_fusion.11), channel_id=1, source_target_pairs={{0,16},{8,24},{16,0},{24,8},{1,17},{9,25},{17,1},{25,9},{2,18},{10... | collective-permute-start | bytes 4718600 | tf_op jit(solution)/shard_map/ppermute | solution.py:358
  497.7 27.7 %collective-permute-start.13 = (bf16[48,2048]{1,0:T(8,128)(2,1)S(1)}, bf16[48,2048]{1,0:T(8,128)(2,1)S(1)}, u32[]{:S(2)}, u32[]{:S(2)}) collective-permute-start(bf16[48,2048]{1,0:T(8,128)(2,1)S(1)} %dynamic-slice_convert_fusion.5), channel_id=1, source_target_pairs={{0,16},{8,24},{16,0},{24,8},{1,17},{9,25},{17,1},{25,9},{2,18},{10... | collective-permute-start | bytes 589832 | tf_op jit(solution)/shard_map/ppermute | solution.py:358
  525.5 7.3 %collective-permute-start.14 = (bf16[48,2048]{1,0:T(8,128)(2,1)S(1)}, bf16[48,2048]{1,0:T(8,128)(2,1)}, u32[]{:S(2)}, u32[]{:S(2)}) collective-permute-start(bf16[48,2048]{1,0:T(8,128)(2,1)S(1)} %add_convert_fusion.7), channel_id=1, source_target_pairs={{0,16},{8,24},{16,0},{24,8},{1,17},{9,25},{17,1},{25,9},{2,18},{10... | collective-permute-start | bytes 589832 | tf_op jit(solution)/shard_map/ppermute | solution.py:358
  527.4 53.0 %collective-permute-start.18 = (bf16[1536,512]{1,0:T(8,128)(2,1)}, bf16[1536,512]{1,0:T(8,128)(2,1)}, u32[]{:S(2)}, u32[]{:S(2)}) collective-permute-start(bf16[1536,512]{1,0:T(8,128)(2,1)} %pad_maximum_fusion.10), channel_id=1, source_target_pairs={{0,8},{8,0},{16,24},{24,16},{1,9},{9,1},{17,25},{25,17},{2,10},{10... | collective-permute-start | bytes 4718600 | tf_op jit(solution)/shard_map/ppermute | solution.py:358
  533.9 36.4 %collective-permute-start.15 = (bf16[96,2048]{1,0:T(8,128)(2,1)S(1)}, bf16[96,2048]{1,0:T(8,128)(2,1)S(1)}, u32[]{:S(2)}, u32[]{:S(2)}) collective-permute-start(bf16[96,2048]{1,0:T(8,128)(2,1)S(1)} %pad_maximum_fusion.23), channel_id=1, source_target_pairs={{0,8},{8,0},{16,24},{24,16},{1,9},{9,1},{17,25},{25,17},{2,10},{10... | collective-permute-start | bytes 1179656 | tf_op jit(solution)/shard_map/ppermute | solution.py:358
  579.2 8.6 %collective-permute-start.8 = (bf16[96,2066]{1,0:T(8,128)(2,1)S(1)}, bf16[96,2066]{1,0:T(8,128)(2,1)S(1)}, u32[]{:S(2)}, u32[]{:S(2)}) collective-permute-start(bf16[96,2066]{1,0:T(8,128)(2,1)S(1)} %constant_dynamic-slice_fusion), channel_id=1, source_target_pairs={{0,16},{8,24},{16,0},{24,8},{1,17},{9,25},{17,1},{25,9},{2,18},{10... | collective-permute-start | bytes 1190024 | tf_op jit(solution)/shard_map/ppermute | solution.py:358
  588.0 8.0 %collective-permute-start.9 = (bf16[48,2066]{1,0:T(8,128)(2,1)S(1)}, bf16[48,2066]{1,0:T(8,128)(2,1)S(1)}, u32[]{:S(2)}, u32[]{:S(2)}) collective-permute-start(bf16[48,2066]{1,0:T(8,128)(2,1)S(1)} %dynamic-slice_convert_fusion.4), channel_id=1, source_target_pairs={{0,8},{8,0},{16,24},{24,16},{1,9},{9,1},{17,25},{25,17},{2,10},{10... | collective-permute-start | bytes 595016 | tf_op jit(solution)/shard_map/ppermute | solution.py:358
  596.0 8.5 %collective-permute-start.10 = (bf16[48,2066]{1,0:T(8,128)(2,1)S(1)}, bf16[48,2066]{1,0:T(8,128)(2,1)S(1)}, u32[]{:S(2)}, u32[]{:S(2)}) collective-permute-start(bf16[48,2066]{1,0:T(8,128)(2,1)S(1)} %add_convert_fusion.6), channel_id=1, source_target_pairs={{0,8},{8,0},{16,24},{24,16},{1,9},{9,1},{17,25},{25,17},{2,10},{10... | collective-permute-start | bytes 595016 | tf_op jit(solution)/shard_map/ppermute | solution.py:358
  604.5 8.1 %collective-permute-start.11 = (bf16[96,2066]{1,0:T(8,128)(2,1)S(1)}, bf16[96,2066]{1,0:T(8,128)(2,1)S(1)}, u32[]{:S(2)}, u32[]{:S(2)}) collective-permute-start(bf16[96,2066]{1,0:T(8,128)(2,1)S(1)} %pad_maximum_fusion.22), channel_id=1, source_target_pairs={{0,16},{8,24},{16,0},{24,8},{1,17},{9,25},{17,1},{25,9},{2,18},{10... | collective-permute-start | bytes 1190024 | tf_op jit(solution)/shard_map/ppermute | solution.py:358
  (72 other events, 248.5 us)
Sparse Core Ops, SparseCore 0:
  11.4 68.3 all-gather.7
  84.4 21.4 all-gather.15
  107.6 46.9 all-gather.13
  156.0 36.9 all-gather.9
  245.0 41.2 reduce-scatter.3
  292.7 36.9 all-gather.11
  332.0 45.5 reduce-scatter.5
  445.3 40.7 reduce-scatter.7

commit v2 on v1

--- a/solution.py
+++ b/solution.py
@@ -81,7 +81,8 @@
     first_ref,
     hidden_ref,
     gain_ref,
-    weight_ref,
+    low_ref,
+    high_ref,
     cosine_ref,
     sine_ref,
     row_segment_ref,
@@ -102,7 +103,8 @@
     scale = lax.rsqrt(jnp.mean(hidden * hidden, -1, keepdims=True) + EPS)
     normed = (hidden * scale * gain_ref[...]).astype(jnp.bfloat16)
     normed_ref[...] = normed
-    raw = dot(normed, weight_ref[...])
+    middle = low_ref.shape[0]
+    raw = dot(normed[:, :middle], low_ref[...]) + dot(normed[:, middle:], high_ref[...])
     cosine = cosine_ref[...]
     sine = sine_ref[...]
     key_raw = raw[:, query_width : query_width + HEAD_SIZE]
@@ -155,8 +157,9 @@
     log_ref[...] = (top + jnp.log(total)).reshape(HEAD_GROUP, block, 1)
 
 
-def attend(hidden, gain, weight, cosine, sine, segment_row, block, first):
-    tokens, features = hidden.shape
+def attend(hidden, gain, weights, cosine, sine, segment_row, block, first):
+    tokens, features = hidden.shape[0], gain.shape[0]
+    width = weights[0].shape[1]
     query_width = HEAD_GROUP * HEAD_SIZE
     steps = tokens // block
     rows = lambda width: pl.BlockSpec((block, width), lambda i, f: (i, 0))
@@ -177,7 +180,8 @@
             in_specs=[
                 rows(features),
                 whole(1, features),
-                whole(*weight.shape),
+                whole(*weights[0].shape),
+                whole(*weights[1].shape),
                 rows(HEAD_SIZE),
                 rows(HEAD_SIZE),
                 rows(1),
@@ -195,15 +199,15 @@
         ),
         compiler_params=pltpu.CompilerParams(vmem_limit_bytes=48 << 20),
         cost_estimate=pl.CostEstimate(
-            flops=2 * tokens * features * weight.shape[1] + 4 * tokens * tokens * query_width,
-            bytes_accessed=4 * tokens * features + 2 * weight.size,
+            flops=2 * tokens * features * width + 4 * tokens * tokens * query_width,
+            bytes_accessed=4 * tokens * features + 2 * features * width,
             transcendentals=tokens * tokens * HEAD_GROUP // 2,
         ),
     )(
         first,
         hidden,
         gain[None, :],
-        weight,
+        *weights,
         cosine,
         sine,
         segment_row[:, None],
@@ -349,8 +353,223 @@
     )
 
 
-def after(value, *others):
-    return lax.optimization_barrier((value, *others))[0]
+def middle_kernel(
+    mixed_ref,
+    low_ref,
+    high_ref,
+    hidden_ref,
+    gain_ref,
+    router_ref,
+    named_ref,
+    middle_ref,
+    normed_ref,
+    gates_ref,
+):
+    groups, _, width = mixed_ref.shape
+    middle = hidden_ref[...].astype(jnp.float32)
+    for g in range(groups):
+        weight_ref = low_ref if g < groups // 2 else high_ref
+        start = (g % (groups // 2)) * width
+        middle = middle + dot(mixed_ref[g], weight_ref[start : start + width, :])
+    middle_ref[...] = middle
+    scale = lax.rsqrt(jnp.mean(middle * middle, -1, keepdims=True) + EPS)
+    normed = (middle * scale * gain_ref[...]).astype(jnp.bfloat16)
+    normed_ref[...] = normed
+    logits = dot(normed, router_ref[...])
+    named = named_ref[...] > 0
+    logits = jnp.where(named, logits, MASK_FLOOR)
+    shifted = jnp.exp(logits - jnp.max(logits, -1, keepdims=True))
+    shifted = jnp.where(named, shifted, 0.0)
+    gates_ref[...] = shifted / jnp.sum(shifted, -1, keepdims=True)
+
+
+def middle_rows(mixed, weights, hidden, gain, router, named, block):
+    groups, tokens, width = mixed.shape
+    features = gain.shape[0]
+    experts = router.shape[1]
+    rows = lambda columns: pl.BlockSpec((block, columns), lambda i: (i, 0))
+    whole = lambda height, columns: pl.BlockSpec(
+        (height, columns), lambda i: (0, 0), pipeline_mode=pl.Buffered(1)
+    )
+    return pl.pallas_call(
+        middle_kernel,
+        out_shape=(
+            jax.ShapeDtypeStruct((tokens, features), jnp.float32),
+            jax.ShapeDtypeStruct((tokens, features), jnp.bfloat16),
+            jax.ShapeDtypeStruct((tokens, experts), jnp.float32),
+        ),
+        grid=(tokens // block,),
+        in_specs=[
+            pl.BlockSpec((groups, block, width), lambda i: (0, i, 0)),
+            whole(*weights[0].shape),
+            whole(*weights[1].shape),
+            rows(features),
+            whole(1, features),
+            whole(features, experts),
+            rows(experts),
+        ],
+        out_specs=[rows(features), rows(features), rows(experts)],
+        compiler_params=pltpu.CompilerParams(vmem_limit_bytes=48 << 20),
+        cost_estimate=pl.CostEstimate(
+            flops=2 * tokens * features * groups * width,
+            bytes_accessed=12 * tokens * features,
+            transcendentals=0,
+        ),
+    )(mixed, *weights, hidden, gain[None, :], router, named)
+
+
+def expert_kernel(
+    place_ref,
+    normed_ref,
+    cotangent_ref,
+    live_ref,
+    gates_ref,
+    gate_weight_ref,
+    up_weight_ref,
+    down_weight_ref,
+    scaled_ref,
+    grad_gate_ref,
+    grad_up_ref,
+    grad_live_ref,
+    extra_ref,
+):
+    experts_own = gate_weight_ref.shape[0]
+    experts_all = gates_ref.shape[1]
+    first = place_ref[1] * experts_own
+    normed = normed_ref[...]
+    grad_live = jnp.where(live_ref[...] > 0, cotangent_ref[...], jnp.zeros((), jnp.bfloat16))
+    grad_live_ref[...] = grad_live
+    gates = gates_ref[...]
+    number = lax.broadcasted_iota(jnp.int32, gates.shape, 1)
+    grad_gates = jnp.zeros(gates.shape, jnp.float32)
+    for e in range(experts_own):
+        gate = jnp.sum(jnp.where(number == first + e, gates, 0.0), -1, keepdims=True)
+        gate_pre = dot(normed, gate_weight_ref[e])
+        up_pre = dot(normed, up_weight_ref[e])
+        grad_plain = dot(grad_live, down_weight_ref[e], COLUMNS)
+        sigma = jax.nn.sigmoid(gate_pre)
+        silu = gate_pre * sigma
+        acted = silu * up_pre
+        grad_gates = grad_gates + jnp.where(
+            number == first + e, jnp.sum(acted * grad_plain, -1, keepdims=True), 0.0
+        )
+        grad_acted = gate * grad_plain
+        scaled_ref[e] = (gate * acted).astype(jnp.bfloat16)
+        grad_gate_ref[e] = (
+            grad_acted * up_pre * (sigma * (1.0 + gate_pre * (1.0 - sigma)))
+        ).astype(jnp.bfloat16)
+        grad_up_ref[e] = (grad_acted * silu).astype(jnp.bfloat16)
+    rough = grad_gates.astype(jnp.bfloat16)
+    fine = (grad_gates - rough.astype(jnp.float32)).astype(jnp.bfloat16)
+    rest = jnp.zeros((gates.shape[0], extra_ref.shape[1] - 2 * experts_all), jnp.bfloat16)
+    extra_ref[...] = jnp.concatenate([rough, fine, rest], 1)
+
+
+def expert_rows(place, normed, cotangent, live, gates, w_gate, w_up, w_down):
+    tokens, features = normed.shape
+    experts_own, _, hidden = w_gate.shape
+    experts_all = gates.shape[1]
+    chips, block, _ = cotangent.shape
+    rows = lambda columns: pl.BlockSpec((block, columns), lambda i, p: (i, 0))
+    whole = lambda *shape: pl.BlockSpec(
+        shape, lambda i, p: (0,) * len(shape), pipeline_mode=pl.Buffered(1)
+    )
+    spread = pl.BlockSpec((experts_own, block, hidden), lambda i, p: (0, i, 0))
+    wide = jax.ShapeDtypeStruct((experts_own, tokens, hidden), jnp.bfloat16)
+    return pl.pallas_call(
+        expert_kernel,
+        out_shape=(
+            wide,
+            wide,
+            wide,
+            jax.ShapeDtypeStruct((tokens, features), jnp.bfloat16),
+            jax.ShapeDtypeStruct((tokens, 128), jnp.bfloat16),
+        ),
+        grid_spec=pltpu.PrefetchScalarGridSpec(
+            num_scalar_prefetch=1,
+            grid=(chips,),
+            in_specs=[
+                rows(features),
+                pl.BlockSpec(
+                    (None, block, features), lambda i, p: (lax.rem(p[0] - i + chips, chips), 0, 0)
+                ),
+                rows(1),
+                rows(experts_all),
+                whole(*w_gate.shape),
+                whole(*w_up.shape),
+                whole(*w_down.shape),
+            ],
+            out_specs=[spread, spread, spread, rows(features), rows(128)],
+        ),
+        compiler_params=pltpu.CompilerParams(vmem_limit_bytes=52 << 20),
+        cost_estimate=pl.CostEstimate(
+            flops=6 * tokens * features * hidden * experts_own,
+            bytes_accessed=6 * features * hidden * experts_own + 10 * tokens * features,
+            transcendentals=tokens * hidden * experts_own,
+        ),
+    )(place, normed, cotangent, live, gates, w_gate, w_up, w_down)
+
+
+def rows_kernel(
+    scaled_ref,
+    grad_gate_ref,
+    grad_up_ref,
+    extra_ref,
+    gate_weight_ref,
+    up_weight_ref,
+    down_weight_ref,
+    grad_ref,
+    out_ref,
+):
+    features = out_ref.shape[1]
+    grad = 0.0
+    out = 0.0
+    for e in range(scaled_ref.shape[0]):
+        grad = grad + dot(grad_gate_ref[e], gate_weight_ref[e], COLUMNS)
+        grad = grad + dot(grad_up_ref[e], up_weight_ref[e], COLUMNS)
+        out = out + dot(scaled_ref[e], down_weight_ref[e])
+    grad_ref[:, :features] = grad.astype(jnp.bfloat16)
+    grad_ref[:, features:] = extra_ref[...]
+    out_ref[...] = out.astype(jnp.bfloat16)
+
+
+def expert_sums(scaled, grad_gate_pre, grad_up_pre, extra, w_gate, w_up, w_down, block):
+    experts_own, tokens, hidden = scaled.shape
+    features = w_gate.shape[1]
+    rows = lambda columns: pl.BlockSpec((block, columns), lambda i: (i, 0))
+    whole = lambda *shape: pl.BlockSpec(
+        shape, lambda i: (0,) * len(shape), pipeline_mode=pl.Buffered(1)
+    )
+    spread = pl.BlockSpec((experts_own, block, hidden), lambda i: (0, i, 0))
+    return pl.pallas_call(
+        rows_kernel,
+        out_shape=(
+            jax.ShapeDtypeStruct((tokens, features + extra.shape[1]), jnp.bfloat16),
+            jax.ShapeDtypeStruct((tokens, features), jnp.bfloat16),
+        ),
+        grid=(tokens // block,),
+        in_specs=[
+            spread,
+            spread,
+            spread,
+            rows(extra.shape[1]),
+            whole(*w_gate.shape),
+            whole(*w_up.shape),
+            whole(*w_down.shape),
+        ],
+        out_specs=[rows(features + extra.shape[1]), rows(features)],
+        compiler_params=pltpu.CompilerParams(vmem_limit_bytes=52 << 20),
+        cost_estimate=pl.CostEstimate(
+            flops=6 * tokens * features * hidden * experts_own,
+            bytes_accessed=6 * features * hidden * experts_own + 10 * tokens * features,
+            transcendentals=0,
+        ),
+    )(scaled, grad_gate_pre, grad_up_pre, extra, w_gate, w_up, w_down)
+
+
+def after(values, *others):
+    values, _ = lax.optimization_barrier((values, others))
+    return values
 
 
 def swap(value, bit):
@@ -362,10 +581,15 @@
     return (lax.axis_index("rep") & bit) != 0
 
 
-def halve(value, bit):
+def halve(value, came, bit):
     half = value.shape[0] // 2
-    kept = lax.dynamic_slice_in_dim(value, jnp.where(has(bit), half, 0), half, 0)
-    sent = lax.dynamic_slice_in_dim(value, jnp.where(has(bit), 0, half), half, 0)
+    keep = jnp.where(has(bit), half, 0)
+    part = lambda array, start: lax.dynamic_slice_in_dim(array, start, half, 0).astype(jnp.float32)
+    kept = part(value, keep)
+    sent = part(value, half - keep)
+    if came is not None:
+        kept = kept + part(came, keep)
+        sent = sent + part(came, half - keep)
     return kept, sent.astype(jnp.bfloat16)
 
 
@@ -376,31 +600,51 @@
     )
 
 
-def rep_sum(value, bits):
-    for bit in bits:
-        value, sent = halve(value, bit)
-        value = value.astype(jnp.float32) + swap(sent, bit).astype(jnp.float32)
-    value = value.astype(jnp.bfloat16)
-    for bit in reversed(bits):
-        value = join(value, swap(value, bit), bit, 0)
-    return value
-
-
-def gather_rows(block, bits):
-    reps = lax.axis_size("rep")
-    share = block.shape[0] // reps
-    own = lax.dynamic_slice_in_dim(block, lax.axis_index("rep") * share, share, 0)
-    fetched = lax.all_gather(own, "ctx", axis=0)
+class Chain:
+    def __init__(self, order):
+        self.order = order
+        self.stage = 0
+        self.steps = 2 * len(order)
+
+    def send(self, sent):
+        bit = self.order[min(self.stage, self.steps - 1 - self.stage)]
+        self.sent = sent
+        self.flying = swap(sent, bit)
+        self.stage += 1
+
+    def start(self, value):
+        self.kept, sent = halve(value, None, self.order[0])
+        self.send(sent)
+
+    def step(self, *others):
+        came = after(self.flying, *others)
+        bits = len(self.order)
+        if self.stage < bits:
+            self.kept, sent = halve(self.kept, came, self.order[self.stage])
+            self.send(sent)
+        elif self.stage == bits:
+            self.send((self.kept + came.astype(jnp.float32)).astype(jnp.bfloat16))
+        else:
+            bit = self.order[self.steps - self.stage]
+            self.send(join(self.sent, came, bit, 0))
+        return self.sent
+
+    def finish(self, *others):
+        came = after(self.flying, *others)
+        return join(self.sent, came, self.order[0], 0)
+
+
+def exchange(fetched, bits):
     size = fetched.shape[0]
     fetched = fetched.reshape((size,) + (1,) * len(bits) + fetched.shape[1:])
-    width = fetched.shape[-1] // 2
-    halves = []
-    for start, order in ((0, bits), (width, bits[::-1])):
-        value = fetched[..., start : start + width]
-        for bit in order:
-            value = join(value, swap(value, bit), bit, len(bits) - (bit.bit_length() - 1))
-        halves.append(value.reshape(-1, width))
-    return jnp.concatenate(halves, 1)
+    values = [fetched[: size // 2], fetched[size // 2 :]]
+    for stage in range(len(bits)):
+        for h, order in enumerate((bits, bits[::-1])):
+            bit = order[stage]
+            values[h] = join(
+                values[h], swap(values[h], bit), bit, len(bits) - (bit.bit_length() - 1)
+            )
+    return [value.reshape(-1, value.shape[-1]) for value in values]
 
 
 def per_device(
@@ -435,100 +679,107 @@
     experts_own = w_gate.shape[0]
     experts_all = size * experts_own
     slots = expert_ids.shape[2]
-    block = min(256, tokens)
+    block = 2 * own
+    chips = size // 2
+    share = rows_own // reps
+    share_start = lax.axis_index("rep") * share
 
     columns = jnp.concatenate(
-        [segments[0][:, None], positions[0][:, None] // 64, positions[0][:, None] % 64, expert_ids[0]],
+        [
+            segments[0][:, None],
+            positions[0][:, None] // 64,
+            positions[0][:, None] % 64,
+            expert_ids[0],
+        ],
         1,
     ).astype(jnp.bfloat16)
     columns = jnp.pad(columns, ((0, 0), (0, 128 - columns.shape[1])))
     gathered = lax.all_gather(
         jnp.concatenate([inputs[0], columns], 1), "ctx", axis=0, tiled=True
     )
-    hidden_low = gathered[:, :MODEL_WIDTH]
-    numbers = gathered[:, MODEL_WIDTH:].astype(jnp.int32)
-    segment_row = numbers[:, 0]
-    position_row = numbers[:, 1] * 64 + numbers[:, 2]
-    ids = numbers[:, 3 : 3 + slots]
-
+
+    shared = lambda array: lax.dynamic_slice_in_dim(array, share_start, share, 0)
     head_columns = jnp.concatenate(
         [
-            w_query.reshape(rows_own, groups, query_width),
-            key_weight.reshape(rows_own, groups, HEAD_SIZE),
-            value_weight.reshape(rows_own, groups, HEAD_SIZE),
-            jnp.broadcast_to(attn_gain[:, None, None], (rows_own, groups, 1)),
-            jnp.broadcast_to(ffn_gain[:, None, None], (rows_own, groups, 1)),
-            jnp.broadcast_to(router[:, None, :], (rows_own, groups, router.shape[1])),
+            shared(w_query).reshape(share, groups, query_width),
+            shared(key_weight).reshape(share, groups, HEAD_SIZE),
+            shared(value_weight).reshape(share, groups, HEAD_SIZE),
+            jnp.broadcast_to(shared(attn_gain)[:, None, None], (share, groups, 1)),
+            jnp.broadcast_to(shared(ffn_gain)[:, None, None], (share, groups, 1)),
+            jnp.broadcast_to(shared(router)[:, None, :], (share, groups, router.shape[1])),
         ],
         -1,
     )
     head_columns = jnp.repeat(jnp.transpose(head_columns, (1, 0, 2)), copies, 0)
     head_columns = lax.all_to_all(head_columns, "ctx", split_axis=0, concat_axis=0, tiled=True)
-    head_columns = head_columns.reshape(size * rows_own, -1)
+    head_halves = exchange(head_columns, bits)
+    head_columns = jnp.concatenate(head_halves, 0)
     w_heads = head_columns[:, :width]
     gain_one = head_columns[:, width].astype(jnp.float32)
     gain_two = head_columns[:, width + 1].astype(jnp.float32)
     router_all = head_columns[:, width + 2 :]
 
-    live = segment_row != 0
+    numbers = gathered[:, MODEL_WIDTH : MODEL_WIDTH + 3 + slots].astype(jnp.int32)
+    segment_row = numbers[:, 0]
+    position_row = numbers[:, 1] * 64 + numbers[:, 2]
+    ids = numbers[:, 3:]
     cosine_table, sine_table = rope_tables(position_row)
     places = jnp.arange(tokens, dtype=jnp.int32)
-    starts = segment_row[:: block]
-    first = jnp.min(
-        jnp.where(segment_row[None, :] == starts[:, None], places[None, :], tokens), 1
-    ) // block
+    starts = segment_row[::block]
+    first = (
+        jnp.min(jnp.where(segment_row[None, :] == starts[:, None], places[None, :], tokens), 1)
+        // block
+    )
     normed_one, query, key, value, mixed, log_total = attend(
-        hidden_low, gain_one, w_heads, cosine_table, sine_table, segment_row, block, first
-    )
-    w_out_all = gather_rows(after(w_out, hidden_low), bits)
-
-    share = tokens // copies
+        gathered,
+        gain_one,
+        [half[:, :width] for half in head_halves],
+        cosine_table,
+        sine_table,
+        segment_row,
+        block,
+        first,
+    )
+    w_out_halves = exchange(
+        lax.all_gather(shared(after(w_out, gathered)), "ctx", axis=0), bits
+    )
+
+    turned = [after(grad_out[0], gathered)]
+    for k in range(1, chips):
+        turned.append(
+            lax.ppermute(turned[0], "ctx", [(i, (i + 2 * k) % size) for i in range(size)])
+        )
+    turned = jnp.stack(turned)
+    other = lax.ppermute(turned, "ctx", [(i, i ^ 1) for i in range(size)])
+    odd = me % 2 == 1
+    cotangent = jnp.concatenate(
+        [jnp.where(odd, other, turned), jnp.where(odd, turned, other)], 1
+    )
+
+    part = tokens // copies
     mixed_all = lax.all_gather(
-        lax.dynamic_slice_in_dim(mixed, copy_index * share, share, 0), "ctx", axis=0
-    )
-    cotangent = lax.all_gather(after(grad_out[0], mixed), "ctx", axis=0, tiled=True)
-    mixed_all = jnp.transpose(mixed_all.reshape(groups, tokens, query_width), (1, 0, 2))
-    mixed_all = mixed_all.reshape(tokens, QUERY_HEADS * HEAD_SIZE)
-    hidden = hidden_low.astype(jnp.float32)
-    middle = hidden + dot(mixed_all, w_out_all)
-    scale_two = lax.rsqrt(jnp.mean(middle * middle, -1, keepdims=True) + EPS)
-    base_two = middle * scale_two
-    normed_two = (base_two * gain_two).astype(jnp.bfloat16)
-
-    logits = dot(normed_two, router_all)
-    named = jnp.any(ids[:, :, None] == jnp.arange(experts_all, dtype=jnp.int32)[None, None, :], 1)
-    top = jnp.max(jnp.where(named, logits, MASK_FLOOR), -1, keepdims=True)
-    shifted = jnp.where(named, jnp.exp(jnp.where(named, logits, top) - top), 0.0)
-    gates = shifted / jnp.sum(shifted, -1, keepdims=True)
-    gates_own = lax.dynamic_slice_in_dim(gates, me * experts_own, experts_own, 1)
-
-    grad_live = jnp.where(live[:, None], cotangent, jnp.zeros((), jnp.bfloat16))
-    gate_list = [gates_own[:, e : e + 1] for e in range(experts_own)]
-    gate_pre = [dot(normed_two, w_gate[e]) for e in range(experts_own)]
-    up_pre = [dot(normed_two, w_up[e]) for e in range(experts_own)]
-    sigma = [jax.nn.sigmoid(v) for v in gate_pre]
-    acted = [gate_pre[e] * sigma[e] * up_pre[e] for e in range(experts_own)]
-    scaled = [(gate_list[e] * acted[e]).astype(jnp.bfloat16) for e in range(experts_own)]
-    grad_plain = [dot(grad_live, w_down[e], COLUMNS) for e in range(experts_own)]
-    grad_acted = [gate_list[e] * grad_plain[e] for e in range(experts_own)]
-    grad_gate_pre = [
-        (
-            grad_acted[e] * up_pre[e] * (sigma[e] * (1.0 + gate_pre[e] * (1.0 - sigma[e])))
-        ).astype(jnp.bfloat16)
-        for e in range(experts_own)
-    ]
-    grad_up_pre = [
-        (grad_acted[e] * gate_pre[e] * sigma[e]).astype(jnp.bfloat16) for e in range(experts_own)
-    ]
-
+        lax.dynamic_slice_in_dim(mixed, copy_index * part, part, 0), "ctx", axis=0
+    ).reshape(groups, tokens, query_width)
+    named = jnp.any(
+        ids[:, :, None] == jnp.arange(experts_all, dtype=jnp.int32)[None, None, :], 1
+    ).astype(jnp.float32)
+    middle, normed_two, gates = middle_rows(
+        mixed_all, w_out_halves, gathered, gain_two, router_all, named, block
+    )
+    place = jnp.stack([me // 2, me]).astype(jnp.int32)
+    scaled, grad_gate_pre, grad_up_pre, grad_live, extra = expert_rows(
+        place,
+        normed_two,
+        cotangent,
+        (segment_row != 0).astype(jnp.float32)[:, None],
+        gates,
+        w_gate,
+        w_up,
+        w_down,
+    )
+
+    pick = experts_own // 2
     half = MODEL_WIDTH // 2
-    chains = [
-        (lambda e: scaled[e], lambda e: grad_live[:, :half], bits),
-        (lambda e: scaled[e], lambda e: grad_live[:, half:], bits[::-1]),
-        (lambda e: normed_two, lambda e: grad_gate_pre[e], bits),
-        (lambda e: normed_two, lambda e: grad_up_pre[e], bits[::-1]),
-    ]
-    pick = experts_own // 2
 
     def product(left, right, upper):
         terms = [
@@ -541,59 +792,56 @@
         ]
         return jnp.concatenate(terms, 0)
 
-    kept, flying = [], []
-    for left, right, order in chains:
-        sent = product(left, right, jnp.logical_not(has(order[0]))).astype(jnp.bfloat16)
-        flying.append(swap(sent, order[0]))
-
-    grad_two_part = 0.0
-    for e in range(experts_own):
-        grad_two_part = (
-            grad_two_part
-            + dot(grad_gate_pre[e], w_gate[e], COLUMNS)
-            + dot(grad_up_pre[e], w_up[e], COLUMNS)
-        )
-    expert_index = jnp.arange(experts_all, dtype=jnp.int32)[None, :]
-    grad_gates = 0.0
-    for e in range(experts_own):
-        grad_gates = grad_gates + jnp.where(
-            expert_index == me * experts_own + e,
-            jnp.sum(acted[e] * grad_plain[e], -1, keepdims=True),
-            0.0,
-        )
-    rough = lax.reduce_precision(grad_gates, 8, 7)
-    extra = jnp.concatenate([rough, grad_gates - rough], 1).astype(jnp.bfloat16)
-    extra = jnp.pad(extra, ((0, 0), (0, 128 - 2 * experts_all)))
-    grad_two_sum = lax.psum_scatter(
-        jnp.concatenate([grad_two_part.astype(jnp.bfloat16), extra], 1),
-        "ctx",
-        scatter_dimension=0,
-        tiled=True,
-    ).astype(jnp.float32)
-    for left, right, order in chains:
-        kept.append(product(left, right, has(order[0])))
-    moe_part = 0.0
-    for e in range(experts_own):
-        moe_part = moe_part + dot(scaled[e], w_down[e])
+    down_sides = [
+        (lambda e: scaled[e], lambda e: grad_live[:, :half]),
+        (lambda e: scaled[e], lambda e: grad_live[:, half:]),
+    ]
+    input_sides = [
+        (lambda e: normed_two, lambda e: grad_gate_pre[e]),
+        (lambda e: normed_two, lambda e: grad_up_pre[e]),
+    ]
+    down = [Chain(bits), Chain(bits[::-1])]
+    into = [Chain(bits), Chain(bits[::-1])]
+    for chain, sides in zip(down + into, down_sides + input_sides):
+        chain.send(product(*sides, jnp.logical_not(has(chain.order[0]))).astype(jnp.bfloat16))
+    sent = [chain.sent for chain in down + into]
+    grad_rows, out_rows = expert_sums(
+        *after((scaled, grad_gate_pre, grad_up_pre), *sent),
+        extra,
+        w_gate,
+        w_up,
+        w_down,
+        block,
+    )
+    grad_two_sum = lax.psum_scatter(grad_rows, "ctx", scatter_dimension=0, tiled=True)
+    scaled, grad_gate_pre, grad_up_pre = after((scaled, grad_gate_pre, grad_up_pre), grad_rows)
+    for chain, sides in zip(down + into, down_sides + input_sides):
+        chain.kept = product(*sides, has(chain.order[0]))
+    sent = [chain.step(*[c.kept for c in down + into]) for chain in down]
+    grad_two_sum = after(grad_two_sum, *sent).astype(jnp.float32)
 
     def mine(array):
         return lax.dynamic_slice_in_dim(array, me * own, own, 0)
 
-    gates_mine = mine(gates)
+    gates_own = mine(gates)
     grad_gates = (
         grad_two_sum[:, MODEL_WIDTH : MODEL_WIDTH + experts_all]
         + grad_two_sum[:, MODEL_WIDTH + experts_all : MODEL_WIDTH + 2 * experts_all]
     )
     grad_logits = (
-        gates_mine * (grad_gates - jnp.sum(gates_mine * grad_gates, -1, keepdims=True))
+        gates_own * (grad_gates - jnp.sum(gates_own * grad_gates, -1, keepdims=True))
     ).astype(jnp.bfloat16)
     grad_normed_two = grad_two_sum[:, :MODEL_WIDTH] + dot(grad_logits, router_all, COLUMNS)
-    base_two_own = mine(base_two)
+    middle_own = mine(middle)
+    scale_two = lax.rsqrt(jnp.mean(middle_own * middle_own, -1, keepdims=True) + EPS)
+    base_two = middle_own * scale_two
     grad_middle = mine(grad_live).astype(jnp.float32) + norm_back(
-        grad_normed_two * gain_two, base_two_own, mine(scale_two)
+        grad_normed_two * gain_two, base_two, scale_two
     )
     grad_branch = grad_middle.astype(jnp.bfloat16)
-    grad_mixed = dot(grad_branch, w_out_all, COLUMNS).astype(jnp.bfloat16)
+    grad_mixed = jnp.concatenate(
+        [dot(grad_branch, weight, COLUMNS) for weight in w_out_halves], 1
+    ).astype(jnp.bfloat16)
     grad_mixed = jnp.transpose(grad_mixed.reshape(own, groups, query_width), (1, 0, 2))
     grad_mixed = jnp.repeat(grad_mixed, copies, 0)
     grad_mixed_all = lax.all_to_all(
@@ -601,24 +849,12 @@
     ).reshape(tokens, query_width)
     grad_branch_all = lax.all_gather(grad_branch, "ctx", axis=0, tiled=True)
 
-    stage = 1
-    sent_list = []
-    for c, (_, _, order) in enumerate(chains):
-        came = after(flying[c], grad_mixed)
-        kept[c] = kept[c] + came.astype(jnp.float32)
-    while stage < len(bits):
-        for c, (_, _, order) in enumerate(chains):
-            kept[c], sent = halve(kept[c], order[stage])
-            sent_list.append(sent)
-            flying[c] = swap(sent, order[stage])
-        stage += 1
-        if stage < len(bits):
-            for c in range(len(chains)):
-                kept[c] = kept[c] + flying[c].astype(jnp.float32)
+    sent = [chain.step(grad_mixed) for chain in into]
+    sent = sent + [chain.step(*sent) for chain in down]
 
     grad_query, grad_pair = attend_back(
         query,
-        after(grad_mixed_all, *sent_list),
+        after(grad_mixed_all, *sent),
         log_total,
         cosine_table,
         sine_table,
@@ -629,7 +865,7 @@
         first,
     )
     if copies > 1:
-        counted = (places // share == copy_index)[:, None]
+        counted = (places // part == copy_index)[:, None]
         grad_query = jnp.where(counted, grad_query, jnp.zeros((), jnp.bfloat16))
         grad_pair = jnp.where(counted, grad_pair, jnp.zeros((), jnp.bfloat16))
     grad_one_part = dot(grad_query, w_heads[:, :query_width], COLUMNS) + dot(
@@ -639,9 +875,10 @@
     grad_one = lax.psum_scatter(
         grad_one_low, "ctx", scatter_dimension=0, tiled=True
     ).astype(jnp.float32)
+    hidden = gathered[:, :MODEL_WIDTH].astype(jnp.float32)
     scale_one = lax.rsqrt(jnp.mean(hidden * hidden, -1, keepdims=True) + EPS)
     gain_one_term = jnp.sum(grad_one_part * (hidden * scale_one), 0)
-    gain_two_term = jnp.sum(grad_normed_two * base_two_own, 0)
+    gain_two_term = jnp.sum(grad_normed_two * base_two, 0)
     head_grads = jnp.concatenate(
         [
             dot(normed_one, grad_query, ROWS),
@@ -657,77 +894,64 @@
         head_grads, "ctx", split_axis=0, concat_axis=0, tiled=True
     )
 
-    shared = []
-    flying_back = []
-    for c, (_, _, order) in enumerate(chains):
-        came = after(flying[c], grad_one_low, head_grads)
-        shared.append((kept[c] + came.astype(jnp.float32)).astype(jnp.bfloat16))
-        flying_back.append(swap(shared[c], order[-1]))
-
+    sent = [chain.step(grad_one_low, head_grads) for chain in into]
+    sent = sent + [chain.step(*sent) for chain in down]
     grad_proj_out = dot(
-        lax.dynamic_slice_in_dim(mixed, copy_index * rows_own, rows_own, 1), grad_branch_all, ROWS
-    )
-    small = jnp.sum(head_grads_all[:, :, width:].astype(jnp.float32), 0)
-    projections = head_grads_all[:, :, :width]
+        lax.dynamic_slice_in_dim(mixed, copy_index * rows_own, rows_own, 1),
+        after(grad_branch_all, *sent),
+        ROWS,
+    )
+    out_chain = Chain(bits[::-1])
+    out_chain.start(grad_proj_out)
     if copies > 1:
-        projections = jnp.sum(
-            projections.reshape(groups, copies, rows_own, width).astype(jnp.float32), 1
+        head_grads_all = jnp.sum(
+            head_grads_all.reshape(groups, copies, rows_own, -1).astype(jnp.float32), 1
         )
-    projections = jnp.transpose(projections.astype(jnp.bfloat16), (1, 0, 2))
-    query_end = query_width + HEAD_SIZE
-    last_one = jnp.concatenate(
-        [
-            projections[:, :, :query_width].reshape(rows_own, -1),
-            projections[:, :, query_width:query_end].reshape(rows_own, -1),
-        ],
-        1,
-    )
-    last_two = jnp.concatenate(
-        [
-            projections[:, :, query_end:].reshape(rows_own, -1),
-            grad_proj_out.astype(jnp.bfloat16),
-            small.astype(jnp.bfloat16),
-        ],
-        1,
-    )
-    for stage in reversed(range(1, len(bits))):
-        for c, (_, _, order) in enumerate(chains):
-            shared[c] = join(shared[c], after(flying_back[c], last_one), order[stage], 0)
-            flying_back[c] = swap(shared[c], order[stage - 1])
-    last_one = rep_sum(last_one, bits).astype(jnp.float32)
-    last_two = rep_sum(last_two, bits[::-1]).astype(jnp.float32)
+    heads = [Chain(bits), Chain(bits[::-1])]
+    head_grads_all = after(head_grads_all, out_chain.sent)
+    heads[0].start(head_grads_all[: groups // 2].reshape(groups // 2 * rows_own, -1))
+    heads[1].start(head_grads_all[groups // 2 :].reshape(groups // 2 * rows_own, -1))
+    sent = [chain.sent for chain in heads]
+    while into[0].stage < into[0].steps:
+        sent = [chain.step(*sent) for chain in into]
+        sent = sent + [chain.step(*sent) for chain in [out_chain] + heads]
+        if down[0].stage < down[0].steps:
+            sent = sent + [chain.step(*sent) for chain in down]
+    whole = lambda value: value.astype(jnp.float32).reshape(experts_own, -1, value.shape[-1])
+    grad_down = jnp.concatenate([whole(chain.finish(*sent)) for chain in down], 2)
+    sent = sent + [grad_down]
+    while heads[0].stage < heads[0].steps:
+        sent = [chain.step(*sent) for chain in [out_chain] + heads]
+    grad_gate, grad_up = [whole(chain.finish(*sent)) for chain in into]
+    last = [chain.finish(grad_gate, grad_up) for chain in [out_chain] + heads]
+    grad_out_rows = last[0].astype(jnp.float32)
+    head_rows = jnp.concatenate(last[1:], 0).reshape(groups, rows_own, -1).astype(jnp.float32)
+    side = lambda begin, end: jnp.transpose(head_rows[:, :, begin:end], (1, 0, 2)).reshape(
+        rows_own, -1
+    )
+    small = jnp.sum(head_rows[:, :, width:], 0)
 
     moe_sum = lax.psum_scatter(
-        after(moe_part.astype(jnp.bfloat16), grad_branch),
-        "ctx",
-        scatter_dimension=0,
-        tiled=True,
+        after(out_rows, grad_branch), "ctx", scatter_dimension=0, tiled=True
     ).astype(jnp.float32)
-    output = jnp.where(mine(live)[:, None], mine(middle) + moe_sum, 0.0).astype(jnp.bfloat16)
+    live_own = (segments[0] != 0)[:, None]
+    output = jnp.where(live_own, middle_own + moe_sum, 0.0).astype(jnp.bfloat16)
     own_hidden = inputs[0].astype(jnp.float32)
     own_scale = lax.rsqrt(jnp.mean(own_hidden * own_hidden, -1, keepdims=True) + EPS)
     grad_in = grad_middle + norm_back(grad_one * gain_one, own_hidden * own_scale, own_scale)
 
-    def whole(c):
-        value = join(shared[c], flying_back[c], chains[c][2][0], 0)
-        return value.astype(jnp.float32).reshape(experts_own, -1, value.shape[-1])
-
-    grad_down = jnp.concatenate([whole(0), whole(1)], 2)
-    kv_all = KEY_VALUE_HEADS * HEAD_SIZE
-    query_all = QUERY_HEADS * HEAD_SIZE
-    out_end = kv_all + MODEL_WIDTH
     return (
         output[None],
         grad_in[None],
-        last_two[:, out_end],
-        last_one[:, :query_all],
-        last_one[:, query_all:],
-        last_two[:, :kv_all],
-        last_two[:, kv_all:out_end],
-        last_two[:, out_end + 1],
-        last_two[:, out_end + 2 :],
-        whole(2),
-        whole(3),
+        small[:, 0],
+        side(0, query_width),
+        side(query_width, query_width + HEAD_SIZE),
+        side(query_width + HEAD_SIZE, width),
+        grad_out_rows,
+        small[:, 1],
+        small[:, 2:],
+        grad_gate,
+        grad_up,
         grad_down,
     )
 

time: 636 us -> 531 us (0.83)
  waiting for transfers between devices: 269 us -> 163 us
  matrix products: 96.6 us -> 41.8 us
  Pallas kernels: 27.6 us -> 72.6 us
  local copies, waits for them, and re-layouts: 76.8 us -> 48.2 us
  blocking collectives: 0 us -> 22.1 us
  starting transfers between devices: 46.6 us -> 66.3 us
    ppermute x28 -> x36, waiting for transfers between devices: 171 us -> 102 us  [swap(): return lax.ppermute(value, 'rep', [(i, i ^ bit) for i in range(size)])]
    dot_general x30 -> x17, matrix products: 96.6 us -> 41.8 us  [dot(): lax.dot_general(left, right, contract, preferred_element_type=jnp.float32)]
    all_gather x1, waiting for transfers between devices: 56.7 us -> 8.45 us  [per_device(): lax.all_gather(jnp.concatenate([inputs[0], columns], 1), 'ctx', axis=0, t...]
    pallas_call x0 -> x3, Pallas kernels: none -> 46.4 us  [the longest x1 18.5 us: expert_rows(): pl.pallas_call(expert_kernel, out_shape=(wide, wide, wide, jax.ShapeDtype...]
    all_to_all x0 -> x1, blocking collectives: none -> 22.1 us  [per_device(): lax.all_to_all(head_columns, 'ctx', split_axis=0, concat_axis=0, tiled=True)]
    all_to_all x1, waiting for transfers between devices: 0.01 us -> 20.5 us  [per_device(): lax.all_to_all(head_grads, 'ctx', split_axis=0, concat_axis=0, tiled=True)]
    reduce_scatter x2, waiting for transfers between devices: 41.3 us -> 21.2 us  [the longest x1 21.2 us: per_device(): lax.psum_scatter(grad_rows, 'ctx', scatter_dimension=0, tiled=True)]
    ppermute x28 -> x36, starting transfers between devices: 30.9 us -> 44.3 us  [swap(): return lax.ppermute(value, 'rep', [(i, i ^ bit) for i in range(size)])]
  transfers between devices with their start and end apart: 39 -> 49, of which waited for: 17 -> 18; matrix products, arithmetic and copies ran while one was open for 30% -> 26% of each run, Pallas kernels for 4% -> 5%
where the time goes in v2:
time: 531 us; the launch traced here: 523 us
  waiting for transfers between devices  163 us (31%)
  other arithmetic  93.4 us (18%)
  Pallas kernels  72.6 us (14%)
  starting transfers between devices  66.3 us (12%)
  local copies, waits for them, and re-layouts  48.2 us (9%)
  matrix products  41.8 us (8%)
  blocking collectives  22.1 us (4%)
  between operations  15.6 us (3%)
    ppermute x36, waiting for transfers between devices, swap(): return lax.ppermute(value, 'rep', [(i, i ^ bit) for i in range(size)])  102 us
    ppermute x36, starting transfers between devices, swap(): return lax.ppermute(value, 'rep', [(i, i ^ bit) for i in range(size)])  44.3 us
    dot_general x17, matrix products, dot(): lax.dot_general(left, right, contract, preferred_element_type=jnp.float32)  41.8 us
    unnamed x175, local copies, waits for them, and re-layouts  23.6 us
    all_to_all x1, blocking collectives, per_device(): lax.all_to_all(head_columns, 'ctx', split_axis=0, concat_axis=0, tiled=True)  22.1 us
    reduce_scatter x1, waiting for transfers between devices, per_device(): lax.psum_scatter(grad_rows, 'ctx', scatter_dimension=0, tiled=True)  21.2 us
    all_to_all x1, waiting for transfers between devices, per_device(): lax.all_to_all(head_grads, 'ctx', split_axis=0, concat_axis=0, tiled=True)  20.5 us
    pallas_call x1, Pallas kernels, expert_rows(): pl.pallas_call(expert_kernel, out_shape=(wide, wide, wide, jax.ShapeDtype...  18.5 us
  transfers between devices with their start and end apart: 49, of which 18 were waited for; matrix products, arithmetic and copies ran while one was open for 26% of the time, Pallas kernels for 5%

profile of v2, /device:TPU:0, one launch (start us, length us, event | category | flops | bytes accessed | tf_op | source)
XLA Modules:
  0.0 523.2 jit_solution(17471998316982626266)
XLA Ops:
  13.6 22.1 %all_to_all.15 = bf16[8,48,338]{2,1,0:T(8,128)(2,1)S(1)} all-to-all(bf16[8,48,338]{2,1,0:T(8,128)(2,1)S(1)} %copy.160), channel_id=1, replica_groups=mesh['rep'=4,'ctx'=8] {'ctx'}, dimensions={0} | all-to-all | bytes 519168 | tf_op jit(solution)/shard_map/all_to_all | solution.py:714
  38.8 2.7 collective-permute-done
  45.3 5.6 %collective-permute-done.3 = bf16[4,2,1,48,338]{4,3,0,2,1:T(8,128)(2,1)S(1)} collective-permute-done((bf16[4,2,1,48,338]{4,3,0,2,1:T(8,128)(2,1)S(1)}, bf16[4,2,1,48,338]{4,3,0,2,1:T(8,128)(2,1)S(1)}, u32[]{:S(2)}, u32[]{:S(2)}) %collective-permute-start.3) | collective-permute-done | bytes 259616 | tf_op jit(solution)/shard_map/ppermute | solution.py:577
  50.9 8.4 %all-gather.7.cloned.1.call-done.hidden_ref = bf16[1024,1664]{1,0:T(8,128)(2,1)} async-done(((bf16[128,1664]{1,0:T(8,128)(2,1)}), bf16[1024,1664]{1,0:T(8,128)(2,1)}) %all-gather.7.cloned.1.call-update) | async-done | bytes 3407888 | tf_op jit(solution)/shard_map/all_gather | solution.py:697
  68.6 14.1 %shard_map.238 = (bf16[1024,1536]{1,0:T(8,128)(2,1)}, bf16[1024,192]{1,0:T(8,128)(2,1)S(1)}, bf16[1024,64]{1,0:T(8,128)(2,1)S(1)}, bf16[1024,64]{1,0:T(8,128)(2,...) custom-call(s32[4]{0:T(128)S(1)} %and_select_fusion.first_ref, ...), custom_call_target="tpu_custom_call" | custom-call | flops 1811939328 | bytes 7274496 | tf_op jit(solution)/shard_map/pallas_call | solution.py:167
  85.4 10.4 %reduce-scatter.4.cloned.1.call-start = ((), (), s32[]{:S(2)}) async-start(), calls=%async_computation.7 | async-start | bytes 3833856 | tf_op jit(solution)/shard_map/reduce_scatter | solution.py:816
  95.8 11.2 %collective-permute-done.9 = bf16[128,1536]{1,0:T(8,128)(2,1)} collective-permute-done((bf16[128,1536]{1,0:T(8,128)(2,1)}, bf16[128,1536]{1,0:T(8,128)(2,1)}, u32[]{:S(2)}, u32[]{:S(2)}) %collective-permute-start.9) | collective-permute-done | bytes 393248 | tf_op jit(solution)/shard_map/ppermute | solution.py:750
  107.0 2.7 pad_maximum_fusion.5
  118.1 9.6 %collective-permute-done.6 = bf16[4,1,1,48,1536]{4,3,2,1,0:T(8,128)(2,1)} collective-permute-done((bf16[4,1,1,48,1536]{4,3,2,1,0:T(8,128)(2,1)S(1)}, bf16[4,1,1,48,1536]{4,3,2,1,0:T(8,128)(2,1)}, u32[]{:S(2)}, u32[]{:S(2)}) %collective-permute-start.6) | collective-permute-done | bytes 589856 | tf_op jit(solution)/shard_map/ppermute | solution.py:577
  137.5 20.1 %collective-permute-done.7 = bf16[4,2,1,48,1536]{4,3,2,1,0:T(8,128)(2,1)S(1)} collective-permute-done((bf16[4,2,1,48,1536]{4,3,2,1,0:T(8,128)(2,1)S(1)}, bf16[4,2,1,48,1536]{4,3,2,1,0:T(8,128)(2,1)S(1)}, u32[]{:S(2)}, u32[]{:S(2)}) %collective-permute-start.7) | collective-permute-done | bytes 1179680 | tf_op jit(solution)/shard_map/ppermute | solution.py:577
  157.9 3.5 collective-permute-done.5
  166.9 11.9 %shard_map.239 = (f32[1024,1536]{1,0:T(8,128)}, bf16[1024,1536]{1,0:T(8,128)(2,1)}, f32[1024,16]{1,0:T(8,128)S(1)}) custom-call(bf16[8,1024,192]{2,1,0:T(8,128)(2,1)} %bitcast.174, bf16[768,1536]{1,0:T(8,128)(2,1)S(1)} %bitcast.153, bf16[768,1536]{1,0:T(8,128)(2,1)S(1)} %bitcast.151, bf16[1024,1664]{1,0:T(8,128)(2,1)} %all-gather.7.cloned.1.call-done.hidden_ref, ...), custom_call_target="tpu_custom_call" | custom-call | flops 4831838208 | bytes 18874368 | tf_op jit(solution)/shard_map/pallas_call | solution.py:394
  178.9 18.5 %shard_map.240 = (bf16[2,1024,512]{2,1,0:T(8,128)(2,1)}, bf16[2,1024,512]{2,1,0:T(8,128)(2,1)}, bf16[2,1024,512]{2,1,0:T(8,128)(2,1)}, bf16[1024,1536]{1,0:T(8,128)(2,1)}, bf16[1024,128]{1,0:T(8,128)(2,1)S(1)}) custom-call(s32[2]{0:T(128)S(1)} %pad_add_fusion.place_ref, bf16[1024,1536]{1,0:T(8,128)(2,1)} %get-tuple-element.74.normed_ref, ...), custom_call_target="tpu_custom_call" | custom-call | flops 9663676416 | bytes 25165824 | tf_op jit(solution)/shard_map/pallas_call | solution.py:479
  197.3 4.2 convolution_convert_fusion.6
  204.4 3.0 convolution_convert_fusion.1
  207.4 3.0 convolution_convert_fusion
  210.4 16.0 %shard_map.241 = (bf16[1024,1664]{1,0:T(8,128)(2,1)}, bf16[1024,1536]{1,0:T(8,128)(2,1)}) custom-call(bf16[2,1024,512]{2,1,0:T(8,128)(2,1)} %get-tuple-element.87.scaled_ref, bf16[2,1024,512]{2,1,0:T(8,128)(2,1)} %get-tuple-element.88.grad_gate_ref, bf16[2,1024,512]{2,1,0:T(8,128)(2,1)} %get-tuple-element.89.grad_up_ref, ...), custom_call_target="tpu_custom_call" | custom-call | flops 9663676416 | bytes 25165824 | tf_op jit(solution)/shard_map/pallas_call | solution.py:544
  228.8 3.1 fusion.6
  232.0 3.6 fusion.11
  238.6 3.5 fusion.9
  242.1 2.8 collective-permute-done.12
  247.7 21.2 %reduce-scatter.4.cloned.1.call-done = bf16[128,1664]{1,0:T(8,128)(2,1)} async-done(((bf16[1024,1664]{1,0:T(8,128)(2,1)}), bf16[128,1664]{1,0:T(8,128)(2,1)}) %reduce-scatter.4.cloned.1.call-update) | async-done | bytes 426000 | tf_op jit(solution)/shard_map/reduce_scatter | solution.py:816
  272.1 2.2 multiply_reduce_fusion
  275.2 2.3 fusion.80
  280.5 2.6 fusion
  287.2 3.5 all-to-all-start.1
  291.1 24.1 %collective-permute-done.14 = bf16[1536,512]{1,0:T(8,128)(2,1)} collective-permute-done((bf16[1536,512]{1,0:T(8,128)(2,1)}, bf16[1536,512]{1,0:T(8,128)(2,1)}, u32[]{:S(2)}, u32[]{:S(2)}) %collective-permute-start.14) | collective-permute-done | bytes 1572896 | tf_op jit(solution)/shard_map/ppermute | solution.py:577
  315.2 2.8 add_convert_fusion.3
  318.0 2.5 add_convert_fusion.2
  330.9 12.1 %shard_map.242 = (bf16[1024,192]{1,0:T(8,128)(2,1)S(1)}, bf16[1024,128]{1,0:T(8,128)(2,1)S(1)}) custom-call(s32[4]{0:T(128)S(1)} %copy-done.16, bf16[1024,192]{1,0:T(8,128)(2,1)S(1)} %copy-done.20, bf16[1024,192]{1,0:T(8,128)(2,1)S(1)} %bitcast.155, f32[3,1024,1]{2,1,0:T(8,128)S(1)} %copy-done.18, f32[1024,64]{1,0:T(8,128)S(1)} %copy-done.11, ...), custom_call_target="tpu_custom_call" | custom-call | flops 2013265920 | bytes 3932160 | tf_op jit(solution)/shard_map/pallas_call | solution.py:304
  344.9 2.9 fusion.2
  350.0 2.6 collective-permute-start.18
  356.9 3.5 convolution_convert_fusion.2
  362.5 3.0 convolution_convert_fusion.3
  365.5 2.3 concatenate.132
  367.7 5.2 all-to-all-start.2
  373.0 2.4 add_convert_fusion.1
  377.5 2.6 add_convert_fusion
  387.6 2.9 fusion.84
  393.1 20.5 %all-to-all-done.2 = bf16[8,192,338]{2,1,0:T(8,128)(2,1)S(1)} async-done(((bf16[8,192,338]{2,1,0:T(8,128)(2,1)}), bf16[8,192,338]{2,1,0:T(8,128)(2,1)S(1)}, u32[]{:S(2)}, u32[]{:S(2)}) %all-to-all-start.2) | async-done | bytes 1038368 | tf_op jit(solution)/shard_map/all_to_all | solution.py:893
  422.4 2.8 collective-permute-done.27
  435.4 3.6 maximum_convert_fusion
  439.0 26.9 %collective-permute-done.32 = bf16[192,338]{1,0:T(8,128)(2,1)S(1)} collective-permute-done((bf16[192,338]{1,0:T(8,128)(2,1)S(1)}, bf16[192,338]{1,0:T(8,128)(2,1)S(1)}, u32[]{:S(2)}, u32[]{:S(2)}) %collective-permute-start.32) | collective-permute-done | bytes 129824 | tf_op jit(solution)/shard_map/ppermute | solution.py:577
  481.2 3.3 fusion.58
  489.0 3.6 convert.61
  492.6 3.6 convert.62
  502.1 2.7 reshape.362
  504.8 2.2 copy.177
  (398 shorter events, 157.9 us)
Async XLA Ops:
  7.2 52.1 %all-gather.7.cloned.1.call-start = ((), (), s32[]{:S(2)}) async-start(), calls=%async_computation.6 | async-start | bytes 3833856 | tf_op jit(solution)/shard_map/all_gather | solution.py:697
  11.3 98.4 %all-gather.13.cloned.1.call-start = ((), (), s32[]{:S(2)}) async-start(), calls=%async_computation.12 | async-start | bytes 1327104 | tf_op jit(solution)/shard_map/all_gather | solution.py:744
  35.7 5.8 %collective-permute-start = (bf16[4,1,1,48,338]{4,3,0,2,1:T(8,128)(2,1)S(1)}, bf16[4,1,1,48,338]{4,3,0,2,1:T(8,128)(2,1)S(1)}, u32[]{:S(2)}, u32[]{:S(2)}) collective-permute-start(bf16[4,1,1,48,338]{4,3,0,2,1:T(8,128)(2,1)S(1)} %get-tuple-element.274), channel_id=1, source_target_pairs={{0,8},{8,0},{16,24},{24,16},{1,9},{9,1},{17,25},{25,17},{2,10},{10... | collective-permute-start | bytes 389384 | tf_op jit(solution)/shard_map/ppermute | solution.py:577
  42.9 7.9 %collective-permute-start.3 = (bf16[4,2,1,48,338]{4,3,0,2,1:T(8,128)(2,1)S(1)}, bf16[4,2,1,48,338]{4,3,0,2,1:T(8,128)(2,1)S(1)}, u32[]{:S(2)}, u32[]{:S(2)}) collective-permute-start(bf16[4,2,1,48,338]{4,3,0,2,1:T(8,128)(2,1)S(1)} %pad_maximum_fusion.22), channel_id=1, source_target_pairs={{0,8},{8,0},{16,24},{24,16},{1,9},{9,1},{17,25},{25,17},{2,10},{10... | collective-permute-start | bytes 778760 | tf_op jit(solution)/shard_map/ppermute | solution.py:577
  43.6 17.6 %collective-permute-start.1 = (bf16[4,1,2,48,338]{4,3,0,2,1:T(8,128)(2,1)S(1)}, bf16[4,1,2,48,338]{4,3,0,2,1:T(8,128)(2,1)S(1)}, u32[]{:S(2)}, u32[]{:S(2)}) collective-permute-start(bf16[4,1,2,48,338]{4,3,0,2,1:T(8,128)(2,1)S(1)} %pad_maximum_fusion.21), channel_id=1, source_target_pairs={{0,16},{8,24},{16,0},{24,8},{1,17},{9,25},{17,1},{25,9},{2,18},{10... | collective-permute-start | bytes 778760 | tf_op jit(solution)/shard_map/ppermute | solution.py:577
  61.0 102.2 %all-gather.11.cloned.1.call-start = ((), (), s32[]{:S(2)}) async-start(), calls=%async_computation.11 | async-start | bytes 4718592 | tf_op jit(solution)/shard_map/all_gather | solution.py:760
  62.1 33.7 %collective-permute-start.10 = (bf16[128,1536]{1,0:T(8,128)(2,1)}, bf16[128,1536]{1,0:T(8,128)(2,1)}, u32[]{:S(2)}, u32[]{:S(2)}) collective-permute-start(bf16[128,1536]{1,0:T(8,128)(2,1)} %bitcast.23), channel_id=1, source_target_pairs={{0,6},{1,7},{2,0},{3,1},{4,2},{5,3},{6,4},{7,5},{8,14},{9,15},{10,... | collective-permute-start | bytes 1179656 | tf_op jit(solution)/shard_map/ppermute | solution.py:750
  63.4 43.6 %collective-permute-start.9 = (bf16[128,1536]{1,0:T(8,128)(2,1)}, bf16[128,1536]{1,0:T(8,128)(2,1)}, u32[]{:S(2)}, u32[]{:S(2)}) collective-permute-start(bf16[128,1536]{1,0:T(8,128)(2,1)} %bitcast.23), channel_id=1, source_target_pairs={{0,4},{1,5},{2,6},{3,7},{4,0},{5,1},{6,2},{7,3},{8,12},{9,13},{10,... | collective-permute-start | bytes 1179656 | tf_op jit(solution)/shard_map/ppermute | solution.py:750
  63.4 43.6 %collective-permute-start.8 = (bf16[128,1536]{1,0:T(8,128)(2,1)}, bf16[128,1536]{1,0:T(8,128)(2,1)}, u32[]{:S(2)}, u32[]{:S(2)}) collective-permute-start(bf16[128,1536]{1,0:T(8,128)(2,1)} %bitcast.23), channel_id=1, source_target_pairs={{0,2},{1,3},{2,4},{3,5},{4,6},{5,7},{6,0},{7,1},{8,10},{9,11},{10,... | collective-permute-start | bytes 1179656 | tf_op jit(solution)/shard_map/ppermute | solution.py:750
  85.4 183.6 %reduce-scatter.4.cloned.1.call-start = ((), (), s32[]{:S(2)}) async-start(), calls=%async_computation.7 | async-start | bytes 3833856 | tf_op jit(solution)/shard_map/reduce_scatter | solution.py:816
  109.7 20.9 %collective-permute-start.11 = (bf16[4,128,1536]{2,1,0:T(8,128)(2,1)}, bf16[4,128,1536]{2,1,0:T(8,128)(2,1)}, u32[]{:S(2)}, u32[]{:S(2)}) collective-permute-start(bf16[4,128,1536]{2,1,0:T(8,128)(2,1)} %pad_maximum_fusion.5), channel_id=1, source_target_pairs={{0,1},{1,0},{2,3},{3,2},{4,5},{5,4},{6,7},{7,6},{8,9},{9,8},{10,11... | collective-permute-start | bytes 4718600 | tf_op jit(solution)/shard_map/ppermute | solution.py:753
  111.9 15.9 %collective-permute-start.6 = (bf16[4,1,1,48,1536]{4,3,2,1,0:T(8,128)(2,1)S(1)}, bf16[4,1,1,48,1536]{4,3,2,1,0:T(8,128)(2,1)}, u32[]{:S(2)}, u32[]{:S(2)}) collective-permute-start(bf16[4,1,1,48,1536]{4,3,2,1,0:T(8,128)(2,1)S(1)} %bitcast.165), channel_id=1, source_target_pairs={{0,16},{8,24},{16,0},{24,8},{1,17},{9,25},{17,1},{25,9},{2,18},{10... | collective-permute-start | bytes 1769480 | tf_op jit(solution)/shard_map/ppermute | solution.py:577
  116.6 16.4 %collective-permute-start.4 = (bf16[4,1,1,48,1536]{4,3,2,1,0:T(8,128)(2,1)}, bf16[4,1,1,48,1536]{4,3,2,1,0:T(8,128)(2,1)S(1)}, u32[]{:S(2)}, u32[]{:S(2)}) collective-permute-start(bf16[4,1,1,48,1536]{4,3,2,1,0:T(8,128)(2,1)} %bitcast.12), channel_id=1, source_target_pairs={{0,8},{8,0},{16,24},{24,16},{1,9},{9,1},{17,25},{25,17},{2,10},{10... | collective-permute-start | bytes 1769480 | tf_op jit(solution)/shard_map/ppermute | solution.py:577
  129.1 28.5 %collective-permute-start.7 = (bf16[4,2,1,48,1536]{4,3,2,1,0:T(8,128)(2,1)S(1)}, bf16[4,2,1,48,1536]{4,3,2,1,0:T(8,128)(2,1)S(1)}, u32[]{:S(2)}, u32[]{:S(2)}) collective-permute-start(bf16[4,2,1,48,1536]{4,3,2,1,0:T(8,128)(2,1)S(1)} %pad_maximum_fusion.11), channel_id=1, source_target_pairs={{0,8},{8,0},{16,24},{24,16},{1,9},{9,1},{17,25},{25,17},{2,10},{10... | collective-permute-start | bytes 3538952 | tf_op jit(solution)/shard_map/ppermute | solution.py:577
  134.2 27.2 %collective-permute-start.5 = (bf16[4,1,2,48,1536]{4,3,2,1,0:T(8,128)(2,1)S(1)}, bf16[4,1,2,48,1536]{4,3,2,1,0:T(8,128)(2,1)S(1)}, u32[]{:S(2)}, u32[]{:S(2)}) collective-permute-start(bf16[4,1,2,48,1536]{4,3,2,1,0:T(8,128)(2,1)S(1)} %pad_maximum_fusion.10), channel_id=1, source_target_pairs={{0,16},{8,24},{16,0},{24,8},{1,17},{9,25},{17,1},{25,9},{2,18},{10... | collective-permute-start | bytes 3538952 | tf_op jit(solution)/shard_map/ppermute | solution.py:577
  226.5 161.1 %all-gather.9.cloned.1.call-start = ((), (), s32[]{:S(2)}) async-start(), calls=%async_computation.10 | async-start | bytes 3538944 | tf_op jit(solution)/shard_map/all_gather | solution.py:850
  226.8 18.1 %collective-permute-start.12 = (bf16[512,768]{1,0:T(8,128)(2,1)}, bf16[512,768]{1,0:T(8,128)(2,1)S(1)}, u32[]{:S(2)}, u32[]{:S(2)}) collective-permute-start(bf16[512,768]{1,0:T(8,128)(2,1)} %convolution_convert_fusion.6), channel_id=1, source_target_pairs={{0,8},{8,0},{16,24},{24,16},{1,9},{9,1},{17,25},{25,17},{2,10},{10... | collective-permute-start | bytes 2359304 | tf_op jit(solution)/shard_map/ppermute | solution.py:577
  227.9 18.2 %collective-permute-start.13 = (bf16[512,768]{1,0:T(8,128)(2,1)}, bf16[512,768]{1,0:T(8,128)(2,1)S(1)}, u32[]{:S(2)}, u32[]{:S(2)}) collective-permute-start(bf16[512,768]{1,0:T(8,128)(2,1)} %convolution_convert_fusion.5), channel_id=1, source_target_pairs={{0,16},{8,24},{16,0},{24,8},{1,17},{9,25},{17,1},{25,9},{2,18},{10... | collective-permute-start | bytes 2359304 | tf_op jit(solution)/shard_map/ppermute | solution.py:577
  277.5 37.7 %collective-permute-start.14 = (bf16[1536,512]{1,0:T(8,128)(2,1)}, bf16[1536,512]{1,0:T(8,128)(2,1)}, u32[]{:S(2)}, u32[]{:S(2)}) collective-permute-start(bf16[1536,512]{1,0:T(8,128)(2,1)} %convolution_convert_fusion.1), channel_id=1, source_target_pairs={{0,8},{8,0},{16,24},{24,16},{1,9},{9,1},{17,25},{25,17},{2,10},{10... | collective-permute-start | bytes 4718600 | tf_op jit(solution)/shard_map/ppermute | solution.py:577
  279.0 39.0 %collective-permute-start.15 = (bf16[1536,512]{1,0:T(8,128)(2,1)}, bf16[1536,512]{1,0:T(8,128)(2,1)}, u32[]{:S(2)}, u32[]{:S(2)}) collective-permute-start(bf16[1536,512]{1,0:T(8,128)(2,1)} %convolution_convert_fusion), channel_id=1, source_target_pairs={{0,16},{8,24},{16,0},{24,8},{1,17},{9,25},{17,1},{25,9},{2,18},{10... | collective-permute-start | bytes 4718600 | tf_op jit(solution)/shard_map/ppermute | solution.py:577
  283.7 37.7 %collective-permute-start.16 = (bf16[256,768]{1,0:T(8,128)(2,1)}, bf16[256,768]{1,0:T(8,128)(2,1)}, u32[]{:S(2)}, u32[]{:S(2)}) collective-permute-start(bf16[256,768]{1,0:T(8,128)(2,1)} %get-tuple-element.221), channel_id=1, source_target_pairs={{0,16},{8,24},{16,0},{24,8},{1,17},{9,25},{17,1},{25,9},{2,18},{10... | collective-permute-start | bytes 1179656 | tf_op jit(solution)/shard_map/ppermute | solution.py:577
  284.2 37.2 %collective-permute-start.17 = (bf16[256,768]{1,0:T(8,128)(2,1)}, bf16[256,768]{1,0:T(8,128)(2,1)}, u32[]{:S(2)}, u32[]{:S(2)}) collective-permute-start(bf16[256,768]{1,0:T(8,128)(2,1)} %add_convert_fusion.6), channel_id=1, source_target_pairs={{0,8},{8,0},{16,24},{24,16},{1,9},{9,1},{17,25},{25,17},{2,10},{10... | collective-permute-start | bytes 1179656 | tf_op jit(solution)/shard_map/ppermute | solution.py:577
  287.2 38.1 %all-to-all-start.1 = ((bf16[8,128,192]{1,2,0:T(8,128)(2,1)}), bf16[8,128,192]{1,2,0:T(8,128)(2,1)S(1)}, u32[]{:S(2)}, u32[]{:S(2)}) async-start(bf16[8,128,192]{1,2,0:T(8,128)(2,1)} %maximum_bitcast_fusion), calls=%async_computation.3 | async-start | bytes 786432 | tf_op jit(solution)/shard_map/all_to_all | solution.py:847
  290.6 188.7 %reduce-scatter.8.cloned.1.call-start = ((), (), s32[]{:S(2)}) async-start(), calls=%async_computation.9 | async-start | bytes 3538944 | tf_op jit(solution)/shard_map/reduce_scatter | solution.py:875
  347.9 133.3 %reduce-scatter.6.cloned.1.call-start = ((), (), s32[]{:S(2)}) async-start(), calls=%async_computation.8 | async-start | bytes 3538944 | tf_op jit(solution)/shard_map/reduce_scatter | solution.py:934
  350.0 23.0 %collective-permute-start.18 = (bf16[768,512]{1,0:T(8,128)(2,1)}, bf16[768,512]{1,0:T(8,128)(2,1)}, u32[]{:S(2)}, u32[]{:S(2)}) collective-permute-start(bf16[768,512]{1,0:T(8,128)(2,1)} %add_convert_fusion.3), channel_id=1, source_target_pairs={{0,16},{8,24},{16,0},{24,8},{1,17},{9,25},{17,1},{25,9},{2,18},{10... | collective-permute-start | bytes 2359304 | tf_op jit(solution)/shard_map/ppermute | solution.py:577
  352.6 22.7 %collective-permute-start.19 = (bf16[768,512]{1,0:T(8,128)(2,1)}, bf16[768,512]{1,0:T(8,128)(2,1)}, u32[]{:S(2)}, u32[]{:S(2)}) collective-permute-start(bf16[768,512]{1,0:T(8,128)(2,1)} %add_convert_fusion.2), channel_id=1, source_target_pairs={{0,8},{8,0},{16,24},{24,16},{1,9},{9,1},{17,25},{25,17},{2,10},{10... | collective-permute-start | bytes 2359304 | tf_op jit(solution)/shard_map/ppermute | solution.py:577
  353.3 27.4 %collective-permute-start.20 = (bf16[256,768]{1,0:T(8,128)(2,1)S(1)}, bf16[256,768]{1,0:T(8,128)(2,1)}, u32[]{:S(2)}, u32[]{:S(2)}) collective-permute-start(bf16[256,768]{1,0:T(8,128)(2,1)S(1)} %copy-done.46), channel_id=1, source_target_pairs={{0,16},{8,24},{16,0},{24,8},{1,17},{9,25},{17,1},{25,9},{2,18},{10... | collective-permute-start | bytes 1179656 | tf_op jit(solution)/shard_map/ppermute | solution.py:577
  353.8 26.8 %collective-permute-start.21 = (bf16[256,768]{1,0:T(8,128)(2,1)}, bf16[256,768]{1,0:T(8,128)(2,1)}, u32[]{:S(2)}, u32[]{:S(2)}) collective-permute-start(bf16[256,768]{1,0:T(8,128)(2,1)} %add_convert_fusion.4), channel_id=1, source_target_pairs={{0,8},{8,0},{16,24},{24,16},{1,9},{9,1},{17,25},{25,17},{2,10},{10... | collective-permute-start | bytes 1179656 | tf_op jit(solution)/shard_map/ppermute | solution.py:577
  367.7 45.9 %all-to-all-start.2 = ((bf16[8,192,338]{2,1,0:T(8,128)(2,1)}), bf16[8,192,338]{2,1,0:T(8,128)(2,1)S(1)}, u32[]{:S(2)}, u32[]{:S(2)}) async-start(bf16[8,192,338]{2,1,0:T(8,128)(2,1)} %concatenate.132), calls=%async_computation.5 | async-start | bytes 2359296 | tf_op jit(solution)/shard_map/all_to_all | solution.py:893
  375.4 38.6 %collective-permute-start.23 = (bf16[768,512]{1,0:T(8,128)(2,1)S(1)}, bf16[768,512]{1,0:T(8,128)(2,1)}, u32[]{:S(2)}, u32[]{:S(2)}) collective-permute-start(bf16[768,512]{1,0:T(8,128)(2,1)S(1)} %add_convert_fusion.1), channel_id=1, source_target_pairs={{0,16},{8,24},{16,0},{24,8},{1,17},{9,25},{17,1},{25,9},{2,18},{10... | collective-permute-start | bytes 2359304 | tf_op jit(solution)/shard_map/ppermute | solution.py:577
  380.1 35.5 %collective-permute-start.24 = (bf16[768,512]{1,0:T(8,128)(2,1)}, bf16[768,512]{1,0:T(8,128)(2,1)}, u32[]{:S(2)}, u32[]{:S(2)}) collective-permute-start(bf16[768,512]{1,0:T(8,128)(2,1)} %add_convert_fusion), channel_id=1, source_target_pairs={{0,8},{8,0},{16,24},{24,16},{1,9},{9,1},{17,25},{25,17},{2,10},{10... | collective-permute-start | bytes 2359304 | tf_op jit(solution)/shard_map/ppermute | solution.py:577
  382.8 47.3 %collective-permute-start.29 = (bf16[512,768]{1,0:T(8,128)(2,1)}, bf16[512,768]{1,0:T(8,128)(2,1)}, u32[]{:S(2)}, u32[]{:S(2)}) collective-permute-start(bf16[512,768]{1,0:T(8,128)(2,1)} %pad_maximum_fusion.14), channel_id=1, source_target_pairs={{0,16},{8,24},{16,0},{24,8},{1,17},{9,25},{17,1},{25,9},{2,18},{10... | collective-permute-start | bytes 2359304 | tf_op jit(solution)/shard_map/ppermute | solution.py:577
  386.3 44.2 %collective-permute-start.28 = (bf16[512,768]{1,0:T(8,128)(2,1)}, bf16[512,768]{1,0:T(8,128)(2,1)}, u32[]{:S(2)}, u32[]{:S(2)}) collective-permute-start(bf16[512,768]{1,0:T(8,128)(2,1)} %pad_maximum_fusion.13), channel_id=1, source_target_pairs={{0,8},{8,0},{16,24},{24,16},{1,9},{9,1},{17,25},{25,17},{2,10},{10... | collective-permute-start | bytes 2359304 | tf_op jit(solution)/shard_map/ppermute | solution.py:577
  391.6 36.0 %collective-permute-start.26 = (bf16[96,1536]{1,0:T(8,128)(2,1)}, bf16[96,1536]{1,0:T(8,128)(2,1)}, u32[]{:S(2)}, u32[]{:S(2)}) collective-permute-start(bf16[96,1536]{1,0:T(8,128)(2,1)} %dynamic-slice_convert_fusion), channel_id=1, source_target_pairs={{0,16},{8,24},{16,0},{24,8},{1,17},{9,25},{17,1},{25,9},{2,18},{10... | collective-permute-start | bytes 884744 | tf_op jit(solution)/shard_map/ppermute | solution.py:577
  414.0 11.2 %collective-permute-start.27 = (bf16[384,338]{1,0:T(8,128)(2,1)S(1)}, bf16[384,338]{1,0:T(8,128)(2,1)S(1)}, u32[]{:S(2)}, u32[]{:S(2)}) collective-permute-start(bf16[384,338]{1,0:T(8,128)(2,1)S(1)} %get-tuple-element.254), channel_id=1, source_target_pairs={{0,16},{8,24},{16,0},{24,8},{1,17},{9,25},{17,1},{25,9},{2,18},{10... | collective-permute-start | bytes 778760 | tf_op jit(solution)/shard_map/ppermute | solution.py:577
  415.5 10.5 %collective-permute-start.22 = (bf16[384,338]{1,0:T(8,128)(2,1)S(1)}, bf16[384,338]{1,0:T(8,128)(2,1)S(1)}, u32[]{:S(2)}, u32[]{:S(2)}) collective-permute-start(bf16[384,338]{1,0:T(8,128)(2,1)S(1)} %get-tuple-element.253), channel_id=1, source_target_pairs={{0,8},{8,0},{16,24},{24,16},{1,9},{9,1},{17,25},{25,17},{2,10},{10... | collective-permute-start | bytes 778760 | tf_op jit(solution)/shard_map/ppermute | solution.py:577
  425.2 59.2 %collective-permute-start.34 = (bf16[1536,512]{1,0:T(8,128)(2,1)}, bf16[1536,512]{1,0:T(8,128)(2,1)}, u32[]{:S(2)}, u32[]{:S(2)}) collective-permute-start(bf16[1536,512]{1,0:T(8,128)(2,1)} %pad_maximum_fusion.6), channel_id=1, source_target_pairs={{0,8},{8,0},{16,24},{24,16},{1,9},{9,1},{17,25},{25,17},{2,10},{10... | collective-permute-start | bytes 4718600 | tf_op jit(solution)/shard_map/ppermute | solution.py:577
  426.0 60.5 %collective-permute-start.37 = (bf16[1536,512]{1,0:T(8,128)(2,1)}, bf16[1536,512]{1,0:T(8,128)(2,1)}, u32[]{:S(2)}, u32[]{:S(2)}) collective-permute-start(bf16[1536,512]{1,0:T(8,128)(2,1)} %pad_maximum_fusion.7), channel_id=1, source_target_pairs={{0,16},{8,24},{16,0},{24,8},{1,17},{9,25},{17,1},{25,9},{2,18},{10... | collective-permute-start | bytes 4718600 | tf_op jit(solution)/shard_map/ppermute | solution.py:577
  427.6 38.2 %collective-permute-start.32 = (bf16[192,338]{1,0:T(8,128)(2,1)S(1)}, bf16[192,338]{1,0:T(8,128)(2,1)S(1)}, u32[]{:S(2)}, u32[]{:S(2)}) collective-permute-start(bf16[192,338]{1,0:T(8,128)(2,1)S(1)} %add_convert_fusion.11), channel_id=1, source_target_pairs={{0,8},{8,0},{16,24},{24,16},{1,9},{9,1},{17,25},{25,17},{2,10},{10... | collective-permute-start | bytes 389384 | tf_op jit(solution)/shard_map/ppermute | solution.py:577
  430.1 36.7 %collective-permute-start.25 = (bf16[192,338]{1,0:T(8,128)(2,1)S(1)}, bf16[192,338]{1,0:T(8,128)(2,1)S(1)}, u32[]{:S(2)}, u32[]{:S(2)}) collective-permute-start(bf16[192,338]{1,0:T(8,128)(2,1)S(1)} %add_convert_fusion.13), channel_id=1, source_target_pairs={{0,16},{8,24},{16,0},{24,8},{1,17},{9,25},{17,1},{25,9},{2,18},{10... | collective-permute-start | bytes 389384 | tf_op jit(solution)/shard_map/ppermute | solution.py:577
  430.5 38.5 %collective-permute-start.31 = (bf16[48,1536]{1,0:T(8,128)(2,1)S(1)}, bf16[48,1536]{1,0:T(8,128)(2,1)S(1)}, u32[]{:S(2)}, u32[]{:S(2)}) collective-permute-start(bf16[48,1536]{1,0:T(8,128)(2,1)S(1)} %add_convert_fusion.12), channel_id=1, source_target_pairs={{0,8},{8,0},{16,24},{24,16},{1,9},{9,1},{17,25},{25,17},{2,10},{10... | collective-permute-start | bytes 442376 | tf_op jit(solution)/shard_map/ppermute | solution.py:577
  465.9 5.6 %collective-permute-start.36 = (bf16[192,338]{1,0:T(8,128)(2,1)S(1)}, bf16[192,338]{1,0:T(8,128)(2,1)S(1)}, u32[]{:S(2)}, u32[]{:S(2)}) collective-permute-start(bf16[192,338]{1,0:T(8,128)(2,1)S(1)} %add_convert_fusion.8), channel_id=1, source_target_pairs={{0,8},{8,0},{16,24},{24,16},{1,9},{9,1},{17,25},{25,17},{2,10},{10... | collective-permute-start | bytes 389384 | tf_op jit(solution)/shard_map/ppermute | solution.py:577
  466.9 7.5 %collective-permute-start.30 = (bf16[192,338]{1,0:T(8,128)(2,1)S(1)}, bf16[192,338]{1,0:T(8,128)(2,1)S(1)}, u32[]{:S(2)}, u32[]{:S(2)}) collective-permute-start(bf16[192,338]{1,0:T(8,128)(2,1)S(1)} %add_convert_fusion.10), channel_id=1, source_target_pairs={{0,16},{8,24},{16,0},{24,8},{1,17},{9,25},{17,1},{25,9},{2,18},{10... | collective-permute-start | bytes 389384 | tf_op jit(solution)/shard_map/ppermute | solution.py:577
  470.0 5.8 %collective-permute-start.35 = (bf16[48,1536]{1,0:T(8,128)(2,1)S(1)}, bf16[48,1536]{1,0:T(8,128)(2,1)S(1)}, u32[]{:S(2)}, u32[]{:S(2)}) collective-permute-start(bf16[48,1536]{1,0:T(8,128)(2,1)S(1)} %add_convert_fusion.9), channel_id=1, source_target_pairs={{0,8},{8,0},{16,24},{24,16},{1,9},{9,1},{17,25},{25,17},{2,10},{10... | collective-permute-start | bytes 442376 | tf_op jit(solution)/shard_map/ppermute | solution.py:577
  472.4 23.9 %collective-permute-start.38 = (bf16[384,338]{1,0:T(8,128)(2,1)}, bf16[384,338]{1,0:T(8,128)(2,1)}, u32[]{:S(2)}, u32[]{:S(2)}) collective-permute-start(bf16[384,338]{1,0:T(8,128)(2,1)} %pad_maximum_fusion.25), channel_id=1, source_target_pairs={{0,16},{8,24},{16,0},{24,8},{1,17},{9,25},{17,1},{25,9},{2,18},{10... | collective-permute-start | bytes 778760 | tf_op jit(solution)/shard_map/ppermute | solution.py:577
  475.2 22.1 %collective-permute-start.33 = (bf16[384,338]{1,0:T(8,128)(2,1)}, bf16[384,338]{1,0:T(8,128)(2,1)}, u32[]{:S(2)}, u32[]{:S(2)}) collective-permute-start(bf16[384,338]{1,0:T(8,128)(2,1)} %pad_maximum_fusion.23), channel_id=1, source_target_pairs={{0,8},{8,0},{16,24},{24,16},{1,9},{9,1},{17,25},{25,17},{2,10},{10... | collective-permute-start | bytes 778760 | tf_op jit(solution)/shard_map/ppermute | solution.py:577
  477.3 36.0 %collective-permute-start.39 = (bf16[96,1536]{1,0:T(8,128)(2,1)}, bf16[96,1536]{1,0:T(8,128)(2,1)}, u32[]{:S(2)}, u32[]{:S(2)}) collective-permute-start(bf16[96,1536]{1,0:T(8,128)(2,1)} %pad_maximum_fusion.24), channel_id=1, source_target_pairs={{0,16},{8,24},{16,0},{24,8},{1,17},{9,25},{17,1},{25,9},{2,18},{10... | collective-permute-start | bytes 884744 | tf_op jit(solution)/shard_map/ppermute | solution.py:577
  (87 other events, 444.3 us)
Sparse Core Ops, SparseCore 0:
  11.4 47.9 all-gather.6
  61.6 42.7 all-gather.12
  106.0 45.7 all-gather.10
  226.6 42.3 reduce-scatter.3
  277.6 45.3 all-gather.8
  348.0 51.7 reduce-scatter.7
  402.1 51.6 reduce-scatter.5

commit v3 on v2

v3 whole, which is shorter than its diff:
```python
import jax
import jax.numpy as jnp
from jax import lax
from jax.experimental import pallas as pl
from jax.experimental.pallas import tpu as pltpu
from jax.sharding import PartitionSpec as P

MODEL_WIDTH = 1536
QUERY_HEADS = 24
KEY_VALUE_HEADS = 8
HEAD_GROUP = QUERY_HEADS // KEY_VALUE_HEADS
HEAD_SIZE = 64
TOPK = 8

EPS = 1e-06
THETA = 10000.0
MASK_FLOOR = -1e30

ROWS = (((0,), (0,)), ((), ()))
COLUMNS = (((1,), (1,)), ((), ()))


def dot(left, right, contract=(((1,), (0,)), ((), ()))):
    return lax.dot_general(left, right, contract, preferred_element_type=jnp.float32)


def norm_back(grad_base, base, scale):
    return scale * (grad_base - base * jnp.mean(grad_base * base, -1, keepdims=True))


def turn(rows):
    half = HEAD_SIZE // 2
    return jnp.concatenate([-rows[:, half:], rows[:, :half]], 1)


def turn_back(rows):
    half = HEAD_SIZE // 2
    return jnp.concatenate([rows[:, half:], -rows[:, :half]], 1)


def stack_heads(rows):
    return jnp.concatenate(
        [rows[:, h * HEAD_SIZE : (h + 1) * HEAD_SIZE] for h in range(HEAD_GROUP)], 0
    )


def side_heads(rows):
    block = rows.shape[0] // HEAD_GROUP
    return jnp.concatenate([rows[h * block : (h + 1) * block] for h in range(HEAD_GROUP)], 1)


def lanes(values, combine):
    total = values[:, :128]
    for start in range(128, values.shape[1], 128):
        total = combine(total, values[:, start : start + 128])
    return total


def masked_scores(stacked, keys, row_segments, key_segments, row_start, key_start):
    block = row_segments.shape[0]
    scores = dot(stacked, keys, COLUMNS) * HEAD_SIZE ** (-0.5)
    row_place = row_start + lax.broadcasted_iota(jnp.int32, (block, block), 0)
    key_place = key_start + lax.broadcasted_iota(jnp.int32, (block, block), 1)
    allowed = (row_segments == key_segments) & (key_place <= row_place)
    scores = scores.reshape(HEAD_GROUP, block, block)
    return jnp.where(allowed[None], scores, MASK_FLOOR).reshape(HEAD_GROUP * block, block)


def first_block(row_segments, segment_ref, step):
    here = jnp.max(row_segments[:1, :1])
    segments = segment_ref[...]
    number = lax.broadcasted_iota(jnp.int32, segments.shape, 0)
    return jnp.min(jnp.where((segments == here) & (number <= step), number, step))


def whole_block(*shape, grid=1, prefetch=0):
    return pl.BlockSpec(shape, lambda *i: (0,) * len(shape), pipeline_mode=pl.Buffered(1))


def attend_kernel(
    hidden_ref,
    column_ref,
    gain_ref,
    low_ref,
    high_ref,
    rate_ref,
    normed_ref,
    query_ref,
    key_ref,
    value_ref,
    mixed_ref,
    log_ref,
    cosine_ref,
    sine_ref,
    segment_ref,
    score_ref,
):
    step = pl.program_id(0)
    block = hidden_ref.shape[0]
    query_width = query_ref.shape[1]
    width = query_width + 2 * HEAD_SIZE
    here = pl.ds(pl.multiple_of(step * block, block), block)
    columns = column_ref[...].astype(jnp.float32)
    row_segments = columns[:, :1]
    segment_ref[step] = jnp.transpose(columns)[:1, :]
    angles = (columns[:, 1:2] * 64.0 + columns[:, 2:3]) * rate_ref[...]
    cosine = jnp.cos(angles)
    sine = jnp.sin(angles)
    cosine_ref[...] = cosine
    sine_ref[...] = sine
    hidden = hidden_ref[...].astype(jnp.float32)
    scale = lax.rsqrt(jnp.mean(hidden * hidden, -1, keepdims=True) + EPS)
    normed = (hidden * scale * gain_ref[...]).astype(jnp.bfloat16)
    normed_ref[...] = normed
    middle = low_ref.shape[0]
    raw = dot(normed[:, :middle], low_ref[:, :width]) + dot(
        normed[:, middle:], high_ref[:, :width]
    )
    key_raw = raw[:, query_width : query_width + HEAD_SIZE]
    key_ref[here, :] = (key_raw * cosine + turn(key_raw) * sine).astype(jnp.bfloat16)
    value_ref[here, :] = raw[:, query_width + HEAD_SIZE :].astype(jnp.bfloat16)
    query_raw = stack_heads(raw[:, :query_width])
    cosine = jnp.concatenate([cosine] * HEAD_GROUP, 0)
    sine = jnp.concatenate([sine] * HEAD_GROUP, 0)
    query = (query_raw * cosine + turn(query_raw) * sine).astype(jnp.bfloat16)
    query_ref[...] = side_heads(query)
    rows = HEAD_GROUP * block
    first = first_block(row_segments, segment_ref, step)

    def first_pass(index, top):
        there = pl.ds(pl.multiple_of(index * block, block), block)
        scores = masked_scores(
            query,
            key_ref[there, :],
            row_segments,
            segment_ref[index],
            step * block,
            index * block,
        )
        score_ref[index] = scores
        return jnp.maximum(top, lanes(scores, jnp.maximum))

    top = lax.fori_loop(
        first, step + 1, first_pass, jnp.full((rows, 128), MASK_FLOOR, jnp.float32)
    )
    top = jnp.max(top, -1, keepdims=True)

    def second_pass(index, carry):
        total, mixed = carry
        there = pl.ds(pl.multiple_of(index * block, block), block)
        weights = jnp.exp(score_ref[index] - top)
        mixed = mixed + dot(weights.astype(jnp.bfloat16), value_ref[there, :])
        return total + lanes(weights, jnp.add), mixed

    total, mixed = lax.fori_loop(
        first,
        step + 1,
        second_pass,
        (
            jnp.zeros((rows, 128), jnp.float32),
            jnp.zeros((rows, HEAD_SIZE), jnp.float32),
        ),
    )
    total = jnp.sum(total, -1, keepdims=True)
    mixed_ref[...] = side_heads((mixed / total).astype(jnp.bfloat16))
    log_ref[...] = (top + jnp.log(total)).reshape(HEAD_GROUP, block, 1)


def attend(gathered, gain, weights, block):
    tokens, features = gathered.shape[0], gain.shape[0]
    query_width = HEAD_GROUP * HEAD_SIZE
    steps = tokens // block
    half = jnp.arange(HEAD_SIZE // 2, dtype=jnp.float32)
    rate = THETA ** (-(2.0 * half) / HEAD_SIZE)
    rate = jnp.concatenate([rate, rate])[None, :]
    rows = lambda width: pl.BlockSpec((block, width), lambda i: (i, 0))
    resident = lambda *shape: pl.BlockSpec(shape, lambda i: (0,) * len(shape))
    shaped = jax.ShapeDtypeStruct
    return pl.pallas_call(
        attend_kernel,
        out_shape=(
            shaped((tokens, features), jnp.bfloat16),
            shaped((tokens, query_width), jnp.bfloat16),
            shaped((tokens, HEAD_SIZE), jnp.bfloat16),
            shaped((tokens, HEAD_SIZE), jnp.bfloat16),
            shaped((tokens, query_width), jnp.bfloat16),
            shaped((HEAD_GROUP, tokens, 1), jnp.float32),
            shaped((tokens, HEAD_SIZE), jnp.float32),
            shaped((tokens, HEAD_SIZE), jnp.float32),
            shaped((steps, 1, block), jnp.float32),
        ),
        grid=(steps,),
        in_specs=[
            rows(features),
            pl.BlockSpec((block, 128), lambda i: (i, features // 128)),
            whole_block(1, features),
            whole_block(*weights[0].shape),
            whole_block(*weights[1].shape),
            whole_block(1, HEAD_SIZE),
        ],
        out_specs=[
            rows(features),
            rows(query_width),
            resident(tokens, HEAD_SIZE),
            resident(tokens, HEAD_SIZE),
            rows(query_width),
            pl.BlockSpec((HEAD_GROUP, block, 1), lambda i: (0, i, 0)),
            rows(HEAD_SIZE),
            rows(HEAD_SIZE),
            resident(steps, 1, block),
        ],
        scratch_shapes=[pltpu.VMEM((steps, HEAD_GROUP * block, block), jnp.float32)],
        compiler_params=pltpu.CompilerParams(vmem_limit_bytes=48 << 20),
        cost_estimate=pl.CostEstimate(
            flops=6 * tokens * features * query_width,
            bytes_accessed=4 * tokens * features,
            transcendentals=tokens * tokens * HEAD_GROUP // 2,
        ),
    )(gathered, gathered, gain[None, :], *weights, rate)


def attend_back_kernel(
    query_ref,
    grad_ref,
    log_ref,
    cosine_ref,
    sine_ref,
    column_ref,
    segment_ref,
    key_ref,
    value_ref,
    key_cosine_ref,
    key_sine_ref,
    grad_query_ref,
    grad_pair_ref,
    probs_ref,
    grad_probs_ref,
    grad_key_ref,
    grad_value_ref,
):
    step = pl.program_id(0)
    block = query_ref.shape[0]
    rows = HEAD_GROUP * block

    @pl.when(step == 0)
    def _():
        grad_key_ref[...] = jnp.zeros_like(grad_key_ref)
        grad_value_ref[...] = jnp.zeros_like(grad_value_ref)

    query = stack_heads(query_ref[...])
    grad = stack_heads(grad_ref[...])
    log_total = log_ref[...].reshape(rows, 1)
    row_segments = column_ref[...].astype(jnp.float32)[:, :1]
    first = first_block(row_segments, segment_ref, step)

    def first_pass(index, delta):
        there = pl.ds(pl.multiple_of(index * block, block), block)
        scores = masked_scores(
            query,
            key_ref[there, :],
            row_segments,
            segment_ref[index],
            step * block,
            index * block,
        )
        probs = jnp.exp(scores - log_total)
        grad_probs = dot(grad, value_ref[there, :], COLUMNS)
        probs_ref[index] = probs
        grad_probs_ref[index] = grad_probs
        grad_value_ref[there, :] += dot(probs.astype(jnp.bfloat16), grad, ROWS)
        return delta + lanes(probs * grad_probs, jnp.add)

    delta = lax.fori_loop(first, step + 1, first_pass, jnp.zeros((rows, 128), jnp.float32))
    delta = jnp.sum(delta, -1, keepdims=True)

    def second_pass(index, grad_query):
        there = pl.ds(pl.multiple_of(index * block, block), block)
        grad_scores = (probs_ref[index] * (grad_probs_ref[index] - delta)).astype(jnp.bfloat16)
        grad_key_ref[there, :] += dot(grad_scores, query, ROWS)
        return grad_query + dot(grad_scores, key_ref[there, :])

    grad_query = lax.fori_loop(
        first, step + 1, second_pass, jnp.zeros((rows, HEAD_SIZE), jnp.float32)
    )
    score_scale = HEAD_SIZE ** (-0.5)
    cosine = jnp.concatenate([cosine_ref[...]] * HEAD_GROUP, 0)
    sine = jnp.concatenate([sine_ref[...]] * HEAD_GROUP, 0)
    grad_query = grad_query * score_scale
    grad_query = grad_query * cosine + turn_back(grad_query * sine)
    grad_query_ref[...] = side_heads(grad_query.astype(jnp.bfloat16))

    @pl.when(step == pl.num_programs(0) - 1)
    def _():
        grad_key = grad_key_ref[...] * score_scale
        grad_key = grad_key * key_cosine_ref[...] + turn_back(grad_key * key_sine_ref[...])
        grad_pair_ref[...] = jnp.concatenate([grad_key, grad_value_ref[...]], 1).astype(
            jnp.bfloat16
        )


def attend_back(query, grad, log_total, cosine, sine, gathered, segments, key, value):
    tokens, query_width = query.shape
    steps, _, block = segments.shape
    features = gathered.shape[1] - 128
    rows = lambda width: pl.BlockSpec((block, width), lambda i: (i, 0))
    resident = lambda *shape: pl.BlockSpec(shape, lambda i: (0,) * len(shape))
    return pl.pallas_call(
        attend_back_kernel,
        out_shape=(
            jax.ShapeDtypeStruct((tokens, query_width), jnp.bfloat16),
            jax.ShapeDtypeStruct((tokens, 2 * HEAD_SIZE), jnp.bfloat16),
        ),
        grid=(steps,),
        in_specs=[
            rows(query_width),
            rows(query_width),
            pl.BlockSpec((HEAD_GROUP, block, 1), lambda i: (0, i, 0)),
            rows(HEAD_SIZE),
            rows(HEAD_SIZE),
            pl.BlockSpec((block, 128), lambda i: (i, features // 128)),
            whole_block(steps, 1, block),
            whole_block(tokens, HEAD_SIZE),
            whole_block(tokens, HEAD_SIZE),
            whole_block(tokens, HEAD_SIZE),
            whole_block(tokens, HEAD_SIZE),
        ],
        out_specs=[rows(query_width), resident(tokens, 2 * HEAD_SIZE)],
        scratch_shapes=[
            pltpu.VMEM((steps, HEAD_GROUP * block, block), jnp.float32),
            pltpu.VMEM((steps, HEAD_GROUP * block, block), jnp.float32),
            pltpu.VMEM((tokens, HEAD_SIZE), jnp.float32),
            pltpu.VMEM((tokens, HEAD_SIZE), jnp.float32),
        ],
        compiler_params=pltpu.CompilerParams(vmem_limit_bytes=48 << 20),
        cost_estimate=pl.CostEstimate(flops=0, bytes_accessed=tokens, transcendentals=0),
    )(query, grad, log_total, cosine, sine, gathered, segments, key, value, cosine, sine)


def middle_kernel(
    mixed_ref,
    low_ref,
    high_ref,
    hidden_ref,
    column_ref,
    gain_ref,
    router_ref,
    middle_ref,
    normed_ref,
    gates_ref,
):
    groups = mixed_ref.shape[0]
    mixed = jnp.concatenate([mixed_ref[g] for g in range(groups)], 1)
    half = low_ref.shape[0]
    middle = dot(mixed[:, :half], low_ref[...]) + dot(mixed[:, half:], high_ref[...])
    middle = hidden_ref[...].astype(jnp.float32) + middle
    middle_ref[...] = middle
    scale = lax.rsqrt(jnp.mean(middle * middle, -1, keepdims=True) + EPS)
    normed = (middle * scale * gain_ref[...]).astype(jnp.bfloat16)
    normed_ref[...] = normed
    logits = dot(normed, router_ref[...])
    columns = column_ref[...].astype(jnp.float32)
    number = lax.broadcasted_iota(jnp.int32, logits.shape, 1).astype(jnp.float32)
    named = columns[:, 3:4] == number
    for slot in range(1, TOPK):
        named = named | (columns[:, 3 + slot : 4 + slot] == number)
    logits = jnp.where(named, logits, MASK_FLOOR)
    shifted = jnp.exp(logits - jnp.max(logits, -1, keepdims=True))
    shifted = jnp.where(named, shifted, 0.0)
    gates_ref[...] = shifted / jnp.sum(shifted, -1, keepdims=True)


def middle_rows(mixed, weights, gathered, gain, router, block):
    groups, tokens, width = mixed.shape
    features = gain.shape[0]
    experts = router.shape[1]
    rows = lambda columns: pl.BlockSpec((block, columns), lambda i: (i, 0))
    return pl.pallas_call(
        middle_kernel,
        out_shape=(
            jax.ShapeDtypeStruct((tokens, features), jnp.float32),
            jax.ShapeDtypeStruct((tokens, features), jnp.bfloat16),
            jax.ShapeDtypeStruct((tokens, experts), jnp.float32),
        ),
        grid=(tokens // block,),
        in_specs=[
            pl.BlockSpec((groups, block, width), lambda i: (0, i, 0)),
            whole_block(*weights[0].shape),
            whole_block(*weights[1].shape),
            rows(features),
            pl.BlockSpec((block, 128), lambda i: (i, features // 128)),
            whole_block(1, features),
            whole_block(features, experts),
        ],
        out_specs=[rows(features), rows(features), rows(experts)],
        compiler_params=pltpu.CompilerParams(vmem_limit_bytes=48 << 20),
        cost_estimate=pl.CostEstimate(
            flops=2 * tokens * features * groups * width,
            bytes_accessed=12 * tokens * features,
            transcendentals=0,
        ),
    )(mixed, *weights, gathered, gathered, gain[None, :], router)


def slot_of(e, keeps, experts_own):
    pick = experts_own // 2
    high, low = e // pick, e % pick
    return (1 - (high ^ keeps)) * pick + low


def expert_kernel(
    place_ref,
    normed_ref,
    cotangent_ref,
    column_ref,
    gates_ref,
    gate_weight_ref,
    up_weight_ref,
    down_weight_ref,
    scaled_one_ref,
    scaled_two_ref,
    grad_gate_ref,
    grad_up_ref,
    grad_live_ref,
    extra_ref,
):
    experts_own = gate_weight_ref.shape[0]
    experts_all = gates_ref.shape[1]
    first = place_ref[1] * experts_own
    normed = normed_ref[...]
    live = column_ref[...].astype(jnp.float32)[:, :1] > 0
    grad_live = jnp.where(live, cotangent_ref[...], jnp.zeros((), jnp.bfloat16))
    grad_live_ref[...] = grad_live
    gates = gates_ref[...]
    number = lax.broadcasted_iota(jnp.int32, gates.shape, 1)
    grad_gates = jnp.zeros(gates.shape, jnp.float32)
    for e in range(experts_own):
        one = slot_of(e, place_ref[2], experts_own)
        two = slot_of(e, place_ref[3], experts_own)
        gate = jnp.sum(jnp.where(number == first + e, gates, 0.0), -1, keepdims=True)
        gate_pre = dot(normed, gate_weight_ref[e])
        up_pre = dot(normed, up_weight_ref[e])
        grad_plain = dot(grad_live, down_weight_ref[e], COLUMNS)
        sigma = jax.nn.sigmoid(gate_pre)
        silu = gate_pre * sigma
        acted = silu * up_pre
        grad_gates = grad_gates + jnp.where(
            number == first + e, jnp.sum(acted * grad_plain, -1, keepdims=True), 0.0
        )
        grad_acted = gate * grad_plain
        scaled = (gate * acted).astype(jnp.bfloat16)
        scaled_one_ref[one] = scaled
        scaled_two_ref[two] = scaled
        grad_gate_ref[one] = (
            grad_acted * up_pre * (sigma * (1.0 + gate_pre * (1.0 - sigma)))
        ).astype(jnp.bfloat16)
        grad_up_ref[two] = (grad_acted * silu).astype(jnp.bfloat16)
    rough = grad_gates.astype(jnp.bfloat16)
    fine = (grad_gates - rough.astype(jnp.float32)).astype(jnp.bfloat16)
    rest = jnp.zeros((gates.shape[0], extra_ref.shape[1] - 2 * experts_all), jnp.bfloat16)
    extra_ref[...] = jnp.concatenate([rough, fine, rest], 1)


def expert_rows(place, normed, cotangent, gathered, gates, w_gate, w_up, w_down):
    tokens, features = normed.shape
    experts_own, _, hidden = w_gate.shape
    experts_all = gates.shape[1]
    chips, block, _ = cotangent.shape
    rows = lambda columns: pl.BlockSpec((block, columns), lambda i, p: (i, 0))
    spread = pl.BlockSpec((experts_own, block, hidden), lambda i, p: (0, i, 0))
    wide = jax.ShapeDtypeStruct((experts_own, tokens, hidden), jnp.bfloat16)
    return pl.pallas_call(
        expert_kernel,
        out_shape=(
            wide,
            wide,
            wide,
            wide,
            jax.ShapeDtypeStruct((tokens, features), jnp.bfloat16),
            jax.ShapeDtypeStruct((tokens, 128), jnp.bfloat16),
        ),
        grid_spec=pltpu.PrefetchScalarGridSpec(
            num_scalar_prefetch=1,
            grid=(chips,),
            in_specs=[
                rows(features),
                pl.BlockSpec(
                    (None, block, features), lambda i, p: (lax.rem(i - p[0] + chips, chips), 0, 0)
                ),
                pl.BlockSpec((block, 128), lambda i, p: (i, features // 128)),
                rows(experts_all),
                whole_block(*w_gate.shape),
                whole_block(*w_up.shape),
                whole_block(*w_down.shape),
            ],
            out_specs=[spread, spread, spread, spread, rows(features), rows(128)],
        ),
        compiler_params=pltpu.CompilerParams(vmem_limit_bytes=52 << 20),
        cost_estimate=pl.CostEstimate(
            flops=6 * tokens * features * hidden * experts_own,
            bytes_accessed=6 * features * hidden * experts_own + 10 * tokens * features,
            transcendentals=tokens * hidden * experts_own,
        ),
    )(place, normed, cotangent, gathered, gates, w_gate, w_up, w_down)


def product_kernel(left_ref, right_ref, scaled_ref, live_ref, out_ref):
    step = pl.program_id(0)
    tile, hidden = left_ref.shape[1], right_ref.shape[1]
    tops = pl.num_programs(0) - 3
    top = tops * tile

    @pl.when(step < tops)
    def _():
        out_ref[pl.ds(pl.multiple_of(step * tile, tile), tile), :] = dot(
            left_ref[...], right_ref[...], ROWS
        ).astype(out_ref.dtype)

    for part in range(3):

        @pl.when(step == tops + part)
        def _():
            product = dot(scaled_ref[...], live_ref[...], ROWS).astype(out_ref.dtype)
            if part < 2:
                out_ref[top : top + hidden, part * tile : (part + 1) * tile] = product
            else:
                out_ref[top + hidden :, :tile] = product[:tile]
                out_ref[top + hidden :, tile:] = product[tile:]


def expert_product(left, right, scaled, live, side, dtype):
    tokens, features = left.shape
    hidden = right.shape[1]
    tile = hidden // 2
    tops = features // tile
    return pl.pallas_call(
        product_kernel,
        out_shape=jax.ShapeDtypeStruct((features + features // 2, hidden), dtype),
        grid=(tops + 3,),
        in_specs=[
            pl.BlockSpec((tokens, tile), lambda i: (0, jnp.minimum(i, tops - 1))),
            whole_block(tokens, hidden),
            whole_block(tokens, hidden),
            pl.BlockSpec((tokens, tile), lambda i: (0, 3 * side + jnp.maximum(i - tops, 0))),
        ],
        out_specs=pl.BlockSpec((features + features // 2, hidden), lambda i: (0, 0)),
        compiler_params=pltpu.CompilerParams(vmem_limit_bytes=40 << 20),
        cost_estimate=pl.CostEstimate(
            flops=3 * tokens * features * hidden,
            bytes_accessed=4 * tokens * features,
            transcendentals=0,
        ),
    )(left, right, scaled, live)


def split_product(value):
    features = value.shape[1] * 2 // 3
    hidden = value.shape[2]
    tile = hidden // 2
    low = value[:, features:]
    down = jnp.concatenate(
        [
            low[:, :hidden],
            jnp.concatenate([low[:, hidden:, :tile], low[:, hidden:, tile:]], 1),
        ],
        2,
    )
    return value[:, :features], down


def rows_kernel(
    place_ref,
    scaled_ref,
    grad_gate_ref,
    grad_up_ref,
    extra_ref,
    gate_weight_ref,
    up_weight_ref,
    down_weight_ref,
    grad_ref,
    out_ref,
):
    experts_own = scaled_ref.shape[0]
    features = out_ref.shape[1]
    one = [slot_of(e, place_ref[2], experts_own) for e in range(experts_own)]
    two = [slot_of(e, place_ref[3], experts_own) for e in range(experts_own)]
    for start in range(0, features, 256):
        part = slice(start, start + 256)
        grad = 0.0
        out = 0.0
        for e in range(experts_own):
            grad = grad + dot(grad_gate_ref[one[e]], gate_weight_ref[e, part, :], COLUMNS)
            grad = grad + dot(grad_up_ref[two[e]], up_weight_ref[e, part, :], COLUMNS)
            out = out + dot(scaled_ref[one[e]], down_weight_ref[e, :, part])
        grad_ref[:, part] = grad.astype(jnp.bfloat16)
        out_ref[:, part] = out.astype(jnp.bfloat16)
    grad_ref[:, features:] = extra_ref[...]


def expert_sums(place, scaled, grad_gate_pre, grad_up_pre, extra, w_gate, w_up, w_down, block):
    experts_own, tokens, hidden = scaled.shape
    features = w_gate.shape[1]
    rows = lambda columns: pl.BlockSpec((block, columns), lambda i, p: (i, 0))
    spread = pl.BlockSpec((experts_own, block, hidden), lambda i, p: (0, i, 0))
    return pl.pallas_call(
        rows_kernel,
        out_shape=(
            jax.ShapeDtypeStruct((tokens, features + extra.shape[1]), jnp.bfloat16),
            jax.ShapeDtypeStruct((tokens, features), jnp.bfloat16),
        ),
        grid_spec=pltpu.PrefetchScalarGridSpec(
            num_scalar_prefetch=1,
            grid=(tokens // block,),
            in_specs=[
                spread,
                spread,
                spread,
                rows(extra.shape[1]),
                whole_block(*w_gate.shape),
                whole_block(*w_up.shape),
                whole_block(*w_down.shape),
            ],
            out_specs=[rows(features + extra.shape[1]), rows(features)],
        ),
        compiler_params=pltpu.CompilerParams(vmem_limit_bytes=52 << 20),
        cost_estimate=pl.CostEstimate(flops=0, bytes_accessed=tokens, transcendentals=0),
    )(place, scaled, grad_gate_pre, grad_up_pre, extra, w_gate, w_up, w_down)


def turn_kernel(
    sum_ref,
    gates_ref,
    router_ref,
    gain_ref,
    middle_ref,
    live_ref,
    low_ref,
    high_ref,
    grad_middle_ref,
    branch_ref,
    mixed_ref,
    logits_ref,
    gain_grad_ref,
):
    features = middle_ref.shape[1]
    experts = gates_ref.shape[1]
    groups, _, width = mixed_ref.shape
    extra = sum_ref[:, features:].astype(jnp.float32)
    grad_gates = extra[:, :experts] + extra[:, experts : 2 * experts]
    gates = gates_ref[...]
    grad_logits = gates * (grad_gates - jnp.sum(gates * grad_gates, -1, keepdims=True))
    grad_logits = grad_logits.astype(jnp.bfloat16)
    logits_ref[...] = grad_logits
    grad = sum_ref[:, :features].astype(jnp.float32) + dot(grad_logits, router_ref[...], COLUMNS)
    middle = middle_ref[...]
    scale = lax.rsqrt(jnp.mean(middle * middle, -1, keepdims=True) + EPS)
    base = middle * scale
    gain_grad_ref[...] = jnp.sum(grad * base, 0, keepdims=True)
    grad_middle = live_ref[...].astype(jnp.float32) + norm_back(grad * gain_ref[...], base, scale)
    grad_middle_ref[...] = grad_middle
    branch = grad_middle.astype(jnp.bfloat16)
    branch_ref[...] = branch
    for half, weight_ref in enumerate((low_ref, high_ref)):
        mixed = dot(branch, weight_ref[...], COLUMNS).astype(jnp.bfloat16)
        for g in range(groups // 2):
            mixed_ref[half * (groups // 2) + g] = mixed[:, g * width : (g + 1) * width]


def turn_rows(sums, gates, router, gain, middle, live, weights):
    own, features = middle.shape
    experts = gates.shape[1]
    groups = KEY_VALUE_HEADS
    shaped = jax.ShapeDtypeStruct
    return pl.pallas_call(
        turn_kernel,
        out_shape=(
            shaped((own, features), jnp.float32),
            shaped((own, features), jnp.bfloat16),
            shaped((groups, own, features // groups), jnp.bfloat16),
            shaped((own, experts), jnp.bfloat16),
            shaped((1, features), jnp.float32),
        ),
        compiler_params=pltpu.CompilerParams(vmem_limit_bytes=32 << 20),
        cost_estimate=pl.CostEstimate(flops=0, bytes_accessed=own, transcendentals=0),
    )(sums, gates, router, gain[None, :], middle, live, *weights)


def close_kernel(
    query_ref, pair_ref, weight_ref, hidden_ref, normed_ref, grad_ref, product_ref, gain_grad_ref
):
    step = pl.program_id(0)
    width = query_ref.shape[1]
    both = width + pair_ref.shape[1]
    query = query_ref[...]
    pair = pair_ref[...]
    grad = dot(query, weight_ref[:, :width], COLUMNS) + dot(
        pair, weight_ref[:, width:both], COLUMNS
    )
    grad_ref[...] = grad.astype(jnp.bfloat16)
    hidden = hidden_ref[...].astype(jnp.float32)
    scale = lax.rsqrt(jnp.mean(hidden * hidden, -1, keepdims=True) + EPS)
    gain_grad = jnp.sum(grad * (hidden * scale), 0, keepdims=True)
    normed = normed_ref[...]

    @pl.when(step == 0)
    def _():
        gain_grad_ref[...] = jnp.zeros_like(gain_grad_ref)
        product_ref[...] = jnp.zeros_like(product_ref)

    gain_grad_ref[...] += gain_grad
    product_ref[:, :width] += dot(normed, query, ROWS)
    product_ref[:, width:] += dot(normed, pair, ROWS)


def close_rows(query, pair, weight, gathered, normed, block):
    tokens, features = normed.shape
    both = query.shape[1] + pair.shape[1]
    rows = lambda width: pl.BlockSpec((block, width), lambda i: (i, 0))
    resident = lambda *shape: pl.BlockSpec(shape, lambda i: (0,) * len(shape))
    shaped = jax.ShapeDtypeStruct
    return pl.pallas_call(
        close_kernel,
        out_shape=(
            shaped((tokens, features), jnp.bfloat16),
            shaped((features, both), jnp.float32),
            shaped((1, features), jnp.float32),
        ),
        grid=(tokens // block,),
        in_specs=[
            rows(query.shape[1]),
            rows(pair.shape[1]),
            whole_block(*weight.shape),
            rows(features),
            rows(features),
        ],
        out_specs=[rows(features), resident(features, both), resident(1, features)],
        compiler_params=pltpu.CompilerParams(vmem_limit_bytes=40 << 20),
        cost_estimate=pl.CostEstimate(flops=0, bytes_accessed=tokens, transcendentals=0),
    )(query, pair, weight, gathered, normed)


def after(values, *others):
    values, _ = lax.optimization_barrier((values, others))
    return values


def swap(value, bit):
    size = lax.axis_size("rep")
    return lax.ppermute(value, "rep", [(i, i ^ bit) for i in range(size)])


def has(bit):
    return (lax.axis_index("rep") & bit) != 0


def halve(value, came, bit):
    half = value.shape[0] // 2
    keep = jnp.where(has(bit), half, 0)
    part = lambda array, start: lax.dynamic_slice_in_dim(array, start, half, 0).astype(jnp.float32)
    kept = part(value, keep)
    sent = part(value, half - keep)
    if came is not None:
        kept = kept + part(came, keep)
        sent = sent + part(came, half - keep)
    return kept, sent.astype(jnp.bfloat16)


def join(value, came, bit, axis):
    upper = has(bit)
    return jnp.concatenate(
        [jnp.where(upper, came, value), jnp.where(upper, value, came)], axis
    )


class Chain:
    def __init__(self, order):
        self.order = order
        self.stage = 0
        self.steps = 2 * len(order)

    def send(self, sent):
        bit = self.order[min(self.stage, self.steps - 1 - self.stage)]
        self.sent = sent
        self.flying = swap(sent, bit)
        self.stage += 1

    def start(self, value):
        self.kept, sent = halve(value, None, self.order[0])
        self.send(sent)
        return self.sent

    def total(self, *others):
        return self.kept + after(self.flying, *others).astype(jnp.float32)

    def step(self, *others):
        bits = len(self.order)
        if self.stage < bits:
            came = after(self.flying, *others)
            self.kept, sent = halve(self.kept, came, self.order[self.stage])
            self.send(sent)
        elif self.stage == bits:
            self.send(self.total(*others).astype(jnp.bfloat16))
        else:
            came = after(self.flying, *others)
            self.send(join(self.sent, came, self.order[self.steps - self.stage], 0))
        return self.sent

    def finish(self, *others):
        return join(self.sent, after(self.flying, *others), self.order[0], 0)


class Exchange:
    def __init__(self, fetched, bits):
        size = fetched.shape[0]
        fetched = fetched.reshape((size,) + (1,) * len(bits) + fetched.shape[1:])
        self.values = [fetched[: size // 2], fetched[size // 2 :]]
        self.orders = (bits, bits[::-1])
        self.stage = 0
        self.fly()

    def fly(self):
        self.flying = [
            swap(value, order[self.stage]) for value, order in zip(self.values, self.orders)
        ]

    def step(self, *others):
        bits = len(self.orders[0])
        for h, order in enumerate(self.orders):
            bit = order[self.stage]
            came = after(self.flying[h], *others)
            self.values[h] = join(self.values[h], came, bit, bits - (bit.bit_length() - 1))
        self.stage += 1
        if self.stage < bits:
            self.fly()
        return list(self.values)

    def finish(self, *others):
        while self.stage < len(self.orders[0]):
            self.step(*others)
        return [value.reshape(-1, value.shape[-1]) for value in self.values]


def per_device(
    inputs,
    segments,
    positions,
    expert_ids,
    attn_gain,
    w_query,
    key_weight,
    value_weight,
    w_out,
    ffn_gain,
    router,
    w_gate,
    w_up,
    w_down,
    grad_out,
):
    size = lax.axis_size("ctx")
    me = lax.axis_index("ctx")
    reps = lax.axis_size("rep")
    bits = [1 << i for i in range(reps.bit_length() - 1)]
    own = inputs.shape[1]
    tokens = size * own
    groups = KEY_VALUE_HEADS
    copies = size // groups
    query_width = HEAD_GROUP * HEAD_SIZE
    width = query_width + 2 * HEAD_SIZE
    copy_index = me % copies
    rows_own = w_out.shape[0]
    experts_own = w_gate.shape[0]
    experts_all = size * experts_own
    block = 2 * own
    chips = size // 2
    chip = me // 2
    odd = me % 2 == 1
    share = rows_own // reps
    share_start = lax.axis_index("rep") * share

    columns = jnp.concatenate(
        [
            segments[0][:, None],
            positions[0][:, None] // 64,
            positions[0][:, None] % 64,
            expert_ids[0],
        ],
        1,
    ).astype(jnp.bfloat16)
    columns = jnp.pad(columns, ((0, 0), (0, 128 - columns.shape[1])))
    gathered = lax.all_gather(
        jnp.concatenate([inputs[0], columns], 1), "ctx", axis=0, tiled=True
    )

    def from_chip(value, k):
        return lax.ppermute(value, "ctx", [(i, (i - 2 * k) % size) for i in range(size)])

    def from_core(value):
        return lax.ppermute(value, "ctx", [(i, i ^ 1) for i in range(size)])

    def cores(mine, others, axis):
        return jnp.concatenate(
            [jnp.where(odd, others, mine), jnp.where(odd, mine, others)], axis
        )

    shared = lambda array: lax.dynamic_slice_in_dim(array, share_start, share, 0)
    side_width = -(-(width + 2 + router.shape[1]) // 128) * 128
    head_columns = jnp.concatenate(
        [
            shared(w_query).reshape(share, groups, query_width),
            shared(key_weight).reshape(share, groups, HEAD_SIZE),
            shared(value_weight).reshape(share, groups, HEAD_SIZE),
            jnp.broadcast_to(shared(attn_gain)[:, None, None], (share, groups, 1)),
            jnp.broadcast_to(shared(ffn_gain)[:, None, None], (share, groups, 1)),
            jnp.broadcast_to(shared(router)[:, None, :], (share, groups, router.shape[1])),
        ],
        -1,
    )
    used = head_columns.shape[-1]
    head_columns = jnp.pad(head_columns, ((0, 0), (0, 0), (0, side_width - used)))
    head_columns = jnp.repeat(jnp.transpose(head_columns, (1, 0, 2)), copies, 0)
    head_columns = head_columns.reshape(chips, 2, share, side_width)
    out_share = shared(w_out)
    parcels = []
    for k in range(chips):
        to = head_columns[(chip - k) % chips]
        parcel = jnp.concatenate([out_share, to[0], to[1]], 1)
        parcels.append(from_chip(parcel, k) if k else parcel)
    parcels = jnp.stack(parcels)
    out_part = parcels[:, :, :MODEL_WIDTH]
    heads = [
        parcels[:, :, MODEL_WIDTH : MODEL_WIDTH + side_width],
        parcels[:, :, MODEL_WIDTH + side_width :],
    ]
    for_core = jnp.where(odd, heads[0], heads[1])
    mine_part = jnp.concatenate([out_part, jnp.where(odd, heads[1], heads[0])], 2)
    core_part = from_core(jnp.concatenate([out_part, for_core], 2))
    fetched = cores(mine_part[:, None], core_part[:, None], 1)
    fetched = lax.dynamic_slice_in_dim(
        jnp.concatenate([fetched, fetched], 0), (chips - chip) % chips, chips, 0
    ).reshape(size, share, MODEL_WIDTH + side_width)
    head_exchange = Exchange(fetched[:, :, MODEL_WIDTH:], bits)
    out_exchange = Exchange(fetched[:, :, :MODEL_WIDTH], bits)
    head_halves = head_exchange.finish()
    ready = out_exchange.step(*head_halves)
    head_all = jnp.concatenate(head_halves, 0)
    gain_one = head_all[:, width].astype(jnp.float32)
    gain_two = head_all[:, width + 1].astype(jnp.float32)
    router_all = head_all[:, width + 2 : used]

    (
        normed_one,
        query,
        key,
        value,
        mixed,
        log_total,
        cosine_table,
        sine_table,
        segment_rows,
    ) = attend(after(gathered, *ready), gain_one, head_halves, block)

    turned = after(grad_out[0], gathered, *ready)
    turned = jnp.stack([turned] + [from_chip(turned, k) for k in range(1, chips)])
    part = tokens // copies
    mixed_all = lax.all_gather(
        lax.dynamic_slice_in_dim(mixed, copy_index * part, part, 0), "ctx", axis=0
    ).reshape(groups, tokens, query_width)
    w_out_halves = out_exchange.finish(mixed)
    cotangent = cores(turned, from_core(turned), 1)

    middle, normed_two, gates = middle_rows(
        mixed_all, after(w_out_halves, cotangent), gathered, gain_two, router_all, block
    )
    flag = lambda bit: has(bit).astype(jnp.int32)
    place = jnp.stack([chip, me, flag(bits[0]), flag(bits[-1])]).astype(jnp.int32)
    scaled_one, scaled_two, grad_gate_pre, grad_up_pre, grad_live, extra = expert_rows(
        place, normed_two, cotangent, gathered, gates, w_gate, w_up, w_down
    )

    pick = experts_own // 2

    def product(side, start, dtype):
        right, scaled = ((grad_gate_pre, scaled_one), (grad_up_pre, scaled_two))[side]
        parts = [
            expert_product(normed_two, right[e], scaled[e], grad_live, side, dtype)
            for e in range(start, start + pick)
        ]
        return parts[0] if pick == 1 else jnp.concatenate(parts, 0)

    chains = [Chain(bits), Chain(bits[::-1])]
    for side, chain in enumerate(chains):
        chain.send(product(side, 0, jnp.bfloat16))
    grad_rows, out_rows = expert_sums(
        place,
        *after((scaled_one, grad_gate_pre, grad_up_pre), *[chain.sent for chain in chains]),
        extra,
        w_gate,
        w_up,
        w_down,
        block,
    )
    grad_two_sum = lax.psum_scatter(grad_rows, "ctx", scatter_dimension=0, tiled=True)
    scaled_one, scaled_two, grad_gate_pre, grad_up_pre = after(
        (scaled_one, scaled_two, grad_gate_pre, grad_up_pre), grad_rows
    )
    for side, chain in enumerate(chains):
        chain.kept = product(side, pick, jnp.float32)

    def mine(array):
        return lax.dynamic_slice_in_dim(array, me * own, own, 0)

    sent = [c.kept for c in chains]
    while chains[0].stage < len(bits):
        sent = [chain.step(*sent) for chain in chains]
    middle_own, gates_own, live_own = mine(middle), mine(gates), mine(grad_live)
    grad_middle, grad_branch, grad_mixed, grad_logits, gain_two_grad = turn_rows(
        after(grad_two_sum, *sent),
        gates_own,
        router_all,
        gain_two,
        middle_own,
        live_own,
        w_out_halves,
    )
    grad_mixed_all = lax.all_to_all(
        jnp.repeat(grad_mixed, copies, 0), "ctx", split_axis=0, concat_axis=0, tiled=True
    ).reshape(tokens, query_width)
    grad_branch_all = lax.all_gather(grad_branch, "ctx", axis=0, tiled=True)

    sent = [chain.step(grad_mixed) for chain in chains]
    grad_query, grad_pair = attend_back(
        query,
        after(grad_mixed_all, *sent),
        log_total,
        cosine_table,
        sine_table,
        gathered,
        segment_rows,
        key,
        value,
    )
    if copies > 1:
        places = jnp.arange(tokens, dtype=jnp.int32)
        counted = (places // part == copy_index)[:, None]
        grad_query = jnp.where(counted, grad_query, jnp.zeros((), jnp.bfloat16))
        grad_pair = jnp.where(counted, grad_pair, jnp.zeros((), jnp.bfloat16))
    grad_one_low, head_product, gain_one_grad = close_rows(
        grad_query, grad_pair, head_all, gathered, normed_one, block
    )
    grad_one = lax.psum_scatter(
        grad_one_low, "ctx", scatter_dimension=0, tiled=True
    ).astype(jnp.float32)
    head_grads = jnp.concatenate(
        [
            head_product,
            gain_one_grad.reshape(-1, 1),
            gain_two_grad.reshape(-1, 1),
            dot(mine(normed_two), grad_logits, ROWS),
        ],
        1,
    )

    spread = head_grads.reshape((size,) + (2,) * len(bits) + (share, used))
    axes = list(range(1, len(bits) + 1))
    head_chains = [Chain(bits), Chain(bits[::-1])]
    sent = []
    for h, chain in enumerate(head_chains):
        part_grads = spread[h * (size // 2) : (h + 1) * (size // 2)]
        lead = axes[::-1] if h == 0 else axes
        part_grads = jnp.transpose(part_grads, lead + [0, len(bits) + 1, len(bits) + 2])
        sent.append(chain.start(part_grads.reshape(-1, used)))

    sent = [chain.step(*sent) for chain in chains]
    grad_proj_out = dot(
        lax.dynamic_slice_in_dim(mixed, copy_index * rows_own, rows_own, 1),
        after(grad_branch_all, *sent),
        ROWS,
    )
    while head_chains[0].stage < len(bits):
        sent = [chain.step(*sent) for chain in head_chains]
    totals = [chain.total(*sent) for chain in head_chains]
    totals = jnp.concatenate(
        [total.reshape(size // 2, share, used) for total in totals], 0
    ).astype(jnp.bfloat16)
    head_sums = lax.all_to_all(totals, "ctx", split_axis=0, concat_axis=0, tiled=True)
    out_chain = Chain(bits[::-1])
    out_sent = out_chain.start(after(grad_proj_out, totals))
    while out_chain.stage < len(bits):
        out_sent = out_chain.step(out_sent)
    back = Exchange(after(head_sums, out_sent), bits)
    out_chain.step(*back.values)
    while out_chain.stage < out_chain.steps:
        ready = back.step(out_chain.sent) if back.stage < len(bits) - 1 else []
        out_chain.step(*ready)
    halves = back.finish(out_chain.sent)
    head_rows = jnp.concatenate(halves, 0).reshape(size, rows_own, used).astype(jnp.float32)
    if copies > 1:
        head_rows = jnp.sum(head_rows.reshape(groups, copies, rows_own, used), 1)
    side = lambda begin, end: jnp.transpose(head_rows[:, :, begin:end], (1, 0, 2)).reshape(
        rows_own, -1
    )
    small = jnp.sum(head_rows[:, :, width:], 0)
    head_outs = (
        side(0, query_width),
        side(query_width, query_width + HEAD_SIZE),
        side(query_width + HEAD_SIZE, width),
    )
    grad_out_rows = out_chain.finish(*head_outs).astype(jnp.float32)
    while chains[0].stage < chains[0].steps:
        sent = [chain.step(grad_out_rows) for chain in chains]
    expert_parts = []
    for chain in chains:
        value = chain.finish(grad_out_rows, *head_outs)
        expert_parts.append(split_product(value.reshape(experts_own, -1, value.shape[1])))
    grad_gate, grad_up = [parts[0].astype(jnp.float32) for parts in expert_parts]
    grad_down = jnp.concatenate([parts[1] for parts in expert_parts], 2).astype(jnp.float32)

    moe_sum = lax.psum_scatter(
        after(out_rows, grad_branch), "ctx", scatter_dimension=0, tiled=True
    ).astype(jnp.float32)
    output = jnp.where((segments[0] != 0)[:, None], middle_own + moe_sum, 0.0)
    own_hidden = inputs[0].astype(jnp.float32)
    own_scale = lax.rsqrt(jnp.mean(own_hidden * own_hidden, -1, keepdims=True) + EPS)
    grad_in = grad_middle + norm_back(grad_one * gain_one, own_hidden * own_scale, own_scale)

    return (
        output.astype(jnp.bfloat16)[None],
        grad_in[None],
        small[:, 0],
        *head_outs,
        grad_out_rows,
        small[:, 1],
        small[:, 2:],
        grad_gate,
        grad_up,
        grad_down,
    )


def solution(mesh):
    return jax.shard_map(
        per_device,
        mesh=mesh,
        in_specs=(
            P("rep", "ctx", None),
            P("rep", "ctx"),
            P("rep", "ctx"),
            P("rep", "ctx", None),
            P("ctx"),
            P("ctx", None),
            P("ctx", None),
            P("ctx", None),
            P("ctx", None),
            P("ctx"),
            P("ctx", None),
            P("ctx", None, None),
            P("ctx", None, None),
            P("ctx", None, None),
            P("rep", "ctx", None),
        ),
        out_specs=(
            P("rep", "ctx", None),
            P("rep", "ctx", None),
            P("ctx"),
            P("ctx", None),
            P("ctx", None),
            P("ctx", None),
            P("ctx", None),
            P("ctx"),
            P("ctx", None),
            P("ctx", None, None),
            P("ctx", None, None),
            P("ctx", None, None),
        ),
        check_vma=False,
    )
```

time: 531 us -> 561 us (1.056)
  matrix products: 41.8 us -> 4.07 us
  waiting for transfers between devices: 163 us -> 199 us
  Pallas kernels: 72.6 us -> 104 us
  local copies, waits for them, and re-layouts: 48.2 us -> 78.8 us
  other arithmetic: 93.4 us -> 65.4 us
  blocking collectives: 22.1 us -> 0 us
  starting transfers between devices: 66.3 us -> 84.8 us
    ppermute x4 -> x8, waiting for transfers between devices: 11.2 us -> 53.8 us  [the longest x6 51.6 us: from_chip(): lax.ppermute(value, 'ctx', [(i, (i - 2 * k) % size) for i in range(size)])]
    dot_general x17 -> x2, matrix products: 41.8 us -> 4.07 us  [dot(): lax.dot_general(left, right, contract, preferred_element_type=jnp.float32)]
    pallas_call x2 -> x8, Pallas kernels: 32.6 us -> 62.7 us  [the longest x4 19.7 us: expert_product(): pl.pallas_call(product_kernel, out_shape=jax.ShapeDtypeStruct((features +...]
    ppermute x36 -> x28, waiting for transfers between devices: 102 us -> 130 us  [swap(): return lax.ppermute(value, 'rep', [(i, i ^ bit) for i in range(size)])]
    ppermute x4 -> x8, starting transfers between devices: 2.14 us -> 26.2 us  [the longest x6 26 us: from_chip(): lax.ppermute(value, 'ctx', [(i, (i - 2 * k) % size) for i in range(size)])]
    all_to_all x1 -> x0, blocking collectives: 22.1 us -> none  [per_device(): lax.all_to_all(head_columns, 'ctx', split_axis=0, concat_axis=0, tiled=True)]
    reduce_scatter x1, waiting for transfers between devices: 21.2 us -> 0.01 us  [per_device(): lax.psum_scatter(grad_rows, 'ctx', scatter_dimension=0, tiled=True)]
    all_to_all x2, waiting for transfers between devices: 20.5 us -> 0.01 us  [the longest x1 0.01 us: per_device(): lax.all_to_all(jnp.repeat(grad_mixed, copies, 0), 'ctx', split_axis=0, co...]
  transfers between devices with their start and end apart: 49 -> 44, of which waited for: 18 -> 21; matrix products, arithmetic and copies ran while one was open for 26% -> 18% of each run, Pallas kernels for 5% -> 5%
where the time goes in v3:
time: 561 us; the launch traced here: 553 us
  waiting for transfers between devices  199 us (35%)
  Pallas kernels  104 us (19%)
  starting transfers between devices  84.8 us (15%)
  local copies, waits for them, and re-layouts  78.8 us (14%)
  other arithmetic  65.4 us (12%)
  between operations  15.9 us (3%)
    ppermute x28, waiting for transfers between devices, swap(): return lax.ppermute(value, 'rep', [(i, i ^ bit) for i in range(size)])  130 us
    ppermute x6, waiting for transfers between devices, from_chip(): lax.ppermute(value, 'ctx', [(i, (i - 2 * k) % size) for i in range(size)])  51.6 us
    unnamed x163, local copies, waits for them, and re-layouts  39.9 us
    ppermute x28, starting transfers between devices, swap(): return lax.ppermute(value, 'rep', [(i, i ^ bit) for i in range(size)])  36.6 us
    ppermute x6, starting transfers between devices, from_chip(): lax.ppermute(value, 'ctx', [(i, (i - 2 * k) % size) for i in range(size)])  26 us
    pallas_call x4, Pallas kernels, expert_product(): pl.pallas_call(product_kernel, out_shape=jax.ShapeDtypeStruct((features +...  19.7 us
    pallas_call x1, Pallas kernels, expert_rows(): pl.pallas_call(expert_kernel, out_shape=(wide, wide, wide, wide, jax.Shap...  18.9 us
    pallas_call x1, Pallas kernels, expert_sums(): pl.pallas_call(rows_kernel, out_shape=(jax.ShapeDtypeStruct((tokens, feat...  16.6 us
  transfers between devices with their start and end apart: 44, of which 21 were waited for; matrix products, arithmetic and copies ran while one was open for 18% of the time, Pallas kernels for 5%

profile of v3, /device:TPU:0, one launch (start us, length us, event | category | flops | bytes accessed | tf_op | source)
XLA Modules:
  0.0 552.7 jit_solution(15364195286931506694)
XLA Ops:
  12.0 3.1 collective-permute-start.2
  15.1 2.6 collective-permute-start.1
  20.1 3.4 collective-permute-done.2
  23.5 13.0 %collective-permute-done.1 = bf16[48,2304]{1,0:T(8,128)(2,1)S(1)} collective-permute-done((bf16[48,2304]{1,0:T(8,128)(2,1)S(1)}, bf16[48,2304]{1,0:T(8,128)(2,1)S(1)}, u32[]{:S(2)}, u32[]{:S(2)}) %collective-permute-start.1) | collective-permute-done | bytes 221216 | tf_op jit(solution)/shard_map/ppermute | solution.py:895
  43.5 2.7 collective-permute-done.7
  52.0 5.6 %collective-permute-done.6 = bf16[4,1,2,48,384]{4,3,0,2,1:T(8,128)(2,1)S(1)} collective-permute-done((bf16[4,1,2,48,384]{4,3,0,2,1:T(8,128)(2,1)S(1)}, bf16[4,1,2,48,384]{4,3,0,2,1:T(8,128)(2,1)S(1)}, u32[]{:S(2)}, u32[]{:S(2)}) %collective-permute-start.6) | collective-permute-done | bytes 294944 | tf_op jit(solution)/shard_map/ppermute | solution.py:748
  57.9 12.1 %collective-permute-done.8 = bf16[4,2,1,48,384]{4,3,0,2,1:T(8,128)(2,1)S(1)} collective-permute-done((bf16[4,2,1,48,384]{4,3,0,2,1:T(8,128)(2,1)S(1)}, bf16[4,2,1,48,384]{4,3,0,2,1:T(8,128)(2,1)S(1)}, u32[]{:S(2)}, u32[]{:S(2)}) %collective-permute-start.8) | collective-permute-done | bytes 294944 | tf_op jit(solution)/shard_map/ppermute | solution.py:748
  75.1 15.5 %shard_map.238 = (bf16[1024,1536]{1,0:T(8,128)(2,1)}, bf16[1024,192]{1,0:T(8,128)(2,1)S(1)}, bf16[1024,64]{1,0:T(8,128)(2,1)S(1)}, bf16[1024,64]{1,0:T(8,128)(2,...) custom-call(bf16[1024,1664]{1,0:T(8,128)(2,1)} %all-gather.5.cloned., ...), custom_call_target="tpu_custom_call" | custom-call | flops 1811939328 | bytes 6291456 | tf_op jit(solution)/shard_map/pallas_call | solution.py:179
  97.0 16.6 %collective-permute-start.14 = (bf16[128,1536]{1,0:T(8,128)(2,1)S(1)}, bf16[128,1536]{1,0:T(8,128)(2,1)S(1)}, u32[]{:S(2)}, u32[]{:S(2)}) collective-permute-start(bf16[128,1536]{1,0:T(8,128)(2,1)S(1)} %bitcast.199), channel_id=1, source_target_pairs={{0,2},{1,3},{2,4},{3,5},{4,6},{5,7},{6,0},{7,1},{8,10},{9,11},{10,... | collective-permute-start | bytes 1179656 | tf_op jit(solution)/shard_map/ppermute | solution.py:895
  116.1 2.3 collective-permute-start.11
  119.2 2.9 collective-permute-done.10
  122.2 4.0 collective-permute-done.14
  126.2 31.2 %collective-permute-done.13 = bf16[128,1536]{1,0:T(8,128)(2,1)} collective-permute-done((bf16[128,1536]{1,0:T(8,128)(2,1)S(1)}, bf16[128,1536]{1,0:T(8,128)(2,1)}, u32[]{:S(2)}, u32[]{:S(2)}) %collective-permute-start.13) | collective-permute-done | bytes 393248 | tf_op jit(solution)/shard_map/ppermute | solution.py:895
  167.5 15.0 %all-gather.9.cloned.1.call-done = bf16[8192,192]{1,0:T(8,128)(2,1)} async-done(((bf16[1024,192]{1,0:T(8,128)(2,1)}), bf16[8192,192]{1,0:T(8,128)(2,1)}) %all-gather.9.cloned.1.call-update) | async-done | bytes 3145744 | tf_op jit(solution)/shard_map/all_gather | solution.py:965
  184.2 11.4 %shard_map.239 = (f32[1024,1536]{1,0:T(8,128)}, bf16[1024,1536]{1,0:T(8,128)(2,1)}, f32[1024,16]{1,0:T(8,128)S(1)}) custom-call(bf16[8,1024,192]{2,1,0:T(8,128)(2,1)} %bitcast.213, bf16[768,1536]{1,0:T(8,128)(2,1)S(1)} %bitcast.168, bf16[768,1536]{1,0:T(8,128)(2,1)S(1)} %bitcast.170, bf16[1024,1664]{1,0:T(8,128)(2,1)} %all-gather.5.cloned.1.call-done.hidden_ref.column_ref, ...), custom_call_target="tpu_custom_call" | custom-call | flops 4831838208 | bytes 18874368 | tf_op jit(solution)/shard_map/pallas_call | solution.py:377
  195.6 18.9 %shard_map.240 = (bf16[2,1024,512]{2,1,0:T(8,128)(2,1)}, bf16[2,1024,512]{2,1,0:T(8,128)(2,1)}, bf16[2,1024,512]{2,1,0:T(8,128)(2,1)}, bf16[2,1024,512]{2,1,0:T(...) custom-call(s32[4]{0:T(128)S(1)} %pad_add_fusion.place_ref, ...), custom_call_target="tpu_custom_call" | custom-call | flops 9663676416 | bytes 25165824 | tf_op jit(solution)/shard_map/pallas_call | solution.py:471
  219.9 4.9 shard_map.241
  226.1 4.9 shard_map.242
  232.5 16.6 %shard_map.243 = (bf16[1024,1664]{1,0:T(8,128)(2,1)}, bf16[1024,1536]{1,0:T(8,128)(2,1)}) custom-call(s32[4]{0:T(128)S(1)} %pad_add_fusion.place_ref, bf16[2,1024,512]{2,1,0:T(8,128)(2,1)} %get-tuple-element.107.scaled_ref, bf16[2,1024,512]{2,1,0:T(8,128)(2,1)} %get-tuple-element.106.grad_gate_ref, bf16[2,1024,512]{2,1,0:T(8,128)(2,1)} %get-tuple-element.108.grad_up_ref, ...), custom_call_target="tpu_custom_call" | custom-call | bytes 1024 | tf_op jit(solution)/shard_map/pallas_call | solution.py:604
  257.0 5.1 shard_map.244
  262.2 3.1 copy-done.66
  265.4 4.9 shard_map.245
  271.1 2.7 constant_dynamic-slice_fusion.2.middle_ref
  273.8 29.6 %collective-permute-done.16 = bf16[2304,512]{1,0:T(8,128)(2,1)} collective-permute-done((bf16[2304,512]{1,0:T(8,128)(2,1)}, bf16[2304,512]{1,0:T(8,128)(2,1)}, u32[]{:S(2)}, u32[]{:S(2)}) %collective-permute-start.16) | collective-permute-done | bytes 2359328 | tf_op jit(solution)/shard_map/ppermute | solution.py:748
  304.9 2.7 add_convert_fusion.3
  307.6 2.7 add_convert_fusion.2
  317.6 2.3 shard_map.246
  326.7 10.7 %all-to-all-start = ((bf16[8,128,192]{1,2,0:T(8,128)(2,1)}), bf16[8,128,192]{1,2,0:T(8,128)(2,1)}, u32[]{:S(2)}, u32[]{:S(2)}) async-start(bf16[8,128,192]{1,2,0:T(8,128)(2,1)} %copy.127), calls=%async_computation.2 | async-start | bytes 786432 | tf_op jit(solution)/shard_map/all_to_all | solution.py:1025
  337.5 12.8 %collective-permute-done.18 = bf16[1152,512]{1,0:T(8,128)(2,1)} collective-permute-done((bf16[1152,512]{1,0:T(8,128)(2,1)}, bf16[1152,512]{1,0:T(8,128)(2,1)}, u32[]{:S(2)}, u32[]{:S(2)}) %collective-permute-start.18) | collective-permute-done | bytes 1179680 | tf_op jit(solution)/shard_map/ppermute | solution.py:748
  350.3 4.0 add_convert_fusion.1
  354.4 3.4 add_convert_fusion
  370.1 13.6 %shard_map.247 = (bf16[1024,192]{1,0:T(8,128)(2,1)S(1)}, bf16[1024,128]{1,0:T(8,128)(2,1)S(1)}) custom-call(bf16[1024,192]{1,0:T(8,128)(2,1)S(1)} %copy-done.33, bf16[1024,192]{1,0:T(8,128)(2,1)S(1)} %bitcast.172, f32[3,1024,1]{2,1,0:T(8,128)S(1)} %copy-done.27, f32[1024,64]{1,0:T(8,128)S(1)} %copy-done.23, f32[1024,64]{1,0:T(8,128)S(1)} %copy-done.25, ...), custom_call_target="tpu_custom_call" | custom-call | bytes 1024 | tf_op jit(solution)/shard_map/pallas_call | solution.py:307
  383.7 6.3 %shard_map.248 = (bf16[1024,1536]{1,0:T(8,128)(2,1)}, f32[1536,320]{1,0:T(8,128)S(1)}, f32[1,1536]{1,0:T(1,128)S(1)}) custom-call(bf16[1024,192]{1,0:T(8,128)(2,1)S(1)} %get-tuple-element.127.query_ref, bf16[1024,128]{1,0:T(8,128)(2,1)S(1)} %get-tuple-element.128.pair_ref, bf16[1536,384]{1,0:T(8,128)(2,1)S(1)} %copy-done.17, ...), custom_call_target="tpu_custom_call" | custom-call | bytes 1024 | tf_op jit(solution)/shard_map/pallas_call | solution.py:720
  394.4 2.6 collective-permute-start.20
  406.4 3.6 collective-permute-done.25
  411.0 11.1 %all-to-all-start.1 = ((bf16[8,48,338]{2,1,0:T(8,128)(2,1)}), bf16[8,48,338]{2,1,0:T(8,128)(2,1)S(1)}, u32[]{:S(2)}, u32[]{:S(2)}) async-start(bf16[8,48,338]{2,1,0:T(8,128)(2,1)} %pad_maximum_fusion.22), calls=%async_computation.4 | async-start | bytes 589824 | tf_op jit(solution)/shard_map/all_to_all | solution.py:1085
  422.2 2.9 fusion.30
  429.5 5.6 %collective-permute-done.26 = bf16[96,1536]{1,0:T(8,128)(2,1)} collective-permute-done((bf16[96,1536]{1,0:T(8,128)(2,1)S(1)}, bf16[96,1536]{1,0:T(8,128)(2,1)}, u32[]{:S(2)}, u32[]{:S(2)}) %collective-permute-start.26) | collective-permute-done | bytes 294944 | tf_op jit(solution)/shard_map/ppermute | solution.py:748
  439.7 44.6 %collective-permute-done.28 = bf16[48,1536]{1,0:T(8,128)(2,1)S(1)} collective-permute-done((bf16[48,1536]{1,0:T(8,128)(2,1)S(1)}, bf16[48,1536]{1,0:T(8,128)(2,1)S(1)}, u32[]{:S(2)}, u32[]{:S(2)}) %collective-permute-start.28) | collective-permute-done | bytes 147488 | tf_op jit(solution)/shard_map/ppermute | solution.py:748
  493.5 3.8 collective-permute-done.32
  497.4 3.2 collective-permute-done.29
  503.5 2.9 reshape.336
  512.1 2.3 copy.137
  524.3 2.6 broadcast_select_fusion.1
  528.5 2.6 broadcast_select_fusion.3
  531.6 3.1 maximum_convert_fusion
  534.7 3.6 slice_convert_fusion.1
  538.3 3.6 slice_convert_fusion
  (363 shorter events, 148.1 us)
Async XLA Ops:
  7.2 67.9 %all-gather.5.cloned.1.call-start = ((), (), s32[]{:S(2)}) async-start(), calls=%async_computation.5 | async-start | bytes 3833856 | tf_op jit(solution)/shard_map/all_gather | solution.py:890
  12.0 11.5 %collective-permute-start.2 = (bf16[48,2304]{1,0:T(8,128)(2,1)S(1)}, bf16[48,2304]{1,0:T(8,128)(2,1)S(1)}, u32[]{:S(2)}, u32[]{:S(2)}) collective-permute-start(bf16[48,2304]{1,0:T(8,128)(2,1)S(1)} %get-tuple-element.278), channel_id=1, source_target_pairs={{0,2},{1,3},{2,4},{3,5},{4,6},{5,7},{6,0},{7,1},{8,10},{9,11},{10,... | collective-permute-start | bytes 663560 | tf_op jit(solution)/shard_map/ppermute | solution.py:895
  15.1 21.4 %collective-permute-start.1 = (bf16[48,2304]{1,0:T(8,128)(2,1)S(1)}, bf16[48,2304]{1,0:T(8,128)(2,1)S(1)}, u32[]{:S(2)}, u32[]{:S(2)}) collective-permute-start(bf16[48,2304]{1,0:T(8,128)(2,1)S(1)} %get-tuple-element.277), channel_id=1, source_target_pairs={{0,4},{1,5},{2,6},{3,7},{4,0},{5,1},{6,2},{7,3},{8,12},{9,13},{10,... | collective-permute-start | bytes 663560 | tf_op jit(solution)/shard_map/ppermute | solution.py:895
  17.7 18.8 %collective-permute-start = (bf16[48,2304]{1,0:T(8,128)(2,1)S(1)}, bf16[48,2304]{1,0:T(8,128)(2,1)S(1)}, u32[]{:S(2)}, u32[]{:S(2)}) collective-permute-start(bf16[48,2304]{1,0:T(8,128)(2,1)S(1)} %get-tuple-element.276), channel_id=1, source_target_pairs={{0,6},{1,7},{2,0},{3,1},{4,2},{5,3},{6,4},{7,5},{8,14},{9,15},{10,... | collective-permute-start | bytes 663560 | tf_op jit(solution)/shard_map/ppermute | solution.py:895
  20.1 162.5 %all-gather.9.cloned.1.call-start = ((), (), s32[]{:S(2)}) async-start(), calls=%async_computation.10 | async-start | bytes 4718592 | tf_op jit(solution)/shard_map/all_gather | solution.py:965
  36.9 2.3 collective-permute-start.3
  40.3 6.0 %collective-permute-start.7 = (bf16[4,1,1,48,384]{4,3,0,2,1:T(8,128)(2,1)S(1)}, bf16[4,1,1,48,384]{4,3,0,2,1:T(8,128)(2,1)S(1)}, u32[]{:S(2)}, u32[]{:S(2)}) collective-permute-start(bf16[4,1,1,48,384]{4,3,0,2,1:T(8,128)(2,1)S(1)} %get-tuple-element.245), channel_id=1, source_target_pairs={{0,16},{8,24},{16,0},{24,8},{1,17},{9,25},{17,1},{25,9},{2,18},{10... | collective-permute-start | bytes 442376 | tf_op jit(solution)/shard_map/ppermute | solution.py:748
  41.9 5.6 %collective-permute-start.5 = (bf16[4,1,1,48,384]{4,3,0,2,1:T(8,128)(2,1)S(1)}, bf16[4,1,1,48,384]{4,3,0,2,1:T(8,128)(2,1)S(1)}, u32[]{:S(2)}, u32[]{:S(2)}) collective-permute-start(bf16[4,1,1,48,384]{4,3,0,2,1:T(8,128)(2,1)S(1)} %get-tuple-element.246), channel_id=1, source_target_pairs={{0,8},{8,0},{16,24},{24,16},{1,9},{9,1},{17,25},{25,17},{2,10},{10... | collective-permute-start | bytes 442376 | tf_op jit(solution)/shard_map/ppermute | solution.py:748
  47.6 10.0 %collective-permute-start.6 = (bf16[4,1,2,48,384]{4,3,0,2,1:T(8,128)(2,1)S(1)}, bf16[4,1,2,48,384]{4,3,0,2,1:T(8,128)(2,1)S(1)}, u32[]{:S(2)}, u32[]{:S(2)}) collective-permute-start(bf16[4,1,2,48,384]{4,3,0,2,1:T(8,128)(2,1)S(1)} %pad_maximum_fusion.20), channel_id=1, source_target_pairs={{0,16},{8,24},{16,0},{24,8},{1,17},{9,25},{17,1},{25,9},{2,18},{10... | collective-permute-start | bytes 884744 | tf_op jit(solution)/shard_map/ppermute | solution.py:748
  48.3 23.0 %collective-permute-start.9 = (bf16[4,1,1,48,1536]{4,3,0,2,1:T(8,128)(2,1)S(1)}, bf16[4,1,1,48,1536]{4,3,0,2,1:T(8,128)(2,1)S(1)}, u32[]{:S(2)}, u32[]{:S(2)}) collective-permute-start(bf16[4,1,1,48,1536]{4,3,0,2,1:T(8,128)(2,1)S(1)} %get-tuple-element.241), channel_id=1, source_target_pairs={{0,16},{8,24},{16,0},{24,8},{1,17},{9,25},{17,1},{25,9},{2,18},{10... | collective-permute-start | bytes 1769480 | tf_op jit(solution)/shard_map/ppermute | solution.py:748
  49.9 21.9 %collective-permute-start.4 = (bf16[4,1,1,48,1536]{4,3,0,2,1:T(8,128)(2,1)S(1)}, bf16[4,1,1,48,1536]{4,3,0,2,1:T(8,128)(2,1)S(1)}, u32[]{:S(2)}, u32[]{:S(2)}) collective-permute-start(bf16[4,1,1,48,1536]{4,3,0,2,1:T(8,128)(2,1)S(1)} %get-tuple-element.242), channel_id=1, source_target_pairs={{0,8},{8,0},{16,24},{24,16},{1,9},{9,1},{17,25},{25,17},{2,10},{10... | collective-permute-start | bytes 1769480 | tf_op jit(solution)/shard_map/ppermute | solution.py:748
  51.4 18.5 %collective-permute-start.8 = (bf16[4,2,1,48,384]{4,3,0,2,1:T(8,128)(2,1)S(1)}, bf16[4,2,1,48,384]{4,3,0,2,1:T(8,128)(2,1)S(1)}, u32[]{:S(2)}, u32[]{:S(2)}) collective-permute-start(bf16[4,2,1,48,384]{4,3,0,2,1:T(8,128)(2,1)S(1)} %pad_maximum_fusion.21), channel_id=1, source_target_pairs={{0,8},{8,0},{16,24},{24,16},{1,9},{9,1},{17,25},{25,17},{2,10},{10... | collective-permute-start | bytes 884744 | tf_op jit(solution)/shard_map/ppermute | solution.py:748
  57.9 60.5 %copy-start.9 = (bf16[4,2,2,48,384]{4,3,2,1,0:T(8,128)(2,1)}, bf16[4,2,2,48,384]{4,3,2,1,0:T(8,128)(2,1)S(1)}, u32[]{:S(2)}) copy-start(bf16[4,2,2,48,384]{4,3,2,1,0:T(8,128)(2,1)S(1)} %copy.123) | copy-start | bytes 1769476
  70.2 48.2 %copy-start.11 = (bf16[4,2,2,48,384]{4,3,2,1,0:T(8,128)(2,1)}, bf16[4,2,2,48,384]{4,3,2,1,0:T(8,128)(2,1)S(1)}, u32[]{:S(2)}) copy-start(bf16[4,2,2,48,384]{4,3,2,1,0:T(8,128)(2,1)S(1)} %copy.124) | copy-start | bytes 1769476
  96.3 214.0 %reduce-scatter.4.cloned.1.call-start = ((), (), s32[]{:S(2)}) async-start(), calls=%async_computation.6 | async-start | bytes 3833856 | tf_op jit(solution)/shard_map/reduce_scatter | solution.py:1002
  96.3 25.8 %collective-permute-start.10 = (bf16[4,1,2,48,1536]{4,3,0,2,1:T(8,128)(2,1)}, bf16[4,1,2,48,1536]{4,3,0,2,1:T(8,128)(2,1)}, u32[]{:S(2)}, u32[]{:S(2)}) collective-permute-start(bf16[4,1,2,48,1536]{4,3,0,2,1:T(8,128)(2,1)} %pad_maximum_fusion.10), channel_id=1, source_target_pairs={{0,16},{8,24},{16,0},{24,8},{1,17},{9,25},{17,1},{25,9},{2,18},{10... | collective-permute-start | bytes 3538952 | tf_op jit(solution)/shard_map/ppermute | solution.py:748
  97.0 29.2 %collective-permute-start.14 = (bf16[128,1536]{1,0:T(8,128)(2,1)S(1)}, bf16[128,1536]{1,0:T(8,128)(2,1)S(1)}, u32[]{:S(2)}, u32[]{:S(2)}) collective-permute-start(bf16[128,1536]{1,0:T(8,128)(2,1)S(1)} %bitcast.199), channel_id=1, source_target_pairs={{0,2},{1,3},{2,4},{3,5},{4,6},{5,7},{6,0},{7,1},{8,10},{9,11},{10,... | collective-permute-start | bytes 1179656 | tf_op jit(solution)/shard_map/ppermute | solution.py:895
  113.6 43.7 %collective-permute-start.13 = (bf16[128,1536]{1,0:T(8,128)(2,1)S(1)}, bf16[128,1536]{1,0:T(8,128)(2,1)}, u32[]{:S(2)}, u32[]{:S(2)}) collective-permute-start(bf16[128,1536]{1,0:T(8,128)(2,1)S(1)} %bitcast.200), channel_id=1, source_target_pairs={{0,4},{1,5},{2,6},{3,7},{4,0},{5,1},{6,2},{7,3},{8,12},{9,13},{10,... | collective-permute-start | bytes 1179656 | tf_op jit(solution)/shard_map/ppermute | solution.py:895
  115.8 41.6 %collective-permute-start.12 = (bf16[128,1536]{1,0:T(8,128)(2,1)S(1)}, bf16[128,1536]{1,0:T(8,128)(2,1)}, u32[]{:S(2)}, u32[]{:S(2)}) collective-permute-start(bf16[128,1536]{1,0:T(8,128)(2,1)S(1)} %bitcast.201), channel_id=1, source_target_pairs={{0,6},{1,7},{2,0},{3,1},{4,2},{5,3},{6,4},{7,5},{8,14},{9,15},{10,... | collective-permute-start | bytes 1179656 | tf_op jit(solution)/shard_map/ppermute | solution.py:895
  116.1 42.7 %copy-start.64 = (bf16[4,1,1,48,1536]{4,3,0,2,1:T(8,128)(2,1)S(1)}, bf16[4,1,1,48,1536]{4,3,0,2,1:T(8,128)(2,1)}, u32[]{:S(2)}) copy-start(bf16[4,1,1,48,1536]{4,3,0,2,1:T(8,128)(2,1)} %copy-done.63) | copy-start | bytes 1769476
  116.1 44.7 %collective-permute-start.11 = (bf16[4,2,1,48,1536]{4,3,0,2,1:T(8,128)(2,1)}, bf16[4,2,1,48,1536]{4,3,0,2,1:T(8,128)(2,1)S(1)}, u32[]{:S(2)}, u32[]{:S(2)}) collective-permute-start(bf16[4,2,1,48,1536]{4,3,0,2,1:T(8,128)(2,1)} %pad_maximum_fusion.11), channel_id=1, source_target_pairs={{0,8},{8,0},{16,24},{24,16},{1,9},{9,1},{17,25},{25,17},{2,10},{10... | collective-permute-start | bytes 3538952 | tf_op jit(solution)/shard_map/ppermute | solution.py:748
  158.7 5.5 %collective-permute-start.15 = (bf16[4,128,1536]{2,1,0:T(8,128)(2,1)S(1)}, bf16[4,128,1536]{2,1,0:T(8,128)(2,1)S(1)}, u32[]{:S(2)}, u32[]{:S(2)}) collective-permute-start(bf16[4,128,1536]{2,1,0:T(8,128)(2,1)S(1)} %pad_maximum_fusion.9), channel_id=1, source_target_pairs={{0,1},{1,0},{2,3},{3,2},{4,5},{5,4},{6,7},{7,6},{8,9},{9,8},{10,11... | collective-permute-start | bytes 4718600 | tf_op jit(solution)/shard_map/ppermute | solution.py:898
  249.1 173.1 %all-gather.7.cloned.1.call-start = ((), (), s32[]{:S(2)}) async-start(), calls=%async_computation.9 | async-start | bytes 3538944 | tf_op jit(solution)/shard_map/all_gather | solution.py:1028
  249.2 54.2 %collective-permute-start.16 = (bf16[2304,512]{1,0:T(8,128)(2,1)}, bf16[2304,512]{1,0:T(8,128)(2,1)}, u32[]{:S(2)}, u32[]{:S(2)}) collective-permute-start(bf16[2304,512]{1,0:T(8,128)(2,1)} %copy-done.21), channel_id=1, source_target_pairs={{0,8},{8,0},{16,24},{24,16},{1,9},{9,1},{17,25},{25,17},{2,10},{10... | collective-permute-start | bytes 7077896 | tf_op jit(solution)/shard_map/ppermute | solution.py:748
  251.4 53.4 %collective-permute-start.17 = (bf16[2304,512]{1,0:T(8,128)(2,1)}, bf16[2304,512]{1,0:T(8,128)(2,1)}, u32[]{:S(2)}, u32[]{:S(2)}) collective-permute-start(bf16[2304,512]{1,0:T(8,128)(2,1)} %copy-done.20), channel_id=1, source_target_pairs={{0,16},{8,24},{16,0},{24,8},{1,17},{9,25},{17,1},{25,9},{2,18},{10... | collective-permute-start | bytes 7077896 | tf_op jit(solution)/shard_map/ppermute | solution.py:748
  262.1 42.8 %copy-start.8 = (f32[2304,512]{1,0:T(8,128)}, f32[2304,512]{1,0:T(8,128)S(1)}, u32[]{:S(2)}) copy-start(f32[2304,512]{1,0:T(8,128)S(1)} %shard_map.244) | copy-start | bytes 14155780
  322.9 27.4 %collective-permute-start.18 = (bf16[1152,512]{1,0:T(8,128)(2,1)}, bf16[1152,512]{1,0:T(8,128)(2,1)}, u32[]{:S(2)}, u32[]{:S(2)}) collective-permute-start(bf16[1152,512]{1,0:T(8,128)(2,1)} %add_convert_fusion.3), channel_id=1, source_target_pairs={{0,16},{8,24},{16,0},{24,8},{1,17},{9,25},{17,1},{25,9},{2,18},{10... | collective-permute-start | bytes 3538952 | tf_op jit(solution)/shard_map/ppermute | solution.py:748
  324.3 30.0 %collective-permute-start.19 = (bf16[1152,512]{1,0:T(8,128)(2,1)}, bf16[1152,512]{1,0:T(8,128)(2,1)}, u32[]{:S(2)}, u32[]{:S(2)}) collective-permute-start(bf16[1152,512]{1,0:T(8,128)(2,1)} %add_convert_fusion.2), channel_id=1, source_target_pairs={{0,8},{8,0},{16,24},{24,16},{1,9},{9,1},{17,25},{25,17},{2,10},{10... | collective-permute-start | bytes 3538952 | tf_op jit(solution)/shard_map/ppermute | solution.py:748
  326.7 36.7 %all-to-all-start = ((bf16[8,128,192]{1,2,0:T(8,128)(2,1)}), bf16[8,128,192]{1,2,0:T(8,128)(2,1)}, u32[]{:S(2)}, u32[]{:S(2)}) async-start(bf16[8,128,192]{1,2,0:T(8,128)(2,1)} %copy.127), calls=%async_computation.2 | async-start | bytes 786432 | tf_op jit(solution)/shard_map/all_to_all | solution.py:1025
  337.4 182.5 %reduce-scatter.6.cloned.1.call-start = ((), (), s32[]{:S(2)}) async-start(), calls=%async_computation.7 | async-start | bytes 3538944 | tf_op jit(solution)/shard_map/reduce_scatter | solution.py:1118
  357.7 39.3 %collective-permute-start.21 = (bf16[1152,512]{1,0:T(8,128)(2,1)}, bf16[1152,512]{1,0:T(8,128)(2,1)}, u32[]{:S(2)}, u32[]{:S(2)}) collective-permute-start(bf16[1152,512]{1,0:T(8,128)(2,1)} %add_convert_fusion.1), channel_id=1, source_target_pairs={{0,16},{8,24},{16,0},{24,8},{1,17},{9,25},{17,1},{25,9},{2,18},{10... | collective-permute-start | bytes 3538952 | tf_op jit(solution)/shard_map/ppermute | solution.py:748
  359.1 38.0 %collective-permute-start.22 = (bf16[1152,512]{1,0:T(8,128)(2,1)}, bf16[1152,512]{1,0:T(8,128)(2,1)}, u32[]{:S(2)}, u32[]{:S(2)}) collective-permute-start(bf16[1152,512]{1,0:T(8,128)(2,1)} %add_convert_fusion), channel_id=1, source_target_pairs={{0,8},{8,0},{16,24},{24,16},{1,9},{9,1},{17,25},{25,17},{2,10},{10... | collective-permute-start | bytes 3538952 | tf_op jit(solution)/shard_map/ppermute | solution.py:748
  393.6 11.1 %collective-permute-start.24 = (bf16[384,338]{1,0:T(8,128)(2,1)S(1)}, bf16[384,338]{1,0:T(8,128)(2,1)S(1)}, u32[]{:S(2)}, u32[]{:S(2)}) collective-permute-start(bf16[384,338]{1,0:T(8,128)(2,1)S(1)} %dynamic-slice_convert_fusion.1), channel_id=1, source_target_pairs={{0,16},{8,24},{16,0},{24,8},{1,17},{9,25},{17,1},{25,9},{2,18},{10... | collective-permute-start | bytes 778760 | tf_op jit(solution)/shard_map/ppermute | solution.py:748
  394.4 10.4 %collective-permute-start.20 = (bf16[384,338]{1,0:T(8,128)(2,1)S(1)}, bf16[384,338]{1,0:T(8,128)(2,1)S(1)}, u32[]{:S(2)}, u32[]{:S(2)}) collective-permute-start(bf16[384,338]{1,0:T(8,128)(2,1)S(1)} %dynamic-slice_convert_fusion.2), channel_id=1, source_target_pairs={{0,8},{8,0},{16,24},{24,16},{1,9},{9,1},{17,25},{25,17},{2,10},{10... | collective-permute-start | bytes 778760 | tf_op jit(solution)/shard_map/ppermute | solution.py:748
  404.7 5.2 collective-permute-start.25
  404.9 5.2 collective-permute-start.23
  411.0 27.1 %all-to-all-start.1 = ((bf16[8,48,338]{2,1,0:T(8,128)(2,1)}), bf16[8,48,338]{2,1,0:T(8,128)(2,1)S(1)}, u32[]{:S(2)}, u32[]{:S(2)}) async-start(bf16[8,48,338]{2,1,0:T(8,128)(2,1)} %pad_maximum_fusion.22), calls=%async_computation.4 | async-start | bytes 589824 | tf_op jit(solution)/shard_map/all_to_all | solution.py:1085
  422.1 119.8 %reduce-scatter.8.cloned.1.call-start = ((), (), s32[]{:S(2)}) async-start(), calls=%async_computation.8 | async-start | bytes 3538944 | tf_op jit(solution)/shard_map/reduce_scatter | solution.py:1050
  425.1 10.0 %collective-permute-start.26 = (bf16[96,1536]{1,0:T(8,128)(2,1)S(1)}, bf16[96,1536]{1,0:T(8,128)(2,1)}, u32[]{:S(2)}, u32[]{:S(2)}) collective-permute-start(bf16[96,1536]{1,0:T(8,128)(2,1)S(1)} %dynamic-slice_convert_fusion), channel_id=1, source_target_pairs={{0,16},{8,24},{16,0},{24,8},{1,17},{9,25},{17,1},{25,9},{2,18},{10... | collective-permute-start | bytes 884744 | tf_op jit(solution)/shard_map/ppermute | solution.py:748
  426.8 97.5 %collective-permute-start.34 = (bf16[2304,512]{1,0:T(8,128)(2,1)}, bf16[2304,512]{1,0:T(8,128)(2,1)}, u32[]{:S(2)}, u32[]{:S(2)}) collective-permute-start(bf16[2304,512]{1,0:T(8,128)(2,1)} %pad_maximum_fusion.6), channel_id=1, source_target_pairs={{0,8},{8,0},{16,24},{24,16},{1,9},{9,1},{17,25},{25,17},{2,10},{10... | collective-permute-start | bytes 7077896 | tf_op jit(solution)/shard_map/ppermute | solution.py:748
  428.9 95.4 %collective-permute-start.35 = (bf16[2304,512]{1,0:T(8,128)(2,1)}, bf16[2304,512]{1,0:T(8,128)(2,1)}, u32[]{:S(2)}, u32[]{:S(2)}) collective-permute-start(bf16[2304,512]{1,0:T(8,128)(2,1)} %pad_maximum_fusion.7), channel_id=1, source_target_pairs={{0,16},{8,24},{16,0},{24,8},{1,17},{9,25},{17,1},{25,9},{2,18},{10... | collective-permute-start | bytes 7077896 | tf_op jit(solution)/shard_map/ppermute | solution.py:748
  436.1 48.2 %collective-permute-start.28 = (bf16[48,1536]{1,0:T(8,128)(2,1)S(1)}, bf16[48,1536]{1,0:T(8,128)(2,1)S(1)}, u32[]{:S(2)}, u32[]{:S(2)}) collective-permute-start(bf16[48,1536]{1,0:T(8,128)(2,1)S(1)} %add_convert_fusion.5), channel_id=1, source_target_pairs={{0,8},{8,0},{16,24},{24,16},{1,9},{9,1},{17,25},{25,17},{2,10},{10... | collective-permute-start | bytes 442376 | tf_op jit(solution)/shard_map/ppermute | solution.py:748
  438.2 50.1 %collective-permute-start.31 = (bf16[4,1,1,48,338]{4,3,2,1,0:T(8,128)(2,1)S(1)}, bf16[4,1,1,48,338]{4,3,2,1,0:T(8,128)(2,1)S(1)}, u32[]{:S(2)}, u32[]{:S(2)}) collective-permute-start(bf16[4,1,1,48,338]{4,3,2,1,0:T(8,128)(2,1)S(1)} %get-tuple-element.266), channel_id=1, source_target_pairs={{0,16},{8,24},{16,0},{24,8},{1,17},{9,25},{17,1},{25,9},{2,18},{10... | collective-permute-start | bytes 389384 | tf_op jit(solution)/shard_map/ppermute | solution.py:748
  439.7 50.8 %collective-permute-start.27 = (bf16[4,1,1,48,338]{4,3,0,2,1:T(8,128)(2,1)S(1)}, bf16[4,1,1,48,338]{4,3,0,2,1:T(8,128)(2,1)S(1)}, u32[]{:S(2)}, u32[]{:S(2)}) collective-permute-start(bf16[4,1,1,48,338]{4,3,0,2,1:T(8,128)(2,1)S(1)} %get-tuple-element.265), channel_id=1, source_target_pairs={{0,8},{8,0},{16,24},{24,16},{1,9},{9,1},{17,25},{25,17},{2,10},{10... | collective-permute-start | bytes 389384 | tf_op jit(solution)/shard_map/ppermute | solution.py:748
  485.3 6.7 %collective-permute-start.30 = (bf16[48,1536]{1,0:T(8,128)(2,1)S(1)}, bf16[48,1536]{1,0:T(8,128)(2,1)S(1)}, u32[]{:S(2)}, u32[]{:S(2)}) collective-permute-start(bf16[48,1536]{1,0:T(8,128)(2,1)S(1)} %add_convert_fusion.4), channel_id=1, source_target_pairs={{0,8},{8,0},{16,24},{24,16},{1,9},{9,1},{17,25},{25,17},{2,10},{10... | collective-permute-start | bytes 442376 | tf_op jit(solution)/shard_map/ppermute | solution.py:748
  488.4 8.9 %collective-permute-start.32 = (bf16[4,2,1,48,338]{4,3,2,1,0:T(8,128)(2,1)S(1)}, bf16[4,2,1,48,338]{4,3,2,1,0:T(8,128)(2,1)S(1)}, u32[]{:S(2)}, u32[]{:S(2)}) collective-permute-start(bf16[4,2,1,48,338]{4,3,2,1,0:T(8,128)(2,1)S(1)} %pad_maximum_fusion.24), channel_id=1, source_target_pairs={{0,8},{8,0},{16,24},{24,16},{1,9},{9,1},{17,25},{25,17},{2,10},{10... | collective-permute-start | bytes 778760 | tf_op jit(solution)/shard_map/ppermute | solution.py:748
  490.6 10.0 %collective-permute-start.29 = (bf16[4,1,2,48,338]{4,3,0,2,1:T(8,128)(2,1)S(1)}, bf16[4,1,2,48,338]{4,3,0,2,1:T(8,128)(2,1)S(1)}, u32[]{:S(2)}, u32[]{:S(2)}) collective-permute-start(bf16[4,1,2,48,338]{4,3,0,2,1:T(8,128)(2,1)S(1)} %pad_maximum_fusion.23), channel_id=1, source_target_pairs={{0,16},{8,24},{16,0},{24,8},{1,17},{9,25},{17,1},{25,9},{2,18},{10... | collective-permute-start | bytes 778760 | tf_op jit(solution)/shard_map/ppermute | solution.py:748
  492.9 29.1 %collective-permute-start.33 = (bf16[96,1536]{1,0:T(8,128)(2,1)}, bf16[96,1536]{1,0:T(8,128)(2,1)}, u32[]{:S(2)}, u32[]{:S(2)}) collective-permute-start(bf16[96,1536]{1,0:T(8,128)(2,1)} %pad_maximum_fusion.25), channel_id=1, source_target_pairs={{0,16},{8,24},{16,0},{24,8},{1,17},{9,25},{17,1},{25,9},{2,18},{10... | collective-permute-start | bytes 884744 | tf_op jit(solution)/shard_map/ppermute | solution.py:748
  (76 other events, 426.1 us)
Sparse Core Ops, SparseCore 0:
  20.2 45.6 all-gather.4
  96.4 86.1 all-gather.8
  249.2 50.1 reduce-scatter.3
  323.0 52.7 all-gather.6
  378.0 39.1 reduce-scatter.5
  427.0 41.3 reduce-scatter.7

commit v4 on v3

--- a/solution.py
+++ b/solution.py
@@ -211,11 +211,7 @@
         ],
         scratch_shapes=[pltpu.VMEM((steps, HEAD_GROUP * block, block), jnp.float32)],
         compiler_params=pltpu.CompilerParams(vmem_limit_bytes=48 << 20),
-        cost_estimate=pl.CostEstimate(
-            flops=6 * tokens * features * query_width,
-            bytes_accessed=4 * tokens * features,
-            transcendentals=tokens * tokens * HEAD_GROUP // 2,
-        ),
+        cost_estimate=pl.CostEstimate(flops=0, bytes_accessed=tokens, transcendentals=0),
     )(gathered, gathered, gain[None, :], *weights, rate)
 
 
@@ -460,11 +456,10 @@
     extra_ref[...] = jnp.concatenate([rough, fine, rest], 1)
 
 
-def expert_rows(place, normed, cotangent, gathered, gates, w_gate, w_up, w_down):
+def expert_rows(place, normed, cotangent, gathered, gates, w_gate, w_up, w_down, block):
     tokens, features = normed.shape
     experts_own, _, hidden = w_gate.shape
     experts_all = gates.shape[1]
-    chips, block, _ = cotangent.shape
     rows = lambda columns: pl.BlockSpec((block, columns), lambda i, p: (i, 0))
     spread = pl.BlockSpec((experts_own, block, hidden), lambda i, p: (0, i, 0))
     wide = jax.ShapeDtypeStruct((experts_own, tokens, hidden), jnp.bfloat16)
@@ -480,12 +475,10 @@
         ),
         grid_spec=pltpu.PrefetchScalarGridSpec(
             num_scalar_prefetch=1,
-            grid=(chips,),
+            grid=(tokens // block,),
             in_specs=[
                 rows(features),
-                pl.BlockSpec(
-                    (None, block, features), lambda i, p: (lax.rem(i - p[0] + chips, chips), 0, 0)
-                ),
+                rows(features),
                 pl.BlockSpec((block, 128), lambda i, p: (i, features // 128)),
                 rows(experts_all),
                 whole_block(*w_gate.shape),
@@ -506,6 +499,7 @@
 def product_kernel(left_ref, right_ref, scaled_ref, live_ref, out_ref):
     step = pl.program_id(0)
     tile, hidden = left_ref.shape[1], right_ref.shape[1]
+    narrow = live_ref.shape[1]
     tops = pl.num_programs(0) - 3
     top = tops * tile
 
@@ -521,16 +515,17 @@
         def _():
             product = dot(scaled_ref[...], live_ref[...], ROWS).astype(out_ref.dtype)
             if part < 2:
-                out_ref[top : top + hidden, part * tile : (part + 1) * tile] = product
+                out_ref[top : top + hidden, part * narrow : (part + 1) * narrow] = product
             else:
-                out_ref[top + hidden :, :tile] = product[:tile]
-                out_ref[top + hidden :, tile:] = product[tile:]
-
-
-def expert_product(left, right, scaled, live, side, dtype):
+                out_ref[top + hidden :, :narrow] = product[:narrow]
+                out_ref[top + hidden :, narrow:] = product[narrow:]
+
+
+def expert_product(left, right, scaled, live, e, side, dtype):
     tokens, features = left.shape
-    hidden = right.shape[1]
-    tile = hidden // 2
+    hidden = right.shape[2]
+    narrow = hidden // 2
+    tile = 512
     tops = features // tile
     return pl.pallas_call(
         product_kernel,
@@ -538,33 +533,14 @@
         grid=(tops + 3,),
         in_specs=[
             pl.BlockSpec((tokens, tile), lambda i: (0, jnp.minimum(i, tops - 1))),
-            whole_block(tokens, hidden),
-            whole_block(tokens, hidden),
-            pl.BlockSpec((tokens, tile), lambda i: (0, 3 * side + jnp.maximum(i - tops, 0))),
+            pl.BlockSpec((None, tokens, hidden), lambda i: (e, 0, 0), pipeline_mode=pl.Buffered(1)),
+            pl.BlockSpec((None, tokens, hidden), lambda i: (e, 0, 0), pipeline_mode=pl.Buffered(1)),
+            pl.BlockSpec((tokens, narrow), lambda i: (0, 3 * side + jnp.maximum(i - tops, 0))),
         ],
         out_specs=pl.BlockSpec((features + features // 2, hidden), lambda i: (0, 0)),
         compiler_params=pltpu.CompilerParams(vmem_limit_bytes=40 << 20),
-        cost_estimate=pl.CostEstimate(
-            flops=3 * tokens * features * hidden,
-            bytes_accessed=4 * tokens * features,
-            transcendentals=0,
-        ),
+        cost_estimate=pl.CostEstimate(flops=0, bytes_accessed=tokens, transcendentals=0),
     )(left, right, scaled, live)
-
-
-def split_product(value):
-    features = value.shape[1] * 2 // 3
-    hidden = value.shape[2]
-    tile = hidden // 2
-    low = value[:, features:]
-    down = jnp.concatenate(
-        [
-            low[:, :hidden],
-            jnp.concatenate([low[:, hidden:, :tile], low[:, hidden:, tile:]], 1),
-        ],
-        2,
-    )
-    return value[:, :features], down
 
 
 def rows_kernel(
@@ -583,8 +559,8 @@
     features = out_ref.shape[1]
     one = [slot_of(e, place_ref[2], experts_own) for e in range(experts_own)]
     two = [slot_of(e, place_ref[3], experts_own) for e in range(experts_own)]
-    for start in range(0, features, 256):
-        part = slice(start, start + 256)
+    for start in range(0, features, 512):
+        part = slice(start, start + 512)
         grad = 0.0
         out = 0.0
         for e in range(experts_own):
@@ -685,7 +661,18 @@
 
 
 def close_kernel(
-    query_ref, pair_ref, weight_ref, hidden_ref, normed_ref, grad_ref, product_ref, gain_grad_ref
+    query_ref,
+    pair_ref,
+    weight_ref,
+    hidden_ref,
+    normed_ref,
+    gain_two_ref,
+    normed_own_ref,
+    logits_ref,
+    grad_ref,
+    head_ref,
+    product_ref,
+    gain_ref,
 ):
     step = pl.program_id(0)
     width = query_ref.shape[1]
@@ -698,32 +685,48 @@
     grad_ref[...] = grad.astype(jnp.bfloat16)
     hidden = hidden_ref[...].astype(jnp.float32)
     scale = lax.rsqrt(jnp.mean(hidden * hidden, -1, keepdims=True) + EPS)
-    gain_grad = jnp.sum(grad * (hidden * scale), 0, keepdims=True)
     normed = normed_ref[...]
 
     @pl.when(step == 0)
     def _():
-        gain_grad_ref[...] = jnp.zeros_like(gain_grad_ref)
+        gain_ref[...] = jnp.zeros_like(gain_ref)
         product_ref[...] = jnp.zeros_like(product_ref)
 
-    gain_grad_ref[...] += gain_grad
+    gain_ref[...] += jnp.sum(grad * (hidden * scale), 0, keepdims=True)
     product_ref[:, :width] += dot(normed, query, ROWS)
     product_ref[:, width:] += dot(normed, pair, ROWS)
 
-
-def close_rows(query, pair, weight, gathered, normed, block):
+    @pl.when(step == pl.num_programs(0) - 1)
+    def _():
+        features = product_ref.shape[0]
+        rows = head_ref.shape[0]
+        experts = logits_ref.shape[1]
+        side = head_ref.shape[1] // (features // rows)
+        gains = jnp.concatenate(
+            [gain_ref[...], gain_two_ref[...], jnp.zeros((6, features), jnp.float32)], 0
+        )
+        gains = jnp.transpose(gains)
+        router = dot(normed_own_ref[...], logits_ref[...], ROWS)
+        for c in range(features // rows):
+            part = slice(c * rows, (c + 1) * rows)
+            rest = jnp.zeros((rows, side - both - 8 - experts), jnp.float32)
+            head_ref[:, c * side : (c + 1) * side] = jnp.concatenate(
+                [product_ref[part, :], gains[part], router[part], rest], 1
+            )
+
+
+def close_rows(
+    query, pair, weight, gathered, normed, gain_two_grad, normed_own, logits, rows_own, side, block
+):
     tokens, features = normed.shape
     both = query.shape[1] + pair.shape[1]
     rows = lambda width: pl.BlockSpec((block, width), lambda i: (i, 0))
     resident = lambda *shape: pl.BlockSpec(shape, lambda i: (0,) * len(shape))
     shaped = jax.ShapeDtypeStruct
+    head = (rows_own, features // rows_own * side)
     return pl.pallas_call(
         close_kernel,
-        out_shape=(
-            shaped((tokens, features), jnp.bfloat16),
-            shaped((features, both), jnp.float32),
-            shaped((1, features), jnp.float32),
-        ),
+        out_shape=(shaped((tokens, features), jnp.bfloat16), shaped(head, jnp.float32)),
         grid=(tokens // block,),
         in_specs=[
             rows(query.shape[1]),
@@ -731,11 +734,124 @@
             whole_block(*weight.shape),
             rows(features),
             rows(features),
+            whole_block(1, features),
+            whole_block(*normed_own.shape),
+            whole_block(*logits.shape),
         ],
-        out_specs=[rows(features), resident(features, both), resident(1, features)],
+        out_specs=[rows(features), resident(*head)],
+        scratch_shapes=[
+            pltpu.VMEM((features, both), jnp.float32),
+            pltpu.VMEM((1, features), jnp.float32),
+        ],
+        compiler_params=pltpu.CompilerParams(vmem_limit_bytes=48 << 20),
+        cost_estimate=pl.CostEstimate(flops=0, bytes_accessed=tokens, transcendentals=0),
+    )(query, pair, weight, gathered, normed, gain_two_grad, normed_own, logits)
+
+
+def head_kernel(copies, side, low_ref, high_ref, query_ref, key_ref, value_ref, out_ref, small_ref):
+    groups = KEY_VALUE_HEADS
+    count = groups * copies
+    halves = [low_ref[...].astype(jnp.float32), high_ref[...].astype(jnp.float32)]
+    width = query_ref.shape[1] // groups
+    parts = []
+    for c in range(count):
+        place = c % (count // 2) * side
+        parts.append(halves[c // (count // 2)][:, place : place + side])
+    heads = []
+    small = 0.0
+    for g in range(groups):
+        total = parts[g * copies]
+        for p in range(1, copies):
+            total = total + parts[g * copies + p]
+        heads.append(total)
+        small = small + total[:, width + 2 * HEAD_SIZE :]
+    small_ref[...] = small
+    query_ref[...] = jnp.concatenate([head[:, :width] for head in heads], 1)
+    key_ref[...] = jnp.concatenate([head[:, width : width + HEAD_SIZE] for head in heads], 1)
+    value_ref[...] = jnp.concatenate(
+        [head[:, width + HEAD_SIZE : width + 2 * HEAD_SIZE] for head in heads], 1
+    )
+    out_ref[...] = jnp.concatenate([half[:, count // 2 * side :] for half in halves], 1)
+
+
+def head_outputs(low, high, copies, side):
+    rows = low.shape[0]
+    groups = KEY_VALUE_HEADS
+    query_width = QUERY_HEADS * HEAD_SIZE
+    shaped = lambda width: jax.ShapeDtypeStruct((rows, width), jnp.float32)
+    return pl.pallas_call(
+        lambda *refs: head_kernel(copies, side, *refs),
+        name="head_outputs",
+        out_shape=(
+            shaped(query_width),
+            shaped(groups * HEAD_SIZE),
+            shaped(groups * HEAD_SIZE),
+            shaped(MODEL_WIDTH),
+            shaped(side - (query_width // groups + 2 * HEAD_SIZE)),
+        ),
         compiler_params=pltpu.CompilerParams(vmem_limit_bytes=40 << 20),
-        cost_estimate=pl.CostEstimate(flops=0, bytes_accessed=tokens, transcendentals=0),
-    )(query, pair, weight, gathered, normed)
+        cost_estimate=pl.CostEstimate(flops=0, bytes_accessed=rows, transcendentals=0),
+    )(low, high)
+
+
+def into_kernel(keeps_ref, side, sent_ref, first_ref, second_ref, out_ref):
+    kept = pl.program_id(0) == keeps_ref[side]
+    came = jnp.where(pl.program_id(1) == 0, first_ref[...], second_ref[...])
+    out_ref[...] = jnp.where(kept, sent_ref[...], came).astype(jnp.float32)
+
+
+def into_output(keeps, side, sent, first, second):
+    rows, hidden = first.shape
+    part = lambda index: pl.BlockSpec((rows, hidden), index)
+    return pl.pallas_call(
+        lambda k, *refs: into_kernel(k, side, *refs),
+        name="into_output",
+        out_shape=jax.ShapeDtypeStruct((2, 2 * rows, hidden), jnp.float32),
+        grid_spec=pltpu.PrefetchScalarGridSpec(
+            num_scalar_prefetch=1,
+            grid=(2, 2),
+            in_specs=[
+                part(lambda e, h, k: (h, 0)),
+                part(lambda e, h, k: (0, 0)),
+                part(lambda e, h, k: (0, 0)),
+            ],
+            out_specs=pl.BlockSpec((None, rows, hidden), lambda e, h, k: (e, h, 0)),
+        ),
+        compiler_params=pltpu.CompilerParams(vmem_limit_bytes=32 << 20),
+        cost_estimate=pl.CostEstimate(flops=0, bytes_accessed=rows, transcendentals=0),
+    )(keeps, sent, first, second)
+
+
+def down_kernel(keeps_ref, sent_low_ref, came_low_ref, sent_high_ref, came_high_ref, out_ref):
+    rows, hidden = came_low_ref.shape
+    narrow = hidden // 2
+    pairs = ((sent_low_ref, came_low_ref), (sent_high_ref, came_high_ref))
+    for side, (sent_ref, came_ref) in enumerate(pairs):
+        kept = pl.program_id(0) == keeps_ref[side]
+        value = jnp.where(kept, sent_ref[...], came_ref[...]).astype(jnp.float32)
+        start = side * rows
+        out_ref[:, start : start + hidden] = value[:hidden]
+        out_ref[:narrow, start + hidden : start + rows] = value[hidden:, :narrow]
+        out_ref[narrow:, start + hidden : start + rows] = value[hidden:, narrow:]
+
+
+def down_output(keeps, sent_low, came_low, sent_high, came_high):
+    rows, hidden = came_low.shape
+    place = sent_low.shape[0] // rows - 1
+    sent = pl.BlockSpec((rows, hidden), lambda e, k: (place, 0))
+    came = pl.BlockSpec((rows, hidden), lambda e, k: (0, 0))
+    return pl.pallas_call(
+        down_kernel,
+        out_shape=jax.ShapeDtypeStruct((2, hidden, 2 * rows), jnp.float32),
+        grid_spec=pltpu.PrefetchScalarGridSpec(
+            num_scalar_prefetch=1,
+            grid=(2,),
+            in_specs=[sent, came, sent, came],
+            out_specs=pl.BlockSpec((None, hidden, 2 * rows), lambda e, k: (e, 0, 0)),
+        ),
+        compiler_params=pltpu.CompilerParams(vmem_limit_bytes=32 << 20),
+        cost_estimate=pl.CostEstimate(flops=0, bytes_accessed=rows, transcendentals=0),
+    )(keeps, sent_low, came_low, sent_high, came_high)
 
 
 def after(values, *others):
@@ -780,32 +896,57 @@
     def send(self, sent):
         bit = self.order[min(self.stage, self.steps - 1 - self.stage)]
         self.sent = sent
-        self.flying = swap(sent, bit)
         self.stage += 1
-
-    def start(self, value):
-        self.kept, sent = halve(value, None, self.order[0])
-        self.send(sent)
-        return self.sent
-
-    def total(self, *others):
-        return self.kept + after(self.flying, *others).astype(jnp.float32)
+        if self.stage < self.steps:
+            self.flying = swap(sent, bit)
 
     def step(self, *others):
         bits = len(self.order)
+        came = after(self.flying, *others)
         if self.stage < bits:
-            came = after(self.flying, *others)
             self.kept, sent = halve(self.kept, came, self.order[self.stage])
             self.send(sent)
         elif self.stage == bits:
-            self.send(self.total(*others).astype(jnp.bfloat16))
+            self.send((self.kept + came.astype(jnp.float32)).astype(jnp.bfloat16))
         else:
-            came = after(self.flying, *others)
             self.send(join(self.sent, came, self.order[self.steps - self.stage], 0))
         return self.sent
 
-    def finish(self, *others):
-        return join(self.sent, after(self.flying, *others), self.order[0], 0)
+    def piece(self, number, count, *others):
+        rows = self.sent.shape[0] // count
+        part = after(self.sent[number * rows : (number + 1) * rows], *others)
+        return swap(part, self.order[0])
+
+
+class Cube:
+    def __init__(self, value, order):
+        self.value = value
+        self.order = order
+        self.stage = 0
+
+    def axis(self, bit):
+        return len(self.order) - bit.bit_length()
+
+    def halve(self, *others):
+        bit = self.order[self.stage]
+        keep = has(bit).astype(jnp.int32)
+        part = lambda index: lax.dynamic_slice_in_dim(self.value, index, 1, self.axis(bit))
+        self.value, sent = part(keep), part(1 - keep).astype(jnp.bfloat16)
+        self.flying = swap(after(sent, *others), bit)
+        self.stage += 1
+        return sent
+
+    def add(self, *others):
+        self.value = self.value + after(self.flying, *others).astype(jnp.float32)
+
+    def back(self, *others):
+        self.stage -= 1
+        self.flying = swap(after(self.value, *others), self.order[self.stage])
+        return self.value
+
+    def join(self, *others):
+        bit = self.order[self.stage]
+        self.value = join(self.value, after(self.flying, *others), bit, self.axis(bit))
 
 
 class Exchange:
@@ -959,62 +1100,50 @@
         segment_rows,
     ) = attend(after(gathered, *ready), gain_one, head_halves, block)
 
-    turned = after(grad_out[0], gathered, *ready)
-    turned = jnp.stack([turned] + [from_chip(turned, k) for k in range(1, chips)])
     part = tokens // copies
+    cotangent = lax.all_gather(after(grad_out[0], *ready), "ctx", axis=0, tiled=True)
     mixed_all = lax.all_gather(
-        lax.dynamic_slice_in_dim(mixed, copy_index * part, part, 0), "ctx", axis=0
+        after(lax.dynamic_slice_in_dim(mixed, copy_index * part, part, 0), cotangent),
+        "ctx",
+        axis=0,
     ).reshape(groups, tokens, query_width)
     w_out_halves = out_exchange.finish(mixed)
-    cotangent = cores(turned, from_core(turned), 1)
-
+
+    wide = min(512, tokens)
     middle, normed_two, gates = middle_rows(
-        mixed_all, after(w_out_halves, cotangent), gathered, gain_two, router_all, block
+        mixed_all, w_out_halves, gathered, gain_two, router_all, wide
     )
     flag = lambda bit: has(bit).astype(jnp.int32)
     place = jnp.stack([chip, me, flag(bits[0]), flag(bits[-1])]).astype(jnp.int32)
     scaled_one, scaled_two, grad_gate_pre, grad_up_pre, grad_live, extra = expert_rows(
-        place, normed_two, cotangent, gathered, gates, w_gate, w_up, w_down
-    )
-
-    pick = experts_own // 2
-
-    def product(side, start, dtype):
+        place, normed_two, cotangent, gathered, gates, w_gate, w_up, w_down, wide
+    )
+    grad_rows, out_rows = expert_sums(
+        place, scaled_one, grad_gate_pre, grad_up_pre, extra, w_gate, w_up, w_down, wide
+    )
+    grad_two_sum = lax.psum_scatter(grad_rows, "ctx", scatter_dimension=0, tiled=True)
+
+    def mine(array):
+        return lax.dynamic_slice_in_dim(array, me * own, own, 0)
+
+    middle_own, gates_own, live_own, normed_own = [
+        mine(array) for array in (middle, gates, grad_live, normed_two)
+    ]
+
+    def product(side, e, dtype):
         right, scaled = ((grad_gate_pre, scaled_one), (grad_up_pre, scaled_two))[side]
-        parts = [
-            expert_product(normed_two, right[e], scaled[e], grad_live, side, dtype)
-            for e in range(start, start + pick)
-        ]
-        return parts[0] if pick == 1 else jnp.concatenate(parts, 0)
-
+        return expert_product(normed_two, right, scaled, grad_live, e, side, dtype)
+
+    normed_two, grad_live = after((normed_two, grad_live), grad_rows)
     chains = [Chain(bits), Chain(bits[::-1])]
     for side, chain in enumerate(chains):
         chain.send(product(side, 0, jnp.bfloat16))
-    grad_rows, out_rows = expert_sums(
-        place,
-        *after((scaled_one, grad_gate_pre, grad_up_pre), *[chain.sent for chain in chains]),
-        extra,
-        w_gate,
-        w_up,
-        w_down,
-        block,
-    )
-    grad_two_sum = lax.psum_scatter(grad_rows, "ctx", scatter_dimension=0, tiled=True)
-    scaled_one, scaled_two, grad_gate_pre, grad_up_pre = after(
-        (scaled_one, scaled_two, grad_gate_pre, grad_up_pre), grad_rows
-    )
+    normed_two, grad_live = after((normed_two, grad_live), *[chain.sent for chain in chains])
     for side, chain in enumerate(chains):
-        chain.kept = product(side, pick, jnp.float32)
-
-    def mine(array):
-        return lax.dynamic_slice_in_dim(array, me * own, own, 0)
-
-    sent = [c.kept for c in chains]
-    while chains[0].stage < len(bits):
-        sent = [chain.step(*sent) for chain in chains]
-    middle_own, gates_own, live_own = mine(middle), mine(gates), mine(grad_live)
+        chain.kept = product(side, 1, jnp.float32)
+
     grad_middle, grad_branch, grad_mixed, grad_logits, gain_two_grad = turn_rows(
-        after(grad_two_sum, *sent),
+        after(grad_two_sum, *[(c.kept, c.flying) for c in chains]),
         gates_own,
         router_all,
         gain_two,
@@ -1022,12 +1151,24 @@
         live_own,
         w_out_halves,
     )
-    grad_mixed_all = lax.all_to_all(
-        jnp.repeat(grad_mixed, copies, 0), "ctx", split_axis=0, concat_axis=0, tiled=True
-    ).reshape(tokens, query_width)
     grad_branch_all = lax.all_gather(grad_branch, "ctx", axis=0, tiled=True)
 
-    sent = [chain.step(grad_mixed) for chain in chains]
+    def deal(blocks, *others):
+        blocks = blocks.reshape((chips, 2) + blocks.shape[1:])
+        got = [blocks[(chip - k) % chips] for k in range(chips)]
+        got = jnp.stack([got[0]] + [from_chip(got[k], k) for k in range(1, chips)])
+        got = after(got, *others)
+        stay = jnp.where(odd, got[:, 1], got[:, 0])
+        go = from_core(jnp.where(odd, got[:, 0], got[:, 1]))
+        both = cores(stay[:, None], go[:, None], 1)
+        both = jnp.concatenate([both, both], 0)
+        both = lax.dynamic_slice_in_dim(both, (chips - chip) % chips, chips, 0)
+        return both.reshape((size,) + both.shape[2:])
+
+    grad_mixed_all = deal(jnp.repeat(grad_mixed, copies, 0)).reshape(tokens, query_width)
+    sent = [grad_mixed_all]
+    while chains[0].stage < len(bits):
+        sent = [chain.step(*sent) for chain in chains]
     grad_query, grad_pair = attend_back(
         query,
         after(grad_mixed_all, *sent),
@@ -1044,76 +1185,84 @@
         counted = (places // part == copy_index)[:, None]
         grad_query = jnp.where(counted, grad_query, jnp.zeros((), jnp.bfloat16))
         grad_pair = jnp.where(counted, grad_pair, jnp.zeros((), jnp.bfloat16))
-    grad_one_low, head_product, gain_one_grad = close_rows(
-        grad_query, grad_pair, head_all, gathered, normed_one, block
+    sent = [chain.step(grad_pair) for chain in chains]
+    grad_one_low, head_grads = close_rows(
+        after(grad_query, *sent),
+        grad_pair,
+        head_all,
+        gathered,
+        normed_one,
+        gain_two_grad,
+        normed_own,
+        grad_logits,
+        rows_own,
+        side_width,
+        block,
     )
     grad_one = lax.psum_scatter(
         grad_one_low, "ctx", scatter_dimension=0, tiled=True
     ).astype(jnp.float32)
-    head_grads = jnp.concatenate(
-        [
-            head_product,
-            gain_one_grad.reshape(-1, 1),
-            gain_two_grad.reshape(-1, 1),
-            dot(mine(normed_two), grad_logits, ROWS),
-        ],
-        1,
-    )
-
-    spread = head_grads.reshape((size,) + (2,) * len(bits) + (share, used))
-    axes = list(range(1, len(bits) + 1))
-    head_chains = [Chain(bits), Chain(bits[::-1])]
-    sent = []
-    for h, chain in enumerate(head_chains):
-        part_grads = spread[h * (size // 2) : (h + 1) * (size // 2)]
-        lead = axes[::-1] if h == 0 else axes
-        part_grads = jnp.transpose(part_grads, lead + [0, len(bits) + 1, len(bits) + 2])
-        sent.append(chain.start(part_grads.reshape(-1, used)))
-
-    sent = [chain.step(*sent) for chain in chains]
     grad_proj_out = dot(
         lax.dynamic_slice_in_dim(mixed, copy_index * rows_own, rows_own, 1),
-        after(grad_branch_all, *sent),
+        grad_branch_all,
         ROWS,
     )
-    while head_chains[0].stage < len(bits):
-        sent = [chain.step(*sent) for chain in head_chains]
-    totals = [chain.total(*sent) for chain in head_chains]
-    totals = jnp.concatenate(
-        [total.reshape(size // 2, share, used) for total in totals], 0
-    ).astype(jnp.bfloat16)
-    head_sums = lax.all_to_all(totals, "ctx", split_axis=0, concat_axis=0, tiled=True)
-    out_chain = Chain(bits[::-1])
-    out_sent = out_chain.start(after(grad_proj_out, totals))
-    while out_chain.stage < len(bits):
-        out_sent = out_chain.step(out_sent)
-    back = Exchange(after(head_sums, out_sent), bits)
-    out_chain.step(*back.values)
-    while out_chain.stage < out_chain.steps:
-        ready = back.step(out_chain.sent) if back.stage < len(bits) - 1 else []
-        out_chain.step(*ready)
-    halves = back.finish(out_chain.sent)
-    head_rows = jnp.concatenate(halves, 0).reshape(size, rows_own, used).astype(jnp.float32)
-    if copies > 1:
-        head_rows = jnp.sum(head_rows.reshape(groups, copies, rows_own, used), 1)
-    side = lambda begin, end: jnp.transpose(head_rows[:, :, begin:end], (1, 0, 2)).reshape(
-        rows_own, -1
-    )
-    small = jnp.sum(head_rows[:, :, width:], 0)
-    head_outs = (
-        side(0, query_width),
-        side(query_width, query_width + HEAD_SIZE),
-        side(query_width + HEAD_SIZE, width),
-    )
-    grad_out_rows = out_chain.finish(*head_outs).astype(jnp.float32)
+
+    line = size // 2 * side_width
+    half = MODEL_WIDTH // 2
+    cubes = []
+    for h, order in enumerate((bits, bits[::-1])):
+        rows = jnp.concatenate(
+            [
+                head_grads[:, h * line : (h + 1) * line],
+                grad_proj_out[:, h * half : (h + 1) * half],
+            ],
+            1,
+        )
+        cubes.append(Cube(rows.reshape((2,) * len(bits) + (share, line + half)), order))
+    sent = [cube.halve() for cube in cubes]
     while chains[0].stage < chains[0].steps:
-        sent = [chain.step(grad_out_rows) for chain in chains]
-    expert_parts = []
-    for chain in chains:
-        value = chain.finish(grad_out_rows, *head_outs)
-        expert_parts.append(split_product(value.reshape(experts_own, -1, value.shape[1])))
-    grad_gate, grad_up = [parts[0].astype(jnp.float32) for parts in expert_parts]
-    grad_down = jnp.concatenate([parts[1] for parts in expert_parts], 2).astype(jnp.float32)
+        sent = [chain.step(*sent) for chain in chains]
+    while cubes[0].stage < len(bits):
+        for cube in cubes:
+            cube.add(*sent)
+        sent = [cube.halve() for cube in cubes]
+    first = [chain.piece(0, 3, *sent) for chain in chains]
+    for cube in cubes:
+        cube.add(*sent)
+    totals = [cube.value.astype(jnp.bfloat16) for cube in cubes]
+    blocks = jnp.concatenate(
+        [
+            jnp.transpose(
+                total.reshape(share, -1)[:, :line].reshape(share, size // 2, side_width), (1, 0, 2)
+            )
+            for total in totals
+        ],
+        0,
+    )
+    head_sums = deal(blocks)
+    for h, cube in enumerate(cubes):
+        rows = jnp.transpose(head_sums[h * (size // 2) : (h + 1) * (size // 2)], (1, 0, 2))
+        rows = jnp.concatenate(
+            [rows.reshape(share, line), totals[h].reshape(share, -1)[:, line:]], 1
+        )
+        cube.value = rows.reshape(totals[h].shape)
+    sent = [cube.back() for cube in cubes]
+    second = [chain.piece(1, 3, *sent) for chain in chains]
+    while cubes[0].stage > 0:
+        for cube in cubes:
+            cube.join(*sent)
+        sent = [cube.back() for cube in cubes]
+    third = [chain.piece(2, 3, *sent, *first) for chain in chains]
+    keeps = place[2:]
+    grad_gate, grad_up = [
+        into_output(keeps, side, *after((chain.sent, first[side], second[side]), *sent))
+        for side, chain in enumerate(chains)
+    ]
+    for cube in cubes:
+        cube.join(grad_gate, grad_up)
+    head_outs = head_outputs(*[cube.value.reshape(rows_own, -1) for cube in cubes], copies, side_width)
+    small = head_outs[4]
 
     moe_sum = lax.psum_scatter(
         after(out_rows, grad_branch), "ctx", scatter_dimension=0, tiled=True
@@ -1122,15 +1271,18 @@
     own_hidden = inputs[0].astype(jnp.float32)
     own_scale = lax.rsqrt(jnp.mean(own_hidden * own_hidden, -1, keepdims=True) + EPS)
     grad_in = grad_middle + norm_back(grad_one * gain_one, own_hidden * own_scale, own_scale)
+    grad_down = down_output(
+        keeps,
+        *after((chains[0].sent, third[0], chains[1].sent, third[1]), head_outs, grad_in, output),
+    )
 
     return (
         output.astype(jnp.bfloat16)[None],
         grad_in[None],
         small[:, 0],
-        *head_outs,
-        grad_out_rows,
+        *head_outs[:4],
         small[:, 1],
-        small[:, 2:],
+        small[:, 8 : 8 + experts_all],
         grad_gate,
         grad_up,
         grad_down,

time: 561 us -> 543 us (0.968)
  Pallas kernels: 104 us -> 139 us
  starting transfers between devices: 84.8 us -> 56 us
  local copies, waits for them, and re-layouts: 78.8 us -> 51.7 us
  waiting for transfers between devices: 199 us -> 224 us
  other arithmetic: 65.4 us -> 46.1 us
    all_gather x1 -> x2, waiting for transfers between devices: 15 us -> 39.1 us  [the longest x1 25.5 us: per_device(): lax.all_gather(after(grad_out[0], *ready), 'ctx', axis=0, tiled=True)]
    all_to_all x2 -> x0, starting transfers between devices: 21.8 us -> none  [the longest x1 11.1 us: per_device(): lax.all_to_all(totals, 'ctx', split_axis=0, concat_axis=0, tiled=True)]
    pallas_call x0 -> x4, Pallas kernels: none -> 17.1 us  [the longest x2 10.3 us: into_output(): pl.pallas_call(lambda k, *refs: into_kernel(k, side, *refs), name='into_o...]
    convert_element_type x8 -> x2, other arithmetic: 20 us -> 5.04 us  [step(): self.send((self.kept + came.astype(jnp.float32)).astype(jnp.bfloat16))]
    ppermute x6 -> x9, waiting for transfers between devices: 51.6 us -> 38.6 us  [from_chip(): lax.ppermute(value, 'ctx', [(i, (i - 2 * k) % size) for i in range(size)])]
    ppermute x28, waiting for transfers between devices: 130 us -> 142 us  [swap(): return lax.ppermute(value, 'rep', [(i, i ^ bit) for i in range(size)])]
    transpose x5 -> x0, local copies, waits for them, and re-layouts: 8.09 us -> none  [per_device(): jnp.transpose(head_rows[:, :, begin:end], (1, 0, 2)).reshape(rows_own, -1)]
    squeeze x8 -> x0, local copies, waits for them, and re-layouts: 7.12 us -> none  [the longest x4 4.25 us: product(): scaled[e]]
  transfers between devices with their start and end apart: 44 -> 47, of which waited for: 21 -> 28; matrix products, arithmetic and copies ran while one was open for 18% -> 11% of each run, Pallas kernels for 5% -> 15%
where the time goes in v4:
time: 543 us; the launch traced here: 535 us
  waiting for transfers between devices  224 us (41%)
  Pallas kernels  139 us (26%)
  starting transfers between devices  56 us (10%)
  local copies, waits for them, and re-layouts  51.7 us (10%)
  other arithmetic  46.1 us (8%)
  between operations  15.6 us (3%)
    ppermute x28, waiting for transfers between devices, swap(): return lax.ppermute(value, 'rep', [(i, i ^ bit) for i in range(size)])  142 us
    ppermute x9, waiting for transfers between devices, from_chip(): lax.ppermute(value, 'ctx', [(i, (i - 2 * k) % size) for i in range(size)])  38.6 us
    unnamed x167, local copies, waits for them, and re-layouts  38.2 us
    ppermute x28, starting transfers between devices, swap(): return lax.ppermute(value, 'rep', [(i, i ^ bit) for i in range(size)])  31.8 us
    all_gather x1, waiting for transfers between devices, per_device(): lax.all_gather(after(grad_out[0], *ready), 'ctx', axis=0, tiled=True)  25.5 us
    pallas_call x4, Pallas kernels, expert_product(): pl.pallas_call(product_kernel, out_shape=jax.ShapeDtypeStruct((features +...  24.4 us
    ppermute x9, starting transfers between devices, from_chip(): lax.ppermute(value, 'ctx', [(i, (i - 2 * k) % size) for i in range(size)])  23.8 us
    pallas_call x1, Pallas kernels, expert_rows(): pl.pallas_call(expert_kernel, out_shape=(wide, wide, wide, wide, jax.Shap...  20.1 us
  transfers between devices with their start and end apart: 47, of which 28 were waited for; matrix products, arithmetic and copies ran while one was open for 11% of the time, Pallas kernels for 15%

profile of v4, /device:TPU:0, one launch (start us, length us, event | category | flops | bytes accessed | tf_op | source)
XLA Modules:
  0.0 534.9 jit_solution(13426658840824545243)
XLA Ops:
  14.7 3.1 collective-permute-start.2
  17.8 2.6 collective-permute-start.1
  21.8 4.5 collective-permute-done.2
  26.2 19.1 %collective-permute-done.1 = bf16[48,2304]{1,0:T(8,128)(2,1)S(1)} collective-permute-done((bf16[48,2304]{1,0:T(8,128)(2,1)S(1)}, bf16[48,2304]{1,0:T(8,128)(2,1)S(1)}, u32[]{:S(2)}, u32[]{:S(2)}) %collective-permute-start.1) | collective-permute-done | bytes 221216 | tf_op jit(solution)/shard_map/ppermute | solution.py:1036
  45.8 2.2 collective-permute-done.3
  52.2 2.9 collective-permute-done.7
  60.8 5.6 %collective-permute-done.6 = bf16[4,1,2,48,384]{4,3,0,2,1:T(8,128)(2,1)S(1)} collective-permute-done((bf16[4,1,2,48,384]{4,3,0,2,1:T(8,128)(2,1)S(1)}, bf16[4,1,2,48,384]{4,3,0,2,1:T(8,128)(2,1)S(1)}, u32[]{:S(2)}, u32[]{:S(2)}) %collective-permute-start.6) | collective-permute-done | bytes 294944 | tf_op jit(solution)/shard_map/ppermute | solution.py:864
  66.7 12.1 %collective-permute-done.8 = bf16[4,2,1,48,384]{4,3,0,2,1:T(8,128)(2,1)S(1)} collective-permute-done((bf16[4,2,1,48,384]{4,3,0,2,1:T(8,128)(2,1)S(1)}, bf16[4,2,1,48,384]{4,3,0,2,1:T(8,128)(2,1)S(1)}, u32[]{:S(2)}, u32[]{:S(2)}) %collective-permute-start.8) | collective-permute-done | bytes 294944 | tf_op jit(solution)/shard_map/ppermute | solution.py:864
  83.0 17.7 %shard_map.238 = (bf16[1024,1536]{1,0:T(8,128)(2,1)}, bf16[1024,192]{1,0:T(8,128)(2,1)S(1)}, bf16[1024,64]{1,0:T(8,128)(2,1)S(1)}, bf16[1024,64]{1,0:T(8,128)(2,...) custom-call(bf16[1024,1664]{1,0:T(8,128)(2,1)} %all-gather.6.cloned., ...), custom_call_target="tpu_custom_call" | custom-call | bytes 1024 | tf_op jit(solution)/shard_map/pallas_call | solution.py:179
  106.2 25.5 %all-gather.8.cloned.1.call-done.cotangent_ref = bf16[1024,1536]{1,0:T(8,128)(2,1)} async-done(((bf16[128,1536]{1,0:T(8,128)(2,1)}), bf16[1024,1536]{1,0:T(8,128)(2,1)}) %all-gather.8.cloned.1.call-update) | async-done | bytes 3145744 | tf_op jit(solution)/shard_map/all_gather | solution.py:1104
  135.0 25.2 %collective-permute-done.10 = bf16[4,1,2,48,1536]{4,3,0,2,1:T(8,128)(2,1)} collective-permute-done((bf16[4,1,2,48,1536]{4,3,0,2,1:T(8,128)(2,1)}, bf16[4,1,2,48,1536]{4,3,0,2,1:T(8,128)(2,1)}, u32[]{:S(2)}, u32[]{:S(2)}) %collective-permute-start.10) | collective-permute-done | bytes 1179680 | tf_op jit(solution)/shard_map/ppermute | solution.py:864
  165.7 13.6 %all-gather.12.cloned.1.call-done = bf16[8192,192]{1,0:T(8,128)(2,1)} async-done(((bf16[1024,192]{1,0:T(8,128)(2,1)}), bf16[8192,192]{1,0:T(8,128)(2,1)}) %all-gather.12.cloned.1.call-update) | async-done | bytes 3145744 | tf_op jit(solution)/shard_map/all_gather | solution.py:1105
  181.0 12.1 %shard_map.239 = (f32[1024,1536]{1,0:T(8,128)}, bf16[1024,1536]{1,0:T(8,128)(2,1)}, f32[1024,16]{1,0:T(8,128)S(1)}) custom-call(bf16[8,1024,192]{2,1,0:T(8,128)(2,1)} %bitcast.237, bf16[768,1536]{1,0:T(8,128)(2,1)S(1)} %bitcast.193, bf16[768,1536]{1,0:T(8,128)(2,1)S(1)} %bitcast.195, bf16[1024,1664]{1,0:T(8,128)(2,1)} %all-gather.6.cloned.1.call-done.hidden_ref.column_ref, ...), custom_call_target="tpu_custom_call" | custom-call | flops 4831838208 | bytes 18874368 | tf_op jit(solution)/shard_map/pallas_call | solution.py:373
  193.2 20.1 %shard_map.240 = (bf16[2,1024,512]{2,1,0:T(8,128)(2,1)}, bf16[2,1024,512]{2,1,0:T(8,128)(2,1)}, bf16[2,1024,512]{2,1,0:T(8,128)(2,1)}, bf16[2,1024,512]{2,1,0:T(...) custom-call(s32[4]{0:T(128)S(1)} %pad_add_fusion.place_ref, ...), custom_call_target="tpu_custom_call" | custom-call | flops 9663676416 | bytes 25165824 | tf_op jit(solution)/shard_map/pallas_call | solution.py:466
  213.3 17.1 %shard_map.241 = (bf16[1024,1664]{1,0:T(8,128)(2,1)}, bf16[1024,1536]{1,0:T(8,128)(2,1)}) custom-call(s32[4]{0:T(128)S(1)} %pad_add_fusion.place_ref, bf16[2,1024,512]{2,1,0:T(8,128)(2,1)} %get-tuple-element.102.scaled_ref, bf16[2,1024,512]{2,1,0:T(8,128)(2,1)} %get-tuple-element.103.grad_gate_ref.right_ref, ...), custom_call_target="tpu_custom_call" | custom-call | bytes 1024 | tf_op jit(solution)/shard_map/pallas_call | solution.py:580
  237.7 6.1 %shard_map.242 = bf16[2304,512]{1,0:T(8,128)(2,1)} custom-call(bf16[1024,1536]{1,0:T(8,128)(2,1)S(1)} %copy-done.2, bf16[2,1024,512]{2,1,0:T(8,128)(2,1)S(1)} %copy-done.11, bf16[2,1024,512]{2,1,0:T(8,128)(2,1)S(1)} %copy-done.9, bf16[1024,1536]{1,0:T(8,128)(2,1)S(1)} %copy-done.3), custom_call_target="tpu_custom_call" | custom-call | bytes 1024 | tf_op jit(solution)/shard_map/pallas_call | solution.py:530
  243.7 5.6 %shard_map.243 = bf16[2304,512]{1,0:T(8,128)(2,1)} custom-call(bf16[1024,1536]{1,0:T(8,128)(2,1)S(1)} %copy-done.2, bf16[2,1024,512]{2,1,0:T(8,128)(2,1)S(1)} %copy-done.7, bf16[2,1024,512]{2,1,0:T(8,128)(2,1)S(1)} %copy-done.21, bf16[1024,1536]{1,0:T(8,128)(2,1)S(1)} %copy-done.3), custom_call_target="tpu_custom_call" | custom-call | bytes 1024 | tf_op jit(solution)/shard_map/pallas_call | solution.py:530
  257.3 6.4 %shard_map.244 = f32[2304,512]{1,0:T(8,128)} custom-call(bf16[1024,1536]{1,0:T(8,128)(2,1)S(1)} %copy-done.2, bf16[2,1024,512]{2,1,0:T(8,128)(2,1)S(1)} %copy-done.12, bf16[2,1024,512]{2,1,0:T(8,128)(2,1)S(1)} %copy-done.10, bf16[1024,1536]{1,0:T(8,128)(2,1)S(1)} %copy-done.4), custom_call_target="tpu_custom_call" | custom-call | bytes 1024 | tf_op jit(solution)/shard_map/pallas_call | solution.py:530
  263.7 6.4 %shard_map.245 = f32[2304,512]{1,0:T(8,128)} custom-call(bf16[1024,1536]{1,0:T(8,128)(2,1)S(1)} %copy-done.2, bf16[2,1024,512]{2,1,0:T(8,128)(2,1)S(1)} %copy-done.8, bf16[2,1024,512]{2,1,0:T(8,128)(2,1)S(1)} %copy-done.22, bf16[1024,1536]{1,0:T(8,128)(2,1)S(1)} %copy-done.4), custom_call_target="tpu_custom_call" | custom-call | bytes 1024 | tf_op jit(solution)/shard_map/pallas_call | solution.py:530
  274.4 28.7 %collective-permute-done.12 = bf16[2304,512]{1,0:T(8,128)(2,1)} collective-permute-done((bf16[2304,512]{1,0:T(8,128)(2,1)}, bf16[2304,512]{1,0:T(8,128)(2,1)}, u32[]{:S(2)}, u32[]{:S(2)}) %collective-permute-start.12) | collective-permute-done | bytes 2359328 | tf_op jit(solution)/shard_map/ppermute | solution.py:864
  311.5 2.3 shard_map.246
  320.2 2.7 collective-permute-start.14
  322.9 4.1 collective-permute-done.16
  327.0 9.8 %collective-permute-done.15 = bf16[2,128,192]{2,1,0:T(8,128)(2,1)S(1)} collective-permute-done((bf16[2,128,192]{2,1,0:T(8,128)(2,1)S(1)}, bf16[2,128,192]{2,1,0:T(8,128)(2,1)S(1)}, u32[]{:S(2)}, u32[]{:S(2)}) %collective-permute-start.15) | collective-permute-done | bytes 98336 | tf_op jit(solution)/shard_map/ppermute | solution.py:1036
  341.6 3.5 add_convert_fusion.3
  346.5 3.4 add_convert_fusion.2
  352.3 17.2 %shard_map.247 = (bf16[1024,192]{1,0:T(8,128)(2,1)S(1)}, bf16[1024,128]{1,0:T(8,128)(2,1)S(1)}) custom-call(bf16[1024,192]{1,0:T(8,128)(2,1)S(1)} %copy-done.35, bf16[1024,192]{1,0:T(8,128)(2,1)S(1)} %bitcast.199, f32[3,1024,1]{2,1,0:T(8,128)S(1)} %copy-done.29, f32[1024,64]{1,0:T(8,128)S(1)} %copy-done.25, f32[1024,64]{1,0:T(8,128)S(1)} %copy-done.27, ...), custom_call_target="tpu_custom_call" | custom-call | bytes 1024 | tf_op jit(solution)/shard_map/pallas_call | solution.py:303
  369.5 3.9 collective-permute-done.18
  373.4 4.6 collective-permute-done.19
  378.0 2.9 add_convert_fusion.1
  384.2 10.6 %shard_map.248 = (bf16[1024,1536]{1,0:T(8,128)(2,1)}, f32[192,3072]{1,0:T(8,128)S(1)}) custom-call(bf16[1024,192]{1,0:T(8,128)(2,1)S(1)} %get-tuple-element.133.query_ref, bf16[1024,128]{1,0:T(8,128)(2,1)S(1)} %get-tuple-element.130.pair_ref, bf16[1536,384]{1,0:T(8,128)(2,1)S(1)} %pad_maximum_fusion.6.weight_ref, ...), custom_call_target="tpu_custom_call" | custom-call | bytes 1024 | tf_op jit(solution)/shard_map/pallas_call | solution.py:727
  396.5 2.9 fusion.41
  402.9 5.2 collective-permute-done.21
  409.5 3.5 collective-permute-done.22
  417.6 2.6 collective-permute-done.20
  421.6 3.0 collective-permute-done.24
  424.8 2.7 collective-permute-done.23
  427.6 3.2 collective-permute-done.25
  431.7 9.9 %collective-permute-start.28 = (bf16[2,48,384]{2,1,0:T(8,128)(2,1)S(1)}, bf16[2,48,384]{2,1,0:T(8,128)(2,1)S(1)}, u32[]{:S(2)}, u32[]{:S(2)}) collective-permute-start(bf16[2,48,384]{2,1,0:T(8,128)(2,1)S(1)} %get-tuple-element.284), channel_id=1, source_target_pairs={{0,2},{1,3},{2,4},{3,5},{4,6},{5,7},{6,0},{7,1},{8,10},{9,11},{10,... | collective-permute-start | bytes 221192 | tf_op jit(solution)/shard_map/ppermute | solution.py:1036
  441.6 2.6 collective-permute-start.26
  444.3 3.1 fusion.38
  457.1 19.1 %collective-permute-done.30 = bf16[1,1,48,2304]{3,2,1,0:T(8,128)(2,1)S(1)} collective-permute-done((bf16[1,1,48,2304]{3,2,1,0:T(8,128)(2,1)S(1)}, bf16[1,1,48,2304]{3,2,1,0:T(8,128)(2,1)S(1)}, u32[]{:S(2)}, u32[]{:S(2)}) %collective-permute-start.30) | collective-permute-done | bytes 221216 | tf_op jit(solution)/shard_map/ppermute | solution.py:864
  478.5 13.1 %collective-permute-done.34 = bf16[1,1,48,2304]{3,2,1,0:T(8,128)(2,1)S(1)} collective-permute-done((bf16[1,1,48,2304]{3,2,1,0:T(8,128)(2,1)S(1)}, bf16[1,1,48,2304]{3,2,1,0:T(8,128)(2,1)S(1)}, u32[]{:S(2)}, u32[]{:S(2)}) %collective-permute-start.34) | collective-permute-done | bytes 221216 | tf_op jit(solution)/shard_map/ppermute | solution.py:864
  498.9 5.1 into_output.2
  504.0 5.2 into_output.3
  516.7 2.3 fusion.9
  520.6 2.3 collective-permute-done.39.came_high_ref
  522.9 4.9 shard_map.249
  (362 shorter events, 127.1 us)
Async XLA Ops:
  7.2 75.8 %all-gather.6.cloned.1.call-start = ((), (), s32[]{:S(2)}) async-start(), calls=%async_computation.3 | async-start | bytes 3833856 | tf_op jit(solution)/shard_map/all_gather | solution.py:1031
  11.2 120.5 %all-gather.8.cloned.1.call-start = ((), (), s32[]{:S(2)}) async-start(), calls=%async_computation.4 | async-start | bytes 3538944 | tf_op jit(solution)/shard_map/all_gather | solution.py:1104
  14.7 11.5 %collective-permute-start.2 = (bf16[48,2304]{1,0:T(8,128)(2,1)S(1)}, bf16[48,2304]{1,0:T(8,128)(2,1)S(1)}, u32[]{:S(2)}, u32[]{:S(2)}) collective-permute-start(bf16[48,2304]{1,0:T(8,128)(2,1)S(1)} %get-tuple-element.298), channel_id=1, source_target_pairs={{0,2},{1,3},{2,4},{3,5},{4,6},{5,7},{6,0},{7,1},{8,10},{9,11},{10,... | collective-permute-start | bytes 663560 | tf_op jit(solution)/shard_map/ppermute | solution.py:1036
  17.8 27.6 %collective-permute-start.1 = (bf16[48,2304]{1,0:T(8,128)(2,1)S(1)}, bf16[48,2304]{1,0:T(8,128)(2,1)S(1)}, u32[]{:S(2)}, u32[]{:S(2)}) collective-permute-start(bf16[48,2304]{1,0:T(8,128)(2,1)S(1)} %get-tuple-element.297), channel_id=1, source_target_pairs={{0,4},{1,5},{2,6},{3,7},{4,0},{5,1},{6,2},{7,3},{8,12},{9,13},{10,... | collective-permute-start | bytes 663560 | tf_op jit(solution)/shard_map/ppermute | solution.py:1036
  20.4 25.0 %collective-permute-start = (bf16[48,2304]{1,0:T(8,128)(2,1)S(1)}, bf16[48,2304]{1,0:T(8,128)(2,1)S(1)}, u32[]{:S(2)}, u32[]{:S(2)}) collective-permute-start(bf16[48,2304]{1,0:T(8,128)(2,1)S(1)} %get-tuple-element.296), channel_id=1, source_target_pairs={{0,6},{1,7},{2,0},{3,1},{4,2},{5,3},{6,4},{7,5},{8,14},{9,15},{10,... | collective-permute-start | bytes 663560 | tf_op jit(solution)/shard_map/ppermute | solution.py:1036
  45.7 2.3 collective-permute-start.3
  49.1 6.0 %collective-permute-start.7 = (bf16[4,1,1,48,384]{4,3,0,2,1:T(8,128)(2,1)S(1)}, bf16[4,1,1,48,384]{4,3,0,2,1:T(8,128)(2,1)S(1)}, u32[]{:S(2)}, u32[]{:S(2)}) collective-permute-start(bf16[4,1,1,48,384]{4,3,0,2,1:T(8,128)(2,1)S(1)} %get-tuple-element.249), channel_id=1, source_target_pairs={{0,16},{8,24},{16,0},{24,8},{1,17},{9,25},{17,1},{25,9},{2,18},{10... | collective-permute-start | bytes 442376 | tf_op jit(solution)/shard_map/ppermute | solution.py:864
  50.7 5.6 %collective-permute-start.5 = (bf16[4,1,1,48,384]{4,3,0,2,1:T(8,128)(2,1)S(1)}, bf16[4,1,1,48,384]{4,3,0,2,1:T(8,128)(2,1)S(1)}, u32[]{:S(2)}, u32[]{:S(2)}) collective-permute-start(bf16[4,1,1,48,384]{4,3,0,2,1:T(8,128)(2,1)S(1)} %get-tuple-element.250), channel_id=1, source_target_pairs={{0,8},{8,0},{16,24},{24,16},{1,9},{9,1},{17,25},{25,17},{2,10},{10... | collective-permute-start | bytes 442376 | tf_op jit(solution)/shard_map/ppermute | solution.py:864
  56.4 10.0 %collective-permute-start.6 = (bf16[4,1,2,48,384]{4,3,0,2,1:T(8,128)(2,1)S(1)}, bf16[4,1,2,48,384]{4,3,0,2,1:T(8,128)(2,1)S(1)}, u32[]{:S(2)}, u32[]{:S(2)}) collective-permute-start(bf16[4,1,2,48,384]{4,3,0,2,1:T(8,128)(2,1)S(1)} %pad_maximum_fusion.19), channel_id=1, source_target_pairs={{0,16},{8,24},{16,0},{24,8},{1,17},{9,25},{17,1},{25,9},{2,18},{10... | collective-permute-start | bytes 884744 | tf_op jit(solution)/shard_map/ppermute | solution.py:864
  57.1 21.9 %collective-permute-start.9 = (bf16[4,1,1,48,1536]{4,3,0,2,1:T(8,128)(2,1)S(1)}, bf16[4,1,1,48,1536]{4,3,0,2,1:T(8,128)(2,1)S(1)}, u32[]{:S(2)}, u32[]{:S(2)}) collective-permute-start(bf16[4,1,1,48,1536]{4,3,0,2,1:T(8,128)(2,1)S(1)} %get-tuple-element.245), channel_id=1, source_target_pairs={{0,16},{8,24},{16,0},{24,8},{1,17},{9,25},{17,1},{25,9},{2,18},{10... | collective-permute-start | bytes 1769480 | tf_op jit(solution)/shard_map/ppermute | solution.py:864
  58.7 20.3 %collective-permute-start.4 = (bf16[4,1,1,48,1536]{4,3,0,2,1:T(8,128)(2,1)S(1)}, bf16[4,1,1,48,1536]{4,3,0,2,1:T(8,128)(2,1)S(1)}, u32[]{:S(2)}, u32[]{:S(2)}) collective-permute-start(bf16[4,1,1,48,1536]{4,3,0,2,1:T(8,128)(2,1)S(1)} %get-tuple-element.246), channel_id=1, source_target_pairs={{0,8},{8,0},{16,24},{24,16},{1,9},{9,1},{17,25},{25,17},{2,10},{10... | collective-permute-start | bytes 1769480 | tf_op jit(solution)/shard_map/ppermute | solution.py:864
  60.2 18.6 %collective-permute-start.8 = (bf16[4,2,1,48,384]{4,3,0,2,1:T(8,128)(2,1)S(1)}, bf16[4,2,1,48,384]{4,3,0,2,1:T(8,128)(2,1)S(1)}, u32[]{:S(2)}, u32[]{:S(2)}) collective-permute-start(bf16[4,2,1,48,384]{4,3,0,2,1:T(8,128)(2,1)S(1)} %pad_maximum_fusion.20), channel_id=1, source_target_pairs={{0,8},{8,0},{16,24},{24,16},{1,9},{9,1},{17,25},{25,17},{2,10},{10... | collective-permute-start | bytes 884744 | tf_op jit(solution)/shard_map/ppermute | solution.py:864
  66.6 68.2 %copy-start.13 = (bf16[4,2,2,48,384]{4,3,2,1,0:T(8,128)(2,1)}, bf16[4,2,2,48,384]{4,3,2,1,0:T(8,128)(2,1)S(1)}, u32[]{:S(2)}) copy-start(bf16[4,2,2,48,384]{4,3,2,1,0:T(8,128)(2,1)S(1)} %copy.94) | copy-start | bytes 1769476
  81.7 97.7 %all-gather.12.cloned.1.call-start = ((), (), s32[]{:S(2)}) async-start(), calls=%async_computation.9 | async-start | bytes 4718592 | tf_op jit(solution)/shard_map/all_gather | solution.py:1105
  131.7 172.5 %reduce-scatter.4.cloned.1.call-start = ((), (), s32[]{:S(2)}) async-start(), calls=%async_computation.5 | async-start | bytes 3833856 | tf_op jit(solution)/shard_map/reduce_scatter | solution.py:1124
  131.8 28.5 %collective-permute-start.10 = (bf16[4,1,2,48,1536]{4,3,0,2,1:T(8,128)(2,1)}, bf16[4,1,2,48,1536]{4,3,0,2,1:T(8,128)(2,1)}, u32[]{:S(2)}, u32[]{:S(2)}) collective-permute-start(bf16[4,1,2,48,1536]{4,3,0,2,1:T(8,128)(2,1)} %pad_maximum_fusion.7), channel_id=1, source_target_pairs={{0,16},{8,24},{16,0},{24,8},{1,17},{9,25},{17,1},{25,9},{2,18},{10... | collective-permute-start | bytes 3538952 | tf_op jit(solution)/shard_map/ppermute | solution.py:864
  133.3 29.0 %collective-permute-start.11 = (bf16[4,2,1,48,1536]{4,3,0,2,1:T(8,128)(2,1)}, bf16[4,2,1,48,1536]{4,3,0,2,1:T(8,128)(2,1)S(1)}, u32[]{:S(2)}, u32[]{:S(2)}) collective-permute-start(bf16[4,2,1,48,1536]{4,3,0,2,1:T(8,128)(2,1)} %pad_maximum_fusion.8), channel_id=1, source_target_pairs={{0,8},{8,0},{16,24},{24,16},{1,9},{9,1},{17,25},{25,17},{2,10},{10... | collective-permute-start | bytes 3538952 | tf_op jit(solution)/shard_map/ppermute | solution.py:864
  230.5 166.0 %all-gather.10.cloned.1.call-start = ((), (), s32[]{:S(2)}) async-start(), calls=%async_computation.8 | async-start | bytes 3538944 | tf_op jit(solution)/shard_map/all_gather | solution.py:1154
  249.4 53.7 %collective-permute-start.12 = (bf16[2304,512]{1,0:T(8,128)(2,1)}, bf16[2304,512]{1,0:T(8,128)(2,1)}, u32[]{:S(2)}, u32[]{:S(2)}) collective-permute-start(bf16[2304,512]{1,0:T(8,128)(2,1)} %shard_map.242), channel_id=1, source_target_pairs={{0,8},{8,0},{16,24},{24,16},{1,9},{9,1},{17,25},{25,17},{2,10},{10... | collective-permute-start | bytes 7077896 | tf_op jit(solution)/shard_map/ppermute | solution.py:864
  250.7 53.5 %collective-permute-start.13 = (bf16[2304,512]{1,0:T(8,128)(2,1)}, bf16[2304,512]{1,0:T(8,128)(2,1)}, u32[]{:S(2)}, u32[]{:S(2)}) collective-permute-start(bf16[2304,512]{1,0:T(8,128)(2,1)} %shard_map.243), channel_id=1, source_target_pairs={{0,16},{8,24},{16,0},{24,8},{1,17},{9,25},{17,1},{25,9},{2,18},{10... | collective-permute-start | bytes 7077896 | tf_op jit(solution)/shard_map/ppermute | solution.py:864
  316.9 178.8 %reduce-scatter.6.cloned.1.call-start = ((), (), s32[]{:S(2)}) async-start(), calls=%async_computation.6 | async-start | bytes 3538944 | tf_op jit(solution)/shard_map/reduce_scatter | solution.py:1267
  317.4 197.7 %reduce-scatter.8.cloned.1.call-start = ((), (), s32[]{:S(2)}) async-start(), calls=%async_computation.7 | async-start | bytes 3538944 | tf_op jit(solution)/shard_map/reduce_scatter | solution.py:1202
  318.6 8.3 %collective-permute-start.16 = (bf16[2,128,192]{2,1,0:T(8,128)(2,1)S(1)}, bf16[2,128,192]{2,1,0:T(8,128)(2,1)S(1)}, u32[]{:S(2)}, u32[]{:S(2)}) collective-permute-start(bf16[2,128,192]{2,1,0:T(8,128)(2,1)S(1)} %get-tuple-element.272), channel_id=1, source_target_pairs={{0,2},{1,3},{2,4},{3,5},{4,6},{5,7},{6,0},{7,1},{8,10},{9,11},{10,... | collective-permute-start | bytes 294920 | tf_op jit(solution)/shard_map/ppermute | solution.py:1036
  318.7 18.1 %collective-permute-start.15 = (bf16[2,128,192]{2,1,0:T(8,128)(2,1)S(1)}, bf16[2,128,192]{2,1,0:T(8,128)(2,1)S(1)}, u32[]{:S(2)}, u32[]{:S(2)}) collective-permute-start(bf16[2,128,192]{2,1,0:T(8,128)(2,1)S(1)} %get-tuple-element.273), channel_id=1, source_target_pairs={{0,4},{1,5},{2,6},{3,7},{4,0},{5,1},{6,2},{7,3},{8,12},{9,13},{10,... | collective-permute-start | bytes 294920 | tf_op jit(solution)/shard_map/ppermute | solution.py:1036
  320.2 16.6 %collective-permute-start.14 = (bf16[2,128,192]{2,1,0:T(8,128)(2,1)S(1)}, bf16[2,128,192]{2,1,0:T(8,128)(2,1)S(1)}, u32[]{:S(2)}, u32[]{:S(2)}) collective-permute-start(bf16[2,128,192]{2,1,0:T(8,128)(2,1)S(1)} %get-tuple-element.274), channel_id=1, source_target_pairs={{0,6},{1,7},{2,0},{3,1},{4,2},{5,3},{6,4},{7,5},{8,14},{9,15},{10,... | collective-permute-start | bytes 294920 | tf_op jit(solution)/shard_map/ppermute | solution.py:1036
  338.4 1.7 collective-permute-start.17
  345.0 28.4 %collective-permute-start.18 = (bf16[1152,512]{1,0:T(8,128)(2,1)}, bf16[1152,512]{1,0:T(8,128)(2,1)}, u32[]{:S(2)}, u32[]{:S(2)}) collective-permute-start(bf16[1152,512]{1,0:T(8,128)(2,1)} %add_convert_fusion.3), channel_id=1, source_target_pairs={{0,16},{8,24},{16,0},{24,8},{1,17},{9,25},{17,1},{25,9},{2,18},{10... | collective-permute-start | bytes 3538952 | tf_op jit(solution)/shard_map/ppermute | solution.py:864
  349.9 28.1 %collective-permute-start.19 = (bf16[1152,512]{1,0:T(8,128)(2,1)}, bf16[1152,512]{1,0:T(8,128)(2,1)}, u32[]{:S(2)}, u32[]{:S(2)}) collective-permute-start(bf16[1152,512]{1,0:T(8,128)(2,1)} %add_convert_fusion.2), channel_id=1, source_target_pairs={{0,8},{8,0},{16,24},{24,16},{1,9},{9,1},{17,25},{25,17},{2,10},{10... | collective-permute-start | bytes 3538952 | tf_op jit(solution)/shard_map/ppermute | solution.py:864
  380.9 27.1 %collective-permute-start.21 = (bf16[1152,512]{1,0:T(8,128)(2,1)S(1)}, bf16[1152,512]{1,0:T(8,128)(2,1)}, u32[]{:S(2)}, u32[]{:S(2)}) collective-permute-start(bf16[1152,512]{1,0:T(8,128)(2,1)S(1)} %add_convert_fusion.1), channel_id=1, source_target_pairs={{0,16},{8,24},{16,0},{24,8},{1,17},{9,25},{17,1},{25,9},{2,18},{10... | collective-permute-start | bytes 3538952 | tf_op jit(solution)/shard_map/ppermute | solution.py:864
  383.9 29.1 %collective-permute-start.22 = (bf16[1152,512]{1,0:T(8,128)(2,1)S(1)}, bf16[1152,512]{1,0:T(8,128)(2,1)}, u32[]{:S(2)}, u32[]{:S(2)}) collective-permute-start(bf16[1152,512]{1,0:T(8,128)(2,1)S(1)} %add_convert_fusion), channel_id=1, source_target_pairs={{0,8},{8,0},{16,24},{24,16},{1,9},{9,1},{17,25},{25,17},{2,10},{10... | collective-permute-start | bytes 3538952 | tf_op jit(solution)/shard_map/ppermute | solution.py:864
  400.9 19.2 %collective-permute-start.20 = (bf16[2,1,48,2304]{3,2,1,0:T(8,128)(2,1)S(1)}, bf16[2,1,48,2304]{3,2,1,0:T(8,128)(2,1)S(1)}, u32[]{:S(2)}, u32[]{:S(2)}) collective-permute-start(bf16[2,1,48,2304]{3,2,1,0:T(8,128)(2,1)S(1)} %dynamic-slice_convert_fusion.1), channel_id=1, source_target_pairs={{0,8},{8,0},{16,24},{24,16},{1,9},{9,1},{17,25},{25,17},{2,10},{10... | collective-permute-start | bytes 1327112 | tf_op jit(solution)/shard_map/ppermute | solution.py:864
  414.4 10.2 %collective-permute-start.24 = (bf16[1,2,48,2304]{3,2,1,0:T(8,128)(2,1)S(1)}, bf16[1,2,48,2304]{3,2,1,0:T(8,128)(2,1)S(1)}, u32[]{:S(2)}, u32[]{:S(2)}) collective-permute-start(bf16[1,2,48,2304]{3,2,1,0:T(8,128)(2,1)S(1)} %dynamic-slice_convert_fusion), channel_id=1, source_target_pairs={{0,16},{8,24},{16,0},{24,8},{1,17},{9,25},{17,1},{25,9},{2,18},{10... | collective-permute-start | bytes 1327112 | tf_op jit(solution)/shard_map/ppermute | solution.py:864
  420.2 7.3 %collective-permute-start.23 = (bf16[1,1,48,2304]{3,2,1,0:T(8,128)(2,1)S(1)}, bf16[1,1,48,2304]{3,2,1,0:T(8,128)(2,1)S(1)}, u32[]{:S(2)}, u32[]{:S(2)}) collective-permute-start(bf16[1,1,48,2304]{3,2,1,0:T(8,128)(2,1)S(1)} %dynamic-slice_convert_fusion.3), channel_id=1, source_target_pairs={{0,16},{8,24},{16,0},{24,8},{1,17},{9,25},{17,1},{25,9},{2,18},{10... | collective-permute-start | bytes 663560 | tf_op jit(solution)/shard_map/ppermute | solution.py:864
  424.7 6.0 %collective-permute-start.25 = (bf16[1,1,48,2304]{3,2,1,0:T(8,128)(2,1)S(1)}, bf16[1,1,48,2304]{3,2,1,0:T(8,128)(2,1)S(1)}, u32[]{:S(2)}, u32[]{:S(2)}) collective-permute-start(bf16[1,1,48,2304]{3,2,1,0:T(8,128)(2,1)S(1)} %dynamic-slice_convert_fusion.2), channel_id=1, source_target_pairs={{0,8},{8,0},{16,24},{24,16},{1,9},{9,1},{17,25},{25,17},{2,10},{10... | collective-permute-start | bytes 663560 | tf_op jit(solution)/shard_map/ppermute | solution.py:864
  431.7 15.7 %collective-permute-start.28 = (bf16[2,48,384]{2,1,0:T(8,128)(2,1)S(1)}, bf16[2,48,384]{2,1,0:T(8,128)(2,1)S(1)}, u32[]{:S(2)}, u32[]{:S(2)}) collective-permute-start(bf16[2,48,384]{2,1,0:T(8,128)(2,1)S(1)} %get-tuple-element.284), channel_id=1, source_target_pairs={{0,2},{1,3},{2,4},{3,5},{4,6},{5,7},{6,0},{7,1},{8,10},{9,11},{10,... | collective-permute-start | bytes 221192 | tf_op jit(solution)/shard_map/ppermute | solution.py:1036
  441.6 6.8 %collective-permute-start.27 = (bf16[2,48,384]{2,1,0:T(8,128)(2,1)S(1)}, bf16[2,48,384]{2,1,0:T(8,128)(2,1)S(1)}, u32[]{:S(2)}, u32[]{:S(2)}) collective-permute-start(bf16[2,48,384]{2,1,0:T(8,128)(2,1)S(1)} %get-tuple-element.285), channel_id=1, source_target_pairs={{0,4},{1,5},{2,6},{3,7},{4,0},{5,1},{6,2},{7,3},{8,12},{9,13},{10,... | collective-permute-start | bytes 221192 | tf_op jit(solution)/shard_map/ppermute | solution.py:1036
  441.6 6.8 %collective-permute-start.26 = (bf16[2,48,384]{2,1,0:T(8,128)(2,1)S(1)}, bf16[2,48,384]{2,1,0:T(8,128)(2,1)S(1)}, u32[]{:S(2)}, u32[]{:S(2)}) collective-permute-start(bf16[2,48,384]{2,1,0:T(8,128)(2,1)S(1)} %get-tuple-element.286), channel_id=1, source_target_pairs={{0,6},{1,7},{2,0},{3,1},{4,2},{5,3},{6,4},{7,5},{8,14},{9,15},{10,... | collective-permute-start | bytes 221192 | tf_op jit(solution)/shard_map/ppermute | solution.py:1036
  448.5 5.4 %collective-permute-start.29 = (bf16[4,48,384]{2,1,0:T(8,128)(2,1)S(1)}, bf16[4,48,384]{2,1,0:T(8,128)(2,1)S(1)}, u32[]{:S(2)}, u32[]{:S(2)}) collective-permute-start(bf16[4,48,384]{2,1,0:T(8,128)(2,1)S(1)} %select_bitcast_fusion.3), channel_id=1, source_target_pairs={{0,1},{1,0},{2,3},{3,2},{4,5},{5,4},{6,7},{7,6},{8,9},{9,8},{10,11... | collective-permute-start | bytes 442376 | tf_op jit(solution)/shard_map/ppermute | solution.py:1039
  450.1 44.0 %collective-permute-start.32 = (bf16[768,512]{1,0:T(8,128)(2,1)S(1)}, bf16[768,512]{1,0:T(8,128)(2,1)S(1)}, u32[]{:S(2)}, u32[]{:S(2)}) collective-permute-start(bf16[768,512]{1,0:T(8,128)(2,1)S(1)} %get-tuple-element.146), channel_id=1, source_target_pairs={{0,8},{8,0},{16,24},{24,16},{1,9},{9,1},{17,25},{25,17},{2,10},{10... | collective-permute-start | bytes 2359304 | tf_op jit(solution)/shard_map/ppermute | solution.py:864
  451.6 46.2 %collective-permute-start.35 = (bf16[768,512]{1,0:T(8,128)(2,1)}, bf16[768,512]{1,0:T(8,128)(2,1)}, u32[]{:S(2)}, u32[]{:S(2)}) collective-permute-start(bf16[768,512]{1,0:T(8,128)(2,1)} %get-tuple-element.152), channel_id=1, source_target_pairs={{0,16},{8,24},{16,0},{24,8},{1,17},{9,25},{17,1},{25,9},{2,18},{10... | collective-permute-start | bytes 2359304 | tf_op jit(solution)/shard_map/ppermute | solution.py:864
  454.3 21.9 %collective-permute-start.30 = (bf16[1,1,48,2304]{3,2,1,0:T(8,128)(2,1)S(1)}, bf16[1,1,48,2304]{3,2,1,0:T(8,128)(2,1)S(1)}, u32[]{:S(2)}, u32[]{:S(2)}) collective-permute-start(bf16[1,1,48,2304]{3,2,1,0:T(8,128)(2,1)S(1)} %maximum_bitcast_fusion), channel_id=1, source_target_pairs={{0,16},{8,24},{16,0},{24,8},{1,17},{9,25},{17,1},{25,9},{2,18},{10... | collective-permute-start | bytes 663560 | tf_op jit(solution)/shard_map/ppermute | solution.py:864
  455.0 43.3 %collective-permute-start.33 = (bf16[768,512]{1,0:T(8,128)(2,1)}, bf16[768,512]{1,0:T(8,128)(2,1)}, u32[]{:S(2)}, u32[]{:S(2)}) collective-permute-start(bf16[768,512]{1,0:T(8,128)(2,1)} %get-tuple-element.147), channel_id=1, source_target_pairs={{0,8},{8,0},{16,24},{24,16},{1,9},{9,1},{17,25},{25,17},{2,10},{10... | collective-permute-start | bytes 2359304 | tf_op jit(solution)/shard_map/ppermute | solution.py:864
  455.6 36.0 %collective-permute-start.34 = (bf16[1,1,48,2304]{3,2,1,0:T(8,128)(2,1)S(1)}, bf16[1,1,48,2304]{3,2,1,0:T(8,128)(2,1)S(1)}, u32[]{:S(2)}, u32[]{:S(2)}) collective-permute-start(bf16[1,1,48,2304]{3,2,1,0:T(8,128)(2,1)S(1)} %maximum_bitcast_fusion.1), channel_id=1, source_target_pairs={{0,8},{8,0},{16,24},{24,16},{1,9},{9,1},{17,25},{25,17},{2,10},{10... | collective-permute-start | bytes 663560 | tf_op jit(solution)/shard_map/ppermute | solution.py:864
  476.2 22.7 %collective-permute-start.36 = (bf16[768,512]{1,0:T(8,128)(2,1)}, bf16[768,512]{1,0:T(8,128)(2,1)}, u32[]{:S(2)}, u32[]{:S(2)}) collective-permute-start(bf16[768,512]{1,0:T(8,128)(2,1)} %get-tuple-element.153), channel_id=1, source_target_pairs={{0,16},{8,24},{16,0},{24,8},{1,17},{9,25},{17,1},{25,9},{2,18},{10... | collective-permute-start | bytes 2359304 | tf_op jit(solution)/shard_map/ppermute | solution.py:864
  491.6 17.5 %collective-permute-start.31 = (bf16[2,1,48,2304]{3,2,1,0:T(8,128)(2,1)}, bf16[2,1,48,2304]{3,2,1,0:T(8,128)(2,1)}, u32[]{:S(2)}, u32[]{:S(2)}) collective-permute-start(bf16[2,1,48,2304]{3,2,1,0:T(8,128)(2,1)} %pad_maximum_fusion.17), channel_id=1, source_target_pairs={{0,8},{8,0},{16,24},{24,16},{1,9},{9,1},{17,25},{25,17},{2,10},{10... | collective-permute-start | bytes 1327112 | tf_op jit(solution)/shard_map/ppermute | solution.py:864
  494.1 15.1 %collective-permute-start.37 = (bf16[1,2,48,2304]{3,2,1,0:T(8,128)(2,1)}, bf16[1,2,48,2304]{3,2,1,0:T(8,128)(2,1)}, u32[]{:S(2)}, u32[]{:S(2)}) collective-permute-start(bf16[1,2,48,2304]{3,2,1,0:T(8,128)(2,1)} %pad_maximum_fusion.18), channel_id=1, source_target_pairs={{0,16},{8,24},{16,0},{24,8},{1,17},{9,25},{17,1},{25,9},{2,18},{10... | collective-permute-start | bytes 1327112 | tf_op jit(solution)/shard_map/ppermute | solution.py:864
  497.7 22.9 %collective-permute-start.38 = (bf16[768,512]{1,0:T(8,128)(2,1)}, bf16[768,512]{1,0:T(8,128)(2,1)}, u32[]{:S(2)}, u32[]{:S(2)}) collective-permute-start(bf16[768,512]{1,0:T(8,128)(2,1)} %get-tuple-element.164), channel_id=1, source_target_pairs={{0,8},{8,0},{16,24},{24,16},{1,9},{9,1},{17,25},{25,17},{2,10},{10... | collective-permute-start | bytes 2359304 | tf_op jit(solution)/shard_map/ppermute | solution.py:864
  498.3 24.6 %collective-permute-start.39 = (bf16[768,512]{1,0:T(8,128)(2,1)}, bf16[768,512]{1,0:T(8,128)(2,1)}, u32[]{:S(2)}, u32[]{:S(2)}) collective-permute-start(bf16[768,512]{1,0:T(8,128)(2,1)} %get-tuple-element.165), channel_id=1, source_target_pairs={{0,16},{8,24},{16,0},{24,8},{1,17},{9,25},{17,1},{25,9},{2,18},{10... | collective-permute-start | bytes 2359304 | tf_op jit(solution)/shard_map/ppermute | solution.py:864
  (81 other events, 472.5 us)
Sparse Core Ops, SparseCore 0:
  11.4 57.0 all-gather.5
  81.8 49.8 all-gather.7
  133.3 45.9 all-gather.11
  230.6 41.2 reduce-scatter.3
  317.0 42.4 all-gather.9
  361.6 38.4 reduce-scatter.5
  402.4 45.5 reduce-scatter.7

commit v5 on v4

--- a/solution.py
+++ b/solution.py
@@ -73,7 +73,19 @@
     return jnp.min(jnp.where((segments == here) & (number <= step), number, step))
 
 
-def whole_block(*shape, grid=1, prefetch=0):
+def token_rows(block, own, features):
+    count = block // own
+    return (
+        pl.BlockSpec((count, own, features), lambda i, *_: (i, 0, 0)),
+        pl.BlockSpec((count, own, 128), lambda i, *_: (i, 0, features // 128)),
+    )
+
+
+def flat(ref):
+    return ref[...].reshape(-1, ref.shape[-1])
+
+
+def whole_block(*shape):
     return pl.BlockSpec(shape, lambda *i: (0,) * len(shape), pipeline_mode=pl.Buffered(1))
 
 
@@ -96,11 +108,11 @@
     score_ref,
 ):
     step = pl.program_id(0)
-    block = hidden_ref.shape[0]
+    block = query_ref.shape[0]
     query_width = query_ref.shape[1]
     width = query_width + 2 * HEAD_SIZE
     here = pl.ds(pl.multiple_of(step * block, block), block)
-    columns = column_ref[...].astype(jnp.float32)
+    columns = flat(column_ref).astype(jnp.float32)
     row_segments = columns[:, :1]
     segment_ref[step] = jnp.transpose(columns)[:1, :]
     angles = (columns[:, 1:2] * 64.0 + columns[:, 2:3]) * rate_ref[...]
@@ -108,7 +120,7 @@
     sine = jnp.sin(angles)
     cosine_ref[...] = cosine
     sine_ref[...] = sine
-    hidden = hidden_ref[...].astype(jnp.float32)
+    hidden = flat(hidden_ref).astype(jnp.float32)
     scale = lax.rsqrt(jnp.mean(hidden * hidden, -1, keepdims=True) + EPS)
     normed = (hidden * scale * gain_ref[...]).astype(jnp.bfloat16)
     normed_ref[...] = normed
@@ -166,8 +178,8 @@
     log_ref[...] = (top + jnp.log(total)).reshape(HEAD_GROUP, block, 1)
 
 
-def attend(gathered, gain, weights, block):
-    tokens, features = gathered.shape[0], gain.shape[0]
+def attend(gathered, gain, weights, own, block):
+    tokens, features = gathered.shape[0] * own, gain.shape[0]
     query_width = HEAD_GROUP * HEAD_SIZE
     steps = tokens // block
     half = jnp.arange(HEAD_SIZE // 2, dtype=jnp.float32)
@@ -191,8 +203,7 @@
         ),
         grid=(steps,),
         in_specs=[
-            rows(features),
-            pl.BlockSpec((block, 128), lambda i: (i, features // 128)),
+            *token_rows(block, own, features),
             whole_block(1, features),
             whole_block(*weights[0].shape),
             whole_block(*weights[1].shape),
@@ -246,7 +257,7 @@
     query = stack_heads(query_ref[...])
     grad = stack_heads(grad_ref[...])
     log_total = log_ref[...].reshape(rows, 1)
-    row_segments = column_ref[...].astype(jnp.float32)[:, :1]
+    row_segments = flat(column_ref).astype(jnp.float32)[:, :1]
     first = first_block(row_segments, segment_ref, step)
 
     def first_pass(index, delta):
@@ -294,10 +305,10 @@
         )
 
 
-def attend_back(query, grad, log_total, cosine, sine, gathered, segments, key, value):
+def attend_back(query, grad, log_total, cosine, sine, gathered, segments, key, value, own):
     tokens, query_width = query.shape
     steps, _, block = segments.shape
-    features = gathered.shape[1] - 128
+    features = gathered.shape[2] - 128
     rows = lambda width: pl.BlockSpec((block, width), lambda i: (i, 0))
     resident = lambda *shape: pl.BlockSpec(shape, lambda i: (0,) * len(shape))
     return pl.pallas_call(
@@ -313,7 +324,7 @@
             pl.BlockSpec((HEAD_GROUP, block, 1), lambda i: (0, i, 0)),
             rows(HEAD_SIZE),
             rows(HEAD_SIZE),
-            pl.BlockSpec((block, 128), lambda i: (i, features // 128)),
+            token_rows(block, own, features)[1],
             whole_block(steps, 1, block),
             whole_block(tokens, HEAD_SIZE),
             whole_block(tokens, HEAD_SIZE),
@@ -348,13 +359,13 @@
     mixed = jnp.concatenate([mixed_ref[g] for g in range(groups)], 1)
     half = low_ref.shape[0]
     middle = dot(mixed[:, :half], low_ref[...]) + dot(mixed[:, half:], high_ref[...])
-    middle = hidden_ref[...].astype(jnp.float32) + middle
+    middle = flat(hidden_ref).astype(jnp.float32) + middle
     middle_ref[...] = middle
     scale = lax.rsqrt(jnp.mean(middle * middle, -1, keepdims=True) + EPS)
     normed = (middle * scale * gain_ref[...]).astype(jnp.bfloat16)
     normed_ref[...] = normed
     logits = dot(normed, router_ref[...])
-    columns = column_ref[...].astype(jnp.float32)
+    columns = flat(column_ref).astype(jnp.float32)
     number = lax.broadcasted_iota(jnp.int32, logits.shape, 1).astype(jnp.float32)
     named = columns[:, 3:4] == number
     for slot in range(1, TOPK):
@@ -365,7 +376,7 @@
     gates_ref[...] = shifted / jnp.sum(shifted, -1, keepdims=True)
 
 
-def middle_rows(mixed, weights, gathered, gain, router, block):
+def middle_rows(mixed, weights, gathered, gain, router, own, block):
     groups, tokens, width = mixed.shape
     features = gain.shape[0]
     experts = router.shape[1]
@@ -382,8 +393,7 @@
             pl.BlockSpec((groups, block, width), lambda i: (0, i, 0)),
             whole_block(*weights[0].shape),
             whole_block(*weights[1].shape),
-            rows(features),
-            pl.BlockSpec((block, 128), lambda i: (i, features // 128)),
+            *token_rows(block, own, features),
             whole_block(1, features),
             whole_block(features, experts),
         ],
@@ -422,26 +432,21 @@
     experts_own = gate_weight_ref.shape[0]
     experts_all = gates_ref.shape[1]
     first = place_ref[1] * experts_own
-    normed = normed_ref[...]
-    live = column_ref[...].astype(jnp.float32)[:, :1] > 0
-    grad_live = jnp.where(live, cotangent_ref[...], jnp.zeros((), jnp.bfloat16))
-    grad_live_ref[...] = grad_live
+    live = flat(column_ref).astype(jnp.float32)[:, :1] > 0
+    grad_live_ref[...] = jnp.where(live, cotangent_ref[...], jnp.zeros((), jnp.bfloat16))
     gates = gates_ref[...]
     number = lax.broadcasted_iota(jnp.int32, gates.shape, 1)
-    grad_gates = jnp.zeros(gates.shape, jnp.float32)
-    for e in range(experts_own):
+
+    def one_expert(e, grad_gates):
         one = slot_of(e, place_ref[2], experts_own)
         two = slot_of(e, place_ref[3], experts_own)
         gate = jnp.sum(jnp.where(number == first + e, gates, 0.0), -1, keepdims=True)
-        gate_pre = dot(normed, gate_weight_ref[e])
-        up_pre = dot(normed, up_weight_ref[e])
-        grad_plain = dot(grad_live, down_weight_ref[e], COLUMNS)
+        gate_pre = dot(normed_ref[...], gate_weight_ref[e])
+        up_pre = dot(normed_ref[...], up_weight_ref[e])
+        grad_plain = dot(grad_live_ref[...], down_weight_ref[e], COLUMNS)
         sigma = jax.nn.sigmoid(gate_pre)
         silu = gate_pre * sigma
         acted = silu * up_pre
-        grad_gates = grad_gates + jnp.where(
-            number == first + e, jnp.sum(acted * grad_plain, -1, keepdims=True), 0.0
-        )
         grad_acted = gate * grad_plain
         scaled = (gate * acted).astype(jnp.bfloat16)
         scaled_one_ref[one] = scaled
@@ -450,13 +455,20 @@
             grad_acted * up_pre * (sigma * (1.0 + gate_pre * (1.0 - sigma)))
         ).astype(jnp.bfloat16)
         grad_up_ref[two] = (grad_acted * silu).astype(jnp.bfloat16)
+        return grad_gates + jnp.where(
+            number == first + e, jnp.sum(acted * grad_plain, -1, keepdims=True), 0.0
+        )
+
+    grad_gates = lax.fori_loop(
+        0, experts_own, one_expert, jnp.zeros(gates.shape, jnp.float32)
+    )
     rough = grad_gates.astype(jnp.bfloat16)
     fine = (grad_gates - rough.astype(jnp.float32)).astype(jnp.bfloat16)
     rest = jnp.zeros((gates.shape[0], extra_ref.shape[1] - 2 * experts_all), jnp.bfloat16)
     extra_ref[...] = jnp.concatenate([rough, fine, rest], 1)
 
 
-def expert_rows(place, normed, cotangent, gathered, gates, w_gate, w_up, w_down, block):
+def expert_rows(place, normed, cotangent, gathered, gates, w_gate, w_up, w_down, own, block):
     tokens, features = normed.shape
     experts_own, _, hidden = w_gate.shape
     experts_all = gates.shape[1]
@@ -479,7 +491,7 @@
             in_specs=[
                 rows(features),
                 rows(features),
-                pl.BlockSpec((block, 128), lambda i, p: (i, features // 128)),
+                token_rows(block, own, features)[1],
                 rows(experts_all),
                 whole_block(*w_gate.shape),
                 whole_block(*w_up.shape),
@@ -496,51 +508,79 @@
     )(place, normed, cotangent, gathered, gates, w_gate, w_up, w_down)
 
 
-def product_kernel(left_ref, right_ref, scaled_ref, live_ref, out_ref):
+def product_kernel(
+    left_ref,
+    gate_ref,
+    up_ref,
+    scaled_one_ref,
+    scaled_two_ref,
+    live_one_ref,
+    live_two_ref,
+    out_one_ref,
+    out_two_ref,
+):
     step = pl.program_id(0)
-    tile, hidden = left_ref.shape[1], right_ref.shape[1]
-    narrow = live_ref.shape[1]
+    tile, hidden = left_ref.shape[1], gate_ref.shape[1]
+    narrow = live_one_ref.shape[1]
     tops = pl.num_programs(0) - 3
     top = tops * tile
 
     @pl.when(step < tops)
     def _():
-        out_ref[pl.ds(pl.multiple_of(step * tile, tile), tile), :] = dot(
-            left_ref[...], right_ref[...], ROWS
-        ).astype(out_ref.dtype)
-
-    for part in range(3):
-
-        @pl.when(step == tops + part)
-        def _():
+        here = pl.ds(pl.multiple_of(step * tile, tile), tile)
+        both = dot(left_ref[...], jnp.concatenate([gate_ref[...], up_ref[...]], 1), ROWS)
+        out_one_ref[here, :] = both[:, :hidden].astype(out_one_ref.dtype)
+        out_two_ref[here, :] = both[:, hidden:].astype(out_two_ref.dtype)
+
+    @pl.when(step >= tops)
+    def _():
+        part = step - tops
+        for scaled_ref, live_ref, out_ref in (
+            (scaled_one_ref, live_one_ref, out_one_ref),
+            (scaled_two_ref, live_two_ref, out_two_ref),
+        ):
             product = dot(scaled_ref[...], live_ref[...], ROWS).astype(out_ref.dtype)
-            if part < 2:
-                out_ref[top : top + hidden, part * narrow : (part + 1) * narrow] = product
-            else:
+
+            @pl.when(part < 2)
+            def _():
+                there = pl.ds(pl.multiple_of(part * narrow, narrow), narrow)
+                out_ref[top : top + hidden, there] = product
+
+            @pl.when(part == 2)
+            def _():
                 out_ref[top + hidden :, :narrow] = product[:narrow]
                 out_ref[top + hidden :, narrow:] = product[narrow:]
 
 
-def expert_product(left, right, scaled, live, e, side, dtype):
+def expert_products(left, gate, up, scaled_one, scaled_two, live, e, dtype):
     tokens, features = left.shape
-    hidden = right.shape[2]
+    hidden = gate.shape[2]
     narrow = hidden // 2
     tile = 512
     tops = features // tile
+    rows = features + features // 2
+    stack = pl.BlockSpec((None, tokens, hidden), lambda i: (e, 0, 0), pipeline_mode=pl.Buffered(1))
+    lives = [
+        pl.BlockSpec((tokens, narrow), lambda i, side=side: (0, 3 * side + jnp.maximum(i - tops, 0)))
+        for side in range(2)
+    ]
+    out = pl.BlockSpec((rows, hidden), lambda i: (0, 0), pipeline_mode=pl.Buffered(1))
     return pl.pallas_call(
         product_kernel,
-        out_shape=jax.ShapeDtypeStruct((features + features // 2, hidden), dtype),
+        out_shape=(jax.ShapeDtypeStruct((rows, hidden), dtype),) * 2,
         grid=(tops + 3,),
         in_specs=[
             pl.BlockSpec((tokens, tile), lambda i: (0, jnp.minimum(i, tops - 1))),
-            pl.BlockSpec((None, tokens, hidden), lambda i: (e, 0, 0), pipeline_mode=pl.Buffered(1)),
-            pl.BlockSpec((None, tokens, hidden), lambda i: (e, 0, 0), pipeline_mode=pl.Buffered(1)),
-            pl.BlockSpec((tokens, narrow), lambda i: (0, 3 * side + jnp.maximum(i - tops, 0))),
+            stack,
+            stack,
+            stack,
+            stack,
+            *lives,
         ],
-        out_specs=pl.BlockSpec((features + features // 2, hidden), lambda i: (0, 0)),
-        compiler_params=pltpu.CompilerParams(vmem_limit_bytes=40 << 20),
+        out_specs=[out, out],
+        compiler_params=pltpu.CompilerParams(vmem_limit_bytes=58 << 20),
         cost_estimate=pl.CostEstimate(flops=0, bytes_accessed=tokens, transcendentals=0),
-    )(left, right, scaled, live)
+    )(left, gate, up, scaled_one, scaled_two, live, live)
 
 
 def rows_kernel(
@@ -559,8 +599,11 @@
     features = out_ref.shape[1]
     one = [slot_of(e, place_ref[2], experts_own) for e in range(experts_own)]
     two = [slot_of(e, place_ref[3], experts_own) for e in range(experts_own)]
-    for start in range(0, features, 512):
-        part = slice(start, start + 512)
+    size = 512
+
+    @pl.loop(0, features // size)
+    def _(index):
+        part = pl.ds(pl.multiple_of(index * size, size), size)
         grad = 0.0
         out = 0.0
         for e in range(experts_own):
@@ -569,6 +612,7 @@
             out = out + dot(scaled_ref[one[e]], down_weight_ref[e, :, part])
         grad_ref[:, part] = grad.astype(jnp.bfloat16)
         out_ref[:, part] = out.astype(jnp.bfloat16)
+
     grad_ref[:, features:] = extra_ref[...]
 
 
@@ -655,7 +699,7 @@
             shaped((own, experts), jnp.bfloat16),
             shaped((1, features), jnp.float32),
         ),
-        compiler_params=pltpu.CompilerParams(vmem_limit_bytes=32 << 20),
+        compiler_params=pltpu.CompilerParams(vmem_limit_bytes=58 << 20),
         cost_estimate=pl.CostEstimate(flops=0, bytes_accessed=own, transcendentals=0),
     )(sums, gates, router, gain[None, :], middle, live, *weights)
 
@@ -669,6 +713,7 @@
     gain_two_ref,
     normed_own_ref,
     logits_ref,
+    rows_ref,
     grad_ref,
     head_ref,
     product_ref,
@@ -682,8 +727,9 @@
     grad = dot(query, weight_ref[:, :width], COLUMNS) + dot(
         pair, weight_ref[:, width:both], COLUMNS
     )
-    grad_ref[...] = grad.astype(jnp.bfloat16)
-    hidden = hidden_ref[...].astype(jnp.float32)
+    grad_ref[:, : grad.shape[1]] = grad.astype(jnp.bfloat16)
+    grad_ref[:, grad.shape[1] :] = rows_ref[...]
+    hidden = flat(hidden_ref).astype(jnp.float32)
     scale = lax.rsqrt(jnp.mean(hidden * hidden, -1, keepdims=True) + EPS)
     normed = normed_ref[...]
 
@@ -716,7 +762,18 @@
 
 
 def close_rows(
-    query, pair, weight, gathered, normed, gain_two_grad, normed_own, logits, rows_own, side, block
+    query,
+    pair,
+    weight,
+    gathered,
+    normed,
+    gain_two_grad,
+    normed_own,
+    logits,
+    out_rows,
+    rows_own,
+    side,
+    block,
 ):
     tokens, features = normed.shape
     both = query.shape[1] + pair.shape[1]
@@ -726,26 +783,27 @@
     head = (rows_own, features // rows_own * side)
     return pl.pallas_call(
         close_kernel,
-        out_shape=(shaped((tokens, features), jnp.bfloat16), shaped(head, jnp.float32)),
+        out_shape=(shaped((tokens, 2 * features), jnp.bfloat16), shaped(head, jnp.float32)),
         grid=(tokens // block,),
         in_specs=[
             rows(query.shape[1]),
             rows(pair.shape[1]),
             whole_block(*weight.shape),
-            rows(features),
+            token_rows(block, normed_own.shape[0], features)[0],
             rows(features),
             whole_block(1, features),
             whole_block(*normed_own.shape),
             whole_block(*logits.shape),
+            rows(features),
         ],
-        out_specs=[rows(features), resident(*head)],
+        out_specs=[rows(2 * features), resident(*head)],
         scratch_shapes=[
             pltpu.VMEM((features, both), jnp.float32),
             pltpu.VMEM((1, features), jnp.float32),
         ],
         compiler_params=pltpu.CompilerParams(vmem_limit_bytes=48 << 20),
         cost_estimate=pl.CostEstimate(flops=0, bytes_accessed=tokens, transcendentals=0),
-    )(query, pair, weight, gathered, normed, gain_two_grad, normed_own, logits)
+    )(query, pair, weight, gathered, normed, gain_two_grad, normed_own, logits, out_rows)
 
 
 def head_kernel(copies, side, low_ref, high_ref, query_ref, key_ref, value_ref, out_ref, small_ref):
@@ -1028,9 +1086,17 @@
         1,
     ).astype(jnp.bfloat16)
     columns = jnp.pad(columns, ((0, 0), (0, 128 - columns.shape[1])))
-    gathered = lax.all_gather(
-        jnp.concatenate([inputs[0], columns], 1), "ctx", axis=0, tiled=True
-    )
+    shared = lambda array: lax.dynamic_slice_in_dim(array, share_start, share, 0)
+
+    rows = jnp.concatenate(
+        [
+            jnp.concatenate([inputs[0], columns], 1),
+            jnp.pad(shared(w_out), ((0, 0), (0, 128))),
+        ],
+        0,
+    )
+    gathered = lax.all_gather(rows, "ctx", axis=0)
+    cotangent = lax.all_gather(after(grad_out[0], rows), "ctx", axis=0, tiled=True)
 
     def from_chip(value, k):
         return lax.ppermute(value, "ctx", [(i, (i - 2 * k) % size) for i in range(size)])
@@ -1043,7 +1109,6 @@
             [jnp.where(odd, others, mine), jnp.where(odd, mine, others)], axis
         )
 
-    shared = lambda array: lax.dynamic_slice_in_dim(array, share_start, share, 0)
     side_width = -(-(width + 2 + router.shape[1]) // 128) * 128
     head_columns = jnp.concatenate(
         [
@@ -1059,30 +1124,8 @@
     used = head_columns.shape[-1]
     head_columns = jnp.pad(head_columns, ((0, 0), (0, 0), (0, side_width - used)))
     head_columns = jnp.repeat(jnp.transpose(head_columns, (1, 0, 2)), copies, 0)
-    head_columns = head_columns.reshape(chips, 2, share, side_width)
-    out_share = shared(w_out)
-    parcels = []
-    for k in range(chips):
-        to = head_columns[(chip - k) % chips]
-        parcel = jnp.concatenate([out_share, to[0], to[1]], 1)
-        parcels.append(from_chip(parcel, k) if k else parcel)
-    parcels = jnp.stack(parcels)
-    out_part = parcels[:, :, :MODEL_WIDTH]
-    heads = [
-        parcels[:, :, MODEL_WIDTH : MODEL_WIDTH + side_width],
-        parcels[:, :, MODEL_WIDTH + side_width :],
-    ]
-    for_core = jnp.where(odd, heads[0], heads[1])
-    mine_part = jnp.concatenate([out_part, jnp.where(odd, heads[1], heads[0])], 2)
-    core_part = from_core(jnp.concatenate([out_part, for_core], 2))
-    fetched = cores(mine_part[:, None], core_part[:, None], 1)
-    fetched = lax.dynamic_slice_in_dim(
-        jnp.concatenate([fetched, fetched], 0), (chips - chip) % chips, chips, 0
-    ).reshape(size, share, MODEL_WIDTH + side_width)
-    head_exchange = Exchange(fetched[:, :, MODEL_WIDTH:], bits)
-    out_exchange = Exchange(fetched[:, :, :MODEL_WIDTH], bits)
-    head_halves = head_exchange.finish()
-    ready = out_exchange.step(*head_halves)
+    head_columns = lax.all_to_all(head_columns, "ctx", split_axis=0, concat_axis=0, tiled=True)
+    head_halves = Exchange(head_columns, bits).finish()
     head_all = jnp.concatenate(head_halves, 0)
     gain_one = head_all[:, width].astype(jnp.float32)
     gain_two = head_all[:, width + 1].astype(jnp.float32)
@@ -1098,28 +1141,29 @@
         cosine_table,
         sine_table,
         segment_rows,
-    ) = attend(after(gathered, *ready), gain_one, head_halves, block)
+    ) = attend(gathered, gain_one, head_halves, own, block)
+    out_exchange = Exchange(gathered[:, own:, :MODEL_WIDTH], bits)
 
     part = tokens // copies
-    cotangent = lax.all_gather(after(grad_out[0], *ready), "ctx", axis=0, tiled=True)
     mixed_all = lax.all_gather(
-        after(lax.dynamic_slice_in_dim(mixed, copy_index * part, part, 0), cotangent),
+        after(
+            lax.dynamic_slice_in_dim(mixed, copy_index * part, part, 0), cotangent, out_exchange.step()
+        ),
         "ctx",
         axis=0,
     ).reshape(groups, tokens, query_width)
-    w_out_halves = out_exchange.finish(mixed)
-
-    wide = min(512, tokens)
+    w_out_halves = out_exchange.finish()
+
     middle, normed_two, gates = middle_rows(
-        mixed_all, w_out_halves, gathered, gain_two, router_all, wide
+        mixed_all, w_out_halves, gathered, gain_two, router_all, own, block
     )
     flag = lambda bit: has(bit).astype(jnp.int32)
     place = jnp.stack([chip, me, flag(bits[0]), flag(bits[-1])]).astype(jnp.int32)
     scaled_one, scaled_two, grad_gate_pre, grad_up_pre, grad_live, extra = expert_rows(
-        place, normed_two, cotangent, gathered, gates, w_gate, w_up, w_down, wide
+        place, normed_two, cotangent, gathered, gates, w_gate, w_up, w_down, own, block
     )
     grad_rows, out_rows = expert_sums(
-        place, scaled_one, grad_gate_pre, grad_up_pre, extra, w_gate, w_up, w_down, wide
+        place, scaled_one, grad_gate_pre, grad_up_pre, extra, w_gate, w_up, w_down, block
     )
     grad_two_sum = lax.psum_scatter(grad_rows, "ctx", scatter_dimension=0, tiled=True)
 
@@ -1130,17 +1174,16 @@
         mine(array) for array in (middle, gates, grad_live, normed_two)
     ]
 
-    def product(side, e, dtype):
-        right, scaled = ((grad_gate_pre, scaled_one), (grad_up_pre, scaled_two))[side]
-        return expert_product(normed_two, right, scaled, grad_live, e, side, dtype)
-
+    products = lambda e, dtype: expert_products(
+        normed_two, grad_gate_pre, grad_up_pre, scaled_one, scaled_two, grad_live, e, dtype
+    )
     normed_two, grad_live = after((normed_two, grad_live), grad_rows)
     chains = [Chain(bits), Chain(bits[::-1])]
-    for side, chain in enumerate(chains):
-        chain.send(product(side, 0, jnp.bfloat16))
+    for chain, sent in zip(chains, products(0, jnp.bfloat16)):
+        chain.send(sent)
     normed_two, grad_live = after((normed_two, grad_live), *[chain.sent for chain in chains])
-    for side, chain in enumerate(chains):
-        chain.kept = product(side, 1, jnp.float32)
+    for chain, kept in zip(chains, products(1, jnp.float32)):
+        chain.kept = kept
 
     grad_middle, grad_branch, grad_mixed, grad_logits, gain_two_grad = turn_rows(
         after(grad_two_sum, *[(c.kept, c.flying) for c in chains]),
@@ -1151,7 +1194,6 @@
         live_own,
         w_out_halves,
     )
-    grad_branch_all = lax.all_gather(grad_branch, "ctx", axis=0, tiled=True)
 
     def deal(blocks, *others):
         blocks = blocks.reshape((chips, 2) + blocks.shape[1:])
@@ -1165,13 +1207,16 @@
         both = lax.dynamic_slice_in_dim(both, (chips - chip) % chips, chips, 0)
         return both.reshape((size,) + both.shape[2:])
 
-    grad_mixed_all = deal(jnp.repeat(grad_mixed, copies, 0)).reshape(tokens, query_width)
-    sent = [grad_mixed_all]
-    while chains[0].stage < len(bits):
+    sent = [grad_mixed]
+    while chains[0].stage <= len(bits):
         sent = [chain.step(*sent) for chain in chains]
+    grad_mixed_all = deal(jnp.repeat(grad_mixed, copies, 0), *sent).reshape(tokens, query_width)
+    grad_branch_all = lax.all_gather(
+        after(grad_branch, grad_mixed_all), "ctx", axis=0, tiled=True
+    )
     grad_query, grad_pair = attend_back(
         query,
-        after(grad_mixed_all, *sent),
+        grad_mixed_all,
         log_total,
         cosine_table,
         sine_table,
@@ -1179,15 +1224,15 @@
         segment_rows,
         key,
         value,
+        own,
     )
     if copies > 1:
         places = jnp.arange(tokens, dtype=jnp.int32)
         counted = (places // part == copy_index)[:, None]
         grad_query = jnp.where(counted, grad_query, jnp.zeros((), jnp.bfloat16))
         grad_pair = jnp.where(counted, grad_pair, jnp.zeros((), jnp.bfloat16))
-    sent = [chain.step(grad_pair) for chain in chains]
-    grad_one_low, head_grads = close_rows(
-        after(grad_query, *sent),
+    both_rows, head_grads = close_rows(
+        grad_query,
         grad_pair,
         head_all,
         gathered,
@@ -1195,13 +1240,15 @@
         gain_two_grad,
         normed_own,
         grad_logits,
+        out_rows,
         rows_own,
         side_width,
         block,
     )
-    grad_one = lax.psum_scatter(
-        grad_one_low, "ctx", scatter_dimension=0, tiled=True
+    both_sums = lax.psum_scatter(
+        both_rows, "ctx", scatter_dimension=0, tiled=True
     ).astype(jnp.float32)
+    grad_one, out_sum = both_sums[:, :MODEL_WIDTH], both_sums[:, MODEL_WIDTH:]
     grad_proj_out = dot(
         lax.dynamic_slice_in_dim(mixed, copy_index * rows_own, rows_own, 1),
         grad_branch_all,
@@ -1223,13 +1270,14 @@
     sent = [cube.halve() for cube in cubes]
     while chains[0].stage < chains[0].steps:
         sent = [chain.step(*sent) for chain in chains]
+    first = [chain.piece(0, 3) for chain in chains]
     while cubes[0].stage < len(bits):
         for cube in cubes:
             cube.add(*sent)
         sent = [cube.halve() for cube in cubes]
-    first = [chain.piece(0, 3, *sent) for chain in chains]
+    second = [chain.piece(1, 3, *sent) for chain in chains]
     for cube in cubes:
-        cube.add(*sent)
+        cube.add(*first)
     totals = [cube.value.astype(jnp.bfloat16) for cube in cubes]
     blocks = jnp.concatenate(
         [
@@ -1247,35 +1295,30 @@
             [rows.reshape(share, line), totals[h].reshape(share, -1)[:, line:]], 1
         )
         cube.value = rows.reshape(totals[h].shape)
-    sent = [cube.back() for cube in cubes]
-    second = [chain.piece(1, 3, *sent) for chain in chains]
-    while cubes[0].stage > 0:
-        for cube in cubes:
-            cube.join(*sent)
-        sent = [cube.back() for cube in cubes]
-    third = [chain.piece(2, 3, *sent, *first) for chain in chains]
+    sent = [cube.back(*second) for cube in cubes]
+    third = [chain.piece(2, 3, *sent) for chain in chains]
     keeps = place[2:]
     grad_gate, grad_up = [
         into_output(keeps, side, *after((chain.sent, first[side], second[side]), *sent))
         for side, chain in enumerate(chains)
     ]
+    while cubes[0].stage > 0:
+        for cube in cubes:
+            cube.join(*sent)
+        sent = [cube.back() for cube in cubes]
+    grad_down = down_output(
+        keeps, *after((chains[0].sent, third[0], chains[1].sent, third[1]), grad_gate, grad_up)
+    )
     for cube in cubes:
-        cube.join(grad_gate, grad_up)
-    head_outs = head_outputs(*[cube.value.reshape(rows_own, -1) for cube in cubes], copies, side_width)
+        cube.join(grad_down)
+    head_outs = head_outputs(
+        *[cube.value.reshape(rows_own, -1) for cube in cubes], copies, side_width
+    )
     small = head_outs[4]
-
-    moe_sum = lax.psum_scatter(
-        after(out_rows, grad_branch), "ctx", scatter_dimension=0, tiled=True
-    ).astype(jnp.float32)
-    output = jnp.where((segments[0] != 0)[:, None], middle_own + moe_sum, 0.0)
+    output = jnp.where((segments[0] != 0)[:, None], middle_own + out_sum, 0.0)
     own_hidden = inputs[0].astype(jnp.float32)
     own_scale = lax.rsqrt(jnp.mean(own_hidden * own_hidden, -1, keepdims=True) + EPS)
     grad_in = grad_middle + norm_back(grad_one * gain_one, own_hidden * own_scale, own_scale)
-    grad_down = down_output(
-        keeps,
-        *after((chains[0].sent, third[0], chains[1].sent, third[1]), head_outs, grad_in, output),
-    )
-
     return (
         output.astype(jnp.bfloat16)[None],
         grad_in[None],

time: 543 us -> 507 us (0.934); the launches traced: 535 us -> 505 us
  blocking collectives: 0 us -> 24.5 us
  waiting for transfers between devices: 224 us -> 204 us
  local copies, waits for them, and re-layouts: 51.7 us -> 35 us
  starting transfers between devices: 56 us -> 42.6 us
    all_to_all x0 -> x1, blocking collectives: none -> 24.5 us  [per_device(): lax.all_to_all(head_columns, 'ctx', split_axis=0, concat_axis=0, tiled=True)]
    unnamed x167 -> x106, local copies, waits for them, and re-layouts: 38.2 us -> 14 us
    ppermute x9 -> x6, waiting for transfers between devices: 38.6 us -> 15.2 us  [from_chip(): lax.ppermute(value, 'ctx', [(i, (i - 2 * k) % size) for i in range(size)])]
    ppermute x9 -> x6, starting transfers between devices: 23.8 us -> 8.01 us  [from_chip(): lax.ppermute(value, 'ctx', [(i, (i - 2 * k) % size) for i in range(size)])]
    all_gather x3, waiting for transfers between devices: 25.5 us -> 34.2 us  [the longest x1 16.5 us: per_device(): gathered = lax.all_gather(rows, 'ctx', axis=0)]
    pallas_call x5 -> x3, Pallas kernels: 35 us -> 40.6 us  [the longest x2 28.9 us: expert_products(): pl.pallas_call(product_kernel, out_shape=(jax.ShapeDtypeStruct((rows, hid...]
  transfers between devices with their start and end apart: 47 -> 42, of which waited for: 28 -> 23; matrix products, arithmetic and copies ran while one was open for 11% -> 10% of each run, Pallas kernels for 15% -> 17%
where the time goes in v5:
time: 507 us; the launch traced here: 505 us
  waiting for transfers between devices  204 us (40%)
  Pallas kernels  140 us (28%)
  starting transfers between devices  42.6 us (8%)
  other arithmetic  41.3 us (8%)
  local copies, waits for them, and re-layouts  35 us (7%)
  blocking collectives  24.5 us (5%)
  between operations  15.1 us (3%)
    ppermute x28, waiting for transfers between devices, swap(): return lax.ppermute(value, 'rep', [(i, i ^ bit) for i in range(size)])  139 us
    ppermute x28, starting transfers between devices, swap(): return lax.ppermute(value, 'rep', [(i, i ^ bit) for i in range(size)])  33.8 us
    pallas_call x2, Pallas kernels, expert_products(): pl.pallas_call(product_kernel, out_shape=(jax.ShapeDtypeStruct((rows, hid...  28.9 us
    all_to_all x1, blocking collectives, per_device(): lax.all_to_all(head_columns, 'ctx', split_axis=0, concat_axis=0, tiled=True)  24.5 us
    pallas_call x1, Pallas kernels, expert_rows(): pl.pallas_call(expert_kernel, out_shape=(wide, wide, wide, wide, jax.Shap...  20.5 us
    pallas_call x1, Pallas kernels, expert_sums(): pl.pallas_call(rows_kernel, out_shape=(jax.ShapeDtypeStruct((tokens, feat...  18.3 us
    all_gather x1, waiting for transfers between devices, per_device(): gathered = lax.all_gather(rows, 'ctx', axis=0)  16.5 us
    pallas_call x1, Pallas kernels, attend(): pl.pallas_call(attend_kernel, out_shape=(shaped((tokens, features), jnp.b...  16.1 us
  transfers between devices with their start and end apart: 42, of which 23 were waited for; matrix products, arithmetic and copies ran while one was open for 10% of the time, Pallas kernels for 17%

profile of v5, /device:TPU:0, one launch (start us, length us, event | category | flops | bytes accessed | tf_op | source)
XLA Modules:
  0.0 505.5 jit_solution(13012317157675950048)
XLA Ops:
  9.5 1.9 fusion.16
  15.4 24.5 %all_to_all.5 = bf16[8,48,384]{2,1,0:T(8,128)(2,1)S(1)} all-to-all(bf16[8,48,384]{2,1,0:T(8,128)(2,1)S(1)} %copy.95), channel_id=1, replica_groups=mesh['rep'=4,'ctx'=8] {'ctx'}, dimensions={0} | all-to-all | bytes 589824 | tf_op jit(solution)/shard_map/all_to_all | solution.py:1127
  43.0 2.8 collective-permute-done
  49.4 5.6 %collective-permute-done.3 = bf16[4,2,1,48,384]{4,3,0,2,1:T(8,128)(2,1)S(1)} collective-permute-done((bf16[4,2,1,48,384]{4,3,0,2,1:T(8,128)(2,1)S(1)}, bf16[4,2,1,48,384]{4,3,0,2,1:T(8,128)(2,1)S(1)}, u32[]{:S(2)}, u32[]{:S(2)}) %collective-permute-start.3) | collective-permute-done | bytes 294944 | tf_op jit(solution)/shard_map/ppermute | solution.py:922
  55.0 16.5 %all-gather.11.cloned.1.call-done = bf16[1408,1664]{1,0:T(8,128)(2,1)} async-done(((bf16[176,1664]{1,0:T(8,128)(2,1)}), bf16[1408,1664]{1,0:T(8,128)(2,1)}) %all-gather.11.cloned.1.call-update) | async-done | bytes 4685840 | tf_op jit(solution)/shard_map/all_gather | solution.py:1098
  77.4 16.1 %shard_map.238 = (bf16[1024,1536]{1,0:T(8,128)(2,1)}, bf16[1024,192]{1,0:T(8,128)(2,1)S(1)}, bf16[1024,64]{1,0:T(8,128)(2,1)S(1)}, bf16[1024,64]{1,0:T(8,128)(2,...) custom-call(bf16[8,176,1664]{2,1,0:T(8,128)(2,1)} %bitcast.171, ...), custom_call_target="tpu_custom_call" | custom-call | bytes 1024 | tf_op jit(solution)/shard_map/pallas_call | solution.py:191
  93.6 2.3 broadcast_select_fusion.9
  98.1 12.3 %all-gather.7.cloned.1.call-done.cotangent_ref = bf16[1024,1536]{1,0:T(8,128)(2,1)} async-done(((bf16[128,1536]{1,0:T(8,128)(2,1)}), bf16[1024,1536]{1,0:T(8,128)(2,1)}) %all-gather.7.cloned.1.call-update) | async-done | bytes 3145744 | tf_op jit(solution)/shard_map/all_gather | solution.py:1099
  115.1 23.6 %collective-permute-done.6 = bf16[4,1,2,48,1536]{4,3,0,2,1:T(8,128)(2,1)} collective-permute-done((bf16[4,1,2,48,1536]{4,3,0,2,1:T(8,128)(2,1)S(1)}, bf16[4,1,2,48,1536]{4,3,0,2,1:T(8,128)(2,1)}, u32[]{:S(2)}, u32[]{:S(2)}) %collective-permute-start.6) | collective-permute-done | bytes 1179680 | tf_op jit(solution)/shard_map/ppermute | solution.py:922
  142.4 1.7 copy.99
  144.1 13.9 %all-gather.13.cloned.1.call-done = bf16[8192,192]{1,0:T(8,128)(2,1)} async-done(((bf16[1024,192]{1,0:T(8,128)(2,1)}), bf16[8192,192]{1,0:T(8,128)(2,1)}) %all-gather.13.cloned.1.call-update) | async-done | bytes 3145744 | tf_op jit(solution)/shard_map/all_gather | solution.py:1148
  158.0 1.7 copy-done.4
  160.7 11.0 %shard_map.239 = (f32[1024,1536]{1,0:T(8,128)}, bf16[1024,1536]{1,0:T(8,128)(2,1)}, f32[1024,16]{1,0:T(8,128)S(1)}) custom-call(bf16[8,1024,192]{2,1,0:T(8,128)(2,1)} %bitcast.184, bf16[768,1536]{1,0:T(8,128)(2,1)S(1)} %bitcast.155, bf16[768,1536]{1,0:T(8,128)(2,1)S(1)} %bitcast.158, bf16[8,176,1664]{2,1,0:T(8,128)(2,1)} %bitcast.174, ...), custom_call_target="tpu_custom_call" | custom-call | flops 4831838208 | bytes 18874368 | tf_op jit(solution)/shard_map/pallas_call | solution.py:384
  171.7 20.5 %shard_map.240 = (bf16[2,1024,512]{2,1,0:T(8,128)(2,1)}, bf16[2,1024,512]{2,1,0:T(8,128)(2,1)}, bf16[2,1024,512]{2,1,0:T(8,128)(2,1)}, bf16[2,1024,512]{2,1,0:T(...) custom-call(s32[4]{0:T(128)S(1)} %pad_add_fusion.place_ref, ...), custom_call_target="tpu_custom_call" | custom-call | flops 9663676416 | bytes 25165824 | tf_op jit(solution)/shard_map/pallas_call | solution.py:478
  192.2 18.3 %shard_map.241 = (bf16[1024,1664]{1,0:T(8,128)(2,1)}, bf16[1024,1536]{1,0:T(8,128)(2,1)}) custom-call(s32[4]{0:T(128)S(1)} %pad_add_fusion.place_ref, bf16[2,1024,512]{2,1,0:T(8,128)(2,1)} %get-tuple-element.96.scaled_ref.scaled_one_ref, bf16[2,1024,512]{2,1,0:T(8,128)(2,1)} %get-tuple-element.97.grad_gate_ref.gate_ref, ...), custom_call_target="tpu_custom_call" | custom-call | bytes 1024 | tf_op jit(solution)/shard_map/pallas_call | solution.py:624
  210.8 13.6 %shard_map.242 = (bf16[2304,512]{1,0:T(8,128)(2,1)}, bf16[2304,512]{1,0:T(8,128)(2,1)}) custom-call(bf16[1024,1536]{1,0:T(8,128)(2,1)} %get-tuple-element.107.normed_ref.left_ref, bf16[2,1024,512]{2,1,0:T(8,128)(2,1)} %get-tuple-element.97.grad_gate_ref.gate_ref, bf16[2,1024,512]{2,1,0:T(8,128)(2,1)} %get-tuple-element.98.grad_up_ref.up_ref, ...), custom_call_target="tpu_custom_call" | custom-call | bytes 1024 | tf_op jit(solution)/shard_map/pallas_call | solution.py:568
  227.4 15.2 %shard_map.243 = (f32[2304,512]{1,0:T(8,128)}, f32[2304,512]{1,0:T(8,128)}) custom-call(bf16[1024,1536]{1,0:T(8,128)(2,1)} %get-tuple-element.107.normed_ref.left_ref, bf16[2,1024,512]{2,1,0:T(8,128)(2,1)} %get-tuple-element.97.grad_gate_ref.gate_ref, bf16[2,1024,512]{2,1,0:T(8,128)(2,1)} %get-tuple-element.98.grad_up_ref.up_ref, ...), custom_call_target="tpu_custom_call" | custom-call | bytes 1024 | tf_op jit(solution)/shard_map/pallas_call | solution.py:568
  244.2 1.8 constant_dynamic-slice_fusion.2.live_ref
  245.9 2.1 constant_dynamic-slice_fusion.4.middle_ref
  248.0 30.2 %collective-permute-done.8 = bf16[2304,512]{1,0:T(8,128)(2,1)} collective-permute-done((bf16[2304,512]{1,0:T(8,128)(2,1)}, bf16[2304,512]{1,0:T(8,128)(2,1)}, u32[]{:S(2)}, u32[]{:S(2)}) %collective-permute-start.8) | collective-permute-done | bytes 2359328 | tf_op jit(solution)/shard_map/ppermute | solution.py:922
  280.7 6.2 %shard_map.244 = (f32[128,1536]{1,0:T(8,128)}, bf16[128,1536]{1,0:T(8,128)(2,1)}, bf16[8,128,192]{2,1,0:T(8,128)(2,1)}, bf16[128,16]{1,0:T(8,128)(2,1)}, f32[1,1536]{1,0:T(1,128)}) custom-call(bf16[128,1664]{1,0:T(8,128)(2,1)} %reduce-scatter.3.cloned.1.call-done.sum_ref, f32[128,16]{1,0:T(8,128)} %constant_dynamic-slice_fusion.3.gates_ref, ...), custom_call_target="tpu_custom_call" | custom-call | bytes 128 | tf_op jit(solution)/shard_map/pallas_call | solution.py:693
  287.0 2.7 add_convert_fusion.3
  291.1 2.4 add_convert_fusion.2
  294.9 1.7 collective-permute-start.11
  296.6 2.3 collective-permute-start.10
  298.9 4.5 collective-permute-done.12
  303.3 3.4 collective-permute-done.11
  308.4 8.5 %collective-permute-done.13 = bf16[1152,512]{1,0:T(8,128)(2,1)} collective-permute-done((bf16[1152,512]{1,0:T(8,128)(2,1)}, bf16[1152,512]{1,0:T(8,128)(2,1)}, u32[]{:S(2)}, u32[]{:S(2)}) %collective-permute-start.13) | collective-permute-done | bytes 1179680 | tf_op jit(solution)/shard_map/ppermute | solution.py:922
  316.9 3.8 add_convert_fusion.1
  320.7 2.6 add_convert_fusion
  328.1 1.7 collective-permute-start.17
  330.6 14.1 %shard_map.245 = (bf16[1024,192]{1,0:T(8,128)(2,1)S(1)}, bf16[1024,128]{1,0:T(8,128)(2,1)S(1)}) custom-call(bf16[1024,192]{1,0:T(8,128)(2,1)S(1)} %copy-done.15, bf16[1024,192]{1,0:T(8,128)(2,1)S(1)} %bitcast.169, f32[3,1024,1]{2,1,0:T(8,128)S(1)} %copy-done.11, f32[1024,64]{1,0:T(8,128)S(1)} %copy-done.7, f32[1024,64]{1,0:T(8,128)S(1)} %copy-done.9, ...), custom_call_target="tpu_custom_call" | custom-call | bytes 1024 | tf_op jit(solution)/shard_map/pallas_call | solution.py:314
  344.7 11.7 %shard_map.246 = (bf16[1024,3072]{1,0:T(8,128)(2,1)}, f32[192,3072]{1,0:T(8,128)S(1)}) custom-call(bf16[1024,192]{1,0:T(8,128)(2,1)S(1)} %get-tuple-element.124.query_ref, bf16[1024,128]{1,0:T(8,128)(2,1)S(1)} %get-tuple-element.125.pair_ref, bf16[1536,384]{1,0:T(8,128)(2,1)S(1)} %pad_maximum_fusion.6.weight_ref, bf16[8,176,1664]{2,1,0:T(8,128)(2,1)} %bitcast.178, ...), custom_call_target="tpu_custom_call" | custom-call | bytes 1024 | tf_op jit(solution)/shard_map/pallas_call | solution.py:784
  357.6 5.5 %all-gather.9.cloned.1.call-done = bf16[1024,1536]{1,0:T(8,128)(2,1)} async-done(((bf16[128,1536]{1,0:T(8,128)(2,1)}), bf16[1024,1536]{1,0:T(8,128)(2,1)}) %all-gather.9.cloned.1.call-update) | async-done | bytes 3145744 | tf_op jit(solution)/shard_map/all_gather | solution.py:1214
  363.1 2.9 fusion.41
  382.5 24.7 %collective-permute-done.22 = bf16[1,2,48,2304]{3,2,1,0:T(8,128)(2,1)S(1)} collective-permute-done((bf16[1,2,48,2304]{3,2,1,0:T(8,128)(2,1)S(1)}, bf16[1,2,48,2304]{3,2,1,0:T(8,128)(2,1)S(1)}, u32[]{:S(2)}, u32[]{:S(2)}) %collective-permute-start.22) | collective-permute-done | bytes 442400 | tf_op jit(solution)/shard_map/ppermute | solution.py:922
  408.3 2.5 collective-permute-done.19
  421.8 2.4 collective-permute-start.24
  424.2 4.7 collective-permute-done.26
  428.9 2.5 collective-permute-done.25
  436.3 15.5 %collective-permute-done.28.refs_2_ = bf16[768,512]{1,0:T(8,128)(2,1)S(1)} collective-permute-done((bf16[768,512]{1,0:T(8,128)(2,1)S(1)}, bf16[768,512]{1,0:T(8,128)(2,1)S(1)}, u32[]{:S(2)}, u32[]{:S(2)}) %collective-permute-start.28) | collective-permute-done | bytes 786464 | tf_op jit(solution)/shard_map/ppermute | solution.py:922
  456.3 4.2 collective-permute-done.30
  462.2 16.9 %collective-permute-done.34 = bf16[1,1,48,2304]{3,2,1,0:T(8,128)(2,1)S(1)} collective-permute-done((bf16[1,1,48,2304]{3,2,1,0:T(8,128)(2,1)S(1)}, bf16[1,1,48,2304]{3,2,1,0:T(8,128)(2,1)S(1)}, u32[]{:S(2)}, u32[]{:S(2)}) %collective-permute-start.34) | collective-permute-done | bytes 221216 | tf_op jit(solution)/shard_map/ppermute | solution.py:922
  479.8 3.7 into_output.2
  483.4 3.6 into_output.3
  487.1 3.5 shard_map.247
  491.0 1.9 head_outputs.1
  496.1 2.5 fusion.10
  (281 shorter events, 92.1 us)
Async XLA Ops:
  7.2 64.3 %all-gather.11.cloned.1.call-start = ((), (), s32[]{:S(2)}) async-start(), calls=%async_computation.7 | async-start | bytes 5271552 | tf_op jit(solution)/shard_map/all_gather | solution.py:1098
  11.4 98.9 %all-gather.7.cloned.1.call-start = ((), (), s32[]{:S(2)}) async-start(), calls=%async_computation.3 | async-start | bytes 3538944 | tf_op jit(solution)/shard_map/all_gather | solution.py:1099
  12.2 145.8 %all-gather.13.cloned.1.call-start = ((), (), s32[]{:S(2)}) async-start(), calls=%async_computation.8 | async-start | bytes 4718592 | tf_op jit(solution)/shard_map/all_gather | solution.py:1148
  39.9 5.9 %collective-permute-start = (bf16[4,1,1,48,384]{4,3,0,2,1:T(8,128)(2,1)S(1)}, bf16[4,1,1,48,384]{4,3,0,2,1:T(8,128)(2,1)S(1)}, u32[]{:S(2)}, u32[]{:S(2)}) collective-permute-start(bf16[4,1,1,48,384]{4,3,0,2,1:T(8,128)(2,1)S(1)} %get-tuple-element.290), channel_id=1, source_target_pairs={{0,8},{8,0},{16,24},{24,16},{1,9},{9,1},{17,25},{25,17},{2,10},{10... | collective-permute-start | bytes 442376 | tf_op jit(solution)/shard_map/ppermute | solution.py:922
  41.4 5.5 %collective-permute-start.2 = (bf16[4,1,1,48,384]{4,3,0,2,1:T(8,128)(2,1)S(1)}, bf16[4,1,1,48,384]{4,3,0,2,1:T(8,128)(2,1)S(1)}, u32[]{:S(2)}, u32[]{:S(2)}) collective-permute-start(bf16[4,1,1,48,384]{4,3,0,2,1:T(8,128)(2,1)S(1)} %get-tuple-element.291), channel_id=1, source_target_pairs={{0,16},{8,24},{16,0},{24,8},{1,17},{9,25},{17,1},{25,9},{2,18},{10... | collective-permute-start | bytes 442376 | tf_op jit(solution)/shard_map/ppermute | solution.py:922
  47.1 8.0 %collective-permute-start.3 = (bf16[4,2,1,48,384]{4,3,0,2,1:T(8,128)(2,1)S(1)}, bf16[4,2,1,48,384]{4,3,0,2,1:T(8,128)(2,1)S(1)}, u32[]{:S(2)}, u32[]{:S(2)}) collective-permute-start(bf16[4,2,1,48,384]{4,3,0,2,1:T(8,128)(2,1)S(1)} %pad_maximum_fusion.17), channel_id=1, source_target_pairs={{0,8},{8,0},{16,24},{24,16},{1,9},{9,1},{17,25},{25,17},{2,10},{10... | collective-permute-start | bytes 884744 | tf_op jit(solution)/shard_map/ppermute | solution.py:922
  47.8 28.3 %collective-permute-start.1 = (bf16[4,1,2,48,384]{4,3,0,2,1:T(8,128)(2,1)S(1)}, bf16[4,1,2,48,384]{4,3,0,2,1:T(8,128)(2,1)S(1)}, u32[]{:S(2)}, u32[]{:S(2)}) collective-permute-start(bf16[4,1,2,48,384]{4,3,0,2,1:T(8,128)(2,1)S(1)} %pad_maximum_fusion.16), channel_id=1, source_target_pairs={{0,16},{8,24},{16,0},{24,8},{1,17},{9,25},{17,1},{25,9},{2,18},{10... | collective-permute-start | bytes 884744 | tf_op jit(solution)/shard_map/ppermute | solution.py:922
  72.8 20.8 %collective-permute-start.5 = (bf16[4,1,1,48,1536]{4,3,0,2,1:T(8,128)(2,1)S(1)}, bf16[4,1,1,48,1536]{4,3,0,2,1:T(8,128)(2,1)S(1)}, u32[]{:S(2)}, u32[]{:S(2)}) collective-permute-start(bf16[4,1,1,48,1536]{4,3,0,2,1:T(8,128)(2,1)S(1)} %get-tuple-element.236), channel_id=1, source_target_pairs={{0,16},{8,24},{16,0},{24,8},{1,17},{9,25},{17,1},{25,9},{2,18},{10... | collective-permute-start | bytes 1769480 | tf_op jit(solution)/shard_map/ppermute | solution.py:922
  74.4 19.2 %collective-permute-start.4 = (bf16[4,1,1,48,1536]{4,3,0,2,1:T(8,128)(2,1)S(1)}, bf16[4,1,1,48,1536]{4,3,0,2,1:T(8,128)(2,1)S(1)}, u32[]{:S(2)}, u32[]{:S(2)}) collective-permute-start(bf16[4,1,1,48,1536]{4,3,0,2,1:T(8,128)(2,1)S(1)} %get-tuple-element.237), channel_id=1, source_target_pairs={{0,8},{8,0},{16,24},{24,16},{1,9},{9,1},{17,25},{25,17},{2,10},{10... | collective-permute-start | bytes 1769480 | tf_op jit(solution)/shard_map/ppermute | solution.py:922
  110.4 168.9 %reduce-scatter.3.cloned.1.call-start = ((), (), s32[]{:S(2)}) async-start(), calls=%async_computation.4 | async-start | bytes 3833856 | tf_op jit(solution)/shard_map/reduce_scatter | solution.py:1168
  110.4 28.3 %collective-permute-start.6 = (bf16[4,1,2,48,1536]{4,3,0,2,1:T(8,128)(2,1)S(1)}, bf16[4,1,2,48,1536]{4,3,0,2,1:T(8,128)(2,1)}, u32[]{:S(2)}, u32[]{:S(2)}) collective-permute-start(bf16[4,1,2,48,1536]{4,3,0,2,1:T(8,128)(2,1)S(1)} %pad_maximum_fusion.7), channel_id=1, source_target_pairs={{0,16},{8,24},{16,0},{24,8},{1,17},{9,25},{17,1},{25,9},{2,18},{10... | collective-permute-start | bytes 3538952 | tf_op jit(solution)/shard_map/ppermute | solution.py:922
  112.0 28.6 %collective-permute-start.7 = (bf16[4,2,1,48,1536]{4,3,0,2,1:T(8,128)(2,1)}, bf16[4,2,1,48,1536]{4,3,0,2,1:T(8,128)(2,1)S(1)}, u32[]{:S(2)}, u32[]{:S(2)}) collective-permute-start(bf16[4,2,1,48,1536]{4,3,0,2,1:T(8,128)(2,1)} %pad_maximum_fusion.8), channel_id=1, source_target_pairs={{0,8},{8,0},{16,24},{24,16},{1,9},{9,1},{17,25},{25,17},{2,10},{10... | collective-permute-start | bytes 3538952 | tf_op jit(solution)/shard_map/ppermute | solution.py:922
  114.2 43.8 %copy-start.20 = (f32[1,1536]{1,0:T(1,128)}, f32[1,1536]{1,0:T(1,128)S(1)}, u32[]{:S(2)}) copy-start(f32[1,1536]{1,0:T(1,128)S(1)} %reshape.322.gain_ref) | copy-start | bytes 18436
  171.7 20.5 %copy-start.22 = (f32[1024,16]{1,0:T(8,128)}, f32[1024,16]{1,0:T(8,128)S(1)}, u32[]{:S(2)}) copy-start(f32[1024,16]{1,0:T(8,128)S(1)} %get-tuple-element.95.gates_ref) | copy-start | bytes 196612
  210.6 152.5 %all-gather.9.cloned.1.call-start = ((), (), s32[]{:S(2)}) async-start(), calls=%async_computation.6 | async-start | bytes 3538944 | tf_op jit(solution)/shard_map/all_gather | solution.py:1214
  224.5 53.7 %collective-permute-start.8 = (bf16[2304,512]{1,0:T(8,128)(2,1)}, bf16[2304,512]{1,0:T(8,128)(2,1)}, u32[]{:S(2)}, u32[]{:S(2)}) collective-permute-start(bf16[2304,512]{1,0:T(8,128)(2,1)} %get-tuple-element.105), channel_id=1, source_target_pairs={{0,8},{8,0},{16,24},{24,16},{1,9},{9,1},{17,25},{25,17},{2,10},{10... | collective-permute-start | bytes 7077896 | tf_op jit(solution)/shard_map/ppermute | solution.py:922
  226.0 53.3 %collective-permute-start.9 = (bf16[2304,512]{1,0:T(8,128)(2,1)}, bf16[2304,512]{1,0:T(8,128)(2,1)S(1)}, u32[]{:S(2)}, u32[]{:S(2)}) collective-permute-start(bf16[2304,512]{1,0:T(8,128)(2,1)} %get-tuple-element.106), channel_id=1, source_target_pairs={{0,16},{8,24},{16,0},{24,8},{1,17},{9,25},{17,1},{25,9},{2,18},{10... | collective-permute-start | bytes 7077896 | tf_op jit(solution)/shard_map/ppermute | solution.py:922
  289.7 27.2 %collective-permute-start.13 = (bf16[1152,512]{1,0:T(8,128)(2,1)}, bf16[1152,512]{1,0:T(8,128)(2,1)}, u32[]{:S(2)}, u32[]{:S(2)}) collective-permute-start(bf16[1152,512]{1,0:T(8,128)(2,1)} %add_convert_fusion.3), channel_id=1, source_target_pairs={{0,16},{8,24},{16,0},{24,8},{1,17},{9,25},{17,1},{25,9},{2,18},{10... | collective-permute-start | bytes 3538952 | tf_op jit(solution)/shard_map/ppermute | solution.py:922
  293.6 27.2 %collective-permute-start.14 = (bf16[1152,512]{1,0:T(8,128)(2,1)S(1)}, bf16[1152,512]{1,0:T(8,128)(2,1)}, u32[]{:S(2)}, u32[]{:S(2)}) collective-permute-start(bf16[1152,512]{1,0:T(8,128)(2,1)S(1)} %add_convert_fusion.2), channel_id=1, source_target_pairs={{0,8},{8,0},{16,24},{24,16},{1,9},{9,1},{17,25},{25,17},{2,10},{10... | collective-permute-start | bytes 3538952 | tf_op jit(solution)/shard_map/ppermute | solution.py:922
  294.9 8.4 %collective-permute-start.12 = (bf16[2,128,192]{2,1,0:T(8,128)(2,1)}, bf16[2,128,192]{2,1,0:T(8,128)(2,1)S(1)}, u32[]{:S(2)}, u32[]{:S(2)}) collective-permute-start(bf16[2,128,192]{2,1,0:T(8,128)(2,1)} %get-tuple-element.269), channel_id=1, source_target_pairs={{0,2},{1,3},{2,4},{3,5},{4,6},{5,7},{6,0},{7,1},{8,10},{9,11},{10,... | collective-permute-start | bytes 294920 | tf_op jit(solution)/shard_map/ppermute | solution.py:1102
  294.9 11.8 %collective-permute-start.11 = (bf16[2,128,192]{2,1,0:T(8,128)(2,1)S(1)}, bf16[2,128,192]{2,1,0:T(8,128)(2,1)S(1)}, u32[]{:S(2)}, u32[]{:S(2)}) collective-permute-start(bf16[2,128,192]{2,1,0:T(8,128)(2,1)S(1)} %get-tuple-element.270), channel_id=1, source_target_pairs={{0,4},{1,5},{2,6},{3,7},{4,0},{5,1},{6,2},{7,3},{8,12},{9,13},{10,... | collective-permute-start | bytes 294920 | tf_op jit(solution)/shard_map/ppermute | solution.py:1102
  296.6 10.2 %collective-permute-start.10 = (bf16[2,128,192]{2,1,0:T(8,128)(2,1)S(1)}, bf16[2,128,192]{2,1,0:T(8,128)(2,1)S(1)}, u32[]{:S(2)}, u32[]{:S(2)}) collective-permute-start(bf16[2,128,192]{2,1,0:T(8,128)(2,1)S(1)} %get-tuple-element.271), channel_id=1, source_target_pairs={{0,6},{1,7},{2,0},{3,1},{4,2},{5,3},{6,4},{7,5},{8,14},{9,15},{10,... | collective-permute-start | bytes 294920 | tf_op jit(solution)/shard_map/ppermute | solution.py:1102
  323.4 1.7 collective-permute-start.15
  326.5 168.0 %reduce-scatter.5.cloned.1.call-start = ((), (), s32[]{:S(2)}) async-start(), calls=%async_computation.5 | async-start | bytes 7077888 | tf_op jit(solution)/shard_map/reduce_scatter | solution.py:1248
  328.1 41.0 %collective-permute-start.17 = (bf16[1152,512]{1,0:T(8,128)(2,1)}, bf16[1152,512]{1,0:T(8,128)(2,1)}, u32[]{:S(2)}, u32[]{:S(2)}) collective-permute-start(bf16[1152,512]{1,0:T(8,128)(2,1)} %add_convert_fusion.1), channel_id=1, source_target_pairs={{0,16},{8,24},{16,0},{24,8},{1,17},{9,25},{17,1},{25,9},{2,18},{10... | collective-permute-start | bytes 3538952 | tf_op jit(solution)/shard_map/ppermute | solution.py:922
  329.8 43.4 %collective-permute-start.18 = (bf16[1152,512]{1,0:T(8,128)(2,1)S(1)}, bf16[1152,512]{1,0:T(8,128)(2,1)}, u32[]{:S(2)}, u32[]{:S(2)}) collective-permute-start(bf16[1152,512]{1,0:T(8,128)(2,1)S(1)} %add_convert_fusion), channel_id=1, source_target_pairs={{0,8},{8,0},{16,24},{24,16},{1,9},{9,1},{17,25},{25,17},{2,10},{10... | collective-permute-start | bytes 3538952 | tf_op jit(solution)/shard_map/ppermute | solution.py:922
  367.4 13.4 %collective-permute-start.16 = (bf16[2,1,48,2304]{3,2,1,0:T(8,128)(2,1)S(1)}, bf16[2,1,48,2304]{3,2,1,0:T(8,128)(2,1)S(1)}, u32[]{:S(2)}, u32[]{:S(2)}) collective-permute-start(bf16[2,1,48,2304]{3,2,1,0:T(8,128)(2,1)S(1)} %dynamic-slice_convert_fusion.1), channel_id=1, source_target_pairs={{0,8},{8,0},{16,24},{24,16},{1,9},{9,1},{17,25},{25,17},{2,10},{10... | collective-permute-start | bytes 1327112 | tf_op jit(solution)/shard_map/ppermute | solution.py:922
  373.2 37.6 %collective-permute-start.20 = (bf16[768,512]{1,0:T(8,128)(2,1)S(1)}, bf16[768,512]{1,0:T(8,128)(2,1)S(1)}, u32[]{:S(2)}, u32[]{:S(2)}) collective-permute-start(bf16[768,512]{1,0:T(8,128)(2,1)S(1)} %get-tuple-element.255), channel_id=1, source_target_pairs={{0,8},{8,0},{16,24},{24,16},{1,9},{9,1},{17,25},{25,17},{2,10},{10... | collective-permute-start | bytes 2359304 | tf_op jit(solution)/shard_map/ppermute | solution.py:922
  377.2 33.6 %collective-permute-start.21 = (bf16[768,512]{1,0:T(8,128)(2,1)S(1)}, bf16[768,512]{1,0:T(8,128)(2,1)S(1)}, u32[]{:S(2)}, u32[]{:S(2)}) collective-permute-start(bf16[768,512]{1,0:T(8,128)(2,1)S(1)} %get-tuple-element.252), channel_id=1, source_target_pairs={{0,16},{8,24},{16,0},{24,8},{1,17},{9,25},{17,1},{25,9},{2,18},{10... | collective-permute-start | bytes 2359304 | tf_op jit(solution)/shard_map/ppermute | solution.py:922
  378.7 28.5 %collective-permute-start.22 = (bf16[1,2,48,2304]{3,2,1,0:T(8,128)(2,1)S(1)}, bf16[1,2,48,2304]{3,2,1,0:T(8,128)(2,1)S(1)}, u32[]{:S(2)}, u32[]{:S(2)}) collective-permute-start(bf16[1,2,48,2304]{3,2,1,0:T(8,128)(2,1)S(1)} %dynamic-slice_convert_fusion), channel_id=1, source_target_pairs={{0,16},{8,24},{16,0},{24,8},{1,17},{9,25},{17,1},{25,9},{2,18},{10... | collective-permute-start | bytes 1327112 | tf_op jit(solution)/shard_map/ppermute | solution.py:922
  380.9 32.4 %copy-start.34 = (f32[2,1,48,2304]{3,2,1,0:T(8,128)}, f32[2,1,48,2304]{3,2,1,0:T(8,128)S(1)}, u32[]{:S(2)}) copy-start(f32[2,1,48,2304]{3,2,1,0:T(8,128)S(1)} %convert_add_fusion.1) | copy-start | bytes 2654212
  381.0 29.9 %collective-permute-start.19 = (bf16[1,1,48,2304]{3,2,1,0:T(8,128)(2,1)S(1)}, bf16[1,1,48,2304]{3,2,1,0:T(8,128)(2,1)S(1)}, u32[]{:S(2)}, u32[]{:S(2)}) collective-permute-start(bf16[1,1,48,2304]{3,2,1,0:T(8,128)(2,1)S(1)} %dynamic-slice_convert_fusion.3), channel_id=1, source_target_pairs={{0,16},{8,24},{16,0},{24,8},{1,17},{9,25},{17,1},{25,9},{2,18},{10... | collective-permute-start | bytes 663560 | tf_op jit(solution)/shard_map/ppermute | solution.py:922
  407.3 6.0 %collective-permute-start.23 = (bf16[1,1,48,2304]{3,2,1,0:T(8,128)(2,1)S(1)}, bf16[1,1,48,2304]{3,2,1,0:T(8,128)(2,1)S(1)}, u32[]{:S(2)}, u32[]{:S(2)}) collective-permute-start(bf16[1,1,48,2304]{3,2,1,0:T(8,128)(2,1)S(1)} %dynamic-slice_convert_fusion.2), channel_id=1, source_target_pairs={{0,8},{8,0},{16,24},{24,16},{1,9},{9,1},{17,25},{25,17},{2,10},{10... | collective-permute-start | bytes 663560 | tf_op jit(solution)/shard_map/ppermute | solution.py:922
  420.2 8.8 %collective-permute-start.26 = (bf16[2,48,384]{2,1,0:T(8,128)(2,1)S(1)}, bf16[2,48,384]{2,1,0:T(8,128)(2,1)S(1)}, u32[]{:S(2)}, u32[]{:S(2)}) collective-permute-start(bf16[2,48,384]{2,1,0:T(8,128)(2,1)S(1)} %get-tuple-element.285), channel_id=1, source_target_pairs={{0,2},{1,3},{2,4},{3,5},{4,6},{5,7},{6,0},{7,1},{8,10},{9,11},{10,... | collective-permute-start | bytes 221192 | tf_op jit(solution)/shard_map/ppermute | solution.py:1102
  420.7 10.8 %collective-permute-start.25 = (bf16[2,48,384]{2,1,0:T(8,128)(2,1)S(1)}, bf16[2,48,384]{2,1,0:T(8,128)(2,1)S(1)}, u32[]{:S(2)}, u32[]{:S(2)}) collective-permute-start(bf16[2,48,384]{2,1,0:T(8,128)(2,1)S(1)} %get-tuple-element.286), channel_id=1, source_target_pairs={{0,4},{1,5},{2,6},{3,7},{4,0},{5,1},{6,2},{7,3},{8,12},{9,13},{10,... | collective-permute-start | bytes 221192 | tf_op jit(solution)/shard_map/ppermute | solution.py:1102
  421.8 9.6 %collective-permute-start.24 = (bf16[2,48,384]{2,1,0:T(8,128)(2,1)S(1)}, bf16[2,48,384]{2,1,0:T(8,128)(2,1)S(1)}, u32[]{:S(2)}, u32[]{:S(2)}) collective-permute-start(bf16[2,48,384]{2,1,0:T(8,128)(2,1)S(1)} %get-tuple-element.287), channel_id=1, source_target_pairs={{0,6},{1,7},{2,0},{3,1},{4,2},{5,3},{6,4},{7,5},{8,14},{9,15},{10,... | collective-permute-start | bytes 221192 | tf_op jit(solution)/shard_map/ppermute | solution.py:1102
  431.6 4.4 collective-permute-start.27
  431.9 20.0 %collective-permute-start.28 = (bf16[768,512]{1,0:T(8,128)(2,1)S(1)}, bf16[768,512]{1,0:T(8,128)(2,1)S(1)}, u32[]{:S(2)}, u32[]{:S(2)}) collective-permute-start(bf16[768,512]{1,0:T(8,128)(2,1)S(1)} %copy-done.41), channel_id=1, source_target_pairs={{0,8},{8,0},{16,24},{24,16},{1,9},{9,1},{17,25},{25,17},{2,10},{10... | collective-permute-start | bytes 2359304 | tf_op jit(solution)/shard_map/ppermute | solution.py:922
  432.5 19.7 %collective-permute-start.29 = (bf16[768,512]{1,0:T(8,128)(2,1)S(1)}, bf16[768,512]{1,0:T(8,128)(2,1)S(1)}, u32[]{:S(2)}, u32[]{:S(2)}) collective-permute-start(bf16[768,512]{1,0:T(8,128)(2,1)S(1)} %copy-done.42), channel_id=1, source_target_pairs={{0,16},{8,24},{16,0},{24,8},{1,17},{9,25},{17,1},{25,9},{2,18},{10... | collective-permute-start | bytes 2359304 | tf_op jit(solution)/shard_map/ppermute | solution.py:922
  436.0 17.9 %copy-start.39 = (bf16[768,512]{1,0:T(8,128)(2,1)S(1)}, bf16[768,512]{1,0:T(8,128)(2,1)}, u32[]{:S(2)}) copy-start(bf16[768,512]{1,0:T(8,128)(2,1)} %get-tuple-element.145) | copy-start | bytes 2359300
  436.0 19.3 %copy-start.40 = (bf16[768,512]{1,0:T(8,128)(2,1)S(1)}, bf16[768,512]{1,0:T(8,128)(2,1)}, u32[]{:S(2)}) copy-start(bf16[768,512]{1,0:T(8,128)(2,1)} %get-tuple-element.146) | copy-start | bytes 2359300
  452.2 8.4 %collective-permute-start.30 = (bf16[1,1,48,2304]{3,2,1,0:T(8,128)(2,1)S(1)}, bf16[1,1,48,2304]{3,2,1,0:T(8,128)(2,1)S(1)}, u32[]{:S(2)}, u32[]{:S(2)}) collective-permute-start(bf16[1,1,48,2304]{3,2,1,0:T(8,128)(2,1)S(1)} %maximum_bitcast_fusion), channel_id=1, source_target_pairs={{0,16},{8,24},{16,0},{24,8},{1,17},{9,25},{17,1},{25,9},{2,18},{10... | collective-permute-start | bytes 663560 | tf_op jit(solution)/shard_map/ppermute | solution.py:922
  453.8 33.3 %collective-permute-start.32 = (bf16[768,512]{1,0:T(8,128)(2,1)S(1)}, bf16[768,512]{1,0:T(8,128)(2,1)S(1)}, u32[]{:S(2)}, u32[]{:S(2)}) collective-permute-start(bf16[768,512]{1,0:T(8,128)(2,1)S(1)} %copy-done.39), channel_id=1, source_target_pairs={{0,8},{8,0},{16,24},{24,16},{1,9},{9,1},{17,25},{25,17},{2,10},{10... | collective-permute-start | bytes 2359304 | tf_op jit(solution)/shard_map/ppermute | solution.py:922
  455.3 24.4 %copy-start.51 = (s32[1,128]{1,0:T(1,128)S(1)}, s32[1,128]{1,0:T(1,128)}, u32[]{:S(2)}) copy-start(s32[1,128]{1,0:T(1,128)} %param.16) | copy-start | bytes 1540
  455.3 31.8 %collective-permute-start.33 = (bf16[768,512]{1,0:T(8,128)(2,1)S(1)}, bf16[768,512]{1,0:T(8,128)(2,1)S(1)}, u32[]{:S(2)}, u32[]{:S(2)}) collective-permute-start(bf16[768,512]{1,0:T(8,128)(2,1)S(1)} %copy-done.40), channel_id=1, source_target_pairs={{0,16},{8,24},{16,0},{24,8},{1,17},{9,25},{17,1},{25,9},{2,18},{10... | collective-permute-start | bytes 2359304 | tf_op jit(solution)/shard_map/ppermute | solution.py:922
  455.8 23.3 %collective-permute-start.34 = (bf16[1,1,48,2304]{3,2,1,0:T(8,128)(2,1)S(1)}, bf16[1,1,48,2304]{3,2,1,0:T(8,128)(2,1)S(1)}, u32[]{:S(2)}, u32[]{:S(2)}) collective-permute-start(bf16[1,1,48,2304]{3,2,1,0:T(8,128)(2,1)S(1)} %maximum_bitcast_fusion.1), channel_id=1, source_target_pairs={{0,8},{8,0},{16,24},{24,16},{1,9},{9,1},{17,25},{25,17},{2,10},{10... | collective-permute-start | bytes 663560 | tf_op jit(solution)/shard_map/ppermute | solution.py:922
  460.7 29.9 %collective-permute-start.31 = (bf16[2,1,48,2304]{3,2,1,0:T(8,128)(2,1)S(1)}, bf16[2,1,48,2304]{3,2,1,0:T(8,128)(2,1)S(1)}, u32[]{:S(2)}, u32[]{:S(2)}) collective-permute-start(bf16[2,1,48,2304]{3,2,1,0:T(8,128)(2,1)S(1)} %pad_maximum_fusion.14), channel_id=1, source_target_pairs={{0,8},{8,0},{16,24},{24,16},{1,9},{9,1},{17,25},{25,17},{2,10},{10... | collective-permute-start | bytes 1327112 | tf_op jit(solution)/shard_map/ppermute | solution.py:922
  479.2 11.4 %collective-permute-start.35 = (bf16[1,2,48,2304]{3,2,1,0:T(8,128)(2,1)S(1)}, bf16[1,2,48,2304]{3,2,1,0:T(8,128)(2,1)S(1)}, u32[]{:S(2)}, u32[]{:S(2)}) collective-permute-start(bf16[1,2,48,2304]{3,2,1,0:T(8,128)(2,1)S(1)} %pad_maximum_fusion.15), channel_id=1, source_target_pairs={{0,16},{8,24},{16,0},{24,8},{1,17},{9,25},{17,1},{25,9},{2,18},{10... | collective-permute-start | bytes 1327112 | tf_op jit(solution)/shard_map/ppermute | solution.py:922
  (46 other events, 219.0 us)
Sparse Core Ops, SparseCore 0:
  11.5 59.9 all-gather.10
  73.1 37.1 all-gather.6
  112.0 45.9 all-gather.12
  210.7 41.2 reduce-scatter.2
  326.6 36.4 all-gather.8
  365.2 73.4 reduce-scatter.4

commit v6 on v5

--- a/solution.py
+++ b/solution.py
@@ -101,6 +101,7 @@
     key_ref,
     value_ref,
     mixed_ref,
+    packed_ref,
     log_ref,
     cosine_ref,
     sine_ref,
@@ -174,7 +175,9 @@
         ),
     )
     total = jnp.sum(total, -1, keepdims=True)
-    mixed_ref[...] = side_heads((mixed / total).astype(jnp.bfloat16))
+    mixed = side_heads((mixed / total).astype(jnp.bfloat16))
+    mixed_ref[...] = mixed
+    packed_ref[...] = jnp.concatenate([mixed[: block // 2], mixed[block // 2 :]], 1)
     log_ref[...] = (top + jnp.log(total)).reshape(HEAD_GROUP, block, 1)
 
 
@@ -196,6 +199,7 @@
             shaped((tokens, HEAD_SIZE), jnp.bfloat16),
             shaped((tokens, HEAD_SIZE), jnp.bfloat16),
             shaped((tokens, query_width), jnp.bfloat16),
+            shaped((tokens // 2, 2 * query_width), jnp.bfloat16),
             shaped((HEAD_GROUP, tokens, 1), jnp.float32),
             shaped((tokens, HEAD_SIZE), jnp.float32),
             shaped((tokens, HEAD_SIZE), jnp.float32),
@@ -215,6 +219,7 @@
             resident(tokens, HEAD_SIZE),
             resident(tokens, HEAD_SIZE),
             rows(query_width),
+            pl.BlockSpec((block // 2, 2 * query_width), lambda i: (i, 0)),
             pl.BlockSpec((HEAD_GROUP, block, 1), lambda i: (0, i, 0)),
             rows(HEAD_SIZE),
             rows(HEAD_SIZE),
@@ -298,11 +303,15 @@
 
     @pl.when(step == pl.num_programs(0) - 1)
     def _():
-        grad_key = grad_key_ref[...] * score_scale
-        grad_key = grad_key * key_cosine_ref[...] + turn_back(grad_key * key_sine_ref[...])
-        grad_pair_ref[...] = jnp.concatenate([grad_key, grad_value_ref[...]], 1).astype(
-            jnp.bfloat16
-        )
+        @pl.loop(0, pl.num_programs(0))
+        def _(index):
+            there = pl.ds(pl.multiple_of(index * block, block), block)
+            grad_key = grad_key_ref[there, :] * score_scale
+            turned = turn_back(grad_key * key_sine_ref[there, :])
+            grad_key = grad_key * key_cosine_ref[there, :] + turned
+            grad_pair_ref[there, :] = jnp.concatenate(
+                [grad_key, grad_value_ref[there, :]], 1
+            ).astype(jnp.bfloat16)
 
 
 def attend_back(query, grad, log_total, cosine, sine, gathered, segments, key, value, own):
@@ -354,13 +363,34 @@
     middle_ref,
     normed_ref,
     gates_ref,
+    mixed_low_ref,
+    mixed_high_ref,
 ):
     groups = mixed_ref.shape[0]
-    mixed = jnp.concatenate([mixed_ref[g] for g in range(groups)], 1)
+    width = mixed_ref.shape[2] // 2
+    mixed = jnp.concatenate(
+        [
+            jnp.concatenate([mixed_ref[g, :, side : side + width] for g in range(groups)], 1)
+            for side in (0, width)
+        ],
+        0,
+    )
     half = low_ref.shape[0]
-    middle = dot(mixed[:, :half], low_ref[...]) + dot(mixed[:, half:], high_ref[...])
-    middle = flat(hidden_ref).astype(jnp.float32) + middle
-    middle_ref[...] = middle
+    mixed_low_ref[...] = mixed[:, :half]
+    mixed_high_ref[...] = mixed[:, half:]
+    size = 512
+
+    @pl.loop(0, middle_ref.shape[1] // size)
+    def _(index):
+        part = pl.ds(pl.multiple_of(index * size, size), size)
+        hidden = hidden_ref[:, :, part].reshape(-1, size).astype(jnp.float32)
+        middle_ref[:, part] = (
+            hidden
+            + dot(mixed_low_ref[...], low_ref[:, part])
+            + dot(mixed_high_ref[...], high_ref[:, part])
+        )
+
+    middle = middle_ref[...]
     scale = lax.rsqrt(jnp.mean(middle * middle, -1, keepdims=True) + EPS)
     normed = (middle * scale * gain_ref[...]).astype(jnp.bfloat16)
     normed_ref[...] = normed
@@ -377,7 +407,8 @@
 
 
 def middle_rows(mixed, weights, gathered, gain, router, own, block):
-    groups, tokens, width = mixed.shape
+    groups, _, width = mixed.shape
+    tokens = gathered.shape[0] * own
     features = gain.shape[0]
     experts = router.shape[1]
     rows = lambda columns: pl.BlockSpec((block, columns), lambda i: (i, 0))
@@ -390,7 +421,7 @@
         ),
         grid=(tokens // block,),
         in_specs=[
-            pl.BlockSpec((groups, block, width), lambda i: (0, i, 0)),
+            pl.BlockSpec((groups, block // 2, width), lambda i: (0, i, 0)),
             whole_block(*weights[0].shape),
             whole_block(*weights[1].shape),
             *token_rows(block, own, features),
@@ -398,9 +429,10 @@
             whole_block(features, experts),
         ],
         out_specs=[rows(features), rows(features), rows(experts)],
+        scratch_shapes=[pltpu.VMEM((block, weights[0].shape[0]), jnp.bfloat16)] * 2,
         compiler_params=pltpu.CompilerParams(vmem_limit_bytes=48 << 20),
         cost_estimate=pl.CostEstimate(
-            flops=2 * tokens * features * groups * width,
+            flops=tokens * features * groups * width,
             bytes_accessed=12 * tokens * features,
             transcendentals=0,
         ),
@@ -647,6 +679,7 @@
 
 
 def turn_kernel(
+    place_ref,
     sum_ref,
     gates_ref,
     router_ref,
@@ -680,31 +713,55 @@
     branch = grad_middle.astype(jnp.bfloat16)
     branch_ref[...] = branch
     for half, weight_ref in enumerate((low_ref, high_ref)):
-        mixed = dot(branch, weight_ref[...], COLUMNS).astype(jnp.bfloat16)
-        for g in range(groups // 2):
-            mixed_ref[half * (groups // 2) + g] = mixed[:, g * width : (g + 1) * width]
-
-
-def turn_rows(sums, gates, router, gain, middle, live, weights):
-    own, features = middle.shape
+
+        @pl.loop(0, groups // 2)
+        def _(g):
+            part = weight_ref[pl.ds(pl.multiple_of(g * width, width), width), :]
+            mixed_ref[half * (groups // 2) + g] = dot(branch_ref[...], part, COLUMNS).astype(
+                jnp.bfloat16
+            )
+
+
+def turn_rows(place, sums, gates, router, gain, middle, live, weights):
+    own, features = sums.shape[0], middle.shape[1]
     experts = gates.shape[1]
     groups = KEY_VALUE_HEADS
     shaped = jax.ShapeDtypeStruct
+    rows = lambda width: pl.BlockSpec((own, width), lambda i, p: (p[1], 0))
+    resident = lambda *shape: pl.BlockSpec(shape, lambda i, p: (0,) * len(shape))
+    outs = (
+        shaped((own, features), jnp.float32),
+        shaped((own, features), jnp.bfloat16),
+        shaped((groups, own, features // groups), jnp.bfloat16),
+        shaped((own, experts), jnp.bfloat16),
+        shaped((1, features), jnp.float32),
+    )
     return pl.pallas_call(
         turn_kernel,
-        out_shape=(
-            shaped((own, features), jnp.float32),
-            shaped((own, features), jnp.bfloat16),
-            shaped((groups, own, features // groups), jnp.bfloat16),
-            shaped((own, experts), jnp.bfloat16),
-            shaped((1, features), jnp.float32),
+        out_shape=outs,
+        grid_spec=pltpu.PrefetchScalarGridSpec(
+            num_scalar_prefetch=1,
+            grid=(1,),
+            in_specs=[
+                whole_block(*sums.shape),
+                rows(experts),
+                whole_block(*router.shape),
+                whole_block(1, features),
+                rows(features),
+                rows(features),
+                whole_block(*weights[0].shape),
+                whole_block(*weights[1].shape),
+            ],
+            out_specs=[resident(*out.shape) for out in outs],
         ),
         compiler_params=pltpu.CompilerParams(vmem_limit_bytes=58 << 20),
         cost_estimate=pl.CostEstimate(flops=0, bytes_accessed=own, transcendentals=0),
-    )(sums, gates, router, gain[None, :], middle, live, *weights)
+    )(place, sums, gates, router, gain[None, :], middle, live, *weights)
 
 
 def close_kernel(
+    reps,
+    place_ref,
     query_ref,
     pair_ref,
     weight_ref,
@@ -714,19 +771,22 @@
     normed_own_ref,
     logits_ref,
     rows_ref,
+    mixed_ref,
+    branch_ref,
     grad_ref,
-    head_ref,
+    kept_one_ref,
+    kept_two_ref,
+    sent_one_ref,
+    sent_two_ref,
     product_ref,
     gain_ref,
+    out_ref,
+    head_ref,
 ):
     step = pl.program_id(0)
-    width = query_ref.shape[1]
-    both = width + pair_ref.shape[1]
-    query = query_ref[...]
-    pair = pair_ref[...]
-    grad = dot(query, weight_ref[:, :width], COLUMNS) + dot(
-        pair, weight_ref[:, width:both], COLUMNS
-    )
+    both = query_ref.shape[1] + pair_ref.shape[1]
+    heads = jnp.concatenate([query_ref[...], pair_ref[...]], 1)
+    grad = dot(heads, weight_ref[:, :both], COLUMNS)
     grad_ref[:, : grad.shape[1]] = grad.astype(jnp.bfloat16)
     grad_ref[:, grad.shape[1] :] = rows_ref[...]
     hidden = flat(hidden_ref).astype(jnp.float32)
@@ -737,73 +797,124 @@
     def _():
         gain_ref[...] = jnp.zeros_like(gain_ref)
         product_ref[...] = jnp.zeros_like(product_ref)
+        out_ref[...] = jnp.zeros_like(out_ref)
 
     gain_ref[...] += jnp.sum(grad * (hidden * scale), 0, keepdims=True)
-    product_ref[:, :width] += dot(normed, query, ROWS)
-    product_ref[:, width:] += dot(normed, pair, ROWS)
+    product_ref[...] += dot(normed, heads, ROWS)
+    out_ref[...] += dot(mixed_ref[...], branch_ref[...], ROWS)
 
     @pl.when(step == pl.num_programs(0) - 1)
     def _():
         features = product_ref.shape[0]
-        rows = head_ref.shape[0]
+        rows = out_ref.shape[0]
+        share = rows // reps
         experts = logits_ref.shape[1]
-        side = head_ref.shape[1] // (features // rows)
+        line = kept_one_ref.shape[1]
+        count = features // rows
+        side = (line - features // 2) // (count // 2)
         gains = jnp.concatenate(
             [gain_ref[...], gain_two_ref[...], jnp.zeros((6, features), jnp.float32)], 0
         )
         gains = jnp.transpose(gains)
         router = dot(normed_own_ref[...], logits_ref[...], ROWS)
-        for c in range(features // rows):
-            part = slice(c * rows, (c + 1) * rows)
-            rest = jnp.zeros((rows, side - both - 8 - experts), jnp.float32)
-            head_ref[:, c * side : (c + 1) * side] = jnp.concatenate(
-                [product_ref[part, :], gains[part], router[part], rest], 1
-            )
+        rest = jnp.zeros((rows, side - both - 8 - experts), jnp.float32)
+        for h in range(2):
+            for c in range(count // 2):
+                place = h * (count // 2) + c
+                part = slice(place * rows, (place + 1) * rows)
+                head_ref[h, :, c * side : (c + 1) * side] = jnp.concatenate(
+                    [product_ref[part, :], gains[part], router[part], rest], 1
+                )
+            half = features // 2
+            head_ref[h, :, count // 2 * side :] = out_ref[:, h * half : (h + 1) * half]
+        sides = ((0, kept_one_ref, sent_one_ref), (1, kept_two_ref, sent_two_ref))
+        for h, kept_ref, sent_ref in sides:
+            bit = 1 if h == 0 else reps // 2
+            for index in range(reps // 2):
+                base = index // bit * 2 * bit + index % bit
+                here = slice(index * share, (index + 1) * share)
+                lower = head_ref[h, base * share : (base + 1) * share, :]
+                upper = head_ref[h, (base + bit) * share : (base + bit + 1) * share, :]
+                kept_ref[here, :] = jnp.where(place_ref[2 + h] > 0, upper, lower)
+                sent_ref[here, :] = jnp.where(place_ref[2 + h] > 0, lower, upper).astype(jnp.bfloat16)
 
 
 def close_rows(
+    place,
     query,
     pair,
     weight,
     gathered,
     normed,
     gain_two_grad,
-    normed_own,
+    normed_two,
     logits,
     out_rows,
-    rows_own,
+    mixed,
+    branch,
+    reps,
     side,
     block,
 ):
     tokens, features = normed.shape
+    own = logits.shape[0]
     both = query.shape[1] + pair.shape[1]
-    rows = lambda width: pl.BlockSpec((block, width), lambda i: (i, 0))
-    resident = lambda *shape: pl.BlockSpec(shape, lambda i: (0,) * len(shape))
+    rows_own = mixed.shape[1]
+    rows = lambda width: pl.BlockSpec((block, width), lambda i, k: (i, 0))
+    resident = lambda *shape: pl.BlockSpec(shape, lambda i, k: (0,) * len(shape))
     shaped = jax.ShapeDtypeStruct
-    head = (rows_own, features // rows_own * side)
+    line = features // rows_own // 2 * side + features // 2
+    half = (rows_own // 2, line)
     return pl.pallas_call(
-        close_kernel,
-        out_shape=(shaped((tokens, 2 * features), jnp.bfloat16), shaped(head, jnp.float32)),
-        grid=(tokens // block,),
-        in_specs=[
-            rows(query.shape[1]),
-            rows(pair.shape[1]),
-            whole_block(*weight.shape),
-            token_rows(block, normed_own.shape[0], features)[0],
-            rows(features),
-            whole_block(1, features),
-            whole_block(*normed_own.shape),
-            whole_block(*logits.shape),
-            rows(features),
-        ],
-        out_specs=[rows(2 * features), resident(*head)],
-        scratch_shapes=[
-            pltpu.VMEM((features, both), jnp.float32),
-            pltpu.VMEM((1, features), jnp.float32),
-        ],
-        compiler_params=pltpu.CompilerParams(vmem_limit_bytes=48 << 20),
+        lambda *refs: close_kernel(reps, *refs),
+        name="close",
+        out_shape=(
+            shaped((tokens, 2 * features), jnp.bfloat16),
+            shaped(half, jnp.float32),
+            shaped(half, jnp.float32),
+            shaped(half, jnp.bfloat16),
+            shaped(half, jnp.bfloat16),
+        ),
+        grid_spec=pltpu.PrefetchScalarGridSpec(
+            num_scalar_prefetch=1,
+            grid=(tokens // block,),
+            in_specs=[
+                rows(query.shape[1]),
+                rows(pair.shape[1]),
+                whole_block(*weight.shape),
+                token_rows(block, own, features)[0],
+                rows(features),
+                whole_block(1, features),
+                pl.BlockSpec((own, features), lambda i, p: (p[1], 0)),
+                whole_block(*logits.shape),
+                rows(features),
+                rows(rows_own),
+                rows(features),
+            ],
+            out_specs=[rows(2 * features), *[resident(*half)] * 4],
+            scratch_shapes=[
+                pltpu.VMEM((features, both), jnp.float32),
+                pltpu.VMEM((1, features), jnp.float32),
+                pltpu.VMEM((rows_own, features), jnp.float32),
+                pltpu.VMEM((2, rows_own, line), jnp.float32),
+            ],
+        ),
+        compiler_params=pltpu.CompilerParams(vmem_limit_bytes=56 << 20),
         cost_estimate=pl.CostEstimate(flops=0, bytes_accessed=tokens, transcendentals=0),
-    )(query, pair, weight, gathered, normed, gain_two_grad, normed_own, logits, out_rows)
+    )(
+        place,
+        query,
+        pair,
+        weight,
+        gathered,
+        normed,
+        gain_two_grad,
+        normed_two,
+        logits,
+        out_rows,
+        mixed,
+        branch,
+    )
 
 
 def head_kernel(copies, side, low_ref, high_ref, query_ref, key_ref, value_ref, out_ref, small_ref):
@@ -977,10 +1088,13 @@
 
 
 class Cube:
-    def __init__(self, value, order):
-        self.value = value
+    def __init__(self, kept, sent, order, share):
+        shape = [2] * len(order)
+        shape[len(order) - order[0].bit_length()] = 1
+        self.value, sent = [array.reshape(*shape, share, -1) for array in (kept, sent)]
         self.order = order
-        self.stage = 0
+        self.flying = swap(sent, order[0])
+        self.stage = 1
 
     def axis(self, bit):
         return len(self.order) - bit.bit_length()
@@ -1137,6 +1251,7 @@
         key,
         value,
         mixed,
+        packed,
         log_total,
         cosine_table,
         sine_table,
@@ -1147,11 +1262,13 @@
     part = tokens // copies
     mixed_all = lax.all_gather(
         after(
-            lax.dynamic_slice_in_dim(mixed, copy_index * part, part, 0), cotangent, out_exchange.step()
+            lax.dynamic_slice_in_dim(packed, copy_index * part // 2, part // 2, 0),
+            cotangent,
+            out_exchange.step(),
         ),
         "ctx",
         axis=0,
-    ).reshape(groups, tokens, query_width)
+    ).reshape(groups, tokens // 2, 2 * query_width)
     w_out_halves = out_exchange.finish()
 
     middle, normed_two, gates = middle_rows(
@@ -1162,21 +1279,16 @@
     scaled_one, scaled_two, grad_gate_pre, grad_up_pre, grad_live, extra = expert_rows(
         place, normed_two, cotangent, gathered, gates, w_gate, w_up, w_down, own, block
     )
+    def mine(array):
+        return lax.dynamic_slice_in_dim(array, me * own, own, 0)
+
+    products = lambda e, dtype: expert_products(
+        normed_two, grad_gate_pre, grad_up_pre, scaled_one, scaled_two, grad_live, e, dtype
+    )
     grad_rows, out_rows = expert_sums(
         place, scaled_one, grad_gate_pre, grad_up_pre, extra, w_gate, w_up, w_down, block
     )
     grad_two_sum = lax.psum_scatter(grad_rows, "ctx", scatter_dimension=0, tiled=True)
-
-    def mine(array):
-        return lax.dynamic_slice_in_dim(array, me * own, own, 0)
-
-    middle_own, gates_own, live_own, normed_own = [
-        mine(array) for array in (middle, gates, grad_live, normed_two)
-    ]
-
-    products = lambda e, dtype: expert_products(
-        normed_two, grad_gate_pre, grad_up_pre, scaled_one, scaled_two, grad_live, e, dtype
-    )
     normed_two, grad_live = after((normed_two, grad_live), grad_rows)
     chains = [Chain(bits), Chain(bits[::-1])]
     for chain, sent in zip(chains, products(0, jnp.bfloat16)):
@@ -1186,14 +1298,16 @@
         chain.kept = kept
 
     grad_middle, grad_branch, grad_mixed, grad_logits, gain_two_grad = turn_rows(
+        place,
         after(grad_two_sum, *[(c.kept, c.flying) for c in chains]),
-        gates_own,
+        gates,
         router_all,
         gain_two,
-        middle_own,
-        live_own,
+        middle,
+        grad_live,
         w_out_halves,
     )
+    grad_branch_all = lax.all_gather(grad_branch, "ctx", axis=0, tiled=True)
 
     def deal(blocks, *others):
         blocks = blocks.reshape((chips, 2) + blocks.shape[1:])
@@ -1211,9 +1325,6 @@
     while chains[0].stage <= len(bits):
         sent = [chain.step(*sent) for chain in chains]
     grad_mixed_all = deal(jnp.repeat(grad_mixed, copies, 0), *sent).reshape(tokens, query_width)
-    grad_branch_all = lax.all_gather(
-        after(grad_branch, grad_mixed_all), "ctx", axis=0, tiled=True
-    )
     grad_query, grad_pair = attend_back(
         query,
         grad_mixed_all,
@@ -1231,17 +1342,20 @@
         counted = (places // part == copy_index)[:, None]
         grad_query = jnp.where(counted, grad_query, jnp.zeros((), jnp.bfloat16))
         grad_pair = jnp.where(counted, grad_pair, jnp.zeros((), jnp.bfloat16))
-    both_rows, head_grads = close_rows(
+    both_rows, *halves = close_rows(
+        place,
         grad_query,
         grad_pair,
         head_all,
         gathered,
         normed_one,
         gain_two_grad,
-        normed_own,
+        normed_two,
         grad_logits,
         out_rows,
-        rows_own,
+        lax.dynamic_slice_in_dim(mixed, copy_index * rows_own, rows_own, 1),
+        grad_branch_all,
+        reps,
         side_width,
         block,
     )
@@ -1249,35 +1363,22 @@
         both_rows, "ctx", scatter_dimension=0, tiled=True
     ).astype(jnp.float32)
     grad_one, out_sum = both_sums[:, :MODEL_WIDTH], both_sums[:, MODEL_WIDTH:]
-    grad_proj_out = dot(
-        lax.dynamic_slice_in_dim(mixed, copy_index * rows_own, rows_own, 1),
-        grad_branch_all,
-        ROWS,
-    )
 
     line = size // 2 * side_width
-    half = MODEL_WIDTH // 2
-    cubes = []
-    for h, order in enumerate((bits, bits[::-1])):
-        rows = jnp.concatenate(
-            [
-                head_grads[:, h * line : (h + 1) * line],
-                grad_proj_out[:, h * half : (h + 1) * half],
-            ],
-            1,
-        )
-        cubes.append(Cube(rows.reshape((2,) * len(bits) + (share, line + half)), order))
-    sent = [cube.halve() for cube in cubes]
+    cubes = [
+        Cube(halves[h], halves[2 + h], order, share)
+        for h, order in enumerate((bits, bits[::-1]))
+    ]
     while chains[0].stage < chains[0].steps:
-        sent = [chain.step(*sent) for chain in chains]
-    first = [chain.piece(0, 3) for chain in chains]
+        sent = [chain.step(*halves, *[cube.flying for cube in cubes]) for chain in chains]
     while cubes[0].stage < len(bits):
         for cube in cubes:
             cube.add(*sent)
         sent = [cube.halve() for cube in cubes]
+    first = [chain.piece(0, 3) for chain in chains]
     second = [chain.piece(1, 3, *sent) for chain in chains]
     for cube in cubes:
-        cube.add(*first)
+        cube.add()
     totals = [cube.value.astype(jnp.bfloat16) for cube in cubes]
     blocks = jnp.concatenate(
         [
@@ -1288,7 +1389,7 @@
         ],
         0,
     )
-    head_sums = deal(blocks)
+    head_sums = deal(after(blocks, *first))
     for h, cube in enumerate(cubes):
         rows = jnp.transpose(head_sums[h * (size // 2) : (h + 1) * (size // 2)], (1, 0, 2))
         rows = jnp.concatenate(
@@ -1302,12 +1403,20 @@
         into_output(keeps, side, *after((chain.sent, first[side], second[side]), *sent))
         for side, chain in enumerate(chains)
     ]
+    for cube in cubes:
+        cube.join(grad_gate, grad_up)
     while cubes[0].stage > 0:
-        for cube in cubes:
-            cube.join(*sent)
         sent = [cube.back() for cube in cubes]
+        if cubes[0].stage > 0:
+            for cube in cubes:
+                cube.join(*sent)
+    output = jnp.where((segments[0] != 0)[:, None], mine(after(middle, grad_mixed)) + out_sum, 0.0)
+    own_hidden = inputs[0].astype(jnp.float32)
+    own_scale = lax.rsqrt(jnp.mean(own_hidden * own_hidden, -1, keepdims=True) + EPS)
+    grad_in = grad_middle + norm_back(grad_one * gain_one, own_hidden * own_scale, own_scale)
     grad_down = down_output(
-        keeps, *after((chains[0].sent, third[0], chains[1].sent, third[1]), grad_gate, grad_up)
+        keeps,
+        *after((chains[0].sent, third[0], chains[1].sent, third[1]), *sent),
     )
     for cube in cubes:
         cube.join(grad_down)
@@ -1315,10 +1424,6 @@
         *[cube.value.reshape(rows_own, -1) for cube in cubes], copies, side_width
     )
     small = head_outs[4]
-    output = jnp.where((segments[0] != 0)[:, None], middle_own + out_sum, 0.0)
-    own_hidden = inputs[0].astype(jnp.float32)
-    own_scale = lax.rsqrt(jnp.mean(own_hidden * own_hidden, -1, keepdims=True) + EPS)
-    grad_in = grad_middle + norm_back(grad_one * gain_one, own_hidden * own_scale, own_scale)
     return (
         output.astype(jnp.bfloat16)[None],
         grad_in[None],

time: 507 us -> 491 us (0.968)
  waiting for transfers between devices: 204 us -> 189 us
  local copies, waits for them, and re-layouts: 35 us -> 26.3 us
  Pallas kernels: 140 us -> 146 us
    all_gather x2, waiting for transfers between devices: 19.4 us -> 5.44 us  [the longest x1 5.44 us: per_device(): lax.all_gather(after(lax.dynamic_slice_in_dim(packed, copy_index * part /...]
    ppermute x28, waiting for transfers between devices: 139 us -> 130 us  [swap(): return lax.ppermute(value, 'rep', [(i, i ^ bit) for i in range(size)])]
    ppermute x6, waiting for transfers between devices: 15.2 us -> 23.1 us  [from_chip(): lax.ppermute(value, 'ctx', [(i, (i - 2 * k) % size) for i in range(size)])]
    dynamic_slice x4 -> x0, local copies, waits for them, and re-layouts: 6.5 us -> none  [mine(): return lax.dynamic_slice_in_dim(array, me * own, own, 0)]
    unnamed x106 -> x100, local copies, waits for them, and re-layouts: 14 us -> 12.5 us
  transfers between devices with their start and end apart: 42 -> 42, of which waited for: 23 -> 24; matrix products, arithmetic and copies ran while one was open for 10% -> 10% of each run, Pallas kernels for 17% -> 18%
where the time goes in v6:
time: 491 us; the launch traced here: 490 us
  waiting for transfers between devices  189 us (38%)
  Pallas kernels  146 us (30%)
  starting transfers between devices  46.9 us (10%)
  other arithmetic  42.9 us (9%)
  local copies, waits for them, and re-layouts  26.3 us (5%)
  blocking collectives  24.5 us (5%)
  between operations  15 us (3%)
    ppermute x28, waiting for transfers between devices, swap(): return lax.ppermute(value, 'rep', [(i, i ^ bit) for i in range(size)])  130 us
    ppermute x28, starting transfers between devices, swap(): return lax.ppermute(value, 'rep', [(i, i ^ bit) for i in range(size)])  34.7 us
    pallas_call x2, Pallas kernels, expert_products(): pl.pallas_call(product_kernel, out_shape=(jax.ShapeDtypeStruct((rows, hid...  28.9 us
    all_to_all x1, blocking collectives, per_device(): lax.all_to_all(head_columns, 'ctx', split_axis=0, concat_axis=0, tiled=True)  24.5 us
    ppermute x6, waiting for transfers between devices, from_chip(): lax.ppermute(value, 'ctx', [(i, (i - 2 * k) % size) for i in range(size)])  23.1 us
    pallas_call x1, Pallas kernels, expert_rows(): pl.pallas_call(expert_kernel, out_shape=(wide, wide, wide, wide, jax.Shap...  20.5 us
    pallas_call x1, Pallas kernels, expert_sums(): pl.pallas_call(rows_kernel, out_shape=(jax.ShapeDtypeStruct((tokens, feat...  18.3 us
    all_gather x1, waiting for transfers between devices, per_device(): gathered = lax.all_gather(rows, 'ctx', axis=0)  16.5 us
  transfers between devices with their start and end apart: 42, of which 24 were waited for; matrix products, arithmetic and copies ran while one was open for 10% of the time, Pallas kernels for 18%

profile of v6, /device:TPU:0, one launch (start us, length us, event | category | flops | bytes accessed | tf_op | source)
XLA Modules:
  0.0 490.1 jit_solution(12386372477050574686)
XLA Ops:
  9.5 1.9 fusion.16
  15.4 24.5 %all_to_all.5 = bf16[8,48,384]{2,1,0:T(8,128)(2,1)S(1)} all-to-all(bf16[8,48,384]{2,1,0:T(8,128)(2,1)S(1)} %copy.103), channel_id=1, replica_groups=mesh['rep'=4,'ctx'=8] {'ctx'}, dimensions={0} | all-to-all | bytes 589824 | tf_op jit(solution)/shard_map/all_to_all | solution.py:1241
  43.0 2.8 collective-permute-done
  49.4 5.6 %collective-permute-done.3 = bf16[4,2,1,48,384]{4,3,0,2,1:T(8,128)(2,1)S(1)} collective-permute-done((bf16[4,2,1,48,384]{4,3,0,2,1:T(8,128)(2,1)S(1)}, bf16[4,2,1,48,384]{4,3,0,2,1:T(8,128)(2,1)S(1)}, u32[]{:S(2)}, u32[]{:S(2)}) %collective-permute-start.3) | collective-permute-done | bytes 294944 | tf_op jit(solution)/shard_map/ppermute | solution.py:1033
  55.0 16.5 %all-gather.11.cloned.1.call-done = bf16[1408,1664]{1,0:T(8,128)(2,1)} async-done(((bf16[176,1664]{1,0:T(8,128)(2,1)}), bf16[1408,1664]{1,0:T(8,128)(2,1)}) %all-gather.11.cloned.1.call-update) | async-done | bytes 4685840 | tf_op jit(solution)/shard_map/all_gather | solution.py:1212
  72.8 1.6 collective-permute-start.5
  77.4 15.3 %shard_map.238 = (bf16[1024,1536]{1,0:T(8,128)(2,1)}, bf16[1024,192]{1,0:T(8,128)(2,1)S(1)}, bf16[1024,64]{1,0:T(8,128)(2,1)S(1)}, bf16[1024,64]{1,0:T(8,128)(2,...) custom-call(bf16[8,176,1664]{2,1,0:T(8,128)(2,1)} %bitcast.175, ...), custom_call_target="tpu_custom_call" | custom-call | bytes 1024 | tf_op jit(solution)/shard_map/pallas_call | solution.py:194
  92.8 2.3 broadcast_select_fusion.9
  97.6 12.7 %all-gather.7.cloned.1.call-done.cotangent_ref = bf16[1024,1536]{1,0:T(8,128)(2,1)} async-done(((bf16[128,1536]{1,0:T(8,128)(2,1)}), bf16[1024,1536]{1,0:T(8,128)(2,1)}) %all-gather.7.cloned.1.call-update) | async-done | bytes 3145744 | tf_op jit(solution)/shard_map/all_gather | solution.py:1213
  115.1 23.8 %collective-permute-done.6 = bf16[4,1,2,48,1536]{4,3,0,2,1:T(8,128)(2,1)} collective-permute-done((bf16[4,1,2,48,1536]{4,3,0,2,1:T(8,128)(2,1)}, bf16[4,1,2,48,1536]{4,3,0,2,1:T(8,128)(2,1)}, u32[]{:S(2)}, u32[]{:S(2)}) %collective-permute-start.6) | collective-permute-done | bytes 1179680 | tf_op jit(solution)/shard_map/ppermute | solution.py:1033
  142.7 1.7 copy.107
  144.3 5.4 %all-gather.13.cloned.1.call-done = bf16[4096,384]{1,0:T(8,128)(2,1)} async-done(((bf16[512,384]{1,0:T(8,128)(2,1)}), bf16[4096,384]{1,0:T(8,128)(2,1)}) %all-gather.13.cloned.1.call-update) | async-done | bytes 3145744 | tf_op jit(solution)/shard_map/all_gather | solution.py:1263
  149.8 1.7 copy-done.4
  152.4 13.0 %shard_map.239 = (f32[1024,1536]{1,0:T(8,128)}, bf16[1024,1536]{1,0:T(8,128)(2,1)}, f32[1024,16]{1,0:T(8,128)S(1)}) custom-call(bf16[8,512,384]{2,1,0:T(8,128)(2,1)} %bitcast.203, bf16[768,1536]{1,0:T(8,128)(2,1)S(1)} %bitcast.167, bf16[768,1536]{1,0:T(8,128)(2,1)S(1)} %bitcast.170, bf16[8,176,1664]{2,1,0:T(8,128)(2,1)} %bitcast.178, ...), custom_call_target="tpu_custom_call" | custom-call | flops 4831838208 | bytes 18874368 | tf_op jit(solution)/shard_map/pallas_call | solution.py:415
  165.5 20.5 %shard_map.240 = (bf16[2,1024,512]{2,1,0:T(8,128)(2,1)}, bf16[2,1024,512]{2,1,0:T(8,128)(2,1)}, bf16[2,1024,512]{2,1,0:T(8,128)(2,1)}, bf16[2,1024,512]{2,1,0:T(...) custom-call(s32[4]{0:T(128)S(1)} %pad_add_fusion.place_ref.refs_0_, ...), custom_call_target="tpu_custom_call" | custom-call | flops 9663676416 | bytes 25165824 | tf_op jit(solution)/shard_map/pallas_call | solution.py:510
  186.0 18.3 %shard_map.241 = (bf16[1024,1664]{1,0:T(8,128)(2,1)}, bf16[1024,1536]{1,0:T(8,128)(2,1)}) custom-call(s32[4]{0:T(128)S(1)} %pad_add_fusion.place_ref.refs_0_, bf16[2,1024,512]{2,1,0:T(8,128)(2,1)} %get-tuple-element.98.scaled_ref.scaled_one_ref, bf16[2,1024,512]{2,1,0:T(8,128)(2,1)} %get-tuple-element.99.grad_gate_ref.gate_ref, ...), custom_call_target="tpu_custom_call" | custom-call | bytes 1024 | tf_op jit(solution)/shard_map/pallas_call | solution.py:656
  204.5 13.6 %shard_map.242 = (bf16[2304,512]{1,0:T(8,128)(2,1)}, bf16[2304,512]{1,0:T(8,128)(2,1)}) custom-call(bf16[1024,1536]{1,0:T(8,128)(2,1)} %get-tuple-element.109.normed_ref.left_ref.refs_7_, bf16[2,1024,512]{2,1,0:T(8,128)(2,1)} %get-tuple-element.99.grad_gate_ref.gate_ref, bf16[2,1024,512]{2,1,0:T(8,128)(2,1)} %get-tuple-element.100.grad_up_ref.up_ref, ...), custom_call_target="tpu_custom_call" | custom-call | bytes 1024 | tf_op jit(solution)/shard_map/pallas_call | solution.py:600
  221.2 15.2 %shard_map.243 = (f32[2304,512]{1,0:T(8,128)}, f32[2304,512]{1,0:T(8,128)}) custom-call(bf16[1024,1536]{1,0:T(8,128)(2,1)} %get-tuple-element.109.normed_ref.left_ref.refs_7_, bf16[2,1024,512]{2,1,0:T(8,128)(2,1)} %get-tuple-element.99.grad_gate_ref.gate_ref, bf16[2,1024,512]{2,1,0:T(8,128)(2,1)} %get-tuple-element.100.grad_up_ref.up_ref, ...), custom_call_target="tpu_custom_call" | custom-call | bytes 1024 | tf_op jit(solution)/shard_map/pallas_call | solution.py:600
  236.4 35.5 %collective-permute-done.8 = bf16[2304,512]{1,0:T(8,128)(2,1)} collective-permute-done((bf16[2304,512]{1,0:T(8,128)(2,1)}, bf16[2304,512]{1,0:T(8,128)(2,1)}, u32[]{:S(2)}, u32[]{:S(2)}) %collective-permute-start.8) | collective-permute-done | bytes 2359328 | tf_op jit(solution)/shard_map/ppermute | solution.py:1033
  273.0 8.1 %shard_map.244 = (f32[128,1536]{1,0:T(8,128)}, bf16[128,1536]{1,0:T(8,128)(2,1)}, bf16[8,128,192]{2,1,0:T(8,128)(2,1)}, bf16[128,16]{1,0:T(8,128)(2,1)}, f32[1,1536]{1,0:T(1,128)}) custom-call(s32[4]{0:T(128)} %copy-done.23, bf16[128,1664]{1,0:T(8,128)(2,1)} %reduce-scatter.3.cloned.1.call-done.sum_ref, f32[1024,16]{1,0:T(8,128)} %copy-done.15, ...), custom_call_target="tpu_custom_call" | custom-call | bytes 128 | tf_op jit(solution)/shard_map/pallas_call | solution.py:739
  281.2 3.6 add_convert_fusion.3
  291.2 2.5 collective-permute-start.10
  293.7 6.6 %collective-permute-done.12 = bf16[2,128,192]{2,1,0:T(8,128)(2,1)S(1)} collective-permute-done((bf16[2,128,192]{2,1,0:T(8,128)(2,1)S(1)}, bf16[2,128,192]{2,1,0:T(8,128)(2,1)S(1)}, u32[]{:S(2)}, u32[]{:S(2)}) %collective-permute-start.12) | collective-permute-done | bytes 98336 | tf_op jit(solution)/shard_map/ppermute | solution.py:1216
  300.3 8.5 %collective-permute-done.11 = bf16[2,128,192]{2,1,0:T(8,128)(2,1)S(1)} collective-permute-done((bf16[2,128,192]{2,1,0:T(8,128)(2,1)S(1)}, bf16[2,128,192]{2,1,0:T(8,128)(2,1)S(1)}, u32[]{:S(2)}, u32[]{:S(2)}) %collective-permute-start.11) | collective-permute-done | bytes 98336 | tf_op jit(solution)/shard_map/ppermute | solution.py:1216
  309.0 3.1 collective-permute-done.13
  312.1 2.7 collective-permute-done.14
  314.7 2.8 add_convert_fusion.1
  318.2 2.5 add_convert_fusion
  323.6 13.1 %shard_map.245 = (bf16[1024,192]{1,0:T(8,128)(2,1)S(1)}, bf16[1024,128]{1,0:T(8,128)(2,1)S(1)}) custom-call(bf16[1024,192]{1,0:T(8,128)(2,1)S(1)} %copy-done.14, bf16[1024,192]{1,0:T(8,128)(2,1)S(1)} %bitcast.173, f32[3,1024,1]{2,1,0:T(8,128)S(1)} %copy-done.10, f32[1024,64]{1,0:T(8,128)S(1)} %copy-done.6, f32[1024,64]{1,0:T(8,128)S(1)} %copy-done.8, ...), custom_call_target="tpu_custom_call" | custom-call | bytes 1024 | tf_op jit(solution)/shard_map/pallas_call | solution.py:323
  338.3 14.6 %close.1 = (bf16[1024,3072]{1,0:T(8,128)(2,1)}, f32[96,2304]{1,0:T(8,128)}, f32[96,2304]{1,0:T(8,128)}, bf16[96,2304]{1,0:T(8,128)(2,1)}, bf16[96,2304]{1,0:T(8,128)(2,1)}) custom-call(s32[4]{0:T(128)} %copy-done.23, bf16[1024,192]{1,0:T(8,128)(2,1)} %copy-done.16, bf16[1024,128]{1,0:T(8,128)(2,1)} %copy-done.17, ...), custom_call_target="tpu_custom_call" | custom-call | bytes 1024 | tf_op jit(solution)/shard_map/close/pallas_call | solution.py:868
  352.9 4.4 collective-permute-start.16
  357.4 10.8 %collective-permute-done.16 = bf16[2,1,48,2304]{3,2,1,0:T(8,128)(2,1)} collective-permute-done((bf16[2,1,48,2304]{3,2,1,0:T(8,128)(2,1)}, bf16[2,1,48,2304]{3,2,1,0:T(8,128)(2,1)}, u32[]{:S(2)}, u32[]{:S(2)}) %collective-permute-start.16) | collective-permute-done | bytes 442400 | tf_op jit(solution)/shard_map/ppermute | solution.py:1033
  384.4 1.8 collective-permute-start.23
  386.1 1.7 collective-permute-done.21
  391.7 1.7 reshape.318
  394.5 8.3 %collective-permute-done.22.refs_1_ = bf16[768,512]{1,0:T(8,128)(2,1)S(1)} collective-permute-done((bf16[768,512]{1,0:T(8,128)(2,1)}, bf16[768,512]{1,0:T(8,128)(2,1)S(1)}, u32[]{:S(2)}, u32[]{:S(2)}) %collective-permute-start.22) | collective-permute-done | bytes 786464 | tf_op jit(solution)/shard_map/ppermute | solution.py:1033
  402.9 4.9 %collective-permute-start.26 = (bf16[2,48,384]{2,1,0:T(8,128)(2,1)S(1)}, bf16[2,48,384]{2,1,0:T(8,128)(2,1)S(1)}, u32[]{:S(2)}, u32[]{:S(2)}) collective-permute-start(bf16[2,48,384]{2,1,0:T(8,128)(2,1)S(1)} %get-tuple-element.287), channel_id=1, source_target_pairs={{0,2},{1,3},{2,4},{3,5},{4,6},{5,7},{6,0},{7,1},{8,10},{9,11},{10,... | collective-permute-start | bytes 221192 | tf_op jit(solution)/shard_map/ppermute | solution.py:1216
  407.8 2.2 collective-permute-start.25
  410.3 4.1 collective-permute-done.26
  414.4 3.8 collective-permute-done.25
  424.6 14.8 %collective-permute-done.28.refs_2_ = bf16[768,512]{1,0:T(8,128)(2,1)S(1)} collective-permute-done((bf16[768,512]{1,0:T(8,128)(2,1)}, bf16[768,512]{1,0:T(8,128)(2,1)S(1)}, u32[]{:S(2)}, u32[]{:S(2)}) %collective-permute-start.28) | collective-permute-done | bytes 786464 | tf_op jit(solution)/shard_map/ppermute | solution.py:1033
  444.0 3.7 into_output.2
  447.6 4.9 %into_output.3 = f32[2,1536,512]{2,1,0:T(8,128)} custom-call(s32[2]{0:T(128)S(1)} %pad_add_fusion.1.k.keeps_ref, bf16[2304,512]{1,0:T(8,128)(2,1)S(1)} %copy-done.2, bf16[768,512]{1,0:T(8,128)(2,1)} %collective-permute-done.23.refs_1_, bf16[768,512]{1,0:T(8,128)(2,1)S(1)} %collective-permute-done.29.refs_2_), custom_call_target="tpu_custom_call" | custom-call | bytes 768 | tf_op jit(solution)/shard_map/into_output/pallas_call | solution.py:975
  454.3 12.4 %collective-permute-done.34 = bf16[1,1,48,2304]{3,2,1,0:T(8,128)(2,1)S(1)} collective-permute-done((bf16[1,1,48,2304]{3,2,1,0:T(8,128)(2,1)S(1)}, bf16[1,1,48,2304]{3,2,1,0:T(8,128)(2,1)S(1)}, u32[]{:S(2)}, u32[]{:S(2)}) %collective-permute-start.34) | collective-permute-done | bytes 221216 | tf_op jit(solution)/shard_map/ppermute | solution.py:1033
  467.4 3.5 shard_map.246
  470.9 3.3 collective-permute-done.31
  475.6 1.9 head_outputs.1
  480.8 2.5 fusion.10
  (264 shorter events, 84.1 us)
Async XLA Ops:
  7.2 64.3 %all-gather.11.cloned.1.call-start = ((), (), s32[]{:S(2)}) async-start(), calls=%async_computation.7 | async-start | bytes 5271552 | tf_op jit(solution)/shard_map/all_gather | solution.py:1212
  11.4 98.9 %all-gather.7.cloned.1.call-start = ((), (), s32[]{:S(2)}) async-start(), calls=%async_computation.3 | async-start | bytes 3538944 | tf_op jit(solution)/shard_map/all_gather | solution.py:1213
  12.2 137.6 %all-gather.13.cloned.1.call-start = ((), (), s32[]{:S(2)}) async-start(), calls=%async_computation.8 | async-start | bytes 3538944 | tf_op jit(solution)/shard_map/all_gather | solution.py:1263
  39.9 5.9 %collective-permute-start = (bf16[4,1,1,48,384]{4,3,0,2,1:T(8,128)(2,1)S(1)}, bf16[4,1,1,48,384]{4,3,0,2,1:T(8,128)(2,1)S(1)}, u32[]{:S(2)}, u32[]{:S(2)}) collective-permute-start(bf16[4,1,1,48,384]{4,3,0,2,1:T(8,128)(2,1)S(1)} %get-tuple-element.292), channel_id=1, source_target_pairs={{0,8},{8,0},{16,24},{24,16},{1,9},{9,1},{17,25},{25,17},{2,10},{10... | collective-permute-start | bytes 442376 | tf_op jit(solution)/shard_map/ppermute | solution.py:1033
  41.4 5.5 %collective-permute-start.2 = (bf16[4,1,1,48,384]{4,3,0,2,1:T(8,128)(2,1)S(1)}, bf16[4,1,1,48,384]{4,3,0,2,1:T(8,128)(2,1)S(1)}, u32[]{:S(2)}, u32[]{:S(2)}) collective-permute-start(bf16[4,1,1,48,384]{4,3,0,2,1:T(8,128)(2,1)S(1)} %get-tuple-element.293), channel_id=1, source_target_pairs={{0,16},{8,24},{16,0},{24,8},{1,17},{9,25},{17,1},{25,9},{2,18},{10... | collective-permute-start | bytes 442376 | tf_op jit(solution)/shard_map/ppermute | solution.py:1033
  47.1 8.0 %collective-permute-start.3 = (bf16[4,2,1,48,384]{4,3,0,2,1:T(8,128)(2,1)S(1)}, bf16[4,2,1,48,384]{4,3,0,2,1:T(8,128)(2,1)S(1)}, u32[]{:S(2)}, u32[]{:S(2)}) collective-permute-start(bf16[4,2,1,48,384]{4,3,0,2,1:T(8,128)(2,1)S(1)} %pad_maximum_fusion.15), channel_id=1, source_target_pairs={{0,8},{8,0},{16,24},{24,16},{1,9},{9,1},{17,25},{25,17},{2,10},{10... | collective-permute-start | bytes 884744 | tf_op jit(solution)/shard_map/ppermute | solution.py:1033
  47.8 28.3 %collective-permute-start.1 = (bf16[4,1,2,48,384]{4,3,0,2,1:T(8,128)(2,1)S(1)}, bf16[4,1,2,48,384]{4,3,0,2,1:T(8,128)(2,1)S(1)}, u32[]{:S(2)}, u32[]{:S(2)}) collective-permute-start(bf16[4,1,2,48,384]{4,3,0,2,1:T(8,128)(2,1)S(1)} %pad_maximum_fusion.14), channel_id=1, source_target_pairs={{0,16},{8,24},{16,0},{24,8},{1,17},{9,25},{17,1},{25,9},{2,18},{10... | collective-permute-start | bytes 884744 | tf_op jit(solution)/shard_map/ppermute | solution.py:1033
  72.8 20.0 %collective-permute-start.5 = (bf16[4,1,1,48,1536]{4,3,0,2,1:T(8,128)(2,1)S(1)}, bf16[4,1,1,48,1536]{4,3,0,2,1:T(8,128)(2,1)S(1)}, u32[]{:S(2)}, u32[]{:S(2)}) collective-permute-start(bf16[4,1,1,48,1536]{4,3,0,2,1:T(8,128)(2,1)S(1)} %get-tuple-element.242), channel_id=1, source_target_pairs={{0,16},{8,24},{16,0},{24,8},{1,17},{9,25},{17,1},{25,9},{2,18},{10... | collective-permute-start | bytes 1769480 | tf_op jit(solution)/shard_map/ppermute | solution.py:1033
  74.4 18.4 %collective-permute-start.4 = (bf16[4,1,1,48,1536]{4,3,0,2,1:T(8,128)(2,1)S(1)}, bf16[4,1,1,48,1536]{4,3,0,2,1:T(8,128)(2,1)S(1)}, u32[]{:S(2)}, u32[]{:S(2)}) collective-permute-start(bf16[4,1,1,48,1536]{4,3,0,2,1:T(8,128)(2,1)S(1)} %get-tuple-element.243), channel_id=1, source_target_pairs={{0,8},{8,0},{16,24},{24,16},{1,9},{9,1},{17,25},{25,17},{2,10},{10... | collective-permute-start | bytes 1769480 | tf_op jit(solution)/shard_map/ppermute | solution.py:1033
  110.4 162.6 %reduce-scatter.3.cloned.1.call-start = ((), (), s32[]{:S(2)}) async-start(), calls=%async_computation.4 | async-start | bytes 3833856 | tf_op jit(solution)/shard_map/reduce_scatter | solution.py:1291
  110.4 28.5 %collective-permute-start.6 = (bf16[4,1,2,48,1536]{4,3,0,2,1:T(8,128)(2,1)}, bf16[4,1,2,48,1536]{4,3,0,2,1:T(8,128)(2,1)}, u32[]{:S(2)}, u32[]{:S(2)}) collective-permute-start(bf16[4,1,2,48,1536]{4,3,0,2,1:T(8,128)(2,1)} %pad_maximum_fusion.5), channel_id=1, source_target_pairs={{0,16},{8,24},{16,0},{24,8},{1,17},{9,25},{17,1},{25,9},{2,18},{10... | collective-permute-start | bytes 3538952 | tf_op jit(solution)/shard_map/ppermute | solution.py:1033
  112.0 28.8 %collective-permute-start.7 = (bf16[4,2,1,48,1536]{4,3,0,2,1:T(8,128)(2,1)}, bf16[4,2,1,48,1536]{4,3,0,2,1:T(8,128)(2,1)S(1)}, u32[]{:S(2)}, u32[]{:S(2)}) collective-permute-start(bf16[4,2,1,48,1536]{4,3,0,2,1:T(8,128)(2,1)} %pad_maximum_fusion.6), channel_id=1, source_target_pairs={{0,8},{8,0},{16,24},{24,16},{1,9},{9,1},{17,25},{25,17},{2,10},{10... | collective-permute-start | bytes 3538952 | tf_op jit(solution)/shard_map/ppermute | solution.py:1033
  113.5 72.5 %copy-start.23 = (s32[4]{0:T(128)}, s32[4]{0:T(128)S(1)}, u32[]{:S(2)}) copy-start(s32[4]{0:T(128)S(1)} %pad_add_fusion.place_ref.refs_0_) | copy-start | bytes 52
  114.2 35.5 %copy-start.22 = (f32[1,1536]{1,0:T(1,128)}, f32[1,1536]{1,0:T(1,128)S(1)}, u32[]{:S(2)}) copy-start(f32[1,1536]{1,0:T(1,128)S(1)} %reshape.330.gain_ref) | copy-start | bytes 18436
  165.5 20.5 %copy-start.15 = (f32[1024,16]{1,0:T(8,128)}, f32[1024,16]{1,0:T(8,128)S(1)}, u32[]{:S(2)}) copy-start(f32[1024,16]{1,0:T(8,128)S(1)} %get-tuple-element.97.gates_ref) | copy-start | bytes 196612
  204.3 134.0 %all-gather.9.cloned.1.call-start = ((), (), s32[]{:S(2)}) async-start(), calls=%async_computation.5 | async-start | bytes 3538944 | tf_op jit(solution)/shard_map/all_gather | solution.py:1310
  218.1 53.7 %collective-permute-start.8 = (bf16[2304,512]{1,0:T(8,128)(2,1)}, bf16[2304,512]{1,0:T(8,128)(2,1)}, u32[]{:S(2)}, u32[]{:S(2)}) collective-permute-start(bf16[2304,512]{1,0:T(8,128)(2,1)} %get-tuple-element.107), channel_id=1, source_target_pairs={{0,8},{8,0},{16,24},{24,16},{1,9},{9,1},{17,25},{25,17},{2,10},{10... | collective-permute-start | bytes 7077896 | tf_op jit(solution)/shard_map/ppermute | solution.py:1033
  219.7 53.3 %collective-permute-start.9 = (bf16[2304,512]{1,0:T(8,128)(2,1)}, bf16[2304,512]{1,0:T(8,128)(2,1)S(1)}, u32[]{:S(2)}, u32[]{:S(2)}) collective-permute-start(bf16[2304,512]{1,0:T(8,128)(2,1)} %get-tuple-element.108), channel_id=1, source_target_pairs={{0,16},{8,24},{16,0},{24,8},{1,17},{9,25},{17,1},{25,9},{2,18},{10... | collective-permute-start | bytes 7077896 | tf_op jit(solution)/shard_map/ppermute | solution.py:1033
  281.1 198.0 %reduce-scatter.5.cloned.1.call-start = ((), (), s32[]{:S(2)}) async-start(), calls=%async_computation.6 | async-start | bytes 7077888 | tf_op jit(solution)/shard_map/reduce_scatter | solution.py:1362
  284.8 27.3 %collective-permute-start.13 = (bf16[1152,512]{1,0:T(8,128)(2,1)}, bf16[1152,512]{1,0:T(8,128)(2,1)}, u32[]{:S(2)}, u32[]{:S(2)}) collective-permute-start(bf16[1152,512]{1,0:T(8,128)(2,1)} %add_convert_fusion.3), channel_id=1, source_target_pairs={{0,16},{8,24},{16,0},{24,8},{1,17},{9,25},{17,1},{25,9},{2,18},{10... | collective-permute-start | bytes 3538952 | tf_op jit(solution)/shard_map/ppermute | solution.py:1033
  287.7 27.0 %collective-permute-start.14 = (bf16[1152,512]{1,0:T(8,128)(2,1)}, bf16[1152,512]{1,0:T(8,128)(2,1)}, u32[]{:S(2)}, u32[]{:S(2)}) collective-permute-start(bf16[1152,512]{1,0:T(8,128)(2,1)} %add_convert_fusion.2), channel_id=1, source_target_pairs={{0,8},{8,0},{16,24},{24,16},{1,9},{9,1},{17,25},{25,17},{2,10},{10... | collective-permute-start | bytes 3538952 | tf_op jit(solution)/shard_map/ppermute | solution.py:1033
  289.3 11.0 %collective-permute-start.12 = (bf16[2,128,192]{2,1,0:T(8,128)(2,1)S(1)}, bf16[2,128,192]{2,1,0:T(8,128)(2,1)S(1)}, u32[]{:S(2)}, u32[]{:S(2)}) collective-permute-start(bf16[2,128,192]{2,1,0:T(8,128)(2,1)S(1)} %get-tuple-element.271), channel_id=1, source_target_pairs={{0,2},{1,3},{2,4},{3,5},{4,6},{5,7},{6,0},{7,1},{8,10},{9,11},{10,... | collective-permute-start | bytes 294920 | tf_op jit(solution)/shard_map/ppermute | solution.py:1216
  290.1 18.8 %collective-permute-start.11 = (bf16[2,128,192]{2,1,0:T(8,128)(2,1)S(1)}, bf16[2,128,192]{2,1,0:T(8,128)(2,1)S(1)}, u32[]{:S(2)}, u32[]{:S(2)}) collective-permute-start(bf16[2,128,192]{2,1,0:T(8,128)(2,1)S(1)} %get-tuple-element.272), channel_id=1, source_target_pairs={{0,4},{1,5},{2,6},{3,7},{4,0},{5,1},{6,2},{7,3},{8,12},{9,13},{10,... | collective-permute-start | bytes 294920 | tf_op jit(solution)/shard_map/ppermute | solution.py:1216
  291.2 17.6 %collective-permute-start.10 = (bf16[2,128,192]{2,1,0:T(8,128)(2,1)S(1)}, bf16[2,128,192]{2,1,0:T(8,128)(2,1)S(1)}, u32[]{:S(2)}, u32[]{:S(2)}) collective-permute-start(bf16[2,128,192]{2,1,0:T(8,128)(2,1)S(1)} %get-tuple-element.273), channel_id=1, source_target_pairs={{0,6},{1,7},{2,0},{3,1},{4,2},{5,3},{6,4},{7,5},{8,14},{9,15},{10,... | collective-permute-start | bytes 294920 | tf_op jit(solution)/shard_map/ppermute | solution.py:1216
  317.6 39.8 %collective-permute-start.17 = (bf16[1152,512]{1,0:T(8,128)(2,1)S(1)}, bf16[1152,512]{1,0:T(8,128)(2,1)}, u32[]{:S(2)}, u32[]{:S(2)}) collective-permute-start(bf16[1152,512]{1,0:T(8,128)(2,1)S(1)} %add_convert_fusion.1), channel_id=1, source_target_pairs={{0,16},{8,24},{16,0},{24,8},{1,17},{9,25},{17,1},{25,9},{2,18},{10... | collective-permute-start | bytes 3538952 | tf_op jit(solution)/shard_map/ppermute | solution.py:1033
  320.8 2.0 collective-permute-start.15
  322.0 49.1 %collective-permute-start.19 = (bf16[1152,512]{1,0:T(8,128)(2,1)S(1)}, bf16[1152,512]{1,0:T(8,128)(2,1)S(1)}, u32[]{:S(2)}, u32[]{:S(2)}) collective-permute-start(bf16[1152,512]{1,0:T(8,128)(2,1)S(1)} %add_convert_fusion), channel_id=1, source_target_pairs={{0,8},{8,0},{16,24},{24,16},{1,9},{9,1},{17,25},{25,17},{2,10},{10... | collective-permute-start | bytes 3538952 | tf_op jit(solution)/shard_map/ppermute | solution.py:1033
  352.9 15.3 %collective-permute-start.16 = (bf16[2,1,48,2304]{3,2,1,0:T(8,128)(2,1)}, bf16[2,1,48,2304]{3,2,1,0:T(8,128)(2,1)}, u32[]{:S(2)}, u32[]{:S(2)}) collective-permute-start(bf16[2,1,48,2304]{3,2,1,0:T(8,128)(2,1)} %bitcast.205), channel_id=1, source_target_pairs={{0,8},{8,0},{16,24},{24,16},{1,9},{9,1},{17,25},{25,17},{2,10},{10... | collective-permute-start | bytes 1327112 | tf_op jit(solution)/shard_map/ppermute | solution.py:1033
  357.3 12.3 %collective-permute-start.18 = (bf16[1,2,48,2304]{3,2,1,0:T(8,128)(2,1)}, bf16[1,2,48,2304]{3,2,1,0:T(8,128)(2,1)}, u32[]{:S(2)}, u32[]{:S(2)}) collective-permute-start(bf16[1,2,48,2304]{3,2,1,0:T(8,128)(2,1)} %bitcast.204), channel_id=1, source_target_pairs={{0,16},{8,24},{16,0},{24,8},{1,17},{9,25},{17,1},{25,9},{2,18},{10... | collective-permute-start | bytes 1327112 | tf_op jit(solution)/shard_map/ppermute | solution.py:1033
  377.9 11.3 %collective-permute-start.20 = (bf16[1,1,48,2304]{3,2,1,0:T(8,128)(2,1)}, bf16[1,1,48,2304]{3,2,1,0:T(8,128)(2,1)S(1)}, u32[]{:S(2)}, u32[]{:S(2)}) collective-permute-start(bf16[1,1,48,2304]{3,2,1,0:T(8,128)(2,1)} %dynamic-slice_convert_fusion.1), channel_id=1, source_target_pairs={{0,16},{8,24},{16,0},{24,8},{1,17},{9,25},{17,1},{25,9},{2,18},{10... | collective-permute-start | bytes 663560 | tf_op jit(solution)/shard_map/ppermute | solution.py:1033
  379.4 8.4 %collective-permute-start.21 = (bf16[1,1,48,2304]{3,2,1,0:T(8,128)(2,1)S(1)}, bf16[1,1,48,2304]{3,2,1,0:T(8,128)(2,1)S(1)}, u32[]{:S(2)}, u32[]{:S(2)}) collective-permute-start(bf16[1,1,48,2304]{3,2,1,0:T(8,128)(2,1)S(1)} %dynamic-slice_convert_fusion), channel_id=1, source_target_pairs={{0,8},{8,0},{16,24},{24,16},{1,9},{9,1},{17,25},{25,17},{2,10},{10... | collective-permute-start | bytes 663560 | tf_op jit(solution)/shard_map/ppermute | solution.py:1033
  381.3 21.5 %collective-permute-start.22 = (bf16[768,512]{1,0:T(8,128)(2,1)}, bf16[768,512]{1,0:T(8,128)(2,1)S(1)}, u32[]{:S(2)}, u32[]{:S(2)}) collective-permute-start(bf16[768,512]{1,0:T(8,128)(2,1)} %get-tuple-element.259), channel_id=1, source_target_pairs={{0,8},{8,0},{16,24},{24,16},{1,9},{9,1},{17,25},{25,17},{2,10},{10... | collective-permute-start | bytes 2359304 | tf_op jit(solution)/shard_map/ppermute | solution.py:1033
  384.4 18.4 %collective-permute-start.23 = (bf16[768,512]{1,0:T(8,128)(2,1)}, bf16[768,512]{1,0:T(8,128)(2,1)}, u32[]{:S(2)}, u32[]{:S(2)}) collective-permute-start(bf16[768,512]{1,0:T(8,128)(2,1)} %get-tuple-element.256), channel_id=1, source_target_pairs={{0,16},{8,24},{16,0},{24,8},{1,17},{9,25},{17,1},{25,9},{2,18},{10... | collective-permute-start | bytes 2359304 | tf_op jit(solution)/shard_map/ppermute | solution.py:1033
  391.7 27.4 %copy-start.24 = (bf16[1,128,1536]{2,1,0:T(8,128)(2,1)S(1)}, bf16[1,128,1536]{2,1,0:T(8,128)(2,1)}, u32[]{:S(2)}) copy-start(bf16[1,128,1536]{2,1,0:T(8,128)(2,1)} %param.15) | copy-start | bytes 1179652
  402.9 11.5 %collective-permute-start.26 = (bf16[2,48,384]{2,1,0:T(8,128)(2,1)S(1)}, bf16[2,48,384]{2,1,0:T(8,128)(2,1)S(1)}, u32[]{:S(2)}, u32[]{:S(2)}) collective-permute-start(bf16[2,48,384]{2,1,0:T(8,128)(2,1)S(1)} %get-tuple-element.287), channel_id=1, source_target_pairs={{0,2},{1,3},{2,4},{3,5},{4,6},{5,7},{6,0},{7,1},{8,10},{9,11},{10,... | collective-permute-start | bytes 221192 | tf_op jit(solution)/shard_map/ppermute | solution.py:1216
  407.8 10.4 %collective-permute-start.25 = (bf16[2,48,384]{2,1,0:T(8,128)(2,1)S(1)}, bf16[2,48,384]{2,1,0:T(8,128)(2,1)S(1)}, u32[]{:S(2)}, u32[]{:S(2)}) collective-permute-start(bf16[2,48,384]{2,1,0:T(8,128)(2,1)S(1)} %get-tuple-element.288), channel_id=1, source_target_pairs={{0,4},{1,5},{2,6},{3,7},{4,0},{5,1},{6,2},{7,3},{8,12},{9,13},{10,... | collective-permute-start | bytes 221192 | tf_op jit(solution)/shard_map/ppermute | solution.py:1216
  410.0 8.2 %collective-permute-start.24 = (bf16[2,48,384]{2,1,0:T(8,128)(2,1)S(1)}, bf16[2,48,384]{2,1,0:T(8,128)(2,1)S(1)}, u32[]{:S(2)}, u32[]{:S(2)}) collective-permute-start(bf16[2,48,384]{2,1,0:T(8,128)(2,1)S(1)} %get-tuple-element.289), channel_id=1, source_target_pairs={{0,6},{1,7},{2,0},{3,1},{4,2},{5,3},{6,4},{7,5},{8,14},{9,15},{10,... | collective-permute-start | bytes 221192 | tf_op jit(solution)/shard_map/ppermute | solution.py:1216
  419.0 4.2 collective-permute-start.27
  419.3 20.2 %collective-permute-start.28 = (bf16[768,512]{1,0:T(8,128)(2,1)}, bf16[768,512]{1,0:T(8,128)(2,1)S(1)}, u32[]{:S(2)}, u32[]{:S(2)}) collective-permute-start(bf16[768,512]{1,0:T(8,128)(2,1)} %get-tuple-element.147), channel_id=1, source_target_pairs={{0,8},{8,0},{16,24},{24,16},{1,9},{9,1},{17,25},{25,17},{2,10},{10... | collective-permute-start | bytes 2359304 | tf_op jit(solution)/shard_map/ppermute | solution.py:1033
  419.9 19.9 %collective-permute-start.29 = (bf16[768,512]{1,0:T(8,128)(2,1)}, bf16[768,512]{1,0:T(8,128)(2,1)S(1)}, u32[]{:S(2)}, u32[]{:S(2)}) collective-permute-start(bf16[768,512]{1,0:T(8,128)(2,1)} %get-tuple-element.148), channel_id=1, source_target_pairs={{0,16},{8,24},{16,0},{24,8},{1,17},{9,25},{17,1},{25,9},{2,18},{10... | collective-permute-start | bytes 2359304 | tf_op jit(solution)/shard_map/ppermute | solution.py:1033
  424.3 17.1 %copy-start.40 = (bf16[768,512]{1,0:T(8,128)(2,1)S(1)}, bf16[768,512]{1,0:T(8,128)(2,1)}, u32[]{:S(2)}) copy-start(bf16[768,512]{1,0:T(8,128)(2,1)} %get-tuple-element.157) | copy-start | bytes 2359300
  424.3 18.4 %copy-start.41 = (bf16[768,512]{1,0:T(8,128)(2,1)S(1)}, bf16[768,512]{1,0:T(8,128)(2,1)}, u32[]{:S(2)}) copy-start(bf16[768,512]{1,0:T(8,128)(2,1)} %get-tuple-element.158) | copy-start | bytes 2359300
  439.8 12.8 %collective-permute-start.30 = (bf16[1,1,48,2304]{3,2,1,0:T(8,128)(2,1)S(1)}, bf16[1,1,48,2304]{3,2,1,0:T(8,128)(2,1)S(1)}, u32[]{:S(2)}, u32[]{:S(2)}) collective-permute-start(bf16[1,1,48,2304]{3,2,1,0:T(8,128)(2,1)S(1)} %maximum_bitcast_fusion), channel_id=1, source_target_pairs={{0,16},{8,24},{16,0},{24,8},{1,17},{9,25},{17,1},{25,9},{2,18},{10... | collective-permute-start | bytes 663560 | tf_op jit(solution)/shard_map/ppermute | solution.py:1033
  441.4 26.0 %collective-permute-start.32 = (bf16[768,512]{1,0:T(8,128)(2,1)S(1)}, bf16[768,512]{1,0:T(8,128)(2,1)S(1)}, u32[]{:S(2)}, u32[]{:S(2)}) collective-permute-start(bf16[768,512]{1,0:T(8,128)(2,1)S(1)} %copy-done.40), channel_id=1, source_target_pairs={{0,8},{8,0},{16,24},{24,16},{1,9},{9,1},{17,25},{25,17},{2,10},{10... | collective-permute-start | bytes 2359304 | tf_op jit(solution)/shard_map/ppermute | solution.py:1033
  442.7 24.7 %collective-permute-start.33 = (bf16[768,512]{1,0:T(8,128)(2,1)S(1)}, bf16[768,512]{1,0:T(8,128)(2,1)S(1)}, u32[]{:S(2)}, u32[]{:S(2)}) collective-permute-start(bf16[768,512]{1,0:T(8,128)(2,1)S(1)} %copy-done.41), channel_id=1, source_target_pairs={{0,16},{8,24},{16,0},{24,8},{1,17},{9,25},{17,1},{25,9},{2,18},{10... | collective-permute-start | bytes 2359304 | tf_op jit(solution)/shard_map/ppermute | solution.py:1033
  443.4 23.3 %collective-permute-start.34 = (bf16[1,1,48,2304]{3,2,1,0:T(8,128)(2,1)S(1)}, bf16[1,1,48,2304]{3,2,1,0:T(8,128)(2,1)S(1)}, u32[]{:S(2)}, u32[]{:S(2)}) collective-permute-start(bf16[1,1,48,2304]{3,2,1,0:T(8,128)(2,1)S(1)} %maximum_bitcast_fusion.1), channel_id=1, source_target_pairs={{0,8},{8,0},{16,24},{24,16},{1,9},{9,1},{17,25},{25,17},{2,10},{10... | collective-permute-start | bytes 663560 | tf_op jit(solution)/shard_map/ppermute | solution.py:1033
  452.7 21.5 %collective-permute-start.31 = (bf16[2,1,48,2304]{3,2,1,0:T(8,128)(2,1)S(1)}, bf16[2,1,48,2304]{3,2,1,0:T(8,128)(2,1)S(1)}, u32[]{:S(2)}, u32[]{:S(2)}) collective-permute-start(bf16[2,1,48,2304]{3,2,1,0:T(8,128)(2,1)S(1)} %pad_maximum_fusion.12), channel_id=1, source_target_pairs={{0,8},{8,0},{16,24},{24,16},{1,9},{9,1},{17,25},{25,17},{2,10},{10... | collective-permute-start | bytes 1327112 | tf_op jit(solution)/shard_map/ppermute | solution.py:1033
  466.8 8.4 %collective-permute-start.35 = (bf16[1,2,48,2304]{3,2,1,0:T(8,128)(2,1)S(1)}, bf16[1,2,48,2304]{3,2,1,0:T(8,128)(2,1)S(1)}, u32[]{:S(2)}, u32[]{:S(2)}) collective-permute-start(bf16[1,2,48,2304]{3,2,1,0:T(8,128)(2,1)S(1)} %pad_maximum_fusion.13), channel_id=1, source_target_pairs={{0,16},{8,24},{16,0},{24,8},{1,17},{9,25},{17,1},{25,9},{2,18},{10... | collective-permute-start | bytes 1327112 | tf_op jit(solution)/shard_map/ppermute | solution.py:1033
  (43 other events, 142.8 us)
Sparse Core Ops, SparseCore 0:
  11.5 59.9 all-gather.10
  73.1 37.1 all-gather.6
  112.6 37.1 all-gather.12
  204.4 41.4 reduce-scatter.2
  281.3 47.4 all-gather.8
  357.5 77.8 reduce-scatter.4

commit v7 on v6

--- a/solution.py
+++ b/solution.py
@@ -363,8 +363,6 @@
     middle_ref,
     normed_ref,
     gates_ref,
-    mixed_low_ref,
-    mixed_high_ref,
 ):
     groups = mixed_ref.shape[0]
     width = mixed_ref.shape[2] // 2
@@ -376,21 +374,9 @@
         0,
     )
     half = low_ref.shape[0]
-    mixed_low_ref[...] = mixed[:, :half]
-    mixed_high_ref[...] = mixed[:, half:]
-    size = 512
-
-    @pl.loop(0, middle_ref.shape[1] // size)
-    def _(index):
-        part = pl.ds(pl.multiple_of(index * size, size), size)
-        hidden = hidden_ref[:, :, part].reshape(-1, size).astype(jnp.float32)
-        middle_ref[:, part] = (
-            hidden
-            + dot(mixed_low_ref[...], low_ref[:, part])
-            + dot(mixed_high_ref[...], high_ref[:, part])
-        )
-
-    middle = middle_ref[...]
+    middle = dot(mixed[:, :half], low_ref[...]) + dot(mixed[:, half:], high_ref[...])
+    middle = flat(hidden_ref).astype(jnp.float32) + middle
+    middle_ref[...] = middle
     scale = lax.rsqrt(jnp.mean(middle * middle, -1, keepdims=True) + EPS)
     normed = (middle * scale * gain_ref[...]).astype(jnp.bfloat16)
     normed_ref[...] = normed
@@ -429,7 +415,6 @@
             whole_block(features, experts),
         ],
         out_specs=[rows(features), rows(features), rows(experts)],
-        scratch_shapes=[pltpu.VMEM((block, weights[0].shape[0]), jnp.bfloat16)] * 2,
         compiler_params=pltpu.CompilerParams(vmem_limit_bytes=48 << 20),
         cost_estimate=pl.CostEstimate(
             flops=tokens * features * groups * width,
@@ -615,20 +600,10 @@
     )(left, gate, up, scaled_one, scaled_two, live, live)
 
 
-def rows_kernel(
-    place_ref,
-    scaled_ref,
-    grad_gate_ref,
-    grad_up_ref,
-    extra_ref,
-    gate_weight_ref,
-    up_weight_ref,
-    down_weight_ref,
-    grad_ref,
-    out_ref,
+def gradient_kernel(
+    place_ref, grad_gate_ref, grad_up_ref, extra_ref, gate_weight_ref, up_weight_ref, grad_ref
 ):
-    experts_own = scaled_ref.shape[0]
-    features = out_ref.shape[1]
+    experts_own, features = gate_weight_ref.shape[:2]
     one = [slot_of(e, place_ref[2], experts_own) for e in range(experts_own)]
     two = [slot_of(e, place_ref[3], experts_own) for e in range(experts_own)]
     size = 512
@@ -637,45 +612,71 @@
     def _(index):
         part = pl.ds(pl.multiple_of(index * size, size), size)
         grad = 0.0
-        out = 0.0
         for e in range(experts_own):
             grad = grad + dot(grad_gate_ref[one[e]], gate_weight_ref[e, part, :], COLUMNS)
             grad = grad + dot(grad_up_ref[two[e]], up_weight_ref[e, part, :], COLUMNS)
-            out = out + dot(scaled_ref[one[e]], down_weight_ref[e, :, part])
         grad_ref[:, part] = grad.astype(jnp.bfloat16)
-        out_ref[:, part] = out.astype(jnp.bfloat16)
 
     grad_ref[:, features:] = extra_ref[...]
 
 
-def expert_sums(place, scaled, grad_gate_pre, grad_up_pre, extra, w_gate, w_up, w_down, block):
-    experts_own, tokens, hidden = scaled.shape
+def gradient_rows(place, grad_gate_pre, grad_up_pre, extra, w_gate, w_up, block):
+    experts_own, tokens, hidden = grad_gate_pre.shape
     features = w_gate.shape[1]
     rows = lambda columns: pl.BlockSpec((block, columns), lambda i, p: (i, 0))
     spread = pl.BlockSpec((experts_own, block, hidden), lambda i, p: (0, i, 0))
     return pl.pallas_call(
-        rows_kernel,
-        out_shape=(
-            jax.ShapeDtypeStruct((tokens, features + extra.shape[1]), jnp.bfloat16),
-            jax.ShapeDtypeStruct((tokens, features), jnp.bfloat16),
-        ),
+        gradient_kernel,
+        out_shape=jax.ShapeDtypeStruct((tokens, features + extra.shape[1]), jnp.bfloat16),
         grid_spec=pltpu.PrefetchScalarGridSpec(
             num_scalar_prefetch=1,
             grid=(tokens // block,),
             in_specs=[
                 spread,
                 spread,
-                spread,
                 rows(extra.shape[1]),
                 whole_block(*w_gate.shape),
                 whole_block(*w_up.shape),
+            ],
+            out_specs=rows(features + extra.shape[1]),
+        ),
+        compiler_params=pltpu.CompilerParams(vmem_limit_bytes=52 << 20),
+        cost_estimate=pl.CostEstimate(flops=0, bytes_accessed=tokens, transcendentals=0),
+    )(place, grad_gate_pre, grad_up_pre, extra, w_gate, w_up)
+
+
+def output_kernel(place_ref, scaled_ref, down_weight_ref, out_ref):
+    experts_own, _, features = down_weight_ref.shape
+    size = 512
+
+    @pl.loop(0, features // size)
+    def _(index):
+        part = pl.ds(pl.multiple_of(index * size, size), size)
+        out = 0.0
+        for e in range(experts_own):
+            slot = slot_of(e, place_ref[2], experts_own)
+            out = out + dot(scaled_ref[slot], down_weight_ref[e, :, part])
+        out_ref[:, part] = out.astype(jnp.bfloat16)
+
+
+def output_rows(place, scaled, w_down, block):
+    experts_own, tokens, hidden = scaled.shape
+    features = w_down.shape[2]
+    return pl.pallas_call(
+        output_kernel,
+        out_shape=jax.ShapeDtypeStruct((tokens, features), jnp.bfloat16),
+        grid_spec=pltpu.PrefetchScalarGridSpec(
+            num_scalar_prefetch=1,
+            grid=(tokens // block,),
+            in_specs=[
+                pl.BlockSpec((experts_own, block, hidden), lambda i, p: (0, i, 0)),
                 whole_block(*w_down.shape),
             ],
-            out_specs=[rows(features + extra.shape[1]), rows(features)],
+            out_specs=pl.BlockSpec((block, features), lambda i, p: (i, 0)),
         ),
         compiler_params=pltpu.CompilerParams(vmem_limit_bytes=52 << 20),
         cost_estimate=pl.CostEstimate(flops=0, bytes_accessed=tokens, transcendentals=0),
-    )(place, scaled, grad_gate_pre, grad_up_pre, extra, w_gate, w_up, w_down)
+    )(place, scaled, w_down)
 
 
 def turn_kernel(
@@ -713,13 +714,9 @@
     branch = grad_middle.astype(jnp.bfloat16)
     branch_ref[...] = branch
     for half, weight_ref in enumerate((low_ref, high_ref)):
-
-        @pl.loop(0, groups // 2)
-        def _(g):
-            part = weight_ref[pl.ds(pl.multiple_of(g * width, width), width), :]
-            mixed_ref[half * (groups // 2) + g] = dot(branch_ref[...], part, COLUMNS).astype(
-                jnp.bfloat16
-            )
+        mixed = dot(branch, weight_ref[...], COLUMNS).astype(jnp.bfloat16)
+        for g in range(groups // 2):
+            mixed_ref[half * (groups // 2) + g] = mixed[:, g * width : (g + 1) * width]
 
 
 def turn_rows(place, sums, gates, router, gain, middle, live, weights):
@@ -1037,18 +1034,6 @@
     return (lax.axis_index("rep") & bit) != 0
 
 
-def halve(value, came, bit):
-    half = value.shape[0] // 2
-    keep = jnp.where(has(bit), half, 0)
-    part = lambda array, start: lax.dynamic_slice_in_dim(array, start, half, 0).astype(jnp.float32)
-    kept = part(value, keep)
-    sent = part(value, half - keep)
-    if came is not None:
-        kept = kept + part(came, keep)
-        sent = sent + part(came, half - keep)
-    return kept, sent.astype(jnp.bfloat16)
-
-
 def join(value, came, bit, axis):
     upper = has(bit)
     return jnp.concatenate(
@@ -1070,12 +1055,8 @@
             self.flying = swap(sent, bit)
 
     def step(self, *others):
-        bits = len(self.order)
         came = after(self.flying, *others)
-        if self.stage < bits:
-            self.kept, sent = halve(self.kept, came, self.order[self.stage])
-            self.send(sent)
-        elif self.stage == bits:
+        if self.stage == len(self.order):
             self.send((self.kept + came.astype(jnp.float32)).astype(jnp.bfloat16))
         else:
             self.send(join(self.sent, came, self.order[self.steps - self.stage], 0))
@@ -1085,6 +1066,51 @@
         rows = self.sent.shape[0] // count
         part = after(self.sent[number * rows : (number + 1) * rows], *others)
         return swap(part, self.order[0])
+
+
+def halve_kernel(keeps_ref, *refs):
+    for chain in range(2):
+        kept_ref, other_ref, came_ref, rest_ref = refs[4 * chain : 4 * chain + 4]
+        out_ref, sent_ref = refs[8 + 2 * chain : 10 + 2 * chain]
+        out_ref[...] = kept_ref[...] + came_ref[...].astype(jnp.float32)
+        sent = other_ref[...] + rest_ref[...].astype(jnp.float32)
+        sent_ref[...] = sent.astype(jnp.bfloat16)
+
+
+def halve_chains(chains, *others):
+    order = [chain.order[chain.stage] for chain in chains]
+    keeps = jnp.stack([has(bit) for bit in order]).astype(jnp.int32)
+    rows, hidden = chains[0].kept.shape
+    count = 4
+    part = rows // 2 // count
+    operands, specs = [], []
+    for c, chain in enumerate(chains):
+        came = after(chain.flying, *others)
+        for array in (chain.kept, came):
+            for flip in range(2):
+                operands.append(array)
+                specs.append(
+                    pl.BlockSpec(
+                        (part, hidden), lambda i, k, c=c, flip=flip: ((k[c] ^ flip) * count + i, 0)
+                    )
+                )
+    block = pl.BlockSpec((part, hidden), lambda i, k: (i, 0))
+    shaped = lambda dtype: jax.ShapeDtypeStruct((rows // 2, hidden), dtype)
+    outs = pl.pallas_call(
+        halve_kernel,
+        out_shape=[shaped(jnp.float32), shaped(jnp.bfloat16)] * 2,
+        grid_spec=pltpu.PrefetchScalarGridSpec(
+            num_scalar_prefetch=1, grid=(count,), in_specs=specs, out_specs=[block] * 4
+        ),
+        compiler_params=pltpu.CompilerParams(vmem_limit_bytes=58 << 20),
+        cost_estimate=pl.CostEstimate(
+            flops=60000 * rows * hidden, bytes_accessed=24 * rows * hidden, transcendentals=0
+        ),
+    )(keeps, *operands)
+    for chain, kept, sent in zip(chains, outs[::2], outs[1::2]):
+        chain.kept = kept
+        chain.send(sent)
+    return [chain.sent for chain in chains]
 
 
 class Cube:
@@ -1285,9 +1311,7 @@
     products = lambda e, dtype: expert_products(
         normed_two, grad_gate_pre, grad_up_pre, scaled_one, scaled_two, grad_live, e, dtype
     )
-    grad_rows, out_rows = expert_sums(
-        place, scaled_one, grad_gate_pre, grad_up_pre, extra, w_gate, w_up, w_down, block
-    )
+    grad_rows = gradient_rows(place, grad_gate_pre, grad_up_pre, extra, w_gate, w_up, block)
     grad_two_sum = lax.psum_scatter(grad_rows, "ctx", scatter_dimension=0, tiled=True)
     normed_two, grad_live = after((normed_two, grad_live), grad_rows)
     chains = [Chain(bits), Chain(bits[::-1])]
@@ -1296,10 +1320,11 @@
     normed_two, grad_live = after((normed_two, grad_live), *[chain.sent for chain in chains])
     for chain, kept in zip(chains, products(1, jnp.float32)):
         chain.kept = kept
+    out_rows = output_rows(place, after(scaled_one, *[c.kept for c in chains]), w_down, block)
 
     grad_middle, grad_branch, grad_mixed, grad_logits, gain_two_grad = turn_rows(
         place,
-        after(grad_two_sum, *[(c.kept, c.flying) for c in chains]),
+        after(grad_two_sum, out_rows),
         gates,
         router_all,
         gain_two,
@@ -1309,11 +1334,12 @@
     )
     grad_branch_all = lax.all_gather(grad_branch, "ctx", axis=0, tiled=True)
 
-    def deal(blocks, *others):
+    def deal_chips(blocks):
         blocks = blocks.reshape((chips, 2) + blocks.shape[1:])
         got = [blocks[(chip - k) % chips] for k in range(chips)]
-        got = jnp.stack([got[0]] + [from_chip(got[k], k) for k in range(1, chips)])
-        got = after(got, *others)
+        return jnp.stack([got[0]] + [from_chip(got[k], k) for k in range(1, chips)])
+
+    def deal_cores(got):
         stay = jnp.where(odd, got[:, 1], got[:, 0])
         go = from_core(jnp.where(odd, got[:, 0], got[:, 1]))
         both = cores(stay[:, None], go[:, None], 1)
@@ -1321,10 +1347,11 @@
         both = lax.dynamic_slice_in_dim(both, (chips - chip) % chips, chips, 0)
         return both.reshape((size,) + both.shape[2:])
 
-    sent = [grad_mixed]
-    while chains[0].stage <= len(bits):
-        sent = [chain.step(*sent) for chain in chains]
-    grad_mixed_all = deal(jnp.repeat(grad_mixed, copies, 0), *sent).reshape(tokens, query_width)
+    got = deal_chips(jnp.repeat(grad_mixed, copies, 0))
+    sent = [got]
+    while chains[0].stage < len(bits):
+        sent = halve_chains(chains, *sent)
+    grad_mixed_all = deal_cores(after(got, *sent)).reshape(tokens, query_width)
     grad_query, grad_pair = attend_back(
         query,
         grad_mixed_all,
@@ -1342,9 +1369,10 @@
         counted = (places // part == copy_index)[:, None]
         grad_query = jnp.where(counted, grad_query, jnp.zeros((), jnp.bfloat16))
         grad_pair = jnp.where(counted, grad_pair, jnp.zeros((), jnp.bfloat16))
+    sent = [chain.step(grad_pair) for chain in chains]
     both_rows, *halves = close_rows(
         place,
-        grad_query,
+        after(grad_query, *sent),
         grad_pair,
         head_all,
         gathered,
@@ -1370,7 +1398,7 @@
         for h, order in enumerate((bits, bits[::-1]))
     ]
     while chains[0].stage < chains[0].steps:
-        sent = [chain.step(*halves, *[cube.flying for cube in cubes]) for chain in chains]
+        sent = [chain.step(*halves) for chain in chains]
     while cubes[0].stage < len(bits):
         for cube in cubes:
             cube.add(*sent)
@@ -1389,14 +1417,15 @@
         ],
         0,
     )
-    head_sums = deal(after(blocks, *first))
+    got = deal_chips(after(blocks, *first))
+    head_sums = deal_cores(after(got, *second))
     for h, cube in enumerate(cubes):
         rows = jnp.transpose(head_sums[h * (size // 2) : (h + 1) * (size // 2)], (1, 0, 2))
         rows = jnp.concatenate(
             [rows.reshape(share, line), totals[h].reshape(share, -1)[:, line:]], 1
         )
         cube.value = rows.reshape(totals[h].shape)
-    sent = [cube.back(*second) for cube in cubes]
+    sent = [cube.back() for cube in cubes]
     third = [chain.piece(2, 3, *sent) for chain in chains]
     keeps = place[2:]
     grad_gate, grad_up = [

time: 491 us -> 443 us (0.902)
  waiting for transfers between devices: 189 us -> 146 us
  Pallas kernels: 146 us -> 157 us
  starting transfers between devices: 46.9 us -> 39.4 us
  other arithmetic: 42.9 us -> 37.7 us
    ppermute x28, waiting for transfers between devices: 130 us -> 94.7 us  [swap(): return lax.ppermute(value, 'rep', [(i, i ^ bit) for i in range(size)])]
    pallas_call x1 -> x3, Pallas kernels: 18.3 us -> 31.3 us  [the longest x1 13.7 us: gradient_rows(): pl.pallas_call(gradient_kernel, out_shape=jax.ShapeDtypeStruct((tokens, f...]
    ppermute x6, waiting for transfers between devices: 23.1 us -> 13.7 us  [from_chip(): lax.ppermute(value, 'ctx', [(i, (i - 2 * k) % size) for i in range(size)])]
    unnamed x100 -> x98, local copies, waits for them, and re-layouts: 12.5 us -> 9.75 us
  transfers between devices with their start and end apart: 42 -> 42, of which waited for: 24 -> 25; matrix products, arithmetic and copies ran while one was open for 10% -> 10% of each run, Pallas kernels for 18% -> 25%
where the time goes in v7:
time: 443 us; the launch traced here: 441 us
  Pallas kernels  157 us (35%)
  waiting for transfers between devices  146 us (33%)
  starting transfers between devices  39.4 us (9%)
  other arithmetic  37.7 us (9%)
  blocking collectives  24.5 us (6%)
  local copies, waits for them, and re-layouts  22.2 us (5%)
  between operations  15.1 us (3%)
    ppermute x28, waiting for transfers between devices, swap(): return lax.ppermute(value, 'rep', [(i, i ^ bit) for i in range(size)])  94.7 us
    ppermute x28, starting transfers between devices, swap(): return lax.ppermute(value, 'rep', [(i, i ^ bit) for i in range(size)])  30.8 us
    pallas_call x2, Pallas kernels, expert_products(): pl.pallas_call(product_kernel, out_shape=(jax.ShapeDtypeStruct((rows, hid...  28.8 us
    all_to_all x1, blocking collectives, per_device(): lax.all_to_all(head_columns, 'ctx', split_axis=0, concat_axis=0, tiled=True)  24.5 us
    pallas_call x1, Pallas kernels, expert_rows(): pl.pallas_call(expert_kernel, out_shape=(wide, wide, wide, wide, jax.Shap...  20.5 us
    all_gather x1, waiting for transfers between devices, per_device(): gathered = lax.all_gather(rows, 'ctx', axis=0)  16.5 us
    pallas_call x1, Pallas kernels, attend(): pl.pallas_call(attend_kernel, out_shape=(shaped((tokens, features), jnp.b...  15.3 us
    pallas_call x1, Pallas kernels, close_rows(): pl.pallas_call(lambda *refs: close_kernel(reps, *refs), name='close', out...  14.6 us
  transfers between devices with their start and end apart: 42, of which 25 were waited for; matrix products, arithmetic and copies ran while one was open for 10% of the time, Pallas kernels for 25%

profile of v7, /device:TPU:0, one launch (start us, length us, event | category | flops | bytes accessed | tf_op | source)
XLA Modules:
  0.0 441.3 jit_solution(12304669905713403881)
XLA Ops:
  9.5 1.9 fusion.16
  15.3 24.5 %all_to_all.5 = bf16[8,48,384]{2,1,0:T(8,128)(2,1)S(1)} all-to-all(bf16[8,48,384]{2,1,0:T(8,128)(2,1)S(1)} %copy.103), channel_id=1, replica_groups=mesh['rep'=4,'ctx'=8] {'ctx'}, dimensions={0} | all-to-all | bytes 589824 | tf_op jit(solution)/shard_map/all_to_all | solution.py:1267
  42.9 2.8 collective-permute-done
  47.8 1.6 collective-permute-start.1
  49.4 5.6 %collective-permute-done.3 = bf16[4,2,1,48,384]{4,3,0,2,1:T(8,128)(2,1)S(1)} collective-permute-done((bf16[4,2,1,48,384]{4,3,0,2,1:T(8,128)(2,1)S(1)}, bf16[4,2,1,48,384]{4,3,0,2,1:T(8,128)(2,1)S(1)}, u32[]{:S(2)}, u32[]{:S(2)}) %collective-permute-start.3) | collective-permute-done | bytes 294944 | tf_op jit(solution)/shard_map/ppermute | solution.py:1030
  55.0 16.5 %all-gather.11.cloned.1.call-done = bf16[1408,1664]{1,0:T(8,128)(2,1)} async-done(((bf16[176,1664]{1,0:T(8,128)(2,1)}), bf16[1408,1664]{1,0:T(8,128)(2,1)}) %all-gather.11.cloned.1.call-update) | async-done | bytes 4685840 | tf_op jit(solution)/shard_map/all_gather | solution.py:1238
  72.8 1.6 collective-permute-start.5
  77.4 15.3 %shard_map.238 = (bf16[1024,1536]{1,0:T(8,128)(2,1)}, bf16[1024,192]{1,0:T(8,128)(2,1)S(1)}, bf16[1024,64]{1,0:T(8,128)(2,1)S(1)}, bf16[1024,64]{1,0:T(8,128)(2,...) custom-call(bf16[8,176,1664]{2,1,0:T(8,128)(2,1)} %bitcast.177, ...), custom_call_target="tpu_custom_call" | custom-call | bytes 1024 | tf_op jit(solution)/shard_map/pallas_call | solution.py:194
  92.8 2.3 broadcast_select_fusion.9
  97.7 12.6 %all-gather.7.cloned.1.call-done.cotangent_ref = bf16[1024,1536]{1,0:T(8,128)(2,1)} async-done(((bf16[128,1536]{1,0:T(8,128)(2,1)}), bf16[1024,1536]{1,0:T(8,128)(2,1)}) %all-gather.7.cloned.1.call-update) | async-done | bytes 3145744 | tf_op jit(solution)/shard_map/all_gather | solution.py:1239
  115.1 23.8 %collective-permute-done.6 = bf16[4,1,2,48,1536]{4,3,0,2,1:T(8,128)(2,1)} collective-permute-done((bf16[4,1,2,48,1536]{4,3,0,2,1:T(8,128)(2,1)}, bf16[4,1,2,48,1536]{4,3,0,2,1:T(8,128)(2,1)}, u32[]{:S(2)}, u32[]{:S(2)}) %collective-permute-start.6) | collective-permute-done | bytes 1179680 | tf_op jit(solution)/shard_map/ppermute | solution.py:1030
  142.6 1.6 copy.107
  144.2 5.5 %all-gather.13.cloned.1.call-done = bf16[4096,384]{1,0:T(8,128)(2,1)} async-done(((bf16[512,384]{1,0:T(8,128)(2,1)}), bf16[4096,384]{1,0:T(8,128)(2,1)}) %all-gather.13.cloned.1.call-update) | async-done | bytes 3145744 | tf_op jit(solution)/shard_map/all_gather | solution.py:1289
  149.7 1.7 copy-done.4
  152.4 10.8 %shard_map.239 = (f32[1024,1536]{1,0:T(8,128)}, bf16[1024,1536]{1,0:T(8,128)(2,1)}, f32[1024,16]{1,0:T(8,128)S(1)}) custom-call(bf16[8,512,384]{2,1,0:T(8,128)(2,1)} %bitcast.205, bf16[768,1536]{1,0:T(8,128)(2,1)S(1)} %bitcast.169, bf16[768,1536]{1,0:T(8,128)(2,1)S(1)} %bitcast.172, bf16[8,176,1664]{2,1,0:T(8,128)(2,1)} %bitcast.180, ...), custom_call_target="tpu_custom_call" | custom-call | flops 4831838208 | bytes 18874368 | tf_op jit(solution)/shard_map/pallas_call | solution.py:401
  163.2 20.5 %shard_map.240 = (bf16[2,1024,512]{2,1,0:T(8,128)(2,1)}, bf16[2,1024,512]{2,1,0:T(8,128)(2,1)}, bf16[2,1024,512]{2,1,0:T(8,128)(2,1)}, bf16[2,1024,512]{2,1,0:T(...) custom-call(s32[4]{0:T(128)S(1)} %pad_add_fusion.place_ref.refs_0_, ...), custom_call_target="tpu_custom_call" | custom-call | flops 9663676416 | bytes 25165824 | tf_op jit(solution)/shard_map/pallas_call | solution.py:495
  183.7 13.7 %shard_map.241 = bf16[1024,1664]{1,0:T(8,128)(2,1)} custom-call(s32[4]{0:T(128)S(1)} %pad_add_fusion.place_ref.refs_0_, bf16[2,1024,512]{2,1,0:T(8,128)(2,1)} %get-tuple-element.101.grad_gate_ref.gate_ref, bf16[2,1024,512]{2,1,0:T(8,128)(2,1)} %get-tuple-element.102.grad_up_ref.up_ref, bf16[1024,128]{1,0:T(8,128)(2,1)S(1)} %get-tuple-element.103.extra_ref, ...), custom_call_target="tpu_custom_call" | custom-call | bytes 1024 | tf_op jit(solution)/shard_map/pallas_call | solution.py:628
  197.7 13.6 %shard_map.242 = (bf16[2304,512]{1,0:T(8,128)(2,1)}, bf16[2304,512]{1,0:T(8,128)(2,1)}) custom-call(bf16[1024,1536]{1,0:T(8,128)(2,1)} %get-tuple-element.111.normed_ref.left_ref.refs_7_, bf16[2,1024,512]{2,1,0:T(8,128)(2,1)} %get-tuple-element.101.grad_gate_ref.gate_ref, bf16[2,1024,512]{2,1,0:T(8,128)(2,1)} %get-tuple-element.102.grad_up_ref.up_ref, ...), custom_call_target="tpu_custom_call" | custom-call | bytes 1024 | tf_op jit(solution)/shard_map/pallas_call | solution.py:585
  214.3 15.2 %shard_map.243 = (f32[2304,512]{1,0:T(8,128)}, f32[2304,512]{1,0:T(8,128)}) custom-call(bf16[1024,1536]{1,0:T(8,128)(2,1)} %get-tuple-element.111.normed_ref.left_ref.refs_7_, bf16[2,1024,512]{2,1,0:T(8,128)(2,1)} %get-tuple-element.101.grad_gate_ref.gate_ref, bf16[2,1024,512]{2,1,0:T(8,128)(2,1)} %get-tuple-element.102.grad_up_ref.up_ref, ...), custom_call_target="tpu_custom_call" | custom-call | bytes 1024 | tf_op jit(solution)/shard_map/pallas_call | solution.py:585
  229.6 8.8 %shard_map.244.refs_9_ = bf16[1024,1536]{1,0:T(8,128)(2,1)} custom-call(s32[4]{0:T(128)S(1)} %pad_add_fusion.place_ref.refs_0_, bf16[2,1024,512]{2,1,0:T(8,128)(2,1)} %get-tuple-element.115.scaled_one_ref.scaled_ref, bf16[2,512,1536]{2,1,0:T(8,128)(2,1)} %down_weight_ref.3), custom_call_target="tpu_custom_call" | custom-call | bytes 1024 | tf_op jit(solution)/shard_map/pallas_call | solution.py:665
  239.1 6.8 %shard_map.245 = (f32[128,1536]{1,0:T(8,128)}, bf16[128,1536]{1,0:T(8,128)(2,1)}, bf16[8,128,192]{2,1,0:T(8,128)(2,1)}, bf16[128,16]{1,0:T(8,128)(2,1)}, f32[1,1536]{1,0:T(1,128)}) custom-call(s32[4]{0:T(128)} %copy-done.23, bf16[128,1664]{1,0:T(8,128)(2,1)} %reduce-scatter.3.cloned.1.call-done.sum_ref, f32[1024,16]{1,0:T(8,128)} %copy-done.15, ...), custom_call_target="tpu_custom_call" | custom-call | bytes 128 | tf_op jit(solution)/shard_map/pallas_call | solution.py:736
  248.1 2.8 collective-permute-start.8
  251.5 3.8 collective-permute-done.10
  255.3 3.7 collective-permute-done.9
  259.1 5.9 %collective-permute-done.11.refs_2_.refs_3_ = bf16[2304,512]{1,0:T(8,128)(2,1)} collective-permute-done((bf16[2304,512]{1,0:T(8,128)(2,1)}, bf16[2304,512]{1,0:T(8,128)(2,1)}, u32[]{:S(2)}, u32[]{:S(2)}) %collective-permute-start.11) | collective-permute-done | bytes 2359328 | tf_op jit(solution)/shard_map/ppermute | solution.py:1030
  266.3 8.8 %shard_map.246 = (f32[1152,512]{1,0:T(8,128)}, bf16[1152,512]{1,0:T(8,128)(2,1)}, f32[1152,512]{1,0:T(8,128)}, bf16[1152,512]{1,0:T(8,128)(2,1)}) custom-call(s32[2]{0:T(128)} %add_convert_fusion.4.keeps_ref, f32[2304,512]{1,0:T(8,128)} %get-tuple-element.113.refs_0_.refs_1_, f32[2304,512]{1,0:T(8,128)} %get-tuple-element.113.refs_0_.refs_1_, ...), custom_call_target="tpu_custom_call" | custom-call | flops 70778880000 | bytes 28311552 | tf_op jit(solution)/shard_map/pallas_call | solution.py:1099
  279.7 13.3 %shard_map.247 = (bf16[1024,192]{1,0:T(8,128)(2,1)S(1)}, bf16[1024,128]{1,0:T(8,128)(2,1)S(1)}) custom-call(bf16[1024,192]{1,0:T(8,128)(2,1)S(1)} %copy-done.14, bf16[1024,192]{1,0:T(8,128)(2,1)S(1)} %bitcast.175, f32[3,1024,1]{2,1,0:T(8,128)S(1)} %copy-done.10, f32[1024,64]{1,0:T(8,128)S(1)} %copy-done.6, f32[1024,64]{1,0:T(8,128)S(1)} %copy-done.8, ...), custom_call_target="tpu_custom_call" | custom-call | bytes 1024 | tf_op jit(solution)/shard_map/pallas_call | solution.py:323
  293.0 9.4 %collective-permute-done.14 = bf16[1152,512]{1,0:T(8,128)(2,1)} collective-permute-done((bf16[1152,512]{1,0:T(8,128)(2,1)}, bf16[1152,512]{1,0:T(8,128)(2,1)}, u32[]{:S(2)}, u32[]{:S(2)}) %collective-permute-start.14) | collective-permute-done | bytes 1179680 | tf_op jit(solution)/shard_map/ppermute | solution.py:1030
  302.4 1.9 add_convert_fusion.1
  305.9 1.7 add_convert_fusion
  309.3 14.6 %close.1 = (bf16[1024,3072]{1,0:T(8,128)(2,1)}, f32[96,2304]{1,0:T(8,128)}, f32[96,2304]{1,0:T(8,128)}, bf16[96,2304]{1,0:T(8,128)(2,1)}, bf16[96,2304]{1,0:T(8,128)(2,1)}) custom-call(s32[4]{0:T(128)} %copy-done.23, bf16[1024,192]{1,0:T(8,128)(2,1)} %copy-done.16, bf16[1024,128]{1,0:T(8,128)(2,1)} %copy-done.17, ...), custom_call_target="tpu_custom_call" | custom-call | bytes 1024 | tf_op jit(solution)/shard_map/close/pallas_call | solution.py:865
  325.5 5.0 %collective-permute-done.17 = bf16[1152,512]{1,0:T(8,128)(2,1)} collective-permute-done((bf16[1152,512]{1,0:T(8,128)(2,1)S(1)}, bf16[1152,512]{1,0:T(8,128)(2,1)}, u32[]{:S(2)}, u32[]{:S(2)}) %collective-permute-start.17) | collective-permute-done | bytes 1179680 | tf_op jit(solution)/shard_map/ppermute | solution.py:1030
  332.0 4.6 %collective-permute-done.18 = bf16[1152,512]{1,0:T(8,128)(2,1)} collective-permute-done((bf16[1152,512]{1,0:T(8,128)(2,1)S(1)}, bf16[1152,512]{1,0:T(8,128)(2,1)}, u32[]{:S(2)}, u32[]{:S(2)}) %collective-permute-start.18) | collective-permute-done | bytes 1179680 | tf_op jit(solution)/shard_map/ppermute | solution.py:1030
  346.0 2.4 collective-permute-done.20
  350.5 1.7 dynamic-slice_convert_fusion.1
  353.3 14.3 %collective-permute-done.21 = bf16[1,1,48,2304]{3,2,1,0:T(8,128)(2,1)S(1)} collective-permute-done((bf16[1,1,48,2304]{3,2,1,0:T(8,128)(2,1)S(1)}, bf16[1,1,48,2304]{3,2,1,0:T(8,128)(2,1)S(1)}, u32[]{:S(2)}, u32[]{:S(2)}) %collective-permute-start.21) | collective-permute-done | bytes 221216 | tf_op jit(solution)/shard_map/ppermute | solution.py:1030
  374.6 2.4 collective-permute-start.24
  376.9 4.5 %collective-permute-done.26 = bf16[2,48,384]{2,1,0:T(8,128)(2,1)S(1)} collective-permute-done((bf16[2,48,384]{2,1,0:T(8,128)(2,1)S(1)}, bf16[2,48,384]{2,1,0:T(8,128)(2,1)S(1)}, u32[]{:S(2)}, u32[]{:S(2)}) %collective-permute-start.26) | collective-permute-done | bytes 73760 | tf_op jit(solution)/shard_map/ppermute | solution.py:1242
  381.5 1.7 collective-permute-done.25
  390.7 1.6 collective-permute-start.34
  392.3 4.9 %into_output.2 = f32[2,1536,512]{2,1,0:T(8,128)} custom-call(s32[2]{0:T(128)S(1)} %pad_add_fusion.1.k.keeps_ref, bf16[2304,512]{1,0:T(8,128)(2,1)S(1)} %pad_maximum_fusion.refs_0_.sent_low_ref, bf16[768,512]{1,0:T(8,128)(2,1)S(1)} %collective-permute-done.22.refs_1_, bf16[768,512]{1,0:T(8,128)(2,1)} %collective-permute-done.27.refs_2_), custom_call_target="tpu_custom_call" | custom-call | bytes 768 | tf_op jit(solution)/shard_map/into_output/pallas_call | solution.py:972
  397.2 5.2 %into_output.3 = f32[2,1536,512]{2,1,0:T(8,128)} custom-call(s32[2]{0:T(128)S(1)} %pad_add_fusion.1.k.keeps_ref, bf16[2304,512]{1,0:T(8,128)(2,1)S(1)} %copy-done.2, bf16[768,512]{1,0:T(8,128)(2,1)} %collective-permute-done.23.refs_1_, bf16[768,512]{1,0:T(8,128)(2,1)} %collective-permute-done.28.refs_2_), custom_call_target="tpu_custom_call" | custom-call | bytes 768 | tf_op jit(solution)/shard_map/into_output/pallas_call | solution.py:972
  403.1 11.1 %collective-permute-done.34 = bf16[1,1,48,2304]{3,2,1,0:T(8,128)(2,1)S(1)} collective-permute-done((bf16[1,1,48,2304]{3,2,1,0:T(8,128)(2,1)S(1)}, bf16[1,1,48,2304]{3,2,1,0:T(8,128)(2,1)S(1)}, u32[]{:S(2)}, u32[]{:S(2)}) %collective-permute-start.34) | collective-permute-done | bytes 221216 | tf_op jit(solution)/shard_map/ppermute | solution.py:1030
  415.6 3.5 shard_map.248
  419.2 4.1 collective-permute-done.31
  423.3 2.5 collective-permute-done.35
  426.1 1.9 head_outputs.1
  432.0 2.5 fusion.10
  (263 shorter events, 79.9 us)
Async XLA Ops:
  7.2 64.3 %all-gather.11.cloned.1.call-start = ((), (), s32[]{:S(2)}) async-start(), calls=%async_computation.7 | async-start | bytes 5271552 | tf_op jit(solution)/shard_map/all_gather | solution.py:1238
  11.4 98.9 %all-gather.7.cloned.1.call-start = ((), (), s32[]{:S(2)}) async-start(), calls=%async_computation.3 | async-start | bytes 3538944 | tf_op jit(solution)/shard_map/all_gather | solution.py:1239
  12.1 137.6 %all-gather.13.cloned.1.call-start = ((), (), s32[]{:S(2)}) async-start(), calls=%async_computation.8 | async-start | bytes 3538944 | tf_op jit(solution)/shard_map/all_gather | solution.py:1289
  39.8 5.9 %collective-permute-start = (bf16[4,1,1,48,384]{4,3,0,2,1:T(8,128)(2,1)S(1)}, bf16[4,1,1,48,384]{4,3,0,2,1:T(8,128)(2,1)S(1)}, u32[]{:S(2)}, u32[]{:S(2)}) collective-permute-start(bf16[4,1,1,48,384]{4,3,0,2,1:T(8,128)(2,1)S(1)} %get-tuple-element.298), channel_id=1, source_target_pairs={{0,8},{8,0},{16,24},{24,16},{1,9},{9,1},{17,25},{25,17},{2,10},{10... | collective-permute-start | bytes 442376 | tf_op jit(solution)/shard_map/ppermute | solution.py:1030
  41.4 5.5 %collective-permute-start.2 = (bf16[4,1,1,48,384]{4,3,0,2,1:T(8,128)(2,1)S(1)}, bf16[4,1,1,48,384]{4,3,0,2,1:T(8,128)(2,1)S(1)}, u32[]{:S(2)}, u32[]{:S(2)}) collective-permute-start(bf16[4,1,1,48,384]{4,3,0,2,1:T(8,128)(2,1)S(1)} %get-tuple-element.299), channel_id=1, source_target_pairs={{0,16},{8,24},{16,0},{24,8},{1,17},{9,25},{17,1},{25,9},{2,18},{10... | collective-permute-start | bytes 442376 | tf_op jit(solution)/shard_map/ppermute | solution.py:1030
  47.0 8.0 %collective-permute-start.3 = (bf16[4,2,1,48,384]{4,3,0,2,1:T(8,128)(2,1)S(1)}, bf16[4,2,1,48,384]{4,3,0,2,1:T(8,128)(2,1)S(1)}, u32[]{:S(2)}, u32[]{:S(2)}) collective-permute-start(bf16[4,2,1,48,384]{4,3,0,2,1:T(8,128)(2,1)S(1)} %pad_maximum_fusion.15), channel_id=1, source_target_pairs={{0,8},{8,0},{16,24},{24,16},{1,9},{9,1},{17,25},{25,17},{2,10},{10... | collective-permute-start | bytes 884744 | tf_op jit(solution)/shard_map/ppermute | solution.py:1030
  47.8 28.3 %collective-permute-start.1 = (bf16[4,1,2,48,384]{4,3,0,2,1:T(8,128)(2,1)S(1)}, bf16[4,1,2,48,384]{4,3,0,2,1:T(8,128)(2,1)S(1)}, u32[]{:S(2)}, u32[]{:S(2)}) collective-permute-start(bf16[4,1,2,48,384]{4,3,0,2,1:T(8,128)(2,1)S(1)} %pad_maximum_fusion.14), channel_id=1, source_target_pairs={{0,16},{8,24},{16,0},{24,8},{1,17},{9,25},{17,1},{25,9},{2,18},{10... | collective-permute-start | bytes 884744 | tf_op jit(solution)/shard_map/ppermute | solution.py:1030
  72.8 20.0 %collective-permute-start.5 = (bf16[4,1,1,48,1536]{4,3,0,2,1:T(8,128)(2,1)S(1)}, bf16[4,1,1,48,1536]{4,3,0,2,1:T(8,128)(2,1)S(1)}, u32[]{:S(2)}, u32[]{:S(2)}) collective-permute-start(bf16[4,1,1,48,1536]{4,3,0,2,1:T(8,128)(2,1)S(1)} %get-tuple-element.248), channel_id=1, source_target_pairs={{0,16},{8,24},{16,0},{24,8},{1,17},{9,25},{17,1},{25,9},{2,18},{10... | collective-permute-start | bytes 1769480 | tf_op jit(solution)/shard_map/ppermute | solution.py:1030
  74.4 18.4 %collective-permute-start.4 = (bf16[4,1,1,48,1536]{4,3,0,2,1:T(8,128)(2,1)S(1)}, bf16[4,1,1,48,1536]{4,3,0,2,1:T(8,128)(2,1)S(1)}, u32[]{:S(2)}, u32[]{:S(2)}) collective-permute-start(bf16[4,1,1,48,1536]{4,3,0,2,1:T(8,128)(2,1)S(1)} %get-tuple-element.249), channel_id=1, source_target_pairs={{0,8},{8,0},{16,24},{24,16},{1,9},{9,1},{17,25},{25,17},{2,10},{10... | collective-permute-start | bytes 1769480 | tf_op jit(solution)/shard_map/ppermute | solution.py:1030
  77.4 15.3 %copy-start.41 = (f32[1536]{0:T(1024)}, f32[1536]{0:T(1024)S(1)}, u32[]{:S(2)}) copy-start(f32[1536]{0:T(1024)S(1)} %get-tuple-element.239) | copy-start | bytes 18436
  110.3 128.7 %reduce-scatter.3.cloned.1.call-start = ((), (), s32[]{:S(2)}) async-start(), calls=%async_computation.4 | async-start | bytes 3833856 | tf_op jit(solution)/shard_map/reduce_scatter | solution.py:1315
  110.4 28.5 %collective-permute-start.6 = (bf16[4,1,2,48,1536]{4,3,0,2,1:T(8,128)(2,1)}, bf16[4,1,2,48,1536]{4,3,0,2,1:T(8,128)(2,1)}, u32[]{:S(2)}, u32[]{:S(2)}) collective-permute-start(bf16[4,1,2,48,1536]{4,3,0,2,1:T(8,128)(2,1)} %pad_maximum_fusion.5), channel_id=1, source_target_pairs={{0,16},{8,24},{16,0},{24,8},{1,17},{9,25},{17,1},{25,9},{2,18},{10... | collective-permute-start | bytes 3538952 | tf_op jit(solution)/shard_map/ppermute | solution.py:1030
  111.9 28.8 %collective-permute-start.7 = (bf16[4,2,1,48,1536]{4,3,0,2,1:T(8,128)(2,1)}, bf16[4,2,1,48,1536]{4,3,0,2,1:T(8,128)(2,1)S(1)}, u32[]{:S(2)}, u32[]{:S(2)}) collective-permute-start(bf16[4,2,1,48,1536]{4,3,0,2,1:T(8,128)(2,1)} %pad_maximum_fusion.6), channel_id=1, source_target_pairs={{0,8},{8,0},{16,24},{24,16},{1,9},{9,1},{17,25},{25,17},{2,10},{10... | collective-permute-start | bytes 3538952 | tf_op jit(solution)/shard_map/ppermute | solution.py:1030
  113.5 116.1 %copy-start.23 = (s32[4]{0:T(128)}, s32[4]{0:T(128)S(1)}, u32[]{:S(2)}) copy-start(s32[4]{0:T(128)S(1)} %pad_add_fusion.place_ref.refs_0_) | copy-start | bytes 52
  114.2 35.5 %copy-start.22 = (f32[1,1536]{1,0:T(1,128)}, f32[1,1536]{1,0:T(1,128)S(1)}, u32[]{:S(2)}) copy-start(f32[1,1536]{1,0:T(1,128)S(1)} %reshape.330.gain_ref) | copy-start | bytes 18436
  163.2 20.5 %copy-start.15 = (f32[1024,16]{1,0:T(8,128)}, f32[1024,16]{1,0:T(8,128)S(1)}, u32[]{:S(2)}) copy-start(f32[1024,16]{1,0:T(8,128)S(1)} %get-tuple-element.100.gates_ref) | copy-start | bytes 196612
  197.5 111.9 %all-gather.9.cloned.1.call-start = ((), (), s32[]{:S(2)}) async-start(), calls=%async_computation.5 | async-start | bytes 3538944 | tf_op jit(solution)/shard_map/all_gather | solution.py:1335
  211.3 53.7 %collective-permute-start.11 = (bf16[2304,512]{1,0:T(8,128)(2,1)}, bf16[2304,512]{1,0:T(8,128)(2,1)}, u32[]{:S(2)}, u32[]{:S(2)}) collective-permute-start(bf16[2304,512]{1,0:T(8,128)(2,1)} %get-tuple-element.109), channel_id=1, source_target_pairs={{0,8},{8,0},{16,24},{24,16},{1,9},{9,1},{17,25},{25,17},{2,10},{10... | collective-permute-start | bytes 7077896 | tf_op jit(solution)/shard_map/ppermute | solution.py:1030
  212.8 53.4 %collective-permute-start.12 = (bf16[2304,512]{1,0:T(8,128)(2,1)}, bf16[2304,512]{1,0:T(8,128)(2,1)}, u32[]{:S(2)}, u32[]{:S(2)}) collective-permute-start(bf16[2304,512]{1,0:T(8,128)(2,1)} %get-tuple-element.110), channel_id=1, source_target_pairs={{0,16},{8,24},{16,0},{24,8},{1,17},{9,25},{17,1},{25,9},{2,18},{10... | collective-permute-start | bytes 7077896 | tf_op jit(solution)/shard_map/ppermute | solution.py:1030
  246.9 8.3 %collective-permute-start.10 = (bf16[2,128,192]{2,1,0:T(8,128)(2,1)S(1)}, bf16[2,128,192]{2,1,0:T(8,128)(2,1)S(1)}, u32[]{:S(2)}, u32[]{:S(2)}) collective-permute-start(bf16[2,128,192]{2,1,0:T(8,128)(2,1)S(1)} %get-tuple-element.277), channel_id=1, source_target_pairs={{0,2},{1,3},{2,4},{3,5},{4,6},{5,7},{6,0},{7,1},{8,10},{9,11},{10,... | collective-permute-start | bytes 294920 | tf_op jit(solution)/shard_map/ppermute | solution.py:1242
  247.0 12.0 %collective-permute-start.9 = (bf16[2,128,192]{2,1,0:T(8,128)(2,1)S(1)}, bf16[2,128,192]{2,1,0:T(8,128)(2,1)S(1)}, u32[]{:S(2)}, u32[]{:S(2)}) collective-permute-start(bf16[2,128,192]{2,1,0:T(8,128)(2,1)S(1)} %get-tuple-element.278), channel_id=1, source_target_pairs={{0,4},{1,5},{2,6},{3,7},{4,0},{5,1},{6,2},{7,3},{8,12},{9,13},{10,... | collective-permute-start | bytes 294920 | tf_op jit(solution)/shard_map/ppermute | solution.py:1242
  248.1 10.9 %collective-permute-start.8 = (bf16[2,128,192]{2,1,0:T(8,128)(2,1)S(1)}, bf16[2,128,192]{2,1,0:T(8,128)(2,1)S(1)}, u32[]{:S(2)}, u32[]{:S(2)}) collective-permute-start(bf16[2,128,192]{2,1,0:T(8,128)(2,1)S(1)} %get-tuple-element.279), channel_id=1, source_target_pairs={{0,6},{1,7},{2,0},{3,1},{4,2},{5,3},{6,4},{7,5},{8,14},{9,15},{10,... | collective-permute-start | bytes 294920 | tf_op jit(solution)/shard_map/ppermute | solution.py:1242
  251.4 178.1 %reduce-scatter.5.cloned.1.call-start = ((), (), s32[]{:S(2)}) async-start(), calls=%async_computation.6 | async-start | bytes 7077888 | tf_op jit(solution)/shard_map/reduce_scatter | solution.py:1390
  266.3 13.4 %copy-start.10 = (f32[3,1024,1]{2,1,0:T(8,128)S(1)}, f32[3,1024,1]{2,1,0:T(8,128)}, u32[]{:S(2)}) copy-start(f32[3,1024,1]{2,1,0:T(8,128)} %copy-done.9) | copy-start | bytes 36868
  275.0 27.3 %collective-permute-start.14 = (bf16[1152,512]{1,0:T(8,128)(2,1)}, bf16[1152,512]{1,0:T(8,128)(2,1)}, u32[]{:S(2)}, u32[]{:S(2)}) collective-permute-start(bf16[1152,512]{1,0:T(8,128)(2,1)} %get-tuple-element.122), channel_id=1, source_target_pairs={{0,16},{8,24},{16,0},{24,8},{1,17},{9,25},{17,1},{25,9},{2,18},{10... | collective-permute-start | bytes 3538952 | tf_op jit(solution)/shard_map/ppermute | solution.py:1030
  276.6 1.7 collective-permute-start.13
  276.7 29.2 %collective-permute-start.15 = (bf16[1152,512]{1,0:T(8,128)(2,1)}, bf16[1152,512]{1,0:T(8,128)(2,1)}, u32[]{:S(2)}, u32[]{:S(2)}) collective-permute-start(bf16[1152,512]{1,0:T(8,128)(2,1)} %get-tuple-element.123), channel_id=1, source_target_pairs={{0,8},{8,0},{16,24},{24,16},{1,9},{9,1},{17,25},{25,17},{2,10},{10... | collective-permute-start | bytes 3538952 | tf_op jit(solution)/shard_map/ppermute | solution.py:1030
  279.7 22.7 %copy-start.33 = (f32[1152,512]{1,0:T(8,128)S(1)}, f32[1152,512]{1,0:T(8,128)}, u32[]{:S(2)}) copy-start(f32[1152,512]{1,0:T(8,128)} %get-tuple-element.132) | copy-start | bytes 7077892
  304.3 26.2 %collective-permute-start.17 = (bf16[1152,512]{1,0:T(8,128)(2,1)S(1)}, bf16[1152,512]{1,0:T(8,128)(2,1)}, u32[]{:S(2)}, u32[]{:S(2)}) collective-permute-start(bf16[1152,512]{1,0:T(8,128)(2,1)S(1)} %add_convert_fusion.1), channel_id=1, source_target_pairs={{0,16},{8,24},{16,0},{24,8},{1,17},{9,25},{17,1},{25,9},{2,18},{10... | collective-permute-start | bytes 3538952 | tf_op jit(solution)/shard_map/ppermute | solution.py:1030
  307.5 29.1 %collective-permute-start.18 = (bf16[1152,512]{1,0:T(8,128)(2,1)S(1)}, bf16[1152,512]{1,0:T(8,128)(2,1)}, u32[]{:S(2)}, u32[]{:S(2)}) collective-permute-start(bf16[1152,512]{1,0:T(8,128)(2,1)S(1)} %add_convert_fusion), channel_id=1, source_target_pairs={{0,8},{8,0},{16,24},{24,16},{1,9},{9,1},{17,25},{25,17},{2,10},{10... | collective-permute-start | bytes 3538952 | tf_op jit(solution)/shard_map/ppermute | solution.py:1030
  324.0 22.0 %collective-permute-start.16 = (bf16[2,1,48,2304]{3,2,1,0:T(8,128)(2,1)}, bf16[2,1,48,2304]{3,2,1,0:T(8,128)(2,1)S(1)}, u32[]{:S(2)}, u32[]{:S(2)}) collective-permute-start(bf16[2,1,48,2304]{3,2,1,0:T(8,128)(2,1)} %bitcast.42), channel_id=1, source_target_pairs={{0,8},{8,0},{16,24},{24,16},{1,9},{9,1},{17,25},{25,17},{2,10},{10... | collective-permute-start | bytes 1327112 | tf_op jit(solution)/shard_map/ppermute | solution.py:1030
  336.6 11.7 %collective-permute-start.20 = (bf16[1,2,48,2304]{3,2,1,0:T(8,128)(2,1)S(1)}, bf16[1,2,48,2304]{3,2,1,0:T(8,128)(2,1)S(1)}, u32[]{:S(2)}, u32[]{:S(2)}) collective-permute-start(bf16[1,2,48,2304]{3,2,1,0:T(8,128)(2,1)S(1)} %bitcast.206), channel_id=1, source_target_pairs={{0,16},{8,24},{16,0},{24,8},{1,17},{9,25},{17,1},{25,9},{2,18},{10... | collective-permute-start | bytes 1327112 | tf_op jit(solution)/shard_map/ppermute | solution.py:1030
  338.6 34.0 %collective-permute-start.22 = (bf16[768,512]{1,0:T(8,128)(2,1)}, bf16[768,512]{1,0:T(8,128)(2,1)S(1)}, u32[]{:S(2)}, u32[]{:S(2)}) collective-permute-start(bf16[768,512]{1,0:T(8,128)(2,1)} %get-tuple-element.265), channel_id=1, source_target_pairs={{0,8},{8,0},{16,24},{24,16},{1,9},{9,1},{17,25},{25,17},{2,10},{10... | collective-permute-start | bytes 2359304 | tf_op jit(solution)/shard_map/ppermute | solution.py:1030
  342.8 29.8 %collective-permute-start.23 = (bf16[768,512]{1,0:T(8,128)(2,1)}, bf16[768,512]{1,0:T(8,128)(2,1)}, u32[]{:S(2)}, u32[]{:S(2)}) collective-permute-start(bf16[768,512]{1,0:T(8,128)(2,1)} %get-tuple-element.262), channel_id=1, source_target_pairs={{0,16},{8,24},{16,0},{24,8},{1,17},{9,25},{17,1},{25,9},{2,18},{10... | collective-permute-start | bytes 2359304 | tf_op jit(solution)/shard_map/ppermute | solution.py:1030
  348.5 19.1 %collective-permute-start.21 = (bf16[1,1,48,2304]{3,2,1,0:T(8,128)(2,1)S(1)}, bf16[1,1,48,2304]{3,2,1,0:T(8,128)(2,1)S(1)}, u32[]{:S(2)}, u32[]{:S(2)}) collective-permute-start(bf16[1,1,48,2304]{3,2,1,0:T(8,128)(2,1)S(1)} %dynamic-slice_convert_fusion), channel_id=1, source_target_pairs={{0,8},{8,0},{16,24},{24,16},{1,9},{9,1},{17,25},{25,17},{2,10},{10... | collective-permute-start | bytes 663560 | tf_op jit(solution)/shard_map/ppermute | solution.py:1030
  352.3 16.7 %collective-permute-start.19 = (bf16[1,1,48,2304]{3,2,1,0:T(8,128)(2,1)}, bf16[1,1,48,2304]{3,2,1,0:T(8,128)(2,1)}, u32[]{:S(2)}, u32[]{:S(2)}) collective-permute-start(bf16[1,1,48,2304]{3,2,1,0:T(8,128)(2,1)} %dynamic-slice_convert_fusion.1), channel_id=1, source_target_pairs={{0,16},{8,24},{16,0},{24,8},{1,17},{9,25},{17,1},{25,9},{2,18},{10... | collective-permute-start | bytes 663560 | tf_op jit(solution)/shard_map/ppermute | solution.py:1030
  352.3 31.0 %collective-permute-start.27 = (bf16[768,512]{1,0:T(8,128)(2,1)}, bf16[768,512]{1,0:T(8,128)(2,1)}, u32[]{:S(2)}, u32[]{:S(2)}) collective-permute-start(bf16[768,512]{1,0:T(8,128)(2,1)} %get-tuple-element.154), channel_id=1, source_target_pairs={{0,8},{8,0},{16,24},{24,16},{1,9},{9,1},{17,25},{25,17},{2,10},{10... | collective-permute-start | bytes 2359304 | tf_op jit(solution)/shard_map/ppermute | solution.py:1030
  367.6 16.3 %collective-permute-start.28 = (bf16[768,512]{1,0:T(8,128)(2,1)}, bf16[768,512]{1,0:T(8,128)(2,1)}, u32[]{:S(2)}, u32[]{:S(2)}) collective-permute-start(bf16[768,512]{1,0:T(8,128)(2,1)} %get-tuple-element.155), channel_id=1, source_target_pairs={{0,16},{8,24},{16,0},{24,8},{1,17},{9,25},{17,1},{25,9},{2,18},{10... | collective-permute-start | bytes 2359304 | tf_op jit(solution)/shard_map/ppermute | solution.py:1030
  372.7 8.8 %collective-permute-start.26 = (bf16[2,48,384]{2,1,0:T(8,128)(2,1)S(1)}, bf16[2,48,384]{2,1,0:T(8,128)(2,1)S(1)}, u32[]{:S(2)}, u32[]{:S(2)}) collective-permute-start(bf16[2,48,384]{2,1,0:T(8,128)(2,1)S(1)} %get-tuple-element.293), channel_id=1, source_target_pairs={{0,2},{1,3},{2,4},{3,5},{4,6},{5,7},{6,0},{7,1},{8,10},{9,11},{10,... | collective-permute-start | bytes 221192 | tf_op jit(solution)/shard_map/ppermute | solution.py:1242
  373.3 9.9 %collective-permute-start.25 = (bf16[2,48,384]{2,1,0:T(8,128)(2,1)S(1)}, bf16[2,48,384]{2,1,0:T(8,128)(2,1)S(1)}, u32[]{:S(2)}, u32[]{:S(2)}) collective-permute-start(bf16[2,48,384]{2,1,0:T(8,128)(2,1)S(1)} %get-tuple-element.294), channel_id=1, source_target_pairs={{0,4},{1,5},{2,6},{3,7},{4,0},{5,1},{6,2},{7,3},{8,12},{9,13},{10,... | collective-permute-start | bytes 221192 | tf_op jit(solution)/shard_map/ppermute | solution.py:1242
  374.6 8.6 %collective-permute-start.24 = (bf16[2,48,384]{2,1,0:T(8,128)(2,1)S(1)}, bf16[2,48,384]{2,1,0:T(8,128)(2,1)S(1)}, u32[]{:S(2)}, u32[]{:S(2)}) collective-permute-start(bf16[2,48,384]{2,1,0:T(8,128)(2,1)S(1)} %get-tuple-element.295), channel_id=1, source_target_pairs={{0,6},{1,7},{2,0},{3,1},{4,2},{5,3},{6,4},{7,5},{8,14},{9,15},{10,... | collective-permute-start | bytes 221192 | tf_op jit(solution)/shard_map/ppermute | solution.py:1242
  384.6 2.0 collective-permute-start.29
  388.0 14.3 %collective-permute-start.30 = (bf16[1,1,48,2304]{3,2,1,0:T(8,128)(2,1)S(1)}, bf16[1,1,48,2304]{3,2,1,0:T(8,128)(2,1)S(1)}, u32[]{:S(2)}, u32[]{:S(2)}) collective-permute-start(bf16[1,1,48,2304]{3,2,1,0:T(8,128)(2,1)S(1)} %maximum_bitcast_fusion), channel_id=1, source_target_pairs={{0,16},{8,24},{16,0},{24,8},{1,17},{9,25},{17,1},{25,9},{2,18},{10... | collective-permute-start | bytes 663560 | tf_op jit(solution)/shard_map/ppermute | solution.py:1030
  389.1 26.5 %collective-permute-start.32 = (bf16[768,512]{1,0:T(8,128)(2,1)S(1)}, bf16[768,512]{1,0:T(8,128)(2,1)S(1)}, u32[]{:S(2)}, u32[]{:S(2)}) collective-permute-start(bf16[768,512]{1,0:T(8,128)(2,1)S(1)} %copy-done.38), channel_id=1, source_target_pairs={{0,8},{8,0},{16,24},{24,16},{1,9},{9,1},{17,25},{25,17},{2,10},{10... | collective-permute-start | bytes 2359304 | tf_op jit(solution)/shard_map/ppermute | solution.py:1030
  389.7 25.9 %collective-permute-start.33 = (bf16[768,512]{1,0:T(8,128)(2,1)S(1)}, bf16[768,512]{1,0:T(8,128)(2,1)S(1)}, u32[]{:S(2)}, u32[]{:S(2)}) collective-permute-start(bf16[768,512]{1,0:T(8,128)(2,1)S(1)} %copy-done.39), channel_id=1, source_target_pairs={{0,16},{8,24},{16,0},{24,8},{1,17},{9,25},{17,1},{25,9},{2,18},{10... | collective-permute-start | bytes 2359304 | tf_op jit(solution)/shard_map/ppermute | solution.py:1030
  390.7 23.5 %collective-permute-start.34 = (bf16[1,1,48,2304]{3,2,1,0:T(8,128)(2,1)S(1)}, bf16[1,1,48,2304]{3,2,1,0:T(8,128)(2,1)S(1)}, u32[]{:S(2)}, u32[]{:S(2)}) collective-permute-start(bf16[1,1,48,2304]{3,2,1,0:T(8,128)(2,1)S(1)} %maximum_bitcast_fusion.1), channel_id=1, source_target_pairs={{0,8},{8,0},{16,24},{24,16},{1,9},{9,1},{17,25},{25,17},{2,10},{10... | collective-permute-start | bytes 663560 | tf_op jit(solution)/shard_map/ppermute | solution.py:1030
  402.5 20.7 %collective-permute-start.31 = (bf16[2,1,48,2304]{3,2,1,0:T(8,128)(2,1)S(1)}, bf16[2,1,48,2304]{3,2,1,0:T(8,128)(2,1)S(1)}, u32[]{:S(2)}, u32[]{:S(2)}) collective-permute-start(bf16[2,1,48,2304]{3,2,1,0:T(8,128)(2,1)S(1)} %pad_maximum_fusion.12), channel_id=1, source_target_pairs={{0,8},{8,0},{16,24},{24,16},{1,9},{9,1},{17,25},{25,17},{2,10},{10... | collective-permute-start | bytes 1327112 | tf_op jit(solution)/shard_map/ppermute | solution.py:1030
  414.3 11.4 %collective-permute-start.35 = (bf16[1,2,48,2304]{3,2,1,0:T(8,128)(2,1)S(1)}, bf16[1,2,48,2304]{3,2,1,0:T(8,128)(2,1)S(1)}, u32[]{:S(2)}, u32[]{:S(2)}) collective-permute-start(bf16[1,2,48,2304]{3,2,1,0:T(8,128)(2,1)S(1)} %pad_maximum_fusion.13), channel_id=1, source_target_pairs={{0,16},{8,24},{16,0},{24,8},{1,17},{9,25},{17,1},{25,9},{2,18},{10... | collective-permute-start | bytes 1327112 | tf_op jit(solution)/shard_map/ppermute | solution.py:1030
  (42 other events, 140.3 us)
Sparse Core Ops, SparseCore 0:
  11.5 59.9 all-gather.10
  73.1 37.1 all-gather.6
  112.5 37.1 all-gather.12
  197.6 41.4 reduce-scatter.2
  251.6 37.8 all-gather.8
  324.1 72.4 reduce-scatter.4

commit v8 on v7

--- a/solution.py
+++ b/solution.py
@@ -914,7 +914,18 @@
     )
 
 
-def head_kernel(copies, side, low_ref, high_ref, query_ref, key_ref, value_ref, out_ref, small_ref):
+def head_kernel(
+    copies,
+    side,
+    low_ref,
+    high_ref,
+    query_ref,
+    key_ref,
+    value_ref,
+    out_ref,
+    gains_ref,
+    router_ref,
+):
     groups = KEY_VALUE_HEADS
     count = groups * copies
     halves = [low_ref[...].astype(jnp.float32), high_ref[...].astype(jnp.float32)]
@@ -931,7 +942,8 @@
             total = total + parts[g * copies + p]
         heads.append(total)
         small = small + total[:, width + 2 * HEAD_SIZE :]
-    small_ref[...] = small
+    gains_ref[...] = jnp.transpose(small[:, :8])
+    router_ref[...] = small[:, 8 : 8 + router_ref.shape[1]]
     query_ref[...] = jnp.concatenate([head[:, :width] for head in heads], 1)
     key_ref[...] = jnp.concatenate([head[:, width : width + HEAD_SIZE] for head in heads], 1)
     value_ref[...] = jnp.concatenate(
@@ -940,7 +952,7 @@
     out_ref[...] = jnp.concatenate([half[:, count // 2 * side :] for half in halves], 1)
 
 
-def head_outputs(low, high, copies, side):
+def head_outputs(low, high, copies, side, experts):
     rows = low.shape[0]
     groups = KEY_VALUE_HEADS
     query_width = QUERY_HEADS * HEAD_SIZE
@@ -953,7 +965,8 @@
             shaped(groups * HEAD_SIZE),
             shaped(groups * HEAD_SIZE),
             shaped(MODEL_WIDTH),
-            shaped(side - (query_width // groups + 2 * HEAD_SIZE)),
+            jax.ShapeDtypeStruct((8, rows), jnp.float32),
+            shaped(experts),
         ),
         compiler_params=pltpu.CompilerParams(vmem_limit_bytes=40 << 20),
         cost_estimate=pl.CostEstimate(flops=0, bytes_accessed=rows, transcendentals=0),
@@ -1056,10 +1069,7 @@
 
     def step(self, *others):
         came = after(self.flying, *others)
-        if self.stage == len(self.order):
-            self.send((self.kept + came.astype(jnp.float32)).astype(jnp.bfloat16))
-        else:
-            self.send(join(self.sent, came, self.order[self.steps - self.stage], 0))
+        self.send(join(self.sent, came, self.order[self.steps - self.stage], 0))
         return self.sent
 
     def piece(self, number, count, *others):
@@ -1069,48 +1079,84 @@
 
 
 def halve_kernel(keeps_ref, *refs):
+    count = len(refs) // 3
     for chain in range(2):
-        kept_ref, other_ref, came_ref, rest_ref = refs[4 * chain : 4 * chain + 4]
-        out_ref, sent_ref = refs[8 + 2 * chain : 10 + 2 * chain]
-        out_ref[...] = kept_ref[...] + came_ref[...].astype(jnp.float32)
-        sent = other_ref[...] + rest_ref[...].astype(jnp.float32)
-        sent_ref[...] = sent.astype(jnp.bfloat16)
+        for place in range(0, count, 2):
+            value_ref, came_ref = refs[count * chain + place : count * chain + place + 2]
+            out_ref = refs[2 * count + chain * (count // 2) + place // 2]
+            out_ref[...] = (value_ref[...] + came_ref[...].astype(jnp.float32)).astype(
+                out_ref.dtype
+            )
 
 
 def halve_chains(chains, *others):
     order = [chain.order[chain.stage] for chain in chains]
+    last = chains[0].stage == len(chains[0].order) - 1
     keeps = jnp.stack([has(bit) for bit in order]).astype(jnp.int32)
     rows, hidden = chains[0].kept.shape
     count = 4
     part = rows // 2 // count
     operands, specs = [], []
     for c, chain in enumerate(chains):
-        came = after(chain.flying, *others)
-        for array in (chain.kept, came):
-            for flip in range(2):
-                operands.append(array)
-                specs.append(
-                    pl.BlockSpec(
-                        (part, hidden), lambda i, k, c=c, flip=flip: ((k[c] ^ flip) * count + i, 0)
-                    )
-                )
+        chain.came = after(chain.flying, *others)
+        for flip in (1,) if last else (1, 0):
+            index = lambda i, k, c=c, flip=flip: ((k[c] ^ flip) * count + i, 0)
+            operands += [chain.kept, chain.came]
+            specs += [pl.BlockSpec((part, hidden), index)] * 2
     block = pl.BlockSpec((part, hidden), lambda i, k: (i, 0))
     shaped = lambda dtype: jax.ShapeDtypeStruct((rows // 2, hidden), dtype)
+    each = [shaped(jnp.bfloat16)] if last else [shaped(jnp.bfloat16), shaped(jnp.float32)]
     outs = pl.pallas_call(
         halve_kernel,
-        out_shape=[shaped(jnp.float32), shaped(jnp.bfloat16)] * 2,
+        out_shape=each * 2,
         grid_spec=pltpu.PrefetchScalarGridSpec(
-            num_scalar_prefetch=1, grid=(count,), in_specs=specs, out_specs=[block] * 4
+            num_scalar_prefetch=1,
+            grid=(count,),
+            in_specs=specs,
+            out_specs=[block] * (2 * len(each)),
         ),
         compiler_params=pltpu.CompilerParams(vmem_limit_bytes=58 << 20),
         cost_estimate=pl.CostEstimate(
-            flops=60000 * rows * hidden, bytes_accessed=24 * rows * hidden, transcendentals=0
+            flops=60000 * rows * hidden, bytes_accessed=12 * rows * hidden, transcendentals=0
         ),
     )(keeps, *operands)
-    for chain, kept, sent in zip(chains, outs[::2], outs[1::2]):
-        chain.kept = kept
-        chain.send(sent)
+    for c, chain in enumerate(chains):
+        if not last:
+            chain.kept = outs[2 * c + 1]
+        chain.send(outs[len(each) * c])
     return [chain.sent for chain in chains]
+
+
+def total_kernel(keeps_ref, *refs):
+    for chain in range(2):
+        kept_ref, first_ref, second_ref = refs[3 * chain : 3 * chain + 3]
+        total = kept_ref[...] + first_ref[...].astype(jnp.float32)
+        refs[6 + chain][...] = (total + second_ref[...].astype(jnp.float32)).astype(jnp.bfloat16)
+
+
+def total_chains(chains, *others):
+    keeps = jnp.stack([has(chain.order[-1]) for chain in chains]).astype(jnp.int32)
+    rows, hidden = chains[0].kept.shape
+    count = 4
+    part = rows // 2 // count
+    block = pl.BlockSpec((part, hidden), lambda i, k: (i, 0))
+    operands, specs = [], []
+    for c, chain in enumerate(chains):
+        stay = pl.BlockSpec((part, hidden), lambda i, k, c=c: (k[c] * count + i, 0))
+        operands += [chain.kept, chain.came, after(chain.flying, *others)]
+        specs += [stay, stay, block]
+    outs = pl.pallas_call(
+        total_kernel,
+        out_shape=[jax.ShapeDtypeStruct((rows // 2, hidden), jnp.bfloat16)] * 2,
+        grid_spec=pltpu.PrefetchScalarGridSpec(
+            num_scalar_prefetch=1, grid=(count,), in_specs=specs, out_specs=[block] * 2
+        ),
+        compiler_params=pltpu.CompilerParams(vmem_limit_bytes=58 << 20),
+        cost_estimate=pl.CostEstimate(flops=0, bytes_accessed=rows, transcendentals=0),
+    )(keeps, *operands)
+    for chain, out in zip(chains, outs):
+        chain.send(out)
+    return list(outs)
 
 
 class Cube:
@@ -1145,6 +1191,135 @@
     def join(self, *others):
         bit = self.order[self.stage]
         self.value = join(self.value, after(self.flying, *others), bit, self.axis(bit))
+
+
+def halve_cubes_kernel(keeps_ref, *refs):
+    for h in range(2):
+        value_ref, came_ref = refs[2 * h : 2 * h + 2]
+        kept_ref, sent_ref = refs[4 + 2 * h : 6 + 2 * h]
+        keep = keeps_ref[h]
+        kept_ref[...] = value_ref[keep] + came_ref[keep].astype(jnp.float32)
+        sent = value_ref[1 - keep] + came_ref[1 - keep].astype(jnp.float32)
+        sent_ref[...] = sent.astype(jnp.bfloat16)
+
+
+def scalar_call(kernel, outs, scalars, *operands, scratch=(), flops=0):
+    whole = lambda array: pl.BlockSpec(array.shape, lambda i, p: (0,) * len(array.shape))
+    return pl.pallas_call(
+        kernel,
+        out_shape=outs,
+        grid_spec=pltpu.PrefetchScalarGridSpec(
+            num_scalar_prefetch=1,
+            grid=(1,),
+            in_specs=[whole(array) for array in operands],
+            out_specs=[whole(out) for out in outs],
+            scratch_shapes=scratch,
+        ),
+        name="scalar_call",
+        compiler_params=pltpu.CompilerParams(vmem_limit_bytes=58 << 20),
+        cost_estimate=pl.CostEstimate(flops=flops, bytes_accessed=1024, transcendentals=0),
+    )(scalars, *operands)
+
+
+def halve_cubes(cubes, *others):
+    share, line = cubes[0].value.shape[-2:]
+    if cubes[0].stage < len(cubes[0].order) - 1:
+        for cube in cubes:
+            cube.add(*others)
+        return [cube.halve() for cube in cubes]
+    order = [cube.order[cube.stage] for cube in cubes]
+    keeps = jnp.stack([has(bit) for bit in order]).astype(jnp.int32)
+    shaped = lambda dtype: jax.ShapeDtypeStruct((share, line), dtype)
+    operands = []
+    for cube in cubes:
+        operands += [cube.value.reshape(2, share, line)]
+        operands += [after(cube.flying, *others).reshape(2, share, line)]
+    outs = scalar_call(
+        halve_cubes_kernel, [shaped(jnp.float32), shaped(jnp.bfloat16)] * 2, keeps, *operands
+    )
+    for h, cube in enumerate(cubes):
+        cube.value, sent = outs[2 * h : 2 * h + 2]
+        cube.flying = swap(sent, order[h])
+        cube.stage += 1
+    return outs[1::2]
+
+
+def pack_kernel(size, side, place_ref, *refs):
+    chips = size // 2
+    values = refs[:4]
+    out_ref = refs[4 + chips]
+    all_ref = refs[5 + chips]
+    for h in range(2):
+        total = values[2 * h][...] + values[2 * h + 1][...].astype(jnp.float32)
+        total = total.astype(jnp.bfloat16)
+        for c in range(chips):
+            all_ref[h * chips + c] = total[:, c * side : (c + 1) * side]
+        out_ref[h] = total[:, chips * side :]
+    for k in range(chips):
+        chip = lax.rem(place_ref[0] - k + chips, chips)
+        for core in range(2):
+            refs[4 + k][core] = all_ref[2 * chip + core]
+
+
+def pack_heads(place, cubes, size, side):
+    chips = size // 2
+    share, line = cubes[0].value.shape[-2:]
+    low = jnp.bfloat16
+    outs = [jax.ShapeDtypeStruct((2, share, side), low)] * chips
+    outs.append(jax.ShapeDtypeStruct((2, share, line - chips * side), low))
+    operands = []
+    for cube in cubes:
+        operands += [cube.value.reshape(share, line), cube.flying.reshape(share, line)]
+    *parcels, out_sums = scalar_call(
+        lambda *refs: pack_kernel(size, side, *refs),
+        outs,
+        place,
+        *operands,
+        scratch=[pltpu.VMEM((size, share, side), low)],
+        flops=200000000000,
+    )
+    return parcels, out_sums
+
+
+def split_kernel(place_ref, *refs):
+    chips = len(refs) - 2
+    core = lax.rem(place_ref[1], 2)
+    for k in range(chips):
+        refs[chips][k] = refs[k][core]
+        refs[chips + 1][k] = refs[k][1 - core]
+
+
+def split_cores(place, got):
+    out = jax.ShapeDtypeStruct((len(got),) + got[0].shape[1:], got[0].dtype)
+    return scalar_call(split_kernel, [out, out], place, *got)
+
+
+def unpack_kernel(place_ref, stay_ref, came_ref, out_ref, low_ref, high_ref, all_ref):
+    chips, _, side = stay_ref.shape
+    core = lax.rem(place_ref[1], 2)
+    for k in range(chips):
+        chip = lax.rem(place_ref[0] + k, chips)
+        all_ref[2 * chip + core] = stay_ref[k]
+        all_ref[2 * chip + 1 - core] = came_ref[k]
+    for h, rows_ref in enumerate((low_ref, high_ref)):
+        for c in range(chips):
+            rows_ref[:, c * side : (c + 1) * side] = all_ref[h * chips + c]
+        rows_ref[:, chips * side :] = out_ref[h]
+
+
+def unpack_heads(place, stay, came, out_sums):
+    chips, share, side = stay.shape
+    line = chips * side + out_sums.shape[2]
+    out = jax.ShapeDtypeStruct((share, line), stay.dtype)
+    return scalar_call(
+        unpack_kernel,
+        [out, out],
+        place,
+        stay,
+        came,
+        out_sums,
+        scratch=[pltpu.VMEM((2 * chips, share, side), stay.dtype)],
+    )
 
 
 class Exchange:
@@ -1369,7 +1544,7 @@
         counted = (places // part == copy_index)[:, None]
         grad_query = jnp.where(counted, grad_query, jnp.zeros((), jnp.bfloat16))
         grad_pair = jnp.where(counted, grad_pair, jnp.zeros((), jnp.bfloat16))
-    sent = [chain.step(grad_pair) for chain in chains]
+    sent = total_chains(chains, grad_pair)
     both_rows, *halves = close_rows(
         place,
         after(grad_query, *sent),
@@ -1400,33 +1575,20 @@
     while chains[0].stage < chains[0].steps:
         sent = [chain.step(*halves) for chain in chains]
     while cubes[0].stage < len(bits):
-        for cube in cubes:
-            cube.add(*sent)
-        sent = [cube.halve() for cube in cubes]
+        sent = halve_cubes(cubes, *sent)
     first = [chain.piece(0, 3) for chain in chains]
     second = [chain.piece(1, 3, *sent) for chain in chains]
     for cube in cubes:
-        cube.add()
-    totals = [cube.value.astype(jnp.bfloat16) for cube in cubes]
-    blocks = jnp.concatenate(
-        [
-            jnp.transpose(
-                total.reshape(share, -1)[:, :line].reshape(share, size // 2, side_width), (1, 0, 2)
-            )
-            for total in totals
-        ],
-        0,
-    )
-    got = deal_chips(after(blocks, *first))
-    head_sums = deal_cores(after(got, *second))
-    for h, cube in enumerate(cubes):
-        rows = jnp.transpose(head_sums[h * (size // 2) : (h + 1) * (size // 2)], (1, 0, 2))
-        rows = jnp.concatenate(
-            [rows.reshape(share, line), totals[h].reshape(share, -1)[:, line:]], 1
-        )
-        cube.value = rows.reshape(totals[h].shape)
+        cube.flying = after(cube.flying, *sent)
+    parcels, out_sums = pack_heads(place, cubes, size, side_width)
+    parcels = after(parcels, *first)
+    got = [parcels[0]] + [from_chip(parcels[k], k) for k in range(1, chips)]
+    stay, go = split_cores(place, got)
+    came = from_core(after(go, *second))
+    for cube, value in zip(cubes, unpack_heads(place, stay, came, out_sums)):
+        cube.value = value.reshape((1,) * len(bits) + value.shape)
     sent = [cube.back() for cube in cubes]
-    third = [chain.piece(2, 3, *sent) for chain in chains]
+    third = [chain.piece(2, 3, *sent, *[cube.flying for cube in cubes]) for chain in chains]
     keeps = place[2:]
     grad_gate, grad_up = [
         into_output(keeps, side, *after((chain.sent, first[side], second[side]), *sent))
@@ -1448,18 +1610,17 @@
         *after((chains[0].sent, third[0], chains[1].sent, third[1]), *sent),
     )
     for cube in cubes:
-        cube.join(grad_down)
+        cube.join(grad_down, output, grad_in)
     head_outs = head_outputs(
-        *[cube.value.reshape(rows_own, -1) for cube in cubes], copies, side_width
-    )
-    small = head_outs[4]
+        *[cube.value.reshape(rows_own, -1) for cube in cubes], copies, side_width, experts_all
+    )
     return (
         output.astype(jnp.bfloat16)[None],
         grad_in[None],
-        small[:, 0],
+        head_outs[4][0],
         *head_outs[:4],
-        small[:, 1],
-        small[:, 8 : 8 + experts_all],
+        head_outs[4][1],
+        head_outs[5],
         grad_gate,
         grad_up,
         grad_down,

time: 443 us -> 460 us (1.038)
  Pallas kernels: 157 us -> 171 us
  waiting for transfers between devices: 146 us -> 158 us
  other arithmetic: 37.7 us -> 30.1 us
    pallas_call x1 -> x6, Pallas kernels: 8.79 us -> 23.3 us  [the longest x4 11.5 us: scalar_call(): pl.pallas_call(kernel, out_shape=outs, grid_spec=pltpu.PrefetchScalarGrid...]
    ppermute x28, waiting for transfers between devices: 94.7 us -> 102 us  [swap(): return lax.ppermute(value, 'rep', [(i, i ^ bit) for i in range(size)])]
    unnamed x98 -> x112, local copies, waits for them, and re-layouts: 9.75 us -> 11.5 us
  transfers between devices with their start and end apart: 42 -> 42, of which waited for: 25 -> 27; matrix products, arithmetic and copies ran while one was open for 10% -> 7% of each run, Pallas kernels for 25% -> 27%
where the time goes in v8:
time: 460 us; the launch traced here: 459 us
  Pallas kernels  171 us (37%)
  waiting for transfers between devices  158 us (34%)
  starting transfers between devices  40.6 us (9%)
  other arithmetic  30.1 us (7%)
  blocking collectives  24.5 us (5%)
  local copies, waits for them, and re-layouts  19.3 us (4%)
  between operations  14.8 us (3%)
    ppermute x28, waiting for transfers between devices, swap(): return lax.ppermute(value, 'rep', [(i, i ^ bit) for i in range(size)])  102 us
    ppermute x28, starting transfers between devices, swap(): return lax.ppermute(value, 'rep', [(i, i ^ bit) for i in range(size)])  33.1 us
    pallas_call x2, Pallas kernels, expert_products(): pl.pallas_call(product_kernel, out_shape=(jax.ShapeDtypeStruct((rows, hid...  28.8 us
    all_to_all x1, blocking collectives, per_device(): lax.all_to_all(head_columns, 'ctx', split_axis=0, concat_axis=0, tiled=True)  24.5 us
    pallas_call x1, Pallas kernels, expert_rows(): pl.pallas_call(expert_kernel, out_shape=(wide, wide, wide, wide, jax.Shap...  20.5 us
    all_gather x1, waiting for transfers between devices, per_device(): gathered = lax.all_gather(rows, 'ctx', axis=0)  16.5 us
    ppermute x6, waiting for transfers between devices, from_chip(): lax.ppermute(value, 'ctx', [(i, (i - 2 * k) % size) for i in range(size)])  15.9 us
    pallas_call x1, Pallas kernels, attend(): pl.pallas_call(attend_kernel, out_shape=(shaped((tokens, features), jnp.b...  15.3 us
  transfers between devices with their start and end apart: 42, of which 27 were waited for; matrix products, arithmetic and copies ran while one was open for 7% of the time, Pallas kernels for 27%

profile of v8, /device:TPU:0, one launch (start us, length us, event | category | flops | bytes accessed | tf_op | source)
XLA Modules:
  0.0 458.9 jit_solution(15185456744524300171)
XLA Ops:
  9.5 1.9 fusion.14
  15.3 24.5 %all_to_all.5 = bf16[8,48,384]{2,1,0:T(8,128)(2,1)S(1)} all-to-all(bf16[8,48,384]{2,1,0:T(8,128)(2,1)S(1)} %copy.54), channel_id=1, replica_groups=mesh['rep'=4,'ctx'=8] {'ctx'}, dimensions={0} | all-to-all | bytes 589824 | tf_op jit(solution)/shard_map/all_to_all | solution.py:1442
  42.9 2.8 collective-permute-done
  49.4 5.6 %collective-permute-done.3 = bf16[4,2,1,48,384]{4,3,0,2,1:T(8,128)(2,1)S(1)} collective-permute-done((bf16[4,2,1,48,384]{4,3,0,2,1:T(8,128)(2,1)S(1)}, bf16[4,2,1,48,384]{4,3,0,2,1:T(8,128)(2,1)S(1)}, u32[]{:S(2)}, u32[]{:S(2)}) %collective-permute-start.3) | collective-permute-done | bytes 294944 | tf_op jit(solution)/shard_map/ppermute | solution.py:1043
  55.0 16.5 %all-gather.11.cloned.1.call-done = bf16[1408,1664]{1,0:T(8,128)(2,1)} async-done(((bf16[176,1664]{1,0:T(8,128)(2,1)}), bf16[1408,1664]{1,0:T(8,128)(2,1)}) %all-gather.11.cloned.1.call-update) | async-done | bytes 4685840 | tf_op jit(solution)/shard_map/all_gather | solution.py:1413
  78.0 15.3 %shard_map.238 = (bf16[1024,1536]{1,0:T(8,128)(2,1)}, bf16[1024,192]{1,0:T(8,128)(2,1)S(1)}, bf16[1024,64]{1,0:T(8,128)(2,1)S(1)}, bf16[1024,64]{1,0:T(8,128)(2,...) custom-call(bf16[8,176,1664]{2,1,0:T(8,128)(2,1)} %bitcast.130, ...), custom_call_target="tpu_custom_call" | custom-call | bytes 1024 | tf_op jit(solution)/shard_map/pallas_call | solution.py:194
  93.3 2.3 broadcast_select_fusion.9
  98.2 12.1 %all-gather.7.cloned.1.call-done.cotangent_ref = bf16[1024,1536]{1,0:T(8,128)(2,1)} async-done(((bf16[128,1536]{1,0:T(8,128)(2,1)}), bf16[1024,1536]{1,0:T(8,128)(2,1)}) %all-gather.7.cloned.1.call-update) | async-done | bytes 3145744 | tf_op jit(solution)/shard_map/all_gather | solution.py:1414
  115.1 23.7 %collective-permute-done.6 = bf16[4,1,2,48,1536]{4,3,0,2,1:T(8,128)(2,1)S(1)} collective-permute-done((bf16[4,1,2,48,1536]{4,3,0,2,1:T(8,128)(2,1)}, bf16[4,1,2,48,1536]{4,3,0,2,1:T(8,128)(2,1)S(1)}, u32[]{:S(2)}, u32[]{:S(2)}) %collective-permute-start.6) | collective-permute-done | bytes 1179680 | tf_op jit(solution)/shard_map/ppermute | solution.py:1043
  141.2 1.6 copy.58
  142.8 6.9 %all-gather.13.cloned.1.call-done = bf16[4096,384]{1,0:T(8,128)(2,1)} async-done(((bf16[512,384]{1,0:T(8,128)(2,1)}), bf16[4096,384]{1,0:T(8,128)(2,1)}) %all-gather.13.cloned.1.call-update) | async-done | bytes 3145744 | tf_op jit(solution)/shard_map/all_gather | solution.py:1464
  149.7 1.7 copy-done.4
  152.4 11.0 %shard_map.239 = (f32[1024,1536]{1,0:T(8,128)}, bf16[1024,1536]{1,0:T(8,128)(2,1)}, f32[1024,16]{1,0:T(8,128)S(1)}) custom-call(bf16[8,512,384]{2,1,0:T(8,128)(2,1)} %bitcast.154, bf16[768,1536]{1,0:T(8,128)(2,1)S(1)} %bitcast.122, bf16[768,1536]{1,0:T(8,128)(2,1)S(1)} %bitcast.125, bf16[8,176,1664]{2,1,0:T(8,128)(2,1)} %bitcast.133, ...), custom_call_target="tpu_custom_call" | custom-call | flops 4831838208 | bytes 18874368 | tf_op jit(solution)/shard_map/pallas_call | solution.py:401
  163.4 20.5 %shard_map.240 = (bf16[2,1024,512]{2,1,0:T(8,128)(2,1)}, bf16[2,1024,512]{2,1,0:T(8,128)(2,1)}, bf16[2,1024,512]{2,1,0:T(8,128)(2,1)}, bf16[2,1024,512]{2,1,0:T(...) custom-call(s32[4]{0:T(128)S(1)} %pad_add_fusion.place_ref.refs_0_, ...), custom_call_target="tpu_custom_call" | custom-call | flops 9663676416 | bytes 25165824 | tf_op jit(solution)/shard_map/pallas_call | solution.py:495
  183.9 13.7 %shard_map.241 = bf16[1024,1664]{1,0:T(8,128)(2,1)} custom-call(s32[4]{0:T(128)S(1)} %pad_add_fusion.place_ref.refs_0_, bf16[2,1024,512]{2,1,0:T(8,128)(2,1)} %get-tuple-element.120.grad_gate_ref.gate_ref, bf16[2,1024,512]{2,1,0:T(8,128)(2,1)} %get-tuple-element.121.grad_up_ref.up_ref, bf16[1024,128]{1,0:T(8,128)(2,1)S(1)} %get-tuple-element.122.extra_ref, ...), custom_call_target="tpu_custom_call" | custom-call | bytes 1024 | tf_op jit(solution)/shard_map/pallas_call | solution.py:628
  197.8 13.5 %shard_map.242 = (bf16[2304,512]{1,0:T(8,128)(2,1)}, bf16[2304,512]{1,0:T(8,128)(2,1)}) custom-call(bf16[1024,1536]{1,0:T(8,128)(2,1)} %get-tuple-element.130.normed_ref.left_ref.refs_7_, bf16[2,1024,512]{2,1,0:T(8,128)(2,1)} %get-tuple-element.120.grad_gate_ref.gate_ref, bf16[2,1024,512]{2,1,0:T(8,128)(2,1)} %get-tuple-element.121.grad_up_ref.up_ref, ...), custom_call_target="tpu_custom_call" | custom-call | bytes 1024 | tf_op jit(solution)/shard_map/pallas_call | solution.py:585
  214.3 15.2 %shard_map.243 = (f32[2304,512]{1,0:T(8,128)}, f32[2304,512]{1,0:T(8,128)}) custom-call(bf16[1024,1536]{1,0:T(8,128)(2,1)} %get-tuple-element.130.normed_ref.left_ref.refs_7_, bf16[2,1024,512]{2,1,0:T(8,128)(2,1)} %get-tuple-element.120.grad_gate_ref.gate_ref, bf16[2,1024,512]{2,1,0:T(8,128)(2,1)} %get-tuple-element.121.grad_up_ref.up_ref, ...), custom_call_target="tpu_custom_call" | custom-call | bytes 1024 | tf_op jit(solution)/shard_map/pallas_call | solution.py:585
  229.6 8.9 %shard_map.244.refs_9_ = bf16[1024,1536]{1,0:T(8,128)(2,1)} custom-call(s32[4]{0:T(128)S(1)} %pad_add_fusion.place_ref.refs_0_, bf16[2,1024,512]{2,1,0:T(8,128)(2,1)} %get-tuple-element.134.scaled_one_ref.scaled_ref, bf16[2,512,1536]{2,1,0:T(8,128)(2,1)} %down_weight_ref.3), custom_call_target="tpu_custom_call" | custom-call | bytes 1024 | tf_op jit(solution)/shard_map/pallas_call | solution.py:665
  239.2 6.8 %shard_map.245 = (f32[128,1536]{1,0:T(8,128)}, bf16[128,1536]{1,0:T(8,128)(2,1)}, bf16[8,128,192]{2,1,0:T(8,128)(2,1)}, bf16[128,16]{1,0:T(8,128)(2,1)}, f32[1,1536]{1,0:T(1,128)}) custom-call(s32[4]{0:T(128)} %copy-done.22, bf16[128,1664]{1,0:T(8,128)(2,1)} %reduce-scatter.3.cloned.1.call-done.sum_ref, f32[1024,16]{1,0:T(8,128)} %copy-done.15, ...), custom_call_target="tpu_custom_call" | custom-call | bytes 128 | tf_op jit(solution)/shard_map/pallas_call | solution.py:736
  248.1 2.8 collective-permute-start.8
  251.6 3.8 collective-permute-done.10
  255.4 3.6 collective-permute-done.9
  259.1 5.9 %collective-permute-done.11.refs_1_ = bf16[2304,512]{1,0:T(8,128)(2,1)} collective-permute-done((bf16[2304,512]{1,0:T(8,128)(2,1)}, bf16[2304,512]{1,0:T(8,128)(2,1)}, u32[]{:S(2)}, u32[]{:S(2)}) %collective-permute-start.11) | collective-permute-done | bytes 2359328 | tf_op jit(solution)/shard_map/ppermute | solution.py:1043
  266.3 5.7 %shard_map.246 = (bf16[1152,512]{1,0:T(8,128)(2,1)}, bf16[1152,512]{1,0:T(8,128)(2,1)}) custom-call(s32[2]{0:T(128)} %add_convert_fusion.keeps_ref, f32[2304,512]{1,0:T(8,128)} %get-tuple-element.132.refs_0_, bf16[2304,512]{1,0:T(8,128)(2,1)} %collective-permute-done.11.refs_1_, f32[2304,512]{1,0:T(8,128)} %get-tuple-element.133.refs_2_.refs_3_, ...), custom_call_target="tpu_custom_call" | custom-call | flops 70778880000 | bytes 14155776 | tf_op jit(solution)/shard_map/pallas_call | solution.py:1109
  274.8 1.7 collective-permute-done.13
  276.9 13.1 %shard_map.247 = (bf16[1024,192]{1,0:T(8,128)(2,1)S(1)}, bf16[1024,128]{1,0:T(8,128)(2,1)S(1)}) custom-call(bf16[1024,192]{1,0:T(8,128)(2,1)S(1)} %copy-done.14, bf16[1024,192]{1,0:T(8,128)(2,1)S(1)} %bitcast.128, f32[3,1024,1]{2,1,0:T(8,128)S(1)} %copy-done.10, f32[1024,64]{1,0:T(8,128)S(1)} %copy-done.6, f32[1024,64]{1,0:T(8,128)S(1)} %copy-done.8, ...), custom_call_target="tpu_custom_call" | custom-call | bytes 1024 | tf_op jit(solution)/shard_map/pallas_call | solution.py:323
  291.6 7.7 %collective-permute-done.14.refs_2_ = bf16[1152,512]{1,0:T(8,128)(2,1)} collective-permute-done((bf16[1152,512]{1,0:T(8,128)(2,1)}, bf16[1152,512]{1,0:T(8,128)(2,1)}, u32[]{:S(2)}, u32[]{:S(2)}) %collective-permute-start.14) | collective-permute-done | bytes 1179680 | tf_op jit(solution)/shard_map/ppermute | solution.py:1043
  300.5 6.1 %shard_map.248 = (bf16[1152,512]{1,0:T(8,128)(2,1)}, bf16[1152,512]{1,0:T(8,128)(2,1)}) custom-call(s32[2]{0:T(128)} %add_convert_fusion.keeps_ref, f32[2304,512]{1,0:T(8,128)} %get-tuple-element.132.refs_0_, bf16[2304,512]{1,0:T(8,128)(2,1)} %collective-permute-done.11.refs_1_, bf16[1152,512]{1,0:T(8,128)(2,1)} %collective-permute-done.14.refs_2_, ...), custom_call_target="tpu_custom_call" | custom-call | bytes 2304 | tf_op jit(solution)/shard_map/pallas_call | solution.py:1148
  308.9 14.6 %close.1 = (bf16[1024,3072]{1,0:T(8,128)(2,1)}, f32[96,2304]{1,0:T(8,128)}, f32[96,2304]{1,0:T(8,128)}, bf16[96,2304]{1,0:T(8,128)(2,1)}, bf16[96,2304]{1,0:T(8,128)(2,1)}) custom-call(s32[4]{0:T(128)} %copy-done.22, bf16[1024,192]{1,0:T(8,128)(2,1)} %copy-done.16, bf16[1024,128]{1,0:T(8,128)(2,1)} %copy-done.17, ...), custom_call_target="tpu_custom_call" | custom-call | bytes 1024 | tf_op jit(solution)/shard_map/close/pallas_call | solution.py:865
  325.0 7.7 %collective-permute-done.17 = bf16[1152,512]{1,0:T(8,128)(2,1)} collective-permute-done((bf16[1152,512]{1,0:T(8,128)(2,1)}, bf16[1152,512]{1,0:T(8,128)(2,1)}, u32[]{:S(2)}, u32[]{:S(2)}) %collective-permute-start.17) | collective-permute-done | bytes 1179680 | tf_op jit(solution)/shard_map/ppermute | solution.py:1043
  334.3 2.0 collective-permute-done.18
  336.4 1.6 collective-permute-start.19
  341.8 3.9 collective-permute-done.16
  346.6 3.6 scalar_call.4
  355.7 3.1 collective-permute-done.20.refs_2_
  360.3 7.0 %collective-permute-done.21.refs_4_ = bf16[48,2304]{1,0:T(8,128)(2,1)S(1)} collective-permute-done((bf16[48,2304]{1,0:T(8,128)(2,1)}, bf16[48,2304]{1,0:T(8,128)(2,1)S(1)}, u32[]{:S(2)}, u32[]{:S(2)}) %collective-permute-start.21) | collective-permute-done | bytes 221216 | tf_op jit(solution)/shard_map/ppermute | solution.py:1043
  368.0 3.0 scalar_call.5
  371.0 4.8 %collective-permute-done.23.refs_1_ = bf16[768,512]{1,0:T(8,128)(2,1)} collective-permute-done((bf16[768,512]{1,0:T(8,128)(2,1)}, bf16[768,512]{1,0:T(8,128)(2,1)}, u32[]{:S(2)}, u32[]{:S(2)}) %collective-permute-start.23) | collective-permute-done | bytes 786464 | tf_op jit(solution)/shard_map/ppermute | solution.py:1043
  378.9 3.3 collective-permute-done.24.refs_1_
  382.2 4.2 collective-permute-done.25.refs_2_
  388.0 2.4 scalar_call.6
  392.7 2.5 scalar_call.7
  397.4 5.1 %into_output.2 = f32[2,1536,512]{2,1,0:T(8,128)} custom-call(s32[2]{0:T(128)S(1)} %pad_add_fusion.1.k.keeps_ref, bf16[2304,512]{1,0:T(8,128)(2,1)S(1)} %pad_maximum_fusion.refs_0_.sent_low_ref, bf16[768,512]{1,0:T(8,128)(2,1)} %collective-permute-done.22.refs_1_, bf16[768,512]{1,0:T(8,128)(2,1)} %collective-permute-done.27.refs_2_), custom_call_target="tpu_custom_call" | custom-call | bytes 768 | tf_op jit(solution)/shard_map/into_output/pallas_call | solution.py:985
  402.6 5.0 %into_output.3 = f32[2,1536,512]{2,1,0:T(8,128)} custom-call(s32[2]{0:T(128)S(1)} %pad_add_fusion.1.k.keeps_ref, bf16[2304,512]{1,0:T(8,128)(2,1)S(1)} %copy-done.2, bf16[768,512]{1,0:T(8,128)(2,1)} %collective-permute-done.23.refs_1_, bf16[768,512]{1,0:T(8,128)(2,1)} %collective-permute-done.28.refs_2_), custom_call_target="tpu_custom_call" | custom-call | bytes 768 | tf_op jit(solution)/shard_map/into_output/pallas_call | solution.py:985
  413.5 23.7 %collective-permute-done.33.came_low_ref = bf16[768,512]{1,0:T(8,128)(2,1)S(1)} collective-permute-done((bf16[768,512]{1,0:T(8,128)(2,1)S(1)}, bf16[768,512]{1,0:T(8,128)(2,1)S(1)}, u32[]{:S(2)}, u32[]{:S(2)}) %collective-permute-start.33) | collective-permute-done | bytes 786464 | tf_op jit(solution)/shard_map/ppermute | solution.py:1043
  437.2 3.5 shard_map.249
  444.3 2.0 fusion.13
  448.7 2.0 head_outputs.1
  (254 shorter events, 84.3 us)
Async XLA Ops:
  7.2 64.3 %all-gather.11.cloned.1.call-start = ((), (), s32[]{:S(2)}) async-start(), calls=%async_computation.7 | async-start | bytes 5271552 | tf_op jit(solution)/shard_map/all_gather | solution.py:1413
  11.4 98.9 %all-gather.7.cloned.1.call-start = ((), (), s32[]{:S(2)}) async-start(), calls=%async_computation.3 | async-start | bytes 3538944 | tf_op jit(solution)/shard_map/all_gather | solution.py:1414
  12.1 137.6 %all-gather.13.cloned.1.call-start = ((), (), s32[]{:S(2)}) async-start(), calls=%async_computation.8 | async-start | bytes 3538944 | tf_op jit(solution)/shard_map/all_gather | solution.py:1464
  39.8 5.9 %collective-permute-start = (bf16[4,1,1,48,384]{4,3,0,2,1:T(8,128)(2,1)S(1)}, bf16[4,1,1,48,384]{4,3,0,2,1:T(8,128)(2,1)S(1)}, u32[]{:S(2)}, u32[]{:S(2)}) collective-permute-start(bf16[4,1,1,48,384]{4,3,0,2,1:T(8,128)(2,1)S(1)} %get-tuple-element.300), channel_id=1, source_target_pairs={{0,8},{8,0},{16,24},{24,16},{1,9},{9,1},{17,25},{25,17},{2,10},{10... | collective-permute-start | bytes 442376 | tf_op jit(solution)/shard_map/ppermute | solution.py:1043
  41.4 5.5 %collective-permute-start.2 = (bf16[4,1,1,48,384]{4,3,0,2,1:T(8,128)(2,1)S(1)}, bf16[4,1,1,48,384]{4,3,0,2,1:T(8,128)(2,1)S(1)}, u32[]{:S(2)}, u32[]{:S(2)}) collective-permute-start(bf16[4,1,1,48,384]{4,3,0,2,1:T(8,128)(2,1)S(1)} %get-tuple-element.301), channel_id=1, source_target_pairs={{0,16},{8,24},{16,0},{24,8},{1,17},{9,25},{17,1},{25,9},{2,18},{10... | collective-permute-start | bytes 442376 | tf_op jit(solution)/shard_map/ppermute | solution.py:1043
  47.0 8.0 %collective-permute-start.3 = (bf16[4,2,1,48,384]{4,3,0,2,1:T(8,128)(2,1)S(1)}, bf16[4,2,1,48,384]{4,3,0,2,1:T(8,128)(2,1)S(1)}, u32[]{:S(2)}, u32[]{:S(2)}) collective-permute-start(bf16[4,2,1,48,384]{4,3,0,2,1:T(8,128)(2,1)S(1)} %pad_maximum_fusion.15), channel_id=1, source_target_pairs={{0,8},{8,0},{16,24},{24,16},{1,9},{9,1},{17,25},{25,17},{2,10},{10... | collective-permute-start | bytes 884744 | tf_op jit(solution)/shard_map/ppermute | solution.py:1043
  47.8 28.3 %collective-permute-start.1 = (bf16[4,1,2,48,384]{4,3,0,2,1:T(8,128)(2,1)S(1)}, bf16[4,1,2,48,384]{4,3,0,2,1:T(8,128)(2,1)S(1)}, u32[]{:S(2)}, u32[]{:S(2)}) collective-permute-start(bf16[4,1,2,48,384]{4,3,0,2,1:T(8,128)(2,1)S(1)} %pad_maximum_fusion.14), channel_id=1, source_target_pairs={{0,16},{8,24},{16,0},{24,8},{1,17},{9,25},{17,1},{25,9},{2,18},{10... | collective-permute-start | bytes 884744 | tf_op jit(solution)/shard_map/ppermute | solution.py:1043
  72.8 20.5 %collective-permute-start.5 = (bf16[4,1,1,48,1536]{4,3,0,2,1:T(8,128)(2,1)S(1)}, bf16[4,1,1,48,1536]{4,3,0,2,1:T(8,128)(2,1)S(1)}, u32[]{:S(2)}, u32[]{:S(2)}) collective-permute-start(bf16[4,1,1,48,1536]{4,3,0,2,1:T(8,128)(2,1)S(1)} %get-tuple-element.260), channel_id=1, source_target_pairs={{0,16},{8,24},{16,0},{24,8},{1,17},{9,25},{17,1},{25,9},{2,18},{10... | collective-permute-start | bytes 1769480 | tf_op jit(solution)/shard_map/ppermute | solution.py:1043
  74.4 18.9 %collective-permute-start.4 = (bf16[4,1,1,48,1536]{4,3,0,2,1:T(8,128)(2,1)S(1)}, bf16[4,1,1,48,1536]{4,3,0,2,1:T(8,128)(2,1)S(1)}, u32[]{:S(2)}, u32[]{:S(2)}) collective-permute-start(bf16[4,1,1,48,1536]{4,3,0,2,1:T(8,128)(2,1)S(1)} %get-tuple-element.261), channel_id=1, source_target_pairs={{0,8},{8,0},{16,24},{24,16},{1,9},{9,1},{17,25},{25,17},{2,10},{10... | collective-permute-start | bytes 1769480 | tf_op jit(solution)/shard_map/ppermute | solution.py:1043
  110.3 128.8 %reduce-scatter.3.cloned.1.call-start = ((), (), s32[]{:S(2)}) async-start(), calls=%async_computation.4 | async-start | bytes 3833856 | tf_op jit(solution)/shard_map/reduce_scatter | solution.py:1490
  110.4 28.4 %collective-permute-start.6 = (bf16[4,1,2,48,1536]{4,3,0,2,1:T(8,128)(2,1)}, bf16[4,1,2,48,1536]{4,3,0,2,1:T(8,128)(2,1)S(1)}, u32[]{:S(2)}, u32[]{:S(2)}) collective-permute-start(bf16[4,1,2,48,1536]{4,3,0,2,1:T(8,128)(2,1)} %pad_maximum_fusion.5), channel_id=1, source_target_pairs={{0,16},{8,24},{16,0},{24,8},{1,17},{9,25},{17,1},{25,9},{2,18},{10... | collective-permute-start | bytes 3538952 | tf_op jit(solution)/shard_map/ppermute | solution.py:1043
  111.9 28.0 %collective-permute-start.7 = (bf16[4,2,1,48,1536]{4,3,0,2,1:T(8,128)(2,1)}, bf16[4,2,1,48,1536]{4,3,0,2,1:T(8,128)(2,1)S(1)}, u32[]{:S(2)}, u32[]{:S(2)}) collective-permute-start(bf16[4,2,1,48,1536]{4,3,0,2,1:T(8,128)(2,1)} %pad_maximum_fusion.6), channel_id=1, source_target_pairs={{0,8},{8,0},{16,24},{24,16},{1,9},{9,1},{17,25},{25,17},{2,10},{10... | collective-permute-start | bytes 3538952 | tf_op jit(solution)/shard_map/ppermute | solution.py:1043
  113.5 116.1 %copy-start.22 = (s32[4]{0:T(128)}, s32[4]{0:T(128)S(1)}, u32[]{:S(2)}) copy-start(s32[4]{0:T(128)S(1)} %pad_add_fusion.place_ref.refs_0_) | copy-start | bytes 52
  114.2 35.5 %copy-start.23 = (f32[1,1536]{1,0:T(1,128)}, f32[1,1536]{1,0:T(1,128)S(1)}, u32[]{:S(2)}) copy-start(f32[1,1536]{1,0:T(1,128)S(1)} %reshape.291.gain_ref) | copy-start | bytes 18436
  163.4 20.5 %copy-start.15 = (f32[1024,16]{1,0:T(8,128)}, f32[1024,16]{1,0:T(8,128)S(1)}, u32[]{:S(2)}) copy-start(f32[1024,16]{1,0:T(8,128)S(1)} %get-tuple-element.119.gates_ref) | copy-start | bytes 196612
  197.6 111.3 %all-gather.9.cloned.1.call-start = ((), (), s32[]{:S(2)}) async-start(), calls=%async_computation.5 | async-start | bytes 3538944 | tf_op jit(solution)/shard_map/all_gather | solution.py:1510
  211.3 53.7 %collective-permute-start.11 = (bf16[2304,512]{1,0:T(8,128)(2,1)}, bf16[2304,512]{1,0:T(8,128)(2,1)}, u32[]{:S(2)}, u32[]{:S(2)}) collective-permute-start(bf16[2304,512]{1,0:T(8,128)(2,1)} %get-tuple-element.128), channel_id=1, source_target_pairs={{0,8},{8,0},{16,24},{24,16},{1,9},{9,1},{17,25},{25,17},{2,10},{10... | collective-permute-start | bytes 7077896 | tf_op jit(solution)/shard_map/ppermute | solution.py:1043
  212.9 53.4 %collective-permute-start.12 = (bf16[2304,512]{1,0:T(8,128)(2,1)}, bf16[2304,512]{1,0:T(8,128)(2,1)}, u32[]{:S(2)}, u32[]{:S(2)}) collective-permute-start(bf16[2304,512]{1,0:T(8,128)(2,1)} %get-tuple-element.129), channel_id=1, source_target_pairs={{0,16},{8,24},{16,0},{24,8},{1,17},{9,25},{17,1},{25,9},{2,18},{10... | collective-permute-start | bytes 7077896 | tf_op jit(solution)/shard_map/ppermute | solution.py:1043
  247.1 8.3 %collective-permute-start.10 = (bf16[2,128,192]{2,1,0:T(8,128)(2,1)S(1)}, bf16[2,128,192]{2,1,0:T(8,128)(2,1)S(1)}, u32[]{:S(2)}, u32[]{:S(2)}) collective-permute-start(bf16[2,128,192]{2,1,0:T(8,128)(2,1)S(1)} %get-tuple-element.287), channel_id=1, source_target_pairs={{0,2},{1,3},{2,4},{3,5},{4,6},{5,7},{6,0},{7,1},{8,10},{9,11},{10,... | collective-permute-start | bytes 294920 | tf_op jit(solution)/shard_map/ppermute | solution.py:1417
  247.1 11.9 %collective-permute-start.9 = (bf16[2,128,192]{2,1,0:T(8,128)(2,1)S(1)}, bf16[2,128,192]{2,1,0:T(8,128)(2,1)S(1)}, u32[]{:S(2)}, u32[]{:S(2)}) collective-permute-start(bf16[2,128,192]{2,1,0:T(8,128)(2,1)S(1)} %get-tuple-element.288), channel_id=1, source_target_pairs={{0,4},{1,5},{2,6},{3,7},{4,0},{5,1},{6,2},{7,3},{8,12},{9,13},{10,... | collective-permute-start | bytes 294920 | tf_op jit(solution)/shard_map/ppermute | solution.py:1417
  248.1 10.9 %collective-permute-start.8 = (bf16[2,128,192]{2,1,0:T(8,128)(2,1)S(1)}, bf16[2,128,192]{2,1,0:T(8,128)(2,1)S(1)}, u32[]{:S(2)}, u32[]{:S(2)}) collective-permute-start(bf16[2,128,192]{2,1,0:T(8,128)(2,1)S(1)} %get-tuple-element.289), channel_id=1, source_target_pairs={{0,6},{1,7},{2,0},{3,1},{4,2},{5,3},{6,4},{7,5},{8,14},{9,15},{10,... | collective-permute-start | bytes 294920 | tf_op jit(solution)/shard_map/ppermute | solution.py:1417
  251.5 189.1 %reduce-scatter.5.cloned.1.call-start = ((), (), s32[]{:S(2)}) async-start(), calls=%async_computation.6 | async-start | bytes 7077888 | tf_op jit(solution)/shard_map/reduce_scatter | solution.py:1565
  272.0 27.3 %collective-permute-start.14 = (bf16[1152,512]{1,0:T(8,128)(2,1)}, bf16[1152,512]{1,0:T(8,128)(2,1)}, u32[]{:S(2)}, u32[]{:S(2)}) collective-permute-start(bf16[1152,512]{1,0:T(8,128)(2,1)} %get-tuple-element.141), channel_id=1, source_target_pairs={{0,16},{8,24},{16,0},{24,8},{1,17},{9,25},{17,1},{25,9},{2,18},{10... | collective-permute-start | bytes 3538952 | tf_op jit(solution)/shard_map/ppermute | solution.py:1043
  273.4 27.0 %collective-permute-start.15 = (bf16[1152,512]{1,0:T(8,128)(2,1)}, bf16[1152,512]{1,0:T(8,128)(2,1)}, u32[]{:S(2)}, u32[]{:S(2)}) collective-permute-start(bf16[1152,512]{1,0:T(8,128)(2,1)} %get-tuple-element.142), channel_id=1, source_target_pairs={{0,8},{8,0},{16,24},{24,16},{1,9},{9,1},{17,25},{25,17},{2,10},{10... | collective-permute-start | bytes 3538952 | tf_op jit(solution)/shard_map/ppermute | solution.py:1043
  274.8 1.7 collective-permute-start.13
  306.6 26.1 %collective-permute-start.17 = (bf16[1152,512]{1,0:T(8,128)(2,1)}, bf16[1152,512]{1,0:T(8,128)(2,1)}, u32[]{:S(2)}, u32[]{:S(2)}) collective-permute-start(bf16[1152,512]{1,0:T(8,128)(2,1)} %get-tuple-element.154), channel_id=1, source_target_pairs={{0,16},{8,24},{16,0},{24,8},{1,17},{9,25},{17,1},{25,9},{2,18},{10... | collective-permute-start | bytes 3538952 | tf_op jit(solution)/shard_map/ppermute | solution.py:1043
  307.1 29.1 %collective-permute-start.18 = (bf16[1152,512]{1,0:T(8,128)(2,1)}, bf16[1152,512]{1,0:T(8,128)(2,1)S(1)}, u32[]{:S(2)}, u32[]{:S(2)}) collective-permute-start(bf16[1152,512]{1,0:T(8,128)(2,1)} %get-tuple-element.155), channel_id=1, source_target_pairs={{0,8},{8,0},{16,24},{24,16},{1,9},{9,1},{17,25},{25,17},{2,10},{10... | collective-permute-start | bytes 3538952 | tf_op jit(solution)/shard_map/ppermute | solution.py:1043
  323.5 22.1 %collective-permute-start.16 = (bf16[2,1,48,2304]{3,2,0,1:T(8,128)(2,1)}, bf16[2,1,48,2304]{3,2,0,1:T(8,128)(2,1)S(1)}, u32[]{:S(2)}, u32[]{:S(2)}) collective-permute-start(bf16[2,1,48,2304]{3,2,0,1:T(8,128)(2,1)} %bitcast.38), channel_id=1, source_target_pairs={{0,8},{8,0},{16,24},{24,16},{1,9},{9,1},{17,25},{25,17},{2,10},{10... | collective-permute-start | bytes 1327112 | tf_op jit(solution)/shard_map/ppermute | solution.py:1043
  336.4 9.3 %collective-permute-start.19 = (bf16[1,2,48,2304]{3,2,1,0:T(8,128)(2,1)S(1)}, bf16[1,2,48,2304]{3,2,1,0:T(8,128)(2,1)S(1)}, u32[]{:S(2)}, u32[]{:S(2)}) collective-permute-start(bf16[1,2,48,2304]{3,2,1,0:T(8,128)(2,1)S(1)} %bitcast.155), channel_id=1, source_target_pairs={{0,16},{8,24},{16,0},{24,8},{1,17},{9,25},{17,1},{25,9},{2,18},{10... | collective-permute-start | bytes 1327112 | tf_op jit(solution)/shard_map/ppermute | solution.py:1043
  339.6 31.4 %collective-permute-start.22 = (bf16[768,512]{1,0:T(8,128)(2,1)}, bf16[768,512]{1,0:T(8,128)(2,1)}, u32[]{:S(2)}, u32[]{:S(2)}) collective-permute-start(bf16[768,512]{1,0:T(8,128)(2,1)} %get-tuple-element.275), channel_id=1, source_target_pairs={{0,8},{8,0},{16,24},{24,16},{1,9},{9,1},{17,25},{25,17},{2,10},{10... | collective-permute-start | bytes 2359304 | tf_op jit(solution)/shard_map/ppermute | solution.py:1043
  350.2 8.6 %collective-permute-start.20 = (bf16[48,2304]{1,0:T(8,128)(2,1)}, bf16[48,2304]{1,0:T(8,128)(2,1)S(1)}, u32[]{:S(2)}, u32[]{:S(2)}) collective-permute-start(bf16[48,2304]{1,0:T(8,128)(2,1)} %get-tuple-element.173), channel_id=1, source_target_pairs={{0,16},{8,24},{16,0},{24,8},{1,17},{9,25},{17,1},{25,9},{2,18},{10... | collective-permute-start | bytes 663560 | tf_op jit(solution)/shard_map/ppermute | solution.py:1043
  351.7 15.6 %collective-permute-start.21 = (bf16[48,2304]{1,0:T(8,128)(2,1)}, bf16[48,2304]{1,0:T(8,128)(2,1)S(1)}, u32[]{:S(2)}, u32[]{:S(2)}) collective-permute-start(bf16[48,2304]{1,0:T(8,128)(2,1)} %get-tuple-element.174), channel_id=1, source_target_pairs={{0,8},{8,0},{16,24},{24,16},{1,9},{9,1},{17,25},{25,17},{2,10},{10... | collective-permute-start | bytes 663560 | tf_op jit(solution)/shard_map/ppermute | solution.py:1043
  353.8 22.0 %collective-permute-start.23 = (bf16[768,512]{1,0:T(8,128)(2,1)}, bf16[768,512]{1,0:T(8,128)(2,1)}, u32[]{:S(2)}, u32[]{:S(2)}) collective-permute-start(bf16[768,512]{1,0:T(8,128)(2,1)} %get-tuple-element.272), channel_id=1, source_target_pairs={{0,16},{8,24},{16,0},{24,8},{1,17},{9,25},{17,1},{25,9},{2,18},{10... | collective-permute-start | bytes 2359304 | tf_op jit(solution)/shard_map/ppermute | solution.py:1043
  354.3 36.1 %collective-permute-start.27 = (bf16[768,512]{1,0:T(8,128)(2,1)}, bf16[768,512]{1,0:T(8,128)(2,1)}, u32[]{:S(2)}, u32[]{:S(2)}) collective-permute-start(bf16[768,512]{1,0:T(8,128)(2,1)} %get-tuple-element.188), channel_id=1, source_target_pairs={{0,8},{8,0},{16,24},{24,16},{1,9},{9,1},{17,25},{25,17},{2,10},{10... | collective-permute-start | bytes 2359304 | tf_op jit(solution)/shard_map/ppermute | solution.py:1043
  358.8 31.6 %collective-permute-start.28 = (bf16[768,512]{1,0:T(8,128)(2,1)}, bf16[768,512]{1,0:T(8,128)(2,1)}, u32[]{:S(2)}, u32[]{:S(2)}) collective-permute-start(bf16[768,512]{1,0:T(8,128)(2,1)} %get-tuple-element.189), channel_id=1, source_target_pairs={{0,16},{8,24},{16,0},{24,8},{1,17},{9,25},{17,1},{25,9},{2,18},{10... | collective-permute-start | bytes 2359304 | tf_op jit(solution)/shard_map/ppermute | solution.py:1043
  368.0 22.6 %copy-start.24 = (bf16[1,128,1536]{2,1,0:T(8,128)(2,1)S(1)}, bf16[1,128,1536]{2,1,0:T(8,128)(2,1)}, u32[]{:S(2)}) copy-start(bf16[1,128,1536]{2,1,0:T(8,128)(2,1)} %param.15) | copy-start | bytes 1179652
  375.7 6.5 %collective-permute-start.24 = (bf16[2,48,384]{2,1,0:T(8,128)(2,1)}, bf16[2,48,384]{2,1,0:T(8,128)(2,1)S(1)}, u32[]{:S(2)}, u32[]{:S(2)}) collective-permute-start(bf16[2,48,384]{2,1,0:T(8,128)(2,1)} %get-tuple-element.183), channel_id=1, source_target_pairs={{0,6},{1,7},{2,0},{3,1},{4,2},{5,3},{6,4},{7,5},{8,14},{9,15},{10,... | collective-permute-start | bytes 221192 | tf_op jit(solution)/shard_map/ppermute | solution.py:1417
  376.9 9.5 %collective-permute-start.25 = (bf16[2,48,384]{2,1,0:T(8,128)(2,1)}, bf16[2,48,384]{2,1,0:T(8,128)(2,1)S(1)}, u32[]{:S(2)}, u32[]{:S(2)}) collective-permute-start(bf16[2,48,384]{2,1,0:T(8,128)(2,1)} %get-tuple-element.184), channel_id=1, source_target_pairs={{0,4},{1,5},{2,6},{3,7},{4,0},{5,1},{6,2},{7,3},{8,12},{9,13},{10,... | collective-permute-start | bytes 221192 | tf_op jit(solution)/shard_map/ppermute | solution.py:1417
  377.7 9.6 %collective-permute-start.26 = (bf16[2,48,384]{2,1,0:T(8,128)(2,1)}, bf16[2,48,384]{2,1,0:T(8,128)(2,1)S(1)}, u32[]{:S(2)}, u32[]{:S(2)}) collective-permute-start(bf16[2,48,384]{2,1,0:T(8,128)(2,1)} %get-tuple-element.185), channel_id=1, source_target_pairs={{0,2},{1,3},{2,4},{3,5},{4,6},{5,7},{6,0},{7,1},{8,10},{9,11},{10,... | collective-permute-start | bytes 221192 | tf_op jit(solution)/shard_map/ppermute | solution.py:1417
  390.4 1.6 collective-permute-start.29
  395.2 12.4 %collective-permute-start.30 = (bf16[1,1,48,2304]{3,2,1,0:T(8,128)(2,1)}, bf16[1,1,48,2304]{3,2,1,0:T(8,128)(2,1)S(1)}, u32[]{:S(2)}, u32[]{:S(2)}) collective-permute-start(bf16[1,1,48,2304]{3,2,1,0:T(8,128)(2,1)} %bitcast.148), channel_id=1, source_target_pairs={{0,16},{8,24},{16,0},{24,8},{1,17},{9,25},{17,1},{25,9},{2,18},{10... | collective-permute-start | bytes 663560 | tf_op jit(solution)/shard_map/ppermute | solution.py:1043
  396.7 13.0 %collective-permute-start.32 = (bf16[1,1,48,2304]{3,2,1,0:T(8,128)(2,1)}, bf16[1,1,48,2304]{3,2,1,0:T(8,128)(2,1)S(1)}, u32[]{:S(2)}, u32[]{:S(2)}) collective-permute-start(bf16[1,1,48,2304]{3,2,1,0:T(8,128)(2,1)} %bitcast.147), channel_id=1, source_target_pairs={{0,8},{8,0},{16,24},{24,16},{1,9},{9,1},{17,25},{25,17},{2,10},{10... | collective-permute-start | bytes 663560 | tf_op jit(solution)/shard_map/ppermute | solution.py:1043
  408.5 37.8 %collective-permute-start.31 = (bf16[2,1,48,2304]{3,2,1,0:T(8,128)(2,1)}, bf16[2,1,48,2304]{3,2,1,0:T(8,128)(2,1)}, u32[]{:S(2)}, u32[]{:S(2)}) collective-permute-start(bf16[2,1,48,2304]{3,2,1,0:T(8,128)(2,1)} %pad_maximum_fusion.12), channel_id=1, source_target_pairs={{0,8},{8,0},{16,24},{24,16},{1,9},{9,1},{17,25},{25,17},{2,10},{10... | collective-permute-start | bytes 1327112 | tf_op jit(solution)/shard_map/ppermute | solution.py:1043
  409.8 27.4 %collective-permute-start.33 = (bf16[768,512]{1,0:T(8,128)(2,1)S(1)}, bf16[768,512]{1,0:T(8,128)(2,1)S(1)}, u32[]{:S(2)}, u32[]{:S(2)}) collective-permute-start(bf16[768,512]{1,0:T(8,128)(2,1)S(1)} %copy-done.35), channel_id=1, source_target_pairs={{0,8},{8,0},{16,24},{24,16},{1,9},{9,1},{17,25},{25,17},{2,10},{10... | collective-permute-start | bytes 2359304 | tf_op jit(solution)/shard_map/ppermute | solution.py:1043
  410.5 26.7 %collective-permute-start.34 = (bf16[768,512]{1,0:T(8,128)(2,1)S(1)}, bf16[768,512]{1,0:T(8,128)(2,1)S(1)}, u32[]{:S(2)}, u32[]{:S(2)}) collective-permute-start(bf16[768,512]{1,0:T(8,128)(2,1)S(1)} %copy-done.36), channel_id=1, source_target_pairs={{0,16},{8,24},{16,0},{24,8},{1,17},{9,25},{17,1},{25,9},{2,18},{10... | collective-permute-start | bytes 2359304 | tf_op jit(solution)/shard_map/ppermute | solution.py:1043
  411.1 26.1 %copy-start.29 = (bf16[1,1,48,2304]{3,2,1,0:T(8,128)(2,1)}, bf16[1,1,48,2304]{3,2,1,0:T(8,128)(2,1)S(1)}, u32[]{:S(2)}) copy-start(bf16[1,1,48,2304]{3,2,1,0:T(8,128)(2,1)S(1)} %get-tuple-element.290) | copy-start | bytes 663556
  411.1 26.1 %copy-start.31 = (bf16[1,1,48,2304]{3,2,1,0:T(8,128)(2,1)}, bf16[1,1,48,2304]{3,2,1,0:T(8,128)(2,1)S(1)}, u32[]{:S(2)}) copy-start(bf16[1,1,48,2304]{3,2,1,0:T(8,128)(2,1)S(1)} %get-tuple-element.291) | copy-start | bytes 663556
  412.0 35.4 %collective-permute-start.35 = (bf16[1,2,48,2304]{3,2,1,0:T(8,128)(2,1)}, bf16[1,2,48,2304]{3,2,1,0:T(8,128)(2,1)}, u32[]{:S(2)}, u32[]{:S(2)}) collective-permute-start(bf16[1,2,48,2304]{3,2,1,0:T(8,128)(2,1)} %pad_maximum_fusion.13), channel_id=1, source_target_pairs={{0,16},{8,24},{16,0},{24,8},{1,17},{9,25},{17,1},{25,9},{2,18},{10... | collective-permute-start | bytes 1327112 | tf_op jit(solution)/shard_map/ppermute | solution.py:1043
  (49 other events, 145.8 us)
Sparse Core Ops, SparseCore 0:
  11.5 59.9 all-gather.10
  73.1 37.1 all-gather.6
  112.5 37.1 all-gather.12
  197.7 41.4 reduce-scatter.2
  251.7 37.9 all-gather.8
  323.7 73.2 reduce-scatter.4

commit v9 on v7

--- a/solution.py
+++ b/solution.py
@@ -914,7 +914,18 @@
     )
 
 
-def head_kernel(copies, side, low_ref, high_ref, query_ref, key_ref, value_ref, out_ref, small_ref):
+def head_kernel(
+    copies,
+    side,
+    low_ref,
+    high_ref,
+    query_ref,
+    key_ref,
+    value_ref,
+    out_ref,
+    gains_ref,
+    router_ref,
+):
     groups = KEY_VALUE_HEADS
     count = groups * copies
     halves = [low_ref[...].astype(jnp.float32), high_ref[...].astype(jnp.float32)]
@@ -931,7 +942,8 @@
             total = total + parts[g * copies + p]
         heads.append(total)
         small = small + total[:, width + 2 * HEAD_SIZE :]
-    small_ref[...] = small
+    gains_ref[...] = jnp.transpose(small[:, :8])
+    router_ref[...] = small[:, 8 : 8 + router_ref.shape[1]]
     query_ref[...] = jnp.concatenate([head[:, :width] for head in heads], 1)
     key_ref[...] = jnp.concatenate([head[:, width : width + HEAD_SIZE] for head in heads], 1)
     value_ref[...] = jnp.concatenate(
@@ -940,7 +952,7 @@
     out_ref[...] = jnp.concatenate([half[:, count // 2 * side :] for half in halves], 1)
 
 
-def head_outputs(low, high, copies, side):
+def head_outputs(low, high, copies, side, experts):
     rows = low.shape[0]
     groups = KEY_VALUE_HEADS
     query_width = QUERY_HEADS * HEAD_SIZE
@@ -953,71 +965,89 @@
             shaped(groups * HEAD_SIZE),
             shaped(groups * HEAD_SIZE),
             shaped(MODEL_WIDTH),
-            shaped(side - (query_width // groups + 2 * HEAD_SIZE)),
+            jax.ShapeDtypeStruct((8, rows), jnp.float32),
+            shaped(experts),
         ),
         compiler_params=pltpu.CompilerParams(vmem_limit_bytes=40 << 20),
         cost_estimate=pl.CostEstimate(flops=0, bytes_accessed=rows, transcendentals=0),
     )(low, high)
 
 
-def into_kernel(keeps_ref, side, sent_ref, first_ref, second_ref, out_ref):
-    kept = pl.program_id(0) == keeps_ref[side]
-    came = jnp.where(pl.program_id(1) == 0, first_ref[...], second_ref[...])
-    out_ref[...] = jnp.where(kept, sent_ref[...], came).astype(jnp.float32)
-
-
-def into_output(keeps, side, sent, first, second):
-    rows, hidden = first.shape
-    part = lambda index: pl.BlockSpec((rows, hidden), index)
+def upper_rows(flags_ref, side, own_ref, came_ref, rows):
+    return jnp.where(flags_ref[2 + side] > 0, own_ref[rows, :], came_ref[rows, :])
+
+
+def into_kernel(flags_ref, side, own_ref, came_ref, low_ref, high_ref, out_ref):
+    rows = own_ref.shape[0]
+    rest = out_ref.shape[0] - rows
+    kept = pl.program_id(0) == flags_ref[side]
+
+    @pl.when(kept)
+    def _():
+        low = jnp.where(flags_ref[2 + side] > 0, came_ref[...], own_ref[...])
+        out_ref[:rows, :] = low.astype(jnp.float32)
+        high = upper_rows(flags_ref, side, own_ref, came_ref, slice(0, rest))
+        out_ref[rows:, :] = high.astype(jnp.float32)
+
+    @pl.when(jnp.logical_not(kept))
+    def _():
+        out_ref[:rows, :] = low_ref[...].astype(jnp.float32)
+        out_ref[rows:, :] = high_ref[:rest, :].astype(jnp.float32)
+
+
+def into_output(flags, side, own, came, low, high):
+    rows, hidden = own.shape
+    total = 2 * rows * 2 // 3
+    whole = lambda array: pl.BlockSpec(array.shape, lambda e, k: (0, 0))
     return pl.pallas_call(
         lambda k, *refs: into_kernel(k, side, *refs),
         name="into_output",
-        out_shape=jax.ShapeDtypeStruct((2, 2 * rows, hidden), jnp.float32),
-        grid_spec=pltpu.PrefetchScalarGridSpec(
-            num_scalar_prefetch=1,
-            grid=(2, 2),
-            in_specs=[
-                part(lambda e, h, k: (h, 0)),
-                part(lambda e, h, k: (0, 0)),
-                part(lambda e, h, k: (0, 0)),
-            ],
-            out_specs=pl.BlockSpec((None, rows, hidden), lambda e, h, k: (e, h, 0)),
-        ),
-        compiler_params=pltpu.CompilerParams(vmem_limit_bytes=32 << 20),
-        cost_estimate=pl.CostEstimate(flops=0, bytes_accessed=rows, transcendentals=0),
-    )(keeps, sent, first, second)
-
-
-def down_kernel(keeps_ref, sent_low_ref, came_low_ref, sent_high_ref, came_high_ref, out_ref):
-    rows, hidden = came_low_ref.shape
-    narrow = hidden // 2
-    pairs = ((sent_low_ref, came_low_ref), (sent_high_ref, came_high_ref))
-    for side, (sent_ref, came_ref) in enumerate(pairs):
-        kept = pl.program_id(0) == keeps_ref[side]
-        value = jnp.where(kept, sent_ref[...], came_ref[...]).astype(jnp.float32)
-        start = side * rows
-        out_ref[:, start : start + hidden] = value[:hidden]
-        out_ref[:narrow, start + hidden : start + rows] = value[hidden:, :narrow]
-        out_ref[narrow:, start + hidden : start + rows] = value[hidden:, narrow:]
-
-
-def down_output(keeps, sent_low, came_low, sent_high, came_high):
-    rows, hidden = came_low.shape
-    place = sent_low.shape[0] // rows - 1
-    sent = pl.BlockSpec((rows, hidden), lambda e, k: (place, 0))
-    came = pl.BlockSpec((rows, hidden), lambda e, k: (0, 0))
-    return pl.pallas_call(
-        down_kernel,
-        out_shape=jax.ShapeDtypeStruct((2, hidden, 2 * rows), jnp.float32),
+        out_shape=jax.ShapeDtypeStruct((2, total, hidden), jnp.float32),
         grid_spec=pltpu.PrefetchScalarGridSpec(
             num_scalar_prefetch=1,
             grid=(2,),
-            in_specs=[sent, came, sent, came],
-            out_specs=pl.BlockSpec((None, hidden, 2 * rows), lambda e, k: (e, 0, 0)),
-        ),
-        compiler_params=pltpu.CompilerParams(vmem_limit_bytes=32 << 20),
+            in_specs=[whole(own), whole(came), whole(low), whole(high)],
+            out_specs=pl.BlockSpec((None, total, hidden), lambda e, k: (e, 0, 0)),
+        ),
+        compiler_params=pltpu.CompilerParams(vmem_limit_bytes=40 << 20),
         cost_estimate=pl.CostEstimate(flops=0, bytes_accessed=rows, transcendentals=0),
-    )(keeps, sent_low, came_low, sent_high, came_high)
+    )(flags, own, came, low, high)
+
+
+def down_kernel(flags_ref, *refs):
+    out_ref = refs[8]
+    hidden = out_ref.shape[0]
+    narrow = hidden // 2
+    for side in range(2):
+        own_ref, came_ref, high_ref, last_ref = refs[4 * side : 4 * side + 4]
+        rows = own_ref.shape[0]
+        rest = rows - out_ref.shape[1] // 2
+        mine = upper_rows(flags_ref, side, own_ref, came_ref, slice(rest, rows))
+        theirs = jnp.concatenate([high_ref[rest:, :], last_ref[...]], 0)
+        kept = pl.program_id(0) == flags_ref[side]
+        value = jnp.where(kept, mine, theirs).astype(jnp.float32)
+        start = side * value.shape[0]
+        out_ref[:, start : start + hidden] = value[:hidden]
+        middle, end = start + hidden, start + value.shape[0]
+        out_ref[:narrow, middle:end] = value[hidden:, :narrow]
+        out_ref[narrow:, middle:end] = value[hidden:, narrow:]
+
+
+def down_output(flags, *operands):
+    rows, hidden = operands[0].shape
+    whole = lambda array: pl.BlockSpec(array.shape, lambda e, k: (0, 0))
+    return pl.pallas_call(
+        down_kernel,
+        out_shape=jax.ShapeDtypeStruct((2, hidden, 3 * hidden), jnp.float32),
+        grid_spec=pltpu.PrefetchScalarGridSpec(
+            num_scalar_prefetch=1,
+            grid=(2,),
+            in_specs=[whole(array) for array in operands],
+            out_specs=pl.BlockSpec((None, hidden, 3 * hidden), lambda e, k: (e, 0, 0)),
+        ),
+        compiler_params=pltpu.CompilerParams(vmem_limit_bytes=40 << 20),
+        cost_estimate=pl.CostEstimate(flops=0, bytes_accessed=rows, transcendentals=0),
+    )(flags, *operands)
 
 
 def after(values, *others):
@@ -1056,61 +1086,104 @@
 
     def step(self, *others):
         came = after(self.flying, *others)
-        if self.stage == len(self.order):
-            self.send((self.kept + came.astype(jnp.float32)).astype(jnp.bfloat16))
-        else:
-            self.send(join(self.sent, came, self.order[self.steps - self.stage], 0))
+        self.send(join(self.sent, came, self.order[self.steps - self.stage], 0))
         return self.sent
 
-    def piece(self, number, count, *others):
-        rows = self.sent.shape[0] // count
-        part = after(self.sent[number * rows : (number + 1) * rows], *others)
-        return swap(part, self.order[0])
+    def ends(self, *others):
+        self.own = self.sent
+        self.came = after(self.flying, *others)
+        bit = self.order[1]
+        half = self.own.shape[0] // 2
+        low = jnp.where(has(bit), self.came, self.own)
+        pieces = [low] + [
+            jnp.where(has(bit), self.own[rows], self.came[rows])
+            for rows in (slice(0, half), slice(half, 2 * half))
+        ]
+        return pieces
+
+    def last(self, piece):
+        return swap(piece, self.order[0])
 
 
 def halve_kernel(keeps_ref, *refs):
+    count = len(refs) // 3
     for chain in range(2):
-        kept_ref, other_ref, came_ref, rest_ref = refs[4 * chain : 4 * chain + 4]
-        out_ref, sent_ref = refs[8 + 2 * chain : 10 + 2 * chain]
-        out_ref[...] = kept_ref[...] + came_ref[...].astype(jnp.float32)
-        sent = other_ref[...] + rest_ref[...].astype(jnp.float32)
-        sent_ref[...] = sent.astype(jnp.bfloat16)
+        for place in range(0, count, 2):
+            value_ref, came_ref = refs[count * chain + place : count * chain + place + 2]
+            out_ref = refs[2 * count + chain * (count // 2) + place // 2]
+            out_ref[...] = (value_ref[...] + came_ref[...].astype(jnp.float32)).astype(
+                out_ref.dtype
+            )
 
 
 def halve_chains(chains, *others):
     order = [chain.order[chain.stage] for chain in chains]
+    last = chains[0].stage == len(chains[0].order) - 1
     keeps = jnp.stack([has(bit) for bit in order]).astype(jnp.int32)
     rows, hidden = chains[0].kept.shape
     count = 4
     part = rows // 2 // count
     operands, specs = [], []
     for c, chain in enumerate(chains):
-        came = after(chain.flying, *others)
-        for array in (chain.kept, came):
-            for flip in range(2):
-                operands.append(array)
-                specs.append(
-                    pl.BlockSpec(
-                        (part, hidden), lambda i, k, c=c, flip=flip: ((k[c] ^ flip) * count + i, 0)
-                    )
-                )
+        chain.came = after(chain.flying, *others)
+        for flip in (1,) if last else (1, 0):
+            index = lambda i, k, c=c, flip=flip: ((k[c] ^ flip) * count + i, 0)
+            operands += [chain.kept, chain.came]
+            specs += [pl.BlockSpec((part, hidden), index)] * 2
     block = pl.BlockSpec((part, hidden), lambda i, k: (i, 0))
     shaped = lambda dtype: jax.ShapeDtypeStruct((rows // 2, hidden), dtype)
+    each = [shaped(jnp.bfloat16)] if last else [shaped(jnp.bfloat16), shaped(jnp.float32)]
     outs = pl.pallas_call(
         halve_kernel,
-        out_shape=[shaped(jnp.float32), shaped(jnp.bfloat16)] * 2,
+        out_shape=each * 2,
         grid_spec=pltpu.PrefetchScalarGridSpec(
-            num_scalar_prefetch=1, grid=(count,), in_specs=specs, out_specs=[block] * 4
+            num_scalar_prefetch=1,
+            grid=(count,),
+            in_specs=specs,
+            out_specs=[block] * (2 * len(each)),
         ),
         compiler_params=pltpu.CompilerParams(vmem_limit_bytes=58 << 20),
         cost_estimate=pl.CostEstimate(
-            flops=60000 * rows * hidden, bytes_accessed=24 * rows * hidden, transcendentals=0
+            flops=60000 * rows * hidden, bytes_accessed=12 * rows * hidden, transcendentals=0
         ),
     )(keeps, *operands)
-    for chain, kept, sent in zip(chains, outs[::2], outs[1::2]):
-        chain.kept = kept
-        chain.send(sent)
+    for c, chain in enumerate(chains):
+        if not last:
+            chain.kept = outs[2 * c + 1]
+        chain.send(outs[len(each) * c])
     return [chain.sent for chain in chains]
+
+
+def total_kernel(keeps_ref, *refs):
+    for chain in range(2):
+        kept_ref, first_ref, second_ref = refs[3 * chain : 3 * chain + 3]
+        total = kept_ref[...] + first_ref[...].astype(jnp.float32)
+        refs[6 + chain][...] = (total + second_ref[...].astype(jnp.float32)).astype(jnp.bfloat16)
+
+
+def total_chains(chains, *others):
+    keeps = jnp.stack([has(chain.order[-1]) for chain in chains]).astype(jnp.int32)
+    rows, hidden = chains[0].kept.shape
+    count = 4
+    part = rows // 2 // count
+    block = pl.BlockSpec((part, hidden), lambda i, k: (i, 0))
+    operands, specs = [], []
+    for c, chain in enumerate(chains):
+        stay = pl.BlockSpec((part, hidden), lambda i, k, c=c: (k[c] * count + i, 0))
+        operands += [chain.kept, chain.came, after(chain.flying, *others)]
+        specs += [stay, stay, block]
+    outs = pl.pallas_call(
+        total_kernel,
+        out_shape=[jax.ShapeDtypeStruct((rows // 2, hidden), jnp.bfloat16)] * 2,
+        grid_spec=pltpu.PrefetchScalarGridSpec(
+            num_scalar_prefetch=1, grid=(count,), in_specs=specs, out_specs=[block] * 2
+        ),
+        compiler_params=pltpu.CompilerParams(vmem_limit_bytes=58 << 20),
+        cost_estimate=pl.CostEstimate(flops=0, bytes_accessed=rows, transcendentals=0),
+    )(keeps, *operands)
+    for chain, out in zip(chains, outs):
+        chain.send(out)
+    return list(outs)
 
 
 class Cube:
@@ -1369,7 +1442,7 @@
         counted = (places // part == copy_index)[:, None]
         grad_query = jnp.where(counted, grad_query, jnp.zeros((), jnp.bfloat16))
         grad_pair = jnp.where(counted, grad_pair, jnp.zeros((), jnp.bfloat16))
-    sent = [chain.step(grad_pair) for chain in chains]
+    sent = total_chains(chains, grad_pair)
     both_rows, *halves = close_rows(
         place,
         after(grad_query, *sent),
@@ -1397,14 +1470,16 @@
         Cube(halves[h], halves[2 + h], order, share)
         for h, order in enumerate((bits, bits[::-1]))
     ]
-    while chains[0].stage < chains[0].steps:
+    while chains[0].stage < chains[0].steps - 1:
         sent = [chain.step(*halves) for chain in chains]
+    pieces = [chain.ends(*halves) for chain in chains]
+    sent = [part[0] for part in pieces]
     while cubes[0].stage < len(bits):
         for cube in cubes:
             cube.add(*sent)
         sent = [cube.halve() for cube in cubes]
-    first = [chain.piece(0, 3) for chain in chains]
-    second = [chain.piece(1, 3, *sent) for chain in chains]
+    first = [chain.last(part[0]) for chain, part in zip(chains, pieces)]
+    second = [chain.last(after(part[1], *sent)) for chain, part in zip(chains, pieces)]
     for cube in cubes:
         cube.add()
     totals = [cube.value.astype(jnp.bfloat16) for cube in cubes]
@@ -1426,14 +1501,17 @@
         )
         cube.value = rows.reshape(totals[h].shape)
     sent = [cube.back() for cube in cubes]
-    third = [chain.piece(2, 3, *sent) for chain in chains]
-    keeps = place[2:]
+    third = [
+        chain.last(after(part[2], *sent)) for chain, part in zip(chains, pieces)
+    ]
+    flags = jnp.stack([flag(chain.order[n]) for n in range(2) for chain in chains])
+    came = [cube.flying for cube in cubes]
     grad_gate, grad_up = [
-        into_output(keeps, side, *after((chain.sent, first[side], second[side]), *sent))
+        into_output(flags, side, *after((chain.own, chain.came, first[side], second[side]), *came))
         for side, chain in enumerate(chains)
     ]
     for cube in cubes:
-        cube.join(grad_gate, grad_up)
+        cube.join(*sent)
     while cubes[0].stage > 0:
         sent = [cube.back() for cube in cubes]
         if cubes[0].stage > 0:
@@ -1443,23 +1521,22 @@
     own_hidden = inputs[0].astype(jnp.float32)
     own_scale = lax.rsqrt(jnp.mean(own_hidden * own_hidden, -1, keepdims=True) + EPS)
     grad_in = grad_middle + norm_back(grad_one * gain_one, own_hidden * own_scale, own_scale)
-    grad_down = down_output(
-        keeps,
-        *after((chains[0].sent, third[0], chains[1].sent, third[1]), *sent),
-    )
+    operands = []
+    for side, chain in enumerate(chains):
+        operands += [chain.own, chain.came, second[side], third[side]]
+    grad_down = down_output(flags, *after(operands, *sent))
     for cube in cubes:
         cube.join(grad_down)
     head_outs = head_outputs(
-        *[cube.value.reshape(rows_own, -1) for cube in cubes], copies, side_width
-    )
-    small = head_outs[4]
+        *[cube.value.reshape(rows_own, -1) for cube in cubes], copies, side_width, experts_all
+    )
     return (
         output.astype(jnp.bfloat16)[None],
         grad_in[None],
-        small[:, 0],
+        head_outs[4][0],
         *head_outs[:4],
-        small[:, 1],
-        small[:, 8 : 8 + experts_all],
+        head_outs[4][1],
+        head_outs[5],
         grad_gate,
         grad_up,
         grad_down,

time: 443 us -> 457 us (1.032)
  Pallas kernels: 157 us -> 164 us
  waiting for transfers between devices: 146 us -> 153 us
  other arithmetic: 37.7 us -> 32.2 us
    ppermute x28, waiting for transfers between devices: 94.7 us -> 104 us  [swap(): return lax.ppermute(value, 'rep', [(i, i ^ bit) for i in range(size)])]
    select_n x0 -> x4, other arithmetic: none -> 5.8 us  [the longest x2 3.52 us: ends(): jnp.where(has(bit), self.own[rows], self.came[rows])]
    pallas_call x2 -> x3, Pallas kernels: 12.3 us -> 16.9 us  [the longest x1 6.11 us: total_chains(): pl.pallas_call(total_kernel, out_shape=[jax.ShapeDtypeStruct((rows // 2,...]
    unnamed x98 -> x90, local copies, waits for them, and re-layouts: 9.75 us -> 9.27 us
  transfers between devices with their start and end apart: 42 -> 42, of which waited for: 25 -> 24; matrix products, arithmetic and copies ran while one was open for 10% -> 9% of each run, Pallas kernels for 25% -> 26%
where the time goes in v9:
time: 457 us; the launch traced here: 456 us
  Pallas kernels  164 us (36%)
  waiting for transfers between devices  153 us (33%)
  starting transfers between devices  43.2 us (9%)
  other arithmetic  32.2 us (7%)
  local copies, waits for them, and re-layouts  24.6 us (5%)
  blocking collectives  24.5 us (5%)
  between operations  15 us (3%)
    ppermute x28, waiting for transfers between devices, swap(): return lax.ppermute(value, 'rep', [(i, i ^ bit) for i in range(size)])  104 us
    ppermute x28, starting transfers between devices, swap(): return lax.ppermute(value, 'rep', [(i, i ^ bit) for i in range(size)])  34.9 us
    pallas_call x2, Pallas kernels, expert_products(): pl.pallas_call(product_kernel, out_shape=(jax.ShapeDtypeStruct((rows, hid...  28.8 us
    all_to_all x1, blocking collectives, per_device(): lax.all_to_all(head_columns, 'ctx', split_axis=0, concat_axis=0, tiled=True)  24.5 us
    pallas_call x1, Pallas kernels, expert_rows(): pl.pallas_call(expert_kernel, out_shape=(wide, wide, wide, wide, jax.Shap...  20.6 us
    all_gather x1, waiting for transfers between devices, per_device(): gathered = lax.all_gather(rows, 'ctx', axis=0)  16.5 us
    pallas_call x1, Pallas kernels, attend(): pl.pallas_call(attend_kernel, out_shape=(shaped((tokens, features), jnp.b...  16 us
    pallas_call x1, Pallas kernels, close_rows(): pl.pallas_call(lambda *refs: close_kernel(reps, *refs), name='close', out...  14.6 us
  transfers between devices with their start and end apart: 42, of which 24 were waited for; matrix products, arithmetic and copies ran while one was open for 9% of the time, Pallas kernels for 26%

profile of v9, /device:TPU:0, one launch (start us, length us, event | category | flops | bytes accessed | tf_op | source)
XLA Modules:
  0.0 455.8 jit_solution(14190009586161461195)
XLA Ops:
  9.5 1.9 fusion.14
  15.3 24.5 %all_to_all.5 = bf16[8,48,384]{2,1,0:T(8,128)(2,1)S(1)} all-to-all(bf16[8,48,384]{2,1,0:T(8,128)(2,1)S(1)} %copy.103), channel_id=1, replica_groups=mesh['rep'=4,'ctx'=8] {'ctx'}, dimensions={0} | all-to-all | bytes 589824 | tf_op jit(solution)/shard_map/all_to_all | solution.py:1340
  42.9 2.8 collective-permute-done
  49.4 5.6 %collective-permute-done.3 = bf16[4,2,1,48,384]{4,3,0,2,1:T(8,128)(2,1)S(1)} collective-permute-done((bf16[4,2,1,48,384]{4,3,0,2,1:T(8,128)(2,1)S(1)}, bf16[4,2,1,48,384]{4,3,0,2,1:T(8,128)(2,1)S(1)}, u32[]{:S(2)}, u32[]{:S(2)}) %collective-permute-start.3) | collective-permute-done | bytes 294944 | tf_op jit(solution)/shard_map/ppermute | solution.py:1060
  55.0 16.5 %all-gather.11.cloned.1.call-done = bf16[1408,1664]{1,0:T(8,128)(2,1)} async-done(((bf16[176,1664]{1,0:T(8,128)(2,1)}), bf16[1408,1664]{1,0:T(8,128)(2,1)}) %all-gather.11.cloned.1.call-update) | async-done | bytes 4685840 | tf_op jit(solution)/shard_map/all_gather | solution.py:1311
  77.4 16.0 %shard_map.238 = (bf16[1024,1536]{1,0:T(8,128)(2,1)}, bf16[1024,192]{1,0:T(8,128)(2,1)S(1)}, bf16[1024,64]{1,0:T(8,128)(2,1)S(1)}, bf16[1024,64]{1,0:T(8,128)(2,...) custom-call(bf16[8,176,1664]{2,1,0:T(8,128)(2,1)} %bitcast.179, ...), custom_call_target="tpu_custom_call" | custom-call | bytes 1024 | tf_op jit(solution)/shard_map/pallas_call | solution.py:194
  93.5 2.3 broadcast_select_fusion.7
  98.4 11.9 %all-gather.7.cloned.1.call-done.cotangent_ref = bf16[1024,1536]{1,0:T(8,128)(2,1)} async-done(((bf16[128,1536]{1,0:T(8,128)(2,1)}), bf16[1024,1536]{1,0:T(8,128)(2,1)}) %all-gather.7.cloned.1.call-update) | async-done | bytes 3145744 | tf_op jit(solution)/shard_map/all_gather | solution.py:1312
  115.1 23.8 %collective-permute-done.6 = bf16[4,1,2,48,1536]{4,3,0,2,1:T(8,128)(2,1)} collective-permute-done((bf16[4,1,2,48,1536]{4,3,0,2,1:T(8,128)(2,1)}, bf16[4,1,2,48,1536]{4,3,0,2,1:T(8,128)(2,1)}, u32[]{:S(2)}, u32[]{:S(2)}) %collective-permute-start.6) | collective-permute-done | bytes 1179680 | tf_op jit(solution)/shard_map/ppermute | solution.py:1060
  142.6 1.7 copy.107
  144.3 5.4 %all-gather.13.cloned.1.call-done = bf16[4096,384]{1,0:T(8,128)(2,1)} async-done(((bf16[512,384]{1,0:T(8,128)(2,1)}), bf16[4096,384]{1,0:T(8,128)(2,1)}) %all-gather.13.cloned.1.call-update) | async-done | bytes 3145744 | tf_op jit(solution)/shard_map/all_gather | solution.py:1362
  149.7 1.7 copy-done.5
  152.4 11.0 %shard_map.239 = (f32[1024,1536]{1,0:T(8,128)}, bf16[1024,1536]{1,0:T(8,128)(2,1)}, f32[1024,16]{1,0:T(8,128)S(1)}) custom-call(bf16[8,512,384]{2,1,0:T(8,128)(2,1)} %bitcast.209, bf16[768,1536]{1,0:T(8,128)(2,1)S(1)} %bitcast.171, bf16[768,1536]{1,0:T(8,128)(2,1)S(1)} %bitcast.174, bf16[8,176,1664]{2,1,0:T(8,128)(2,1)} %bitcast.182, ...), custom_call_target="tpu_custom_call" | custom-call | flops 4831838208 | bytes 18874368 | tf_op jit(solution)/shard_map/pallas_call | solution.py:401
  163.4 20.6 %shard_map.240 = (bf16[2,1024,512]{2,1,0:T(8,128)(2,1)}, bf16[2,1024,512]{2,1,0:T(8,128)(2,1)}, bf16[2,1024,512]{2,1,0:T(8,128)(2,1)}, bf16[2,1024,512]{2,1,0:T(...) custom-call(s32[4]{0:T(128)S(1)} %pad_add_fusion.place_ref.refs_0_, ...), custom_call_target="tpu_custom_call" | custom-call | flops 9663676416 | bytes 25165824 | tf_op jit(solution)/shard_map/pallas_call | solution.py:495
  183.9 13.7 %shard_map.241 = bf16[1024,1664]{1,0:T(8,128)(2,1)} custom-call(s32[4]{0:T(128)S(1)} %pad_add_fusion.place_ref.refs_0_, bf16[2,1024,512]{2,1,0:T(8,128)(2,1)} %get-tuple-element.108.grad_gate_ref.gate_ref, bf16[2,1024,512]{2,1,0:T(8,128)(2,1)} %get-tuple-element.109.grad_up_ref.up_ref, bf16[1024,128]{1,0:T(8,128)(2,1)S(1)} %get-tuple-element.110.extra_ref, ...), custom_call_target="tpu_custom_call" | custom-call | bytes 1024 | tf_op jit(solution)/shard_map/pallas_call | solution.py:628
  197.9 13.6 %shard_map.242 = (bf16[2304,512]{1,0:T(8,128)(2,1)}, bf16[2304,512]{1,0:T(8,128)(2,1)}) custom-call(bf16[1024,1536]{1,0:T(8,128)(2,1)} %get-tuple-element.118.normed_ref.left_ref.refs_7_, bf16[2,1024,512]{2,1,0:T(8,128)(2,1)} %get-tuple-element.108.grad_gate_ref.gate_ref, bf16[2,1024,512]{2,1,0:T(8,128)(2,1)} %get-tuple-element.109.grad_up_ref.up_ref, ...), custom_call_target="tpu_custom_call" | custom-call | bytes 1024 | tf_op jit(solution)/shard_map/pallas_call | solution.py:585
  214.5 15.2 %shard_map.243 = (f32[2304,512]{1,0:T(8,128)}, f32[2304,512]{1,0:T(8,128)}) custom-call(bf16[1024,1536]{1,0:T(8,128)(2,1)} %get-tuple-element.118.normed_ref.left_ref.refs_7_, bf16[2,1024,512]{2,1,0:T(8,128)(2,1)} %get-tuple-element.108.grad_gate_ref.gate_ref, bf16[2,1024,512]{2,1,0:T(8,128)(2,1)} %get-tuple-element.109.grad_up_ref.up_ref, ...), custom_call_target="tpu_custom_call" | custom-call | bytes 1024 | tf_op jit(solution)/shard_map/pallas_call | solution.py:585
  229.7 8.9 %shard_map.244.refs_9_ = bf16[1024,1536]{1,0:T(8,128)(2,1)} custom-call(s32[4]{0:T(128)S(1)} %pad_add_fusion.place_ref.refs_0_, bf16[2,1024,512]{2,1,0:T(8,128)(2,1)} %get-tuple-element.122.scaled_one_ref.scaled_ref, bf16[2,512,1536]{2,1,0:T(8,128)(2,1)} %down_weight_ref.3), custom_call_target="tpu_custom_call" | custom-call | bytes 1024 | tf_op jit(solution)/shard_map/pallas_call | solution.py:665
  239.2 6.8 %shard_map.245 = (f32[128,1536]{1,0:T(8,128)}, bf16[128,1536]{1,0:T(8,128)(2,1)}, bf16[8,128,192]{2,1,0:T(8,128)(2,1)}, bf16[128,16]{1,0:T(8,128)(2,1)}, f32[1,1536]{1,0:T(1,128)}) custom-call(s32[4]{0:T(128)} %copy-done.24, bf16[128,1664]{1,0:T(8,128)(2,1)} %reduce-scatter.3.cloned.1.call-done.sum_ref, f32[1024,16]{1,0:T(8,128)} %copy-done.16, ...), custom_call_target="tpu_custom_call" | custom-call | bytes 128 | tf_op jit(solution)/shard_map/pallas_call | solution.py:736
  248.2 2.8 collective-permute-start.8
  251.7 3.8 collective-permute-done.10
  255.5 3.7 collective-permute-done.9
  259.3 5.9 %collective-permute-done.11.refs_1_ = bf16[2304,512]{1,0:T(8,128)(2,1)} collective-permute-done((bf16[2304,512]{1,0:T(8,128)(2,1)}, bf16[2304,512]{1,0:T(8,128)(2,1)}, u32[]{:S(2)}, u32[]{:S(2)}) %collective-permute-start.11) | collective-permute-done | bytes 2359328 | tf_op jit(solution)/shard_map/ppermute | solution.py:1060
  266.4 5.7 %shard_map.246 = (bf16[1152,512]{1,0:T(8,128)(2,1)}, bf16[1152,512]{1,0:T(8,128)(2,1)}) custom-call(s32[2]{0:T(128)} %add_convert_fusion.2.keeps_ref, f32[2304,512]{1,0:T(8,128)} %get-tuple-element.120.refs_0_, bf16[2304,512]{1,0:T(8,128)(2,1)} %collective-permute-done.11.refs_1_, f32[2304,512]{1,0:T(8,128)} %get-tuple-element.121.refs_2_.refs_3_, ...), custom_call_target="tpu_custom_call" | custom-call | flops 70778880000 | bytes 14155776 | tf_op jit(solution)/shard_map/pallas_call | solution.py:1136
  277.3 14.3 %shard_map.247 = (bf16[1024,192]{1,0:T(8,128)(2,1)S(1)}, bf16[1024,128]{1,0:T(8,128)(2,1)S(1)}) custom-call(bf16[1024,192]{1,0:T(8,128)(2,1)S(1)} %copy-done.15, bf16[1024,192]{1,0:T(8,128)(2,1)S(1)} %bitcast.177, f32[3,1024,1]{2,1,0:T(8,128)S(1)} %copy-done.11, f32[1024,64]{1,0:T(8,128)S(1)} %copy-done.7, f32[1024,64]{1,0:T(8,128)S(1)} %copy-done.9, ...), custom_call_target="tpu_custom_call" | custom-call | bytes 1024 | tf_op jit(solution)/shard_map/pallas_call | solution.py:323
  293.1 6.2 %collective-permute-done.14.refs_2_ = bf16[1152,512]{1,0:T(8,128)(2,1)} collective-permute-done((bf16[1152,512]{1,0:T(8,128)(2,1)}, bf16[1152,512]{1,0:T(8,128)(2,1)}, u32[]{:S(2)}, u32[]{:S(2)}) %collective-permute-start.14) | collective-permute-done | bytes 1179680 | tf_op jit(solution)/shard_map/ppermute | solution.py:1060
  300.5 6.1 %shard_map.248 = (bf16[1152,512]{1,0:T(8,128)(2,1)}, bf16[1152,512]{1,0:T(8,128)(2,1)}) custom-call(s32[2]{0:T(128)} %add_convert_fusion.2.keeps_ref, f32[2304,512]{1,0:T(8,128)} %get-tuple-element.120.refs_0_, bf16[2304,512]{1,0:T(8,128)(2,1)} %collective-permute-done.11.refs_1_, bf16[1152,512]{1,0:T(8,128)(2,1)} %collective-permute-done.14.refs_2_, ...), custom_call_target="tpu_custom_call" | custom-call | bytes 2304 | tf_op jit(solution)/shard_map/pallas_call | solution.py:1175
  308.9 14.6 %close.1 = (bf16[1024,3072]{1,0:T(8,128)(2,1)}, f32[96,2304]{1,0:T(8,128)}, f32[96,2304]{1,0:T(8,128)}, bf16[96,2304]{1,0:T(8,128)(2,1)}, bf16[96,2304]{1,0:T(8,128)(2,1)}) custom-call(s32[4]{0:T(128)} %copy-done.24, bf16[1024,192]{1,0:T(8,128)(2,1)} %copy-done.17, bf16[1024,128]{1,0:T(8,128)(2,1)} %copy-done.18, ...), custom_call_target="tpu_custom_call" | custom-call | bytes 1024 | tf_op jit(solution)/shard_map/close/pallas_call | solution.py:865
  325.1 7.5 %collective-permute-done.17.refs_1_ = bf16[1152,512]{1,0:T(8,128)(2,1)S(1)} collective-permute-done((bf16[1152,512]{1,0:T(8,128)(2,1)}, bf16[1152,512]{1,0:T(8,128)(2,1)S(1)}, u32[]{:S(2)}, u32[]{:S(2)}) %collective-permute-start.17) | collective-permute-done | bytes 1179680 | tf_op jit(solution)/shard_map/ppermute | solution.py:1060
  332.5 3.8 collective-permute-done.18.refs_5_.refs_1_
  340.1 2.0 collective-permute-start.22
  343.8 1.9 collective-permute-done.16
  347.4 4.3 collective-permute-done.20
  351.9 2.1 collective-permute-start.21
  354.0 2.4 slice_select_fusion
  356.4 22.3 %collective-permute-done.19 = bf16[1,1,48,2304]{3,2,1,0:T(8,128)(2,1)S(1)} collective-permute-done((bf16[1,1,48,2304]{3,2,1,0:T(8,128)(2,1)S(1)}, bf16[1,1,48,2304]{3,2,1,0:T(8,128)(2,1)S(1)}, u32[]{:S(2)}, u32[]{:S(2)}) %collective-permute-start.19) | collective-permute-done | bytes 221216 | tf_op jit(solution)/shard_map/ppermute | solution.py:1060
  385.5 1.6 reshape.317
  390.2 2.1 collective-permute-start.24
  392.3 2.3 collective-permute-done.26
  394.6 1.7 collective-permute-done.25
  403.1 1.6 collective-permute-start.32
  406.0 3.9 collective-permute-done.30
  411.6 12.5 %collective-permute-done.34 = bf16[1,1,48,2304]{3,2,1,0:T(8,128)(2,1)S(1)} collective-permute-done((bf16[1,1,48,2304]{3,2,1,0:T(8,128)(2,1)S(1)}, bf16[1,1,48,2304]{3,2,1,0:T(8,128)(2,1)S(1)}, u32[]{:S(2)}, u32[]{:S(2)}) %collective-permute-start.34) | collective-permute-done | bytes 221216 | tf_op jit(solution)/shard_map/ppermute | solution.py:1060
  425.0 4.9 %into_output.2 = f32[2,1536,512]{2,1,0:T(8,128)} custom-call(s32[4]{0:T(128)S(1)} %pad_add_fusion.1.flags_ref.k, bf16[1152,512]{1,0:T(8,128)(2,1)S(1)} %copy-done.2, bf16[1152,512]{1,0:T(8,128)(2,1)S(1)} %collective-permute-done.17.refs_1_, bf16[1152,512]{1,0:T(8,128)(2,1)} %collective-permute-done.22.refs_2_, ...), custom_call_target="tpu_custom_call" | custom-call | bytes 1152 | tf_op jit(solution)/shard_map/into_output/pallas_call | solution.py:1002
  429.9 5.3 %into_output.3 = f32[2,1536,512]{2,1,0:T(8,128)} custom-call(s32[4]{0:T(128)S(1)} %pad_add_fusion.1.flags_ref.k, bf16[1152,512]{1,0:T(8,128)(2,1)S(1)} %copy-done.3, bf16[1152,512]{1,0:T(8,128)(2,1)} %collective-permute-done.18.refs_5_.refs_1_, bf16[1152,512]{1,0:T(8,128)(2,1)} %collective-permute-done.23.refs_2_, ...), custom_call_target="tpu_custom_call" | custom-call | bytes 1152 | tf_op jit(solution)/shard_map/into_output/pallas_call | solution.py:1002
  435.2 5.1 %shard_map.249 = f32[2,512,1536]{2,1,0:T(8,128)} custom-call(s32[4]{0:T(128)S(1)} %pad_add_fusion.1.flags_ref.k, bf16[1152,512]{1,0:T(8,128)(2,1)S(1)} %copy-done.2, bf16[1152,512]{1,0:T(8,128)(2,1)S(1)} %collective-permute-done.17.refs_1_, bf16[576,512]{1,0:T(8,128)(2,1)} %collective-permute-done.27.refs_2_.refs_3_, ...), custom_call_target="tpu_custom_call" | custom-call | bytes 1152 | tf_op jit(solution)/shard_map/pallas_call | solution.py:1039
  440.7 2.0 head_outputs.1
  446.5 2.5 fusion.10
  (251 shorter events, 82.1 us)
Async XLA Ops:
  7.2 64.3 %all-gather.11.cloned.1.call-start = ((), (), s32[]{:S(2)}) async-start(), calls=%async_computation.7 | async-start | bytes 5271552 | tf_op jit(solution)/shard_map/all_gather | solution.py:1311
  11.4 98.9 %all-gather.7.cloned.1.call-start = ((), (), s32[]{:S(2)}) async-start(), calls=%async_computation.3 | async-start | bytes 3538944 | tf_op jit(solution)/shard_map/all_gather | solution.py:1312
  12.1 137.6 %all-gather.13.cloned.1.call-start = ((), (), s32[]{:S(2)}) async-start(), calls=%async_computation.8 | async-start | bytes 3538944 | tf_op jit(solution)/shard_map/all_gather | solution.py:1362
  39.8 5.9 %collective-permute-start = (bf16[4,1,1,48,384]{4,3,0,2,1:T(8,128)(2,1)S(1)}, bf16[4,1,1,48,384]{4,3,0,2,1:T(8,128)(2,1)S(1)}, u32[]{:S(2)}, u32[]{:S(2)}) collective-permute-start(bf16[4,1,1,48,384]{4,3,0,2,1:T(8,128)(2,1)S(1)} %get-tuple-element.304), channel_id=1, source_target_pairs={{0,8},{8,0},{16,24},{24,16},{1,9},{9,1},{17,25},{25,17},{2,10},{10... | collective-permute-start | bytes 442376 | tf_op jit(solution)/shard_map/ppermute | solution.py:1060
  41.4 5.5 %collective-permute-start.2 = (bf16[4,1,1,48,384]{4,3,0,2,1:T(8,128)(2,1)S(1)}, bf16[4,1,1,48,384]{4,3,0,2,1:T(8,128)(2,1)S(1)}, u32[]{:S(2)}, u32[]{:S(2)}) collective-permute-start(bf16[4,1,1,48,384]{4,3,0,2,1:T(8,128)(2,1)S(1)} %get-tuple-element.305), channel_id=1, source_target_pairs={{0,16},{8,24},{16,0},{24,8},{1,17},{9,25},{17,1},{25,9},{2,18},{10... | collective-permute-start | bytes 442376 | tf_op jit(solution)/shard_map/ppermute | solution.py:1060
  47.0 8.0 %collective-permute-start.3 = (bf16[4,2,1,48,384]{4,3,0,2,1:T(8,128)(2,1)S(1)}, bf16[4,2,1,48,384]{4,3,0,2,1:T(8,128)(2,1)S(1)}, u32[]{:S(2)}, u32[]{:S(2)}) collective-permute-start(bf16[4,2,1,48,384]{4,3,0,2,1:T(8,128)(2,1)S(1)} %pad_maximum_fusion.13), channel_id=1, source_target_pairs={{0,8},{8,0},{16,24},{24,16},{1,9},{9,1},{17,25},{25,17},{2,10},{10... | collective-permute-start | bytes 884744 | tf_op jit(solution)/shard_map/ppermute | solution.py:1060
  47.8 28.3 %collective-permute-start.1 = (bf16[4,1,2,48,384]{4,3,0,2,1:T(8,128)(2,1)S(1)}, bf16[4,1,2,48,384]{4,3,0,2,1:T(8,128)(2,1)S(1)}, u32[]{:S(2)}, u32[]{:S(2)}) collective-permute-start(bf16[4,1,2,48,384]{4,3,0,2,1:T(8,128)(2,1)S(1)} %pad_maximum_fusion.12), channel_id=1, source_target_pairs={{0,16},{8,24},{16,0},{24,8},{1,17},{9,25},{17,1},{25,9},{2,18},{10... | collective-permute-start | bytes 884744 | tf_op jit(solution)/shard_map/ppermute | solution.py:1060
  72.8 20.7 %collective-permute-start.5 = (bf16[4,1,1,48,1536]{4,3,0,2,1:T(8,128)(2,1)S(1)}, bf16[4,1,1,48,1536]{4,3,0,2,1:T(8,128)(2,1)S(1)}, u32[]{:S(2)}, u32[]{:S(2)}) collective-permute-start(bf16[4,1,1,48,1536]{4,3,0,2,1:T(8,128)(2,1)S(1)} %get-tuple-element.260), channel_id=1, source_target_pairs={{0,16},{8,24},{16,0},{24,8},{1,17},{9,25},{17,1},{25,9},{2,18},{10... | collective-permute-start | bytes 1769480 | tf_op jit(solution)/shard_map/ppermute | solution.py:1060
  74.4 19.1 %collective-permute-start.4 = (bf16[4,1,1,48,1536]{4,3,0,2,1:T(8,128)(2,1)S(1)}, bf16[4,1,1,48,1536]{4,3,0,2,1:T(8,128)(2,1)S(1)}, u32[]{:S(2)}, u32[]{:S(2)}) collective-permute-start(bf16[4,1,1,48,1536]{4,3,0,2,1:T(8,128)(2,1)S(1)} %get-tuple-element.261), channel_id=1, source_target_pairs={{0,8},{8,0},{16,24},{24,16},{1,9},{9,1},{17,25},{25,17},{2,10},{10... | collective-permute-start | bytes 1769480 | tf_op jit(solution)/shard_map/ppermute | solution.py:1060
  77.4 16.1 %copy-start.37 = (f32[1536]{0:T(1024)}, f32[1536]{0:T(1024)S(1)}, u32[]{:S(2)}) copy-start(f32[1536]{0:T(1024)S(1)} %get-tuple-element.253) | copy-start | bytes 18436
  110.3 128.9 %reduce-scatter.3.cloned.1.call-start = ((), (), s32[]{:S(2)}) async-start(), calls=%async_computation.4 | async-start | bytes 3833856 | tf_op jit(solution)/shard_map/reduce_scatter | solution.py:1388
  110.4 28.5 %collective-permute-start.6 = (bf16[4,1,2,48,1536]{4,3,0,2,1:T(8,128)(2,1)}, bf16[4,1,2,48,1536]{4,3,0,2,1:T(8,128)(2,1)}, u32[]{:S(2)}, u32[]{:S(2)}) collective-permute-start(bf16[4,1,2,48,1536]{4,3,0,2,1:T(8,128)(2,1)} %pad_maximum_fusion.3), channel_id=1, source_target_pairs={{0,16},{8,24},{16,0},{24,8},{1,17},{9,25},{17,1},{25,9},{2,18},{10... | collective-permute-start | bytes 3538952 | tf_op jit(solution)/shard_map/ppermute | solution.py:1060
  111.9 28.8 %collective-permute-start.7 = (bf16[4,2,1,48,1536]{4,3,0,2,1:T(8,128)(2,1)}, bf16[4,2,1,48,1536]{4,3,0,2,1:T(8,128)(2,1)S(1)}, u32[]{:S(2)}, u32[]{:S(2)}) collective-permute-start(bf16[4,2,1,48,1536]{4,3,0,2,1:T(8,128)(2,1)} %pad_maximum_fusion.4), channel_id=1, source_target_pairs={{0,8},{8,0},{16,24},{24,16},{1,9},{9,1},{17,25},{25,17},{2,10},{10... | collective-permute-start | bytes 3538952 | tf_op jit(solution)/shard_map/ppermute | solution.py:1060
  113.5 116.2 %copy-start.24 = (s32[4]{0:T(128)}, s32[4]{0:T(128)S(1)}, u32[]{:S(2)}) copy-start(s32[4]{0:T(128)S(1)} %pad_add_fusion.place_ref.refs_0_) | copy-start | bytes 52
  114.2 35.5 %copy-start.23 = (f32[1,1536]{1,0:T(1,128)}, f32[1,1536]{1,0:T(1,128)S(1)}, u32[]{:S(2)}) copy-start(f32[1,1536]{1,0:T(1,128)S(1)} %reshape.330.gain_ref) | copy-start | bytes 18436
  163.4 20.6 %copy-start.16 = (f32[1024,16]{1,0:T(8,128)}, f32[1024,16]{1,0:T(8,128)S(1)}, u32[]{:S(2)}) copy-start(f32[1024,16]{1,0:T(8,128)S(1)} %get-tuple-element.107.gates_ref) | copy-start | bytes 196612
  197.6 111.3 %all-gather.9.cloned.1.call-start = ((), (), s32[]{:S(2)}) async-start(), calls=%async_computation.5 | async-start | bytes 3538944 | tf_op jit(solution)/shard_map/all_gather | solution.py:1408
  211.4 53.7 %collective-permute-start.11 = (bf16[2304,512]{1,0:T(8,128)(2,1)}, bf16[2304,512]{1,0:T(8,128)(2,1)}, u32[]{:S(2)}, u32[]{:S(2)}) collective-permute-start(bf16[2304,512]{1,0:T(8,128)(2,1)} %get-tuple-element.116), channel_id=1, source_target_pairs={{0,8},{8,0},{16,24},{24,16},{1,9},{9,1},{17,25},{25,17},{2,10},{10... | collective-permute-start | bytes 7077896 | tf_op jit(solution)/shard_map/ppermute | solution.py:1060
  213.0 53.4 %collective-permute-start.12 = (bf16[2304,512]{1,0:T(8,128)(2,1)}, bf16[2304,512]{1,0:T(8,128)(2,1)}, u32[]{:S(2)}, u32[]{:S(2)}) collective-permute-start(bf16[2304,512]{1,0:T(8,128)(2,1)} %get-tuple-element.117), channel_id=1, source_target_pairs={{0,16},{8,24},{16,0},{24,8},{1,17},{9,25},{17,1},{25,9},{2,18},{10... | collective-permute-start | bytes 7077896 | tf_op jit(solution)/shard_map/ppermute | solution.py:1060
  247.1 8.3 %collective-permute-start.10 = (bf16[2,128,192]{2,1,0:T(8,128)(2,1)S(1)}, bf16[2,128,192]{2,1,0:T(8,128)(2,1)S(1)}, u32[]{:S(2)}, u32[]{:S(2)}) collective-permute-start(bf16[2,128,192]{2,1,0:T(8,128)(2,1)S(1)} %get-tuple-element.283), channel_id=1, source_target_pairs={{0,2},{1,3},{2,4},{3,5},{4,6},{5,7},{6,0},{7,1},{8,10},{9,11},{10,... | collective-permute-start | bytes 294920 | tf_op jit(solution)/shard_map/ppermute | solution.py:1315
  247.2 11.9 %collective-permute-start.9 = (bf16[2,128,192]{2,1,0:T(8,128)(2,1)S(1)}, bf16[2,128,192]{2,1,0:T(8,128)(2,1)S(1)}, u32[]{:S(2)}, u32[]{:S(2)}) collective-permute-start(bf16[2,128,192]{2,1,0:T(8,128)(2,1)S(1)} %get-tuple-element.284), channel_id=1, source_target_pairs={{0,4},{1,5},{2,6},{3,7},{4,0},{5,1},{6,2},{7,3},{8,12},{9,13},{10,... | collective-permute-start | bytes 294920 | tf_op jit(solution)/shard_map/ppermute | solution.py:1315
  248.2 10.9 %collective-permute-start.8 = (bf16[2,128,192]{2,1,0:T(8,128)(2,1)S(1)}, bf16[2,128,192]{2,1,0:T(8,128)(2,1)S(1)}, u32[]{:S(2)}, u32[]{:S(2)}) collective-permute-start(bf16[2,128,192]{2,1,0:T(8,128)(2,1)S(1)} %get-tuple-element.285), channel_id=1, source_target_pairs={{0,6},{1,7},{2,0},{3,1},{4,2},{5,3},{6,4},{7,5},{8,14},{9,15},{10,... | collective-permute-start | bytes 294920 | tf_op jit(solution)/shard_map/ppermute | solution.py:1315
  251.6 192.4 %reduce-scatter.5.cloned.1.call-start = ((), (), s32[]{:S(2)}) async-start(), calls=%async_computation.6 | async-start | bytes 7077888 | tf_op jit(solution)/shard_map/reduce_scatter | solution.py:1463
  272.1 27.2 %collective-permute-start.14 = (bf16[1152,512]{1,0:T(8,128)(2,1)}, bf16[1152,512]{1,0:T(8,128)(2,1)}, u32[]{:S(2)}, u32[]{:S(2)}) collective-permute-start(bf16[1152,512]{1,0:T(8,128)(2,1)} %get-tuple-element.129), channel_id=1, source_target_pairs={{0,16},{8,24},{16,0},{24,8},{1,17},{9,25},{17,1},{25,9},{2,18},{10... | collective-permute-start | bytes 3538952 | tf_op jit(solution)/shard_map/ppermute | solution.py:1060
  273.5 27.0 %collective-permute-start.15 = (bf16[1152,512]{1,0:T(8,128)(2,1)}, bf16[1152,512]{1,0:T(8,128)(2,1)}, u32[]{:S(2)}, u32[]{:S(2)}) collective-permute-start(bf16[1152,512]{1,0:T(8,128)(2,1)} %get-tuple-element.130), channel_id=1, source_target_pairs={{0,8},{8,0},{16,24},{24,16},{1,9},{9,1},{17,25},{25,17},{2,10},{10... | collective-permute-start | bytes 3538952 | tf_op jit(solution)/shard_map/ppermute | solution.py:1060
  274.2 1.7 collective-permute-start.13
  306.6 25.9 %collective-permute-start.17 = (bf16[1152,512]{1,0:T(8,128)(2,1)}, bf16[1152,512]{1,0:T(8,128)(2,1)S(1)}, u32[]{:S(2)}, u32[]{:S(2)}) collective-permute-start(bf16[1152,512]{1,0:T(8,128)(2,1)} %get-tuple-element.184.refs_0_), channel_id=1, source_target_pairs={{0,16},{8,24},{16,0},{24,8},{1,17},{9,25},{17,1},{25,9},{2,18},{10... | collective-permute-start | bytes 3538952 | tf_op jit(solution)/shard_map/ppermute | solution.py:1060
  307.2 29.2 %collective-permute-start.18 = (bf16[1152,512]{1,0:T(8,128)(2,1)}, bf16[1152,512]{1,0:T(8,128)(2,1)}, u32[]{:S(2)}, u32[]{:S(2)}) collective-permute-start(bf16[1152,512]{1,0:T(8,128)(2,1)} %get-tuple-element.188.refs_4_.refs_0_), channel_id=1, source_target_pairs={{0,8},{8,0},{16,24},{24,16},{1,9},{9,1},{17,25},{25,17},{2,10},{10... | collective-permute-start | bytes 3538952 | tf_op jit(solution)/shard_map/ppermute | solution.py:1060
  323.6 12.8 %copy-start.2 = (bf16[1152,512]{1,0:T(8,128)(2,1)S(1)}, bf16[1152,512]{1,0:T(8,128)(2,1)}, u32[]{:S(2)}) copy-start(bf16[1152,512]{1,0:T(8,128)(2,1)} %get-tuple-element.184.refs_0_) | copy-start | bytes 3538948
  323.6 22.1 %collective-permute-start.16 = (bf16[2,1,48,2304]{3,2,1,0:T(8,128)(2,1)}, bf16[2,1,48,2304]{3,2,1,0:T(8,128)(2,1)S(1)}, u32[]{:S(2)}, u32[]{:S(2)}) collective-permute-start(bf16[2,1,48,2304]{3,2,1,0:T(8,128)(2,1)} %bitcast.42), channel_id=1, source_target_pairs={{0,8},{8,0},{16,24},{24,16},{1,9},{9,1},{17,25},{25,17},{2,10},{10... | collective-permute-start | bytes 1327112 | tf_op jit(solution)/shard_map/ppermute | solution.py:1060
  338.7 13.1 %collective-permute-start.20 = (bf16[1,2,48,2304]{3,2,1,0:T(8,128)(2,1)S(1)}, bf16[1,2,48,2304]{3,2,1,0:T(8,128)(2,1)S(1)}, u32[]{:S(2)}, u32[]{:S(2)}) collective-permute-start(bf16[1,2,48,2304]{3,2,1,0:T(8,128)(2,1)S(1)} %bitcast.210), channel_id=1, source_target_pairs={{0,16},{8,24},{16,0},{24,8},{1,17},{9,25},{17,1},{25,9},{2,18},{10... | collective-permute-start | bytes 1327112 | tf_op jit(solution)/shard_map/ppermute | solution.py:1060
  340.1 48.1 %collective-permute-start.22 = (bf16[1152,512]{1,0:T(8,128)(2,1)}, bf16[1152,512]{1,0:T(8,128)(2,1)}, u32[]{:S(2)}, u32[]{:S(2)}) collective-permute-start(bf16[1152,512]{1,0:T(8,128)(2,1)} %broadcast_select_fusion.1), channel_id=1, source_target_pairs={{0,8},{8,0},{16,24},{24,16},{1,9},{9,1},{17,25},{25,17},{2,10},{10... | collective-permute-start | bytes 3538952 | tf_op jit(solution)/shard_map/ppermute | solution.py:1060
  342.2 46.1 %collective-permute-start.23 = (bf16[1152,512]{1,0:T(8,128)(2,1)}, bf16[1152,512]{1,0:T(8,128)(2,1)}, u32[]{:S(2)}, u32[]{:S(2)}) collective-permute-start(bf16[1152,512]{1,0:T(8,128)(2,1)} %broadcast_select_fusion), channel_id=1, source_target_pairs={{0,16},{8,24},{16,0},{24,8},{1,17},{9,25},{17,1},{25,9},{2,18},{10... | collective-permute-start | bytes 3538952 | tf_op jit(solution)/shard_map/ppermute | solution.py:1060
  345.9 32.8 %collective-permute-start.19 = (bf16[1,1,48,2304]{3,2,1,0:T(8,128)(2,1)S(1)}, bf16[1,1,48,2304]{3,2,1,0:T(8,128)(2,1)S(1)}, u32[]{:S(2)}, u32[]{:S(2)}) collective-permute-start(bf16[1,1,48,2304]{3,2,1,0:T(8,128)(2,1)S(1)} %dynamic-slice_convert_fusion.1), channel_id=1, source_target_pairs={{0,16},{8,24},{16,0},{24,8},{1,17},{9,25},{17,1},{25,9},{2,18},{10... | collective-permute-start | bytes 663560 | tf_op jit(solution)/shard_map/ppermute | solution.py:1060
  351.9 28.3 %collective-permute-start.21 = (bf16[1,1,48,2304]{3,2,1,0:T(8,128)(2,1)S(1)}, bf16[1,1,48,2304]{3,2,1,0:T(8,128)(2,1)S(1)}, u32[]{:S(2)}, u32[]{:S(2)}) collective-permute-start(bf16[1,1,48,2304]{3,2,1,0:T(8,128)(2,1)S(1)} %dynamic-slice_convert_fusion), channel_id=1, source_target_pairs={{0,8},{8,0},{16,24},{24,16},{1,9},{9,1},{17,25},{25,17},{2,10},{10... | collective-permute-start | bytes 663560 | tf_op jit(solution)/shard_map/ppermute | solution.py:1060
  356.4 40.0 %collective-permute-start.27 = (bf16[576,512]{1,0:T(8,128)(2,1)}, bf16[576,512]{1,0:T(8,128)(2,1)}, u32[]{:S(2)}, u32[]{:S(2)}) collective-permute-start(bf16[576,512]{1,0:T(8,128)(2,1)} %get-tuple-element.161), channel_id=1, source_target_pairs={{0,8},{8,0},{16,24},{24,16},{1,9},{9,1},{17,25},{25,17},{2,10},{10... | collective-permute-start | bytes 1769480 | tf_op jit(solution)/shard_map/ppermute | solution.py:1060
  378.7 17.7 %collective-permute-start.28 = (bf16[576,512]{1,0:T(8,128)(2,1)}, bf16[576,512]{1,0:T(8,128)(2,1)}, u32[]{:S(2)}, u32[]{:S(2)}) collective-permute-start(bf16[576,512]{1,0:T(8,128)(2,1)} %get-tuple-element.162), channel_id=1, source_target_pairs={{0,16},{8,24},{16,0},{24,8},{1,17},{9,25},{17,1},{25,9},{2,18},{10... | collective-permute-start | bytes 1769480 | tf_op jit(solution)/shard_map/ppermute | solution.py:1060
  388.4 6.2 %collective-permute-start.26 = (bf16[2,48,384]{2,1,0:T(8,128)(2,1)S(1)}, bf16[2,48,384]{2,1,0:T(8,128)(2,1)S(1)}, u32[]{:S(2)}, u32[]{:S(2)}) collective-permute-start(bf16[2,48,384]{2,1,0:T(8,128)(2,1)S(1)} %get-tuple-element.299), channel_id=1, source_target_pairs={{0,2},{1,3},{2,4},{3,5},{4,6},{5,7},{6,0},{7,1},{8,10},{9,11},{10,... | collective-permute-start | bytes 221192 | tf_op jit(solution)/shard_map/ppermute | solution.py:1315
  388.8 7.5 %collective-permute-start.25 = (bf16[2,48,384]{2,1,0:T(8,128)(2,1)S(1)}, bf16[2,48,384]{2,1,0:T(8,128)(2,1)S(1)}, u32[]{:S(2)}, u32[]{:S(2)}) collective-permute-start(bf16[2,48,384]{2,1,0:T(8,128)(2,1)S(1)} %get-tuple-element.300), channel_id=1, source_target_pairs={{0,4},{1,5},{2,6},{3,7},{4,0},{5,1},{6,2},{7,3},{8,12},{9,13},{10,... | collective-permute-start | bytes 221192 | tf_op jit(solution)/shard_map/ppermute | solution.py:1315
  390.2 6.1 %collective-permute-start.24 = (bf16[2,48,384]{2,1,0:T(8,128)(2,1)S(1)}, bf16[2,48,384]{2,1,0:T(8,128)(2,1)S(1)}, u32[]{:S(2)}, u32[]{:S(2)}) collective-permute-start(bf16[2,48,384]{2,1,0:T(8,128)(2,1)S(1)} %get-tuple-element.301), channel_id=1, source_target_pairs={{0,6},{1,7},{2,0},{3,1},{4,2},{5,3},{6,4},{7,5},{8,14},{9,15},{10,... | collective-permute-start | bytes 221192 | tf_op jit(solution)/shard_map/ppermute | solution.py:1315
  397.2 3.0 collective-permute-start.29
  401.6 8.3 %collective-permute-start.30 = (bf16[1,1,48,2304]{3,2,1,0:T(8,128)(2,1)S(1)}, bf16[1,1,48,2304]{3,2,1,0:T(8,128)(2,1)S(1)}, u32[]{:S(2)}, u32[]{:S(2)}) collective-permute-start(bf16[1,1,48,2304]{3,2,1,0:T(8,128)(2,1)S(1)} %maximum_bitcast_fusion), channel_id=1, source_target_pairs={{0,16},{8,24},{16,0},{24,8},{1,17},{9,25},{17,1},{25,9},{2,18},{10... | collective-permute-start | bytes 663560 | tf_op jit(solution)/shard_map/ppermute | solution.py:1060
  403.1 32.1 %collective-permute-start.32 = (bf16[576,512]{1,0:T(8,128)(2,1)S(1)}, bf16[576,512]{1,0:T(8,128)(2,1)S(1)}, u32[]{:S(2)}, u32[]{:S(2)}) collective-permute-start(bf16[576,512]{1,0:T(8,128)(2,1)S(1)} %copy-done.35), channel_id=1, source_target_pairs={{0,8},{8,0},{16,24},{24,16},{1,9},{9,1},{17,25},{25,17},{2,10},{10... | collective-permute-start | bytes 1769480 | tf_op jit(solution)/shard_map/ppermute | solution.py:1060
  404.8 30.4 %collective-permute-start.33 = (bf16[576,512]{1,0:T(8,128)(2,1)S(1)}, bf16[576,512]{1,0:T(8,128)(2,1)S(1)}, u32[]{:S(2)}, u32[]{:S(2)}) collective-permute-start(bf16[576,512]{1,0:T(8,128)(2,1)S(1)} %copy-done.36), channel_id=1, source_target_pairs={{0,16},{8,24},{16,0},{24,8},{1,17},{9,25},{17,1},{25,9},{2,18},{10... | collective-permute-start | bytes 1769480 | tf_op jit(solution)/shard_map/ppermute | solution.py:1060
  405.5 18.6 %collective-permute-start.34 = (bf16[1,1,48,2304]{3,2,1,0:T(8,128)(2,1)S(1)}, bf16[1,1,48,2304]{3,2,1,0:T(8,128)(2,1)S(1)}, u32[]{:S(2)}, u32[]{:S(2)}) collective-permute-start(bf16[1,1,48,2304]{3,2,1,0:T(8,128)(2,1)S(1)} %maximum_bitcast_fusion.1), channel_id=1, source_target_pairs={{0,8},{8,0},{16,24},{24,16},{1,9},{9,1},{17,25},{25,17},{2,10},{10... | collective-permute-start | bytes 663560 | tf_op jit(solution)/shard_map/ppermute | solution.py:1060
  410.0 15.0 %copy-start.43 = (s32[1,128]{1,0:T(1,128)S(1)}, s32[1,128]{1,0:T(1,128)}, u32[]{:S(2)}) copy-start(s32[1,128]{1,0:T(1,128)} %param.16) | copy-start | bytes 1540
  410.1 30.3 %collective-permute-start.31 = (bf16[2,1,48,2304]{3,2,1,0:T(8,128)(2,1)S(1)}, bf16[2,1,48,2304]{3,2,1,0:T(8,128)(2,1)S(1)}, u32[]{:S(2)}, u32[]{:S(2)}) collective-permute-start(bf16[2,1,48,2304]{3,2,1,0:T(8,128)(2,1)S(1)} %pad_maximum_fusion.10), channel_id=1, source_target_pairs={{0,8},{8,0},{16,24},{24,16},{1,9},{9,1},{17,25},{25,17},{2,10},{10... | collective-permute-start | bytes 1327112 | tf_op jit(solution)/shard_map/ppermute | solution.py:1060
  424.2 16.1 %collective-permute-start.35 = (bf16[1,2,48,2304]{3,2,1,0:T(8,128)(2,1)S(1)}, bf16[1,2,48,2304]{3,2,1,0:T(8,128)(2,1)S(1)}, u32[]{:S(2)}, u32[]{:S(2)}) collective-permute-start(bf16[1,2,48,2304]{3,2,1,0:T(8,128)(2,1)S(1)} %pad_maximum_fusion.11), channel_id=1, source_target_pairs={{0,16},{8,24},{16,0},{24,8},{1,17},{9,25},{17,1},{25,9},{2,18},{10... | collective-permute-start | bytes 1327112 | tf_op jit(solution)/shard_map/ppermute | solution.py:1060
  (38 other events, 104.3 us)
Sparse Core Ops, SparseCore 0:
  11.5 59.9 all-gather.10
  73.1 37.1 all-gather.6
  112.5 37.1 all-gather.12
  197.8 41.4 reduce-scatter.2
  251.7 37.8 all-gather.8
  323.8 70.9 reduce-scatter.4

commit v10 on v9

--- a/solution.py
+++ b/solution.py
@@ -352,7 +352,14 @@
     )(query, grad, log_total, cosine, sine, gathered, segments, key, value, cosine, sine)
 
 
-def middle_kernel(
+def slot_of(e, keeps, experts_own):
+    pick = experts_own // 2
+    high, low = e // pick, e % pick
+    return (1 - (high ^ keeps)) * pick + low
+
+
+def layer_kernel(
+    place_ref,
     mixed_ref,
     low_ref,
     high_ref,
@@ -360,11 +367,49 @@
     column_ref,
     gain_ref,
     router_ref,
+    cotangent_ref,
+    gate_any,
+    up_any,
+    down_any,
+    normed_ref,
+    scaled_one_ref,
+    scaled_two_ref,
+    grad_gate_ref,
+    grad_up_ref,
+    grad_live_ref,
+    grad_rows_ref,
+    middle_own_ref,
+    normed_own_ref,
+    gates_own_ref,
+    gate_weight_ref,
+    up_weight_ref,
+    down_weight_ref,
     middle_ref,
-    normed_ref,
     gates_ref,
+    semaphores,
 ):
+    step = pl.program_id(0)
+    block, features = cotangent_ref.shape
+    own = middle_own_ref.shape[0]
     groups = mixed_ref.shape[0]
+    experts_own = gate_weight_ref.shape[0]
+    experts_all = router_ref.shape[1]
+    copies = [
+        pltpu.make_async_copy(source, target, semaphores.at[n])
+        for n, (source, target) in enumerate(
+            (
+                (gate_any, gate_weight_ref),
+                (up_any, up_weight_ref),
+                (down_any, down_weight_ref),
+            )
+        )
+    ]
+
+    @pl.when(step == 0)
+    def _():
+        for copy in copies:
+            copy.start()
+
     width = mixed_ref.shape[2] // 2
     mixed = jnp.concatenate(
         [
@@ -382,81 +427,37 @@
     normed_ref[...] = normed
     logits = dot(normed, router_ref[...])
     columns = flat(column_ref).astype(jnp.float32)
-    number = lax.broadcasted_iota(jnp.int32, logits.shape, 1).astype(jnp.float32)
-    named = columns[:, 3:4] == number
+    number = lax.broadcasted_iota(jnp.int32, logits.shape, 1)
+    named = columns[:, 3:4] == number.astype(jnp.float32)
     for slot in range(1, TOPK):
-        named = named | (columns[:, 3 + slot : 4 + slot] == number)
+        named = named | (columns[:, 3 + slot : 4 + slot] == number.astype(jnp.float32))
     logits = jnp.where(named, logits, MASK_FLOOR)
     shifted = jnp.exp(logits - jnp.max(logits, -1, keepdims=True))
     shifted = jnp.where(named, shifted, 0.0)
-    gates_ref[...] = shifted / jnp.sum(shifted, -1, keepdims=True)
-
-
-def middle_rows(mixed, weights, gathered, gain, router, own, block):
-    groups, _, width = mixed.shape
-    tokens = gathered.shape[0] * own
-    features = gain.shape[0]
-    experts = router.shape[1]
-    rows = lambda columns: pl.BlockSpec((block, columns), lambda i: (i, 0))
-    return pl.pallas_call(
-        middle_kernel,
-        out_shape=(
-            jax.ShapeDtypeStruct((tokens, features), jnp.float32),
-            jax.ShapeDtypeStruct((tokens, features), jnp.bfloat16),
-            jax.ShapeDtypeStruct((tokens, experts), jnp.float32),
-        ),
-        grid=(tokens // block,),
-        in_specs=[
-            pl.BlockSpec((groups, block // 2, width), lambda i: (0, i, 0)),
-            whole_block(*weights[0].shape),
-            whole_block(*weights[1].shape),
-            *token_rows(block, own, features),
-            whole_block(1, features),
-            whole_block(features, experts),
-        ],
-        out_specs=[rows(features), rows(features), rows(experts)],
-        compiler_params=pltpu.CompilerParams(vmem_limit_bytes=48 << 20),
-        cost_estimate=pl.CostEstimate(
-            flops=tokens * features * groups * width,
-            bytes_accessed=12 * tokens * features,
-            transcendentals=0,
-        ),
-    )(mixed, *weights, gathered, gathered, gain[None, :], router)
-
-
-def slot_of(e, keeps, experts_own):
-    pick = experts_own // 2
-    high, low = e // pick, e % pick
-    return (1 - (high ^ keeps)) * pick + low
-
-
-def expert_kernel(
-    place_ref,
-    normed_ref,
-    cotangent_ref,
-    column_ref,
-    gates_ref,
-    gate_weight_ref,
-    up_weight_ref,
-    down_weight_ref,
-    scaled_one_ref,
-    scaled_two_ref,
-    grad_gate_ref,
-    grad_up_ref,
-    grad_live_ref,
-    extra_ref,
-):
-    experts_own = gate_weight_ref.shape[0]
-    experts_all = gates_ref.shape[1]
+    gates = shifted / jnp.sum(shifted, -1, keepdims=True)
+    gates_ref[...] = gates
+    grad_live_ref[...] = jnp.where(
+        columns[:, :1] > 0, cotangent_ref[...], jnp.zeros((), jnp.bfloat16)
+    )
+
+    @pl.when(place_ref[0] == step)
+    def _():
+        there = pl.ds(pl.multiple_of(lax.rem(place_ref[1], 2) * own, own), own)
+        middle_own_ref[...] = middle_ref[there, :]
+        normed_own_ref[...] = normed_ref[there, :]
+        gates_own_ref[...] = gates_ref[there, :]
+
+    @pl.when(step == 0)
+    def _():
+        for copy in copies:
+            copy.wait()
+
     first = place_ref[1] * experts_own
-    live = flat(column_ref).astype(jnp.float32)[:, :1] > 0
-    grad_live_ref[...] = jnp.where(live, cotangent_ref[...], jnp.zeros((), jnp.bfloat16))
-    gates = gates_ref[...]
-    number = lax.broadcasted_iota(jnp.int32, gates.shape, 1)
 
     def one_expert(e, grad_gates):
         one = slot_of(e, place_ref[2], experts_own)
         two = slot_of(e, place_ref[3], experts_own)
+        gates = gates_ref[...]
         gate = jnp.sum(jnp.where(number == first + e, gates, 0.0), -1, keepdims=True)
         gate_pre = dot(normed_ref[...], gate_weight_ref[e])
         up_pre = dot(normed_ref[...], up_weight_ref[e])
@@ -479,50 +480,99 @@
     grad_gates = lax.fori_loop(
         0, experts_own, one_expert, jnp.zeros(gates.shape, jnp.float32)
     )
+    one = [slot_of(e, place_ref[2], experts_own) for e in range(experts_own)]
+    two = [slot_of(e, place_ref[3], experts_own) for e in range(experts_own)]
+    size = 512
+
+    @pl.loop(0, features // size)
+    def _(index):
+        part = pl.ds(pl.multiple_of(index * size, size), size)
+        grad = 0.0
+        for e in range(experts_own):
+            grad = grad + dot(grad_gate_ref[one[e]], gate_weight_ref[e, part, :], COLUMNS)
+            grad = grad + dot(grad_up_ref[two[e]], up_weight_ref[e, part, :], COLUMNS)
+        grad_rows_ref[:, part] = grad.astype(jnp.bfloat16)
+
     rough = grad_gates.astype(jnp.bfloat16)
     fine = (grad_gates - rough.astype(jnp.float32)).astype(jnp.bfloat16)
-    rest = jnp.zeros((gates.shape[0], extra_ref.shape[1] - 2 * experts_all), jnp.bfloat16)
-    extra_ref[...] = jnp.concatenate([rough, fine, rest], 1)
-
-
-def expert_rows(place, normed, cotangent, gathered, gates, w_gate, w_up, w_down, own, block):
-    tokens, features = normed.shape
-    experts_own, _, hidden = w_gate.shape
-    experts_all = gates.shape[1]
+    rest = jnp.zeros((block, 128 - 2 * experts_all), jnp.bfloat16)
+    grad_rows_ref[:, features:] = jnp.concatenate([rough, fine, rest], 1)
+
+
+def layer_rows(place, mixed, weights, gathered, gain, router, cotangent, experts, own, block):
+    groups, _, width = mixed.shape
+    tokens, features = cotangent.shape
+    experts_all = router.shape[1]
+    experts_own, _, hidden = experts[0].shape
     rows = lambda columns: pl.BlockSpec((block, columns), lambda i, p: (i, 0))
+    resident = lambda *shape: pl.BlockSpec(shape, lambda i, p: (0,) * len(shape))
     spread = pl.BlockSpec((experts_own, block, hidden), lambda i, p: (0, i, 0))
-    wide = jax.ShapeDtypeStruct((experts_own, tokens, hidden), jnp.bfloat16)
+    low = jnp.bfloat16
+    shaped = jax.ShapeDtypeStruct
+    wide = shaped((experts_own, tokens, hidden), low)
     return pl.pallas_call(
-        expert_kernel,
+        layer_kernel,
         out_shape=(
+            shaped((tokens, features), low),
             wide,
             wide,
             wide,
             wide,
-            jax.ShapeDtypeStruct((tokens, features), jnp.bfloat16),
-            jax.ShapeDtypeStruct((tokens, 128), jnp.bfloat16),
+            shaped((tokens, features), low),
+            shaped((tokens, features + 128), low),
+            shaped((own, features), jnp.float32),
+            shaped((own, features), low),
+            shaped((own, experts_all), jnp.float32),
         ),
         grid_spec=pltpu.PrefetchScalarGridSpec(
             num_scalar_prefetch=1,
             grid=(tokens // block,),
             in_specs=[
+                pl.BlockSpec((groups, block // 2, width), lambda i, p: (0, i, 0)),
+                whole_block(*weights[0].shape),
+                whole_block(*weights[1].shape),
+                *token_rows(block, own, features),
+                whole_block(1, features),
+                whole_block(features, experts_all),
                 rows(features),
+                *[pl.BlockSpec(memory_space=pl.ANY)] * 3,
+            ],
+            out_specs=[
                 rows(features),
-                token_rows(block, own, features)[1],
-                rows(experts_all),
-                whole_block(*w_gate.shape),
-                whole_block(*w_up.shape),
-                whole_block(*w_down.shape),
+                spread,
+                spread,
+                spread,
+                spread,
+                rows(features),
+                rows(features + 128),
+                resident(own, features),
+                resident(own, features),
+                resident(own, experts_all),
             ],
-            out_specs=[spread, spread, spread, spread, rows(features), rows(128)],
-        ),
-        compiler_params=pltpu.CompilerParams(vmem_limit_bytes=52 << 20),
+            scratch_shapes=[
+                *[pltpu.VMEM(array.shape, low) for array in experts],
+                pltpu.VMEM((block, features), jnp.float32),
+                pltpu.VMEM((block, experts_all), jnp.float32),
+                pltpu.SemaphoreType.DMA((3,)),
+            ],
+        ),
+        compiler_params=pltpu.CompilerParams(vmem_limit_bytes=58 << 20),
         cost_estimate=pl.CostEstimate(
-            flops=6 * tokens * features * hidden * experts_own,
-            bytes_accessed=6 * features * hidden * experts_own + 10 * tokens * features,
+            flops=12 * tokens * features * hidden * experts_own,
+            bytes_accessed=6 * features * hidden * experts_own + 20 * tokens * features,
             transcendentals=tokens * hidden * experts_own,
         ),
-    )(place, normed, cotangent, gathered, gates, w_gate, w_up, w_down)
+    )(
+        place,
+        mixed,
+        *weights,
+        gathered,
+        gathered,
+        gain[None, :],
+        router,
+        cotangent,
+        *experts,
+    )
 
 
 def product_kernel(
@@ -598,51 +648,6 @@
         compiler_params=pltpu.CompilerParams(vmem_limit_bytes=58 << 20),
         cost_estimate=pl.CostEstimate(flops=0, bytes_accessed=tokens, transcendentals=0),
     )(left, gate, up, scaled_one, scaled_two, live, live)
-
-
-def gradient_kernel(
-    place_ref, grad_gate_ref, grad_up_ref, extra_ref, gate_weight_ref, up_weight_ref, grad_ref
-):
-    experts_own, features = gate_weight_ref.shape[:2]
-    one = [slot_of(e, place_ref[2], experts_own) for e in range(experts_own)]
-    two = [slot_of(e, place_ref[3], experts_own) for e in range(experts_own)]
-    size = 512
-
-    @pl.loop(0, features // size)
-    def _(index):
-        part = pl.ds(pl.multiple_of(index * size, size), size)
-        grad = 0.0
-        for e in range(experts_own):
-            grad = grad + dot(grad_gate_ref[one[e]], gate_weight_ref[e, part, :], COLUMNS)
-            grad = grad + dot(grad_up_ref[two[e]], up_weight_ref[e, part, :], COLUMNS)
-        grad_ref[:, part] = grad.astype(jnp.bfloat16)
-
-    grad_ref[:, features:] = extra_ref[...]
-
-
-def gradient_rows(place, grad_gate_pre, grad_up_pre, extra, w_gate, w_up, block):
-    experts_own, tokens, hidden = grad_gate_pre.shape
-    features = w_gate.shape[1]
-    rows = lambda columns: pl.BlockSpec((block, columns), lambda i, p: (i, 0))
-    spread = pl.BlockSpec((experts_own, block, hidden), lambda i, p: (0, i, 0))
-    return pl.pallas_call(
-        gradient_kernel,
-        out_shape=jax.ShapeDtypeStruct((tokens, features + extra.shape[1]), jnp.bfloat16),
-        grid_spec=pltpu.PrefetchScalarGridSpec(
-            num_scalar_prefetch=1,
-            grid=(tokens // block,),
-            in_specs=[
-                spread,
-                spread,
-                rows(extra.shape[1]),
-                whole_block(*w_gate.shape),
-                whole_block(*w_up.shape),
-            ],
-            out_specs=rows(features + extra.shape[1]),
-        ),
-        compiler_params=pltpu.CompilerParams(vmem_limit_bytes=52 << 20),
-        cost_estimate=pl.CostEstimate(flops=0, bytes_accessed=tokens, transcendentals=0),
-    )(place, grad_gate_pre, grad_up_pre, extra, w_gate, w_up)
 
 
 def output_kernel(place_ref, scaled_ref, down_weight_ref, out_ref):
@@ -741,10 +746,10 @@
             grid=(1,),
             in_specs=[
                 whole_block(*sums.shape),
-                rows(experts),
+                whole_block(*gates.shape),
                 whole_block(*router.shape),
                 whole_block(1, features),
-                rows(features),
+                whole_block(*middle.shape),
                 rows(features),
                 whole_block(*weights[0].shape),
                 whole_block(*weights[1].shape),
@@ -882,7 +887,7 @@
                 token_rows(block, own, features)[0],
                 rows(features),
                 whole_block(1, features),
-                pl.BlockSpec((own, features), lambda i, p: (p[1], 0)),
+                whole_block(own, features),
                 whole_block(*logits.shape),
                 rows(features),
                 rows(rows_own),
@@ -977,9 +982,10 @@
     return jnp.where(flags_ref[2 + side] > 0, own_ref[rows, :], came_ref[rows, :])
 
 
-def into_kernel(flags_ref, side, own_ref, came_ref, low_ref, high_ref, out_ref):
+def into_kernel(flags_ref, side, own_ref, came_ref, first_ref, second_ref, third_ref, out_ref):
     rows = own_ref.shape[0]
     rest = out_ref.shape[0] - rows
+    half = first_ref.shape[0]
     kept = pl.program_id(0) == flags_ref[side]
 
     @pl.when(kept)
@@ -991,11 +997,12 @@
 
     @pl.when(jnp.logical_not(kept))
     def _():
-        out_ref[:rows, :] = low_ref[...].astype(jnp.float32)
-        out_ref[rows:, :] = high_ref[:rest, :].astype(jnp.float32)
-
-
-def into_output(flags, side, own, came, low, high):
+        out_ref[:half, :] = first_ref[...].astype(jnp.float32)
+        out_ref[half:rows, :] = second_ref[...].astype(jnp.float32)
+        out_ref[rows:, :] = third_ref[:rest, :].astype(jnp.float32)
+
+
+def into_output(flags, side, own, came, first, second, third):
     rows, hidden = own.shape
     total = 2 * rows * 2 // 3
     whole = lambda array: pl.BlockSpec(array.shape, lambda e, k: (0, 0))
@@ -1006,12 +1013,12 @@
         grid_spec=pltpu.PrefetchScalarGridSpec(
             num_scalar_prefetch=1,
             grid=(2,),
-            in_specs=[whole(own), whole(came), whole(low), whole(high)],
+            in_specs=[whole(own), whole(came), whole(first), whole(second), whole(third)],
             out_specs=pl.BlockSpec((None, total, hidden), lambda e, k: (e, 0, 0)),
         ),
         compiler_params=pltpu.CompilerParams(vmem_limit_bytes=40 << 20),
         cost_estimate=pl.CostEstimate(flops=0, bytes_accessed=rows, transcendentals=0),
-    )(flags, own, came, low, high)
+    )(flags, own, came, first, second, third)
 
 
 def down_kernel(flags_ref, *refs):
@@ -1019,11 +1026,11 @@
     hidden = out_ref.shape[0]
     narrow = hidden // 2
     for side in range(2):
-        own_ref, came_ref, high_ref, last_ref = refs[4 * side : 4 * side + 4]
+        own_ref, came_ref, third_ref, last_ref = refs[4 * side : 4 * side + 4]
         rows = own_ref.shape[0]
         rest = rows - out_ref.shape[1] // 2
         mine = upper_rows(flags_ref, side, own_ref, came_ref, slice(rest, rows))
-        theirs = jnp.concatenate([high_ref[rest:, :], last_ref[...]], 0)
+        theirs = jnp.concatenate([third_ref[rest:, :], last_ref[...]], 0)
         kept = pl.program_id(0) == flags_ref[side]
         value = jnp.where(kept, mine, theirs).astype(jnp.float32)
         start = side * value.shape[0]
@@ -1092,14 +1099,12 @@
     def ends(self, *others):
         self.own = self.sent
         self.came = after(self.flying, *others)
-        bit = self.order[1]
+        upper = has(self.order[1])
         half = self.own.shape[0] // 2
-        low = jnp.where(has(bit), self.came, self.own)
-        pieces = [low] + [
-            jnp.where(has(bit), self.own[rows], self.came[rows])
-            for rows in (slice(0, half), slice(half, 2 * half))
-        ]
-        return pieces
+        begin, end = slice(0, half), slice(half, 2 * half)
+        low = lambda rows: jnp.where(upper, self.came[rows], self.own[rows])
+        high = lambda rows: jnp.where(upper, self.own[rows], self.came[rows])
+        return [low(begin), low(end), high(begin), high(end)]
 
     def last(self, piece):
         return swap(piece, self.order[0])
@@ -1218,6 +1223,102 @@
     def join(self, *others):
         bit = self.order[self.stage]
         self.value = join(self.value, after(self.flying, *others), bit, self.axis(bit))
+
+
+def scalar_call(kernel, outs, scalars, *operands, scratch=(), flops=0):
+    whole = lambda array: pl.BlockSpec(array.shape, lambda i, p: (0,) * len(array.shape))
+    return pl.pallas_call(
+        kernel,
+        out_shape=outs,
+        grid_spec=pltpu.PrefetchScalarGridSpec(
+            num_scalar_prefetch=1,
+            grid=(1,),
+            in_specs=[whole(array) for array in operands],
+            out_specs=[whole(out) for out in outs],
+            scratch_shapes=scratch,
+        ),
+        name="scalar_call",
+        compiler_params=pltpu.CompilerParams(vmem_limit_bytes=58 << 20),
+        cost_estimate=pl.CostEstimate(flops=flops, bytes_accessed=1024, transcendentals=0),
+    )(scalars, *operands)
+
+
+def pack_kernel(size, side, place_ref, *refs):
+    chips = size // 2
+    values = refs[:4]
+    out_ref = refs[4 + chips]
+    all_ref = refs[5 + chips]
+    for h in range(2):
+        total = values[2 * h][...] + values[2 * h + 1][...].astype(jnp.float32)
+        total = total.astype(jnp.bfloat16)
+        for c in range(chips):
+            all_ref[h * chips + c] = total[:, c * side : (c + 1) * side]
+        out_ref[h] = total[:, chips * side :]
+    for k in range(chips):
+        chip = lax.rem(place_ref[0] - k + chips, chips)
+        for core in range(2):
+            refs[4 + k][core] = all_ref[2 * chip + core]
+
+
+def pack_heads(place, cubes, size, side):
+    chips = size // 2
+    share, line = cubes[0].value.shape[-2:]
+    low = jnp.bfloat16
+    outs = [jax.ShapeDtypeStruct((2, share, side), low)] * chips
+    outs.append(jax.ShapeDtypeStruct((2, share, line - chips * side), low))
+    operands = []
+    for cube in cubes:
+        operands += [cube.value.reshape(share, line), cube.flying.reshape(share, line)]
+    *parcels, out_sums = scalar_call(
+        lambda *refs: pack_kernel(size, side, *refs),
+        outs,
+        place,
+        *operands,
+        scratch=[pltpu.VMEM((size, share, side), low)],
+        flops=200000000000,
+    )
+    return parcels, out_sums
+
+
+def split_kernel(place_ref, *refs):
+    chips = len(refs) - 2
+    core = lax.rem(place_ref[1], 2)
+    for k in range(chips):
+        refs[chips][k] = refs[k][core]
+        refs[chips + 1][k] = refs[k][1 - core]
+
+
+def split_cores(place, got):
+    out = jax.ShapeDtypeStruct((len(got),) + got[0].shape[1:], got[0].dtype)
+    return scalar_call(split_kernel, [out, out], place, *got)
+
+
+def unpack_kernel(place_ref, stay_ref, came_ref, out_ref, low_ref, high_ref, all_ref):
+    chips, _, side = stay_ref.shape
+    core = lax.rem(place_ref[1], 2)
+    for k in range(chips):
+        chip = lax.rem(place_ref[0] + k, chips)
+        all_ref[2 * chip + core] = stay_ref[k]
+        all_ref[2 * chip + 1 - core] = came_ref[k]
+    for h, rows_ref in enumerate((low_ref, high_ref)):
+        for c in range(chips):
+            rows_ref[:, c * side : (c + 1) * side] = all_ref[h * chips + c]
+        rows_ref[:, chips * side :] = out_ref[h]
+
+
+def unpack_heads(place, stay, came, out_sums):
+    chips, share, side = stay.shape
+    line = chips * side + out_sums.shape[2]
+    out = jax.ShapeDtypeStruct((share, line), stay.dtype)
+    return scalar_call(
+        unpack_kernel,
+        [out, out],
+        place,
+        stay,
+        came,
+        out_sums,
+        scratch=[pltpu.VMEM((2 * chips, share, side), stay.dtype)],
+    )
 
 
 class Exchange:
@@ -1370,21 +1471,35 @@
     ).reshape(groups, tokens // 2, 2 * query_width)
     w_out_halves = out_exchange.finish()
 
-    middle, normed_two, gates = middle_rows(
-        mixed_all, w_out_halves, gathered, gain_two, router_all, own, block
-    )
     flag = lambda bit: has(bit).astype(jnp.int32)
     place = jnp.stack([chip, me, flag(bits[0]), flag(bits[-1])]).astype(jnp.int32)
-    scaled_one, scaled_two, grad_gate_pre, grad_up_pre, grad_live, extra = expert_rows(
-        place, normed_two, cotangent, gathered, gates, w_gate, w_up, w_down, own, block
-    )
-    def mine(array):
-        return lax.dynamic_slice_in_dim(array, me * own, own, 0)
+    (
+        normed_two,
+        scaled_one,
+        scaled_two,
+        grad_gate_pre,
+        grad_up_pre,
+        grad_live,
+        grad_rows,
+        middle_own,
+        normed_own,
+        gates_own,
+    ) = layer_rows(
+        place,
+        mixed_all,
+        w_out_halves,
+        gathered,
+        gain_two,
+        router_all,
+        cotangent,
+        (w_gate, w_up, w_down),
+        own,
+        block,
+    )
 
     products = lambda e, dtype: expert_products(
         normed_two, grad_gate_pre, grad_up_pre, scaled_one, scaled_two, grad_live, e, dtype
     )
-    grad_rows = gradient_rows(place, grad_gate_pre, grad_up_pre, extra, w_gate, w_up, block)
     grad_two_sum = lax.psum_scatter(grad_rows, "ctx", scatter_dimension=0, tiled=True)
     normed_two, grad_live = after((normed_two, grad_live), grad_rows)
     chains = [Chain(bits), Chain(bits[::-1])]
@@ -1398,10 +1513,10 @@
     grad_middle, grad_branch, grad_mixed, grad_logits, gain_two_grad = turn_rows(
         place,
         after(grad_two_sum, out_rows),
-        gates,
+        gates_own,
         router_all,
         gain_two,
-        middle,
+        middle_own,
         grad_live,
         w_out_halves,
     )
@@ -1451,7 +1566,7 @@
         gathered,
         normed_one,
         gain_two_grad,
-        normed_two,
+        normed_own,
         grad_logits,
         out_rows,
         lax.dynamic_slice_in_dim(mixed, copy_index * rows_own, rows_own, 1),
@@ -1481,55 +1596,44 @@
     first = [chain.last(part[0]) for chain, part in zip(chains, pieces)]
     second = [chain.last(after(part[1], *sent)) for chain, part in zip(chains, pieces)]
     for cube in cubes:
-        cube.add()
-    totals = [cube.value.astype(jnp.bfloat16) for cube in cubes]
-    blocks = jnp.concatenate(
-        [
-            jnp.transpose(
-                total.reshape(share, -1)[:, :line].reshape(share, size // 2, side_width), (1, 0, 2)
-            )
-            for total in totals
-        ],
-        0,
-    )
-    got = deal_chips(after(blocks, *first))
-    head_sums = deal_cores(after(got, *second))
-    for h, cube in enumerate(cubes):
-        rows = jnp.transpose(head_sums[h * (size // 2) : (h + 1) * (size // 2)], (1, 0, 2))
-        rows = jnp.concatenate(
-            [rows.reshape(share, line), totals[h].reshape(share, -1)[:, line:]], 1
+        cube.flying = after(cube.flying, *sent)
+    parcels, out_sums = pack_heads(place, cubes, size, side_width)
+    parcels = after(parcels, *first)
+    got = [parcels[0]] + [from_chip(parcels[k], k) for k in range(1, chips)]
+    stay, go = split_cores(place, got)
+    came = from_core(after(go, *second))
+    third = [chain.last(after(part[2], *second)) for chain, part in zip(chains, pieces)]
+    for cube, value in zip(cubes, unpack_heads(place, stay, came, out_sums)):
+        cube.value = value.reshape((1,) * len(bits) + value.shape)
+    sent = [cube.back() for cube in cubes]
+    fourth = [chain.last(after(part[3], *third)) for chain, part in zip(chains, pieces)]
+    flags = jnp.stack([flag(chain.order[n]) for n in range(2) for chain in chains])
+    while cubes[0].stage > 0:
+        for cube in cubes:
+            cube.join(*third)
+        sent = [cube.back() for cube in cubes]
+    grad_gate, grad_up = [
+        into_output(
+            flags,
+            side,
+            *after((chain.own, chain.came, first[side], second[side], third[side]), *sent),
         )
-        cube.value = rows.reshape(totals[h].shape)
-    sent = [cube.back() for cube in cubes]
-    third = [
-        chain.last(after(part[2], *sent)) for chain, part in zip(chains, pieces)
-    ]
-    flags = jnp.stack([flag(chain.order[n]) for n in range(2) for chain in chains])
-    came = [cube.flying for cube in cubes]
-    grad_gate, grad_up = [
-        into_output(flags, side, *after((chain.own, chain.came, first[side], second[side]), *came))
         for side, chain in enumerate(chains)
     ]
-    for cube in cubes:
-        cube.join(*sent)
-    while cubes[0].stage > 0:
-        sent = [cube.back() for cube in cubes]
-        if cubes[0].stage > 0:
-            for cube in cubes:
-                cube.join(*sent)
-    output = jnp.where((segments[0] != 0)[:, None], mine(after(middle, grad_mixed)) + out_sum, 0.0)
+    output = jnp.where((segments[0] != 0)[:, None], middle_own + out_sum, 0.0)
     own_hidden = inputs[0].astype(jnp.float32)
     own_scale = lax.rsqrt(jnp.mean(own_hidden * own_hidden, -1, keepdims=True) + EPS)
     grad_in = grad_middle + norm_back(grad_one * gain_one, own_hidden * own_scale, own_scale)
+    for cube in cubes:
+        cube.join(grad_gate, grad_up, output, grad_in)
+    head_outs = head_outputs(
+        *[cube.value.reshape(rows_own, -1) for cube in cubes], copies, side_width, experts_all
+    )
     operands = []
     for side, chain in enumerate(chains):
-        operands += [chain.own, chain.came, second[side], third[side]]
-    grad_down = down_output(flags, *after(operands, *sent))
-    for cube in cubes:
-        cube.join(grad_down)
-    head_outs = head_outputs(
-        *[cube.value.reshape(rows_own, -1) for cube in cubes], copies, side_width, experts_all
-    )
+        operands += [chain.own, chain.came, third[side], fourth[side]]
+    grad_down = down_output(flags, *after(operands, head_outs))
+
     return (
         output.astype(jnp.bfloat16)[None],
         grad_in[None],

time: 457 us -> 432 us (0.945)
  waiting for transfers between devices: 153 us -> 131 us
    ppermute x28 -> x30, waiting for transfers between devices: 104 us -> 80.4 us  [swap(): return lax.ppermute(value, 'rep', [(i, i ^ bit) for i in range(size)])]
    unnamed x90 -> x118, local copies, waits for them, and re-layouts: 9.27 us -> 11.7 us
    ppermute x28 -> x30, starting transfers between devices: 34.9 us -> 32.6 us  [swap(): return lax.ppermute(value, 'rep', [(i, i ^ bit) for i in range(size)])]
    pallas_call x3 -> x4, Pallas kernels: 45.2 us -> 47.4 us  [the longest x1 39.4 us: layer_rows(): pl.pallas_call(layer_kernel, out_shape=(shaped((tokens, features), low),...]
  transfers between devices with their start and end apart: 42 -> 44, of which waited for: 24 -> 27; matrix products, arithmetic and copies ran while one was open for 9% -> 10% of each run, Pallas kernels for 26% -> 28%
where the time goes in v10:
time: 432 us; the launch traced here: 430 us
  Pallas kernels  165 us (38%)
  waiting for transfers between devices  131 us (30%)
  starting transfers between devices  40.2 us (9%)
  other arithmetic  32.4 us (8%)
  blocking collectives  24.5 us (6%)
  local copies, waits for them, and re-layouts  22.4 us (5%)
  between operations  14.8 us (3%)
    ppermute x30, waiting for transfers between devices, swap(): return lax.ppermute(value, 'rep', [(i, i ^ bit) for i in range(size)])  80.4 us
    pallas_call x1, Pallas kernels, layer_rows(): pl.pallas_call(layer_kernel, out_shape=(shaped((tokens, features), low),...  39.4 us
    ppermute x30, starting transfers between devices, swap(): return lax.ppermute(value, 'rep', [(i, i ^ bit) for i in range(size)])  32.6 us
    pallas_call x2, Pallas kernels, expert_products(): pl.pallas_call(product_kernel, out_shape=(jax.ShapeDtypeStruct((rows, hid...  28.8 us
    all_to_all x1, blocking collectives, per_device(): lax.all_to_all(head_columns, 'ctx', split_axis=0, concat_axis=0, tiled=True)  24.5 us
    all_gather x1, waiting for transfers between devices, per_device(): gathered = lax.all_gather(rows, 'ctx', axis=0)  16.5 us
    pallas_call x1, Pallas kernels, attend(): pl.pallas_call(attend_kernel, out_shape=(shaped((tokens, features), jnp.b...  16 us
    pallas_call x1, Pallas kernels, close_rows(): pl.pallas_call(lambda *refs: close_kernel(reps, *refs), name='close', out...  14.6 us
  transfers between devices with their start and end apart: 44, of which 27 were waited for; matrix products, arithmetic and copies ran while one was open for 10% of the time, Pallas kernels for 28%

profile of v10, /device:TPU:0, one launch (start us, length us, event | category | flops | bytes accessed | tf_op | source)
XLA Modules:
  0.0 430.3 jit_solution(3802379947226608004)
XLA Ops:
  9.5 1.9 fusion.12
  15.3 24.5 %all_to_all.5 = bf16[8,48,384]{2,1,0:T(8,128)(2,1)S(1)} all-to-all(bf16[8,48,384]{2,1,0:T(8,128)(2,1)S(1)} %copy.54), channel_id=1, replica_groups=mesh['rep'=4,'ctx'=8] {'ctx'}, dimensions={0} | all-to-all | bytes 589824 | tf_op jit(solution)/shard_map/all_to_all | solution.py:1441
  39.8 1.6 collective-permute-start
  42.9 2.8 collective-permute-done
  47.8 1.6 collective-permute-start.1
  49.4 5.6 %collective-permute-done.3 = bf16[4,2,1,48,384]{4,3,0,2,1:T(8,128)(2,1)S(1)} collective-permute-done((bf16[4,2,1,48,384]{4,3,0,2,1:T(8,128)(2,1)S(1)}, bf16[4,2,1,48,384]{4,3,0,2,1:T(8,128)(2,1)S(1)}, u32[]{:S(2)}, u32[]{:S(2)}) %collective-permute-start.3) | collective-permute-done | bytes 294944 | tf_op jit(solution)/shard_map/ppermute | solution.py:1067
  55.0 16.5 %all-gather.11.cloned.1.call-done = bf16[1408,1664]{1,0:T(8,128)(2,1)} async-done(((bf16[176,1664]{1,0:T(8,128)(2,1)}), bf16[1408,1664]{1,0:T(8,128)(2,1)}) %all-gather.11.cloned.1.call-update) | async-done | bytes 4685840 | tf_op jit(solution)/shard_map/all_gather | solution.py:1412
  72.8 1.6 collective-permute-start.5
  76.9 16.0 %shard_map.238 = (bf16[1024,1536]{1,0:T(8,128)(2,1)}, bf16[1024,192]{1,0:T(8,128)(2,1)S(1)}, bf16[1024,64]{1,0:T(8,128)(2,1)S(1)}, bf16[1024,64]{1,0:T(8,128)(2,...) custom-call(bf16[8,176,1664]{2,1,0:T(8,128)(2,1)} %bitcast.132, ...), custom_call_target="tpu_custom_call" | custom-call | bytes 1024 | tf_op jit(solution)/shard_map/pallas_call | solution.py:194
  93.0 2.2 broadcast_select_fusion.13
  98.1 12.3 %all-gather.7.cloned.1.call-done.cotangent_ref = bf16[1024,1536]{1,0:T(8,128)(2,1)} async-done(((bf16[128,1536]{1,0:T(8,128)(2,1)}), bf16[1024,1536]{1,0:T(8,128)(2,1)}) %all-gather.7.cloned.1.call-update) | async-done | bytes 3145744 | tf_op jit(solution)/shard_map/all_gather | solution.py:1413
  115.6 23.3 %collective-permute-done.6 = bf16[4,1,2,48,1536]{4,3,0,2,1:T(8,128)(2,1)} collective-permute-done((bf16[4,1,2,48,1536]{4,3,0,2,1:T(8,128)(2,1)}, bf16[4,1,2,48,1536]{4,3,0,2,1:T(8,128)(2,1)}, u32[]{:S(2)}, u32[]{:S(2)}) %collective-permute-start.6) | collective-permute-done | bytes 1179680 | tf_op jit(solution)/shard_map/ppermute | solution.py:1067
  140.6 1.6 copy.57
  142.6 1.6 copy.58
  144.2 5.5 %all-gather.13.cloned.1.call-done = bf16[4096,384]{1,0:T(8,128)(2,1)} async-done(((bf16[512,384]{1,0:T(8,128)(2,1)}), bf16[4096,384]{1,0:T(8,128)(2,1)}) %all-gather.13.cloned.1.call-update) | async-done | bytes 3145744 | tf_op jit(solution)/shard_map/all_gather | solution.py:1463
  149.7 39.4 %shard_map.239 = (bf16[1024,1536]{1,0:T(8,128)(2,1)}, bf16[2,1024,512]{2,1,0:T(8,128)(2,1)}, bf16[2,1024,512]{2,1,0:T(8,128)(2,1)}, bf16[2,1024,512]{2,1,0:T(8,1...) custom-call(s32[4]{0:T(128)} %pad_add_fusion.place_ref.refs_0_, ...), custom_call_target="tpu_custom_call" | custom-call | flops 19327352832 | bytes 40894464 | tf_op jit(solution)/shard_map/pallas_call | solution.py:513
  189.4 13.6 %shard_map.240 = (bf16[2304,512]{1,0:T(8,128)(2,1)}, bf16[2304,512]{1,0:T(8,128)(2,1)}) custom-call(bf16[1024,1536]{1,0:T(8,128)(2,1)} %get-tuple-element.136.left_ref, bf16[2,1024,512]{2,1,0:T(8,128)(2,1)} %get-tuple-element.131.gate_ref, bf16[2,1024,512]{2,1,0:T(8,128)(2,1)} %get-tuple-element.132.up_ref, ...), custom_call_target="tpu_custom_call" | custom-call | bytes 1024 | tf_op jit(solution)/shard_map/pallas_call | solution.py:635
  206.0 15.2 %shard_map.241 = (f32[2304,512]{1,0:T(8,128)}, f32[2304,512]{1,0:T(8,128)}) custom-call(bf16[1024,1536]{1,0:T(8,128)(2,1)} %get-tuple-element.136.left_ref, bf16[2,1024,512]{2,1,0:T(8,128)(2,1)} %get-tuple-element.131.gate_ref, bf16[2,1024,512]{2,1,0:T(8,128)(2,1)} %get-tuple-element.132.up_ref, ...), custom_call_target="tpu_custom_call" | custom-call | bytes 1024 | tf_op jit(solution)/shard_map/pallas_call | solution.py:635
  221.3 8.9 %shard_map.242.refs_9_ = bf16[1024,1536]{1,0:T(8,128)(2,1)} custom-call(s32[4]{0:T(128)S(1)} %copy-done.19, bf16[2,1024,512]{2,1,0:T(8,128)(2,1)} %get-tuple-element.140.scaled_one_ref.scaled_ref, bf16[2,512,1536]{2,1,0:T(8,128)(2,1)} %down_weight_ref.1), custom_call_target="tpu_custom_call" | custom-call | bytes 1024 | tf_op jit(solution)/shard_map/pallas_call | solution.py:670
  230.9 6.8 %shard_map.243 = (f32[128,1536]{1,0:T(8,128)}, bf16[128,1536]{1,0:T(8,128)(2,1)}, bf16[8,128,192]{2,1,0:T(8,128)(2,1)}, bf16[128,16]{1,0:T(8,128)(2,1)}, f32[1,1536]{1,0:T(1,128)}) custom-call(s32[4]{0:T(128)} %pad_add_fusion.place_ref.refs_0_, bf16[128,1664]{1,0:T(8,128)(2,1)} %reduce-scatter.3.cloned.1.call-done.sum_ref, ...), custom_call_target="tpu_custom_call" | custom-call | bytes 128 | tf_op jit(solution)/shard_map/pallas_call | solution.py:741
  237.6 1.8 dynamic-slice_bitcast_fusion.5
  240.5 2.8 collective-permute-start.8
  244.0 4.0 collective-permute-done.10
  248.1 3.6 collective-permute-done.9
  251.7 2.0 pad_maximum_fusion.9
  253.7 3.0 collective-permute-done.11.refs_1_
  258.0 5.6 %shard_map.244 = (bf16[1152,512]{1,0:T(8,128)(2,1)}, bf16[1152,512]{1,0:T(8,128)(2,1)}) custom-call(s32[2]{0:T(128)} %add_convert_fusion.keeps_ref, f32[2304,512]{1,0:T(8,128)} %get-tuple-element.138.refs_0_, bf16[2304,512]{1,0:T(8,128)(2,1)} %collective-permute-done.11.refs_1_, f32[2304,512]{1,0:T(8,128)} %get-tuple-element.139.refs_2_.refs_3_, ...), custom_call_target="tpu_custom_call" | custom-call | flops 70778880000 | bytes 14155776 | tf_op jit(solution)/shard_map/pallas_call | solution.py:1141
  265.6 1.8 select_bitcast_fusion
  267.4 1.7 collective-permute-done.13
  270.5 14.3 %shard_map.245 = (bf16[1024,192]{1,0:T(8,128)(2,1)S(1)}, bf16[1024,128]{1,0:T(8,128)(2,1)S(1)}) custom-call(bf16[1024,192]{1,0:T(8,128)(2,1)S(1)} %get-tuple-element.124.query_ref, bf16[1024,192]{1,0:T(8,128)(2,1)S(1)} %bitcast.130, f32[3,1024,1]{2,1,0:T(8,128)S(1)} %copy-done.15, f32[1024,64]{1,0:T(8,128)S(1)} %get-tuple-element.150.cosine_ref.key_cosine_ref, ...), custom_call_target="tpu_custom_call" | custom-call | bytes 1024 | tf_op jit(solution)/shard_map/pallas_call | solution.py:323
  286.3 4.5 %collective-permute-done.14.refs_2_ = bf16[1152,512]{1,0:T(8,128)(2,1)} collective-permute-done((bf16[1152,512]{1,0:T(8,128)(2,1)}, bf16[1152,512]{1,0:T(8,128)(2,1)}, u32[]{:S(2)}, u32[]{:S(2)}) %collective-permute-start.14) | collective-permute-done | bytes 1179680 | tf_op jit(solution)/shard_map/ppermute | solution.py:1067
  292.1 6.1 %shard_map.246 = (bf16[1152,512]{1,0:T(8,128)(2,1)}, bf16[1152,512]{1,0:T(8,128)(2,1)}) custom-call(s32[2]{0:T(128)} %add_convert_fusion.keeps_ref, f32[2304,512]{1,0:T(8,128)} %get-tuple-element.138.refs_0_, bf16[2304,512]{1,0:T(8,128)(2,1)} %collective-permute-done.11.refs_1_, bf16[1152,512]{1,0:T(8,128)(2,1)} %collective-permute-done.14.refs_2_, ...), custom_call_target="tpu_custom_call" | custom-call | bytes 2304 | tf_op jit(solution)/shard_map/pallas_call | solution.py:1180
  300.4 14.6 %close.1 = (bf16[1024,3072]{1,0:T(8,128)(2,1)}, f32[96,2304]{1,0:T(8,128)}, f32[96,2304]{1,0:T(8,128)}, bf16[96,2304]{1,0:T(8,128)(2,1)}, bf16[96,2304]{1,0:T(8,128)(2,1)}) custom-call(s32[4]{0:T(128)} %pad_add_fusion.place_ref.refs_0_, bf16[1024,192]{1,0:T(8,128)(2,1)} %copy-done.17, bf16[1024,128]{1,0:T(8,128)(2,1)} %copy-done.18, ...), custom_call_target="tpu_custom_call" | custom-call | bytes 1024 | tf_op jit(solution)/shard_map/close/pallas_call | solution.py:870
  316.6 7.6 %collective-permute-done.17.refs_1_ = bf16[1152,512]{1,0:T(8,128)(2,1)S(1)} collective-permute-done((bf16[1152,512]{1,0:T(8,128)(2,1)}, bf16[1152,512]{1,0:T(8,128)(2,1)S(1)}, u32[]{:S(2)}, u32[]{:S(2)}) %collective-permute-start.17) | collective-permute-done | bytes 1179680 | tf_op jit(solution)/shard_map/ppermute | solution.py:1067
  326.0 1.8 collective-permute-done.18.refs_1_.refs_5_
  332.0 5.3 %collective-permute-done.16 = bf16[2,1,48,2304]{3,2,1,0:T(8,128)(2,1)S(1)} collective-permute-done((bf16[2,1,48,2304]{3,2,1,0:T(8,128)(2,1)}, bf16[2,1,48,2304]{3,2,1,0:T(8,128)(2,1)S(1)}, u32[]{:S(2)}, u32[]{:S(2)}) %collective-permute-start.16) | collective-permute-done | bytes 442400 | tf_op jit(solution)/shard_map/ppermute | solution.py:1067
  337.4 1.6 collective-permute-start.19
  343.9 11.3 %collective-permute-done.19 = bf16[1,1,48,2304]{3,2,1,0:T(8,128)(2,1)S(1)} collective-permute-done((bf16[1,1,48,2304]{3,2,1,0:T(8,128)(2,1)S(1)}, bf16[1,1,48,2304]{3,2,1,0:T(8,128)(2,1)S(1)}, u32[]{:S(2)}, u32[]{:S(2)}) %collective-permute-start.19) | collective-permute-done | bytes 221216 | tf_op jit(solution)/shard_map/ppermute | solution.py:1067
  356.9 3.0 scalar_call.3
  364.5 2.2 collective-permute-done.28.refs_3_
  367.3 3.2 collective-permute-done.25.refs_2_
  372.3 2.4 scalar_call.4
  376.9 2.5 scalar_call.5
  381.1 6.0 %collective-permute-done.30 = bf16[1,1,48,2304]{3,2,1,0:T(8,128)(2,1)S(1)} collective-permute-done((bf16[1,1,48,2304]{3,2,1,0:T(8,128)(2,1)}, bf16[1,1,48,2304]{3,2,1,0:T(8,128)(2,1)S(1)}, u32[]{:S(2)}, u32[]{:S(2)}) %collective-permute-start.30) | collective-permute-done | bytes 221216 | tf_op jit(solution)/shard_map/ppermute | solution.py:1067
  394.3 4.7 %into_output.2 = f32[2,1536,512]{2,1,0:T(8,128)} custom-call(s32[4]{0:T(128)S(1)} %pad_add_fusion.1.k.flags_ref, bf16[1152,512]{1,0:T(8,128)(2,1)S(1)} %copy-done.2, bf16[1152,512]{1,0:T(8,128)(2,1)S(1)} %copy-done.7, bf16[576,512]{1,0:T(8,128)(2,1)} %collective-permute-done.22.refs_2_, bf16[576,512]{1,0:T(8,128)(2,1)} %collective-permute-done.27.refs_3_, ...), custom_call_target="tpu_custom_call" | custom-call | bytes 1152 | tf_op jit(solution)/shard_map/into_output/pallas_call | solution.py:1009
  399.0 4.7 %into_output.3 = f32[2,1536,512]{2,1,0:T(8,128)} custom-call(s32[4]{0:T(128)S(1)} %pad_add_fusion.1.k.flags_ref, bf16[1152,512]{1,0:T(8,128)(2,1)S(1)} %copy-done.5, bf16[1152,512]{1,0:T(8,128)(2,1)S(1)} %copy-done.10, bf16[576,512]{1,0:T(8,128)(2,1)} %collective-permute-done.23.refs_2_, bf16[576,512]{1,0:T(8,128)(2,1)} %collective-permute-done.28.refs_3_, ...), custom_call_target="tpu_custom_call" | custom-call | bytes 1152 | tf_op jit(solution)/shard_map/into_output/pallas_call | solution.py:1009
  411.0 2.0 head_outputs.1
  418.6 4.9 %shard_map.247 = f32[2,512,1536]{2,1,0:T(8,128)} custom-call(s32[4]{0:T(128)S(1)} %pad_add_fusion.1.k.flags_ref, bf16[1152,512]{1,0:T(8,128)(2,1)S(1)} %copy-done.3, bf16[1152,512]{1,0:T(8,128)(2,1)S(1)} %copy-done.8, bf16[576,512]{1,0:T(8,128)(2,1)S(1)} %collective-permute-done.31.refs_4_.refs_2_, bf16[576,512]{1,0:T(8,128)(2,1)} %collective-permute-done.36.refs_3_, ...), custom_call_target="tpu_custom_call" | custom-call | bytes 1152 | tf_op jit(solution)/shard_map/pallas_call | solution.py:1046
  (263 shorter events, 84.1 us)
Async XLA Ops:
  7.2 64.3 %all-gather.11.cloned.1.call-start = ((), (), s32[]{:S(2)}) async-start(), calls=%async_computation.7 | async-start | bytes 5271552 | tf_op jit(solution)/shard_map/all_gather | solution.py:1412
  11.4 98.9 %all-gather.7.cloned.1.call-start = ((), (), s32[]{:S(2)}) async-start(), calls=%async_computation.3 | async-start | bytes 3538944 | tf_op jit(solution)/shard_map/all_gather | solution.py:1413
  12.1 137.6 %all-gather.13.cloned.1.call-start = ((), (), s32[]{:S(2)}) async-start(), calls=%async_computation.8 | async-start | bytes 3538944 | tf_op jit(solution)/shard_map/all_gather | solution.py:1463
  39.8 5.9 %collective-permute-start = (bf16[4,1,1,48,384]{4,3,0,2,1:T(8,128)(2,1)S(1)}, bf16[4,1,1,48,384]{4,3,0,2,1:T(8,128)(2,1)S(1)}, u32[]{:S(2)}, u32[]{:S(2)}) collective-permute-start(bf16[4,1,1,48,384]{4,3,0,2,1:T(8,128)(2,1)S(1)} %get-tuple-element.310), channel_id=1, source_target_pairs={{0,8},{8,0},{16,24},{24,16},{1,9},{9,1},{17,25},{25,17},{2,10},{10... | collective-permute-start | bytes 442376 | tf_op jit(solution)/shard_map/ppermute | solution.py:1067
  41.4 5.5 %collective-permute-start.2 = (bf16[4,1,1,48,384]{4,3,0,2,1:T(8,128)(2,1)S(1)}, bf16[4,1,1,48,384]{4,3,0,2,1:T(8,128)(2,1)S(1)}, u32[]{:S(2)}, u32[]{:S(2)}) collective-permute-start(bf16[4,1,1,48,384]{4,3,0,2,1:T(8,128)(2,1)S(1)} %get-tuple-element.311), channel_id=1, source_target_pairs={{0,16},{8,24},{16,0},{24,8},{1,17},{9,25},{17,1},{25,9},{2,18},{10... | collective-permute-start | bytes 442376 | tf_op jit(solution)/shard_map/ppermute | solution.py:1067
  47.0 8.0 %collective-permute-start.3 = (bf16[4,2,1,48,384]{4,3,0,2,1:T(8,128)(2,1)S(1)}, bf16[4,2,1,48,384]{4,3,0,2,1:T(8,128)(2,1)S(1)}, u32[]{:S(2)}, u32[]{:S(2)}) collective-permute-start(bf16[4,2,1,48,384]{4,3,0,2,1:T(8,128)(2,1)S(1)} %pad_maximum_fusion.13), channel_id=1, source_target_pairs={{0,8},{8,0},{16,24},{24,16},{1,9},{9,1},{17,25},{25,17},{2,10},{10... | collective-permute-start | bytes 884744 | tf_op jit(solution)/shard_map/ppermute | solution.py:1067
  47.8 28.3 %collective-permute-start.1 = (bf16[4,1,2,48,384]{4,3,0,2,1:T(8,128)(2,1)S(1)}, bf16[4,1,2,48,384]{4,3,0,2,1:T(8,128)(2,1)S(1)}, u32[]{:S(2)}, u32[]{:S(2)}) collective-permute-start(bf16[4,1,2,48,384]{4,3,0,2,1:T(8,128)(2,1)S(1)} %pad_maximum_fusion.12), channel_id=1, source_target_pairs={{0,16},{8,24},{16,0},{24,8},{1,17},{9,25},{17,1},{25,9},{2,18},{10... | collective-permute-start | bytes 884744 | tf_op jit(solution)/shard_map/ppermute | solution.py:1067
  72.8 20.2 %collective-permute-start.5 = (bf16[4,1,1,48,1536]{4,3,0,2,1:T(8,128)(2,1)S(1)}, bf16[4,1,1,48,1536]{4,3,0,2,1:T(8,128)(2,1)S(1)}, u32[]{:S(2)}, u32[]{:S(2)}) collective-permute-start(bf16[4,1,1,48,1536]{4,3,0,2,1:T(8,128)(2,1)S(1)} %get-tuple-element.272), channel_id=1, source_target_pairs={{0,16},{8,24},{16,0},{24,8},{1,17},{9,25},{17,1},{25,9},{2,18},{10... | collective-permute-start | bytes 1769480 | tf_op jit(solution)/shard_map/ppermute | solution.py:1067
  74.4 18.6 %collective-permute-start.4 = (bf16[4,1,1,48,1536]{4,3,0,2,1:T(8,128)(2,1)S(1)}, bf16[4,1,1,48,1536]{4,3,0,2,1:T(8,128)(2,1)S(1)}, u32[]{:S(2)}, u32[]{:S(2)}) collective-permute-start(bf16[4,1,1,48,1536]{4,3,0,2,1:T(8,128)(2,1)S(1)} %get-tuple-element.273), channel_id=1, source_target_pairs={{0,8},{8,0},{16,24},{24,16},{1,9},{9,1},{17,25},{25,17},{2,10},{10... | collective-permute-start | bytes 1769480 | tf_op jit(solution)/shard_map/ppermute | solution.py:1067
  76.9 16.1 %copy-start.46 = (f32[1536]{0:T(1024)}, f32[1536]{0:T(1024)S(1)}, u32[]{:S(2)}) copy-start(f32[1536]{0:T(1024)S(1)} %get-tuple-element.265) | copy-start | bytes 18436
  110.3 120.5 %reduce-scatter.3.cloned.1.call-start = ((), (), s32[]{:S(2)}) async-start(), calls=%async_computation.4 | async-start | bytes 3833856 | tf_op jit(solution)/shard_map/reduce_scatter | solution.py:1503
  110.4 28.5 %collective-permute-start.6 = (bf16[4,1,2,48,1536]{4,3,0,2,1:T(8,128)(2,1)}, bf16[4,1,2,48,1536]{4,3,0,2,1:T(8,128)(2,1)}, u32[]{:S(2)}, u32[]{:S(2)}) collective-permute-start(bf16[4,1,2,48,1536]{4,3,0,2,1:T(8,128)(2,1)} %pad_maximum_fusion.3), channel_id=1, source_target_pairs={{0,16},{8,24},{16,0},{24,8},{1,17},{9,25},{17,1},{25,9},{2,18},{10... | collective-permute-start | bytes 3538952 | tf_op jit(solution)/shard_map/ppermute | solution.py:1067
  111.9 27.0 %copy-start.27 = (bf16[4,1,1,48,1536]{4,3,0,2,1:T(8,128)(2,1)S(1)}, bf16[4,1,1,48,1536]{4,3,0,2,1:T(8,128)(2,1)}, u32[]{:S(2)}) copy-start(bf16[4,1,1,48,1536]{4,3,0,2,1:T(8,128)(2,1)} %copy-done.26) | copy-start | bytes 1769476
  111.9 27.0 %copy-start.29 = (bf16[4,1,1,48,1536]{4,3,0,2,1:T(8,128)(2,1)S(1)}, bf16[4,1,1,48,1536]{4,3,0,2,1:T(8,128)(2,1)}, u32[]{:S(2)}) copy-start(bf16[4,1,1,48,1536]{4,3,0,2,1:T(8,128)(2,1)} %copy-done.28) | copy-start | bytes 1769476
  111.9 30.3 %collective-permute-start.7 = (bf16[4,2,1,48,1536]{4,3,0,2,1:T(8,128)(2,1)}, bf16[4,2,1,48,1536]{4,3,0,2,1:T(8,128)(2,1)S(1)}, u32[]{:S(2)}, u32[]{:S(2)}) collective-permute-start(bf16[4,2,1,48,1536]{4,3,0,2,1:T(8,128)(2,1)} %pad_maximum_fusion.4), channel_id=1, source_target_pairs={{0,8},{8,0},{16,24},{24,16},{1,9},{9,1},{17,25},{25,17},{2,10},{10... | collective-permute-start | bytes 3538952 | tf_op jit(solution)/shard_map/ppermute | solution.py:1067
  189.2 111.2 %all-gather.9.cloned.1.call-start = ((), (), s32[]{:S(2)}) async-start(), calls=%async_computation.5 | async-start | bytes 3538944 | tf_op jit(solution)/shard_map/all_gather | solution.py:1523
  203.0 53.7 %collective-permute-start.11 = (bf16[2304,512]{1,0:T(8,128)(2,1)}, bf16[2304,512]{1,0:T(8,128)(2,1)}, u32[]{:S(2)}, u32[]{:S(2)}) collective-permute-start(bf16[2304,512]{1,0:T(8,128)(2,1)} %get-tuple-element.134), channel_id=1, source_target_pairs={{0,8},{8,0},{16,24},{24,16},{1,9},{9,1},{17,25},{25,17},{2,10},{10... | collective-permute-start | bytes 7077896 | tf_op jit(solution)/shard_map/ppermute | solution.py:1067
  204.5 53.4 %collective-permute-start.12 = (bf16[2304,512]{1,0:T(8,128)(2,1)}, bf16[2304,512]{1,0:T(8,128)(2,1)}, u32[]{:S(2)}, u32[]{:S(2)}) collective-permute-start(bf16[2304,512]{1,0:T(8,128)(2,1)} %get-tuple-element.135), channel_id=1, source_target_pairs={{0,16},{8,24},{16,0},{24,8},{1,17},{9,25},{17,1},{25,9},{2,18},{10... | collective-permute-start | bytes 7077896 | tf_op jit(solution)/shard_map/ppermute | solution.py:1067
  239.5 8.6 %collective-permute-start.10 = (bf16[2,128,192]{2,1,0:T(8,128)(2,1)}, bf16[2,128,192]{2,1,0:T(8,128)(2,1)}, u32[]{:S(2)}, u32[]{:S(2)}) collective-permute-start(bf16[2,128,192]{2,1,0:T(8,128)(2,1)} %get-tuple-element.297), channel_id=1, source_target_pairs={{0,2},{1,3},{2,4},{3,5},{4,6},{5,7},{6,0},{7,1},{8,10},{9,11},{10,... | collective-permute-start | bytes 294920 | tf_op jit(solution)/shard_map/ppermute | solution.py:1416
  239.5 12.2 %collective-permute-start.9 = (bf16[2,128,192]{2,1,0:T(8,128)(2,1)}, bf16[2,128,192]{2,1,0:T(8,128)(2,1)}, u32[]{:S(2)}, u32[]{:S(2)}) collective-permute-start(bf16[2,128,192]{2,1,0:T(8,128)(2,1)} %get-tuple-element.298), channel_id=1, source_target_pairs={{0,4},{1,5},{2,6},{3,7},{4,0},{5,1},{6,2},{7,3},{8,12},{9,13},{10,... | collective-permute-start | bytes 294920 | tf_op jit(solution)/shard_map/ppermute | solution.py:1416
  240.5 11.2 %collective-permute-start.8 = (bf16[2,128,192]{2,1,0:T(8,128)(2,1)S(1)}, bf16[2,128,192]{2,1,0:T(8,128)(2,1)}, u32[]{:S(2)}, u32[]{:S(2)}) collective-permute-start(bf16[2,128,192]{2,1,0:T(8,128)(2,1)S(1)} %get-tuple-element.299), channel_id=1, source_target_pairs={{0,6},{1,7},{2,0},{3,1},{4,2},{5,3},{6,4},{7,5},{8,14},{9,15},{10,... | collective-permute-start | bytes 294920 | tf_op jit(solution)/shard_map/ppermute | solution.py:1416
  244.0 159.8 %reduce-scatter.5.cloned.1.call-start = ((), (), s32[]{:S(2)}) async-start(), calls=%async_computation.6 | async-start | bytes 7077888 | tf_op jit(solution)/shard_map/reduce_scatter | solution.py:1578
  263.5 27.3 %collective-permute-start.14 = (bf16[1152,512]{1,0:T(8,128)(2,1)}, bf16[1152,512]{1,0:T(8,128)(2,1)}, u32[]{:S(2)}, u32[]{:S(2)}) collective-permute-start(bf16[1152,512]{1,0:T(8,128)(2,1)} %get-tuple-element.146), channel_id=1, source_target_pairs={{0,16},{8,24},{16,0},{24,8},{1,17},{9,25},{17,1},{25,9},{2,18},{10... | collective-permute-start | bytes 3538952 | tf_op jit(solution)/shard_map/ppermute | solution.py:1067
  265.0 27.0 %collective-permute-start.15 = (bf16[1152,512]{1,0:T(8,128)(2,1)}, bf16[1152,512]{1,0:T(8,128)(2,1)}, u32[]{:S(2)}, u32[]{:S(2)}) collective-permute-start(bf16[1152,512]{1,0:T(8,128)(2,1)} %get-tuple-element.147), channel_id=1, source_target_pairs={{0,8},{8,0},{16,24},{24,16},{1,9},{9,1},{17,25},{25,17},{2,10},{10... | collective-permute-start | bytes 3538952 | tf_op jit(solution)/shard_map/ppermute | solution.py:1067
  267.3 1.7 collective-permute-start.13
  298.2 26.0 %collective-permute-start.17 = (bf16[1152,512]{1,0:T(8,128)(2,1)}, bf16[1152,512]{1,0:T(8,128)(2,1)S(1)}, u32[]{:S(2)}, u32[]{:S(2)}) collective-permute-start(bf16[1152,512]{1,0:T(8,128)(2,1)} %get-tuple-element.220.refs_0_), channel_id=1, source_target_pairs={{0,16},{8,24},{16,0},{24,8},{1,17},{9,25},{17,1},{25,9},{2,18},{10... | collective-permute-start | bytes 3538952 | tf_op jit(solution)/shard_map/ppermute | solution.py:1067
  298.7 29.1 %collective-permute-start.18 = (bf16[1152,512]{1,0:T(8,128)(2,1)}, bf16[1152,512]{1,0:T(8,128)(2,1)S(1)}, u32[]{:S(2)}, u32[]{:S(2)}) collective-permute-start(bf16[1152,512]{1,0:T(8,128)(2,1)} %get-tuple-element.224.refs_0_.refs_4_), channel_id=1, source_target_pairs={{0,8},{8,0},{16,24},{24,16},{1,9},{9,1},{17,25},{25,17},{2,10},{10... | collective-permute-start | bytes 3538952 | tf_op jit(solution)/shard_map/ppermute | solution.py:1067
  315.1 22.2 %collective-permute-start.16 = (bf16[2,1,48,2304]{3,2,1,0:T(8,128)(2,1)}, bf16[2,1,48,2304]{3,2,1,0:T(8,128)(2,1)S(1)}, u32[]{:S(2)}, u32[]{:S(2)}) collective-permute-start(bf16[2,1,48,2304]{3,2,1,0:T(8,128)(2,1)} %bitcast.156), channel_id=1, source_target_pairs={{0,8},{8,0},{16,24},{24,16},{1,9},{9,1},{17,25},{25,17},{2,10},{10... | collective-permute-start | bytes 1327112 | tf_op jit(solution)/shard_map/ppermute | solution.py:1067
  327.8 13.1 %collective-permute-start.20 = (bf16[1,2,48,2304]{3,2,1,0:T(8,128)(2,1)S(1)}, bf16[1,2,48,2304]{3,2,1,0:T(8,128)(2,1)S(1)}, u32[]{:S(2)}, u32[]{:S(2)}) collective-permute-start(bf16[1,2,48,2304]{3,2,1,0:T(8,128)(2,1)S(1)} %bitcast.155), channel_id=1, source_target_pairs={{0,16},{8,24},{16,0},{24,8},{1,17},{9,25},{17,1},{25,9},{2,18},{10... | collective-permute-start | bytes 1327112 | tf_op jit(solution)/shard_map/ppermute | solution.py:1067
  329.3 30.5 %collective-permute-start.22 = (bf16[576,512]{1,0:T(8,128)(2,1)}, bf16[576,512]{1,0:T(8,128)(2,1)}, u32[]{:S(2)}, u32[]{:S(2)}) collective-permute-start(bf16[576,512]{1,0:T(8,128)(2,1)} %get-tuple-element.281), channel_id=1, source_target_pairs={{0,8},{8,0},{16,24},{24,16},{1,9},{9,1},{17,25},{25,17},{2,10},{10... | collective-permute-start | bytes 1769480 | tf_op jit(solution)/shard_map/ppermute | solution.py:1067
  331.5 28.3 %collective-permute-start.23 = (bf16[576,512]{1,0:T(8,128)(2,1)}, bf16[576,512]{1,0:T(8,128)(2,1)}, u32[]{:S(2)}, u32[]{:S(2)}) collective-permute-start(bf16[576,512]{1,0:T(8,128)(2,1)} %get-tuple-element.277), channel_id=1, source_target_pairs={{0,16},{8,24},{16,0},{24,8},{1,17},{9,25},{17,1},{25,9},{2,18},{10... | collective-permute-start | bytes 1769480 | tf_op jit(solution)/shard_map/ppermute | solution.py:1067
  337.4 17.8 %collective-permute-start.19 = (bf16[1,1,48,2304]{3,2,1,0:T(8,128)(2,1)S(1)}, bf16[1,1,48,2304]{3,2,1,0:T(8,128)(2,1)S(1)}, u32[]{:S(2)}, u32[]{:S(2)}) collective-permute-start(bf16[1,1,48,2304]{3,2,1,0:T(8,128)(2,1)S(1)} %dynamic-slice_convert_fusion.1), channel_id=1, source_target_pairs={{0,16},{8,24},{16,0},{24,8},{1,17},{9,25},{17,1},{25,9},{2,18},{10... | collective-permute-start | bytes 663560 | tf_op jit(solution)/shard_map/ppermute | solution.py:1067
  341.1 15.1 %collective-permute-start.21 = (bf16[1,1,48,2304]{3,2,1,0:T(8,128)(2,1)S(1)}, bf16[1,1,48,2304]{3,2,1,0:T(8,128)(2,1)S(1)}, u32[]{:S(2)}, u32[]{:S(2)}) collective-permute-start(bf16[1,1,48,2304]{3,2,1,0:T(8,128)(2,1)S(1)} %dynamic-slice_convert_fusion), channel_id=1, source_target_pairs={{0,8},{8,0},{16,24},{24,16},{1,9},{9,1},{17,25},{25,17},{2,10},{10... | collective-permute-start | bytes 663560 | tf_op jit(solution)/shard_map/ppermute | solution.py:1067
  341.7 22.8 %collective-permute-start.27 = (bf16[576,512]{1,0:T(8,128)(2,1)}, bf16[576,512]{1,0:T(8,128)(2,1)}, u32[]{:S(2)}, u32[]{:S(2)}) collective-permute-start(bf16[576,512]{1,0:T(8,128)(2,1)} %get-tuple-element.190), channel_id=1, source_target_pairs={{0,8},{8,0},{16,24},{24,16},{1,9},{9,1},{17,25},{25,17},{2,10},{10... | collective-permute-start | bytes 1769480 | tf_op jit(solution)/shard_map/ppermute | solution.py:1067
  355.2 11.5 %collective-permute-start.28 = (bf16[576,512]{1,0:T(8,128)(2,1)}, bf16[576,512]{1,0:T(8,128)(2,1)}, u32[]{:S(2)}, u32[]{:S(2)}) collective-permute-start(bf16[576,512]{1,0:T(8,128)(2,1)} %get-tuple-element.191), channel_id=1, source_target_pairs={{0,16},{8,24},{16,0},{24,8},{1,17},{9,25},{17,1},{25,9},{2,18},{10... | collective-permute-start | bytes 1769480 | tf_op jit(solution)/shard_map/ppermute | solution.py:1067
  356.9 17.9 %copy-start.20 = (bf16[1,128,1536]{2,1,0:T(8,128)(2,1)S(1)}, bf16[1,128,1536]{2,1,0:T(8,128)(2,1)}, u32[]{:S(2)}) copy-start(bf16[1,128,1536]{2,1,0:T(8,128)(2,1)} %param.15) | copy-start | bytes 1179652
  359.8 7.5 %collective-permute-start.24 = (bf16[2,48,384]{2,1,0:T(8,128)(2,1)}, bf16[2,48,384]{2,1,0:T(8,128)(2,1)S(1)}, u32[]{:S(2)}, u32[]{:S(2)}) collective-permute-start(bf16[2,48,384]{2,1,0:T(8,128)(2,1)} %get-tuple-element.185), channel_id=1, source_target_pairs={{0,6},{1,7},{2,0},{3,1},{4,2},{5,3},{6,4},{7,5},{8,14},{9,15},{10,... | collective-permute-start | bytes 221192 | tf_op jit(solution)/shard_map/ppermute | solution.py:1416
  361.2 9.3 %collective-permute-start.25 = (bf16[2,48,384]{2,1,0:T(8,128)(2,1)}, bf16[2,48,384]{2,1,0:T(8,128)(2,1)S(1)}, u32[]{:S(2)}, u32[]{:S(2)}) collective-permute-start(bf16[2,48,384]{2,1,0:T(8,128)(2,1)} %get-tuple-element.186), channel_id=1, source_target_pairs={{0,4},{1,5},{2,6},{3,7},{4,0},{5,1},{6,2},{7,3},{8,12},{9,13},{10,... | collective-permute-start | bytes 221192 | tf_op jit(solution)/shard_map/ppermute | solution.py:1416
  361.9 9.8 %collective-permute-start.26 = (bf16[2,48,384]{2,1,0:T(8,128)(2,1)}, bf16[2,48,384]{2,1,0:T(8,128)(2,1)S(1)}, u32[]{:S(2)}, u32[]{:S(2)}) collective-permute-start(bf16[2,48,384]{2,1,0:T(8,128)(2,1)} %get-tuple-element.187), channel_id=1, source_target_pairs={{0,2},{1,3},{2,4},{3,5},{4,6},{5,7},{6,0},{7,1},{8,10},{9,11},{10,... | collective-permute-start | bytes 221192 | tf_op jit(solution)/shard_map/ppermute | solution.py:1416
  366.7 20.4 %collective-permute-start.31 = (bf16[576,512]{1,0:T(8,128)(2,1)S(1)}, bf16[576,512]{1,0:T(8,128)(2,1)S(1)}, u32[]{:S(2)}, u32[]{:S(2)}) collective-permute-start(bf16[576,512]{1,0:T(8,128)(2,1)S(1)} %copy-done.42), channel_id=1, source_target_pairs={{0,8},{8,0},{16,24},{24,16},{1,9},{9,1},{17,25},{25,17},{2,10},{10... | collective-permute-start | bytes 1769480 | tf_op jit(solution)/shard_map/ppermute | solution.py:1067
  366.7 20.4 %collective-permute-start.32 = (bf16[576,512]{1,0:T(8,128)(2,1)S(1)}, bf16[576,512]{1,0:T(8,128)(2,1)S(1)}, u32[]{:S(2)}, u32[]{:S(2)}) collective-permute-start(bf16[576,512]{1,0:T(8,128)(2,1)S(1)} %copy-done.43), channel_id=1, source_target_pairs={{0,16},{8,24},{16,0},{24,8},{1,17},{9,25},{17,1},{25,9},{2,18},{10... | collective-permute-start | bytes 1769480 | tf_op jit(solution)/shard_map/ppermute | solution.py:1067
  374.7 1.6 collective-permute-start.29
  379.5 7.7 %collective-permute-start.30 = (bf16[1,1,48,2304]{3,2,1,0:T(8,128)(2,1)}, bf16[1,1,48,2304]{3,2,1,0:T(8,128)(2,1)S(1)}, u32[]{:S(2)}, u32[]{:S(2)}) collective-permute-start(bf16[1,1,48,2304]{3,2,1,0:T(8,128)(2,1)} %bitcast.151), channel_id=1, source_target_pairs={{0,16},{8,24},{16,0},{24,8},{1,17},{9,25},{17,1},{25,9},{2,18},{10... | collective-permute-start | bytes 663560 | tf_op jit(solution)/shard_map/ppermute | solution.py:1067
  380.5 9.3 %collective-permute-start.34 = (bf16[1,1,48,2304]{3,2,1,0:T(8,128)(2,1)}, bf16[1,1,48,2304]{3,2,1,0:T(8,128)(2,1)S(1)}, u32[]{:S(2)}, u32[]{:S(2)}) collective-permute-start(bf16[1,1,48,2304]{3,2,1,0:T(8,128)(2,1)} %bitcast.150), channel_id=1, source_target_pairs={{0,8},{8,0},{16,24},{24,16},{1,9},{9,1},{17,25},{25,17},{2,10},{10... | collective-permute-start | bytes 663560 | tf_op jit(solution)/shard_map/ppermute | solution.py:1067
  389.2 19.1 %collective-permute-start.33 = (bf16[2,1,48,2304]{3,2,1,0:T(8,128)(2,1)}, bf16[2,1,48,2304]{3,2,1,0:T(8,128)(2,1)}, u32[]{:S(2)}, u32[]{:S(2)}) collective-permute-start(bf16[2,1,48,2304]{3,2,1,0:T(8,128)(2,1)} %pad_maximum_fusion.10), channel_id=1, source_target_pairs={{0,8},{8,0},{16,24},{24,16},{1,9},{9,1},{17,25},{25,17},{2,10},{10... | collective-permute-start | bytes 1327112 | tf_op jit(solution)/shard_map/ppermute | solution.py:1067
  390.8 18.9 %collective-permute-start.35 = (bf16[1,2,48,2304]{3,2,1,0:T(8,128)(2,1)}, bf16[1,2,48,2304]{3,2,1,0:T(8,128)(2,1)}, u32[]{:S(2)}, u32[]{:S(2)}) collective-permute-start(bf16[1,2,48,2304]{3,2,1,0:T(8,128)(2,1)} %pad_maximum_fusion.11), channel_id=1, source_target_pairs={{0,16},{8,24},{16,0},{24,8},{1,17},{9,25},{17,1},{25,9},{2,18},{10... | collective-permute-start | bytes 1327112 | tf_op jit(solution)/shard_map/ppermute | solution.py:1067
  391.8 22.4 %collective-permute-start.36 = (bf16[576,512]{1,0:T(8,128)(2,1)}, bf16[576,512]{1,0:T(8,128)(2,1)}, u32[]{:S(2)}, u32[]{:S(2)}) collective-permute-start(bf16[576,512]{1,0:T(8,128)(2,1)} %get-tuple-element.218), channel_id=1, source_target_pairs={{0,8},{8,0},{16,24},{24,16},{1,9},{9,1},{17,25},{25,17},{2,10},{10... | collective-permute-start | bytes 1769480 | tf_op jit(solution)/shard_map/ppermute | solution.py:1067
  393.3 21.8 %collective-permute-start.37 = (bf16[576,512]{1,0:T(8,128)(2,1)}, bf16[576,512]{1,0:T(8,128)(2,1)}, u32[]{:S(2)}, u32[]{:S(2)}) collective-permute-start(bf16[576,512]{1,0:T(8,128)(2,1)} %get-tuple-element.219), channel_id=1, source_target_pairs={{0,16},{8,24},{16,0},{24,8},{1,17},{9,25},{17,1},{25,9},{2,18},{10... | collective-permute-start | bytes 1769480 | tf_op jit(solution)/shard_map/ppermute | solution.py:1067
  (54 other events, 193.3 us)
Sparse Core Ops, SparseCore 0:
  11.5 59.9 all-gather.10
  73.1 37.1 all-gather.6
  112.5 37.1 all-gather.12
  189.3 41.5 reduce-scatter.2
  244.1 37.8 all-gather.8
  315.2 73.3 reduce-scatter.4

commit v11 on v10

--- a/solution.py
+++ b/solution.py
@@ -576,78 +576,113 @@
 
 
 def product_kernel(
+    e,
+    left_any,
+    gate_any,
+    up_any,
+    scaled_one_any,
+    scaled_two_any,
+    live_any,
+    out_one_any,
+    out_two_any,
     left_ref,
-    gate_ref,
-    up_ref,
-    scaled_one_ref,
-    scaled_two_ref,
-    live_one_ref,
-    live_two_ref,
-    out_one_ref,
-    out_two_ref,
+    right_ref,
+    scaled_ref,
+    live_ref,
+    out_ref,
+    came,
+    gone,
 ):
-    step = pl.program_id(0)
-    tile, hidden = left_ref.shape[1], gate_ref.shape[1]
-    narrow = live_one_ref.shape[1]
-    tops = pl.num_programs(0) - 3
-    top = tops * tile
-
-    @pl.when(step < tops)
-    def _():
-        here = pl.ds(pl.multiple_of(step * tile, tile), tile)
-        both = dot(left_ref[...], jnp.concatenate([gate_ref[...], up_ref[...]], 1), ROWS)
-        out_one_ref[here, :] = both[:, :hidden].astype(out_one_ref.dtype)
-        out_two_ref[here, :] = both[:, hidden:].astype(out_two_ref.dtype)
-
-    @pl.when(step >= tops)
-    def _():
-        part = step - tops
-        for scaled_ref, live_ref, out_ref in (
-            (scaled_one_ref, live_one_ref, out_one_ref),
-            (scaled_two_ref, live_two_ref, out_two_ref),
-        ):
-            product = dot(scaled_ref[...], live_ref[...], ROWS).astype(out_ref.dtype)
-
-            @pl.when(part < 2)
-            def _():
-                there = pl.ds(pl.multiple_of(part * narrow, narrow), narrow)
-                out_ref[top : top + hidden, there] = product
-
-            @pl.when(part == 2)
-            def _():
-                out_ref[top + hidden :, :narrow] = product[:narrow]
-                out_ref[top + hidden :, narrow:] = product[narrow:]
+    tiles, _, tile = left_ref.shape
+    hidden = scaled_ref.shape[2]
+    half = live_ref.shape[2]
+    narrow = half - hidden
+    top = tiles * tile
+    copy = pltpu.make_async_copy
+    rights = [
+        copy(source.at[e], right_ref.at[:, n * hidden : (n + 1) * hidden], came.at[n])
+        for n, source in enumerate((gate_any, up_any))
+    ]
+    lefts = [
+        copy(left_any.at[:, i * tile : (i + 1) * tile], left_ref.at[i], came.at[2 + i])
+        for i in range(tiles)
+    ]
+
+    def result(n, rows, place):
+        target = (out_one_any, out_two_any)[n]
+        return copy(out_ref.at[n, rows, :], target.at[rows, :], gone.at[place])
+
+    def tile_rows(i):
+        return pl.ds(pl.multiple_of(i * tile, tile), tile)
+
+    downs = []
+    for n, source in enumerate((scaled_one_any, scaled_two_any)):
+        place = 2 + tiles + 2 * n
+        downs.append(copy(source.at[e], scaled_ref.at[n], came.at[place]))
+        downs.append(
+            copy(
+                live_any.at[:, n * half : (n + 1) * half], live_ref.at[n], came.at[place + 1]
+            )
+        )
+    for each in rights + lefts + downs:
+        each.start()
+    for each in rights:
+        each.wait()
+
+    @pl.loop(0, tiles)
+    def _(i):
+        copy(left_any.at[:, tile_rows(i)], left_ref.at[i], came.at[2 + i]).wait()
+        both = dot(left_ref[i], right_ref[...], ROWS).astype(out_ref.dtype)
+        for n in range(2):
+            out_ref[n, tile_rows(i), :] = both[:, n * hidden : (n + 1) * hidden]
+            result(n, tile_rows(i), 2 * i + n).start()
+
+    rest = slice(top, top + half)
+    for n in range(2):
+        downs[2 * n].wait()
+        downs[2 * n + 1].wait()
+        product = dot(scaled_ref[n], live_ref[n], ROWS).astype(out_ref.dtype)
+        out_ref[n, top : top + hidden, :] = product[:, :hidden]
+        out_ref[n, top + hidden : top + half, :narrow] = product[:narrow, hidden:]
+        out_ref[n, top + hidden : top + half, narrow:] = product[narrow:, hidden:]
+        result(n, rest, 2 * tiles + n).start()
+
+    @pl.loop(0, tiles)
+    def _(i):
+        for n in range(2):
+            result(n, tile_rows(i), 2 * i + n).wait()
+
+    for n in range(2):
+        result(n, rest, 2 * tiles + n).wait()
 
 
 def expert_products(left, gate, up, scaled_one, scaled_two, live, e, dtype):
     tokens, features = left.shape
     hidden = gate.shape[2]
-    narrow = hidden // 2
+    half = features // 2
     tile = 512
-    tops = features // tile
-    rows = features + features // 2
-    stack = pl.BlockSpec((None, tokens, hidden), lambda i: (e, 0, 0), pipeline_mode=pl.Buffered(1))
-    lives = [
-        pl.BlockSpec((tokens, narrow), lambda i, side=side: (0, 3 * side + jnp.maximum(i - tops, 0)))
-        for side in range(2)
-    ]
-    out = pl.BlockSpec((rows, hidden), lambda i: (0, 0), pipeline_mode=pl.Buffered(1))
+    tiles = features // tile
+    rows = features + half
+    low = jnp.bfloat16
+    anywhere = pl.BlockSpec(memory_space=pl.ANY)
     return pl.pallas_call(
-        product_kernel,
+        lambda *refs: product_kernel(e, *refs),
+        name="expert_products",
         out_shape=(jax.ShapeDtypeStruct((rows, hidden), dtype),) * 2,
-        grid=(tops + 3,),
-        in_specs=[
-            pl.BlockSpec((tokens, tile), lambda i: (0, jnp.minimum(i, tops - 1))),
-            stack,
-            stack,
-            stack,
-            stack,
-            *lives,
+        in_specs=[anywhere] * 6,
+        out_specs=[anywhere] * 2,
+        scratch_shapes=[
+            pltpu.VMEM((tiles, tokens, tile), low),
+            pltpu.VMEM((tokens, 2 * hidden), low),
+            pltpu.VMEM((2, tokens, hidden), low),
+            pltpu.VMEM((2, tokens, half), low),
+            pltpu.VMEM((2, rows, hidden), dtype),
+            pltpu.SemaphoreType.DMA((6 + tiles,)),
+            pltpu.SemaphoreType.DMA((2 * tiles + 2,)),
         ],
-        out_specs=[out, out],
         compiler_params=pltpu.CompilerParams(vmem_limit_bytes=58 << 20),
         cost_estimate=pl.CostEstimate(flops=0, bytes_accessed=tokens, transcendentals=0),
-    )(left, gate, up, scaled_one, scaled_two, live, live)
+    )(left, gate, up, scaled_one, scaled_two, live)
 
 
 def output_kernel(place_ref, scaled_ref, down_weight_ref, out_ref):
@@ -973,88 +1008,132 @@
             jax.ShapeDtypeStruct((8, rows), jnp.float32),
             shaped(experts),
         ),
-        compiler_params=pltpu.CompilerParams(vmem_limit_bytes=40 << 20),
+        compiler_params=pltpu.CompilerParams(vmem_limit_bytes=58 << 20),
         cost_estimate=pl.CostEstimate(flops=0, bytes_accessed=rows, transcendentals=0),
     )(low, high)
 
 
-def upper_rows(flags_ref, side, own_ref, came_ref, rows):
-    return jnp.where(flags_ref[2 + side] > 0, own_ref[rows, :], came_ref[rows, :])
-
-
-def into_kernel(flags_ref, side, own_ref, came_ref, first_ref, second_ref, third_ref, out_ref):
-    rows = own_ref.shape[0]
-    rest = out_ref.shape[0] - rows
-    half = first_ref.shape[0]
-    kept = pl.program_id(0) == flags_ref[side]
-
-    @pl.when(kept)
-    def _():
-        low = jnp.where(flags_ref[2 + side] > 0, came_ref[...], own_ref[...])
-        out_ref[:rows, :] = low.astype(jnp.float32)
-        high = upper_rows(flags_ref, side, own_ref, came_ref, slice(0, rest))
-        out_ref[rows:, :] = high.astype(jnp.float32)
-
-    @pl.when(jnp.logical_not(kept))
-    def _():
-        out_ref[:half, :] = first_ref[...].astype(jnp.float32)
-        out_ref[half:rows, :] = second_ref[...].astype(jnp.float32)
-        out_ref[rows:, :] = third_ref[:rest, :].astype(jnp.float32)
-
-
-def into_output(flags, side, own, came, first, second, third):
-    rows, hidden = own.shape
-    total = 2 * rows * 2 // 3
-    whole = lambda array: pl.BlockSpec(array.shape, lambda e, k: (0, 0))
+def fold_down(out_ref, value):
+    hidden = out_ref.shape[0]
+    narrow = hidden // 2
+    out_ref[:, :hidden] = value[:hidden]
+    out_ref[:narrow, hidden:] = value[hidden:, :narrow]
+    out_ref[narrow:, hidden:] = value[hidden:, narrow:]
+
+
+def own_kernel(flags_ref, *refs):
+    down_ref = refs[6]
+    for side in range(2):
+
+        @pl.when(pl.program_id(0) == side)
+        def _():
+            own, came = refs[2 * side][...], refs[2 * side + 1][...]
+            out_ref = refs[4 + side]
+            rows = own.shape[0]
+            rest = out_ref.shape[0] - rows
+            late = flags_ref[2 + side] > 0
+            high = jnp.where(late, own, came).astype(jnp.float32)
+            out_ref[:rows, :] = jnp.where(late, came, own).astype(jnp.float32)
+            out_ref[rows:, :] = high[:rest]
+            fold_down(down_ref, high[rest:])
+
+
+def own_outputs(flags, chains):
+    rows, hidden = chains[0].own.shape
+    features = 2 * rows * 2 // 3
+    operands = []
+    for chain in chains:
+        operands += [chain.own, chain.came]
+    into = lambda side: pl.BlockSpec((None, features, hidden), lambda s, k: (k[side], 0, 0))
+    shaped = lambda *shape: jax.ShapeDtypeStruct((2,) + shape, jnp.float32)
     return pl.pallas_call(
-        lambda k, *refs: into_kernel(k, side, *refs),
-        name="into_output",
-        out_shape=jax.ShapeDtypeStruct((2, total, hidden), jnp.float32),
+        own_kernel,
+        name="own_outputs",
+        out_shape=(
+            shaped(features, hidden),
+            shaped(features, hidden),
+            shaped(hidden, features),
+        ),
         grid_spec=pltpu.PrefetchScalarGridSpec(
             num_scalar_prefetch=1,
             grid=(2,),
-            in_specs=[whole(own), whole(came), whole(first), whole(second), whole(third)],
-            out_specs=pl.BlockSpec((None, total, hidden), lambda e, k: (e, 0, 0)),
-        ),
-        compiler_params=pltpu.CompilerParams(vmem_limit_bytes=40 << 20),
+            in_specs=[whole_block(rows, hidden)] * 4,
+            out_specs=[
+                into(0),
+                into(1),
+                pl.BlockSpec((None, hidden, features // 2), lambda s, k: (k[s], 0, s)),
+            ],
+        ),
+        compiler_params=pltpu.CompilerParams(vmem_limit_bytes=58 << 20),
         cost_estimate=pl.CostEstimate(flops=0, bytes_accessed=rows, transcendentals=0),
-    )(flags, own, came, first, second, third)
-
-
-def down_kernel(flags_ref, *refs):
-    out_ref = refs[8]
-    hidden = out_ref.shape[0]
-    narrow = hidden // 2
+    )(flags, *operands)
+
+
+def into_kernel(flags_ref, gate_any, up_any, *refs):
     for side in range(2):
-        own_ref, came_ref, third_ref, last_ref = refs[4 * side : 4 * side + 4]
-        rows = own_ref.shape[0]
-        rest = rows - out_ref.shape[1] // 2
-        mine = upper_rows(flags_ref, side, own_ref, came_ref, slice(rest, rows))
-        theirs = jnp.concatenate([third_ref[rest:, :], last_ref[...]], 0)
-        kept = pl.program_id(0) == flags_ref[side]
-        value = jnp.where(kept, mine, theirs).astype(jnp.float32)
-        start = side * value.shape[0]
-        out_ref[:, start : start + hidden] = value[:hidden]
-        middle, end = start + hidden, start + value.shape[0]
-        out_ref[:narrow, middle:end] = value[hidden:, :narrow]
-        out_ref[narrow:, middle:end] = value[hidden:, narrow:]
-
-
-def down_output(flags, *operands):
-    rows, hidden = operands[0].shape
-    whole = lambda array: pl.BlockSpec(array.shape, lambda e, k: (0, 0))
+
+        @pl.when(pl.program_id(0) == side)
+        def _():
+            first_ref, second_ref, third_ref = refs[3 * side : 3 * side + 3]
+            out_ref = refs[6 + side]
+            half = first_ref.shape[0]
+            rest = out_ref.shape[0] - 2 * half
+            out_ref[:half, :] = first_ref[...].astype(jnp.float32)
+            out_ref[half : 2 * half, :] = second_ref[...].astype(jnp.float32)
+            out_ref[2 * half :, :] = third_ref[:rest, :].astype(jnp.float32)
+
+
+def into_outputs(flags, gate, up, pieces):
+    _, features, hidden = gate.shape
+    into = lambda side: pl.BlockSpec((None, features, hidden), lambda s, k: (1 - k[side], 0, 0))
+    anywhere = pl.BlockSpec(memory_space=pl.ANY)
     return pl.pallas_call(
-        down_kernel,
-        out_shape=jax.ShapeDtypeStruct((2, hidden, 3 * hidden), jnp.float32),
+        into_kernel,
+        name="into_outputs",
+        out_shape=(jax.ShapeDtypeStruct(gate.shape, gate.dtype),) * 2,
         grid_spec=pltpu.PrefetchScalarGridSpec(
             num_scalar_prefetch=1,
             grid=(2,),
-            in_specs=[whole(array) for array in operands],
-            out_specs=pl.BlockSpec((None, hidden, 3 * hidden), lambda e, k: (e, 0, 0)),
-        ),
-        compiler_params=pltpu.CompilerParams(vmem_limit_bytes=40 << 20),
-        cost_estimate=pl.CostEstimate(flops=0, bytes_accessed=rows, transcendentals=0),
-    )(flags, *operands)
+            in_specs=[anywhere] * 2 + [whole_block(*piece.shape) for piece in pieces],
+            out_specs=[into(0), into(1)],
+        ),
+        input_output_aliases={1: 0, 2: 1},
+        compiler_params=pltpu.CompilerParams(vmem_limit_bytes=58 << 20),
+        cost_estimate=pl.CostEstimate(flops=0, bytes_accessed=features, transcendentals=0),
+    )(flags, gate, up, *pieces)
+
+
+def down_kernel(flags_ref, down_any, *refs):
+    for side in range(2):
+
+        @pl.when(pl.program_id(0) == side)
+        def _():
+            third_ref, last_ref = refs[2 * side : 2 * side + 2]
+            out_ref = refs[4]
+            rest = third_ref.shape[0] + last_ref.shape[0] - out_ref.shape[1]
+            value = jnp.concatenate([third_ref[rest:, :], last_ref[...]], 0)
+            fold_down(out_ref, value.astype(jnp.float32))
+
+
+def down_outputs(flags, down, pieces):
+    _, hidden, features = down.shape
+    return pl.pallas_call(
+        down_kernel,
+        name="down_outputs",
+        out_shape=jax.ShapeDtypeStruct(down.shape, down.dtype),
+        grid_spec=pltpu.PrefetchScalarGridSpec(
+            num_scalar_prefetch=1,
+            grid=(2,),
+            in_specs=[pl.BlockSpec(memory_space=pl.ANY)]
+            + [whole_block(*piece.shape) for piece in pieces],
+            out_specs=pl.BlockSpec(
+                (None, hidden, features // 2), lambda s, k: (1 - k[s], 0, s)
+            ),
+        ),
+        input_output_aliases={1: 0},
+        compiler_params=pltpu.CompilerParams(vmem_limit_bytes=58 << 20),
+        cost_estimate=pl.CostEstimate(flops=0, bytes_accessed=features, transcendentals=0),
+    )(flags, down, *pieces)
 
 
 def after(values, *others):
@@ -1590,13 +1669,19 @@
     pieces = [chain.ends(*halves) for chain in chains]
     sent = [part[0] for part in pieces]
     while cubes[0].stage < len(bits):
-        for cube in cubes:
-            cube.add(*sent)
+        flying = after([cube.flying for cube in cubes], *sent)
+        for cube, arrived in zip(cubes, flying):
+            cube.flying = arrived
+            cube.add()
         sent = [cube.halve() for cube in cubes]
     first = [chain.last(part[0]) for chain, part in zip(chains, pieces)]
     second = [chain.last(after(part[1], *sent)) for chain, part in zip(chains, pieces)]
+    flags = jnp.stack([flag(chain.order[n]) for n in range(2) for chain in chains])
+    for chain in chains:
+        chain.own, chain.came = after((chain.own, chain.came), *sent)
+    grad_gate, grad_up, grad_down = own_outputs(flags, chains)
     for cube in cubes:
-        cube.flying = after(cube.flying, *sent)
+        cube.flying = after(cube.flying, grad_gate, grad_up, grad_down)
     parcels, out_sums = pack_heads(place, cubes, size, side_width)
     parcels = after(parcels, *first)
     got = [parcels[0]] + [from_chip(parcels[k], k) for k in range(1, chips)]
@@ -1607,19 +1692,14 @@
         cube.value = value.reshape((1,) * len(bits) + value.shape)
     sent = [cube.back() for cube in cubes]
     fourth = [chain.last(after(part[3], *third)) for chain, part in zip(chains, pieces)]
-    flags = jnp.stack([flag(chain.order[n]) for n in range(2) for chain in chains])
     while cubes[0].stage > 0:
         for cube in cubes:
             cube.join(*third)
         sent = [cube.back() for cube in cubes]
-    grad_gate, grad_up = [
-        into_output(
-            flags,
-            side,
-            *after((chain.own, chain.came, first[side], second[side], third[side]), *sent),
-        )
-        for side, chain in enumerate(chains)
-    ]
+    arrived = []
+    for side in range(2):
+        arrived += [first[side], second[side], third[side]]
+    grad_gate, grad_up = into_outputs(flags, grad_gate, grad_up, after(arrived, *sent))
     output = jnp.where((segments[0] != 0)[:, None], middle_own + out_sum, 0.0)
     own_hidden = inputs[0].astype(jnp.float32)
     own_scale = lax.rsqrt(jnp.mean(own_hidden * own_hidden, -1, keepdims=True) + EPS)
@@ -1629,10 +1709,10 @@
     head_outs = head_outputs(
         *[cube.value.reshape(rows_own, -1) for cube in cubes], copies, side_width, experts_all
     )
-    operands = []
-    for side, chain in enumerate(chains):
-        operands += [chain.own, chain.came, third[side], fourth[side]]
-    grad_down = down_output(flags, *after(operands, head_outs))
+    arrived = []
+    for side in range(2):
+        arrived += [third[side], fourth[side]]
+    grad_down = down_outputs(flags, grad_down, after(arrived, head_outs))
 
     return (
         output.astype(jnp.bfloat16)[None],

time: 432 us -> 426 us (0.986)
  waiting for transfers between devices: 131 us -> 123 us
  Pallas kernels: 165 us -> 159 us
    ppermute x30, waiting for transfers between devices: 80.4 us -> 62.4 us  [swap(): return lax.ppermute(value, 'rep', [(i, i ^ bit) for i in range(size)])]
    reduce_scatter x1, waiting for transfers between devices: 0.75 us -> 10.6 us  [per_device(): lax.psum_scatter(grad_rows, 'ctx', scatter_dimension=0, tiled=True)]
    pallas_call x5, Pallas kernels: 43.1 us -> 36 us  [the longest x2 18.9 us: expert_products(): pl.pallas_call(lambda *refs: product_kernel(e, *refs), name='expert_produ...]
    unnamed x118 -> x92, local copies, waits for them, and re-layouts: 11.7 us -> 11 us
  transfers between devices with their start and end apart: 44 -> 44, of which waited for: 27 -> 24; matrix products, arithmetic and copies ran while one was open for 10% -> 11% of each run, Pallas kernels for 28% -> 27%
where the time goes in v11:
time: 426 us; the launch traced here: 424 us
  Pallas kernels  159 us (37%)
  waiting for transfers between devices  123 us (29%)
  starting transfers between devices  44.3 us (10%)
  other arithmetic  35.9 us (8%)
  blocking collectives  24.5 us (6%)
  local copies, waits for them, and re-layouts  22.5 us (5%)
  between operations  14.7 us (3%)
    ppermute x30, waiting for transfers between devices, swap(): return lax.ppermute(value, 'rep', [(i, i ^ bit) for i in range(size)])  62.4 us
    pallas_call x1, Pallas kernels, layer_rows(): pl.pallas_call(layer_kernel, out_shape=(shaped((tokens, features), low),...  39.4 us
    ppermute x30, starting transfers between devices, swap(): return lax.ppermute(value, 'rep', [(i, i ^ bit) for i in range(size)])  35.3 us
    all_to_all x1, blocking collectives, per_device(): lax.all_to_all(head_columns, 'ctx', split_axis=0, concat_axis=0, tiled=True)  24.5 us
    pallas_call x2, Pallas kernels, expert_products(): pl.pallas_call(lambda *refs: product_kernel(e, *refs), name='expert_produ...  18.9 us
    all_gather x1, waiting for transfers between devices, per_device(): gathered = lax.all_gather(rows, 'ctx', axis=0)  16.5 us
    pallas_call x1, Pallas kernels, attend(): pl.pallas_call(attend_kernel, out_shape=(shaped((tokens, features), jnp.b...  16 us
    pallas_call x1, Pallas kernels, close_rows(): pl.pallas_call(lambda *refs: close_kernel(reps, *refs), name='close', out...  14.6 us
  transfers between devices with their start and end apart: 44, of which 24 were waited for; matrix products, arithmetic and copies ran while one was open for 11% of the time, Pallas kernels for 27%

profile of v11, /device:TPU:0, one launch (start us, length us, event | category | flops | bytes accessed | tf_op | source)
XLA Modules:
  0.0 424.3 jit_solution(8547248398386676762)
XLA Ops:
  9.5 1.9 fusion.12
  15.3 24.5 %all_to_all.5 = bf16[8,48,384]{2,1,0:T(8,128)(2,1)S(1)} all-to-all(bf16[8,48,384]{2,1,0:T(8,128)(2,1)S(1)} %copy.57), channel_id=1, replica_groups=mesh['rep'=4,'ctx'=8] {'ctx'}, dimensions={0} | all-to-all | bytes 589824 | tf_op jit(solution)/shard_map/all_to_all | solution.py:1520
  42.9 2.8 collective-permute-done
  47.8 1.6 collective-permute-start.1
  49.4 5.6 %collective-permute-done.3 = bf16[4,2,1,48,384]{4,3,0,2,1:T(8,128)(2,1)S(1)} collective-permute-done((bf16[4,2,1,48,384]{4,3,0,2,1:T(8,128)(2,1)S(1)}, bf16[4,2,1,48,384]{4,3,0,2,1:T(8,128)(2,1)S(1)}, u32[]{:S(2)}, u32[]{:S(2)}) %collective-permute-start.3) | collective-permute-done | bytes 294944 | tf_op jit(solution)/shard_map/ppermute | solution.py:1146
  55.0 16.5 %all-gather.11.cloned.1.call-done = bf16[1408,1664]{1,0:T(8,128)(2,1)} async-done(((bf16[176,1664]{1,0:T(8,128)(2,1)}), bf16[1408,1664]{1,0:T(8,128)(2,1)}) %all-gather.11.cloned.1.call-update) | async-done | bytes 4685840 | tf_op jit(solution)/shard_map/all_gather | solution.py:1491
  72.8 1.6 collective-permute-start.5
  77.5 16.0 %shard_map.238 = (bf16[1024,1536]{1,0:T(8,128)(2,1)}, bf16[1024,192]{1,0:T(8,128)(2,1)S(1)}, bf16[1024,64]{1,0:T(8,128)(2,1)S(1)}, bf16[1024,64]{1,0:T(8,128)(2,...) custom-call(bf16[8,176,1664]{2,1,0:T(8,128)(2,1)} %bitcast.130, ...), custom_call_target="tpu_custom_call" | custom-call | bytes 1024 | tf_op jit(solution)/shard_map/pallas_call | solution.py:194
  93.5 2.2 broadcast_select_fusion.13
  98.6 11.7 %all-gather.7.cloned.1.call-done.cotangent_ref = bf16[1024,1536]{1,0:T(8,128)(2,1)} async-done(((bf16[128,1536]{1,0:T(8,128)(2,1)}), bf16[1024,1536]{1,0:T(8,128)(2,1)}) %all-gather.7.cloned.1.call-update) | async-done | bytes 3145744 | tf_op jit(solution)/shard_map/all_gather | solution.py:1492
  115.6 23.3 %collective-permute-done.6 = bf16[4,1,2,48,1536]{4,3,0,2,1:T(8,128)(2,1)} collective-permute-done((bf16[4,1,2,48,1536]{4,3,0,2,1:T(8,128)(2,1)}, bf16[4,1,2,48,1536]{4,3,0,2,1:T(8,128)(2,1)}, u32[]{:S(2)}, u32[]{:S(2)}) %collective-permute-start.6) | collective-permute-done | bytes 1179680 | tf_op jit(solution)/shard_map/ppermute | solution.py:1146
  140.6 1.6 copy.60
  144.2 5.5 %all-gather.13.cloned.1.call-done = bf16[4096,384]{1,0:T(8,128)(2,1)} async-done(((bf16[512,384]{1,0:T(8,128)(2,1)}), bf16[4096,384]{1,0:T(8,128)(2,1)}) %all-gather.13.cloned.1.call-update) | async-done | bytes 3145744 | tf_op jit(solution)/shard_map/all_gather | solution.py:1542
  149.7 39.4 %shard_map.239 = (bf16[1024,1536]{1,0:T(8,128)(2,1)}, bf16[2,1024,512]{2,1,0:T(8,128)(2,1)}, bf16[2,1024,512]{2,1,0:T(8,128)(2,1)}, bf16[2,1024,512]{2,1,0:T(8,1...) custom-call(s32[4]{0:T(128)} %pad_add_fusion.place_ref.refs_0_, ...), custom_call_target="tpu_custom_call" | custom-call | flops 19327352832 | bytes 40894464 | tf_op jit(solution)/shard_map/pallas_call | solution.py:513
  189.4 9.3 %expert_products.2 = (bf16[2304,512]{1,0:T(8,128)(2,1)}, bf16[2304,512]{1,0:T(8,128)(2,1)}) custom-call(bf16[1024,1536]{1,0:T(8,128)(2,1)} %get-tuple-element.137.refs_0_, bf16[2,1024,512]{2,1,0:T(8,128)(2,1)} %get-tuple-element.132.refs_1_, bf16[2,1024,512]{2,1,0:T(8,128)(2,1)} %get-tuple-element.133.refs_2_, ...), custom_call_target="tpu_custom_call" | custom-call | bytes 1024 | tf_op jit(solution)/shard_map/expert_products/pallas_call | solution.py:668
  201.8 9.6 %expert_products.3 = (f32[2304,512]{1,0:T(8,128)}, f32[2304,512]{1,0:T(8,128)}) custom-call(bf16[1024,1536]{1,0:T(8,128)(2,1)} %get-tuple-element.137.refs_0_, bf16[2,1024,512]{2,1,0:T(8,128)(2,1)} %get-tuple-element.132.refs_1_, bf16[2,1024,512]{2,1,0:T(8,128)(2,1)} %get-tuple-element.133.refs_2_, ...), custom_call_target="tpu_custom_call" | custom-call | bytes 1024 | tf_op jit(solution)/shard_map/expert_products/pallas_call | solution.py:668
  211.4 8.9 %shard_map.240.refs_9_ = bf16[1024,1536]{1,0:T(8,128)(2,1)} custom-call(s32[4]{0:T(128)S(1)} %copy-done.7, bf16[2,1024,512]{2,1,0:T(8,128)(2,1)} %get-tuple-element.141.refs_3_.scaled_ref, bf16[2,512,1536]{2,1,0:T(8,128)(2,1)} %down_weight_ref.1), custom_call_target="tpu_custom_call" | custom-call | bytes 1024 | tf_op jit(solution)/shard_map/pallas_call | solution.py:705
  220.2 10.6 %reduce-scatter.3.cloned.1.call-done.sum_ref = bf16[128,1664]{1,0:T(8,128)(2,1)} async-done(((bf16[1024,1664]{1,0:T(8,128)(2,1)}), bf16[128,1664]{1,0:T(8,128)(2,1)}) %reduce-scatter.3.cloned.1.call-update) | async-done | bytes 426000 | tf_op jit(solution)/shard_map/reduce_scatter | solution.py:1582
  230.9 6.8 %shard_map.241 = (f32[128,1536]{1,0:T(8,128)}, bf16[128,1536]{1,0:T(8,128)(2,1)}, bf16[8,128,192]{2,1,0:T(8,128)(2,1)}, bf16[128,16]{1,0:T(8,128)(2,1)}, f32[1,1536]{1,0:T(1,128)}) custom-call(s32[4]{0:T(128)} %pad_add_fusion.place_ref.refs_0_, bf16[128,1664]{1,0:T(8,128)(2,1)} %reduce-scatter.3.cloned.1.call-done.sum_ref, ...), custom_call_target="tpu_custom_call" | custom-call | bytes 128 | tf_op jit(solution)/shard_map/pallas_call | solution.py:776
  237.6 1.8 dynamic-slice_bitcast_fusion.5
  240.0 3.3 collective-permute-start.8
  244.2 3.8 collective-permute-done.10
  248.0 2.9 collective-permute-done.9
  251.0 1.9 pad_maximum_fusion.9
  253.7 5.5 %shard_map.242 = (bf16[1152,512]{1,0:T(8,128)(2,1)}, bf16[1152,512]{1,0:T(8,128)(2,1)}) custom-call(s32[2]{0:T(128)} %add_convert_fusion.keeps_ref, f32[2304,512]{1,0:T(8,128)} %get-tuple-element.139.refs_0_, bf16[2304,512]{1,0:T(8,128)(2,1)} %collective-permute-done.11.refs_1_, f32[2304,512]{1,0:T(8,128)} %get-tuple-element.140.refs_2_.refs_3_, ...), custom_call_target="tpu_custom_call" | custom-call | flops 70778880000 | bytes 14155776 | tf_op jit(solution)/shard_map/pallas_call | solution.py:1220
  261.4 1.8 select_bitcast_fusion
  263.2 1.9 collective-permute-done.13
  266.5 14.3 %shard_map.243 = (bf16[1024,192]{1,0:T(8,128)(2,1)S(1)}, bf16[1024,128]{1,0:T(8,128)(2,1)S(1)}) custom-call(bf16[1024,192]{1,0:T(8,128)(2,1)S(1)} %get-tuple-element.125.query_ref, bf16[1024,192]{1,0:T(8,128)(2,1)S(1)} %bitcast.128, f32[3,1024,1]{2,1,0:T(8,128)S(1)} %copy-done.3, f32[1024,64]{1,0:T(8,128)S(1)} %get-tuple-element.151.cosine_ref.key_cosine_ref, ...), custom_call_target="tpu_custom_call" | custom-call | bytes 1024 | tf_op jit(solution)/shard_map/pallas_call | solution.py:323
  282.2 4.3 %collective-permute-done.14.refs_2_ = bf16[1152,512]{1,0:T(8,128)(2,1)} collective-permute-done((bf16[1152,512]{1,0:T(8,128)(2,1)}, bf16[1152,512]{1,0:T(8,128)(2,1)}, u32[]{:S(2)}, u32[]{:S(2)}) %collective-permute-start.14) | collective-permute-done | bytes 1179680 | tf_op jit(solution)/shard_map/ppermute | solution.py:1146
  287.8 6.1 %shard_map.244 = (bf16[1152,512]{1,0:T(8,128)(2,1)}, bf16[1152,512]{1,0:T(8,128)(2,1)}) custom-call(s32[2]{0:T(128)} %add_convert_fusion.keeps_ref, f32[2304,512]{1,0:T(8,128)} %get-tuple-element.139.refs_0_, bf16[2304,512]{1,0:T(8,128)(2,1)} %collective-permute-done.11.refs_1_, bf16[1152,512]{1,0:T(8,128)(2,1)} %collective-permute-done.14.refs_2_, ...), custom_call_target="tpu_custom_call" | custom-call | bytes 2304 | tf_op jit(solution)/shard_map/pallas_call | solution.py:1259
  297.0 14.6 %close.1 = (bf16[1024,3072]{1,0:T(8,128)(2,1)}, f32[96,2304]{1,0:T(8,128)}, f32[96,2304]{1,0:T(8,128)}, bf16[96,2304]{1,0:T(8,128)(2,1)}, bf16[96,2304]{1,0:T(8,128)(2,1)}) custom-call(s32[4]{0:T(128)} %pad_add_fusion.place_ref.refs_0_, bf16[1024,192]{1,0:T(8,128)(2,1)} %copy-done.5, bf16[1024,128]{1,0:T(8,128)(2,1)} %copy-done.6, ...), custom_call_target="tpu_custom_call" | custom-call | bytes 1024 | tf_op jit(solution)/shard_map/close/pallas_call | solution.py:905
  314.4 8.6 %collective-permute-done.18.refs_1_ = bf16[1152,512]{1,0:T(8,128)(2,1)S(1)} collective-permute-done((bf16[1152,512]{1,0:T(8,128)(2,1)}, bf16[1152,512]{1,0:T(8,128)(2,1)S(1)}, u32[]{:S(2)}, u32[]{:S(2)}) %collective-permute-start.18) | collective-permute-done | bytes 1179680 | tf_op jit(solution)/shard_map/ppermute | solution.py:1146
  325.6 2.8 broadcast_select_fusion.4
  328.9 4.1 collective-permute-done.16
  338.7 7.1 %own_outputs.1 = (f32[2,1536,512]{2,1,0:T(8,128)}, f32[2,1536,512]{2,1,0:T(8,128)}, f32[2,512,1536]{2,1,0:T(8,128)}) custom-call(s32[4]{0:T(128)} %pad_add_fusion.1.flags_ref, bf16[1152,512]{1,0:T(8,128)(2,1)} %get-tuple-element.179.refs_0_, bf16[1152,512]{1,0:T(8,128)(2,1)} %copy-done.19, bf16[1152,512]{1,0:T(8,128)(2,1)} %get-tuple-element.181.refs_2_, ...), custom_call_target="tpu_custom_call" | custom-call | bytes 1152 | tf_op jit(solution)/shard_map/own_outputs/pallas_call | solution.py:1049
  347.3 3.1 collective-permute-done.21
  351.1 3.0 scalar_call.3
  354.1 3.9 collective-permute-start.24
  358.6 1.6 collective-permute-done.27.refs_1_
  362.8 5.5 %collective-permute-done.25.refs_2_ = bf16[2,48,384]{2,1,0:T(8,128)(2,1)S(1)} collective-permute-done((bf16[2,48,384]{2,1,0:T(8,128)(2,1)}, bf16[2,48,384]{2,1,0:T(8,128)(2,1)S(1)}, u32[]{:S(2)}, u32[]{:S(2)}) %collective-permute-start.25) | collective-permute-done | bytes 73760 | tf_op jit(solution)/shard_map/ppermute | solution.py:1495
  369.6 2.4 scalar_call.4
  374.2 2.5 scalar_call.5
  377.9 1.7 collective-permute-start.34
  379.7 4.8 %collective-permute-done.30 = bf16[1,1,48,2304]{3,2,1,0:T(8,128)(2,1)S(1)} collective-permute-done((bf16[1,1,48,2304]{3,2,1,0:T(8,128)(2,1)}, bf16[1,1,48,2304]{3,2,1,0:T(8,128)(2,1)S(1)}, u32[]{:S(2)}, u32[]{:S(2)}) %collective-permute-start.30) | collective-permute-done | bytes 221216 | tf_op jit(solution)/shard_map/ppermute | solution.py:1146
  391.5 5.8 %into_outputs.1 = (f32[2,1536,512]{2,1,0:T(8,128)}, f32[2,1536,512]{2,1,0:T(8,128)}) custom-call(s32[4]{0:T(128)} %pad_add_fusion.1.flags_ref, f32[2,1536,512]{2,1,0:T(8,128)} %get-tuple-element.183.gate_any, f32[2,1536,512]{2,1,0:T(8,128)} %get-tuple-element.184.up_any, ...), custom_call_target="tpu_custom_call", output_to_operand_aliasing={{0}: (1, {}), {1}: (2, {})} | custom-call | bytes 1536 | tf_op jit(solution)/shard_map/into_outputs/pallas_call | solution.py:1090
  406.0 3.5 head_outputs.1
  409.5 1.6 copy.64
  413.2 4.2 down_outputs.1
  (237 shorter events, 81.7 us)
Async XLA Ops:
  7.2 64.3 %all-gather.11.cloned.1.call-start = ((), (), s32[]{:S(2)}) async-start(), calls=%async_computation.7 | async-start | bytes 5271552 | tf_op jit(solution)/shard_map/all_gather | solution.py:1491
  11.4 98.9 %all-gather.7.cloned.1.call-start = ((), (), s32[]{:S(2)}) async-start(), calls=%async_computation.3 | async-start | bytes 3538944 | tf_op jit(solution)/shard_map/all_gather | solution.py:1492
  12.1 137.6 %all-gather.13.cloned.1.call-start = ((), (), s32[]{:S(2)}) async-start(), calls=%async_computation.8 | async-start | bytes 3538944 | tf_op jit(solution)/shard_map/all_gather | solution.py:1542
  39.8 5.9 %collective-permute-start = (bf16[4,1,1,48,384]{4,3,0,2,1:T(8,128)(2,1)S(1)}, bf16[4,1,1,48,384]{4,3,0,2,1:T(8,128)(2,1)S(1)}, u32[]{:S(2)}, u32[]{:S(2)}) collective-permute-start(bf16[4,1,1,48,384]{4,3,0,2,1:T(8,128)(2,1)S(1)} %get-tuple-element.312), channel_id=1, source_target_pairs={{0,8},{8,0},{16,24},{24,16},{1,9},{9,1},{17,25},{25,17},{2,10},{10... | collective-permute-start | bytes 442376 | tf_op jit(solution)/shard_map/ppermute | solution.py:1146
  41.4 5.5 %collective-permute-start.2 = (bf16[4,1,1,48,384]{4,3,0,2,1:T(8,128)(2,1)S(1)}, bf16[4,1,1,48,384]{4,3,0,2,1:T(8,128)(2,1)S(1)}, u32[]{:S(2)}, u32[]{:S(2)}) collective-permute-start(bf16[4,1,1,48,384]{4,3,0,2,1:T(8,128)(2,1)S(1)} %get-tuple-element.313), channel_id=1, source_target_pairs={{0,16},{8,24},{16,0},{24,8},{1,17},{9,25},{17,1},{25,9},{2,18},{10... | collective-permute-start | bytes 442376 | tf_op jit(solution)/shard_map/ppermute | solution.py:1146
  47.0 8.0 %collective-permute-start.3 = (bf16[4,2,1,48,384]{4,3,0,2,1:T(8,128)(2,1)S(1)}, bf16[4,2,1,48,384]{4,3,0,2,1:T(8,128)(2,1)S(1)}, u32[]{:S(2)}, u32[]{:S(2)}) collective-permute-start(bf16[4,2,1,48,384]{4,3,0,2,1:T(8,128)(2,1)S(1)} %pad_maximum_fusion.13), channel_id=1, source_target_pairs={{0,8},{8,0},{16,24},{24,16},{1,9},{9,1},{17,25},{25,17},{2,10},{10... | collective-permute-start | bytes 884744 | tf_op jit(solution)/shard_map/ppermute | solution.py:1146
  47.8 28.3 %collective-permute-start.1 = (bf16[4,1,2,48,384]{4,3,0,2,1:T(8,128)(2,1)S(1)}, bf16[4,1,2,48,384]{4,3,0,2,1:T(8,128)(2,1)S(1)}, u32[]{:S(2)}, u32[]{:S(2)}) collective-permute-start(bf16[4,1,2,48,384]{4,3,0,2,1:T(8,128)(2,1)S(1)} %pad_maximum_fusion.12), channel_id=1, source_target_pairs={{0,16},{8,24},{16,0},{24,8},{1,17},{9,25},{17,1},{25,9},{2,18},{10... | collective-permute-start | bytes 884744 | tf_op jit(solution)/shard_map/ppermute | solution.py:1146
  72.8 20.7 %collective-permute-start.5 = (bf16[4,1,1,48,1536]{4,3,0,2,1:T(8,128)(2,1)S(1)}, bf16[4,1,1,48,1536]{4,3,0,2,1:T(8,128)(2,1)S(1)}, u32[]{:S(2)}, u32[]{:S(2)}) collective-permute-start(bf16[4,1,1,48,1536]{4,3,0,2,1:T(8,128)(2,1)S(1)} %get-tuple-element.274), channel_id=1, source_target_pairs={{0,16},{8,24},{16,0},{24,8},{1,17},{9,25},{17,1},{25,9},{2,18},{10... | collective-permute-start | bytes 1769480 | tf_op jit(solution)/shard_map/ppermute | solution.py:1146
  74.4 19.1 %collective-permute-start.4 = (bf16[4,1,1,48,1536]{4,3,0,2,1:T(8,128)(2,1)S(1)}, bf16[4,1,1,48,1536]{4,3,0,2,1:T(8,128)(2,1)S(1)}, u32[]{:S(2)}, u32[]{:S(2)}) collective-permute-start(bf16[4,1,1,48,1536]{4,3,0,2,1:T(8,128)(2,1)S(1)} %get-tuple-element.275), channel_id=1, source_target_pairs={{0,8},{8,0},{16,24},{24,16},{1,9},{9,1},{17,25},{25,17},{2,10},{10... | collective-permute-start | bytes 1769480 | tf_op jit(solution)/shard_map/ppermute | solution.py:1146
  110.3 120.5 %reduce-scatter.3.cloned.1.call-start = ((), (), s32[]{:S(2)}) async-start(), calls=%async_computation.4 | async-start | bytes 3833856 | tf_op jit(solution)/shard_map/reduce_scatter | solution.py:1582
  110.4 28.5 %collective-permute-start.6 = (bf16[4,1,2,48,1536]{4,3,0,2,1:T(8,128)(2,1)}, bf16[4,1,2,48,1536]{4,3,0,2,1:T(8,128)(2,1)}, u32[]{:S(2)}, u32[]{:S(2)}) collective-permute-start(bf16[4,1,2,48,1536]{4,3,0,2,1:T(8,128)(2,1)} %pad_maximum_fusion.3), channel_id=1, source_target_pairs={{0,16},{8,24},{16,0},{24,8},{1,17},{9,25},{17,1},{25,9},{2,18},{10... | collective-permute-start | bytes 3538952 | tf_op jit(solution)/shard_map/ppermute | solution.py:1146
  111.9 26.9 %copy-start.14 = (bf16[4,1,1,48,1536]{4,3,0,2,1:T(8,128)(2,1)S(1)}, bf16[4,1,1,48,1536]{4,3,0,2,1:T(8,128)(2,1)}, u32[]{:S(2)}) copy-start(bf16[4,1,1,48,1536]{4,3,0,2,1:T(8,128)(2,1)} %copy-done.13) | copy-start | bytes 1769476
  111.9 26.9 %copy-start.16 = (bf16[4,1,1,48,1536]{4,3,0,2,1:T(8,128)(2,1)S(1)}, bf16[4,1,1,48,1536]{4,3,0,2,1:T(8,128)(2,1)}, u32[]{:S(2)}) copy-start(bf16[4,1,1,48,1536]{4,3,0,2,1:T(8,128)(2,1)} %copy-done.15) | copy-start | bytes 1769476
  111.9 30.3 %collective-permute-start.7 = (bf16[4,2,1,48,1536]{4,3,0,2,1:T(8,128)(2,1)}, bf16[4,2,1,48,1536]{4,3,0,2,1:T(8,128)(2,1)S(1)}, u32[]{:S(2)}, u32[]{:S(2)}) collective-permute-start(bf16[4,2,1,48,1536]{4,3,0,2,1:T(8,128)(2,1)} %pad_maximum_fusion.4), channel_id=1, source_target_pairs={{0,8},{8,0},{16,24},{24,16},{1,9},{9,1},{17,25},{25,17},{2,10},{10... | collective-permute-start | bytes 3538952 | tf_op jit(solution)/shard_map/ppermute | solution.py:1146
  189.2 107.8 %all-gather.9.cloned.1.call-start = ((), (), s32[]{:S(2)}) async-start(), calls=%async_computation.5 | async-start | bytes 3538944 | tf_op jit(solution)/shard_map/all_gather | solution.py:1602
  198.8 54.2 %collective-permute-start.11 = (bf16[2304,512]{1,0:T(8,128)(2,1)}, bf16[2304,512]{1,0:T(8,128)(2,1)}, u32[]{:S(2)}, u32[]{:S(2)}) collective-permute-start(bf16[2304,512]{1,0:T(8,128)(2,1)} %get-tuple-element.135), channel_id=1, source_target_pairs={{0,8},{8,0},{16,24},{24,16},{1,9},{9,1},{17,25},{25,17},{2,10},{10... | collective-permute-start | bytes 7077896 | tf_op jit(solution)/shard_map/ppermute | solution.py:1146
  200.3 53.4 %collective-permute-start.12 = (bf16[2304,512]{1,0:T(8,128)(2,1)}, bf16[2304,512]{1,0:T(8,128)(2,1)}, u32[]{:S(2)}, u32[]{:S(2)}) collective-permute-start(bf16[2304,512]{1,0:T(8,128)(2,1)} %get-tuple-element.136), channel_id=1, source_target_pairs={{0,16},{8,24},{16,0},{24,8},{1,17},{9,25},{17,1},{25,9},{2,18},{10... | collective-permute-start | bytes 7077896 | tf_op jit(solution)/shard_map/ppermute | solution.py:1146
  239.5 8.6 %collective-permute-start.10 = (bf16[2,128,192]{2,1,0:T(8,128)(2,1)}, bf16[2,128,192]{2,1,0:T(8,128)(2,1)}, u32[]{:S(2)}, u32[]{:S(2)}) collective-permute-start(bf16[2,128,192]{2,1,0:T(8,128)(2,1)} %get-tuple-element.299), channel_id=1, source_target_pairs={{0,2},{1,3},{2,4},{3,5},{4,6},{5,7},{6,0},{7,1},{8,10},{9,11},{10,... | collective-permute-start | bytes 294920 | tf_op jit(solution)/shard_map/ppermute | solution.py:1495
  239.5 11.5 %collective-permute-start.9 = (bf16[2,128,192]{2,1,0:T(8,128)(2,1)}, bf16[2,128,192]{2,1,0:T(8,128)(2,1)}, u32[]{:S(2)}, u32[]{:S(2)}) collective-permute-start(bf16[2,128,192]{2,1,0:T(8,128)(2,1)} %get-tuple-element.300), channel_id=1, source_target_pairs={{0,4},{1,5},{2,6},{3,7},{4,0},{5,1},{6,2},{7,3},{8,12},{9,13},{10,... | collective-permute-start | bytes 294920 | tf_op jit(solution)/shard_map/ppermute | solution.py:1495
  240.0 11.0 %collective-permute-start.8 = (bf16[2,128,192]{2,1,0:T(8,128)(2,1)S(1)}, bf16[2,128,192]{2,1,0:T(8,128)(2,1)}, u32[]{:S(2)}, u32[]{:S(2)}) collective-permute-start(bf16[2,128,192]{2,1,0:T(8,128)(2,1)S(1)} %get-tuple-element.301), channel_id=1, source_target_pairs={{0,6},{1,7},{2,0},{3,1},{4,2},{5,3},{6,4},{7,5},{8,14},{9,15},{10,... | collective-permute-start | bytes 294920 | tf_op jit(solution)/shard_map/ppermute | solution.py:1495
  244.0 153.3 %reduce-scatter.5.cloned.1.call-start = ((), (), s32[]{:S(2)}) async-start(), calls=%async_computation.6 | async-start | bytes 7077888 | tf_op jit(solution)/shard_map/reduce_scatter | solution.py:1657
  259.2 27.3 %collective-permute-start.14 = (bf16[1152,512]{1,0:T(8,128)(2,1)}, bf16[1152,512]{1,0:T(8,128)(2,1)}, u32[]{:S(2)}, u32[]{:S(2)}) collective-permute-start(bf16[1152,512]{1,0:T(8,128)(2,1)} %get-tuple-element.147), channel_id=1, source_target_pairs={{0,16},{8,24},{16,0},{24,8},{1,17},{9,25},{17,1},{25,9},{2,18},{10... | collective-permute-start | bytes 3538952 | tf_op jit(solution)/shard_map/ppermute | solution.py:1146
  260.7 27.1 %collective-permute-start.15 = (bf16[1152,512]{1,0:T(8,128)(2,1)}, bf16[1152,512]{1,0:T(8,128)(2,1)}, u32[]{:S(2)}, u32[]{:S(2)}) collective-permute-start(bf16[1152,512]{1,0:T(8,128)(2,1)} %get-tuple-element.148), channel_id=1, source_target_pairs={{0,8},{8,0},{16,24},{24,16},{1,9},{9,1},{17,25},{25,17},{2,10},{10... | collective-permute-start | bytes 3538952 | tf_op jit(solution)/shard_map/ppermute | solution.py:1146
  263.2 1.9 collective-permute-start.13
  293.9 29.1 %collective-permute-start.18 = (bf16[1152,512]{1,0:T(8,128)(2,1)}, bf16[1152,512]{1,0:T(8,128)(2,1)S(1)}, u32[]{:S(2)}, u32[]{:S(2)}) collective-permute-start(bf16[1152,512]{1,0:T(8,128)(2,1)} %get-tuple-element.179.refs_0_), channel_id=1, source_target_pairs={{0,16},{8,24},{16,0},{24,8},{1,17},{9,25},{17,1},{25,9},{2,18},{10... | collective-permute-start | bytes 3538952 | tf_op jit(solution)/shard_map/ppermute | solution.py:1146
  294.4 30.4 %collective-permute-start.19 = (bf16[1152,512]{1,0:T(8,128)(2,1)}, bf16[1152,512]{1,0:T(8,128)(2,1)}, u32[]{:S(2)}, u32[]{:S(2)}) collective-permute-start(bf16[1152,512]{1,0:T(8,128)(2,1)} %get-tuple-element.181.refs_2_), channel_id=1, source_target_pairs={{0,8},{8,0},{16,24},{24,16},{1,9},{9,1},{17,25},{25,17},{2,10},{10... | collective-permute-start | bytes 3538952 | tf_op jit(solution)/shard_map/ppermute | solution.py:1146
  311.6 21.4 %collective-permute-start.16 = (bf16[2,1,48,2304]{3,2,1,0:T(8,128)(2,1)}, bf16[2,1,48,2304]{3,2,1,0:T(8,128)(2,1)S(1)}, u32[]{:S(2)}, u32[]{:S(2)}) collective-permute-start(bf16[2,1,48,2304]{3,2,1,0:T(8,128)(2,1)} %bitcast.40), channel_id=1, source_target_pairs={{0,8},{8,0},{16,24},{24,16},{1,9},{9,1},{17,25},{25,17},{2,10},{10... | collective-permute-start | bytes 1327112 | tf_op jit(solution)/shard_map/ppermute | solution.py:1146
  312.9 20.1 %collective-permute-start.17 = (bf16[1,2,48,2304]{3,2,1,0:T(8,128)(2,1)S(1)}, bf16[1,2,48,2304]{3,2,1,0:T(8,128)(2,1)S(1)}, u32[]{:S(2)}, u32[]{:S(2)}) collective-permute-start(bf16[1,2,48,2304]{3,2,1,0:T(8,128)(2,1)S(1)} %bitcast.155), channel_id=1, source_target_pairs={{0,16},{8,24},{16,0},{24,8},{1,17},{9,25},{17,1},{25,9},{2,18},{10... | collective-permute-start | bytes 1327112 | tf_op jit(solution)/shard_map/ppermute | solution.py:1146
  324.8 29.3 %collective-permute-start.22 = (bf16[576,512]{1,0:T(8,128)(2,1)}, bf16[576,512]{1,0:T(8,128)(2,1)}, u32[]{:S(2)}, u32[]{:S(2)}) collective-permute-start(bf16[576,512]{1,0:T(8,128)(2,1)} %get-tuple-element.283), channel_id=1, source_target_pairs={{0,8},{8,0},{16,24},{24,16},{1,9},{9,1},{17,25},{25,17},{2,10},{10... | collective-permute-start | bytes 1769480 | tf_op jit(solution)/shard_map/ppermute | solution.py:1146
  328.4 25.7 %collective-permute-start.23 = (bf16[576,512]{1,0:T(8,128)(2,1)}, bf16[576,512]{1,0:T(8,128)(2,1)}, u32[]{:S(2)}, u32[]{:S(2)}) collective-permute-start(bf16[576,512]{1,0:T(8,128)(2,1)} %get-tuple-element.279), channel_id=1, source_target_pairs={{0,16},{8,24},{16,0},{24,8},{1,17},{9,25},{17,1},{25,9},{2,18},{10... | collective-permute-start | bytes 1769480 | tf_op jit(solution)/shard_map/ppermute | solution.py:1146
  335.1 11.7 %collective-permute-start.20 = (bf16[1,1,48,2304]{3,2,1,0:T(8,128)(2,1)S(1)}, bf16[1,1,48,2304]{3,2,1,0:T(8,128)(2,1)S(1)}, u32[]{:S(2)}, u32[]{:S(2)}) collective-permute-start(bf16[1,1,48,2304]{3,2,1,0:T(8,128)(2,1)S(1)} %dynamic-slice_convert_fusion.1), channel_id=1, source_target_pairs={{0,16},{8,24},{16,0},{24,8},{1,17},{9,25},{17,1},{25,9},{2,18},{10... | collective-permute-start | bytes 663560 | tf_op jit(solution)/shard_map/ppermute | solution.py:1146
  336.6 13.8 %collective-permute-start.21 = (bf16[1,1,48,2304]{3,2,1,0:T(8,128)(2,1)S(1)}, bf16[1,1,48,2304]{3,2,1,0:T(8,128)(2,1)S(1)}, u32[]{:S(2)}, u32[]{:S(2)}) collective-permute-start(bf16[1,1,48,2304]{3,2,1,0:T(8,128)(2,1)S(1)} %dynamic-slice_convert_fusion), channel_id=1, source_target_pairs={{0,8},{8,0},{16,24},{24,16},{1,9},{9,1},{17,25},{25,17},{2,10},{10... | collective-permute-start | bytes 663560 | tf_op jit(solution)/shard_map/ppermute | solution.py:1146
  337.4 22.8 %collective-permute-start.27 = (bf16[576,512]{1,0:T(8,128)(2,1)}, bf16[576,512]{1,0:T(8,128)(2,1)}, u32[]{:S(2)}, u32[]{:S(2)}) collective-permute-start(bf16[576,512]{1,0:T(8,128)(2,1)} %get-tuple-element.198), channel_id=1, source_target_pairs={{0,8},{8,0},{16,24},{24,16},{1,9},{9,1},{17,25},{25,17},{2,10},{10... | collective-permute-start | bytes 1769480 | tf_op jit(solution)/shard_map/ppermute | solution.py:1146
  346.8 13.5 %collective-permute-start.28 = (bf16[576,512]{1,0:T(8,128)(2,1)}, bf16[576,512]{1,0:T(8,128)(2,1)}, u32[]{:S(2)}, u32[]{:S(2)}) collective-permute-start(bf16[576,512]{1,0:T(8,128)(2,1)} %get-tuple-element.199), channel_id=1, source_target_pairs={{0,16},{8,24},{16,0},{24,8},{1,17},{9,25},{17,1},{25,9},{2,18},{10... | collective-permute-start | bytes 1769480 | tf_op jit(solution)/shard_map/ppermute | solution.py:1146
  351.1 20.9 %copy-start.44 = (s32[1,128]{1,0:T(1,128)S(1)}, s32[1,128]{1,0:T(1,128)}, u32[]{:S(2)}) copy-start(s32[1,128]{1,0:T(1,128)} %param.16) | copy-start | bytes 1540
  351.1 20.9 %copy-start.8 = (bf16[1,128,1536]{2,1,0:T(8,128)(2,1)S(1)}, bf16[1,128,1536]{2,1,0:T(8,128)(2,1)}, u32[]{:S(2)}) copy-start(bf16[1,128,1536]{2,1,0:T(8,128)(2,1)} %param.15) | copy-start | bytes 1179652
  354.1 8.7 %collective-permute-start.24 = (bf16[2,48,384]{2,1,0:T(8,128)(2,1)}, bf16[2,48,384]{2,1,0:T(8,128)(2,1)S(1)}, u32[]{:S(2)}, u32[]{:S(2)}) collective-permute-start(bf16[2,48,384]{2,1,0:T(8,128)(2,1)} %get-tuple-element.193), channel_id=1, source_target_pairs={{0,6},{1,7},{2,0},{3,1},{4,2},{5,3},{6,4},{7,5},{8,14},{9,15},{10,... | collective-permute-start | bytes 221192 | tf_op jit(solution)/shard_map/ppermute | solution.py:1495
  358.0 10.3 %collective-permute-start.25 = (bf16[2,48,384]{2,1,0:T(8,128)(2,1)}, bf16[2,48,384]{2,1,0:T(8,128)(2,1)S(1)}, u32[]{:S(2)}, u32[]{:S(2)}) collective-permute-start(bf16[2,48,384]{2,1,0:T(8,128)(2,1)} %get-tuple-element.194), channel_id=1, source_target_pairs={{0,4},{1,5},{2,6},{3,7},{4,0},{5,1},{6,2},{7,3},{8,12},{9,13},{10,... | collective-permute-start | bytes 221192 | tf_op jit(solution)/shard_map/ppermute | solution.py:1495
  358.3 10.0 %collective-permute-start.26 = (bf16[2,48,384]{2,1,0:T(8,128)(2,1)}, bf16[2,48,384]{2,1,0:T(8,128)(2,1)S(1)}, u32[]{:S(2)}, u32[]{:S(2)}) collective-permute-start(bf16[2,48,384]{2,1,0:T(8,128)(2,1)} %get-tuple-element.195), channel_id=1, source_target_pairs={{0,2},{1,3},{2,4},{3,5},{4,6},{5,7},{6,0},{7,1},{8,10},{9,11},{10,... | collective-permute-start | bytes 221192 | tf_op jit(solution)/shard_map/ppermute | solution.py:1495
  360.3 24.2 %collective-permute-start.31 = (bf16[576,512]{1,0:T(8,128)(2,1)S(1)}, bf16[576,512]{1,0:T(8,128)(2,1)S(1)}, u32[]{:S(2)}, u32[]{:S(2)}) collective-permute-start(bf16[576,512]{1,0:T(8,128)(2,1)S(1)} %copy-done.28), channel_id=1, source_target_pairs={{0,8},{8,0},{16,24},{24,16},{1,9},{9,1},{17,25},{25,17},{2,10},{10... | collective-permute-start | bytes 1769480 | tf_op jit(solution)/shard_map/ppermute | solution.py:1146
  361.1 23.4 %collective-permute-start.32 = (bf16[576,512]{1,0:T(8,128)(2,1)S(1)}, bf16[576,512]{1,0:T(8,128)(2,1)S(1)}, u32[]{:S(2)}, u32[]{:S(2)}) collective-permute-start(bf16[576,512]{1,0:T(8,128)(2,1)S(1)} %copy-done.29), channel_id=1, source_target_pairs={{0,16},{8,24},{16,0},{24,8},{1,17},{9,25},{17,1},{25,9},{2,18},{10... | collective-permute-start | bytes 1769480 | tf_op jit(solution)/shard_map/ppermute | solution.py:1146
  372.0 1.6 collective-permute-start.29
  376.8 7.7 %collective-permute-start.30 = (bf16[1,1,48,2304]{3,2,1,0:T(8,128)(2,1)}, bf16[1,1,48,2304]{3,2,1,0:T(8,128)(2,1)S(1)}, u32[]{:S(2)}, u32[]{:S(2)}) collective-permute-start(bf16[1,1,48,2304]{3,2,1,0:T(8,128)(2,1)} %bitcast.151), channel_id=1, source_target_pairs={{0,16},{8,24},{16,0},{24,8},{1,17},{9,25},{17,1},{25,9},{2,18},{10... | collective-permute-start | bytes 663560 | tf_op jit(solution)/shard_map/ppermute | solution.py:1146
  377.9 10.1 %collective-permute-start.34 = (bf16[1,1,48,2304]{3,2,1,0:T(8,128)(2,1)}, bf16[1,1,48,2304]{3,2,1,0:T(8,128)(2,1)S(1)}, u32[]{:S(2)}, u32[]{:S(2)}) collective-permute-start(bf16[1,1,48,2304]{3,2,1,0:T(8,128)(2,1)} %bitcast.150), channel_id=1, source_target_pairs={{0,8},{8,0},{16,24},{24,16},{1,9},{9,1},{17,25},{25,17},{2,10},{10... | collective-permute-start | bytes 663560 | tf_op jit(solution)/shard_map/ppermute | solution.py:1146
  386.5 15.2 %collective-permute-start.33 = (bf16[2,1,48,2304]{3,2,1,0:T(8,128)(2,1)}, bf16[2,1,48,2304]{3,2,1,0:T(8,128)(2,1)}, u32[]{:S(2)}, u32[]{:S(2)}) collective-permute-start(bf16[2,1,48,2304]{3,2,1,0:T(8,128)(2,1)} %pad_maximum_fusion.10), channel_id=1, source_target_pairs={{0,8},{8,0},{16,24},{24,16},{1,9},{9,1},{17,25},{25,17},{2,10},{10... | collective-permute-start | bytes 1327112 | tf_op jit(solution)/shard_map/ppermute | solution.py:1146
  388.9 13.9 %collective-permute-start.35 = (bf16[1,2,48,2304]{3,2,1,0:T(8,128)(2,1)}, bf16[1,2,48,2304]{3,2,1,0:T(8,128)(2,1)}, u32[]{:S(2)}, u32[]{:S(2)}) collective-permute-start(bf16[1,2,48,2304]{3,2,1,0:T(8,128)(2,1)} %pad_maximum_fusion.11), channel_id=1, source_target_pairs={{0,16},{8,24},{16,0},{24,8},{1,17},{9,25},{17,1},{25,9},{2,18},{10... | collective-permute-start | bytes 1327112 | tf_op jit(solution)/shard_map/ppermute | solution.py:1146
  390.3 22.0 %collective-permute-start.36 = (bf16[576,512]{1,0:T(8,128)(2,1)S(1)}, bf16[576,512]{1,0:T(8,128)(2,1)S(1)}, u32[]{:S(2)}, u32[]{:S(2)}) collective-permute-start(bf16[576,512]{1,0:T(8,128)(2,1)S(1)} %copy-done.26), channel_id=1, source_target_pairs={{0,8},{8,0},{16,24},{24,16},{1,9},{9,1},{17,25},{25,17},{2,10},{10... | collective-permute-start | bytes 1769480 | tf_op jit(solution)/shard_map/ppermute | solution.py:1146
  390.6 22.5 %collective-permute-start.37 = (bf16[576,512]{1,0:T(8,128)(2,1)S(1)}, bf16[576,512]{1,0:T(8,128)(2,1)}, u32[]{:S(2)}, u32[]{:S(2)}) collective-permute-start(bf16[576,512]{1,0:T(8,128)(2,1)S(1)} %copy-done.27), channel_id=1, source_target_pairs={{0,16},{8,24},{16,0},{24,8},{1,17},{9,25},{17,1},{25,9},{2,18},{10... | collective-permute-start | bytes 1769480 | tf_op jit(solution)/shard_map/ppermute | solution.py:1146
  (41 other events, 134.5 us)
Sparse Core Ops, SparseCore 0:
  11.5 59.9 all-gather.10
  73.1 37.1 all-gather.6
  112.5 37.1 all-gather.12
  189.3 41.5 reduce-scatter.2
  244.1 37.8 all-gather.8
  311.8 76.0 reduce-scatter.4

commit v12 on v11

--- a/solution.py
+++ b/solution.py
@@ -1021,6 +1021,32 @@
     out_ref[narrow:, hidden:] = value[hidden:, narrow:]
 
 
+def finish_kernel(
+    sum_ref, middle_ref, segment_ref, grad_ref, gain_ref, hidden_ref, out_ref, grad_in_ref
+):
+    features = middle_ref.shape[1]
+    live = segment_ref[...] != 0
+    rows = middle_ref[...] + sum_ref[:, features:].astype(jnp.float32)
+    out_ref[...] = jnp.where(live, rows, 0.0).astype(jnp.bfloat16)
+    grad_one = sum_ref[:, :features].astype(jnp.float32)
+    hidden = hidden_ref[...].astype(jnp.float32)
+    scale = lax.rsqrt(jnp.mean(hidden * hidden, -1, keepdims=True) + EPS)
+    grad_in_ref[...] = grad_ref[...] + norm_back(grad_one * gain_ref[...], hidden * scale, scale)
+
+
+def finish_rows(sums, middle, segments, grad_middle, gain, hidden):
+    return pl.pallas_call(
+        finish_kernel,
+        name="finish_rows",
+        out_shape=(
+            jax.ShapeDtypeStruct(middle.shape, jnp.bfloat16),
+            jax.ShapeDtypeStruct(middle.shape, jnp.float32),
+        ),
+        compiler_params=pltpu.CompilerParams(vmem_limit_bytes=58 << 20),
+        cost_estimate=pl.CostEstimate(flops=0, bytes_accessed=1024, transcendentals=0),
+    )(sums, middle, segments, grad_middle, gain[None, :], hidden)
+
+
 def own_kernel(flags_ref, *refs):
     down_ref = refs[6]
     for side in range(2):
@@ -1397,6 +1423,7 @@
         came,
         out_sums,
         scratch=[pltpu.VMEM((2 * chips, share, side), stay.dtype)],
+        flops=2000000000,
     )
 
 
@@ -1654,10 +1681,7 @@
         side_width,
         block,
     )
-    both_sums = lax.psum_scatter(
-        both_rows, "ctx", scatter_dimension=0, tiled=True
-    ).astype(jnp.float32)
-    grad_one, out_sum = both_sums[:, :MODEL_WIDTH], both_sums[:, MODEL_WIDTH:]
+    both_sums = lax.psum_scatter(both_rows, "ctx", scatter_dimension=0, tiled=True)
 
     line = size // 2 * side_width
     cubes = [
@@ -1700,10 +1724,9 @@
     for side in range(2):
         arrived += [first[side], second[side], third[side]]
     grad_gate, grad_up = into_outputs(flags, grad_gate, grad_up, after(arrived, *sent))
-    output = jnp.where((segments[0] != 0)[:, None], middle_own + out_sum, 0.0)
-    own_hidden = inputs[0].astype(jnp.float32)
-    own_scale = lax.rsqrt(jnp.mean(own_hidden * own_hidden, -1, keepdims=True) + EPS)
-    grad_in = grad_middle + norm_back(grad_one * gain_one, own_hidden * own_scale, own_scale)
+    output, grad_in = finish_rows(
+        both_sums, middle_own, segments[0][:, None], grad_middle, gain_one, inputs[0]
+    )
     for cube in cubes:
         cube.join(grad_gate, grad_up, output, grad_in)
     head_outs = head_outputs(
@@ -1715,7 +1738,7 @@
     grad_down = down_outputs(flags, grad_down, after(arrived, head_outs))
 
     return (
-        output.astype(jnp.bfloat16)[None],
+        output[None],
         grad_in[None],
         head_outs[4][0],
         *head_outs[:4],

time: 426 us -> 425 us (level)
  other arithmetic: 35.9 us -> 31.3 us
    unnamed x92 -> x84, local copies, waits for them, and re-layouts: 11 us -> 9.39 us
  transfers between devices with their start and end apart: 44 -> 44, of which waited for: 24 -> 26; matrix products, arithmetic and copies ran while one was open for 11% -> 10% of each run, Pallas kernels for 27% -> 28%
where the time goes in v12:
time: 425 us; the launch traced here: 424 us
  Pallas kernels  160 us (38%)
  waiting for transfers between devices  126 us (30%)
  starting transfers between devices  44.7 us (11%)
  other arithmetic  31.3 us (7%)
  blocking collectives  24.5 us (6%)
  local copies, waits for them, and re-layouts  21.6 us (5%)
  between operations  14.7 us (3%)
    ppermute x30, waiting for transfers between devices, swap(): return lax.ppermute(value, 'rep', [(i, i ^ bit) for i in range(size)])  63.8 us
    pallas_call x1, Pallas kernels, layer_rows(): pl.pallas_call(layer_kernel, out_shape=(shaped((tokens, features), low),...  39.4 us
    ppermute x30, starting transfers between devices, swap(): return lax.ppermute(value, 'rep', [(i, i ^ bit) for i in range(size)])  35.5 us
    all_to_all x1, blocking collectives, per_device(): lax.all_to_all(head_columns, 'ctx', split_axis=0, concat_axis=0, tiled=True)  24.5 us
    pallas_call x2, Pallas kernels, expert_products(): pl.pallas_call(lambda *refs: product_kernel(e, *refs), name='expert_produ...  18.9 us
    all_gather x1, waiting for transfers between devices, per_device(): gathered = lax.all_gather(rows, 'ctx', axis=0)  16.5 us
    pallas_call x1, Pallas kernels, attend(): pl.pallas_call(attend_kernel, out_shape=(shaped((tokens, features), jnp.b...  15.3 us
    pallas_call x1, Pallas kernels, close_rows(): pl.pallas_call(lambda *refs: close_kernel(reps, *refs), name='close', out...  14.7 us
  transfers between devices with their start and end apart: 44, of which 26 were waited for; matrix products, arithmetic and copies ran while one was open for 10% of the time, Pallas kernels for 28%

profile of v12, /device:TPU:0, one launch (start us, length us, event | category | flops | bytes accessed | tf_op | source)
XLA Modules:
  0.0 423.6 jit_solution(1845624994856697902)
XLA Ops:
  9.5 1.9 fusion.4
  15.3 24.5 %all_to_all.5 = bf16[8,48,384]{2,1,0:T(8,128)(2,1)S(1)} all-to-all(bf16[8,48,384]{2,1,0:T(8,128)(2,1)S(1)} %copy.59), channel_id=1, replica_groups=mesh['rep'=4,'ctx'=8] {'ctx'}, dimensions={0} | all-to-all | bytes 589824 | tf_op jit(solution)/shard_map/all_to_all | solution.py:1547
  42.9 2.8 collective-permute-done
  47.8 1.6 collective-permute-start.1
  49.4 5.6 %collective-permute-done.3 = bf16[4,2,1,48,384]{4,3,0,2,1:T(8,128)(2,1)S(1)} collective-permute-done((bf16[4,2,1,48,384]{4,3,0,2,1:T(8,128)(2,1)S(1)}, bf16[4,2,1,48,384]{4,3,0,2,1:T(8,128)(2,1)S(1)}, u32[]{:S(2)}, u32[]{:S(2)}) %collective-permute-start.3) | collective-permute-done | bytes 294944 | tf_op jit(solution)/shard_map/ppermute | solution.py:1172
  55.0 16.5 %all-gather.11.cloned.1.call-done = bf16[1408,1664]{1,0:T(8,128)(2,1)} async-done(((bf16[176,1664]{1,0:T(8,128)(2,1)}), bf16[1408,1664]{1,0:T(8,128)(2,1)}) %all-gather.11.cloned.1.call-update) | async-done | bytes 4685840 | tf_op jit(solution)/shard_map/all_gather | solution.py:1518
  72.8 1.6 collective-permute-start.5
  76.9 15.3 %shard_map.238 = (bf16[1024,1536]{1,0:T(8,128)(2,1)}, bf16[1024,192]{1,0:T(8,128)(2,1)S(1)}, bf16[1024,64]{1,0:T(8,128)(2,1)S(1)}, bf16[1024,64]{1,0:T(8,128)(2,...) custom-call(bf16[8,176,1664]{2,1,0:T(8,128)(2,1)} %bitcast.123, ...), custom_call_target="tpu_custom_call" | custom-call | bytes 1024 | tf_op jit(solution)/shard_map/pallas_call | solution.py:194
  92.2 2.2 broadcast_select_fusion.13
  97.3 13.1 %all-gather.7.cloned.1.call-done.cotangent_ref = bf16[1024,1536]{1,0:T(8,128)(2,1)} async-done(((bf16[128,1536]{1,0:T(8,128)(2,1)}), bf16[1024,1536]{1,0:T(8,128)(2,1)}) %all-gather.7.cloned.1.call-update) | async-done | bytes 3145744 | tf_op jit(solution)/shard_map/all_gather | solution.py:1519
  115.5 23.4 %collective-permute-done.6 = bf16[4,1,2,48,1536]{4,3,0,2,1:T(8,128)(2,1)} collective-permute-done((bf16[4,1,2,48,1536]{4,3,0,2,1:T(8,128)(2,1)}, bf16[4,1,2,48,1536]{4,3,0,2,1:T(8,128)(2,1)}, u32[]{:S(2)}, u32[]{:S(2)}) %collective-permute-start.6) | collective-permute-done | bytes 1179680 | tf_op jit(solution)/shard_map/ppermute | solution.py:1172
  140.6 1.6 copy.62
  144.2 5.5 %all-gather.13.cloned.1.call-done = bf16[4096,384]{1,0:T(8,128)(2,1)} async-done(((bf16[512,384]{1,0:T(8,128)(2,1)}), bf16[4096,384]{1,0:T(8,128)(2,1)}) %all-gather.13.cloned.1.call-update) | async-done | bytes 3145744 | tf_op jit(solution)/shard_map/all_gather | solution.py:1569
  149.7 39.4 %shard_map.239 = (bf16[1024,1536]{1,0:T(8,128)(2,1)}, bf16[2,1024,512]{2,1,0:T(8,128)(2,1)}, bf16[2,1024,512]{2,1,0:T(8,128)(2,1)}, bf16[2,1024,512]{2,1,0:T(8,1...) custom-call(s32[4]{0:T(128)} %pad_add_fusion.place_ref.refs_0_, ...), custom_call_target="tpu_custom_call" | custom-call | flops 19327352832 | bytes 40894464 | tf_op jit(solution)/shard_map/pallas_call | solution.py:513
  189.4 9.3 %expert_products.2 = (bf16[2304,512]{1,0:T(8,128)(2,1)}, bf16[2304,512]{1,0:T(8,128)(2,1)}) custom-call(bf16[1024,1536]{1,0:T(8,128)(2,1)} %get-tuple-element.138.refs_0_, bf16[2,1024,512]{2,1,0:T(8,128)(2,1)} %get-tuple-element.133.refs_1_, bf16[2,1024,512]{2,1,0:T(8,128)(2,1)} %get-tuple-element.134.refs_2_, ...), custom_call_target="tpu_custom_call" | custom-call | bytes 1024 | tf_op jit(solution)/shard_map/expert_products/pallas_call | solution.py:668
  201.8 9.6 %expert_products.3 = (f32[2304,512]{1,0:T(8,128)}, f32[2304,512]{1,0:T(8,128)}) custom-call(bf16[1024,1536]{1,0:T(8,128)(2,1)} %get-tuple-element.138.refs_0_, bf16[2,1024,512]{2,1,0:T(8,128)(2,1)} %get-tuple-element.133.refs_1_, bf16[2,1024,512]{2,1,0:T(8,128)(2,1)} %get-tuple-element.134.refs_2_, ...), custom_call_target="tpu_custom_call" | custom-call | bytes 1024 | tf_op jit(solution)/shard_map/expert_products/pallas_call | solution.py:668
  211.4 8.9 %shard_map.240.refs_9_ = bf16[1024,1536]{1,0:T(8,128)(2,1)} custom-call(s32[4]{0:T(128)S(1)} %copy-done.8, bf16[2,1024,512]{2,1,0:T(8,128)(2,1)} %get-tuple-element.142.refs_3_.scaled_ref, bf16[2,512,1536]{2,1,0:T(8,128)(2,1)} %down_weight_ref.1), custom_call_target="tpu_custom_call" | custom-call | bytes 1024 | tf_op jit(solution)/shard_map/pallas_call | solution.py:705
  220.2 10.7 %reduce-scatter.3.cloned.1.call-done.sum_ref = bf16[128,1664]{1,0:T(8,128)(2,1)} async-done(((bf16[1024,1664]{1,0:T(8,128)(2,1)}), bf16[128,1664]{1,0:T(8,128)(2,1)}) %reduce-scatter.3.cloned.1.call-update) | async-done | bytes 426000 | tf_op jit(solution)/shard_map/reduce_scatter | solution.py:1609
  230.9 6.8 %shard_map.241 = (f32[128,1536]{1,0:T(8,128)}, bf16[128,1536]{1,0:T(8,128)(2,1)}, bf16[8,128,192]{2,1,0:T(8,128)(2,1)}, bf16[128,16]{1,0:T(8,128)(2,1)}, f32[1,1536]{1,0:T(1,128)}) custom-call(s32[4]{0:T(128)} %pad_add_fusion.place_ref.refs_0_, bf16[128,1664]{1,0:T(8,128)(2,1)} %reduce-scatter.3.cloned.1.call-done.sum_ref, ...), custom_call_target="tpu_custom_call" | custom-call | bytes 128 | tf_op jit(solution)/shard_map/pallas_call | solution.py:776
  237.7 1.8 dynamic-slice_bitcast_fusion.5
  240.0 3.3 collective-permute-start.8
  244.2 3.9 collective-permute-done.10
  248.1 2.9 collective-permute-done.9
  251.0 1.9 pad_maximum_fusion.9
  253.7 5.5 %shard_map.242 = (bf16[1152,512]{1,0:T(8,128)(2,1)}, bf16[1152,512]{1,0:T(8,128)(2,1)}) custom-call(s32[2]{0:T(128)} %add_convert_fusion.keeps_ref, f32[2304,512]{1,0:T(8,128)} %get-tuple-element.140.refs_0_, bf16[2304,512]{1,0:T(8,128)(2,1)} %collective-permute-done.11.refs_1_, f32[2304,512]{1,0:T(8,128)} %get-tuple-element.141.refs_2_.refs_3_, ...), custom_call_target="tpu_custom_call" | custom-call | flops 70778880000 | bytes 14155776 | tf_op jit(solution)/shard_map/pallas_call | solution.py:1246
  261.4 1.8 select_bitcast_fusion
  263.2 1.8 collective-permute-done.13
  266.4 13.1 %shard_map.243 = (bf16[1024,192]{1,0:T(8,128)(2,1)S(1)}, bf16[1024,128]{1,0:T(8,128)(2,1)S(1)}) custom-call(bf16[1024,192]{1,0:T(8,128)(2,1)S(1)} %get-tuple-element.123.query_ref, bf16[1024,192]{1,0:T(8,128)(2,1)S(1)} %bitcast.121, f32[3,1024,1]{2,1,0:T(8,128)S(1)} %copy-done.3, f32[1024,64]{1,0:T(8,128)S(1)} %get-tuple-element.153.cosine_ref.key_cosine_ref, ...), custom_call_target="tpu_custom_call" | custom-call | bytes 1024 | tf_op jit(solution)/shard_map/pallas_call | solution.py:323
  281.1 5.4 %collective-permute-done.14.refs_2_ = bf16[1152,512]{1,0:T(8,128)(2,1)} collective-permute-done((bf16[1152,512]{1,0:T(8,128)(2,1)}, bf16[1152,512]{1,0:T(8,128)(2,1)}, u32[]{:S(2)}, u32[]{:S(2)}) %collective-permute-start.14) | collective-permute-done | bytes 1179680 | tf_op jit(solution)/shard_map/ppermute | solution.py:1172
  287.7 6.1 %shard_map.244 = (bf16[1152,512]{1,0:T(8,128)(2,1)}, bf16[1152,512]{1,0:T(8,128)(2,1)}) custom-call(s32[2]{0:T(128)} %add_convert_fusion.keeps_ref, f32[2304,512]{1,0:T(8,128)} %get-tuple-element.140.refs_0_, bf16[2304,512]{1,0:T(8,128)(2,1)} %collective-permute-done.11.refs_1_, bf16[1152,512]{1,0:T(8,128)(2,1)} %collective-permute-done.14.refs_2_, ...), custom_call_target="tpu_custom_call" | custom-call | bytes 2304 | tf_op jit(solution)/shard_map/pallas_call | solution.py:1285
  297.0 14.7 %close.1 = (bf16[1024,3072]{1,0:T(8,128)(2,1)}, f32[96,2304]{1,0:T(8,128)}, f32[96,2304]{1,0:T(8,128)}, bf16[96,2304]{1,0:T(8,128)(2,1)}, bf16[96,2304]{1,0:T(8,128)(2,1)}) custom-call(s32[4]{0:T(128)} %pad_add_fusion.place_ref.refs_0_, bf16[1024,192]{1,0:T(8,128)(2,1)} %copy-done.5, bf16[1024,128]{1,0:T(8,128)(2,1)} %copy-done.6, ...), custom_call_target="tpu_custom_call" | custom-call | bytes 1024 | tf_op jit(solution)/shard_map/close/pallas_call | solution.py:905
  314.5 8.5 %collective-permute-done.18.refs_1_ = bf16[1152,512]{1,0:T(8,128)(2,1)S(1)} collective-permute-done((bf16[1152,512]{1,0:T(8,128)(2,1)}, bf16[1152,512]{1,0:T(8,128)(2,1)S(1)}, u32[]{:S(2)}, u32[]{:S(2)}) %collective-permute-start.18) | collective-permute-done | bytes 1179680 | tf_op jit(solution)/shard_map/ppermute | solution.py:1172
  325.7 2.8 broadcast_select_fusion.4
  328.9 4.1 collective-permute-done.16
  338.6 7.0 %own_outputs.1 = (f32[2,1536,512]{2,1,0:T(8,128)}, f32[2,1536,512]{2,1,0:T(8,128)}, f32[2,512,1536]{2,1,0:T(8,128)}) custom-call(s32[4]{0:T(128)} %pad_add_fusion.1.flags_ref, bf16[1152,512]{1,0:T(8,128)(2,1)} %get-tuple-element.183.refs_0_, bf16[1152,512]{1,0:T(8,128)(2,1)} %copy-done.19, bf16[1152,512]{1,0:T(8,128)(2,1)} %get-tuple-element.185.refs_2_, ...), custom_call_target="tpu_custom_call" | custom-call | bytes 1152 | tf_op jit(solution)/shard_map/own_outputs/pallas_call | solution.py:1075
  347.3 3.1 collective-permute-done.21
  351.1 3.0 scalar_call.3
  354.0 4.1 collective-permute-start.24
  362.8 5.7 %collective-permute-done.25.refs_2_ = bf16[2,48,384]{2,1,0:T(8,128)(2,1)S(1)} collective-permute-done((bf16[2,48,384]{2,1,0:T(8,128)(2,1)}, bf16[2,48,384]{2,1,0:T(8,128)(2,1)S(1)}, u32[]{:S(2)}, u32[]{:S(2)}) %collective-permute-start.25) | collective-permute-done | bytes 73760 | tf_op jit(solution)/shard_map/ppermute | solution.py:1522
  369.7 2.4 scalar_call.4
  372.1 1.6 collective-permute-done.29.came_ref
  374.4 2.7 scalar_call.5
  379.0 1.7 collective-permute-start.34
  380.7 4.1 collective-permute-done.30
  391.1 5.8 %into_outputs.1 = (f32[2,1536,512]{2,1,0:T(8,128)}, f32[2,1536,512]{2,1,0:T(8,128)}) custom-call(s32[4]{0:T(128)} %pad_add_fusion.1.flags_ref, f32[2,1536,512]{2,1,0:T(8,128)} %get-tuple-element.187.gate_any, f32[2,1536,512]{2,1,0:T(8,128)} %get-tuple-element.188.up_any, ...), custom_call_target="tpu_custom_call", output_to_operand_aliasing={{0}: (1, {}), {1}: (2, {})} | custom-call | bytes 1536 | tf_op jit(solution)/shard_map/into_outputs/pallas_call | solution.py:1116
  396.9 3.2 finish_rows.1
  404.8 3.5 head_outputs.1
  412.5 4.2 down_outputs.1
  (223 shorter events, 79.1 us)
Async XLA Ops:
  7.2 64.3 %all-gather.11.cloned.1.call-start = ((), (), s32[]{:S(2)}) async-start(), calls=%async_computation.7 | async-start | bytes 5271552 | tf_op jit(solution)/shard_map/all_gather | solution.py:1518
  11.4 98.9 %all-gather.7.cloned.1.call-start = ((), (), s32[]{:S(2)}) async-start(), calls=%async_computation.3 | async-start | bytes 3538944 | tf_op jit(solution)/shard_map/all_gather | solution.py:1519
  12.1 137.6 %all-gather.13.cloned.1.call-start = ((), (), s32[]{:S(2)}) async-start(), calls=%async_computation.8 | async-start | bytes 3538944 | tf_op jit(solution)/shard_map/all_gather | solution.py:1569
  39.8 5.9 %collective-permute-start = (bf16[4,1,1,48,384]{4,3,0,2,1:T(8,128)(2,1)S(1)}, bf16[4,1,1,48,384]{4,3,0,2,1:T(8,128)(2,1)S(1)}, u32[]{:S(2)}, u32[]{:S(2)}) collective-permute-start(bf16[4,1,1,48,384]{4,3,0,2,1:T(8,128)(2,1)S(1)} %get-tuple-element.316), channel_id=1, source_target_pairs={{0,8},{8,0},{16,24},{24,16},{1,9},{9,1},{17,25},{25,17},{2,10},{10... | collective-permute-start | bytes 442376 | tf_op jit(solution)/shard_map/ppermute | solution.py:1172
  41.4 5.5 %collective-permute-start.2 = (bf16[4,1,1,48,384]{4,3,0,2,1:T(8,128)(2,1)S(1)}, bf16[4,1,1,48,384]{4,3,0,2,1:T(8,128)(2,1)S(1)}, u32[]{:S(2)}, u32[]{:S(2)}) collective-permute-start(bf16[4,1,1,48,384]{4,3,0,2,1:T(8,128)(2,1)S(1)} %get-tuple-element.317), channel_id=1, source_target_pairs={{0,16},{8,24},{16,0},{24,8},{1,17},{9,25},{17,1},{25,9},{2,18},{10... | collective-permute-start | bytes 442376 | tf_op jit(solution)/shard_map/ppermute | solution.py:1172
  47.0 8.0 %collective-permute-start.3 = (bf16[4,2,1,48,384]{4,3,0,2,1:T(8,128)(2,1)S(1)}, bf16[4,2,1,48,384]{4,3,0,2,1:T(8,128)(2,1)S(1)}, u32[]{:S(2)}, u32[]{:S(2)}) collective-permute-start(bf16[4,2,1,48,384]{4,3,0,2,1:T(8,128)(2,1)S(1)} %pad_maximum_fusion.13), channel_id=1, source_target_pairs={{0,8},{8,0},{16,24},{24,16},{1,9},{9,1},{17,25},{25,17},{2,10},{10... | collective-permute-start | bytes 884744 | tf_op jit(solution)/shard_map/ppermute | solution.py:1172
  47.8 28.3 %collective-permute-start.1 = (bf16[4,1,2,48,384]{4,3,0,2,1:T(8,128)(2,1)S(1)}, bf16[4,1,2,48,384]{4,3,0,2,1:T(8,128)(2,1)S(1)}, u32[]{:S(2)}, u32[]{:S(2)}) collective-permute-start(bf16[4,1,2,48,384]{4,3,0,2,1:T(8,128)(2,1)S(1)} %pad_maximum_fusion.12), channel_id=1, source_target_pairs={{0,16},{8,24},{16,0},{24,8},{1,17},{9,25},{17,1},{25,9},{2,18},{10... | collective-permute-start | bytes 884744 | tf_op jit(solution)/shard_map/ppermute | solution.py:1172
  72.8 19.4 %collective-permute-start.5 = (bf16[4,1,1,48,1536]{4,3,0,2,1:T(8,128)(2,1)S(1)}, bf16[4,1,1,48,1536]{4,3,0,2,1:T(8,128)(2,1)S(1)}, u32[]{:S(2)}, u32[]{:S(2)}) collective-permute-start(bf16[4,1,1,48,1536]{4,3,0,2,1:T(8,128)(2,1)S(1)} %get-tuple-element.278), channel_id=1, source_target_pairs={{0,16},{8,24},{16,0},{24,8},{1,17},{9,25},{17,1},{25,9},{2,18},{10... | collective-permute-start | bytes 1769480 | tf_op jit(solution)/shard_map/ppermute | solution.py:1172
  74.4 17.8 %collective-permute-start.4 = (bf16[4,1,1,48,1536]{4,3,0,2,1:T(8,128)(2,1)S(1)}, bf16[4,1,1,48,1536]{4,3,0,2,1:T(8,128)(2,1)S(1)}, u32[]{:S(2)}, u32[]{:S(2)}) collective-permute-start(bf16[4,1,1,48,1536]{4,3,0,2,1:T(8,128)(2,1)S(1)} %get-tuple-element.279), channel_id=1, source_target_pairs={{0,8},{8,0},{16,24},{24,16},{1,9},{9,1},{17,25},{25,17},{2,10},{10... | collective-permute-start | bytes 1769480 | tf_op jit(solution)/shard_map/ppermute | solution.py:1172
  76.9 15.3 %copy-start.7 = (f32[1,1536]{1,0:T(1,128)}, f32[1,1536]{1,0:T(1,128)S(1)}, u32[]{:S(2)}) copy-start(f32[1,1536]{1,0:T(1,128)S(1)} %reshape.283.gain_ref) | copy-start | bytes 18436
  110.3 120.5 %reduce-scatter.3.cloned.1.call-start = ((), (), s32[]{:S(2)}) async-start(), calls=%async_computation.4 | async-start | bytes 3833856 | tf_op jit(solution)/shard_map/reduce_scatter | solution.py:1609
  110.4 28.5 %collective-permute-start.6 = (bf16[4,1,2,48,1536]{4,3,0,2,1:T(8,128)(2,1)}, bf16[4,1,2,48,1536]{4,3,0,2,1:T(8,128)(2,1)}, u32[]{:S(2)}, u32[]{:S(2)}) collective-permute-start(bf16[4,1,2,48,1536]{4,3,0,2,1:T(8,128)(2,1)} %pad_maximum_fusion.3), channel_id=1, source_target_pairs={{0,16},{8,24},{16,0},{24,8},{1,17},{9,25},{17,1},{25,9},{2,18},{10... | collective-permute-start | bytes 3538952 | tf_op jit(solution)/shard_map/ppermute | solution.py:1172
  111.9 27.0 %copy-start.14 = (bf16[4,1,1,48,1536]{4,3,0,2,1:T(8,128)(2,1)S(1)}, bf16[4,1,1,48,1536]{4,3,0,2,1:T(8,128)(2,1)}, u32[]{:S(2)}) copy-start(bf16[4,1,1,48,1536]{4,3,0,2,1:T(8,128)(2,1)} %copy-done.13) | copy-start | bytes 1769476
  111.9 27.0 %copy-start.16 = (bf16[4,1,1,48,1536]{4,3,0,2,1:T(8,128)(2,1)S(1)}, bf16[4,1,1,48,1536]{4,3,0,2,1:T(8,128)(2,1)}, u32[]{:S(2)}) copy-start(bf16[4,1,1,48,1536]{4,3,0,2,1:T(8,128)(2,1)} %copy-done.15) | copy-start | bytes 1769476
  111.9 30.3 %collective-permute-start.7 = (bf16[4,2,1,48,1536]{4,3,0,2,1:T(8,128)(2,1)}, bf16[4,2,1,48,1536]{4,3,0,2,1:T(8,128)(2,1)S(1)}, u32[]{:S(2)}, u32[]{:S(2)}) collective-permute-start(bf16[4,2,1,48,1536]{4,3,0,2,1:T(8,128)(2,1)} %pad_maximum_fusion.4), channel_id=1, source_target_pairs={{0,8},{8,0},{16,24},{24,16},{1,9},{9,1},{17,25},{25,17},{2,10},{10... | collective-permute-start | bytes 3538952 | tf_op jit(solution)/shard_map/ppermute | solution.py:1172
  189.2 107.9 %all-gather.9.cloned.1.call-start = ((), (), s32[]{:S(2)}) async-start(), calls=%async_computation.5 | async-start | bytes 3538944 | tf_op jit(solution)/shard_map/all_gather | solution.py:1629
  198.7 54.2 %collective-permute-start.11 = (bf16[2304,512]{1,0:T(8,128)(2,1)}, bf16[2304,512]{1,0:T(8,128)(2,1)}, u32[]{:S(2)}, u32[]{:S(2)}) collective-permute-start(bf16[2304,512]{1,0:T(8,128)(2,1)} %get-tuple-element.136), channel_id=1, source_target_pairs={{0,8},{8,0},{16,24},{24,16},{1,9},{9,1},{17,25},{25,17},{2,10},{10... | collective-permute-start | bytes 7077896 | tf_op jit(solution)/shard_map/ppermute | solution.py:1172
  200.3 53.4 %collective-permute-start.12 = (bf16[2304,512]{1,0:T(8,128)(2,1)}, bf16[2304,512]{1,0:T(8,128)(2,1)}, u32[]{:S(2)}, u32[]{:S(2)}) collective-permute-start(bf16[2304,512]{1,0:T(8,128)(2,1)} %get-tuple-element.137), channel_id=1, source_target_pairs={{0,16},{8,24},{16,0},{24,8},{1,17},{9,25},{17,1},{25,9},{2,18},{10... | collective-permute-start | bytes 7077896 | tf_op jit(solution)/shard_map/ppermute | solution.py:1172
  239.5 8.6 %collective-permute-start.10 = (bf16[2,128,192]{2,1,0:T(8,128)(2,1)}, bf16[2,128,192]{2,1,0:T(8,128)(2,1)}, u32[]{:S(2)}, u32[]{:S(2)}) collective-permute-start(bf16[2,128,192]{2,1,0:T(8,128)(2,1)} %get-tuple-element.303), channel_id=1, source_target_pairs={{0,2},{1,3},{2,4},{3,5},{4,6},{5,7},{6,0},{7,1},{8,10},{9,11},{10,... | collective-permute-start | bytes 294920 | tf_op jit(solution)/shard_map/ppermute | solution.py:1522
  239.5 11.5 %collective-permute-start.9 = (bf16[2,128,192]{2,1,0:T(8,128)(2,1)}, bf16[2,128,192]{2,1,0:T(8,128)(2,1)}, u32[]{:S(2)}, u32[]{:S(2)}) collective-permute-start(bf16[2,128,192]{2,1,0:T(8,128)(2,1)} %get-tuple-element.304), channel_id=1, source_target_pairs={{0,4},{1,5},{2,6},{3,7},{4,0},{5,1},{6,2},{7,3},{8,12},{9,13},{10,... | collective-permute-start | bytes 294920 | tf_op jit(solution)/shard_map/ppermute | solution.py:1522
  240.0 11.0 %collective-permute-start.8 = (bf16[2,128,192]{2,1,0:T(8,128)(2,1)S(1)}, bf16[2,128,192]{2,1,0:T(8,128)(2,1)}, u32[]{:S(2)}, u32[]{:S(2)}) collective-permute-start(bf16[2,128,192]{2,1,0:T(8,128)(2,1)S(1)} %get-tuple-element.305), channel_id=1, source_target_pairs={{0,6},{1,7},{2,0},{3,1},{4,2},{5,3},{6,4},{7,5},{8,14},{9,15},{10,... | collective-permute-start | bytes 294920 | tf_op jit(solution)/shard_map/ppermute | solution.py:1522
  243.9 153.0 %reduce-scatter.5.cloned.1.call-start = ((), (), s32[]{:S(2)}) async-start(), calls=%async_computation.6 | async-start | bytes 7077888 | tf_op jit(solution)/shard_map/reduce_scatter | solution.py:1684
  259.2 27.3 %collective-permute-start.14 = (bf16[1152,512]{1,0:T(8,128)(2,1)}, bf16[1152,512]{1,0:T(8,128)(2,1)}, u32[]{:S(2)}, u32[]{:S(2)}) collective-permute-start(bf16[1152,512]{1,0:T(8,128)(2,1)} %get-tuple-element.149), channel_id=1, source_target_pairs={{0,16},{8,24},{16,0},{24,8},{1,17},{9,25},{17,1},{25,9},{2,18},{10... | collective-permute-start | bytes 3538952 | tf_op jit(solution)/shard_map/ppermute | solution.py:1172
  260.7 27.0 %collective-permute-start.15 = (bf16[1152,512]{1,0:T(8,128)(2,1)}, bf16[1152,512]{1,0:T(8,128)(2,1)}, u32[]{:S(2)}, u32[]{:S(2)}) collective-permute-start(bf16[1152,512]{1,0:T(8,128)(2,1)} %get-tuple-element.150), channel_id=1, source_target_pairs={{0,8},{8,0},{16,24},{24,16},{1,9},{9,1},{17,25},{25,17},{2,10},{10... | collective-permute-start | bytes 3538952 | tf_op jit(solution)/shard_map/ppermute | solution.py:1172
  263.2 1.8 collective-permute-start.13
  293.9 29.1 %collective-permute-start.18 = (bf16[1152,512]{1,0:T(8,128)(2,1)}, bf16[1152,512]{1,0:T(8,128)(2,1)S(1)}, u32[]{:S(2)}, u32[]{:S(2)}) collective-permute-start(bf16[1152,512]{1,0:T(8,128)(2,1)} %get-tuple-element.183.refs_0_), channel_id=1, source_target_pairs={{0,16},{8,24},{16,0},{24,8},{1,17},{9,25},{17,1},{25,9},{2,18},{10... | collective-permute-start | bytes 3538952 | tf_op jit(solution)/shard_map/ppermute | solution.py:1172
  294.4 30.4 %collective-permute-start.19 = (bf16[1152,512]{1,0:T(8,128)(2,1)}, bf16[1152,512]{1,0:T(8,128)(2,1)}, u32[]{:S(2)}, u32[]{:S(2)}) collective-permute-start(bf16[1152,512]{1,0:T(8,128)(2,1)} %get-tuple-element.185.refs_2_), channel_id=1, source_target_pairs={{0,8},{8,0},{16,24},{24,16},{1,9},{9,1},{17,25},{25,17},{2,10},{10... | collective-permute-start | bytes 3538952 | tf_op jit(solution)/shard_map/ppermute | solution.py:1172
  311.7 21.3 %collective-permute-start.16 = (bf16[2,1,48,2304]{3,2,1,0:T(8,128)(2,1)}, bf16[2,1,48,2304]{3,2,1,0:T(8,128)(2,1)S(1)}, u32[]{:S(2)}, u32[]{:S(2)}) collective-permute-start(bf16[2,1,48,2304]{3,2,1,0:T(8,128)(2,1)} %bitcast.39), channel_id=1, source_target_pairs={{0,8},{8,0},{16,24},{24,16},{1,9},{9,1},{17,25},{25,17},{2,10},{10... | collective-permute-start | bytes 1327112 | tf_op jit(solution)/shard_map/ppermute | solution.py:1172
  313.0 20.0 %collective-permute-start.17 = (bf16[1,2,48,2304]{3,2,1,0:T(8,128)(2,1)S(1)}, bf16[1,2,48,2304]{3,2,1,0:T(8,128)(2,1)S(1)}, u32[]{:S(2)}, u32[]{:S(2)}) collective-permute-start(bf16[1,2,48,2304]{3,2,1,0:T(8,128)(2,1)S(1)} %bitcast.149), channel_id=1, source_target_pairs={{0,16},{8,24},{16,0},{24,8},{1,17},{9,25},{17,1},{25,9},{2,18},{10... | collective-permute-start | bytes 1327112 | tf_op jit(solution)/shard_map/ppermute | solution.py:1172
  324.8 29.2 %collective-permute-start.22 = (bf16[576,512]{1,0:T(8,128)(2,1)}, bf16[576,512]{1,0:T(8,128)(2,1)}, u32[]{:S(2)}, u32[]{:S(2)}) collective-permute-start(bf16[576,512]{1,0:T(8,128)(2,1)} %get-tuple-element.287), channel_id=1, source_target_pairs={{0,8},{8,0},{16,24},{24,16},{1,9},{9,1},{17,25},{25,17},{2,10},{10... | collective-permute-start | bytes 1769480 | tf_op jit(solution)/shard_map/ppermute | solution.py:1172
  328.5 25.6 %collective-permute-start.23 = (bf16[576,512]{1,0:T(8,128)(2,1)}, bf16[576,512]{1,0:T(8,128)(2,1)}, u32[]{:S(2)}, u32[]{:S(2)}) collective-permute-start(bf16[576,512]{1,0:T(8,128)(2,1)} %get-tuple-element.283), channel_id=1, source_target_pairs={{0,16},{8,24},{16,0},{24,8},{1,17},{9,25},{17,1},{25,9},{2,18},{10... | collective-permute-start | bytes 1769480 | tf_op jit(solution)/shard_map/ppermute | solution.py:1172
  335.1 11.7 %collective-permute-start.20 = (bf16[1,1,48,2304]{3,2,1,0:T(8,128)(2,1)S(1)}, bf16[1,1,48,2304]{3,2,1,0:T(8,128)(2,1)S(1)}, u32[]{:S(2)}, u32[]{:S(2)}) collective-permute-start(bf16[1,1,48,2304]{3,2,1,0:T(8,128)(2,1)S(1)} %dynamic-slice_convert_fusion.1), channel_id=1, source_target_pairs={{0,16},{8,24},{16,0},{24,8},{1,17},{9,25},{17,1},{25,9},{2,18},{10... | collective-permute-start | bytes 663560 | tf_op jit(solution)/shard_map/ppermute | solution.py:1172
  336.6 13.8 %collective-permute-start.21 = (bf16[1,1,48,2304]{3,2,1,0:T(8,128)(2,1)S(1)}, bf16[1,1,48,2304]{3,2,1,0:T(8,128)(2,1)S(1)}, u32[]{:S(2)}, u32[]{:S(2)}) collective-permute-start(bf16[1,1,48,2304]{3,2,1,0:T(8,128)(2,1)S(1)} %dynamic-slice_convert_fusion), channel_id=1, source_target_pairs={{0,8},{8,0},{16,24},{24,16},{1,9},{9,1},{17,25},{25,17},{2,10},{10... | collective-permute-start | bytes 663560 | tf_op jit(solution)/shard_map/ppermute | solution.py:1172
  337.5 22.7 %collective-permute-start.27 = (bf16[576,512]{1,0:T(8,128)(2,1)}, bf16[576,512]{1,0:T(8,128)(2,1)}, u32[]{:S(2)}, u32[]{:S(2)}) collective-permute-start(bf16[576,512]{1,0:T(8,128)(2,1)} %get-tuple-element.202), channel_id=1, source_target_pairs={{0,8},{8,0},{16,24},{24,16},{1,9},{9,1},{17,25},{25,17},{2,10},{10... | collective-permute-start | bytes 1769480 | tf_op jit(solution)/shard_map/ppermute | solution.py:1172
  346.8 13.5 %collective-permute-start.28 = (bf16[576,512]{1,0:T(8,128)(2,1)}, bf16[576,512]{1,0:T(8,128)(2,1)}, u32[]{:S(2)}, u32[]{:S(2)}) collective-permute-start(bf16[576,512]{1,0:T(8,128)(2,1)} %get-tuple-element.203), channel_id=1, source_target_pairs={{0,16},{8,24},{16,0},{24,8},{1,17},{9,25},{17,1},{25,9},{2,18},{10... | collective-permute-start | bytes 1769480 | tf_op jit(solution)/shard_map/ppermute | solution.py:1172
  354.0 8.8 %collective-permute-start.24 = (bf16[2,48,384]{2,1,0:T(8,128)(2,1)}, bf16[2,48,384]{2,1,0:T(8,128)(2,1)S(1)}, u32[]{:S(2)}, u32[]{:S(2)}) collective-permute-start(bf16[2,48,384]{2,1,0:T(8,128)(2,1)} %get-tuple-element.197), channel_id=1, source_target_pairs={{0,6},{1,7},{2,0},{3,1},{4,2},{5,3},{6,4},{7,5},{8,14},{9,15},{10,... | collective-permute-start | bytes 221192 | tf_op jit(solution)/shard_map/ppermute | solution.py:1522
  358.1 10.3 %collective-permute-start.25 = (bf16[2,48,384]{2,1,0:T(8,128)(2,1)}, bf16[2,48,384]{2,1,0:T(8,128)(2,1)S(1)}, u32[]{:S(2)}, u32[]{:S(2)}) collective-permute-start(bf16[2,48,384]{2,1,0:T(8,128)(2,1)} %get-tuple-element.198), channel_id=1, source_target_pairs={{0,4},{1,5},{2,6},{3,7},{4,0},{5,1},{6,2},{7,3},{8,12},{9,13},{10,... | collective-permute-start | bytes 221192 | tf_op jit(solution)/shard_map/ppermute | solution.py:1522
  358.4 10.1 %collective-permute-start.26 = (bf16[2,48,384]{2,1,0:T(8,128)(2,1)}, bf16[2,48,384]{2,1,0:T(8,128)(2,1)S(1)}, u32[]{:S(2)}, u32[]{:S(2)}) collective-permute-start(bf16[2,48,384]{2,1,0:T(8,128)(2,1)} %get-tuple-element.199), channel_id=1, source_target_pairs={{0,2},{1,3},{2,4},{3,5},{4,6},{5,7},{6,0},{7,1},{8,10},{9,11},{10,... | collective-permute-start | bytes 221192 | tf_op jit(solution)/shard_map/ppermute | solution.py:1522
  360.2 24.5 %collective-permute-start.31 = (bf16[576,512]{1,0:T(8,128)(2,1)S(1)}, bf16[576,512]{1,0:T(8,128)(2,1)S(1)}, u32[]{:S(2)}, u32[]{:S(2)}) collective-permute-start(bf16[576,512]{1,0:T(8,128)(2,1)S(1)} %copy-done.26), channel_id=1, source_target_pairs={{0,8},{8,0},{16,24},{24,16},{1,9},{9,1},{17,25},{25,17},{2,10},{10... | collective-permute-start | bytes 1769480 | tf_op jit(solution)/shard_map/ppermute | solution.py:1172
  361.1 23.7 %collective-permute-start.32 = (bf16[576,512]{1,0:T(8,128)(2,1)S(1)}, bf16[576,512]{1,0:T(8,128)(2,1)S(1)}, u32[]{:S(2)}, u32[]{:S(2)}) collective-permute-start(bf16[576,512]{1,0:T(8,128)(2,1)S(1)} %copy-done.27), channel_id=1, source_target_pairs={{0,16},{8,24},{16,0},{24,8},{1,17},{9,25},{17,1},{25,9},{2,18},{10... | collective-permute-start | bytes 1769480 | tf_op jit(solution)/shard_map/ppermute | solution.py:1172
  372.1 1.6 collective-permute-start.29
  377.1 11.3 %copy-start.29 = (bf16[48,2304]{1,0:T(8,128)(2,1)S(1)}, bf16[48,2304]{1,0:T(8,128)(2,1)}, u32[]{:S(2)}) copy-start(bf16[48,2304]{1,0:T(8,128)(2,1)} %get-tuple-element.210) | copy-start | bytes 663556
  377.1 7.7 %collective-permute-start.30 = (bf16[1,1,48,2304]{3,2,1,0:T(8,128)(2,1)}, bf16[1,1,48,2304]{3,2,1,0:T(8,128)(2,1)S(1)}, u32[]{:S(2)}, u32[]{:S(2)}) collective-permute-start(bf16[1,1,48,2304]{3,2,1,0:T(8,128)(2,1)} %bitcast.143), channel_id=1, source_target_pairs={{0,16},{8,24},{16,0},{24,8},{1,17},{9,25},{17,1},{25,9},{2,18},{10... | collective-permute-start | bytes 663560 | tf_op jit(solution)/shard_map/ppermute | solution.py:1172
  379.0 9.4 %collective-permute-start.34 = (bf16[1,1,48,2304]{3,2,1,0:T(8,128)(2,1)}, bf16[1,1,48,2304]{3,2,1,0:T(8,128)(2,1)S(1)}, u32[]{:S(2)}, u32[]{:S(2)}) collective-permute-start(bf16[1,1,48,2304]{3,2,1,0:T(8,128)(2,1)} %bitcast.142), channel_id=1, source_target_pairs={{0,8},{8,0},{16,24},{24,16},{1,9},{9,1},{17,25},{25,17},{2,10},{10... | collective-permute-start | bytes 663560 | tf_op jit(solution)/shard_map/ppermute | solution.py:1172
  386.9 13.4 %collective-permute-start.33 = (bf16[2,1,48,2304]{3,2,1,0:T(8,128)(2,1)}, bf16[2,1,48,2304]{3,2,1,0:T(8,128)(2,1)}, u32[]{:S(2)}, u32[]{:S(2)}) collective-permute-start(bf16[2,1,48,2304]{3,2,1,0:T(8,128)(2,1)} %pad_maximum_fusion.10), channel_id=1, source_target_pairs={{0,8},{8,0},{16,24},{24,16},{1,9},{9,1},{17,25},{25,17},{2,10},{10... | collective-permute-start | bytes 1327112 | tf_op jit(solution)/shard_map/ppermute | solution.py:1172
  388.5 13.3 %collective-permute-start.35 = (bf16[1,2,48,2304]{3,2,1,0:T(8,128)(2,1)S(1)}, bf16[1,2,48,2304]{3,2,1,0:T(8,128)(2,1)}, u32[]{:S(2)}, u32[]{:S(2)}) collective-permute-start(bf16[1,2,48,2304]{3,2,1,0:T(8,128)(2,1)S(1)} %pad_maximum_fusion.11), channel_id=1, source_target_pairs={{0,16},{8,24},{16,0},{24,8},{1,17},{9,25},{17,1},{25,9},{2,18},{10... | collective-permute-start | bytes 1327112 | tf_op jit(solution)/shard_map/ppermute | solution.py:1172
  389.9 21.3 %collective-permute-start.36 = (bf16[576,512]{1,0:T(8,128)(2,1)S(1)}, bf16[576,512]{1,0:T(8,128)(2,1)S(1)}, u32[]{:S(2)}, u32[]{:S(2)}) collective-permute-start(bf16[576,512]{1,0:T(8,128)(2,1)S(1)} %copy-done.24), channel_id=1, source_target_pairs={{0,8},{8,0},{16,24},{24,16},{1,9},{9,1},{17,25},{25,17},{2,10},{10... | collective-permute-start | bytes 1769480 | tf_op jit(solution)/shard_map/ppermute | solution.py:1172
  390.3 22.2 %collective-permute-start.37 = (bf16[576,512]{1,0:T(8,128)(2,1)S(1)}, bf16[576,512]{1,0:T(8,128)(2,1)}, u32[]{:S(2)}, u32[]{:S(2)}) collective-permute-start(bf16[576,512]{1,0:T(8,128)(2,1)S(1)} %copy-done.25), channel_id=1, source_target_pairs={{0,16},{8,24},{16,0},{24,8},{1,17},{9,25},{17,1},{25,9},{2,18},{10... | collective-permute-start | bytes 1769480 | tf_op jit(solution)/shard_map/ppermute | solution.py:1172
  (37 other events, 122.1 us)
Sparse Core Ops, SparseCore 0:
  11.5 59.9 all-gather.10
  73.1 37.1 all-gather.6
  112.5 37.1 all-gather.12
  189.3 41.5 reduce-scatter.2
  244.0 37.8 all-gather.8
  311.9 76.0 reduce-scatter.4

commit v13 on v11

--- a/solution.py
+++ b/solution.py
@@ -1205,7 +1205,7 @@
     last = chains[0].stage == len(chains[0].order) - 1
     keeps = jnp.stack([has(bit) for bit in order]).astype(jnp.int32)
     rows, hidden = chains[0].kept.shape
-    count = 4
+    count = 2
     part = rows // 2 // count
     operands, specs = [], []
     for c, chain in enumerate(chains):
@@ -1248,7 +1248,7 @@
 def total_chains(chains, *others):
     keeps = jnp.stack([has(chain.order[-1]) for chain in chains]).astype(jnp.int32)
     rows, hidden = chains[0].kept.shape
-    count = 4
+    count = 2
     part = rows // 2 // count
     block = pl.BlockSpec((part, hidden), lambda i, k: (i, 0))
     operands, specs = [], []

time: 426 us -> 425 us (level)
  transfers between devices with their start and end apart: 44 -> 44, of which waited for: 24 -> 24; matrix products, arithmetic and copies ran while one was open for 11% -> 11% of each run, Pallas kernels for 27% -> 28%
where the time goes in v13:
time: 425 us; the launch traced here: 423 us
  Pallas kernels  162 us (38%)
  waiting for transfers between devices  120 us (28%)
  starting transfers between devices  44.3 us (10%)
  other arithmetic  35.9 us (8%)
  blocking collectives  24.5 us (6%)
  local copies, waits for them, and re-layouts  22.5 us (5%)
  between operations  14.7 us (3%)
    ppermute x30, waiting for transfers between devices, swap(): return lax.ppermute(value, 'rep', [(i, i ^ bit) for i in range(size)])  60.3 us
    pallas_call x1, Pallas kernels, layer_rows(): pl.pallas_call(layer_kernel, out_shape=(shaped((tokens, features), low),...  39.4 us
    ppermute x30, starting transfers between devices, swap(): return lax.ppermute(value, 'rep', [(i, i ^ bit) for i in range(size)])  35.2 us
    all_to_all x1, blocking collectives, per_device(): lax.all_to_all(head_columns, 'ctx', split_axis=0, concat_axis=0, tiled=True)  24.5 us
    pallas_call x2, Pallas kernels, expert_products(): pl.pallas_call(lambda *refs: product_kernel(e, *refs), name='expert_produ...  18.9 us
    pallas_call x1, Pallas kernels, attend(): pl.pallas_call(attend_kernel, out_shape=(shaped((tokens, features), jnp.b...  17.4 us
    pallas_call x1, Pallas kernels, attend_back(): pl.pallas_call(attend_back_kernel, out_shape=(jax.ShapeDtypeStruct((token...  16.5 us
    all_gather x1, waiting for transfers between devices, per_device(): gathered = lax.all_gather(rows, 'ctx', axis=0)  16.5 us
  transfers between devices with their start and end apart: 44, of which 24 were waited for; matrix products, arithmetic and copies ran while one was open for 11% of the time, Pallas kernels for 28%

profile of v13, /device:TPU:0, one launch (start us, length us, event | category | flops | bytes accessed | tf_op | source)
XLA Modules:
  0.0 423.4 jit_solution(5536971852903052470)
XLA Ops:
  9.5 1.9 fusion.12
  15.3 24.5 %all_to_all.5 = bf16[8,48,384]{2,1,0:T(8,128)(2,1)S(1)} all-to-all(bf16[8,48,384]{2,1,0:T(8,128)(2,1)S(1)} %copy.57), channel_id=1, replica_groups=mesh['rep'=4,'ctx'=8] {'ctx'}, dimensions={0} | all-to-all | bytes 589824 | tf_op jit(solution)/shard_map/all_to_all | solution.py:1520
  42.9 2.8 collective-permute-done
  47.8 1.6 collective-permute-start.1
  49.4 5.6 %collective-permute-done.3 = bf16[4,2,1,48,384]{4,3,0,2,1:T(8,128)(2,1)S(1)} collective-permute-done((bf16[4,2,1,48,384]{4,3,0,2,1:T(8,128)(2,1)S(1)}, bf16[4,2,1,48,384]{4,3,0,2,1:T(8,128)(2,1)S(1)}, u32[]{:S(2)}, u32[]{:S(2)}) %collective-permute-start.3) | collective-permute-done | bytes 294944 | tf_op jit(solution)/shard_map/ppermute | solution.py:1146
  55.0 16.5 %all-gather.11.cloned.1.call-done = bf16[1408,1664]{1,0:T(8,128)(2,1)} async-done(((bf16[176,1664]{1,0:T(8,128)(2,1)}), bf16[1408,1664]{1,0:T(8,128)(2,1)}) %all-gather.11.cloned.1.call-update) | async-done | bytes 4685840 | tf_op jit(solution)/shard_map/all_gather | solution.py:1491
  72.8 1.6 collective-permute-start.5
  77.5 17.4 %shard_map.238 = (bf16[1024,1536]{1,0:T(8,128)(2,1)}, bf16[1024,192]{1,0:T(8,128)(2,1)S(1)}, bf16[1024,64]{1,0:T(8,128)(2,1)S(1)}, bf16[1024,64]{1,0:T(8,128)(2,...) custom-call(bf16[8,176,1664]{2,1,0:T(8,128)(2,1)} %bitcast.130, ...), custom_call_target="tpu_custom_call" | custom-call | bytes 1024 | tf_op jit(solution)/shard_map/pallas_call | solution.py:194
  94.9 2.2 broadcast_select_fusion.13
  100.0 10.3 %all-gather.7.cloned.1.call-done.cotangent_ref = bf16[1024,1536]{1,0:T(8,128)(2,1)} async-done(((bf16[128,1536]{1,0:T(8,128)(2,1)}), bf16[1024,1536]{1,0:T(8,128)(2,1)}) %all-gather.7.cloned.1.call-update) | async-done | bytes 3145744 | tf_op jit(solution)/shard_map/all_gather | solution.py:1492
  115.6 23.3 %collective-permute-done.6 = bf16[4,1,2,48,1536]{4,3,0,2,1:T(8,128)(2,1)} collective-permute-done((bf16[4,1,2,48,1536]{4,3,0,2,1:T(8,128)(2,1)}, bf16[4,1,2,48,1536]{4,3,0,2,1:T(8,128)(2,1)}, u32[]{:S(2)}, u32[]{:S(2)}) %collective-permute-start.6) | collective-permute-done | bytes 1179680 | tf_op jit(solution)/shard_map/ppermute | solution.py:1146
  140.6 1.6 copy.60
  144.2 5.5 %all-gather.13.cloned.1.call-done = bf16[4096,384]{1,0:T(8,128)(2,1)} async-done(((bf16[512,384]{1,0:T(8,128)(2,1)}), bf16[4096,384]{1,0:T(8,128)(2,1)}) %all-gather.13.cloned.1.call-update) | async-done | bytes 3145744 | tf_op jit(solution)/shard_map/all_gather | solution.py:1542
  149.7 39.4 %shard_map.239 = (bf16[1024,1536]{1,0:T(8,128)(2,1)}, bf16[2,1024,512]{2,1,0:T(8,128)(2,1)}, bf16[2,1024,512]{2,1,0:T(8,128)(2,1)}, bf16[2,1024,512]{2,1,0:T(8,1...) custom-call(s32[4]{0:T(128)} %pad_add_fusion.place_ref.refs_0_, ...), custom_call_target="tpu_custom_call" | custom-call | flops 19327352832 | bytes 40894464 | tf_op jit(solution)/shard_map/pallas_call | solution.py:513
  189.4 9.3 %expert_products.2 = (bf16[2304,512]{1,0:T(8,128)(2,1)}, bf16[2304,512]{1,0:T(8,128)(2,1)}) custom-call(bf16[1024,1536]{1,0:T(8,128)(2,1)} %get-tuple-element.137.refs_0_, bf16[2,1024,512]{2,1,0:T(8,128)(2,1)} %get-tuple-element.132.refs_1_, bf16[2,1024,512]{2,1,0:T(8,128)(2,1)} %get-tuple-element.133.refs_2_, ...), custom_call_target="tpu_custom_call" | custom-call | bytes 1024 | tf_op jit(solution)/shard_map/expert_products/pallas_call | solution.py:668
  201.8 9.6 %expert_products.3 = (f32[2304,512]{1,0:T(8,128)}, f32[2304,512]{1,0:T(8,128)}) custom-call(bf16[1024,1536]{1,0:T(8,128)(2,1)} %get-tuple-element.137.refs_0_, bf16[2,1024,512]{2,1,0:T(8,128)(2,1)} %get-tuple-element.132.refs_1_, bf16[2,1024,512]{2,1,0:T(8,128)(2,1)} %get-tuple-element.133.refs_2_, ...), custom_call_target="tpu_custom_call" | custom-call | bytes 1024 | tf_op jit(solution)/shard_map/expert_products/pallas_call | solution.py:668
  211.4 8.9 %shard_map.240.refs_9_ = bf16[1024,1536]{1,0:T(8,128)(2,1)} custom-call(s32[4]{0:T(128)S(1)} %copy-done.7, bf16[2,1024,512]{2,1,0:T(8,128)(2,1)} %get-tuple-element.141.refs_3_.scaled_ref, bf16[2,512,1536]{2,1,0:T(8,128)(2,1)} %down_weight_ref.1), custom_call_target="tpu_custom_call" | custom-call | bytes 1024 | tf_op jit(solution)/shard_map/pallas_call | solution.py:705
  220.2 10.6 %reduce-scatter.3.cloned.1.call-done.sum_ref = bf16[128,1664]{1,0:T(8,128)(2,1)} async-done(((bf16[1024,1664]{1,0:T(8,128)(2,1)}), bf16[128,1664]{1,0:T(8,128)(2,1)}) %reduce-scatter.3.cloned.1.call-update) | async-done | bytes 426000 | tf_op jit(solution)/shard_map/reduce_scatter | solution.py:1582
  230.9 6.8 %shard_map.241 = (f32[128,1536]{1,0:T(8,128)}, bf16[128,1536]{1,0:T(8,128)(2,1)}, bf16[8,128,192]{2,1,0:T(8,128)(2,1)}, bf16[128,16]{1,0:T(8,128)(2,1)}, f32[1,1536]{1,0:T(1,128)}) custom-call(s32[4]{0:T(128)} %pad_add_fusion.place_ref.refs_0_, bf16[128,1664]{1,0:T(8,128)(2,1)} %reduce-scatter.3.cloned.1.call-done.sum_ref, ...), custom_call_target="tpu_custom_call" | custom-call | bytes 128 | tf_op jit(solution)/shard_map/pallas_call | solution.py:776
  237.6 1.8 dynamic-slice_bitcast_fusion.5
  240.0 3.3 collective-permute-start.8
  244.2 3.8 collective-permute-done.10
  248.0 2.9 collective-permute-done.9
  251.0 1.9 pad_maximum_fusion.9
  253.7 4.9 %shard_map.242 = (bf16[1152,512]{1,0:T(8,128)(2,1)}, bf16[1152,512]{1,0:T(8,128)(2,1)}) custom-call(s32[2]{0:T(128)} %add_convert_fusion.keeps_ref, f32[2304,512]{1,0:T(8,128)} %get-tuple-element.139.refs_0_, bf16[2304,512]{1,0:T(8,128)(2,1)} %collective-permute-done.11.refs_1_, f32[2304,512]{1,0:T(8,128)} %get-tuple-element.140.refs_2_.refs_3_, ...), custom_call_target="tpu_custom_call" | custom-call | flops 70778880000 | bytes 14155776 | tf_op jit(solution)/shard_map/pallas_call | solution.py:1220
  260.8 1.8 select_bitcast_fusion
  262.5 1.7 collective-permute-done.13
  265.7 16.5 %shard_map.243 = (bf16[1024,192]{1,0:T(8,128)(2,1)S(1)}, bf16[1024,128]{1,0:T(8,128)(2,1)S(1)}) custom-call(bf16[1024,192]{1,0:T(8,128)(2,1)S(1)} %get-tuple-element.125.query_ref, bf16[1024,192]{1,0:T(8,128)(2,1)S(1)} %bitcast.128, f32[3,1024,1]{2,1,0:T(8,128)S(1)} %copy-done.3, f32[1024,64]{1,0:T(8,128)S(1)} %get-tuple-element.151.cosine_ref.key_cosine_ref, ...), custom_call_target="tpu_custom_call" | custom-call | bytes 1024 | tf_op jit(solution)/shard_map/pallas_call | solution.py:323
  283.7 2.2 collective-permute-done.14.refs_2_
  287.2 6.0 %shard_map.244 = (bf16[1152,512]{1,0:T(8,128)(2,1)}, bf16[1152,512]{1,0:T(8,128)(2,1)}) custom-call(s32[2]{0:T(128)} %add_convert_fusion.keeps_ref, f32[2304,512]{1,0:T(8,128)} %get-tuple-element.139.refs_0_, bf16[2304,512]{1,0:T(8,128)(2,1)} %collective-permute-done.11.refs_1_, bf16[1152,512]{1,0:T(8,128)(2,1)} %collective-permute-done.14.refs_2_, ...), custom_call_target="tpu_custom_call" | custom-call | bytes 2304 | tf_op jit(solution)/shard_map/pallas_call | solution.py:1259
  296.2 14.6 %close.1 = (bf16[1024,3072]{1,0:T(8,128)(2,1)}, f32[96,2304]{1,0:T(8,128)}, f32[96,2304]{1,0:T(8,128)}, bf16[96,2304]{1,0:T(8,128)(2,1)}, bf16[96,2304]{1,0:T(8,128)(2,1)}) custom-call(s32[4]{0:T(128)} %pad_add_fusion.place_ref.refs_0_, bf16[1024,192]{1,0:T(8,128)(2,1)} %copy-done.5, bf16[1024,128]{1,0:T(8,128)(2,1)} %copy-done.6, ...), custom_call_target="tpu_custom_call" | custom-call | bytes 1024 | tf_op jit(solution)/shard_map/close/pallas_call | solution.py:905
  313.7 8.6 %collective-permute-done.18.refs_1_ = bf16[1152,512]{1,0:T(8,128)(2,1)S(1)} collective-permute-done((bf16[1152,512]{1,0:T(8,128)(2,1)}, bf16[1152,512]{1,0:T(8,128)(2,1)S(1)}, u32[]{:S(2)}, u32[]{:S(2)}) %collective-permute-start.18) | collective-permute-done | bytes 1179680 | tf_op jit(solution)/shard_map/ppermute | solution.py:1146
  324.8 2.8 broadcast_select_fusion.4
  328.1 4.1 collective-permute-done.16
  337.9 7.1 %own_outputs.1 = (f32[2,1536,512]{2,1,0:T(8,128)}, f32[2,1536,512]{2,1,0:T(8,128)}, f32[2,512,1536]{2,1,0:T(8,128)}) custom-call(s32[4]{0:T(128)} %pad_add_fusion.1.flags_ref, bf16[1152,512]{1,0:T(8,128)(2,1)} %get-tuple-element.179.refs_0_, bf16[1152,512]{1,0:T(8,128)(2,1)} %copy-done.19, bf16[1152,512]{1,0:T(8,128)(2,1)} %get-tuple-element.181.refs_2_, ...), custom_call_target="tpu_custom_call" | custom-call | bytes 1152 | tf_op jit(solution)/shard_map/own_outputs/pallas_call | solution.py:1049
  346.7 3.0 collective-permute-done.21
  350.3 3.0 scalar_call.3
  353.3 3.9 collective-permute-start.24
  357.9 1.6 collective-permute-done.27.refs_1_
  362.1 5.4 %collective-permute-done.25.refs_2_ = bf16[2,48,384]{2,1,0:T(8,128)(2,1)S(1)} collective-permute-done((bf16[2,48,384]{2,1,0:T(8,128)(2,1)}, bf16[2,48,384]{2,1,0:T(8,128)(2,1)S(1)}, u32[]{:S(2)}, u32[]{:S(2)}) %collective-permute-start.25) | collective-permute-done | bytes 73760 | tf_op jit(solution)/shard_map/ppermute | solution.py:1495
  368.7 2.4 scalar_call.4
  373.4 2.5 scalar_call.5
  377.2 1.6 collective-permute-start.34
  378.9 4.7 %collective-permute-done.30 = bf16[1,1,48,2304]{3,2,1,0:T(8,128)(2,1)S(1)} collective-permute-done((bf16[1,1,48,2304]{3,2,1,0:T(8,128)(2,1)}, bf16[1,1,48,2304]{3,2,1,0:T(8,128)(2,1)S(1)}, u32[]{:S(2)}, u32[]{:S(2)}) %collective-permute-start.30) | collective-permute-done | bytes 221216 | tf_op jit(solution)/shard_map/ppermute | solution.py:1146
  390.6 5.8 %into_outputs.1 = (f32[2,1536,512]{2,1,0:T(8,128)}, f32[2,1536,512]{2,1,0:T(8,128)}) custom-call(s32[4]{0:T(128)} %pad_add_fusion.1.flags_ref, f32[2,1536,512]{2,1,0:T(8,128)} %get-tuple-element.183.gate_any, f32[2,1536,512]{2,1,0:T(8,128)} %get-tuple-element.184.up_any, ...), custom_call_target="tpu_custom_call", output_to_operand_aliasing={{0}: (1, {}), {1}: (2, {})} | custom-call | bytes 1536 | tf_op jit(solution)/shard_map/into_outputs/pallas_call | solution.py:1090
  405.1 3.5 head_outputs.1
  408.6 1.6 copy.64
  412.4 4.2 down_outputs.1
  (237 shorter events, 82.0 us)
Async XLA Ops:
  7.2 64.3 %all-gather.11.cloned.1.call-start = ((), (), s32[]{:S(2)}) async-start(), calls=%async_computation.7 | async-start | bytes 5271552 | tf_op jit(solution)/shard_map/all_gather | solution.py:1491
  11.4 98.9 %all-gather.7.cloned.1.call-start = ((), (), s32[]{:S(2)}) async-start(), calls=%async_computation.3 | async-start | bytes 3538944 | tf_op jit(solution)/shard_map/all_gather | solution.py:1492
  12.1 137.6 %all-gather.13.cloned.1.call-start = ((), (), s32[]{:S(2)}) async-start(), calls=%async_computation.8 | async-start | bytes 3538944 | tf_op jit(solution)/shard_map/all_gather | solution.py:1542
  39.8 5.9 %collective-permute-start = (bf16[4,1,1,48,384]{4,3,0,2,1:T(8,128)(2,1)S(1)}, bf16[4,1,1,48,384]{4,3,0,2,1:T(8,128)(2,1)S(1)}, u32[]{:S(2)}, u32[]{:S(2)}) collective-permute-start(bf16[4,1,1,48,384]{4,3,0,2,1:T(8,128)(2,1)S(1)} %get-tuple-element.312), channel_id=1, source_target_pairs={{0,8},{8,0},{16,24},{24,16},{1,9},{9,1},{17,25},{25,17},{2,10},{10... | collective-permute-start | bytes 442376 | tf_op jit(solution)/shard_map/ppermute | solution.py:1146
  41.4 5.5 %collective-permute-start.2 = (bf16[4,1,1,48,384]{4,3,0,2,1:T(8,128)(2,1)S(1)}, bf16[4,1,1,48,384]{4,3,0,2,1:T(8,128)(2,1)S(1)}, u32[]{:S(2)}, u32[]{:S(2)}) collective-permute-start(bf16[4,1,1,48,384]{4,3,0,2,1:T(8,128)(2,1)S(1)} %get-tuple-element.313), channel_id=1, source_target_pairs={{0,16},{8,24},{16,0},{24,8},{1,17},{9,25},{17,1},{25,9},{2,18},{10... | collective-permute-start | bytes 442376 | tf_op jit(solution)/shard_map/ppermute | solution.py:1146
  47.0 8.0 %collective-permute-start.3 = (bf16[4,2,1,48,384]{4,3,0,2,1:T(8,128)(2,1)S(1)}, bf16[4,2,1,48,384]{4,3,0,2,1:T(8,128)(2,1)S(1)}, u32[]{:S(2)}, u32[]{:S(2)}) collective-permute-start(bf16[4,2,1,48,384]{4,3,0,2,1:T(8,128)(2,1)S(1)} %pad_maximum_fusion.13), channel_id=1, source_target_pairs={{0,8},{8,0},{16,24},{24,16},{1,9},{9,1},{17,25},{25,17},{2,10},{10... | collective-permute-start | bytes 884744 | tf_op jit(solution)/shard_map/ppermute | solution.py:1146
  47.8 28.3 %collective-permute-start.1 = (bf16[4,1,2,48,384]{4,3,0,2,1:T(8,128)(2,1)S(1)}, bf16[4,1,2,48,384]{4,3,0,2,1:T(8,128)(2,1)S(1)}, u32[]{:S(2)}, u32[]{:S(2)}) collective-permute-start(bf16[4,1,2,48,384]{4,3,0,2,1:T(8,128)(2,1)S(1)} %pad_maximum_fusion.12), channel_id=1, source_target_pairs={{0,16},{8,24},{16,0},{24,8},{1,17},{9,25},{17,1},{25,9},{2,18},{10... | collective-permute-start | bytes 884744 | tf_op jit(solution)/shard_map/ppermute | solution.py:1146
  72.8 22.1 %collective-permute-start.5 = (bf16[4,1,1,48,1536]{4,3,0,2,1:T(8,128)(2,1)S(1)}, bf16[4,1,1,48,1536]{4,3,0,2,1:T(8,128)(2,1)S(1)}, u32[]{:S(2)}, u32[]{:S(2)}) collective-permute-start(bf16[4,1,1,48,1536]{4,3,0,2,1:T(8,128)(2,1)S(1)} %get-tuple-element.274), channel_id=1, source_target_pairs={{0,16},{8,24},{16,0},{24,8},{1,17},{9,25},{17,1},{25,9},{2,18},{10... | collective-permute-start | bytes 1769480 | tf_op jit(solution)/shard_map/ppermute | solution.py:1146
  74.4 20.5 %collective-permute-start.4 = (bf16[4,1,1,48,1536]{4,3,0,2,1:T(8,128)(2,1)S(1)}, bf16[4,1,1,48,1536]{4,3,0,2,1:T(8,128)(2,1)S(1)}, u32[]{:S(2)}, u32[]{:S(2)}) collective-permute-start(bf16[4,1,1,48,1536]{4,3,0,2,1:T(8,128)(2,1)S(1)} %get-tuple-element.275), channel_id=1, source_target_pairs={{0,8},{8,0},{16,24},{24,16},{1,9},{9,1},{17,25},{25,17},{2,10},{10... | collective-permute-start | bytes 1769480 | tf_op jit(solution)/shard_map/ppermute | solution.py:1146
  110.3 120.5 %reduce-scatter.3.cloned.1.call-start = ((), (), s32[]{:S(2)}) async-start(), calls=%async_computation.4 | async-start | bytes 3833856 | tf_op jit(solution)/shard_map/reduce_scatter | solution.py:1582
  110.4 28.5 %collective-permute-start.6 = (bf16[4,1,2,48,1536]{4,3,0,2,1:T(8,128)(2,1)}, bf16[4,1,2,48,1536]{4,3,0,2,1:T(8,128)(2,1)}, u32[]{:S(2)}, u32[]{:S(2)}) collective-permute-start(bf16[4,1,2,48,1536]{4,3,0,2,1:T(8,128)(2,1)} %pad_maximum_fusion.3), channel_id=1, source_target_pairs={{0,16},{8,24},{16,0},{24,8},{1,17},{9,25},{17,1},{25,9},{2,18},{10... | collective-permute-start | bytes 3538952 | tf_op jit(solution)/shard_map/ppermute | solution.py:1146
  111.9 26.9 %copy-start.14 = (bf16[4,1,1,48,1536]{4,3,0,2,1:T(8,128)(2,1)S(1)}, bf16[4,1,1,48,1536]{4,3,0,2,1:T(8,128)(2,1)}, u32[]{:S(2)}) copy-start(bf16[4,1,1,48,1536]{4,3,0,2,1:T(8,128)(2,1)} %copy-done.13) | copy-start | bytes 1769476
  111.9 26.9 %copy-start.16 = (bf16[4,1,1,48,1536]{4,3,0,2,1:T(8,128)(2,1)S(1)}, bf16[4,1,1,48,1536]{4,3,0,2,1:T(8,128)(2,1)}, u32[]{:S(2)}) copy-start(bf16[4,1,1,48,1536]{4,3,0,2,1:T(8,128)(2,1)} %copy-done.15) | copy-start | bytes 1769476
  111.9 30.3 %collective-permute-start.7 = (bf16[4,2,1,48,1536]{4,3,0,2,1:T(8,128)(2,1)}, bf16[4,2,1,48,1536]{4,3,0,2,1:T(8,128)(2,1)S(1)}, u32[]{:S(2)}, u32[]{:S(2)}) collective-permute-start(bf16[4,2,1,48,1536]{4,3,0,2,1:T(8,128)(2,1)} %pad_maximum_fusion.4), channel_id=1, source_target_pairs={{0,8},{8,0},{16,24},{24,16},{1,9},{9,1},{17,25},{25,17},{2,10},{10... | collective-permute-start | bytes 3538952 | tf_op jit(solution)/shard_map/ppermute | solution.py:1146
  189.2 107.0 %all-gather.9.cloned.1.call-start = ((), (), s32[]{:S(2)}) async-start(), calls=%async_computation.5 | async-start | bytes 3538944 | tf_op jit(solution)/shard_map/all_gather | solution.py:1602
  198.8 54.2 %collective-permute-start.11 = (bf16[2304,512]{1,0:T(8,128)(2,1)}, bf16[2304,512]{1,0:T(8,128)(2,1)}, u32[]{:S(2)}, u32[]{:S(2)}) collective-permute-start(bf16[2304,512]{1,0:T(8,128)(2,1)} %get-tuple-element.135), channel_id=1, source_target_pairs={{0,8},{8,0},{16,24},{24,16},{1,9},{9,1},{17,25},{25,17},{2,10},{10... | collective-permute-start | bytes 7077896 | tf_op jit(solution)/shard_map/ppermute | solution.py:1146
  200.3 53.4 %collective-permute-start.12 = (bf16[2304,512]{1,0:T(8,128)(2,1)}, bf16[2304,512]{1,0:T(8,128)(2,1)}, u32[]{:S(2)}, u32[]{:S(2)}) collective-permute-start(bf16[2304,512]{1,0:T(8,128)(2,1)} %get-tuple-element.136), channel_id=1, source_target_pairs={{0,16},{8,24},{16,0},{24,8},{1,17},{9,25},{17,1},{25,9},{2,18},{10... | collective-permute-start | bytes 7077896 | tf_op jit(solution)/shard_map/ppermute | solution.py:1146
  239.5 8.6 %collective-permute-start.10 = (bf16[2,128,192]{2,1,0:T(8,128)(2,1)}, bf16[2,128,192]{2,1,0:T(8,128)(2,1)}, u32[]{:S(2)}, u32[]{:S(2)}) collective-permute-start(bf16[2,128,192]{2,1,0:T(8,128)(2,1)} %get-tuple-element.299), channel_id=1, source_target_pairs={{0,2},{1,3},{2,4},{3,5},{4,6},{5,7},{6,0},{7,1},{8,10},{9,11},{10,... | collective-permute-start | bytes 294920 | tf_op jit(solution)/shard_map/ppermute | solution.py:1495
  239.5 11.5 %collective-permute-start.9 = (bf16[2,128,192]{2,1,0:T(8,128)(2,1)}, bf16[2,128,192]{2,1,0:T(8,128)(2,1)}, u32[]{:S(2)}, u32[]{:S(2)}) collective-permute-start(bf16[2,128,192]{2,1,0:T(8,128)(2,1)} %get-tuple-element.300), channel_id=1, source_target_pairs={{0,4},{1,5},{2,6},{3,7},{4,0},{5,1},{6,2},{7,3},{8,12},{9,13},{10,... | collective-permute-start | bytes 294920 | tf_op jit(solution)/shard_map/ppermute | solution.py:1495
  240.0 11.0 %collective-permute-start.8 = (bf16[2,128,192]{2,1,0:T(8,128)(2,1)S(1)}, bf16[2,128,192]{2,1,0:T(8,128)(2,1)}, u32[]{:S(2)}, u32[]{:S(2)}) collective-permute-start(bf16[2,128,192]{2,1,0:T(8,128)(2,1)S(1)} %get-tuple-element.301), channel_id=1, source_target_pairs={{0,6},{1,7},{2,0},{3,1},{4,2},{5,3},{6,4},{7,5},{8,14},{9,15},{10,... | collective-permute-start | bytes 294920 | tf_op jit(solution)/shard_map/ppermute | solution.py:1495
  244.0 152.5 %reduce-scatter.5.cloned.1.call-start = ((), (), s32[]{:S(2)}) async-start(), calls=%async_computation.6 | async-start | bytes 7077888 | tf_op jit(solution)/shard_map/reduce_scatter | solution.py:1657
  258.6 27.3 %collective-permute-start.14 = (bf16[1152,512]{1,0:T(8,128)(2,1)}, bf16[1152,512]{1,0:T(8,128)(2,1)}, u32[]{:S(2)}, u32[]{:S(2)}) collective-permute-start(bf16[1152,512]{1,0:T(8,128)(2,1)} %get-tuple-element.147), channel_id=1, source_target_pairs={{0,16},{8,24},{16,0},{24,8},{1,17},{9,25},{17,1},{25,9},{2,18},{10... | collective-permute-start | bytes 3538952 | tf_op jit(solution)/shard_map/ppermute | solution.py:1146
  260.1 27.1 %collective-permute-start.15 = (bf16[1152,512]{1,0:T(8,128)(2,1)}, bf16[1152,512]{1,0:T(8,128)(2,1)}, u32[]{:S(2)}, u32[]{:S(2)}) collective-permute-start(bf16[1152,512]{1,0:T(8,128)(2,1)} %get-tuple-element.148), channel_id=1, source_target_pairs={{0,8},{8,0},{16,24},{24,16},{1,9},{9,1},{17,25},{25,17},{2,10},{10... | collective-permute-start | bytes 3538952 | tf_op jit(solution)/shard_map/ppermute | solution.py:1146
  262.5 1.7 collective-permute-start.13
  293.2 29.1 %collective-permute-start.18 = (bf16[1152,512]{1,0:T(8,128)(2,1)}, bf16[1152,512]{1,0:T(8,128)(2,1)S(1)}, u32[]{:S(2)}, u32[]{:S(2)}) collective-permute-start(bf16[1152,512]{1,0:T(8,128)(2,1)} %get-tuple-element.179.refs_0_), channel_id=1, source_target_pairs={{0,16},{8,24},{16,0},{24,8},{1,17},{9,25},{17,1},{25,9},{2,18},{10... | collective-permute-start | bytes 3538952 | tf_op jit(solution)/shard_map/ppermute | solution.py:1146
  293.7 30.4 %collective-permute-start.19 = (bf16[1152,512]{1,0:T(8,128)(2,1)}, bf16[1152,512]{1,0:T(8,128)(2,1)}, u32[]{:S(2)}, u32[]{:S(2)}) collective-permute-start(bf16[1152,512]{1,0:T(8,128)(2,1)} %get-tuple-element.181.refs_2_), channel_id=1, source_target_pairs={{0,8},{8,0},{16,24},{24,16},{1,9},{9,1},{17,25},{25,17},{2,10},{10... | collective-permute-start | bytes 3538952 | tf_op jit(solution)/shard_map/ppermute | solution.py:1146
  310.9 21.4 %collective-permute-start.16 = (bf16[2,1,48,2304]{3,2,1,0:T(8,128)(2,1)}, bf16[2,1,48,2304]{3,2,1,0:T(8,128)(2,1)S(1)}, u32[]{:S(2)}, u32[]{:S(2)}) collective-permute-start(bf16[2,1,48,2304]{3,2,1,0:T(8,128)(2,1)} %bitcast.40), channel_id=1, source_target_pairs={{0,8},{8,0},{16,24},{24,16},{1,9},{9,1},{17,25},{25,17},{2,10},{10... | collective-permute-start | bytes 1327112 | tf_op jit(solution)/shard_map/ppermute | solution.py:1146
  312.2 20.1 %collective-permute-start.17 = (bf16[1,2,48,2304]{3,2,1,0:T(8,128)(2,1)S(1)}, bf16[1,2,48,2304]{3,2,1,0:T(8,128)(2,1)S(1)}, u32[]{:S(2)}, u32[]{:S(2)}) collective-permute-start(bf16[1,2,48,2304]{3,2,1,0:T(8,128)(2,1)S(1)} %bitcast.155), channel_id=1, source_target_pairs={{0,16},{8,24},{16,0},{24,8},{1,17},{9,25},{17,1},{25,9},{2,18},{10... | collective-permute-start | bytes 1327112 | tf_op jit(solution)/shard_map/ppermute | solution.py:1146
  324.1 29.2 %collective-permute-start.22 = (bf16[576,512]{1,0:T(8,128)(2,1)}, bf16[576,512]{1,0:T(8,128)(2,1)}, u32[]{:S(2)}, u32[]{:S(2)}) collective-permute-start(bf16[576,512]{1,0:T(8,128)(2,1)} %get-tuple-element.283), channel_id=1, source_target_pairs={{0,8},{8,0},{16,24},{24,16},{1,9},{9,1},{17,25},{25,17},{2,10},{10... | collective-permute-start | bytes 1769480 | tf_op jit(solution)/shard_map/ppermute | solution.py:1146
  327.6 25.7 %collective-permute-start.23 = (bf16[576,512]{1,0:T(8,128)(2,1)}, bf16[576,512]{1,0:T(8,128)(2,1)}, u32[]{:S(2)}, u32[]{:S(2)}) collective-permute-start(bf16[576,512]{1,0:T(8,128)(2,1)} %get-tuple-element.279), channel_id=1, source_target_pairs={{0,16},{8,24},{16,0},{24,8},{1,17},{9,25},{17,1},{25,9},{2,18},{10... | collective-permute-start | bytes 1769480 | tf_op jit(solution)/shard_map/ppermute | solution.py:1146
  334.4 11.7 %collective-permute-start.20 = (bf16[1,1,48,2304]{3,2,1,0:T(8,128)(2,1)S(1)}, bf16[1,1,48,2304]{3,2,1,0:T(8,128)(2,1)S(1)}, u32[]{:S(2)}, u32[]{:S(2)}) collective-permute-start(bf16[1,1,48,2304]{3,2,1,0:T(8,128)(2,1)S(1)} %dynamic-slice_convert_fusion.1), channel_id=1, source_target_pairs={{0,16},{8,24},{16,0},{24,8},{1,17},{9,25},{17,1},{25,9},{2,18},{10... | collective-permute-start | bytes 663560 | tf_op jit(solution)/shard_map/ppermute | solution.py:1146
  335.9 13.7 %collective-permute-start.21 = (bf16[1,1,48,2304]{3,2,1,0:T(8,128)(2,1)S(1)}, bf16[1,1,48,2304]{3,2,1,0:T(8,128)(2,1)S(1)}, u32[]{:S(2)}, u32[]{:S(2)}) collective-permute-start(bf16[1,1,48,2304]{3,2,1,0:T(8,128)(2,1)S(1)} %dynamic-slice_convert_fusion), channel_id=1, source_target_pairs={{0,8},{8,0},{16,24},{24,16},{1,9},{9,1},{17,25},{25,17},{2,10},{10... | collective-permute-start | bytes 663560 | tf_op jit(solution)/shard_map/ppermute | solution.py:1146
  336.6 22.9 %collective-permute-start.27 = (bf16[576,512]{1,0:T(8,128)(2,1)}, bf16[576,512]{1,0:T(8,128)(2,1)}, u32[]{:S(2)}, u32[]{:S(2)}) collective-permute-start(bf16[576,512]{1,0:T(8,128)(2,1)} %get-tuple-element.198), channel_id=1, source_target_pairs={{0,8},{8,0},{16,24},{24,16},{1,9},{9,1},{17,25},{25,17},{2,10},{10... | collective-permute-start | bytes 1769480 | tf_op jit(solution)/shard_map/ppermute | solution.py:1146
  346.1 13.4 %collective-permute-start.28 = (bf16[576,512]{1,0:T(8,128)(2,1)}, bf16[576,512]{1,0:T(8,128)(2,1)}, u32[]{:S(2)}, u32[]{:S(2)}) collective-permute-start(bf16[576,512]{1,0:T(8,128)(2,1)} %get-tuple-element.199), channel_id=1, source_target_pairs={{0,16},{8,24},{16,0},{24,8},{1,17},{9,25},{17,1},{25,9},{2,18},{10... | collective-permute-start | bytes 1769480 | tf_op jit(solution)/shard_map/ppermute | solution.py:1146
  350.3 20.8 %copy-start.44 = (s32[1,128]{1,0:T(1,128)S(1)}, s32[1,128]{1,0:T(1,128)}, u32[]{:S(2)}) copy-start(s32[1,128]{1,0:T(1,128)} %param.16) | copy-start | bytes 1540
  350.3 20.8 %copy-start.8 = (bf16[1,128,1536]{2,1,0:T(8,128)(2,1)S(1)}, bf16[1,128,1536]{2,1,0:T(8,128)(2,1)}, u32[]{:S(2)}) copy-start(bf16[1,128,1536]{2,1,0:T(8,128)(2,1)} %param.15) | copy-start | bytes 1179652
  353.3 8.8 %collective-permute-start.24 = (bf16[2,48,384]{2,1,0:T(8,128)(2,1)}, bf16[2,48,384]{2,1,0:T(8,128)(2,1)S(1)}, u32[]{:S(2)}, u32[]{:S(2)}) collective-permute-start(bf16[2,48,384]{2,1,0:T(8,128)(2,1)} %get-tuple-element.193), channel_id=1, source_target_pairs={{0,6},{1,7},{2,0},{3,1},{4,2},{5,3},{6,4},{7,5},{8,14},{9,15},{10,... | collective-permute-start | bytes 221192 | tf_op jit(solution)/shard_map/ppermute | solution.py:1495
  357.3 10.2 %collective-permute-start.25 = (bf16[2,48,384]{2,1,0:T(8,128)(2,1)}, bf16[2,48,384]{2,1,0:T(8,128)(2,1)S(1)}, u32[]{:S(2)}, u32[]{:S(2)}) collective-permute-start(bf16[2,48,384]{2,1,0:T(8,128)(2,1)} %get-tuple-element.194), channel_id=1, source_target_pairs={{0,4},{1,5},{2,6},{3,7},{4,0},{5,1},{6,2},{7,3},{8,12},{9,13},{10,... | collective-permute-start | bytes 221192 | tf_op jit(solution)/shard_map/ppermute | solution.py:1495
  357.7 9.7 %collective-permute-start.26 = (bf16[2,48,384]{2,1,0:T(8,128)(2,1)}, bf16[2,48,384]{2,1,0:T(8,128)(2,1)S(1)}, u32[]{:S(2)}, u32[]{:S(2)}) collective-permute-start(bf16[2,48,384]{2,1,0:T(8,128)(2,1)} %get-tuple-element.195), channel_id=1, source_target_pairs={{0,2},{1,3},{2,4},{3,5},{4,6},{5,7},{6,0},{7,1},{8,10},{9,11},{10,... | collective-permute-start | bytes 221192 | tf_op jit(solution)/shard_map/ppermute | solution.py:1495
  359.5 24.1 %collective-permute-start.31 = (bf16[576,512]{1,0:T(8,128)(2,1)S(1)}, bf16[576,512]{1,0:T(8,128)(2,1)S(1)}, u32[]{:S(2)}, u32[]{:S(2)}) collective-permute-start(bf16[576,512]{1,0:T(8,128)(2,1)S(1)} %copy-done.28), channel_id=1, source_target_pairs={{0,8},{8,0},{16,24},{24,16},{1,9},{9,1},{17,25},{25,17},{2,10},{10... | collective-permute-start | bytes 1769480 | tf_op jit(solution)/shard_map/ppermute | solution.py:1146
  360.3 23.3 %collective-permute-start.32 = (bf16[576,512]{1,0:T(8,128)(2,1)S(1)}, bf16[576,512]{1,0:T(8,128)(2,1)S(1)}, u32[]{:S(2)}, u32[]{:S(2)}) collective-permute-start(bf16[576,512]{1,0:T(8,128)(2,1)S(1)} %copy-done.29), channel_id=1, source_target_pairs={{0,16},{8,24},{16,0},{24,8},{1,17},{9,25},{17,1},{25,9},{2,18},{10... | collective-permute-start | bytes 1769480 | tf_op jit(solution)/shard_map/ppermute | solution.py:1146
  371.1 1.6 collective-permute-start.29
  375.9 7.7 %collective-permute-start.30 = (bf16[1,1,48,2304]{3,2,1,0:T(8,128)(2,1)}, bf16[1,1,48,2304]{3,2,1,0:T(8,128)(2,1)S(1)}, u32[]{:S(2)}, u32[]{:S(2)}) collective-permute-start(bf16[1,1,48,2304]{3,2,1,0:T(8,128)(2,1)} %bitcast.151), channel_id=1, source_target_pairs={{0,16},{8,24},{16,0},{24,8},{1,17},{9,25},{17,1},{25,9},{2,18},{10... | collective-permute-start | bytes 663560 | tf_op jit(solution)/shard_map/ppermute | solution.py:1146
  377.2 10.0 %collective-permute-start.34 = (bf16[1,1,48,2304]{3,2,1,0:T(8,128)(2,1)}, bf16[1,1,48,2304]{3,2,1,0:T(8,128)(2,1)S(1)}, u32[]{:S(2)}, u32[]{:S(2)}) collective-permute-start(bf16[1,1,48,2304]{3,2,1,0:T(8,128)(2,1)} %bitcast.150), channel_id=1, source_target_pairs={{0,8},{8,0},{16,24},{24,16},{1,9},{9,1},{17,25},{25,17},{2,10},{10... | collective-permute-start | bytes 663560 | tf_op jit(solution)/shard_map/ppermute | solution.py:1146
  385.7 15.2 %collective-permute-start.33 = (bf16[2,1,48,2304]{3,2,1,0:T(8,128)(2,1)}, bf16[2,1,48,2304]{3,2,1,0:T(8,128)(2,1)}, u32[]{:S(2)}, u32[]{:S(2)}) collective-permute-start(bf16[2,1,48,2304]{3,2,1,0:T(8,128)(2,1)} %pad_maximum_fusion.10), channel_id=1, source_target_pairs={{0,8},{8,0},{16,24},{24,16},{1,9},{9,1},{17,25},{25,17},{2,10},{10... | collective-permute-start | bytes 1327112 | tf_op jit(solution)/shard_map/ppermute | solution.py:1146
  388.1 13.9 %collective-permute-start.35 = (bf16[1,2,48,2304]{3,2,1,0:T(8,128)(2,1)}, bf16[1,2,48,2304]{3,2,1,0:T(8,128)(2,1)}, u32[]{:S(2)}, u32[]{:S(2)}) collective-permute-start(bf16[1,2,48,2304]{3,2,1,0:T(8,128)(2,1)} %pad_maximum_fusion.11), channel_id=1, source_target_pairs={{0,16},{8,24},{16,0},{24,8},{1,17},{9,25},{17,1},{25,9},{2,18},{10... | collective-permute-start | bytes 1327112 | tf_op jit(solution)/shard_map/ppermute | solution.py:1146
  389.5 22.0 %collective-permute-start.36 = (bf16[576,512]{1,0:T(8,128)(2,1)S(1)}, bf16[576,512]{1,0:T(8,128)(2,1)S(1)}, u32[]{:S(2)}, u32[]{:S(2)}) collective-permute-start(bf16[576,512]{1,0:T(8,128)(2,1)S(1)} %copy-done.26), channel_id=1, source_target_pairs={{0,8},{8,0},{16,24},{24,16},{1,9},{9,1},{17,25},{25,17},{2,10},{10... | collective-permute-start | bytes 1769480 | tf_op jit(solution)/shard_map/ppermute | solution.py:1146
  389.9 22.3 %collective-permute-start.37 = (bf16[576,512]{1,0:T(8,128)(2,1)S(1)}, bf16[576,512]{1,0:T(8,128)(2,1)}, u32[]{:S(2)}, u32[]{:S(2)}) collective-permute-start(bf16[576,512]{1,0:T(8,128)(2,1)S(1)} %copy-done.27), channel_id=1, source_target_pairs={{0,16},{8,24},{16,0},{24,8},{1,17},{9,25},{17,1},{25,9},{2,18},{10... | collective-permute-start | bytes 1769480 | tf_op jit(solution)/shard_map/ppermute | solution.py:1146
  (41 other events, 134.4 us)
Sparse Core Ops, SparseCore 0:
  11.5 59.9 all-gather.10
  73.1 37.1 all-gather.6
  112.5 37.1 all-gather.12
  189.3 41.5 reduce-scatter.2
  244.1 37.8 all-gather.8
  311.0 76.0 reduce-scatter.4
